TPU v7x, 32 devices: a whole 2x2x4 slice. The times are simulated.
32 devices in a mesh: dp: 8 (over z, y), ctx: 4 (over x, core).
Axes of the slice: x: 2, y: 2, z: 4, core: 2. Of those that a mesh axis runs over, the one named last changes fastest.
Arguments:
- tokens: bfloat16 [32768, 768], P(('dp', 'ctx')), may hold values from -6 to 6
- out_grad: bfloat16 [32768, 768], P(('dp', 'ctx')), may hold values from -6 to 6
- positions: int32 [32768], P(('dp', 'ctx')), may hold values from -1 to 2047, as said below
- master: float32 [55392, 128], P(('dp', 'ctx'))
- first_moment: float32 [55392, 128], P(('dp', 'ctx'))
- second_moment: float32 [55392, 128], P(('dp', 'ctx'))
- step_count: int32 [1], replicated, may hold values from 2 to 20
Outputs:
- layer_out: bfloat16 [32768, 768], P(('dp', 'ctx'))
- input_grad: float32 [32768, 768], P(('dp', 'ctx'))
- new_master: float32 [55392, 128], P(('dp', 'ctx'))
- new_first: float32 [55392, 128], P(('dp', 'ctx'))
- new_second: float32 [55392, 128], P(('dp', 'ctx'))
- weight_copy: bfloat16 [55392, 128], P(('dp', 'ctx'))
Inputs may be any that keep to these rules, and one draw needn't show every extreme that they name: `positions`: rows form blocks of 4096, one per index of dp. In a block, sequences of 1024 or 2048 rows start at multiples of 1024 from the block's start, each row holding its place in its sequence (0, 1, 2, ...); a block's first row holds 0, and the rows after its last sequence hold -1.
All inputs are finite; a program needn't handle non-finite values.
Results may differ from a plain program's by a relative error of at most 0.015.
The roundings to bfloat16 on the way count: a program that leaves them out, or rounds other values in their place, can miss the bound.
Values may be sent and summed in bfloat16 or wider, within the bound.
No kernel may reach another device: no remote copies, remote signals or barrier semaphores. Data moves between devices by JAX's collectives and lax.ppermute only.
A program may use at most 448 MiB of HBM per device.

v0:
```python
import jax
import jax.numpy as jnp
from jax import lax
from jax.sharding import PartitionSpec as P

D = 768
HEADS = 12
HEAD_DIM = 64
FF = 3072
SEQ_MIN = 1024


norm_eps = 1e-06


def from_behind(block, axis, distance):
    devices = range(lax.axis_size(axis))
    route = [(i - distance, i) for i in devices if i - distance in devices]
    return lax.ppermute(block, axis, route)


def unpack(flat):
    values = flat.reshape(-1)
    square_size = D * D
    wide_size = D * FF
    in_weight = jnp.concatenate(
        [
            values[0:square_size].reshape(D, D),
            values[square_size : 2 * square_size].reshape(D, D),
            values[2 * square_size : 3 * square_size].reshape(D, D),
        ],
        1,
    )
    out_weight = values[3 * square_size : 4 * square_size].reshape(D, D)
    up_weight = values[4 * square_size : 4 * square_size + wide_size].reshape(D, FF)
    down_weight = values[4 * square_size + wide_size : 4 * square_size + 2 * wide_size].reshape(
        FF, D
    )
    small_start = 4 * square_size + 2 * wide_size
    gain_first = values[small_start : small_start + D].astype(jnp.float32)
    gain_second = values[small_start + D : small_start + 2 * D].astype(jnp.float32)
    conv_taps = (
        values[small_start + 2 * D : small_start + 11 * D].reshape(3, 3 * D).astype(jnp.float32)
    )
    return (in_weight, out_weight, up_weight, down_weight, gain_first, gain_second, conv_taps)


def normalize(values, gain):
    factor = lax.rsqrt(jnp.mean(values * values, axis=-1, keepdims=True) + norm_eps)
    scaled = values * factor
    return (scaled, factor, scaled * gain)


def norm_back(grad_in, scaled, factor, gain):
    weighted = grad_in * gain
    inner_mean = jnp.mean(weighted * scaled, axis=-1, keepdims=True)
    return (factor * (weighted - scaled * inner_mean), jnp.sum(grad_in * scaled, axis=0))


def masked_scores(query_part, key_heads, query_rows, lowest_part, key_index):
    scores = (
        jnp.einsum("qhd,khd->hqk", query_part, key_heads, preferred_element_type=jnp.float32)
        * 0.125
    )
    allowed = (key_index[None, :] <= query_rows[:, None]) & (
        key_index[None, :] >= lowest_part[:, None]
    )
    return jnp.where(allowed[None], scores, -1e30)


def adam_update(master, moment_one, moment_two, gradient, step_count, row_start):
    row_index = row_start + jnp.arange(master.shape[0], dtype=jnp.int32)
    matrix_rows = (4 * D * D + 2 * D * FF) // 128
    out_first = 3 * D * D // 128
    out_last = 4 * D * D // 128
    is_matrix = (row_index < matrix_rows)[:, None]
    is_out = ((row_index >= out_first) & (row_index < out_last))[:, None]
    step_rate = jnp.where(is_matrix, jnp.where(is_out, 0.5, 0.1), 1.0)
    decay_rate = jnp.where(is_matrix, 0.1, 0.0)
    step_value = step_count[0].astype(jnp.float32)
    new_one = 0.9 * moment_one + 0.1 * gradient
    new_two = 0.999 * moment_two + 0.001 * gradient * gradient
    corr_first = 1.0 - jnp.power(0.9, step_value)
    corr_second = 1.0 - jnp.power(0.999, step_value)
    new_weights = master - step_rate * (
        new_one / corr_first / (jnp.sqrt(new_two / corr_second) + 1e-08) + decay_rate * master
    )
    return (new_weights, new_one, new_two)


def shards(tokens, out_grad, positions, master, first_moment, second_moment, step_count):
    rows_here = tokens.shape[0]
    span_rows = min(512, rows_here)
    span_count = rows_here // span_rows
    ctx_count = lax.axis_size("ctx")
    reach_back = min(ctx_count - 1, max(1, 2 * SEQ_MIN // rows_here - 1))
    ctx_place = lax.axis_index("ctx")
    triple_width = 3 * D
    shard_low = master.astype(jnp.bfloat16)
    gathered = lax.all_gather(shard_low, ("dp", "ctx"), axis=0, tiled=True)
    in_weight, out_weight, up_weight, down_weight, gain_first, gain_second, conv_taps = unpack(
        gathered
    )
    inputs = tokens.astype(jnp.float32)
    scaled_one, factor_one, normed_one = normalize(inputs, gain_first)
    normed_low = normed_one.astype(jnp.bfloat16)
    projected = jnp.dot(normed_low, in_weight, preferred_element_type=jnp.float32).astype(
        jnp.bfloat16
    )
    rim_rows = from_behind(projected[rows_here - 2 :], "ctx", 1)
    extended = jnp.concatenate([rim_rows, projected], 0).astype(jnp.float32)
    after_one = (positions >= 1).astype(jnp.float32)[:, None]
    after_two = (positions >= 2).astype(jnp.float32)[:, None]
    mixed_full = (
        conv_taps[0] * extended[2:]
        + after_one * conv_taps[1] * extended[1:-1]
        + after_two * conv_taps[2] * extended[:-2]
    )
    mixed_low = mixed_full.astype(jnp.bfloat16)
    query_heads = mixed_low[:, :D].reshape(rows_here, HEADS, HEAD_DIM)
    own_pairs = mixed_low[:, D:]
    earlier = [from_behind(own_pairs, "ctx", 1)]
    key_values = jnp.concatenate(earlier + [own_pairs], 0)
    key_heads = key_values[:, :D].reshape(-1, HEADS, HEAD_DIM)
    value_heads = key_values[:, D:].reshape(-1, HEADS, HEAD_DIM)
    key_index = (ctx_place - reach_back) * rows_here + jnp.arange(
        key_values.shape[0], dtype=jnp.int32
    )
    query_index = ctx_place * rows_here + jnp.arange(rows_here, dtype=jnp.int32)
    lowest = query_index - jnp.maximum(positions, 0)
    attended = []
    log_totals = []
    for span_at in range(span_count):
        rows_part = slice(span_at * span_rows, (span_at + 1) * span_rows)
        scores = masked_scores(
            query_heads[rows_part], key_heads, query_index[rows_part], lowest[rows_part], key_index
        )
        peak_score = jnp.max(scores, axis=-1, keepdims=True)
        raised = jnp.exp(scores - peak_score)
        total_sum = jnp.sum(raised, axis=-1, keepdims=True)
        probs_low = (raised / total_sum).astype(jnp.bfloat16)
        span_out = jnp.einsum(
            "hqk,khd->qhd", probs_low, value_heads, preferred_element_type=jnp.float32
        )
        attended.append(span_out.reshape(span_rows, D))
        log_totals.append(peak_score + jnp.log(total_sum))
    attn_low = jnp.concatenate(attended, 0).astype(jnp.bfloat16)
    hidden = inputs + jnp.dot(attn_low, out_weight, preferred_element_type=jnp.float32)
    scaled_two, factor_two, normed_two = normalize(hidden, gain_second)
    second_low = normed_two.astype(jnp.bfloat16)
    before = jnp.dot(second_low, up_weight, preferred_element_type=jnp.float32)
    active = jnp.maximum(before, 0.0)
    squared_low = (active * active).astype(jnp.bfloat16)
    layer_out = (
        hidden + jnp.dot(squared_low, down_weight, preferred_element_type=jnp.float32)
    ).astype(jnp.bfloat16)
    regathered = lax.all_gather(shard_low, ("dp", "ctx"), axis=0, tiled=True)
    in_weight, out_weight, up_weight, down_weight, gain_first, gain_second, conv_taps = unpack(
        regathered
    )
    fetched = [from_behind(own_pairs, "ctx", 1)]
    key_values = jnp.concatenate(fetched + [own_pairs], 0)
    key_heads = key_values[:, :D].reshape(-1, HEADS, HEAD_DIM)
    value_heads = key_values[:, D:].reshape(-1, HEADS, HEAD_DIM)
    grad_out = out_grad.astype(jnp.float32) * (positions >= 0).astype(jnp.float32)[:, None]
    grad_low = grad_out.astype(jnp.bfloat16)
    grad_down = jnp.einsum("tf,td->fd", squared_low, grad_low, preferred_element_type=jnp.float32)
    grad_squared = jnp.einsum(
        "td,fd->tf", grad_low, down_weight, preferred_element_type=jnp.float32
    )
    grad_before = (grad_squared * 2.0 * active).astype(jnp.bfloat16)
    grad_up = jnp.einsum("td,tf->df", second_low, grad_before, preferred_element_type=jnp.float32)
    grad_normed_two = jnp.einsum(
        "tf,df->td", grad_before, up_weight, preferred_element_type=jnp.float32
    )
    back_two, grad_gain_two = norm_back(grad_normed_two, scaled_two, factor_two, gain_second)
    grad_hidden = grad_out + back_two
    hidden_low = grad_hidden.astype(jnp.bfloat16)
    grad_outw = jnp.einsum("td,te->de", attn_low, hidden_low, preferred_element_type=jnp.float32)
    grad_attended = jnp.einsum(
        "te,de->td", hidden_low, out_weight, preferred_element_type=jnp.float32
    ).astype(jnp.bfloat16)
    grad_heads = grad_attended.reshape(rows_here, HEADS, HEAD_DIM)
    grad_query_parts = []
    grad_keys = jnp.zeros(key_heads.shape, jnp.float32)
    grad_values = jnp.zeros(value_heads.shape, jnp.float32)
    for span_at in range(span_count):
        rows_part = slice(span_at * span_rows, (span_at + 1) * span_rows)
        scores = masked_scores(
            query_heads[rows_part], key_heads, query_index[rows_part], lowest[rows_part], key_index
        )
        probs_full = jnp.exp(scores - log_totals[span_at])
        probs_low = probs_full.astype(jnp.bfloat16)
        grad_probs = jnp.einsum(
            "qhd,khd->hqk", grad_heads[rows_part], value_heads, preferred_element_type=jnp.float32
        )
        inner_sum = jnp.sum(probs_full * grad_probs, axis=-1, keepdims=True)
        grad_scores = (probs_full * (grad_probs - inner_sum)).astype(jnp.bfloat16)
        grad_query_parts.append(
            jnp.einsum("hqk,khd->qhd", grad_scores, key_heads, preferred_element_type=jnp.float32)
            * 0.125
        )
        grad_keys = (
            grad_keys
            + jnp.einsum(
                "hqk,qhd->khd",
                grad_scores,
                query_heads[rows_part],
                preferred_element_type=jnp.float32,
            )
            * 0.125
        )
        grad_values = grad_values + jnp.einsum(
            "hqk,qhd->khd", probs_low, grad_heads[rows_part], preferred_element_type=jnp.float32
        )
    grad_query = jnp.concatenate(grad_query_parts, 0).reshape(rows_here, D)
    grad_pairs = jnp.concatenate([grad_keys.reshape(-1, D), grad_values.reshape(-1, D)], 1)
    own_grad = grad_pairs[reach_back * rows_here :]
    piece_rows = grad_pairs[(reach_back - 1) * rows_here : (reach_back - 1 + 1) * rows_here]
    own_grad = own_grad + from_behind(piece_rows.astype(jnp.bfloat16), "ctx", -1).astype(
        piece_rows.dtype
    )
    grad_mixed = jnp.concatenate([grad_query, own_grad], 1)
    lead_rows = jnp.stack(
        [
            conv_taps[2] * after_two[0] * grad_mixed[0],
            conv_taps[1] * after_one[0] * grad_mixed[0]
            + conv_taps[2] * after_two[1] * grad_mixed[1],
        ]
    )
    tail_rows = from_behind(lead_rows, "ctx", -1)
    grad_projected = (
        conv_taps[0] * grad_mixed
        + jnp.concatenate(
            [
                conv_taps[1] * after_one[1:] * grad_mixed[1:],
                jnp.zeros((1, triple_width), jnp.float32),
            ],
            0,
        )
        + jnp.concatenate(
            [
                conv_taps[2] * after_two[2:] * grad_mixed[2:],
                jnp.zeros((2, triple_width), jnp.float32),
            ],
            0,
        )
        + jnp.concatenate([jnp.zeros((rows_here - 2, triple_width), jnp.float32), tail_rows], 0)
    )
    tap_grads = jnp.stack(
        [
            jnp.sum(grad_mixed * extended[2:], axis=0),
            jnp.sum(after_one * grad_mixed * extended[1:-1], axis=0),
            jnp.sum(after_two * grad_mixed * extended[:-2], axis=0),
        ]
    )
    projected_grad_low = grad_projected.astype(jnp.bfloat16)
    grad_inw = jnp.einsum(
        "td,te->de", normed_low, projected_grad_low, preferred_element_type=jnp.float32
    )
    grad_normed_one = jnp.einsum(
        "te,de->td", projected_grad_low, in_weight, preferred_element_type=jnp.float32
    )
    back_one, grad_gain_one = norm_back(grad_normed_one, scaled_one, factor_one, gain_first)
    input_grad = grad_hidden + back_one
    total_rows = gathered.shape[0]
    used_count = 4 * D * D + 2 * D * FF + 11 * D
    flat_grad = jnp.concatenate(
        [
            grad_inw[:, :D].reshape(-1),
            grad_inw[:, D : 2 * D].reshape(-1),
            grad_inw[:, 2 * D :].reshape(-1),
            grad_outw.reshape(-1),
            grad_up.reshape(-1),
            grad_down.reshape(-1),
            grad_gain_one,
            grad_gain_two,
            tap_grads.reshape(-1),
            jnp.zeros((total_rows * 128 - used_count,), jnp.float32),
        ]
    ).reshape(total_rows, 128)
    grad_shard = lax.psum_scatter(flat_grad, ("dp", "ctx"), scatter_dimension=0, tiled=True)
    row_start = lax.axis_index(("dp", "ctx")) * master.shape[0]
    new_weights, new_one, new_two = adam_update(
        master, first_moment, second_moment, grad_shard, step_count, row_start
    )
    return (layer_out, input_grad, new_weights, new_one, new_two, new_weights.astype(jnp.bfloat16))


def solution(mesh):
    return jax.shard_map(
        shards,
        mesh=mesh,
        in_specs=(
            P(("dp", "ctx"), None),
            P(("dp", "ctx"), None),
            P(("dp", "ctx")),
            P(("dp", "ctx"), None),
            P(("dp", "ctx"), None),
            P(("dp", "ctx"), None),
            P(),
        ),
        out_specs=(
            P(("dp", "ctx"), None),
            P(("dp", "ctx"), None),
            P(("dp", "ctx"), None),
            P(("dp", "ctx"), None),
            P(("dp", "ctx"), None),
            P(("dp", "ctx"), None),
        ),
        check_vma=False,
    )
```

profile of v0, /device:TPU:0, one launch (start us, length us, event | category | flops | bytes accessed | tf_op | source)
XLA Modules:
  0.0 1156.1 jit_solution(14164347562141519024)
XLA Ops:
  22.5 95.3 %all-gather.3.cloned.1.call-done = bf16[32,1731,128]{2,1,0:T(8,128)(2,1)} async-done(((bf16[1,1731,128]{2,1,0:T(8,128)(2,1)}), bf16[32,1731,128]{2,1,0:T(8,128)(2,1)}) %all-gather.3.cloned.1.call-update) | async-done | bytes 14180368 | tf_op jit(solution)/shard_map/all_gather | solution.py:100
  117.8 11.5 reshape.356
  131.3 4.2 fusion.78
  148.2 4.4 convolution_convert_fusion
  158.4 4.7 add_convert_fusion.1
  165.1 5.3 collective-permute-start.1
  174.3 8.3 reshape.340
  184.5 9.2 reshape.341
  197.6 5.2 pad_maximum_fusion.2
  205.9 5.4 copy.54
  211.4 21.5 %fusion.13 = (f32[12,512]{1,0:T(8,128)S(1)}, f32[12,512,2048]{2,1,0:T(8,128)}) fusion(pred[512,2048]{1,0:T(8,128)(4,1)} %get-tuple-element.61, bf16[512,12,64]{0,2,1:T(8,128)(2,1)} %bitcast.124, bf16[2048,12,64]{0,2,1:T(8,128)(2,1)S(1)} %bitcast.103), kind=kOutput, calls=%fused_computation.27 | convolution fusion | flops 1648355328 | bytes 55336960 | tf_op jit(solution)/shard_map/qhd,khd->hqk/dot_general | solution.py:62
  232.9 22.9 %fusion.1 = f32[12,512]{1,0:T(8,128)S(1)} fusion(f32[12,512]{1,0:T(8,128)S(1)} %get-tuple-element.74, f32[12,512,2048]{2,1,0:T(8,128)} %get-tuple-element.75, pred[512,2048]{1,0:T(8,128)(4,1)} %get-tuple-element.61), kind=kLoop, calls=%fused_computation.12 | loop fusion | flops 50325504 | bytes 51429376 | tf_op jit(solution)/shard_map/reduce_sum | solution.py:140
  256.4 22.1 %fusion.40 = bf16[12,64,512]{2,1,0:T(8,128)(2,1)} fusion(bf16[2048,12,64]{0,2,1:T(8,128)(2,1)} %bitcast.114, f32[12,512]{1,0:T(8,128)S(1)} %fusion.1, f32[12,512]{1,0:T(8,128)S(1)} %get-tuple-element.74, f32[12,512,2048]{2,1,0:T(8,128)} %get-tuple-element.75, pred[512,2048]{1,0:T(8,128)(4,1)S(1)} %copy-done.4), kind=kOutput, calls=%fused_computation.90 | convolution fusion | flops 1673920512 | bytes 55361536 | tf_op jit(solution)/shard_map/hqk,khd->qhd/dot_general | solution.py:142
  278.5 21.5 %fusion.14 = (f32[12,512]{1,0:T(8,128)S(1)}, f32[12,512,2048]{2,1,0:T(8,128)}) fusion(pred[512,2048]{1,0:T(8,128)(4,1)} %get-tuple-element.62, bf16[512,12,64]{0,2,1:T(8,128)(2,1)} %bitcast.122, bf16[2048,12,64]{0,2,1:T(8,128)(2,1)S(1)} %bitcast.104), kind=kOutput, calls=%fused_computation.28 | convolution fusion | flops 1648355328 | bytes 55336960 | tf_op jit(solution)/shard_map/qhd,khd->hqk/dot_general | solution.py:62
  300.0 22.9 %fusion.2 = f32[12,512]{1,0:T(8,128)S(1)} fusion(f32[12,512]{1,0:T(8,128)S(1)} %get-tuple-element.72, f32[12,512,2048]{2,1,0:T(8,128)} %get-tuple-element.73, pred[512,2048]{1,0:T(8,128)(4,1)} %get-tuple-element.62), kind=kLoop, calls=%fused_computation.13 | loop fusion | flops 50325504 | bytes 51429376 | tf_op jit(solution)/shard_map/reduce_sum | solution.py:140
  323.0 22.0 %fusion.39 = bf16[12,64,512]{2,1,0:T(8,128)(2,1)} fusion(bf16[2048,12,64]{0,2,1:T(8,128)(2,1)} %bitcast.115, f32[12,512]{1,0:T(8,128)S(1)} %fusion.2, f32[12,512]{1,0:T(8,128)S(1)} %get-tuple-element.72, f32[12,512,2048]{2,1,0:T(8,128)} %get-tuple-element.73, pred[512,2048]{1,0:T(8,128)(4,1)S(1)} %copy-done.3), kind=kOutput, calls=%fused_computation.89 | convolution fusion | flops 1673920512 | bytes 55361536 | tf_op jit(solution)/shard_map/hqk,khd->qhd/dot_general | solution.py:142
  348.2 8.6 fusion.73
  356.8 10.5 add_convert_fusion.2
  367.3 10.1 multiply_convert_fusion.2
  377.5 12.6 %fusion.38 = f32[3072,768]{1,0:T(8,128)} fusion(f32[1024,3072]{1,0:T(8,128)} %fusion.73, bf16[1024,768]{0,1:T(8,128)(2,1)S(1)} %copy-done.16, f32[1024]{0:T(1024)S(1)} %copy-done.43), kind=kOutput, calls=%fused_computation.85 | convolution fusion | flops 4843634688 | bytes 23597056 | tf_op jit(solution)/shard_map/tf,td->fd/dot_general | solution.py:167
  390.1 6.2 multiply_reduce_fusion.5
  396.2 7.9 convolution_bitcast_fusion
  410.6 22.9 %fusion.5 = f32[12,64,2048]{2,1,0:T(8,128)} fusion(bf16[512,12,64]{0,2,1:T(8,128)(2,1)S(1)} %bitcast.131, f32[12,512]{1,0:T(8,128)S(1)} %log_add_fusion, f32[12,512,2048]{2,1,0:T(8,128)} %get-tuple-element.73, pred[512,2048]{1,0:T(8,128)(4,1)S(1)} %copy-done.3), kind=kOutput, calls=%fused_computation.16 | convolution fusion | flops 1660944384 | bytes 58482688 | tf_op jit(solution)/shard_map/hqk,qhd->khd/dot_general | solution.py:213
  433.5 37.1 %multiply_reduce_fusion = (f32[12,512]{1,0:T(8,128)S(1)}, f32[12,512,2048]{2,1,0:T(8,128)}) fusion(f32[12,512]{1,0:T(8,128)S(1)} %log_add_fusion, f32[12,512,2048]{2,1,0:T(8,128)} %get-tuple-element.73, pred[512,2048]{1,0:T(8,128)(4,1)S(1)} %copy-done.3, bf16[512,12,64]{0,2,1:T(8,128)(2,1)S(1)} %bitcast.132, bf16[2048,12,64]{0,2,1:T(8,128)(2,1)} %bitcast.116), kind=kOutput, calls=%fused_computation.1 | convolution fusion | flops 1673521152 | bytes 105693184 | tf_op jit(solution)/shard_map/qhd,khd->hqk/dot_general | solution.py:194
  473.2 10.9 reshape.350
  484.2 9.5 copy.75
  496.9 37.1 %multiply_reduce_fusion.1 = (f32[12,512]{1,0:T(8,128)S(1)}, f32[12,512,2048]{2,1,0:T(8,128)}) fusion(f32[12,512]{1,0:T(8,128)S(1)} %copy-done.21, f32[12,512,2048]{2,1,0:T(8,128)} %get-tuple-element.75, pred[512,2048]{1,0:T(8,128)(4,1)S(1)} %copy-done.5, bf16[512,12,64]{0,2,1:T(8,128)(2,1)S(1)} %bitcast.129, bf16[2048,12,64]{0,2,1:T(8,128)(2,1)} %bitcast.117), kind=kOutput, calls=%fused_computation.4 | convolution fusion | flops 1673521152 | bytes 105693184 | tf_op jit(solution)/shard_map/qhd,khd->hqk/dot_general | solution.py:194
  534.0 25.3 %fusion.26 = f32[12,64,2048]{2,1,0:T(8,128)} fusion(f32[12,64,2048]{2,1,0:T(8,128)} %fusion.5, bf16[512,12,64]{0,2,1:T(8,128)(2,1)S(1)} %bitcast.130, f32[12,512]{1,0:T(8,128)S(1)} %copy-done.21, f32[12,512,2048]{2,1,0:T(8,128)} %get-tuple-element.75, pred[512,2048]{1,0:T(8,128)(4,1)S(1)} %copy-done.5), kind=kOutput, calls=%fused_computation.65 | convolution fusion | flops 1662517248 | bytes 64774144 | tf_op jit(solution)/shard_map/hqk,qhd->khd/dot_general | solution.py:213
  559.4 6.6 copy.62
  565.9 40.8 %multiply_convert_fusion.1 = bf16[12,512,2048]{2,1,0:T(8,128)(2,1)} fusion(f32[12,512,2048]{2,1,0:T(8,128)} %get-tuple-element.80, f32[12,512]{1,0:T(8,128)S(1)} %get-tuple-element.79, f32[12,512]{1,0:T(8,128)S(1)} %copy-done.21, f32[12,512,2048]{2,1,0:T(8,128)} %get-tuple-element.75, pred[512,2048]{1,0:T(8,128)(4,1)S(1)} %copy-done.5), kind=kLoop, calls=%fused_computation.3 | loop fusion | flops 75497472 | bytes 126926848 | tf_op jit(solution)/shard_map/convert_element_type | solution.py:198
  606.8 15.4 %fusion.85 = f32[12,64,2048]{2,1,0:T(8,128)} fusion(bf16[512,12,64]{0,2,1:T(8,128)(2,1)S(1)} %bitcast.125, bf16[12,512,2048]{2,1,0:T(8,128)(2,1)} %multiply_convert_fusion.1), kind=kOutput, calls=%fused_computation.173 | convolution fusion | flops 1610612736 | bytes 32243712 | tf_op jit(solution)/shard_map/hqk,qhd->khd/dot_general | solution.py:205
  622.1 40.4 %multiply_convert_fusion = bf16[12,512,2048]{2,1,0:T(8,128)(2,1)} fusion(f32[12,512,2048]{2,1,0:T(8,128)} %get-tuple-element.82, f32[12,512]{1,0:T(8,128)S(1)} %get-tuple-element.81, f32[12,512]{1,0:T(8,128)S(1)} %log_add_fusion, f32[12,512,2048]{2,1,0:T(8,128)} %get-tuple-element.73, pred[512,2048]{1,0:T(8,128)(4,1)S(1)} %copy-done.3), kind=kLoop, calls=%fused_computation | loop fusion | flops 75497472 | bytes 126926848 | tf_op jit(solution)/shard_map/convert_element_type | solution.py:198
  662.6 17.2 %add_multiply_fusion = f32[12,64,2048]{2,1,0:T(8,128)} fusion(f32[12,64,2048]{2,1,0:T(8,128)} %fusion.85, bf16[512,12,64]{0,2,1:T(8,128)(2,1)S(1)} %bitcast.123, bf16[12,512,2048]{2,1,0:T(8,128)(2,1)} %multiply_convert_fusion), kind=kOutput, calls=%fused_computation.52 | convolution fusion | flops 1613758464 | bytes 38535168 | tf_op jit(solution)/shard_map/hqk,qhd->khd/dot_general | solution.py:205
  679.8 6.6 copy.61
  686.3 5.0 fusion.21
  692.6 13.7 %multiply_bitcast_fusion.1 = f32[512,12,64]{0,2,1:T(8,128)} fusion(bf16[2048,12,64]{0,2,1:T(8,128)(2,1)S(1)} %bitcast.105, bf16[12,512,2048]{2,1,0:T(8,128)(2,1)} %multiply_convert_fusion.1), kind=kOutput, calls=%fused_computation.88 | convolution fusion | flops 1611005952 | bytes 29884416 | tf_op jit(solution)/shard_map/hqk,khd->qhd/dot_general | solution.py:200
  706.3 13.7 %multiply_bitcast_fusion = f32[512,12,64]{0,2,1:T(8,128)} fusion(bf16[2048,12,64]{0,2,1:T(8,128)(2,1)S(1)} %bitcast.106, bf16[12,512,2048]{2,1,0:T(8,128)(2,1)} %multiply_convert_fusion), kind=kOutput, calls=%fused_computation.87 | convolution fusion | flops 1611005952 | bytes 29884416 | tf_op jit(solution)/shard_map/hqk,khd->qhd/dot_general | solution.py:200
  726.4 4.2 fusion.20
  732.8 5.7 fusion.16
  738.5 4.6 fusion.18
  744.5 13.6 %multiply_reduce_fusion.4 = (f32[2304]{0:T(1024)S(1)}, f32[2304]{0:T(1024)S(1)}, f32[2304]{0:T(1024)S(1)}, bf16[1024,2304]{1,0:T(8,128)(2,1)}) fusion(f32[1026,2304]{1,0:T(8,128)S(1)} %bitcast.102, f32[1024,1536]{1,0:T(8,128)S(1)} %fusion.20, f32[1024,768]{1,0:T(8,128)S(1)} %copy.63, f32[1024]{0:T(1024)S(1)} %copy-done.31, f32[1024]{0:T(1024)S(1)} %copy-done.33, ...), kind=kLoop, calls=%fused_computation.43 | loop fusion | flops 33023232 | bytes 61377536 | tf_op jit(solution)/shard_map/reduce_sum | solution.py:252
  758.2 9.3 fusion.34
  767.5 6.0 fusion.47
  773.6 5.8 fusion.79
  798.7 4.9 constant_dynamic-update-slice_fusion.8
  814.1 303.4 %fusion = f32[1744,128]{1,0:T(8,128)S(1)} fusion(f32[55392,128]{1,0:T(8,128)} %bitcast.26), kind=kCustom, calls=%all-reduce-scatter | all-reduce-scatter fusion | flops 7143425 | bytes 29253632
  1118.3 16.1 %collective-permute-start.4 = (f32[403,128]{1,0:T(8,128)}, f32[403,128]{1,0:T(8,128)}, u32[]{:S(2)}, u32[]{:S(2)}) collective-permute-start(f32[403,128]{1,0:T(8,128)} %slice.268), channel_id=1, source_target_pairs={{0,1},{1,2},{2,3},{3,4},{4,5},{5,6},{6,7},{7,8},{8,9},{9,10},{10,1... | collective-permute-start | bytes 619016
  1134.3 5.2 fusion.33
  (224 shorter events, 116.7 us)
Async XLA Ops:
  7.2 12.4 %copy-start.44 = (s32[1024]{0:T(1024)S(1)}, s32[1024]{0:T(1024)}, u32[]{:S(2)}) copy-start(s32[1024]{0:T(1024)} %param.9) | copy-start | bytes 12292
  7.2 110.6 %all-gather.3.cloned.1.call-start = ((), (), s32[]{:S(2)}) async-start(), calls=%async_computation | async-start | bytes 14665728 | tf_op jit(solution)/shard_map/all_gather | solution.py:100
  10.5 147.8 %copy-start.30 = (f32[1024]{0:T(1024)}, f32[1024]{0:T(1024)S(1)}, u32[]{:S(2)}) copy-start(f32[1024]{0:T(1024)S(1)} %get-tuple-element.66) | copy-start | bytes 12292
  10.5 147.9 %copy-start.32 = (f32[1024]{0:T(1024)}, f32[1024]{0:T(1024)S(1)}, u32[]{:S(2)}) copy-start(f32[1024]{0:T(1024)S(1)} %get-tuple-element.67) | copy-start | bytes 12292
  14.8 133.3 %copy-start.7 = (bf16[1024,768]{0,1:T(8,128)(2,1)}, bf16[1024,768]{0,1:T(8,128)(2,1)S(1)}, u32[]{:S(2)}) copy-start(bf16[1024,768]{0,1:T(8,128)(2,1)S(1)} %copy.53) | copy-start | bytes 4718596
  19.6 128.6 %copy-start.41 = (f32[1024]{0:T(1024)}, f32[1024]{0:T(1024)S(1)}, u32[]{:S(2)}) copy-start(f32[1024]{0:T(1024)S(1)} %add_rsqrt_fusion.1) | copy-start | bytes 12292
  130.6 17.6 %copy-start.39 = (f32[768]{0:T(1024)}, f32[768]{0:T(1024)S(1)}, u32[]{:S(2)}) copy-start(f32[768]{0:T(1024)S(1)} %get-tuple-element.38) | copy-start | bytes 9220
  152.7 4.7 collective-permute-start
  158.4 12.0 %slice-start.3 = ((s8[14180352]{0:T(1024)(128)(4,1)}), s8[4194304]{0:T(1024)(128)(4,1)S(1)}, s32[]{:S(2)}) async-start(s8[14180352]{0:T(1024)(128)(4,1)} %bitcast.107), calls=%async_computation.4 | async-start | bytes 8388608
  158.4 12.0 %slice-start.4 = ((s8[14180352]{0:T(1024)(128)(4,1)}), s8[4194304]{0:T(1024)(128)(4,1)S(1)}, s32[]{:S(2)}) async-start(s8[14180352]{0:T(1024)(128)(4,1)} %bitcast.107), calls=%async_computation.5 | async-start | bytes 8388608
  158.4 12.0 %slice-start.5 = ((s8[14180352]{0:T(1024)(128)(4,1)}), s8[4194304]{0:T(1024)(128)(4,1)S(1)}, s32[]{:S(2)}) async-start(s8[14180352]{0:T(1024)(128)(4,1)} %bitcast.107), calls=%async_computation.6 | async-start | bytes 8388608
  158.4 12.0 %slice-start.6 = ((s8[14180352]{0:T(1024)(128)(4,1)}), s8[1597440]{0:T(1024)(128)(4,1)S(1)}, s32[]{:S(2)}) async-start(s8[14180352]{0:T(1024)(128)(4,1)} %bitcast.107), calls=%async_computation.7 | async-start | bytes 3194880
  163.2 11.2 copy-start.6
  165.1 32.5 %collective-permute-start.1 = (bf16[1024,1536]{1,0:T(8,128)(2,1)}, bf16[1024,1536]{1,0:T(8,128)(2,1)}, u32[]{:S(2)}, u32[]{:S(2)}) collective-permute-start(bf16[1024,1536]{1,0:T(8,128)(2,1)} %slice.244), channel_id=1, source_target_pairs={{0,1},{1,2},{2,3},{4,5},{5,6},{6,7},{8,9},{9,10},{10,11},{12,13},{... | collective-permute-start | bytes 9437192 | tf_op jit(solution)/shard_map/ppermute | solution.py:19
  174.3 8.3 copy-start.18
  205.9 72.6 %copy-start.1 = (bf16[2048,768]{0,1:T(8,128)(2,1)}, bf16[2048,768]{0,1:T(8,128)(2,1)S(1)}, u32[]{:S(2)}) copy-start(bf16[2048,768]{0,1:T(8,128)(2,1)S(1)} %copy.56) | copy-start | bytes 9437188
  232.9 23.6 %copy-start.4 = (pred[512,2048]{1,0:T(8,128)(4,1)S(1)}, pred[512,2048]{1,0:T(8,128)(4,1)}, u32[]{:S(2)}) copy-start(pred[512,2048]{1,0:T(8,128)(4,1)} %get-tuple-element.61) | copy-start | bytes 3145732
  300.0 22.9 %copy-start.3 = (pred[512,2048]{1,0:T(8,128)(4,1)S(1)}, pred[512,2048]{1,0:T(8,128)(4,1)}, u32[]{:S(2)}) copy-start(pred[512,2048]{1,0:T(8,128)(4,1)} %get-tuple-element.62) | copy-start | bytes 3145732
  322.9 22.0 %copy-start.8 = (bf16[1024,768]{0,1:T(8,128)(2,1)S(1)}, bf16[1024,768]{0,1:T(8,128)(2,1)}, u32[]{:S(2)}) copy-start(bf16[1024,768]{0,1:T(8,128)(2,1)} %copy-done.7) | copy-start | bytes 4718596
  323.0 22.0 %copy-start.20 = (bf16[768,768]{1,0:T(8,128)(2,1)S(1)}, bf16[768,768]{1,0:T(8,128)(2,1)}, u32[]{:S(2)}) copy-start(bf16[768,768]{1,0:T(8,128)(2,1)} %reshape.339) | copy-start | bytes 3538948
  348.2 19.1 %slice-start.15 = ((s8[4718592]{0:T(1024)(128)(4,1)}), s8[4194304]{0:T(1024)(128)(4,1)S(1)}, s32[]{:S(2)}) async-start(s8[4718592]{0:T(1024)(128)(4,1)} %bitcast.127), calls=%async_computation.16 | async-start | bytes 8388608
  356.8 10.6 copy-start.16
  356.8 10.6 slice-start.16
  356.8 10.6 copy-start.43
  377.4 12.6 %copy-start.50 = (bf16[1024,3072]{1,0:T(8,128)(2,1)S(1)}, bf16[1024,3072]{1,0:T(8,128)(2,1)}, u32[]{:S(2)}) copy-start(bf16[1024,3072]{1,0:T(8,128)(2,1)} %multiply_convert_fusion.2) | copy-start | bytes 18874372
  484.1 12.7 %copy-start.5 = (pred[512,2048]{1,0:T(8,128)(4,1)S(1)}, pred[512,2048]{1,0:T(8,128)(4,1)}, u32[]{:S(2)}) copy-start(pred[512,2048]{1,0:T(8,128)(4,1)} %get-tuple-element.61) | copy-start | bytes 3145732
  484.1 12.7 %copy-start.21 = (f32[12,512]{1,0:T(8,128)S(1)}, f32[12,512]{1,0:T(8,128)}, u32[]{:S(2)}) copy-start(f32[12,512]{1,0:T(8,128)} %log_add_fusion.1) | copy-start | bytes 73732
  565.9 40.8 %copy-start.15 = (bf16[512,768]{0,1:T(8,128)(2,1)S(1)}, bf16[512,768]{0,1:T(8,128)(2,1)}, u32[]{:S(2)}) copy-start(bf16[512,768]{0,1:T(8,128)(2,1)} %copy.55) | copy-start | bytes 2359300
  622.1 40.4 %copy-start.14 = (bf16[512,768]{0,1:T(8,128)(2,1)S(1)}, bf16[512,768]{0,1:T(8,128)(2,1)}, u32[]{:S(2)}) copy-start(bf16[512,768]{0,1:T(8,128)(2,1)} %copy.57) | copy-start | bytes 2359300
  686.3 6.3 copy-start.2
  691.3 35.1 %collective-permute-start.2 = (bf16[1024,1536]{1,0:T(8,128)(2,1)}, bf16[1024,1536]{1,0:T(8,128)(2,1)}, u32[]{:S(2)}, u32[]{:S(2)}) collective-permute-start(bf16[1024,1536]{1,0:T(8,128)(2,1)} %fusion.21), channel_id=1, source_target_pairs={{1,0},{2,1},{3,2},{5,4},{6,5},{7,6},{9,8},{10,9},{11,10},{13,12},{... | collective-permute-start | bytes 9437192 | tf_op jit(solution)/shard_map/ppermute | solution.py:19
  731.4 7.1 copy-start.25
  731.4 7.1 copy-start.46
  731.5 13.0 %collective-permute-start.3 = (f32[2,2304]{1,0:T(2,128)S(1)}, f32[2,2304]{1,0:T(2,128)S(1)}, u32[]{:S(2)}, u32[]{:S(2)}) collective-permute-start(f32[2,2304]{1,0:T(2,128)S(1)} %pad_maximum_fusion.8), channel_id=1, source_target_pairs={{1,0},{2,1},{3,2},{5,4},{6,5},{7,6},{9,8},{10,9},{11,10},{13,12},{... | collective-permute-start | bytes 55304 | tf_op jit(solution)/shard_map/ppermute | solution.py:19
  732.8 11.7 %slice-start = ((s8[9510912]{0:T(1024)(128)(4,1)}), s8[4194304]{0:T(1024)(128)(4,1)S(1)}, s32[]{:S(2)}) async-start(s8[9510912]{0:T(1024)(128)(4,1)} %bitcast.101), calls=%async_computation.1 | async-start | bytes 8388608
  732.8 11.7 %slice-start.1 = ((s8[9510912]{0:T(1024)(128)(4,1)}), s8[4194304]{0:T(1024)(128)(4,1)S(1)}, s32[]{:S(2)}) async-start(s8[9510912]{0:T(1024)(128)(4,1)} %bitcast.101), calls=%async_computation.2 | async-start | bytes 8388608
  743.1 15.1 %copy-start.9 = (bf16[1024,768]{0,1:T(8,128)(2,1)S(1)}, bf16[1024,768]{0,1:T(8,128)(2,1)}, u32[]{:S(2)}) copy-start(bf16[1024,768]{0,1:T(8,128)(2,1)} %copy-done.7) | copy-start | bytes 4718596
  743.1 15.1 %copy-start.40 = (f32[768]{0:T(1024)S(1)}, f32[768]{0:T(1024)}, u32[]{:S(2)}) copy-start(f32[768]{0:T(1024)} %copy-done.39) | copy-start | bytes 9220
  743.1 15.1 %copy-start.42 = (f32[1024]{0:T(1024)S(1)}, f32[1024]{0:T(1024)}, u32[]{:S(2)}) copy-start(f32[1024]{0:T(1024)} %copy-done.41) | copy-start | bytes 12292
  758.2 9.3 copy-start.17
  785.8 12.2 %slice-start.10 = ((s8[9437184]{0:T(1024)(128)(4,1)}), s8[1048576]{0:T(1024)(128)(4,1)S(1)}, s32[]{:S(2)}) async-start(s8[9437184]{0:T(1024)(128)(4,1)} %bitcast.111), calls=%async_computation.11 | async-start | bytes 2097152
  787.4 7.4 copy-start.13
  787.4 9.0 copy-start.12
  787.4 10.6 slice-start.11
  798.7 6.1 slice-start.8
  798.7 6.3 slice-start.9
  814.1 320.2 %copy-start.10 = (bf16[1024,768]{0,1:T(8,128)(2,1)S(1)}, bf16[1024,768]{0,1:T(8,128)(2,1)}, u32[]{:S(2)}) copy-start(bf16[1024,768]{0,1:T(8,128)(2,1)} %copy-done.7) | copy-start | bytes 4718596
  1118.3 24.9 %collective-permute-start.4 = (f32[403,128]{1,0:T(8,128)}, f32[403,128]{1,0:T(8,128)}, u32[]{:S(2)}, u32[]{:S(2)}) collective-permute-start(f32[403,128]{1,0:T(8,128)} %slice.268), channel_id=1, source_target_pairs={{0,1},{1,2},{2,3},{3,4},{4,5},{5,6},{6,7},{7,8},{8,9},{9,10},{10,1... | collective-permute-start | bytes 619016
  (26 other events, 97.5 us)
Sparse Core Ops, SparseCore 0:
  11.5 106.2 all-gather.2
where the time goes:
time: 1170 us; the launch traced here: 1160 us
  matrix products  353 us (30%)
  blocking collectives  303 us (26%)
  other arithmetic  197 us (17%)
  local copies, waits for them, and re-layouts  164 us (14%)
  waiting for transfers between devices  96.7 us (8%)
  starting transfers between devices  26.1 us (2%)
  between operations  15.9 us (1%)
    unnamed x1, blocking collectives  303 us
    all_gather x1, waiting for transfers between devices, shards(): gathered = lax.all_gather(shard_low, ('dp', 'ctx'), axis=0, tiled=True)  95.3 us
    convert_element_type x2, other arithmetic, shards(): grad_scores = (probs_full * (grad_probs - inner_sum)).astype(jnp.bfloat16)  81.2 us
    dot_general x2, matrix products, shards(): jnp.einsum('qhd,khd->hqk', grad_heads[rows_part], value_heads, preferred_...  74.3 us
    unnamed x155, local copies, waits for them, and re-layouts  65 us
    dot_general x2, matrix products, shards(): jnp.einsum('hqk,qhd->khd', probs_low, grad_heads[rows_part], preferred_el...  48.3 us
    reduce_sum x2, other arithmetic, shards(): total_sum = jnp.sum(raised, axis=-1, keepdims=True)  45.8 us
    dot_general x2, matrix products, shards(): jnp.einsum('hqk,khd->qhd', probs_low, value_heads, preferred_element_type...  44.1 us
  transfers between devices with their start and end apart: 6, of which 2 were waited for; matrix products, arithmetic and copies ran while one was open for 8% of the time, Pallas kernels for 0%

commit v1 on v0

v1 whole, which is shorter than its diff:
```python
import jax
import jax.numpy as jnp
from jax import lax
from jax.experimental import pallas as pl
from jax.experimental.pallas import tpu as pltpu
from jax.sharding import PartitionSpec as P

D = 768
HEADS = 12
HEAD_DIM = 64
FF = 3072
SEQ_MIN = 1024
AXES = ("dp", "ctx")
QB = 256
F32 = jnp.float32
BF = jnp.bfloat16
NT = (((1,), (1,)), ((), ()))
TN = (((0,), (0,)), ((), ()))
norm_eps = 1e-06
VMEM_LIMIT = 56 << 20


def dot(left, right):
    return jnp.dot(left, right, preferred_element_type=F32)


def dot_nt(left, right):
    return lax.dot_general(left, right, NT, preferred_element_type=F32)


def dot_tn(left, right):
    return lax.dot_general(left, right, TN, preferred_element_type=F32)


def cost(flops, nbytes, exps=0):
    return pl.CostEstimate(flops=int(flops), bytes_accessed=int(nbytes), transcendentals=int(exps))


def conv(x, taps, mask_one, mask_two):
    one = pltpu.roll(x, 1, 0) * mask_one
    two = pltpu.roll(x, 2, 0) * mask_two
    return (taps[0:1] * x + taps[1:2] * one + taps[2:3] * two).astype(BF)


def att_fwd_kernel(
    state_ref, tail_ref, q_ref, k_ref, v_ref, tq_ref, tk_ref, tv_ref, one_ref, two_ref,
    o_ref, l_ref, qm_ref, km_ref, vm_ref,
):
    rows = q_ref.shape[0]
    lane = lax.broadcasted_iota(jnp.int32, (1, 128), 1)
    state = state_ref[0]
    second = state == 2
    empty = state == 0
    one = one_ref[...]
    two = two_ref[...]
    x = jnp.concatenate([tail_ref[...].astype(F32), q_ref[...].astype(F32)], 0)
    qm_ref[...] = conv(x, tq_ref[...], one[rows - 8 :], two[rows - 8 :])[8:]
    km_ref[...] = conv(k_ref[...].astype(F32), tk_ref[...], one, two)
    vm_ref[...] = conv(v_ref[...].astype(F32), tv_ref[...], one, two)
    for i in range(rows // QB):
        rs = pl.ds(i * QB, QB)
        outs = []
        sums = []
        qf = qm_ref[rs, :].astype(F32) * 0.125
        for h in range(2):
            mine = (lane < 64) if h == 0 else (lane >= 64)
            qh = jnp.where(mine, qf, 0.0).astype(BF)
            nk = (i + 1) * QB
            vh = jnp.where(mine, vm_ref[rows : rows + nk, :], jnp.ones((), BF))
            s = dot_nt(qh, km_ref[rows : rows + nk, :])
            r = lax.broadcasted_iota(jnp.int32, (QB, QB), 0)
            c = lax.broadcasted_iota(jnp.int32, (QB, QB), 1)
            sd = jnp.where(c <= r, s[:, i * QB :], -1e30)
            m = jnp.max(sd, axis=1, keepdims=True)
            if i > 0:
                m = jnp.maximum(m, jnp.max(s[:, : i * QB], axis=1, keepdims=True))
            o = dot(jnp.exp(sd - m).astype(BF), vh[i * QB :])
            if i > 0:
                o = o + dot(jnp.exp(s[:, : i * QB] - m).astype(BF), vh[: i * QB])

            def prev(args):
                o1, m1 = args
                s2 = dot_nt(qh, km_ref[0:rows, :])
                m2 = jnp.maximum(m1, jnp.max(s2, axis=1, keepdims=True))
                p2 = jnp.exp(s2 - m2).astype(BF)
                vph = jnp.where(mine, vm_ref[0:rows, :], jnp.ones((), BF))
                return o1 * jnp.exp(m1 - m2) + dot(p2, vph), m2

            o, m = lax.cond(second, prev, lambda a: a, (o, m))
            outs.append(o / pltpu.roll(o, 64, 1))
            sums.append(m + jnp.log(o))
        res = jnp.where(lane < 64, outs[0], outs[1])
        res = jnp.where(empty, vm_ref[pl.ds(rows + i * QB, QB), :].astype(F32), res)
        o_ref[rs, :] = res.astype(BF)
        l_ref[rs, :] = jnp.where(lane < 64, sums[1], sums[0])


def att_fwd(state, projected, taps, one, two, rows):
    def cols(height, row, off):
        return pl.BlockSpec((height, 128), lambda p: (row, p + off))

    full = pl.BlockSpec((2 * rows, 128), lambda p: (0, 0))
    taps_at = [pl.BlockSpec((3, 128), lambda p, off=off: (0, p + off)) for off in (0, 6, 12)]
    return pl.pallas_call(
        att_fwd_kernel,
        grid=(6,),
        in_specs=[
            pl.BlockSpec(memory_space=pltpu.SMEM),
            cols(8, rows // 8 - 1, 0),
            cols(rows, 1, 0),
            cols(2 * rows, 0, 6),
            cols(2 * rows, 0, 12),
            *taps_at,
            full,
            full,
        ],
        out_specs=[cols(rows, 0, 0)] * 3 + [cols(2 * rows, 0, 0)] * 2,
        out_shape=[
            jax.ShapeDtypeStruct((rows, D), BF),
            jax.ShapeDtypeStruct((rows, D), F32),
            jax.ShapeDtypeStruct((rows, D), BF),
            jax.ShapeDtypeStruct((2 * rows, D), BF),
            jax.ShapeDtypeStruct((2 * rows, D), BF),
        ],
        compiler_params=pltpu.CompilerParams(vmem_limit_bytes=VMEM_LIMIT),
        cost_estimate=cost(2 * 2 * 12 * rows * rows * 1.5 * 256, rows * D * 30, 12 * rows * rows * 1.5),
        name="att_fwd",
    )(state, projected, projected, projected, projected, taps, taps, taps, one, two)


def three(x, lane, base):
    hi = x.astype(BF).astype(F32)
    r = x - hi
    mid = r.astype(BF).astype(F32)
    lo = r - mid
    return jnp.where(
        lane == base, hi, jnp.where(lane == base + 1, mid, jnp.where(lane == base + 2, lo, 0.0))
    )


def conv_back(grad, x, taps, mask_one, mask_two):
    height = grad.shape[0]
    one = pltpu.roll(grad, height - 1, 0) * mask_one
    two = pltpu.roll(grad, height - 2, 0) * mask_two
    back = (taps[0:1] * grad + taps[1:2] * one + taps[2:3] * two).astype(BF)
    sums = [jnp.sum(g * x, axis=0, keepdims=True) for g in (grad, one, two)]
    return back, sums


def att_bwd_kernel(
    state_ref, q_ref, k_ref, v_ref, o_ref, l_ref, do_ref, xt_ref, xq_ref, xk_ref, xv_ref,
    tq_ref, tk_ref, tv_ref, one_ref, two_ref,
    pq_ref, pt_ref, pk_ref, pv_ref, tg_ref, qa, da, dqs, dks, dvs,
):
    rows = q_ref.shape[0]
    lane = lax.broadcasted_iota(jnp.int32, (1, 128), 1)
    second = state_ref[0] == 2
    do = do_ref[...].astype(F32)
    od = do * o_ref[...].astype(F32)
    qf = q_ref[...].astype(F32) * 0.125
    lv = l_ref[...]
    zero = jnp.zeros((), BF)
    dks[...] = jnp.zeros(dks.shape, F32)
    dvs[...] = jnp.zeros(dvs.shape, F32)
    dqs[...] = jnp.zeros(dqs.shape, F32)
    for h in range(2):
        mine = (lane < 64) if h == 0 else (lane >= 64)
        base = 64 if h == 0 else 0
        ones3 = ((lane >= base) & (lane < base + 3)).astype(BF)
        delta = jnp.sum(jnp.where(mine, od, 0.0), axis=1, keepdims=True)
        qa[...] = jnp.where(mine, qf, three(-lv, lane, base)).astype(BF)
        da[...] = jnp.where(mine, do, three(-delta, lane, base)).astype(BF)

        def part(ks, qs, dos, mask):
            kk = k_ref[ks, :]
            st = dot_nt(jnp.where(mine, kk, ones3), qs)
            dp = dot_nt(jnp.where(mine, v_ref[ks, :], ones3), dos)
            p = jnp.exp(st)
            if mask is not None:
                p = jnp.where(mask, p, 0.0)
            ds = (p * dp).astype(BF)
            dvs[ks, :] += dot(p.astype(BF), jnp.where(mine, dos, zero))
            dks[ks, :] += dot(ds, jnp.where(mine, qs, zero))
            return dot_tn(ds, jnp.where(mine, kk, zero))

        for i in range(rows // QB):
            qs = qa[pl.ds(i * QB, QB), :]
            dos = da[pl.ds(i * QB, QB), :]
            kr = lax.broadcasted_iota(jnp.int32, (QB, QB), 0)
            qr = lax.broadcasted_iota(jnp.int32, (QB, QB), 1)
            dq = part(pl.ds(rows + i * QB, QB), qs, dos, kr <= qr)
            if i > 0:
                dq = dq + part(pl.ds(rows, i * QB), qs, dos, None)
            dqs[pl.ds(8 + i * QB, QB), :] += dq * 0.125

        @pl.when(second)
        def _():
            for i in range(rows // QB):
                rs = pl.ds(i * QB, QB)
                dq = part(pl.ds(0, rows), qa[rs, :], da[rs, :], None)
                dqs[pl.ds(8 + i * QB, QB), :] += dq * 0.125

    one = one_ref[...]
    two = two_ref[...]
    xq = jnp.concatenate([xt_ref[...].astype(F32), xq_ref[...].astype(F32)], 0)
    pq, sq = conv_back(dqs[...], xq, tq_ref[...], one[rows - 8 :], two[rows - 8 :])
    pt_ref[...] = pq[:8]
    pq_ref[...] = pq[8:]
    pk_ref[...], sk = conv_back(dks[...], xk_ref[...].astype(F32), tk_ref[...], one, two)
    pv_ref[...], sv = conv_back(dvs[...], xv_ref[...].astype(F32), tv_ref[...], one, two)
    tg_ref[...] = jnp.zeros(tg_ref.shape, F32)
    for j in range(3):
        for m, s in enumerate((sq, sk, sv)):
            tg_ref[3 * j + m : 3 * j + m + 1, :] = s[j]


def att_bwd(state, mixed, attended, logs, grad, projected, taps, one, two, rows):
    def cols(height, row, off):
        return pl.BlockSpec((height, 128), lambda p: (row, p + off))

    full = pl.BlockSpec((2 * rows, 128), lambda p: (0, 0))
    taps_at = [pl.BlockSpec((3, 128), lambda p, off=off: (0, p + off)) for off in (0, 6, 12)]
    own = cols(rows, 0, 0)
    both = cols(2 * rows, 0, 0)
    return pl.pallas_call(
        att_bwd_kernel,
        grid=(6,),
        in_specs=[
            pl.BlockSpec(memory_space=pltpu.SMEM),
            own, both, both, own, own, own,
            cols(8, rows // 8 - 1, 0),
            cols(rows, 1, 0),
            cols(2 * rows, 0, 6),
            cols(2 * rows, 0, 12),
            *taps_at,
            full,
            full,
        ],
        out_specs=[own, cols(8, 0, 0), both, both, cols(16, 0, 0)],
        out_shape=[
            jax.ShapeDtypeStruct((rows, D), BF),
            jax.ShapeDtypeStruct((8, D), BF),
            jax.ShapeDtypeStruct((2 * rows, D), BF),
            jax.ShapeDtypeStruct((2 * rows, D), BF),
            jax.ShapeDtypeStruct((16, D), F32),
        ],
        scratch_shapes=[
            pltpu.VMEM((rows, 128), BF),
            pltpu.VMEM((rows, 128), BF),
            pltpu.VMEM((rows + 8, 128), F32),
            pltpu.VMEM((2 * rows, 128), F32),
            pltpu.VMEM((2 * rows, 128), F32),
        ],
        compiler_params=pltpu.CompilerParams(vmem_limit_bytes=VMEM_LIMIT),
        cost_estimate=cost(5 * 2 * 12 * rows * rows * 1.5 * 256, rows * D * 40, 12 * rows * rows * 1.5),
        name="att_bwd",
    )(state, *mixed, attended, logs, grad, projected, projected, projected, projected,
      taps, taps, taps, one, two)


def qkv_bwd_kernel(
    core_ref, x_ref, dq_ref, dt_ref, dk_ref, dv_ref, w_ref, gain_ref, gain_two_ref, tg_ref,
    *refs, pieces, blocks,
):
    if pieces:
        send_ref, keep_ref, prev_ref, own_ref, acc, gacc = refs
    else:
        keep_ref, small_ref, prev_ref, own_ref, acc, gacc = refs
    i = pl.program_id(0)
    half = blocks // 2

    @pl.when(i == 0)
    def _():
        acc[...] = jnp.zeros(acc.shape, F32)
        gacc[...] = jnp.zeros(gacc.shape, F32)

    x = x_ref[...].astype(F32)
    hat = x * lax.rsqrt(jnp.mean(x * x, axis=-1, keepdims=True) + norm_eps)
    low = (hat * gain_ref[...]).astype(BF)
    dk = dk_ref[...]
    dv = dv_ref[...]
    gn = dot_nt(dk, w_ref[D : 2 * D, :]) + dot_nt(dv, w_ref[2 * D : 3 * D, :])
    acc[D : 2 * D, :] += dot_tn(low, dk)
    acc[2 * D : 3 * D, :] += dot_tn(low, dv)

    @pl.when(i < half - 1)
    def _():
        prev_ref[...] = gn.astype(BF)
        gacc[0:1, :] += jnp.sum(gn * hat, axis=0, keepdims=True)

    @pl.when(i == half - 1)
    def _():
        dt = dt_ref[...]
        last = gn.shape[0] - 8
        acc[0:D, :] += dot_tn(low[last:], dt)
        full = jnp.concatenate([gn[:last], gn[last:] + dot_nt(dt, w_ref[0:D, :])], 0)
        prev_ref[...] = full.astype(BF)
        gacc[0:1, :] += jnp.sum(full * hat, axis=0, keepdims=True)

    @pl.when(i >= half)
    def _():
        dq = dq_ref[...]
        acc[0:D, :] += dot_tn(low, dq)
        full = gn + dot_nt(dq, w_ref[0:D, :])
        own_ref[...] = full
        gacc[0:1, :] += jnp.sum(full * hat, axis=0, keepdims=True)

    @pl.when(i == blocks - 1)
    def _():
        small = jnp.concatenate(
            [gacc[0:1, :], gain_two_ref[...], tg_ref[0:9, :], jnp.zeros((5, D), F32)], 0
        )
        if pieces:
            core = core_ref[0]
            height = 3 * D // (2 * pieces)
            for j in range(pieces):
                to = pl.ds(j * height, height)
                away = pl.ds(pl.multiple_of((2 * j + 1 - core) * height, 16), height)
                here = pl.ds(pl.multiple_of((2 * j + core) * height, 16), height)
                send_ref[to, :] = acc[away, :].astype(BF)
                keep_ref[to, :] = acc[here, :]
            send_ref[pieces * height :, :] = small.astype(BF)
            keep_ref[pieces * height :, :] = small
        else:
            keep_ref[...] = acc[...].astype(BF)
            small_ref[...] = small


def qkv_bwd(core, x_both, back, wide, gain, gain_two_grad, tap_grads, rows, pieces):
    dq, dt, dk, dv = back
    blocks = 4
    half = blocks // 2
    height = 2 * rows // blocks
    step = pl.BlockSpec((height, D), lambda i: (i, 0))
    late = pl.BlockSpec((height, D), lambda i: (jnp.maximum(i - half, 0), 0))
    early = pl.BlockSpec((height, D), lambda i: (jnp.minimum(i, half - 1), 0))

    def whole(shape):
        return pl.BlockSpec(shape, lambda i: (0, 0))

    if pieces:
        packed = 3 * D // 2 + 16
        outs = [jax.ShapeDtypeStruct((packed, D), BF), jax.ShapeDtypeStruct((packed, D), F32)]
        out_at = [whole((packed, D))] * 2
    else:
        outs = [jax.ShapeDtypeStruct((3 * D, D), BF), jax.ShapeDtypeStruct((16, D), F32)]
        out_at = [whole((3 * D, D)), whole((16, D))]

    def body(*refs):
        qkv_bwd_kernel(*refs, pieces=pieces, blocks=blocks)

    return pl.pallas_call(
        body,
        grid=(blocks,),
        in_specs=[
            pl.BlockSpec(memory_space=pltpu.SMEM),
            step, late, whole((8, D)), step, step, whole((3 * D, D)),
            whole((1, D)), whole((1, D)), whole((16, D)),
        ],
        out_specs=out_at + [early, late],
        out_shape=outs
        + [jax.ShapeDtypeStruct((rows, D), BF), jax.ShapeDtypeStruct((rows, D), F32)],
        scratch_shapes=[pltpu.VMEM((3 * D, D), F32), pltpu.VMEM((8, D), F32)],
        compiler_params=pltpu.CompilerParams(vmem_limit_bytes=VMEM_LIMIT),
        cost_estimate=cost(2 * 2 * D * D * 5 * rows, rows * D * 30),
        name="qkv_bwd",
    )(core, x_both, dq, dt, dk, dv, wide, gain, gain_two_grad, tap_grads)


def merge(index, keep, got, height, taken):
    rows = keep.shape[0]
    out_rows = taken * height + 16 if taken else rows

    def body(index_ref, keep_ref, got_ref, send_ref, stay_ref):
        if not taken:
            total = keep_ref[...] + got_ref[...].astype(F32)
            send_ref[...] = total.astype(BF)
            stay_ref[...] = total
            return
        for j in range(taken):
            to = pl.ds(j * height, height)
            away = pl.ds(pl.multiple_of(index_ref[j] * height, 16), height)
            here = pl.ds(pl.multiple_of(index_ref[taken + j] * height, 16), height)
            send_ref[to, :] = (keep_ref[away, :] + got_ref[away, :].astype(F32)).astype(BF)
            stay_ref[to, :] = keep_ref[here, :] + got_ref[here, :].astype(F32)
        end = keep_ref[rows - 16 :, :] + got_ref[rows - 16 :, :].astype(F32)
        send_ref[taken * height :, :] = end.astype(BF)
        stay_ref[taken * height :, :] = end

    vmem = pl.BlockSpec(memory_space=pltpu.VMEM)
    return pl.pallas_call(
        body,
        in_specs=[pl.BlockSpec(memory_space=pltpu.SMEM), vmem, vmem],
        out_specs=[vmem, vmem],
        out_shape=[
            jax.ShapeDtypeStruct((out_rows, D), BF),
            jax.ShapeDtypeStruct((out_rows, D), F32),
        ],
        compiler_params=pltpu.CompilerParams(vmem_limit_bytes=32 << 20),
        cost_estimate=cost(rows * D, rows * D * 12),
        name="merge",
    )(index, keep, got)


def shift_flat(block, distance):
    count = lax.axis_size(AXES)
    route = [(i - distance, i) for i in range(count) if 0 <= i - distance < count]
    return lax.ppermute(block, AXES, route)


def shift_ctx(block, distance):
    count = lax.axis_size("ctx")
    route = [(i - distance, i) for i in range(count) if 0 <= i - distance < count]
    return lax.ppermute(block, "ctx", route)


def swap(block, even_bit, odd_bit):
    count = lax.axis_size(AXES)
    route = [(i, i ^ (odd_bit if i & 1 else even_bit)) for i in range(count)]
    return lax.ppermute(block, AXES, route)


def to_aligned(shard, place, count, delta):
    rows = shard.shape[0]
    lag = delta * (count - 1)
    back = -(-lag // rows)
    if back == 1:
        keep = -(-lag // 8) * 8
        parts = [shift_flat(shard[rows - keep :], 1), shard]
    else:
        keep = back * rows
        parts = [shift_flat(shard, s) for s in range(back, 0, -1)] + [shard]
    joined = jnp.concatenate(parts, 0)
    return lax.dynamic_slice_in_dim(joined, keep - delta * place, rows - delta, 0)


def small_part(shard, place, count, delta):
    rows = shard.shape[0]
    extra = count * delta
    zeros = jnp.zeros((extra, 128), shard.dtype)
    joined = jnp.concatenate([zeros, shard, zeros], 0)
    start = extra + count * (rows - delta) - place * rows
    return lax.dynamic_slice_in_dim(joined, jnp.minimum(start, rows + extra), extra, 0)


def from_aligned(chunk, small, place, count, delta, rows):
    aligned = rows - delta
    ahead = -(-(count * delta) // aligned)
    parts = [chunk]
    if ahead == 1:
        keep = small.shape[0]
        got = shift_flat(chunk[:keep], -1)
        parts.append(jnp.where(place == count - 1, small, got))
    else:
        pad = ahead * aligned - small.shape[0]
        tail = jnp.concatenate([small, jnp.zeros((pad, 128), small.dtype)], 0)
        for s in range(1, ahead + 1):
            got = shift_flat(chunk, -s)
            for e in range(s):
                piece = tail[e * aligned : (e + 1) * aligned]
                got = jnp.where(place == count - s + e, piece, got)
            parts.append(got)
    return lax.dynamic_slice_in_dim(jnp.concatenate(parts, 0), delta * place, rows, 0)


def normalize(values, gain):
    factor = lax.rsqrt(jnp.mean(values * values, axis=-1, keepdims=True) + norm_eps)
    scaled = values * factor
    return (scaled, factor, scaled * gain)


def norm_back(grad_in, scaled, factor, gain):
    weighted = grad_in * gain
    inner_mean = jnp.mean(weighted * scaled, axis=-1, keepdims=True)
    return factor * (weighted - scaled * inner_mean)


def adam_update(master, moment_one, moment_two, gradient, step_count, row_start):
    row_index = row_start + jnp.arange(master.shape[0], dtype=jnp.int32)
    matrix_rows = (4 * D * D + 2 * D * FF) // 128
    out_first = 3 * D * D // 128
    out_last = 4 * D * D // 128
    is_matrix = (row_index < matrix_rows)[:, None]
    is_out = ((row_index >= out_first) & (row_index < out_last))[:, None]
    step_rate = jnp.where(is_matrix, jnp.where(is_out, 0.5, 0.1), 1.0)
    decay_rate = jnp.where(is_matrix, 0.1, 0.0)
    step_value = step_count[0].astype(jnp.float32)
    new_one = 0.9 * moment_one + 0.1 * gradient
    new_two = 0.999 * moment_two + 0.001 * gradient * gradient
    corr_first = 1.0 - jnp.power(0.9, step_value)
    corr_second = 1.0 - jnp.power(0.999, step_value)
    new_weights = master - step_rate * (
        new_one / corr_first / (jnp.sqrt(new_two / corr_second) + 1e-08) + decay_rate * master
    )
    return (new_weights, new_one, new_two)


def shards(tokens, out_grad, positions, master, first_moment, second_moment, step_count):
    rows = tokens.shape[0]
    assert rows == SEQ_MIN
    count = lax.axis_size(AXES)
    place = lax.axis_index(AXES).astype(jnp.int32)
    owned = master.shape[0]
    aligned = (4 * D * D + 2 * D * FF) // 128 // count
    delta = owned - aligned
    height = aligned * 128 // D
    staged = count == 32
    first_place = positions[0]
    state = jnp.where(first_place < 0, 0, jnp.where(first_place >= SEQ_MIN, 2, 1)).astype(jnp.int32)
    state_vec = state[None]

    tokens_before = shift_ctx(tokens, 1)
    chunk = to_aligned(master, place, count, delta).reshape(-1, D).astype(BF)
    wide = lax.all_gather(chunk, AXES, axis=0, tiled=True)
    small = lax.psum(lax.reduce_precision(small_part(master, place, count, delta), 8, 7), AXES)
    small = small.reshape(-1)
    gain_first = small[:D]
    gain_second = small[D : 2 * D]
    taps = small[2 * D : 11 * D].reshape(3, 3 * D)
    in_weight = jnp.concatenate([wide[:D], wide[D : 2 * D], wide[2 * D : 3 * D]], 1)
    out_weight = wide[3 * D : 4 * D]
    up_weight = wide[4 * D : 8 * D].reshape(D, FF)
    down_weight = wide[8 * D : 12 * D]

    tokens_both = jnp.concatenate([tokens_before, tokens], 0)
    inputs_both = tokens_both.astype(F32)
    normed_low = normalize(inputs_both, gain_first)[2].astype(BF)
    projected = dot(normed_low, in_weight).astype(BF)

    def masks(row_id):
        own_one = (state == 2) | ((state == 1) & (row_id > rows))
        own_two = (state == 2) | ((state == 1) & (row_id > rows + 1))
        one = jnp.where(row_id < rows, row_id >= 1, own_one) & (row_id < 2 * rows)
        two = jnp.where(row_id < rows, row_id >= 2, own_two) & (row_id < 2 * rows)
        return one.astype(F32), two.astype(F32)

    row_id = lax.broadcasted_iota(jnp.int32, (2 * rows, 128), 0)
    after_one, after_two = masks(row_id)
    ahead_one = masks(row_id + 1)[0]
    ahead_two = masks(row_id + 2)[1]
    attn_low, logs, *mixed = att_fwd(state_vec, projected, taps, after_one, after_two, rows)

    inputs = tokens.astype(F32)
    hidden = inputs + dot(attn_low, out_weight)
    scaled_two, factor_two, normed_two = normalize(hidden, gain_second)
    second_low = normed_two.astype(BF)
    active = jnp.maximum(dot(second_low, up_weight), 0.0)
    squared_low = (active * active).astype(BF)
    layer_out = (hidden + dot(squared_low, down_weight)).astype(BF)

    grad_low = jnp.where(state > 0, out_grad, jnp.zeros((), BF))
    grad_out = grad_low.astype(F32)
    grad_down = dot_tn(squared_low, grad_low)
    grad_before = (dot_nt(grad_low, down_weight) * 2.0 * active).astype(BF)
    grad_up = dot_tn(second_low, grad_before)
    grad_normed_two = dot_nt(grad_before, up_weight)
    grad_gain_two = jnp.sum(grad_normed_two * scaled_two, axis=0)
    grad_hidden = grad_out + norm_back(grad_normed_two, scaled_two, factor_two, gain_second)
    hidden_low = grad_hidden.astype(BF)
    grad_outw = dot_tn(attn_low, hidden_low)
    grad_attended = dot_nt(hidden_low, out_weight).astype(BF)

    if staged:
        late_grad = jnp.concatenate(
            [
                jnp.zeros((3 * D, D), BF),
                grad_outw.astype(BF),
                grad_up.astype(BF).reshape(-1, D),
                grad_down.astype(BF),
            ],
            0,
        )
        late_chunk = lax.psum_scatter(late_grad, AXES, scatter_dimension=0, tiled=True)

    *back, tap_grads = att_bwd(
        state_vec, mixed, attn_low, logs, grad_attended, projected, taps, ahead_one, ahead_two, rows
    )
    core = (place & 1)[None]
    sums = qkv_bwd(
        core, tokens_both, back, wide, gain_first[None], grad_gain_two[None], tap_grads, rows,
        4 if staged else 0,
    )
    grads_before, grad_normed_one = sums[2:]
    from_next = shift_ctx(grads_before, -1)
    scaled_one, factor_one, _ = normalize(inputs, gain_first)
    input_grad = grad_hidden + norm_back(
        grad_normed_one + from_next.astype(F32), scaled_one, factor_one, gain_first
    )

    if staged:
        send, keep = sums[:2]
        x_bit = (place >> 1) & 1
        y_bit = (place >> 2) & 1
        got = swap(send, 1, 1)
        even = (place & 1) == 0
        stay = [jnp.where(even, 2 * j + x_bit, 2 * y_bit + j) for j in range(2)]
        away = [jnp.where(even, 2 * j + 1 - x_bit, 2 * (1 - y_bit) + j) for j in range(2)]
        send, keep = merge(jnp.stack(away + stay), keep, got, height, 2)
        got = swap(send, 2, 4)
        other = jnp.where(even, y_bit, x_bit)
        send, keep = merge(jnp.stack([1 - other, other]), keep, got, height, 1)
        got = swap(send, 4, 2)
        send, keep = merge(core, keep, got, height, 0)
        got = swap(send, 8, 8)
        send, keep = merge(core, keep, got, height, 0)
        got = swap(send, 16, 16)
        first = keep + got.astype(F32)
        small_grad = first[height:].reshape(-1, 128)
        chunk_grad = jnp.where(place < count // 4, first[:height], late_chunk.astype(F32))
    else:
        wide_grad = jnp.concatenate(
            [
                sums[0],
                grad_outw.astype(BF),
                grad_up.astype(BF).reshape(-1, D),
                grad_down.astype(BF),
            ],
            0,
        )
        chunk_grad = lax.psum_scatter(wide_grad, AXES, scatter_dimension=0, tiled=True).astype(F32)
        used = sums[1].reshape(-1, 128)
        extra = count * delta
        small_grad = jnp.concatenate([used, jnp.zeros((extra - used.shape[0], 128), F32)], 0)
        small_grad = lax.psum(small_grad, AXES)
    gradient = from_aligned(chunk_grad.reshape(-1, 128), small_grad, place, count, delta, owned)
    new_weights, new_one, new_two = adam_update(
        master, first_moment, second_moment, gradient, step_count, place * owned
    )
    return (layer_out, input_grad, new_weights, new_one, new_two, new_weights.astype(BF))


def solution(mesh):
    spread = P(AXES, None)
    return jax.shard_map(
        shards,
        mesh=mesh,
        in_specs=(spread, spread, P(AXES), spread, spread, spread, P()),
        out_specs=(spread,) * 6,
        check_vma=False,
    )
```

time: 1170 us -> 541 us (0.46)
  matrix products: 353 us -> 74.2 us
  blocking collectives: 303 us -> 52.4 us
  other arithmetic: 197 us -> 55.2 us
  local copies, waits for them, and re-layouts: 164 us -> 49.1 us
  Pallas kernels: 0 us -> 113 us
  starting transfers between devices: 26.1 us -> 71.8 us
    unnamed x1 -> x0, blocking collectives: 303 us -> none
    dot_general x24 -> x10, matrix products: 353 us -> 74.2 us  [the longest x4 32.8 us: dot(): return jnp.dot(left, right, preferred_element_type=F32)]
    pallas_call x0 -> x7, Pallas kernels: none -> 113 us  [the longest x1 45.9 us: att_bwd(): pl.pallas_call(att_bwd_kernel, grid=(6,), in_specs=[pl.BlockSpec(memory_s...]
    convert_element_type x8 -> x4, other arithmetic: 93.8 us -> 5.71 us  [the longest x1 4.28 us: shards(): new_weights.astype(BF)]
    ppermute x4 -> x9, starting transfers between devices: 10 us -> 71.7 us  [the longest x5 60.7 us: swap(): return lax.ppermute(block, AXES, route)]
    reduce_sum x3 -> x1, other arithmetic: 59.4 us -> 2.45 us  [norm_back(): inner_mean = jnp.mean(weighted * scaled, axis=-1, keepdims=True)]
    ppermute x4 -> x9, waiting for transfers between devices: 1.42 us -> 57.7 us  [the longest x5 56.9 us: swap(): return lax.ppermute(block, AXES, route)]
    all_gather x1, waiting for transfers between devices: 95.3 us -> 42.3 us  [shards(): wide = lax.all_gather(chunk, AXES, axis=0, tiled=True)]
  transfers between devices with their start and end apart: 6 -> 11, of which waited for: 2 -> 7; matrix products, arithmetic and copies ran while one was open for 8% -> 6% of each run, Pallas kernels for 0% -> 13%
where the time goes in v1:
time: 541 us; the launch traced here: 532 us
  Pallas kernels  113 us (21%)
  waiting for transfers between devices  100 us (18%)
  matrix products  74.2 us (14%)
  starting transfers between devices  71.8 us (13%)
  other arithmetic  55.2 us (10%)
  blocking collectives  52.4 us (10%)
  local copies, waits for them, and re-layouts  49.1 us (9%)
  between operations  16.7 us (3%)
    ppermute x5, starting transfers between devices, swap(): return lax.ppermute(block, AXES, route)  60.7 us
    ppermute x5, waiting for transfers between devices, swap(): return lax.ppermute(block, AXES, route)  56.9 us
    psum x1, blocking collectives, shards(): lax.psum(lax.reduce_precision(small_part(master, place, count, delta), 8,...  52.4 us
    pallas_call x1, Pallas kernels, att_bwd(): pl.pallas_call(att_bwd_kernel, grid=(6,), in_specs=[pl.BlockSpec(memory_s...  45.9 us
    all_gather x1, waiting for transfers between devices, shards(): wide = lax.all_gather(chunk, AXES, axis=0, tiled=True)  42.3 us
    pallas_call x1, Pallas kernels, att_fwd(): pl.pallas_call(att_fwd_kernel, grid=(6,), in_specs=[pl.BlockSpec(memory_s...  42 us
    concatenate x1, other arithmetic, shards(): jnp.concatenate([jnp.zeros((3 * D, D), BF), grad_outw.astype(BF), grad_up...  32.9 us
    dot_general x4, matrix products, dot(): return jnp.dot(left, right, preferred_element_type=F32)  32.8 us
  transfers between devices with their start and end apart: 11, of which 7 were waited for; matrix products, arithmetic and copies ran while one was open for 6% of the time, Pallas kernels for 13%

profile of v1, /device:TPU:0, one launch (start us, length us, event | category | flops | bytes accessed | tf_op | source)
XLA Modules:
  0.0 532.5 jit_solution(3997646918057439990)
XLA Ops:
  8.1 2.3 collective-permute-start.1
  11.3 1.4 fusion.28
  13.9 5.9 %collective-permute-start = (bf16[1024,768]{1,0:T(8,128)(2,1)}, bf16[1024,768]{1,0:T(8,128)(2,1)}, u32[]{:S(2)}, u32[]{:S(2)}) collective-permute-start(bf16[1024,768]{1,0:T(8,128)(2,1)} %param.7), channel_id=1, source_target_pairs={{0,1},{1,2},{2,3},{4,5},{5,6},{6,7},{8,9},{9,10},{10,11},{12,13},{... | collective-permute-start | bytes 4718600 | tf_op jit(solution)/shard_map/ppermute | solution.py:414
  23.2 52.4 %psum.7 = f32[96,128]{1,0:T(8,128)S(1)} all-reduce(f32[96,128]{1,0:T(8,128)S(1)} %dynamic-slice_reduce-precision_fusion), channel_id=1, replica_groups=mesh['dp'=8,'ctx'=4] {'dp','ctx'}, use_global_device_ids=true, to_apply=%region_1.2 | all-reduce | flops 12288 | bytes 98304 | tf_op jit(solution)/shard_map/psum | solution.py:515
  76.4 2.0 constant_dynamic-update-slice_fusion.1
  78.5 1.7 copy-done.13
  80.8 42.3 %all-gather.2.cloned.1.call-done.refs_6_ = bf16[9216,768]{1,0:T(8,128)(2,1)} async-done(((bf16[288,768]{1,0:T(8,128)(2,1)}), bf16[9216,768]{1,0:T(8,128)(2,1)}) %all-gather.2.cloned.1.call-update) | async-done | bytes 14155792 | tf_op jit(solution)/shard_map/all_gather | solution.py:514
  123.2 4.8 slice.70
  128.0 8.5 %reshape.113 = bf16[768,3072]{1,0:T(8,128)(2,1)} reshape(bf16[3072,768]{1,0:T(8,128)(2,1)} %slice.70) | data formatting | bytes 9437184 | tf_op jit(solution)/shard_map/reshape | solution.py:522
  136.4 2.4 fusion.74
  139.4 10.1 %convolution_convert_fusion.tail_ref.q_ref.k_ref.v_ref.xt_ref.xq_ref.xk_ref.xv_ref = bf16[2048,2304]{1,0:T(8,128)(2,1)} fusion(bf16[768,768]{1,0:T(8,128)(2,1)S(1)} %get-tuple-element.57, bf16[768,768]{1,0:T(8,128)(2,1)S(1)} %get-tuple-element.58, bf16[768,768]{1,0:T(8,128)(2,1)S(1)} %get-tuple-element.56, bf16[2048,768]{1,0:T(8,128)(2,1)S(1)} %copy-done.14, ...), kind=kOutput, calls=%fused_computation.3 | convolution fusion | flops 7269384192 | bytes 16133120 | tf_op jit(solution)/shard_map/dot_general | solution.py:24
  149.5 1.3 iota.53.one_ref
  150.8 1.4 iota.56.two_ref
  152.2 42.0 %att_fwd.1 = (bf16[1024,768]{1,0:T(8,128)(2,1)}, f32[1024,768]{1,0:T(8,128)}, bf16[1024,768]{1,0:T(8,128)(2,1)}, bf16[2048,768]{1,0:T(8,128)(2,1)}, bf16[2048,768]{1,0:T(8,128)(2,1)}) custom-call(s32[1]{0:T(128)S(6)} %select_n.103.state_ref, bf16[2048,2304]{1,0:T(8,128)(2,1)} %convolution_convert_fusion.tail_ref.q_ref.k_ref.v_ref.xt_ref.xq_ref.xk_ref.xv_ref, ...), custom_call_target="tpu_custom_call" | custom-call | flops 19327352832 | bytes 23592960 | tf_op jit(solution)/shard_map/att_fwd/pallas_call | solution.py:104
  194.2 3.3 multiply_reduce_fusion.2
  197.5 8.3 %fusion.71 = f32[1024,3072]{1,0:T(8,128)} fusion(bf16[768,3072]{1,0:T(8,128)(2,1)S(1)} %bitcast.29, f32[1024,768]{1,0:T(8,128)S(1)} %get-tuple-element.63, f32[768]{0:T(1024)S(1)} %get-tuple-element.60, f32[1024]{0:T(1024)S(1)} %add_rsqrt_fusion.2), kind=kOutput, calls=%fused_computation.123 | convolution fusion | flops 4834197504 | bytes 20454400 | tf_op jit(solution)/shard_map/dot_general | solution.py:24
  205.8 12.1 %convolution_convert_fusion.1 = bf16[3072,768]{1,0:T(8,128)(2,1)} fusion(f32[1024,3072]{1,0:T(8,128)} %fusion.71, bf16[1024,768]{1,0:T(8,128)(2,1)S(1)} %copy-done.17, pred[]{:T(512)} %bitcast.4), kind=kOutput, calls=%fused_computation.9 | convolution fusion | flops 4844421120 | bytes 18874368 | tf_op jit(solution)/shard_map/dot_general | solution.py:32
  217.9 9.6 %multiply_convert_fusion = bf16[1024,3072]{1,0:T(8,128)(2,1)S(1)} fusion(f32[1024,3072]{1,0:T(8,128)} %fusion.71, bf16[9216,768]{1,0:T(8,128)(2,1)} %all-gather.2.cloned.1.call-done.refs_6_, bf16[1024,768]{1,0:T(8,128)(2,1)S(1)} %copy-done.17, pred[]{:T(512)} %bitcast.4), kind=kOutput, calls=%fused_computation.1 | convolution fusion | flops 4845207552 | bytes 25166336 | tf_op jit(solution)/shard_map/dot_general | solution.py:28
  227.5 7.0 %multiply_reduce_fusion = (f32[768]{0:T(1024)S(1)}, f32[1024]{0:T(1024)S(1)}, f32[1024,768]{1,0:T(8,128)}) fusion(f32[1024,768]{1,0:T(8,128)S(1)} %get-tuple-element.63, f32[1024]{0:T(1024)S(1)} %add_rsqrt_fusion.2, f32[768]{0:T(1024)S(1)} %get-tuple-element.60, bf16[1024,3072]{1,0:T(8,128)(2,1)S(1)} %multiply_convert_fusion, bf16[768,3072]{1,0:T(8,128)(2,1)S(1)} %bitcast.29), kind=kOutput, calls=%fused_computation.30 | convolution fusion | flops 4836554752 | bytes 17315840 | tf_op jit(solution)/shard_map/dot_general | solution.py:28
  234.5 7.4 %convolution_convert_fusion.2 = bf16[768,3072]{1,0:T(8,128)(2,1)} fusion(bf16[1024,3072]{1,0:T(8,128)(2,1)S(1)} %multiply_convert_fusion, f32[1024,768]{1,0:T(8,128)S(1)} %get-tuple-element.63, f32[768]{0:T(1024)S(1)} %get-tuple-element.60, f32[1024]{0:T(1024)S(1)} %add_rsqrt_fusion.2), kind=kOutput, calls=%fused_computation.10 | convolution fusion | flops 4836556800 | bytes 14162944 | tf_op jit(solution)/shard_map/dot_general | solution.py:32
  241.9 8.5 %reshape.114 = bf16[3072,768]{1,0:T(8,128)(2,1)} reshape(bf16[768,3072]{1,0:T(8,128)(2,1)} %convolution_convert_fusion.2) | data formatting | bytes 9437184 | tf_op jit(solution)/shard_map/reshape | solution.py:568
  250.3 4.2 multiply_add_fusion
  254.6 1.5 convolution_convert_fusion.4
  256.1 2.0 copy-done.8
  258.1 32.9 %pad_maximum_fusion = bf16[9216,768]{1,0:T(8,128)(2,1)} fusion(bf16[3072,768]{1,0:T(8,128)(2,1)} %convolution_convert_fusion.1, bf16[3072,768]{1,0:T(8,128)(2,1)S(1)} %copy-done.8, bf16[768,768]{1,0:T(8,128)(2,1)S(1)} %convolution_convert_fusion.4, bf16[9216]{0:T(1024)(128)(2,1)S(1)} %pad.2.clone), kind=kLoop, calls=%fused_computation | loop fusion | flops 56623104 | bytes 24791040 | tf_op jit(solution)/shard_map/concatenate | solution.py:564
  292.2 3.8 convolution_convert_fusion.3.do_ref
  296.0 1.3 iota.58.one_ref
  297.4 1.3 iota.60.two_ref
  298.7 45.9 %att_bwd.1 = (bf16[1024,768]{1,0:T(8,128)(2,1)}, bf16[8,768]{1,0:T(8,128)(2,1)}, bf16[2048,768]{1,0:T(8,128)(2,1)}, bf16[2048,768]{1,0:T(8,128)(2,1)}, f32[16,768]{1,0:T(8,128)}) custom-call(s32[1]{0:T(128)S(6)} %select_n.103.state_ref, bf16[1024,768]{1,0:T(8,128)(2,1)} %get-tuple-element.29.q_ref, bf16[2048,768]{1,0:T(8,128)(2,1)} %get-tuple-element.30.k_ref, ...), custom_call_target="tpu_custom_call" | custom-call | flops 48318382080 | bytes 31457280 | tf_op jit(solution)/shard_map/att_bwd/pallas_call | solution.py:225
  344.6 22.3 %qkv_bwd.1 = (bf16[1168,768]{1,0:T(8,128)(2,1)}, f32[1168,768]{1,0:T(8,128)}, bf16[1024,768]{1,0:T(8,128)(2,1)}, f32[1024,768]{1,0:T(8,128)}) custom-call(s32[1]{0:T(128)} %bitcast.5.refs_0_.index_ref, bf16[2048,768]{1,0:T(8,128)(2,1)} %copy-done.13, bf16[1024,768]{1,0:T(8,128)(2,1)} %get-tuple-element.33.refs_2_, bf16[8,768]{1,0:T(8,128)(2,1)} %get-tuple-element.34.refs_3_, ...), custom_call_target="tpu_custom_call" | custom-call | flops 12079595520 | bytes 23592960 | tf_op jit(solution)/shard_map/qkv_bwd/pallas_call | solution.py:352
  367.3 3.6 collective-permute-done.3.got_ref
  370.9 1.2 copy-done.1
  372.1 2.0 copy-done
  374.1 2.0 copy-done.2
  376.1 1.9 merge.4
  378.0 1.4 collective-permute-start.4
  379.5 19.4 %collective-permute-done.4.got_ref = bf16[592,768]{1,0:T(8,128)(2,1)S(1)} collective-permute-done((bf16[592,768]{1,0:T(8,128)(2,1)}, bf16[592,768]{1,0:T(8,128)(2,1)S(1)}, u32[]{:S(2)}, u32[]{:S(2)}) %collective-permute-start.4) | collective-permute-done | bytes 909344 | tf_op jit(solution)/shard_map/ppermute | solution.py:420
  401.7 57.6 %collective-permute-start.5 = (bf16[304,768]{1,0:T(8,128)(2,1)S(1)}, bf16[304,768]{1,0:T(8,128)(2,1)S(1)}, u32[]{:S(2)}, u32[]{:S(2)}) collective-permute-start(bf16[304,768]{1,0:T(8,128)(2,1)S(1)} %get-tuple-element.45), channel_id=1, source_target_pairs={{0,4},{1,3},{2,6},{3,1},{4,0},{5,7},{6,2},{7,5},{8,12},{9,11},{10,... | collective-permute-start | bytes 1400840 | tf_op jit(solution)/shard_map/ppermute | solution.py:420
  459.7 1.3 collective-permute-start.2
  462.4 3.5 collective-permute-done.5.got_ref
  466.8 11.2 %add_convert_fusion = bf16[1024,768]{1,0:T(8,128)(2,1)} fusion(f32[1024,768]{1,0:T(8,128)} %copy-done.16, bf16[9216,768]{1,0:T(8,128)(2,1)} %all-gather.2.cloned.1.call-done.refs_6_, f32[1024,3072]{1,0:T(8,128)} %fusion.71), kind=kOutput, calls=%fused_computation.33 | convolution fusion | flops 4842848256 | bytes 22020096 | tf_op jit(solution)/shard_map/dot_general | solution.py:24
  478.0 9.8 %collective-permute-done.6.got_ref = bf16[304,768]{1,0:T(8,128)(2,1)S(1)} collective-permute-done((bf16[304,768]{1,0:T(8,128)(2,1)S(1)}, bf16[304,768]{1,0:T(8,128)(2,1)S(1)}, u32[]{:S(2)}, u32[]{:S(2)}) %collective-permute-start.6) | collective-permute-done | bytes 466976 | tf_op jit(solution)/shard_map/ppermute | solution.py:420
  488.5 2.4 fusion.13
  491.6 20.6 %collective-permute-done.7 = bf16[304,768]{1,0:T(8,128)(2,1)S(1)} collective-permute-done((bf16[304,768]{1,0:T(8,128)(2,1)S(1)}, bf16[304,768]{1,0:T(8,128)(2,1)S(1)}, u32[]{:S(2)}, u32[]{:S(2)}) %collective-permute-start.7) | collective-permute-done | bytes 466976 | tf_op jit(solution)/shard_map/ppermute | solution.py:420
  512.3 1.4 slice_select_fusion
  513.8 1.4 collective-permute-start.8
  515.2 5.9 %fusion.16 = f32[1024,768]{1,0:T(8,128)} fusion(f32[1024,768]{1,0:T(8,128)} %copy-done.9, bf16[1024,768]{1,0:T(8,128)(2,1)S(1)} %copy-done.7, f32[1024,768]{1,0:T(8,128)} %get-tuple-element.38, bf16[1024,768]{1,0:T(8,128)(2,1)} %collective-permute-done.2, f32[1024]{0:T(1024)} %broadcast_multiply_fusion, f32[768]{0:T(1024)S(1)} %copy-done.19, ...), kind=kLoop, calls=%fused_computation.27 | loop fusion | flops 7077888 | bytes 12594176 | tf_op jit(solution)/shard_map/add | solution.py:586
  521.2 4.3 fusion.72
  (91 shorter events, 15.0 us)
Async XLA Ops:
  7.2 15.2 %copy-start.11 = (f32[1731,128]{1,0:T(8,128)S(1)}, f32[1731,128]{1,0:T(8,128)}, u32[]{:S(2)}) copy-start(f32[1731,128]{1,0:T(8,128)} %param.10) | copy-start | bytes 2658820
  7.2 116.0 %all-gather.2.cloned.1.call-start = ((), (), s32[]{:S(2)}) async-start(), calls=%async_computation.1 | async-start | bytes 14598144 | tf_op jit(solution)/shard_map/all_gather | solution.py:514
  8.1 3.2 collective-permute-start.1
  13.9 64.5 %copy-start.5 = (bf16[1024,768]{1,0:T(8,128)(2,1)S(1)}, bf16[1024,768]{1,0:T(8,128)(2,1)}, u32[]{:S(2)}) copy-start(bf16[1024,768]{1,0:T(8,128)(2,1)} %param.7) | copy-start | bytes 4718596
  13.9 498.4 %reduce-scatter.2.cloned.1.call-start = ((), (), s32[]{:S(2)}) async-start(), calls=%async_computation.2 | async-start | bytes 14598144 | tf_op jit(solution)/shard_map/reduce_scatter | solution.py:573
  13.9 62.4 %collective-permute-start = (bf16[1024,768]{1,0:T(8,128)(2,1)}, bf16[1024,768]{1,0:T(8,128)(2,1)}, u32[]{:S(2)}, u32[]{:S(2)}) collective-permute-start(bf16[1024,768]{1,0:T(8,128)(2,1)} %param.7), channel_id=1, source_target_pairs={{0,1},{1,2},{2,3},{4,5},{5,6},{6,7},{8,9},{9,10},{10,11},{12,13},{... | collective-permute-start | bytes 4718600 | tf_op jit(solution)/shard_map/ppermute | solution.py:414
  76.3 62.5 %copy-start.18 = (f32[768]{0:T(1024)}, f32[768]{0:T(1024)S(1)}, u32[]{:S(2)}) copy-start(f32[768]{0:T(1024)S(1)} %get-tuple-element.61) | copy-start | bytes 9220
  78.5 1.7 copy-start.13
  136.4 3.0 copy-start.14
  149.5 48.0 %slice-start = ((s8[4718592]{0:T(1024)(128)(4,1)}), s8[4194304]{0:T(1024)(128)(4,1)S(1)}, s32[]{:S(2)}) async-start(s8[4718592]{0:T(1024)(128)(4,1)} %bitcast.28), calls=%async_computation.3 | async-start | bytes 8388608
  152.2 45.3 %slice-start.1 = ((s8[4718592]{0:T(1024)(128)(4,1)}), s8[524288]{0:T(1024)(128)(4,1)S(1)}, s32[]{:S(2)}) async-start(s8[4718592]{0:T(1024)(128)(4,1)} %bitcast.28), calls=%async_computation.4 | async-start | bytes 1048576
  197.5 37.0 %copy-start.16 = (f32[1024,768]{1,0:T(8,128)}, f32[1024,768]{1,0:T(8,128)S(1)}, u32[]{:S(2)}) copy-start(f32[1024,768]{1,0:T(8,128)S(1)} %get-tuple-element.63) | copy-start | bytes 9437188
  197.5 8.3 %copy-start.17 = (bf16[1024,768]{1,0:T(8,128)(2,1)S(1)}, bf16[1024,768]{1,0:T(8,128)(2,1)}, u32[]{:S(2)}) copy-start(bf16[1024,768]{1,0:T(8,128)(2,1)} %param.8) | copy-start | bytes 4718596
  250.3 4.3 copy-start.20
  254.6 37.6 %copy-start.9 = (f32[1024,768]{1,0:T(8,128)}, f32[1024,768]{1,0:T(8,128)S(1)}, u32[]{:S(2)}) copy-start(f32[1024,768]{1,0:T(8,128)S(1)} %multiply_add_fusion) | copy-start | bytes 9437188
  254.6 3.5 copy-start.8
  366.9 3.9 collective-permute-start.3
  370.9 1.2 copy-start.1
  372.1 2.0 copy-start
  374.1 2.0 copy-start.2
  378.0 20.9 %collective-permute-start.4 = (bf16[592,768]{1,0:T(8,128)(2,1)}, bf16[592,768]{1,0:T(8,128)(2,1)S(1)}, u32[]{:S(2)}, u32[]{:S(2)}) collective-permute-start(bf16[592,768]{1,0:T(8,128)(2,1)} %get-tuple-element.43), channel_id=1, source_target_pairs={{0,2},{1,5},{2,0},{3,7},{4,6},{5,1},{6,4},{7,3},{8,10},{9,13},{10,... | collective-permute-start | bytes 2727944 | tf_op jit(solution)/shard_map/ppermute | solution.py:420
  398.9 0.9 copy-start.3
  399.8 1.2 copy-start.4
  401.0 58.4 %copy-start.6 = (bf16[1024,768]{1,0:T(8,128)(2,1)S(1)}, bf16[1024,768]{1,0:T(8,128)(2,1)}, u32[]{:S(2)}) copy-start(bf16[1024,768]{1,0:T(8,128)(2,1)} %param.7) | copy-start | bytes 4718596
  401.7 64.1 %collective-permute-start.5 = (bf16[304,768]{1,0:T(8,128)(2,1)S(1)}, bf16[304,768]{1,0:T(8,128)(2,1)S(1)}, u32[]{:S(2)}, u32[]{:S(2)}) collective-permute-start(bf16[304,768]{1,0:T(8,128)(2,1)S(1)} %get-tuple-element.45), channel_id=1, source_target_pairs={{0,4},{1,3},{2,6},{3,1},{4,0},{5,7},{6,2},{7,5},{8,12},{9,11},{10,... | collective-permute-start | bytes 1400840 | tf_op jit(solution)/shard_map/ppermute | solution.py:420
  459.7 28.8 %collective-permute-start.2 = (bf16[1024,768]{1,0:T(8,128)(2,1)}, bf16[1024,768]{1,0:T(8,128)(2,1)}, u32[]{:S(2)}, u32[]{:S(2)}) collective-permute-start(bf16[1024,768]{1,0:T(8,128)(2,1)} %get-tuple-element.39), channel_id=1, source_target_pairs={{1,0},{2,1},{3,2},{5,4},{6,5},{7,6},{9,8},{10,9},{11,10},{13,12},{... | collective-permute-start | bytes 4718600 | tf_op jit(solution)/shard_map/ppermute | solution.py:414
  466.0 22.5 %copy-start.7 = (bf16[1024,768]{1,0:T(8,128)(2,1)S(1)}, bf16[1024,768]{1,0:T(8,128)(2,1)}, u32[]{:S(2)}) copy-start(bf16[1024,768]{1,0:T(8,128)(2,1)} %param.7) | copy-start | bytes 4718596
  466.0 22.5 %copy-start.19 = (f32[768]{0:T(1024)S(1)}, f32[768]{0:T(1024)}, u32[]{:S(2)}) copy-start(f32[768]{0:T(1024)} %copy-done.18) | copy-start | bytes 9220
  466.0 21.8 %collective-permute-start.6 = (bf16[304,768]{1,0:T(8,128)(2,1)S(1)}, bf16[304,768]{1,0:T(8,128)(2,1)S(1)}, u32[]{:S(2)}, u32[]{:S(2)}) collective-permute-start(bf16[304,768]{1,0:T(8,128)(2,1)S(1)} %get-tuple-element.47), channel_id=1, source_target_pairs={{0,8},{1,9},{2,10},{3,11},{4,12},{5,13},{6,14},{7,15},{8,0},{9,1},... | collective-permute-start | bytes 1400840 | tf_op jit(solution)/shard_map/ppermute | solution.py:420
  466.8 21.7 %copy-start.10 = (f32[1024,768]{1,0:T(8,128)S(1)}, f32[1024,768]{1,0:T(8,128)}, u32[]{:S(2)}) copy-start(f32[1024,768]{1,0:T(8,128)} %get-tuple-element.38) | copy-start | bytes 9437188
  487.9 24.3 %collective-permute-start.7 = (bf16[304,768]{1,0:T(8,128)(2,1)S(1)}, bf16[304,768]{1,0:T(8,128)(2,1)S(1)}, u32[]{:S(2)}, u32[]{:S(2)}) collective-permute-start(bf16[304,768]{1,0:T(8,128)(2,1)S(1)} %get-tuple-element.49), channel_id=1, source_target_pairs={{0,16},{1,17},{2,18},{3,19},{4,20},{5,21},{6,22},{7,23},{8,24},{9,... | collective-permute-start | bytes 1400840 | tf_op jit(solution)/shard_map/ppermute | solution.py:420
  512.3 1.5 copy-start.15
  513.7 7.3 %slice-start.2 = ((f32[304,768]{1,0:T(8,128)}), f32[16,768]{1,0:T(8,128)S(1)}, s32[]{:S(2)}) async-start(f32[304,768]{1,0:T(8,128)} %copy-done.15), calls=%async_computation.5 | async-start | bytes 98304 | tf_op jit(solution)/shard_map/slice | solution.py:608
  513.8 7.4 %copy-start.12 = (f32[1731,128]{1,0:T(8,128)S(1)}, f32[1731,128]{1,0:T(8,128)}, u32[]{:S(2)}) copy-start(f32[1731,128]{1,0:T(8,128)} %param.10) | copy-start | bytes 2658820
  513.8 7.4 %collective-permute-start.8 = (f32[96,128]{1,0:T(8,128)S(1)}, f32[96,128]{1,0:T(8,128)S(1)}, u32[]{:S(2)}, u32[]{:S(2)}) collective-permute-start(f32[96,128]{1,0:T(8,128)S(1)} %slice.62), channel_id=1, source_target_pairs={{1,0},{2,1},{3,2},{4,3},{5,4},{6,5},{7,6},{8,7},{9,8},{10,9},{11,1... | collective-permute-start | bytes 147464 | tf_op jit(solution)/shard_map/ppermute | solution.py:408
Sparse Core Ops, SparseCore 0:
  14.0 109.0 all-gather.1
  291.1 196.4 reduce-scatter.1

commit v2 on v1

--- a/solution.py
+++ b/solution.py
@@ -402,6 +402,128 @@
     )(index, keep, got)
 
 
+def ffn_kernel(
+    state_ref, x_ref, att_ref, cot_ref, gain_ref, wo_ref, up_ref, down_ref,
+    out_ref, gh_ref, ga_ref, gain_grad_ref, flat_ref,
+    hidden, low, total, back, cot, sq, gb, stage_up, stage_down, stage_out, sems,
+):
+    c = pl.program_id(0)
+    rows = x_ref.shape[0]
+    blocks = [pl.ds(i * QB, QB) for i in range(rows // QB)]
+    last = c == pl.num_programs(0) - 1
+
+    def put_zero(i):
+        return pltpu.make_async_copy(stage_out, flat_ref.at[pl.ds(8 * i, 8)], sems.at[8 + i])
+
+    def put_up(i):
+        return pltpu.make_async_copy(stage_up.at[i], flat_ref.at[pl.ds(32, 32), i], sems.at[i])
+
+    def put_down(i):
+        return pltpu.make_async_copy(stage_down.at[i], flat_ref.at[pl.ds(64 + 8 * i, 8)], sems.at[4 + i])
+
+    def put_out():
+        return pltpu.make_async_copy(stage_out, flat_ref.at[pl.ds(24, 8)], sems.at[11])
+
+    @pl.when(c == 0)
+    def _():
+        stage_out[...] = jnp.zeros(stage_out.shape, BF)
+        for i in range(3):
+            put_zero(i).start()
+        cot[...] = jnp.where(state_ref[0] > 0, cot_ref[...], jnp.zeros((), BF))
+        total[...] = jnp.zeros(total.shape, F32)
+        back[...] = jnp.zeros(back.shape, F32)
+        for b in blocks:
+            h = x_ref[b, :].astype(F32) + dot(att_ref[b, :], wo_ref[...])
+            hidden[b, :] = h
+            hat = h * lax.rsqrt(jnp.mean(h * h, axis=-1, keepdims=True) + norm_eps)
+            low[b, :] = (hat * gain_ref[...]).astype(BF)
+
+    up = up_ref[...].reshape(D, D)
+    for b in blocks:
+        act = jnp.maximum(dot(low[b, :], up), 0.0)
+        s = (act * act).astype(BF)
+        sq[b, :] = s
+        total[b, :] += dot(s, down_ref[...])
+        g = (dot_nt(cot[b, :], down_ref[...]) * 2.0 * act).astype(BF)
+        gb[b, :] = g
+        back[b, :] += dot_nt(g, up)
+    stage_down[c] = dot_tn(sq[...], cot[...]).reshape(8, 4, 24, D).astype(BF)
+    stage_up[c] = dot_tn(low[...], gb[...]).reshape(32, 24, D).astype(BF)
+    put_down(c).start()
+    put_up(c).start()
+
+    @pl.when(last)
+    def _():
+        for i in range(3):
+            put_zero(i).wait()
+        gain = gain_ref[...]
+        sums = jnp.zeros((1, D), F32)
+        for b in blocks:
+            h = hidden[b, :]
+            out_ref[b, :] = (h + total[b, :]).astype(BF)
+            factor = lax.rsqrt(jnp.mean(h * h, axis=-1, keepdims=True) + norm_eps)
+            hat = h * factor
+            g = back[b, :]
+            sums = sums + jnp.sum(g * hat, axis=0, keepdims=True)
+            weighted = g * gain
+            inner = jnp.mean(weighted * hat, axis=-1, keepdims=True)
+            grad = cot[b, :].astype(F32) + factor * (weighted - hat * inner)
+            gh_ref[b, :] = grad
+            grad_low = grad.astype(BF)
+            gb[b, :] = grad_low
+            ga_ref[b, :] = dot_nt(grad_low, wo_ref[...]).astype(BF)
+        gain_grad_ref[...] = sums
+        stage_out[...] = dot_tn(att_ref[...], gb[...]).reshape(8, 4, 24, D).astype(BF)
+        put_out().start()
+        for i in range(pl.num_programs(0)):
+            put_down(i).wait()
+            put_up(i).wait()
+        put_out().wait()
+
+
+def ffn(state, tokens, attended, out_grad, gain, wide, rows):
+    def whole(shape):
+        return pl.BlockSpec(shape, lambda c: (0,) * len(shape))
+
+    act = whole((rows, D))
+    square = wide.reshape(12 * D, D)
+    return pl.pallas_call(
+        ffn_kernel,
+        grid=(4,),
+        in_specs=[
+            pl.BlockSpec(memory_space=pltpu.SMEM),
+            act, act, act, whole((1, D)),
+            pl.BlockSpec((D, D), lambda c: (3, 0)),
+            pl.BlockSpec((32, 1, 24, D), lambda c: (1, c, 0, 0)),
+            pl.BlockSpec((D, D), lambda c: (8 + c, 0)),
+        ],
+        out_specs=[act, act, act, whole((1, D)), pl.BlockSpec(memory_space=pl.ANY)],
+        out_shape=[
+            jax.ShapeDtypeStruct((rows, D), BF),
+            jax.ShapeDtypeStruct((rows, D), F32),
+            jax.ShapeDtypeStruct((rows, D), BF),
+            jax.ShapeDtypeStruct((1, D), F32),
+            jax.ShapeDtypeStruct((96, 4, 24, D), BF),
+        ],
+        scratch_shapes=[
+            pltpu.VMEM((rows, D), F32),
+            pltpu.VMEM((rows, D), BF),
+            pltpu.VMEM((rows, D), F32),
+            pltpu.VMEM((rows, D), F32),
+            pltpu.VMEM((rows, D), BF),
+            pltpu.VMEM((rows, D), BF),
+            pltpu.VMEM((rows, D), BF),
+            pltpu.VMEM((4, 32, 24, D), BF),
+            pltpu.VMEM((4, 8, 4, 24, D), BF),
+            pltpu.VMEM((8, 4, 24, D), BF),
+            pltpu.SemaphoreType.DMA((12,)),
+        ],
+        compiler_params=pltpu.CompilerParams(vmem_limit_bytes=60 << 20),
+        cost_estimate=cost(2 * rows * D * D * (24 + 3), 2 * 12 * D * D * 2 + rows * D * 16),
+        name="ffn",
+    )(state, tokens, attended, out_grad, gain, square, wide, square)
+
+
 def shift_flat(block, distance):
     count = lax.axis_size(AXES)
     route = [(i - distance, i) for i in range(count) if 0 <= i - distance < count]
@@ -463,6 +585,14 @@
     return lax.dynamic_slice_in_dim(jnp.concatenate(parts, 0), delta * place, rows, 0)
 
 
+def regroup(block):
+    return block.reshape(-1, 24, 4, D).transpose(0, 2, 1, 3)
+
+
+def ungroup(block):
+    return block.reshape(-1, 4, 24, D).transpose(0, 2, 1, 3)
+
+
 def normalize(values, gain):
     factor = lax.rsqrt(jnp.mean(values * values, axis=-1, keepdims=True) + norm_eps)
     scaled = values * factor
@@ -510,17 +640,24 @@
     state_vec = state[None]
 
     tokens_before = shift_ctx(tokens, 1)
-    chunk = to_aligned(master, place, count, delta).reshape(-1, D).astype(BF)
-    wide = lax.all_gather(chunk, AXES, axis=0, tiled=True)
+    chunk = to_aligned(master, place, count, delta).reshape(-1, D)
+    if staged:
+        group = 3 * place + jnp.arange(3, dtype=jnp.int32)
+        in_up = ((group >= 32) & (group < 64))[:, None, None, None]
+        chunk = jnp.where(in_up, regroup(chunk), chunk.reshape(3, 4, 24, D)).reshape(-1, D)
+    wide = lax.all_gather(chunk.astype(BF), AXES, axis=0, tiled=True)
     small = lax.psum(lax.reduce_precision(small_part(master, place, count, delta), 8, 7), AXES)
     small = small.reshape(-1)
     gain_first = small[:D]
     gain_second = small[D : 2 * D]
     taps = small[2 * D : 11 * D].reshape(3, 3 * D)
     in_weight = jnp.concatenate([wide[:D], wide[D : 2 * D], wide[2 * D : 3 * D]], 1)
-    out_weight = wide[3 * D : 4 * D]
-    up_weight = wide[4 * D : 8 * D].reshape(D, FF)
-    down_weight = wide[8 * D : 12 * D]
+    if staged:
+        grouped = wide.reshape(96, 4, 24, D)
+    else:
+        grouped = jnp.concatenate(
+            [wide[: 4 * D].reshape(-1, 4, 24, D), regroup(wide[4 * D : 8 * D]), wide[8 * D :].reshape(-1, 4, 24, D)], 0
+        )
 
     tokens_both = jnp.concatenate([tokens_before, tokens], 0)
     inputs_both = tokens_both.astype(F32)
@@ -540,49 +677,25 @@
     ahead_two = masks(row_id + 2)[1]
     attn_low, logs, *mixed = att_fwd(state_vec, projected, taps, after_one, after_two, rows)
 
-    inputs = tokens.astype(F32)
-    hidden = inputs + dot(attn_low, out_weight)
-    scaled_two, factor_two, normed_two = normalize(hidden, gain_second)
-    second_low = normed_two.astype(BF)
-    active = jnp.maximum(dot(second_low, up_weight), 0.0)
-    squared_low = (active * active).astype(BF)
-    layer_out = (hidden + dot(squared_low, down_weight)).astype(BF)
-
-    grad_low = jnp.where(state > 0, out_grad, jnp.zeros((), BF))
-    grad_out = grad_low.astype(F32)
-    grad_down = dot_tn(squared_low, grad_low)
-    grad_before = (dot_nt(grad_low, down_weight) * 2.0 * active).astype(BF)
-    grad_up = dot_tn(second_low, grad_before)
-    grad_normed_two = dot_nt(grad_before, up_weight)
-    grad_gain_two = jnp.sum(grad_normed_two * scaled_two, axis=0)
-    grad_hidden = grad_out + norm_back(grad_normed_two, scaled_two, factor_two, gain_second)
-    hidden_low = grad_hidden.astype(BF)
-    grad_outw = dot_tn(attn_low, hidden_low)
-    grad_attended = dot_nt(hidden_low, out_weight).astype(BF)
-
+    layer_out, grad_hidden, grad_attended, grad_gain_two, flat_grad = ffn(
+        state_vec, tokens, attn_low, out_grad, gain_second[None], grouped, rows
+    )
     if staged:
-        late_grad = jnp.concatenate(
-            [
-                jnp.zeros((3 * D, D), BF),
-                grad_outw.astype(BF),
-                grad_up.astype(BF).reshape(-1, D),
-                grad_down.astype(BF),
-            ],
-            0,
+        late_chunk = lax.psum_scatter(
+            flat_grad.reshape(12 * D, D), AXES, scatter_dimension=0, tiled=True
         )
-        late_chunk = lax.psum_scatter(late_grad, AXES, scatter_dimension=0, tiled=True)
 
     *back, tap_grads = att_bwd(
         state_vec, mixed, attn_low, logs, grad_attended, projected, taps, ahead_one, ahead_two, rows
     )
     core = (place & 1)[None]
     sums = qkv_bwd(
-        core, tokens_both, back, wide, gain_first[None], grad_gain_two[None], tap_grads, rows,
+        core, tokens_both, back, wide, gain_first[None], grad_gain_two, tap_grads, rows,
         4 if staged else 0,
     )
     grads_before, grad_normed_one = sums[2:]
     from_next = shift_ctx(grads_before, -1)
-    scaled_one, factor_one, _ = normalize(inputs, gain_first)
+    scaled_one, factor_one, _ = normalize(tokens.astype(F32), gain_first)
     input_grad = grad_hidden + norm_back(
         grad_normed_one + from_next.astype(F32), scaled_one, factor_one, gain_first
     )
@@ -606,14 +719,16 @@
         got = swap(send, 16, 16)
         first = keep + got.astype(F32)
         small_grad = first[height:].reshape(-1, 128)
-        chunk_grad = jnp.where(place < count // 4, first[:height], late_chunk.astype(F32))
+        late_grad = late_chunk.astype(F32)
+        late_grad = jnp.where(in_up, ungroup(late_grad).reshape(3, 4, 24, D), late_grad.reshape(3, 4, 24, D))
+        chunk_grad = jnp.where(place < count // 4, first[:height], late_grad.reshape(-1, D))
     else:
         wide_grad = jnp.concatenate(
             [
                 sums[0],
-                grad_outw.astype(BF),
-                grad_up.astype(BF).reshape(-1, D),
-                grad_down.astype(BF),
+                flat_grad[24:32].reshape(-1, D),
+                ungroup(flat_grad[32:64]).reshape(-1, D),
+                flat_grad[64:].reshape(-1, D),
             ],
             0,
         )

time: 541 us -> 478 us (0.88)
  matrix products: 74.2 us -> 10.2 us
  Pallas kernels: 113 us -> 157 us
  other arithmetic: 55.2 us -> 22.5 us
  local copies, waits for them, and re-layouts: 49.1 us -> 23.8 us
  waiting for transfers between devices: 100 us -> 114 us
    pallas_call x0 -> x1, Pallas kernels: none -> 43.9 us  [ffn(): pl.pallas_call(ffn_kernel, grid=(4,), in_specs=[pl.BlockSpec(memory_space...]
    dot_general x6 -> x0, matrix products: 41.4 us -> none  [the longest x3 20.9 us: dot_tn(): return lax.dot_general(left, right, TN, preferred_element_type=F32)]
    concatenate x1, other arithmetic: 32.9 us -> 1.42 us  [to_aligned(): joined = jnp.concatenate(parts, 0)]
    dot_general x4 -> x1, matrix products: 32.8 us -> 10.2 us  [dot(): return jnp.dot(left, right, preferred_element_type=F32)]
    reshape x2 -> x1, local copies, waits for them, and re-layouts: 16.9 us -> 0.31 us  [shards(): ungroup(late_grad).reshape(3, 4, 24, D)]
    ppermute x5, waiting for transfers between devices: 56.9 us -> 70.8 us  [swap(): return lax.ppermute(block, AXES, route)]
    unnamed x49 -> x22, local copies, waits for them, and re-layouts: 14.2 us -> 9.57 us
  transfers between devices with their start and end apart: 11 -> 11, of which waited for: 7 -> 7; matrix products, arithmetic and copies ran while one was open for 6% -> 5% of each run, Pallas kernels for 13% -> 15%
where the time goes in v2:
time: 478 us; the launch traced here: 470 us
  Pallas kernels  157 us (33%)
  waiting for transfers between devices  114 us (24%)
  starting transfers between devices  74.3 us (16%)
  blocking collectives  52.3 us (11%)
  local copies, waits for them, and re-layouts  23.8 us (5%)
  other arithmetic  22.5 us (5%)
  between operations  16.9 us (4%)
  matrix products  10.2 us (2%)
    ppermute x5, waiting for transfers between devices, swap(): return lax.ppermute(block, AXES, route)  70.8 us
    ppermute x5, starting transfers between devices, swap(): return lax.ppermute(block, AXES, route)  63.6 us
    psum x1, blocking collectives, shards(): lax.psum(lax.reduce_precision(small_part(master, place, count, delta), 8,...  52.3 us
    pallas_call x1, Pallas kernels, att_bwd(): pl.pallas_call(att_bwd_kernel, grid=(6,), in_specs=[pl.BlockSpec(memory_s...  45.7 us
    pallas_call x1, Pallas kernels, ffn(): pl.pallas_call(ffn_kernel, grid=(4,), in_specs=[pl.BlockSpec(memory_space...  43.9 us
    pallas_call x1, Pallas kernels, att_fwd(): pl.pallas_call(att_fwd_kernel, grid=(6,), in_specs=[pl.BlockSpec(memory_s...  42.2 us
    all_gather x1, waiting for transfers between devices, shards(): wide = lax.all_gather(chunk.astype(BF), AXES, axis=0, tiled=True)  42 us
    pallas_call x1, Pallas kernels, qkv_bwd(): pl.pallas_call(body, grid=(blocks,), in_specs=[pl.BlockSpec(memory_space=...  22.3 us
  transfers between devices with their start and end apart: 11, of which 7 were waited for; matrix products, arithmetic and copies ran while one was open for 5% of the time, Pallas kernels for 15%

profile of v2, /device:TPU:0, one launch (start us, length us, event | category | flops | bytes accessed | tf_op | source)
XLA Modules:
  0.0 470.4 jit_solution(5862454527822815407)
XLA Ops:
  7.2 1.0 slice.41
  8.2 2.3 collective-permute-start.1
  10.6 0.8 collective-permute-done.1
  11.4 1.4 fusion.20
  13.0 1.2 reshape_reshape.7
  14.1 1.3 fusion.21
  15.5 0.8 copy.17
  16.4 5.8 %collective-permute-start = (bf16[1024,768]{1,0:T(8,128)(2,1)S(1)}, bf16[1024,768]{1,0:T(8,128)(2,1)}, u32[]{:S(2)}, u32[]{:S(2)}) collective-permute-start(bf16[1024,768]{1,0:T(8,128)(2,1)S(1)} %copy-done.3), channel_id=1, source_target_pairs={{0,1},{1,2},{2,3},{4,5},{5,6},{6,7},{8,9},{9,10},{10,11},{12,13},{... | collective-permute-start | bytes 4718600 | tf_op jit(solution)/shard_map/ppermute | solution.py:536
  22.1 1.2 slice.39
  24.7 0.8 concatenate.16
  25.5 52.3 %psum.7 = f32[96,128]{1,0:T(8,128)S(1)} all-reduce(f32[96,128]{1,0:T(8,128)S(1)} %dynamic-slice_reduce-precision_fusion), channel_id=1, replica_groups=mesh['dp'=8,'ctx'=4] {'dp','ctx'}, use_global_device_ids=true, to_apply=%region_1.2 | all-reduce | flops 12288 | bytes 98304 | tf_op jit(solution)/shard_map/psum | solution.py:649
  77.8 0.6 reshape.114.tq_ref.tk_ref.tv_ref
  79.0 2.0 constant_dynamic-update-slice_fusion.1
  81.1 1.7 copy-done.7
  82.8 0.7 fusion
  83.5 42.0 %all-gather.2.cloned.1.call-done.wo_ref.down_ref.refs_6_ = bf16[9216,768]{1,0:T(8,128)(2,1)} async-done(((bf16[288,768]{1,0:T(8,128)(2,1)}), bf16[9216,768]{1,0:T(8,128)(2,1)}) %all-gather.2.cloned.1.call-update) | async-done | bytes 14155792 | tf_op jit(solution)/shard_map/all_gather | solution.py:648
  125.5 2.2 fusion.58
  127.8 10.2 %convolution_convert_fusion.tail_ref.q_ref.k_ref.v_ref.xt_ref.xq_ref.xk_ref.xv_ref = bf16[2048,2304]{1,0:T(8,128)(2,1)} fusion(bf16[768,768]{1,0:T(8,128)(2,1)S(1)} %get-tuple-element.65, bf16[768,768]{1,0:T(8,128)(2,1)S(1)} %get-tuple-element.66, bf16[768,768]{1,0:T(8,128)(2,1)S(1)} %get-tuple-element.64, bf16[2048,768]{1,0:T(8,128)(2,1)S(1)} %copy-done.8, ...), kind=kOutput, calls=%fused_computation | convolution fusion | flops 7269384192 | bytes 16133120 | tf_op jit(solution)/shard_map/dot_general | solution.py:24
  138.0 1.3 iota.59.one_ref
  139.3 1.3 iota.62.two_ref
  140.6 42.2 %att_fwd.1 = (bf16[1024,768]{1,0:T(8,128)(2,1)}, f32[1024,768]{1,0:T(8,128)}, bf16[1024,768]{1,0:T(8,128)(2,1)}, bf16[2048,768]{1,0:T(8,128)(2,1)}, bf16[2048,768]{1,0:T(8,128)(2,1)}) custom-call(s32[1]{0:T(128)S(6)} %select_n.103.state_ref, bf16[2048,2304]{1,0:T(8,128)(2,1)} %convolution_convert_fusion.tail_ref.q_ref.k_ref.v_ref.xt_ref.xq_ref.xk_ref.xv_ref, ...), custom_call_target="tpu_custom_call" | custom-call | flops 19327352832 | bytes 23592960 | tf_op jit(solution)/shard_map/att_fwd/pallas_call | solution.py:104
  182.8 43.9 %ffn.1 = (bf16[1024,768]{1,0:T(8,128)(2,1)}, f32[1024,768]{1,0:T(8,128)}, bf16[1024,768]{1,0:T(8,128)(2,1)}, f32[1,768]{1,0:T(1,128)}, bf16[96,4,24,768]{3,2,1,0:T(8,128)(2,1)}) custom-call(s32[1]{0:T(128)S(6)} %select_n.103.state_ref, bf16[1024,768]{1,0:T(8,128)(2,1)} %x_ref.1, bf16[1024,768]{1,0:T(8,128)(2,1)} %get-tuple-element.33.att_ref.o_ref, ...), custom_call_target="tpu_custom_call" | custom-call | flops 32614907904 | bytes 40894464 | tf_op jit(solution)/shard_map/ffn/pallas_call | solution.py:490
  227.3 1.3 iota.64.one_ref
  228.7 1.3 iota.66.two_ref
  230.0 45.7 %att_bwd.1 = (bf16[1024,768]{1,0:T(8,128)(2,1)}, bf16[8,768]{1,0:T(8,128)(2,1)}, bf16[2048,768]{1,0:T(8,128)(2,1)}, bf16[2048,768]{1,0:T(8,128)(2,1)}, f32[16,768]{1,0:T(8,128)}) custom-call(s32[1]{0:T(128)S(6)} %select_n.103.state_ref, bf16[1024,768]{1,0:T(8,128)(2,1)} %get-tuple-element.36.q_ref, bf16[2048,768]{1,0:T(8,128)(2,1)} %get-tuple-element.37.k_ref, ...), custom_call_target="tpu_custom_call" | custom-call | flops 48318382080 | bytes 31457280 | tf_op jit(solution)/shard_map/att_bwd/pallas_call | solution.py:225
  275.7 22.3 %qkv_bwd.1 = (bf16[1168,768]{1,0:T(8,128)(2,1)}, f32[1168,768]{1,0:T(8,128)}, bf16[1024,768]{1,0:T(8,128)(2,1)}, f32[1024,768]{1,0:T(8,128)}) custom-call(s32[1]{0:T(128)} %bitcast.6.refs_0_.index_ref, bf16[2048,768]{1,0:T(8,128)(2,1)} %copy-done.7, bf16[1024,768]{1,0:T(8,128)(2,1)} %get-tuple-element.41.refs_2_, bf16[8,768]{1,0:T(8,128)(2,1)} %get-tuple-element.42.refs_3_, ...), custom_call_target="tpu_custom_call" | custom-call | flops 12079595520 | bytes 23592960 | tf_op jit(solution)/shard_map/qkv_bwd/pallas_call | solution.py:352
  298.3 3.6 collective-permute-done.3.got_ref
  301.9 1.2 copy-done.1
  303.1 2.0 copy-done
  305.2 1.5 copy-done.2
  306.6 1.7 merge.4
  308.4 1.7 collective-permute-start.4
  310.1 1.3 collective-permute-start.2
  311.5 23.0 %collective-permute-done.4.got_ref = bf16[592,768]{1,0:T(8,128)(2,1)S(1)} collective-permute-done((bf16[592,768]{1,0:T(8,128)(2,1)}, bf16[592,768]{1,0:T(8,128)(2,1)S(1)}, u32[]{:S(2)}, u32[]{:S(2)}) %collective-permute-start.4) | collective-permute-done | bytes 909344 | tf_op jit(solution)/shard_map/ppermute | solution.py:542
  334.5 0.7 merge.5
  335.2 58.9 %collective-permute-start.5 = (bf16[304,768]{1,0:T(8,128)(2,1)S(1)}, bf16[304,768]{1,0:T(8,128)(2,1)S(1)}, u32[]{:S(2)}, u32[]{:S(2)}) collective-permute-start(bf16[304,768]{1,0:T(8,128)(2,1)S(1)} %get-tuple-element.54), channel_id=1, source_target_pairs={{0,4},{1,3},{2,6},{3,1},{4,0},{5,7},{6,2},{7,5},{8,12},{9,11},{10,... | collective-permute-start | bytes 1400840 | tf_op jit(solution)/shard_map/ppermute | solution.py:542
  394.2 8.2 %collective-permute-done.5.got_ref = bf16[304,768]{1,0:T(8,128)(2,1)S(1)} collective-permute-done((bf16[304,768]{1,0:T(8,128)(2,1)S(1)}, bf16[304,768]{1,0:T(8,128)(2,1)S(1)}, u32[]{:S(2)}, u32[]{:S(2)}) %collective-permute-start.5) | collective-permute-done | bytes 466976 | tf_op jit(solution)/shard_map/ppermute | solution.py:542
  403.5 1.8 fusion.14
  405.3 10.9 %collective-permute-done.6.got_ref = bf16[304,768]{1,0:T(8,128)(2,1)S(1)} collective-permute-done((bf16[304,768]{1,0:T(8,128)(2,1)S(1)}, bf16[304,768]{1,0:T(8,128)(2,1)S(1)}, u32[]{:S(2)}, u32[]{:S(2)}) %collective-permute-start.6) | collective-permute-done | bytes 466976 | tf_op jit(solution)/shard_map/ppermute | solution.py:542
  416.2 2.6 collective-permute-start.7
  418.8 3.3 fusion.10
  422.2 25.1 %collective-permute-done.7 = bf16[304,768]{1,0:T(8,128)(2,1)S(1)} collective-permute-done((bf16[304,768]{1,0:T(8,128)(2,1)S(1)}, bf16[304,768]{1,0:T(8,128)(2,1)S(1)}, u32[]{:S(2)}, u32[]{:S(2)}) %collective-permute-start.7) | collective-permute-done | bytes 466976 | tf_op jit(solution)/shard_map/ppermute | solution.py:542
  447.3 1.1 convert_add_fusion
  448.3 1.1 convert_element_type.58
  450.1 1.4 slice_select_fusion
  451.6 1.3 collective-permute-start.8
  452.9 6.0 %fusion.13 = f32[1024,768]{1,0:T(8,128)} fusion(f32[1024,768]{1,0:T(8,128)} %get-tuple-element.35, bf16[1024,768]{1,0:T(8,128)(2,1)S(1)} %copy-done.4, f32[1024,768]{1,0:T(8,128)} %get-tuple-element.47, bf16[1024,768]{1,0:T(8,128)(2,1)} %collective-permute-done.2, f32[1024]{0:T(1024)S(1)} %broadcast_multiply_fusion, f32[768]{0:T(1024)S(1)} %get-tuple-element.69, ...), kind=kLoop, calls=%fused_computation.18 | loop fusion | flops 7077888 | bytes 12594176 | tf_op jit(solution)/shard_map/add | solution.py:699
  459.0 4.1 fusion.56
  (54 shorter events, 3.3 us)
Async XLA Ops:
  7.2 17.5 %copy-start.5 = (f32[1731,128]{1,0:T(8,128)S(1)}, f32[1731,128]{1,0:T(8,128)}, u32[]{:S(2)}) copy-start(f32[1731,128]{1,0:T(8,128)} %param.10) | copy-start | bytes 2658820
  7.2 9.2 %copy-start.3 = (bf16[1024,768]{1,0:T(8,128)(2,1)S(1)}, bf16[1024,768]{1,0:T(8,128)(2,1)}, u32[]{:S(2)}) copy-start(bf16[1024,768]{1,0:T(8,128)(2,1)} %x_ref.1) | copy-start | bytes 4718596
  7.2 118.4 %all-gather.2.cloned.1.call-start = ((), (), s32[]{:S(2)}) async-start(), calls=%async_computation.1 | async-start | bytes 14598144 | tf_op jit(solution)/shard_map/all_gather | solution.py:648
  8.2 3.2 collective-permute-start.1
  16.3 432.0 %reduce-scatter.2.cloned.1.call-start = ((), (), s32[]{:S(2)}) async-start(), calls=%async_computation.2 | async-start | bytes 14598144 | tf_op jit(solution)/shard_map/reduce_scatter | solution.py:684
  16.4 62.7 %collective-permute-start = (bf16[1024,768]{1,0:T(8,128)(2,1)S(1)}, bf16[1024,768]{1,0:T(8,128)(2,1)}, u32[]{:S(2)}, u32[]{:S(2)}) collective-permute-start(bf16[1024,768]{1,0:T(8,128)(2,1)S(1)} %copy-done.3), channel_id=1, source_target_pairs={{0,1},{1,2},{2,3},{4,5},{5,6},{6,7},{8,9},{9,10},{10,11},{12,13},{... | collective-permute-start | bytes 4718600 | tf_op jit(solution)/shard_map/ppermute | solution.py:536
  81.1 1.7 copy-start.7
  83.5 44.3 %copy-start.8 = (bf16[2048,768]{1,0:T(8,128)(2,1)S(1)}, bf16[2048,768]{1,0:T(8,128)(2,1)}, u32[]{:S(2)}) copy-start(bf16[2048,768]{1,0:T(8,128)(2,1)} %copy-done.7) | copy-start | bytes 9437188
  298.0 3.9 collective-permute-start.3
  301.9 1.2 copy-start.1
  303.1 2.0 copy-start
  305.2 1.5 copy-start.2
  308.4 26.2 %collective-permute-start.4 = (bf16[592,768]{1,0:T(8,128)(2,1)}, bf16[592,768]{1,0:T(8,128)(2,1)S(1)}, u32[]{:S(2)}, u32[]{:S(2)}) collective-permute-start(bf16[592,768]{1,0:T(8,128)(2,1)} %get-tuple-element.52), channel_id=1, source_target_pairs={{0,2},{1,5},{2,0},{3,7},{4,6},{5,1},{6,4},{7,3},{8,10},{9,13},{10,... | collective-permute-start | bytes 2727944 | tf_op jit(solution)/shard_map/ppermute | solution.py:542
  310.1 108.7 %collective-permute-start.2 = (bf16[1024,768]{1,0:T(8,128)(2,1)}, bf16[1024,768]{1,0:T(8,128)(2,1)}, u32[]{:S(2)}, u32[]{:S(2)}) collective-permute-start(bf16[1024,768]{1,0:T(8,128)(2,1)} %get-tuple-element.48), channel_id=1, source_target_pairs={{1,0},{2,1},{3,2},{5,4},{6,5},{7,6},{9,8},{10,9},{11,10},{13,12},{... | collective-permute-start | bytes 4718600 | tf_op jit(solution)/shard_map/ppermute | solution.py:536
  335.2 83.6 %copy-start.4 = (bf16[1024,768]{1,0:T(8,128)(2,1)S(1)}, bf16[1024,768]{1,0:T(8,128)(2,1)}, u32[]{:S(2)}) copy-start(bf16[1024,768]{1,0:T(8,128)(2,1)} %x_ref.1) | copy-start | bytes 4718596
  335.2 67.1 %collective-permute-start.5 = (bf16[304,768]{1,0:T(8,128)(2,1)S(1)}, bf16[304,768]{1,0:T(8,128)(2,1)S(1)}, u32[]{:S(2)}, u32[]{:S(2)}) collective-permute-start(bf16[304,768]{1,0:T(8,128)(2,1)S(1)} %get-tuple-element.54), channel_id=1, source_target_pairs={{0,4},{1,3},{2,6},{3,1},{4,0},{5,7},{6,2},{7,5},{8,12},{9,11},{10,... | collective-permute-start | bytes 1400840 | tf_op jit(solution)/shard_map/ppermute | solution.py:542
  402.5 13.7 %collective-permute-start.6 = (bf16[304,768]{1,0:T(8,128)(2,1)S(1)}, bf16[304,768]{1,0:T(8,128)(2,1)S(1)}, u32[]{:S(2)}, u32[]{:S(2)}) collective-permute-start(bf16[304,768]{1,0:T(8,128)(2,1)S(1)} %get-tuple-element.56), channel_id=1, source_target_pairs={{0,8},{1,9},{2,10},{3,11},{4,12},{5,13},{6,14},{7,15},{8,0},{9,1},... | collective-permute-start | bytes 1400840 | tf_op jit(solution)/shard_map/ppermute | solution.py:542
  416.2 31.0 %collective-permute-start.7 = (bf16[304,768]{1,0:T(8,128)(2,1)S(1)}, bf16[304,768]{1,0:T(8,128)(2,1)S(1)}, u32[]{:S(2)}, u32[]{:S(2)}) collective-permute-start(bf16[304,768]{1,0:T(8,128)(2,1)S(1)} %get-tuple-element.58), channel_id=1, source_target_pairs={{0,16},{1,17},{2,18},{3,19},{4,20},{5,21},{6,22},{7,23},{8,24},{9,... | collective-permute-start | bytes 1400840 | tf_op jit(solution)/shard_map/ppermute | solution.py:542
  451.6 7.4 %collective-permute-start.8 = (f32[96,128]{1,0:T(8,128)S(1)}, f32[96,128]{1,0:T(8,128)S(1)}, u32[]{:S(2)}, u32[]{:S(2)}) collective-permute-start(f32[96,128]{1,0:T(8,128)S(1)} %slice.50), channel_id=1, source_target_pairs={{1,0},{2,1},{3,2},{4,3},{5,4},{6,5},{7,6},{8,7},{9,8},{10,9},{11,1... | collective-permute-start | bytes 147464 | tf_op jit(solution)/shard_map/ppermute | solution.py:530
  452.9 6.0 %slice-start = ((f32[304,768]{1,0:T(8,128)}), f32[16,768]{1,0:T(8,128)S(1)}, s32[]{:S(2)}) async-start(f32[304,768]{1,0:T(8,128)} %convert_add_fusion), calls=%async_computation.3 | async-start | bytes 98304 | tf_op jit(solution)/shard_map/slice | solution.py:721
  452.9 6.1 %copy-start.6 = (f32[1731,128]{1,0:T(8,128)S(1)}, f32[1731,128]{1,0:T(8,128)}, u32[]{:S(2)}) copy-start(f32[1731,128]{1,0:T(8,128)} %param.10) | copy-start | bytes 2658820
Sparse Core Ops, SparseCore 0:
  16.4 109.0 all-gather.1
  226.8 216.1 reduce-scatter.1

commit v3 on v2

--- a/solution.py
+++ b/solution.py
@@ -36,6 +36,14 @@
     return pl.CostEstimate(flops=int(flops), bytes_accessed=int(nbytes), transcendentals=int(exps))
 
 
+def taps_seen(height, start, rows, state, distance, ahead):
+    row = lax.broadcasted_iota(jnp.int32, (height, 128), 0) + (start + ahead)
+    own = row - rows
+    inside = (own >= distance) | ((own < 0) & (row >= distance)) | ((own >= 0) & (state == 2))
+    filled = ((own < 0) | (state > 0)) & (row < 2 * rows)
+    return (inside & filled).astype(F32)
+
+
 def conv(x, taps, mask_one, mask_two):
     one = pltpu.roll(x, 1, 0) * mask_one
     two = pltpu.roll(x, 2, 0) * mask_two
@@ -43,7 +51,7 @@
 
 
 def att_fwd_kernel(
-    state_ref, tail_ref, q_ref, k_ref, v_ref, tq_ref, tk_ref, tv_ref, one_ref, two_ref,
+    state_ref, tail_ref, q_ref, k_ref, v_ref, tq_ref, tk_ref, tv_ref,
     o_ref, l_ref, qm_ref, km_ref, vm_ref,
 ):
     rows = q_ref.shape[0]
@@ -51,8 +59,8 @@
     state = state_ref[0]
     second = state == 2
     empty = state == 0
-    one = one_ref[...]
-    two = two_ref[...]
+    one = taps_seen(2 * rows, 0, rows, state, 1, 0)
+    two = taps_seen(2 * rows, 0, rows, state, 2, 0)
     x = jnp.concatenate([tail_ref[...].astype(F32), q_ref[...].astype(F32)], 0)
     qm_ref[...] = conv(x, tq_ref[...], one[rows - 8 :], two[rows - 8 :])[8:]
     km_ref[...] = conv(k_ref[...].astype(F32), tk_ref[...], one, two)
@@ -95,11 +103,10 @@
         l_ref[rs, :] = jnp.where(lane < 64, sums[1], sums[0])
 
 
-def att_fwd(state, projected, taps, one, two, rows):
+def att_fwd(state, projected, taps, rows):
     def cols(height, row, off):
         return pl.BlockSpec((height, 128), lambda p: (row, p + off))
 
-    full = pl.BlockSpec((2 * rows, 128), lambda p: (0, 0))
     taps_at = [pl.BlockSpec((3, 128), lambda p, off=off: (0, p + off)) for off in (0, 6, 12)]
     return pl.pallas_call(
         att_fwd_kernel,
@@ -111,8 +118,6 @@
             cols(2 * rows, 0, 6),
             cols(2 * rows, 0, 12),
             *taps_at,
-            full,
-            full,
         ],
         out_specs=[cols(rows, 0, 0)] * 3 + [cols(2 * rows, 0, 0)] * 2,
         out_shape=[
@@ -125,7 +130,7 @@
         compiler_params=pltpu.CompilerParams(vmem_limit_bytes=VMEM_LIMIT),
         cost_estimate=cost(2 * 2 * 12 * rows * rows * 1.5 * 256, rows * D * 30, 12 * rows * rows * 1.5),
         name="att_fwd",
-    )(state, projected, projected, projected, projected, taps, taps, taps, one, two)
+    )(state, projected, projected, projected, projected, taps, taps, taps)
 
 
 def three(x, lane, base):
@@ -149,7 +154,7 @@
 
 def att_bwd_kernel(
     state_ref, q_ref, k_ref, v_ref, o_ref, l_ref, do_ref, xt_ref, xq_ref, xk_ref, xv_ref,
-    tq_ref, tk_ref, tv_ref, one_ref, two_ref,
+    tq_ref, tk_ref, tv_ref,
     pq_ref, pt_ref, pk_ref, pv_ref, tg_ref, qa, da, dqs, dks, dvs,
 ):
     rows = q_ref.shape[0]
@@ -200,8 +205,8 @@
                 dq = part(pl.ds(0, rows), qa[rs, :], da[rs, :], None)
                 dqs[pl.ds(8 + i * QB, QB), :] += dq * 0.125
 
-    one = one_ref[...]
-    two = two_ref[...]
+    one = taps_seen(2 * rows, 0, rows, state_ref[0], 1, 1)
+    two = taps_seen(2 * rows, 0, rows, state_ref[0], 2, 2)
     xq = jnp.concatenate([xt_ref[...].astype(F32), xq_ref[...].astype(F32)], 0)
     pq, sq = conv_back(dqs[...], xq, tq_ref[...], one[rows - 8 :], two[rows - 8 :])
     pt_ref[...] = pq[:8]
@@ -214,11 +219,10 @@
             tg_ref[3 * j + m : 3 * j + m + 1, :] = s[j]
 
 
-def att_bwd(state, mixed, attended, logs, grad, projected, taps, one, two, rows):
+def att_bwd(state, mixed, attended, logs, grad, projected, taps, rows):
     def cols(height, row, off):
         return pl.BlockSpec((height, 128), lambda p: (row, p + off))
 
-    full = pl.BlockSpec((2 * rows, 128), lambda p: (0, 0))
     taps_at = [pl.BlockSpec((3, 128), lambda p, off=off: (0, p + off)) for off in (0, 6, 12)]
     own = cols(rows, 0, 0)
     both = cols(2 * rows, 0, 0)
@@ -233,8 +237,6 @@
             cols(2 * rows, 0, 6),
             cols(2 * rows, 0, 12),
             *taps_at,
-            full,
-            full,
         ],
         out_specs=[own, cols(8, 0, 0), both, both, cols(16, 0, 0)],
         out_shape=[
@@ -255,7 +257,7 @@
         cost_estimate=cost(5 * 2 * 12 * rows * rows * 1.5 * 256, rows * D * 40, 12 * rows * rows * 1.5),
         name="att_bwd",
     )(state, *mixed, attended, logs, grad, projected, projected, projected, projected,
-      taps, taps, taps, one, two)
+      taps, taps, taps)
 
 
 def qkv_bwd_kernel(
@@ -400,6 +402,90 @@
         cost_estimate=cost(rows * D, rows * D * 12),
         name="merge",
     )(index, keep, got)
+
+
+def join(own, got, height):
+    rows = own.shape[0]
+    body_rows = rows - 16
+
+    def body(own_ref, got_ref, out_ref):
+        out_ref[0:body_rows, :] = own_ref[0:body_rows, :]
+        out_ref[body_rows : 2 * body_rows, :] = got_ref[0:body_rows, :]
+        out_ref[2 * body_rows :, :] = own_ref[body_rows:, :] + got_ref[body_rows:, :]
+
+    vmem = pl.BlockSpec(memory_space=pltpu.VMEM)
+    return pl.pallas_call(
+        body,
+        in_specs=[vmem, vmem],
+        out_specs=vmem,
+        out_shape=jax.ShapeDtypeStruct((2 * body_rows + 16, D), BF),
+        compiler_params=pltpu.CompilerParams(vmem_limit_bytes=32 << 20),
+        cost_estimate=cost(rows * D, rows * D * 8),
+        name="join",
+    )(own, got)
+
+
+def qkv_fwd_kernel(index_ref, x_ref, *refs, pieces, blocks):
+    if pieces:
+        own_ref, got_ref, out_ref, small_ref, weight = refs
+    else:
+        weight, given_ref, out_ref, small_ref = refs
+    i = pl.program_id(0)
+
+    @pl.when(i == 0)
+    def _():
+        if pieces:
+            height = 3 * D // (2 * pieces)
+            for j in range(pieces):
+                at = pl.ds(j * height, height)
+                for k, ref in enumerate((own_ref, got_ref)):
+                    to = pl.multiple_of(index_ref[k * pieces + j] * height, 16)
+                    weight[pl.ds(to, height), :] = ref[at, :]
+            end = pl.ds(pieces * height, 16)
+            small_ref[...] = own_ref[end, :].astype(F32) + got_ref[end, :].astype(F32)
+        else:
+            small_ref[...] = given_ref[...]
+
+    x = x_ref[...].astype(F32)
+    hat = x * lax.rsqrt(jnp.mean(x * x, axis=-1, keepdims=True) + norm_eps)
+    low = (hat * small_ref[0:1, :]).astype(BF)
+
+    @pl.when(i >= blocks // 2 - 1)
+    def _():
+        out_ref[:, 0:D] = dot(low, weight[0:D, :]).astype(BF)
+
+    out_ref[:, D : 2 * D] = dot(low, weight[D : 2 * D, :]).astype(BF)
+    out_ref[:, 2 * D : 3 * D] = dot(low, weight[2 * D : 3 * D, :]).astype(BF)
+
+
+def qkv_fwd(index, x_both, weights, rows, pieces):
+    blocks = 4
+    height = 2 * rows // blocks
+
+    def body(*refs):
+        qkv_fwd_kernel(*refs, pieces=pieces, blocks=blocks)
+
+    return pl.pallas_call(
+        body,
+        grid=(blocks,),
+        in_specs=[
+            pl.BlockSpec(memory_space=pltpu.SMEM),
+            pl.BlockSpec((height, D), lambda i: (i, 0)),
+            *[pl.BlockSpec(w.shape, lambda i: (0, 0)) for w in weights],
+        ],
+        out_specs=[
+            pl.BlockSpec((height, 3 * D), lambda i: (i, 0)),
+            pl.BlockSpec((16, D), lambda i: (0, 0)),
+        ],
+        out_shape=[
+            jax.ShapeDtypeStruct((2 * rows, 3 * D), BF),
+            jax.ShapeDtypeStruct((16, D), F32),
+        ],
+        scratch_shapes=[pltpu.VMEM((3 * D, D), BF)] if pieces else [],
+        compiler_params=pltpu.CompilerParams(vmem_limit_bytes=VMEM_LIMIT),
+        cost_estimate=cost(2 * 2 * rows * D * 3 * D, rows * D * 20),
+        name="qkv_fwd",
+    )(index, x_both, *weights)
 
 
 def ffn_kernel(
@@ -645,13 +731,40 @@
         group = 3 * place + jnp.arange(3, dtype=jnp.int32)
         in_up = ((group >= 32) & (group < 64))[:, None, None, None]
         chunk = jnp.where(in_up, regroup(chunk), chunk.reshape(3, 4, 24, D)).reshape(-1, D)
-    wide = lax.all_gather(chunk.astype(BF), AXES, axis=0, tiled=True)
-    small = lax.psum(lax.reduce_precision(small_part(master, place, count, delta), 8, 7), AXES)
-    small = small.reshape(-1)
-    gain_first = small[:D]
-    gain_second = small[D : 2 * D]
-    taps = small[2 * D : 11 * D].reshape(3, 3 * D)
-    in_weight = jnp.concatenate([wide[:D], wide[D : 2 * D], wide[2 * D : 3 * D]], 1)
+    chunk = chunk.astype(BF)
+    small = lax.reduce_precision(small_part(master, place, count, delta), 8, 7)
+    core = (place & 1)[None]
+    x_bit = (place >> 1) & 1
+    y_bit = (place >> 2) & 1
+    even = (place & 1) == 0
+    tokens_both = jnp.concatenate([tokens_before, tokens], 0)
+    if staged:
+        mine = jnp.concatenate(
+            [jnp.where(place < count // 4, chunk, jnp.zeros((), BF)), small.astype(BF).reshape(-1, D)], 0
+        )
+        mine = mine + swap(mine, 16, 16)
+        mine = mine + swap(mine, 8, 8)
+        mine = join(mine, swap(mine, 2, 4), height)
+        mine = join(mine, swap(mine, 4, 2), height)
+        got = swap(mine, 1, 1)
+        where_at = []
+        for k in (0, 1):
+            turn = even if k == 0 else jnp.logical_not(even)
+            for j in range(4):
+                near, far = j & 1, j >> 1
+                x_of = x_bit ^ jnp.where(turn, near, far)
+                y_of = y_bit ^ jnp.where(turn, far, near)
+                where_at.append(4 * y_of + 2 * x_of + (core[0] ^ k))
+        index = jnp.stack(where_at).astype(jnp.int32)
+        projected, small = qkv_fwd(index, tokens_both, (mine, got), rows, 4)
+        wide = lax.all_gather(chunk, AXES, axis=0, tiled=True)
+    else:
+        wide = lax.all_gather(chunk, AXES, axis=0, tiled=True)
+        small = lax.psum(small, AXES)[:96].reshape(-1, D)
+        projected, small = qkv_fwd(core, tokens_both, (wide[: 3 * D], small), rows, 0)
+    gain_first = small[0]
+    gain_second = small[1]
+    taps = small[2:11].reshape(3, 3 * D)
     if staged:
         grouped = wide.reshape(96, 4, 24, D)
     else:
@@ -659,23 +772,7 @@
             [wide[: 4 * D].reshape(-1, 4, 24, D), regroup(wide[4 * D : 8 * D]), wide[8 * D :].reshape(-1, 4, 24, D)], 0
         )
 
-    tokens_both = jnp.concatenate([tokens_before, tokens], 0)
-    inputs_both = tokens_both.astype(F32)
-    normed_low = normalize(inputs_both, gain_first)[2].astype(BF)
-    projected = dot(normed_low, in_weight).astype(BF)
-
-    def masks(row_id):
-        own_one = (state == 2) | ((state == 1) & (row_id > rows))
-        own_two = (state == 2) | ((state == 1) & (row_id > rows + 1))
-        one = jnp.where(row_id < rows, row_id >= 1, own_one) & (row_id < 2 * rows)
-        two = jnp.where(row_id < rows, row_id >= 2, own_two) & (row_id < 2 * rows)
-        return one.astype(F32), two.astype(F32)
-
-    row_id = lax.broadcasted_iota(jnp.int32, (2 * rows, 128), 0)
-    after_one, after_two = masks(row_id)
-    ahead_one = masks(row_id + 1)[0]
-    ahead_two = masks(row_id + 2)[1]
-    attn_low, logs, *mixed = att_fwd(state_vec, projected, taps, after_one, after_two, rows)
+    attn_low, logs, *mixed = att_fwd(state_vec, projected, taps, rows)
 
     layer_out, grad_hidden, grad_attended, grad_gain_two, flat_grad = ffn(
         state_vec, tokens, attn_low, out_grad, gain_second[None], grouped, rows
@@ -686,9 +783,8 @@
         )
 
     *back, tap_grads = att_bwd(
-        state_vec, mixed, attn_low, logs, grad_attended, projected, taps, ahead_one, ahead_two, rows
+        state_vec, mixed, attn_low, logs, grad_attended, projected, taps, rows
     )
-    core = (place & 1)[None]
     sums = qkv_bwd(
         core, tokens_both, back, wide, gain_first[None], grad_gain_two, tap_grads, rows,
         4 if staged else 0,
@@ -702,10 +798,7 @@
 
     if staged:
         send, keep = sums[:2]
-        x_bit = (place >> 1) & 1
-        y_bit = (place >> 2) & 1
         got = swap(send, 1, 1)
-        even = (place & 1) == 0
         stay = [jnp.where(even, 2 * j + x_bit, 2 * y_bit + j) for j in range(2)]
         away = [jnp.where(even, 2 * j + 1 - x_bit, 2 * (1 - y_bit) + j) for j in range(2)]
         send, keep = merge(jnp.stack(away + stay), keep, got, height, 2)

time: 478 us -> 493 us (1.031)
  waiting for transfers between devices: 114 us -> 170 us
  blocking collectives: 52.3 us -> 0 us
  starting transfers between devices: 74.3 us -> 95.7 us
  matrix products: 10.2 us -> 0 us
  Pallas kernels: 157 us -> 166 us
  local copies, waits for them, and re-layouts: 23.8 us -> 17 us
    ppermute x5 -> x10, waiting for transfers between devices: 70.8 us -> 169 us  [swap(): return lax.ppermute(block, AXES, route)]
    psum x1 -> x0, blocking collectives: 52.3 us -> none  [shards(): lax.psum(lax.reduce_precision(small_part(master, place, count, delta), 8,...]
    all_gather x1, waiting for transfers between devices: 42 us -> 0.02 us  [shards(): wide = lax.all_gather(chunk, AXES, axis=0, tiled=True)]
    ppermute x5 -> x10, starting transfers between devices: 63.6 us -> 88.1 us  [swap(): return lax.ppermute(block, AXES, route)]
    pallas_call x0 -> x3, Pallas kernels: none -> 13.7 us  [the longest x1 13.5 us: qkv_fwd(): pl.pallas_call(body, grid=(blocks,), in_specs=[pl.BlockSpec(memory_space=...]
    dot_general x1 -> x0, matrix products: 10.2 us -> none  [dot(): return jnp.dot(left, right, preferred_element_type=F32)]
    iota x4 -> x0, local copies, waits for them, and re-layouts: 5.29 us -> none  [shards(): row_id = lax.broadcasted_iota(jnp.int32, (2 * rows, 128), 0)]
  transfers between devices with their start and end apart: 11 -> 16, of which waited for: 7 -> 11; matrix products, arithmetic and copies ran while one was open for 5% -> 4% of each run, Pallas kernels for 15% -> 25%
where the time goes in v3:
time: 493 us; the launch traced here: 487 us
  waiting for transfers between devices  170 us (34%)
  Pallas kernels  166 us (34%)
  starting transfers between devices  95.7 us (19%)
  other arithmetic  22.5 us (5%)
  local copies, waits for them, and re-layouts  17 us (3%)
  between operations  16.8 us (3%)
    ppermute x10, waiting for transfers between devices, swap(): return lax.ppermute(block, AXES, route)  169 us
    ppermute x10, starting transfers between devices, swap(): return lax.ppermute(block, AXES, route)  88.1 us
    pallas_call x1, Pallas kernels, att_bwd(): pl.pallas_call(att_bwd_kernel, grid=(6,), in_specs=[pl.BlockSpec(memory_s...  44.5 us
    pallas_call x1, Pallas kernels, ffn(): pl.pallas_call(ffn_kernel, grid=(4,), in_specs=[pl.BlockSpec(memory_space...  44.1 us
    pallas_call x1, Pallas kernels, att_fwd(): pl.pallas_call(att_fwd_kernel, grid=(6,), in_specs=[pl.BlockSpec(memory_s...  38.4 us
    pallas_call x1, Pallas kernels, qkv_bwd(): pl.pallas_call(body, grid=(blocks,), in_specs=[pl.BlockSpec(memory_space=...  22.3 us
    pallas_call x1, Pallas kernels, qkv_fwd(): pl.pallas_call(body, grid=(blocks,), in_specs=[pl.BlockSpec(memory_space=...  13.5 us
  transfers between devices with their start and end apart: 16, of which 11 were waited for; matrix products, arithmetic and copies ran while one was open for 4% of the time, Pallas kernels for 25%

profile of v3, /device:TPU:0, one launch (start us, length us, event | category | flops | bytes accessed | tf_op | source)
XLA Modules:
  0.0 487.5 jit_solution(6548541401072002585)
XLA Ops:
  7.2 0.9 slice.28
  8.1 2.3 collective-permute-start.1
  10.5 0.8 collective-permute-done.1
  11.3 1.4 fusion.9
  13.6 0.8 copy.17
  14.5 0.8 concatenate.17
  15.4 1.2 broadcast_select_fusion
  16.6 7.8 %collective-permute-start.2 = (bf16[304,768]{1,0:T(8,128)(2,1)S(1)}, bf16[304,768]{1,0:T(8,128)(2,1)S(1)}, u32[]{:S(2)}, u32[]{:S(2)}) collective-permute-start(bf16[304,768]{1,0:T(8,128)(2,1)S(1)} %pad_maximum_fusion), channel_id=1, source_target_pairs={{0,16},{1,17},{2,18},{3,19},{4,20},{5,21},{6,22},{7,23},{8,24},{9,... | collective-permute-start | bytes 1400840 | tf_op jit(solution)/shard_map/ppermute | solution.py:628
  24.5 27.9 %collective-permute-done.2 = bf16[304,768]{1,0:T(8,128)(2,1)S(1)} collective-permute-done((bf16[304,768]{1,0:T(8,128)(2,1)S(1)}, bf16[304,768]{1,0:T(8,128)(2,1)S(1)}, u32[]{:S(2)}, u32[]{:S(2)}) %collective-permute-start.2) | collective-permute-done | bytes 466976 | tf_op jit(solution)/shard_map/ppermute | solution.py:628
  52.5 0.7 collective-permute-start.3
  53.2 27.1 %collective-permute-done.3 = bf16[304,768]{1,0:T(8,128)(2,1)S(1)} collective-permute-done((bf16[304,768]{1,0:T(8,128)(2,1)S(1)}, bf16[304,768]{1,0:T(8,128)(2,1)S(1)}, u32[]{:S(2)}, u32[]{:S(2)}) %collective-permute-start.3) | collective-permute-done | bytes 466976 | tf_op jit(solution)/shard_map/ppermute | solution.py:628
  80.4 1.6 collective-permute-start.4
  82.0 12.6 %collective-permute-done.4.got_ref = bf16[304,768]{1,0:T(8,128)(2,1)S(1)} collective-permute-done((bf16[304,768]{1,0:T(8,128)(2,1)S(1)}, bf16[304,768]{1,0:T(8,128)(2,1)S(1)}, u32[]{:S(2)}, u32[]{:S(2)}) %collective-permute-start.4) | collective-permute-done | bytes 466976 | tf_op jit(solution)/shard_map/ppermute | solution.py:628
  94.6 8.8 %collective-permute-start.5 = (bf16[592,768]{1,0:T(8,128)(2,1)S(1)}, bf16[592,768]{1,0:T(8,128)(2,1)S(1)}, u32[]{:S(2)}, u32[]{:S(2)}) collective-permute-start(bf16[592,768]{1,0:T(8,128)(2,1)S(1)} %join.2.own_ref), channel_id=1, source_target_pairs={{0,4},{1,3},{2,6},{3,1},{4,0},{5,7},{6,2},{7,5},{8,12},{9,11},{10,... | collective-permute-start | bytes 2727944 | tf_op jit(solution)/shard_map/ppermute | solution.py:628
  103.4 2.6 collective-permute-start
  106.0 20.9 %collective-permute-done.5.got_ref = bf16[592,768]{1,0:T(8,128)(2,1)S(1)} collective-permute-done((bf16[592,768]{1,0:T(8,128)(2,1)S(1)}, bf16[592,768]{1,0:T(8,128)(2,1)S(1)}, u32[]{:S(2)}, u32[]{:S(2)}) %collective-permute-start.5) | collective-permute-done | bytes 909344 | tf_op jit(solution)/shard_map/ppermute | solution.py:628
  127.2 1.2 slice.27
  130.3 1.5 constant_dynamic-update-slice_fusion.1
  132.0 1.6 copy-done.8
  133.7 13.5 %qkv_fwd.1 = (bf16[2048,2304]{1,0:T(8,128)(2,1)}, f32[16,768]{1,0:T(8,128)}) custom-call(s32[8]{0:T(128)} %stack.59.refs_0_, bf16[2048,768]{1,0:T(8,128)(2,1)} %copy-done.8, bf16[1168,768]{1,0:T(8,128)(2,1)} %copy-done.1, bf16[1168,768]{1,0:T(8,128)(2,1)} %collective-permute-done.6.refs_3_), custom_call_target="tpu_custom_call" | custom-call | flops 7247757312 | bytes 15728640 | tf_op jit(solution)/shard_map/qkv_fwd/pallas_call | solution.py:468
  147.2 0.8 slice.29
  148.6 1.4 slice_reduce_fusion
  150.0 38.4 %att_fwd.1 = (bf16[1024,768]{1,0:T(8,128)(2,1)}, f32[1024,768]{1,0:T(8,128)}, bf16[1024,768]{1,0:T(8,128)(2,1)}, bf16[2048,768]{1,0:T(8,128)(2,1)}, bf16[2048,768]{1,0:T(8,128)(2,1)}) custom-call(s32[1]{0:T(128)S(6)} %select_n.112.state_ref, bf16[2048,2304]{1,0:T(8,128)(2,1)} %get-tuple-element.35.tail_ref.q_ref.k_ref.v_ref.xt_ref.xq_ref.xk_ref.xv_ref, ...), custom_call_target="tpu_custom_call" | custom-call | flops 19327352832 | bytes 23592960 | tf_op jit(solution)/shard_map/att_fwd/pallas_call | solution.py:111
  188.5 44.1 %ffn.1 = (bf16[1024,768]{1,0:T(8,128)(2,1)}, f32[1024,768]{1,0:T(8,128)}, bf16[1024,768]{1,0:T(8,128)(2,1)}, f32[1,768]{1,0:T(1,128)}, bf16[96,4,24,768]{3,2,1,0:T(8,128)(2,1)}) custom-call(s32[1]{0:T(128)S(6)} %select_n.112.state_ref, bf16[1024,768]{1,0:T(8,128)(2,1)} %x_ref.1, bf16[1024,768]{1,0:T(8,128)(2,1)} %get-tuple-element.37.att_ref.o_ref, ...), custom_call_target="tpu_custom_call" | custom-call | flops 32614907904 | bytes 40894464 | tf_op jit(solution)/shard_map/ffn/pallas_call | solution.py:576
  232.6 44.5 %att_bwd.1 = (bf16[1024,768]{1,0:T(8,128)(2,1)}, bf16[8,768]{1,0:T(8,128)(2,1)}, bf16[2048,768]{1,0:T(8,128)(2,1)}, bf16[2048,768]{1,0:T(8,128)(2,1)}, f32[16,768]{1,0:T(8,128)}) custom-call(s32[1]{0:T(128)S(6)} %select_n.112.state_ref, bf16[1024,768]{1,0:T(8,128)(2,1)} %get-tuple-element.40.q_ref, bf16[2048,768]{1,0:T(8,128)(2,1)} %get-tuple-element.41.k_ref, ...), custom_call_target="tpu_custom_call" | custom-call | flops 48318382080 | bytes 31457280 | tf_op jit(solution)/shard_map/att_bwd/pallas_call | solution.py:229
  277.1 22.3 %qkv_bwd.1 = (bf16[1168,768]{1,0:T(8,128)(2,1)}, f32[1168,768]{1,0:T(8,128)}, bf16[1024,768]{1,0:T(8,128)(2,1)}, f32[1024,768]{1,0:T(8,128)}) custom-call(s32[1]{0:T(128)} %bitcast.11.refs_0_.index_ref, bf16[2048,768]{1,0:T(8,128)(2,1)} %copy-done.8, bf16[1024,768]{1,0:T(8,128)(2,1)} %get-tuple-element.45.refs_2_, bf16[8,768]{1,0:T(8,128)(2,1)} %get-tuple-element.46.refs_3_, ...), custom_call_target="tpu_custom_call" | custom-call | flops 12079595520 | bytes 23592960 | tf_op jit(solution)/shard_map/qkv_bwd/pallas_call | solution.py:354
  299.4 9.5 %collective-permute-start.8 = (bf16[1168,768]{1,0:T(8,128)(2,1)}, bf16[1168,768]{1,0:T(8,128)(2,1)S(1)}, u32[]{:S(2)}, u32[]{:S(2)}) collective-permute-start(bf16[1168,768]{1,0:T(8,128)(2,1)} %get-tuple-element.54), channel_id=1, source_target_pairs={{0,1},{1,0},{2,3},{3,2},{4,5},{5,4},{6,7},{7,6},{8,9},{9,8},{10,11... | collective-permute-start | bytes 5382152 | tf_op jit(solution)/shard_map/ppermute | solution.py:628
  308.9 3.5 collective-permute-done.8.got_ref
  312.4 1.2 copy-done.2
  313.6 2.3 copy-done
  315.8 1.5 copy-done.3
  317.4 1.7 merge.4
  319.1 3.1 collective-permute-start.9
  322.2 1.3 collective-permute-start.7
  323.6 22.4 %collective-permute-done.9.got_ref = bf16[592,768]{1,0:T(8,128)(2,1)S(1)} collective-permute-done((bf16[592,768]{1,0:T(8,128)(2,1)}, bf16[592,768]{1,0:T(8,128)(2,1)S(1)}, u32[]{:S(2)}, u32[]{:S(2)}) %collective-permute-start.9) | collective-permute-done | bytes 909344 | tf_op jit(solution)/shard_map/ppermute | solution.py:628
  346.7 55.6 %collective-permute-start.10 = (bf16[304,768]{1,0:T(8,128)(2,1)S(1)}, bf16[304,768]{1,0:T(8,128)(2,1)S(1)}, u32[]{:S(2)}, u32[]{:S(2)}) collective-permute-start(bf16[304,768]{1,0:T(8,128)(2,1)S(1)} %get-tuple-element.58), channel_id=1, source_target_pairs={{0,4},{1,3},{2,6},{3,1},{4,0},{5,7},{6,2},{7,5},{8,12},{9,11},{10,... | collective-permute-start | bytes 1400840 | tf_op jit(solution)/shard_map/ppermute | solution.py:628
  402.3 11.4 %collective-permute-done.10.got_ref = bf16[304,768]{1,0:T(8,128)(2,1)S(1)} collective-permute-done((bf16[304,768]{1,0:T(8,128)(2,1)S(1)}, bf16[304,768]{1,0:T(8,128)(2,1)S(1)}, u32[]{:S(2)}, u32[]{:S(2)}) %collective-permute-start.10) | collective-permute-done | bytes 466976 | tf_op jit(solution)/shard_map/ppermute | solution.py:628
  413.8 0.9 collective-permute-start.11
  415.6 1.8 fusion.6
  417.4 13.7 %collective-permute-done.11.got_ref = bf16[304,768]{1,0:T(8,128)(2,1)S(1)} collective-permute-done((bf16[304,768]{1,0:T(8,128)(2,1)S(1)}, bf16[304,768]{1,0:T(8,128)(2,1)S(1)}, u32[]{:S(2)}, u32[]{:S(2)}) %collective-permute-start.11) | collective-permute-done | bytes 466976 | tf_op jit(solution)/shard_map/ppermute | solution.py:628
  431.3 3.6 fusion.2
  434.9 29.5 %collective-permute-done.12 = bf16[304,768]{1,0:T(8,128)(2,1)S(1)} collective-permute-done((bf16[304,768]{1,0:T(8,128)(2,1)S(1)}, bf16[304,768]{1,0:T(8,128)(2,1)S(1)}, u32[]{:S(2)}, u32[]{:S(2)}) %collective-permute-start.12) | collective-permute-done | bytes 466976 | tf_op jit(solution)/shard_map/ppermute | solution.py:628
  464.4 1.1 convert_add_fusion
  465.7 1.1 convert_element_type.34
  467.4 1.4 slice_select_fusion
  468.9 1.3 collective-permute-start.13
  470.2 6.0 %fusion.5 = f32[1024,768]{1,0:T(8,128)} fusion(f32[1024,768]{1,0:T(8,128)} %get-tuple-element.39, bf16[1024,768]{1,0:T(8,128)(2,1)S(1)} %copy-done.5, f32[1024,768]{1,0:T(8,128)} %get-tuple-element.51, bf16[1024,768]{1,0:T(8,128)(2,1)} %collective-permute-done.7, f32[1024]{0:T(1024)S(1)} %broadcast_multiply_fusion, f32[768]{0:T(1024)S(1)} %get-tuple-element.68, ...), kind=kLoop, calls=%fused_computation.7 | loop fusion | flops 7077888 | bytes 12594176 | tf_op jit(solution)/shard_map/add | solution.py:795
  476.3 4.1 fusion.17
  (60 shorter events, 5.2 us)
Async XLA Ops:
  7.2 7.4 %copy-start.6 = (f32[1731,128]{1,0:T(8,128)S(1)}, f32[1731,128]{1,0:T(8,128)}, u32[]{:S(2)}) copy-start(f32[1731,128]{1,0:T(8,128)} %param.10) | copy-start | bytes 2658820
  7.2 181.3 %all-gather.2.cloned.1.call-start = ((), (), s32[]{:S(2)}) async-start(), calls=%async_computation.1 | async-start | bytes 14598144 | tf_op jit(solution)/shard_map/all_gather | solution.py:760
  8.1 3.2 collective-permute-start.1
  14.4 451.2 %reduce-scatter.2.cloned.1.call-start = ((), (), s32[]{:S(2)}) async-start(), calls=%async_computation.2 | async-start | bytes 14598144 | tf_op jit(solution)/shard_map/reduce_scatter | solution.py:781
  15.4 88.0 %copy-start.4 = (bf16[1024,768]{1,0:T(8,128)(2,1)S(1)}, bf16[1024,768]{1,0:T(8,128)(2,1)}, u32[]{:S(2)}) copy-start(bf16[1024,768]{1,0:T(8,128)(2,1)} %x_ref.1) | copy-start | bytes 4718596
  16.6 35.7 %collective-permute-start.2 = (bf16[304,768]{1,0:T(8,128)(2,1)S(1)}, bf16[304,768]{1,0:T(8,128)(2,1)S(1)}, u32[]{:S(2)}, u32[]{:S(2)}) collective-permute-start(bf16[304,768]{1,0:T(8,128)(2,1)S(1)} %pad_maximum_fusion), channel_id=1, source_target_pairs={{0,16},{1,17},{2,18},{3,19},{4,20},{5,21},{6,22},{7,23},{8,24},{9,... | collective-permute-start | bytes 1400840 | tf_op jit(solution)/shard_map/ppermute | solution.py:628
  52.5 27.8 %collective-permute-start.3 = (bf16[304,768]{1,0:T(8,128)(2,1)S(1)}, bf16[304,768]{1,0:T(8,128)(2,1)S(1)}, u32[]{:S(2)}, u32[]{:S(2)}) collective-permute-start(bf16[304,768]{1,0:T(8,128)(2,1)S(1)} %fusion.16), channel_id=1, source_target_pairs={{0,8},{1,9},{2,10},{3,11},{4,12},{5,13},{6,14},{7,15},{8,0},{9,1},... | collective-permute-start | bytes 1400840 | tf_op jit(solution)/shard_map/ppermute | solution.py:628
  80.4 14.1 %collective-permute-start.4 = (bf16[304,768]{1,0:T(8,128)(2,1)S(1)}, bf16[304,768]{1,0:T(8,128)(2,1)S(1)}, u32[]{:S(2)}, u32[]{:S(2)}) collective-permute-start(bf16[304,768]{1,0:T(8,128)(2,1)S(1)} %add.146.own_ref), channel_id=1, source_target_pairs={{0,2},{1,5},{2,0},{3,7},{4,6},{5,1},{6,4},{7,3},{8,10},{9,13},{10,... | collective-permute-start | bytes 1400840 | tf_op jit(solution)/shard_map/ppermute | solution.py:628
  94.6 32.3 %collective-permute-start.5 = (bf16[592,768]{1,0:T(8,128)(2,1)S(1)}, bf16[592,768]{1,0:T(8,128)(2,1)S(1)}, u32[]{:S(2)}, u32[]{:S(2)}) collective-permute-start(bf16[592,768]{1,0:T(8,128)(2,1)S(1)} %join.2.own_ref), channel_id=1, source_target_pairs={{0,4},{1,3},{2,6},{3,1},{4,0},{5,7},{6,2},{7,5},{8,12},{9,11},{10,... | collective-permute-start | bytes 2727944 | tf_op jit(solution)/shard_map/ppermute | solution.py:628
  103.4 26.9 %collective-permute-start = (bf16[1024,768]{1,0:T(8,128)(2,1)S(1)}, bf16[1024,768]{1,0:T(8,128)(2,1)}, u32[]{:S(2)}, u32[]{:S(2)}) collective-permute-start(bf16[1024,768]{1,0:T(8,128)(2,1)S(1)} %copy-done.4), channel_id=1, source_target_pairs={{0,1},{1,2},{2,3},{4,5},{5,6},{6,7},{8,9},{9,10},{10,11},{12,13},{... | collective-permute-start | bytes 4718600 | tf_op jit(solution)/shard_map/ppermute | solution.py:622
  127.1 4.9 %copy-start.1 = (bf16[1168,768]{1,0:T(8,128)(2,1)}, bf16[1168,768]{1,0:T(8,128)(2,1)S(1)}, u32[]{:S(2)}) copy-start(bf16[1168,768]{1,0:T(8,128)(2,1)S(1)} %join.3.refs_2_) | copy-start | bytes 5382148
  127.1 5.0 %collective-permute-start.6 = (bf16[1168,768]{1,0:T(8,128)(2,1)S(1)}, bf16[1168,768]{1,0:T(8,128)(2,1)}, u32[]{:S(2)}, u32[]{:S(2)}) collective-permute-start(bf16[1168,768]{1,0:T(8,128)(2,1)S(1)} %join.3.refs_2_), channel_id=1, source_target_pairs={{0,1},{1,0},{2,3},{3,2},{4,5},{5,4},{6,7},{7,6},{8,9},{9,8},{10,11... | collective-permute-start | bytes 5382152 | tf_op jit(solution)/shard_map/ppermute | solution.py:628
  132.0 1.7 copy-start.8
  299.4 13.0 %collective-permute-start.8 = (bf16[1168,768]{1,0:T(8,128)(2,1)}, bf16[1168,768]{1,0:T(8,128)(2,1)S(1)}, u32[]{:S(2)}, u32[]{:S(2)}) collective-permute-start(bf16[1168,768]{1,0:T(8,128)(2,1)} %get-tuple-element.54), channel_id=1, source_target_pairs={{0,1},{1,0},{2,3},{3,2},{4,5},{5,4},{6,7},{7,6},{8,9},{9,8},{10,11... | collective-permute-start | bytes 5382152 | tf_op jit(solution)/shard_map/ppermute | solution.py:628
  312.4 1.2 copy-start.2
  313.6 2.3 copy-start
  315.8 1.5 copy-start.3
  319.1 26.9 %collective-permute-start.9 = (bf16[592,768]{1,0:T(8,128)(2,1)}, bf16[592,768]{1,0:T(8,128)(2,1)S(1)}, u32[]{:S(2)}, u32[]{:S(2)}) collective-permute-start(bf16[592,768]{1,0:T(8,128)(2,1)} %get-tuple-element.56), channel_id=1, source_target_pairs={{0,2},{1,5},{2,0},{3,7},{4,6},{5,1},{6,4},{7,3},{8,10},{9,13},{10,... | collective-permute-start | bytes 2727944 | tf_op jit(solution)/shard_map/ppermute | solution.py:628
  322.2 109.1 %collective-permute-start.7 = (bf16[1024,768]{1,0:T(8,128)(2,1)}, bf16[1024,768]{1,0:T(8,128)(2,1)}, u32[]{:S(2)}, u32[]{:S(2)}) collective-permute-start(bf16[1024,768]{1,0:T(8,128)(2,1)} %get-tuple-element.52), channel_id=1, source_target_pairs={{1,0},{2,1},{3,2},{5,4},{6,5},{7,6},{9,8},{10,9},{11,10},{13,12},{... | collective-permute-start | bytes 4718600 | tf_op jit(solution)/shard_map/ppermute | solution.py:622
  346.7 84.6 %copy-start.5 = (bf16[1024,768]{1,0:T(8,128)(2,1)S(1)}, bf16[1024,768]{1,0:T(8,128)(2,1)}, u32[]{:S(2)}) copy-start(bf16[1024,768]{1,0:T(8,128)(2,1)} %x_ref.1) | copy-start | bytes 4718596
  346.7 67.0 %collective-permute-start.10 = (bf16[304,768]{1,0:T(8,128)(2,1)S(1)}, bf16[304,768]{1,0:T(8,128)(2,1)S(1)}, u32[]{:S(2)}, u32[]{:S(2)}) collective-permute-start(bf16[304,768]{1,0:T(8,128)(2,1)S(1)} %get-tuple-element.58), channel_id=1, source_target_pairs={{0,4},{1,3},{2,6},{3,1},{4,0},{5,7},{6,2},{7,5},{8,12},{9,11},{10,... | collective-permute-start | bytes 1400840 | tf_op jit(solution)/shard_map/ppermute | solution.py:628
  413.8 17.3 %collective-permute-start.11 = (bf16[304,768]{1,0:T(8,128)(2,1)S(1)}, bf16[304,768]{1,0:T(8,128)(2,1)S(1)}, u32[]{:S(2)}, u32[]{:S(2)}) collective-permute-start(bf16[304,768]{1,0:T(8,128)(2,1)S(1)} %get-tuple-element.60), channel_id=1, source_target_pairs={{0,8},{1,9},{2,10},{3,11},{4,12},{5,13},{6,14},{7,15},{8,0},{9,1},... | collective-permute-start | bytes 1400840 | tf_op jit(solution)/shard_map/ppermute | solution.py:628
  431.2 33.2 %collective-permute-start.12 = (bf16[304,768]{1,0:T(8,128)(2,1)S(1)}, bf16[304,768]{1,0:T(8,128)(2,1)S(1)}, u32[]{:S(2)}, u32[]{:S(2)}) collective-permute-start(bf16[304,768]{1,0:T(8,128)(2,1)S(1)} %get-tuple-element.62), channel_id=1, source_target_pairs={{0,16},{1,17},{2,18},{3,19},{4,20},{5,21},{6,22},{7,23},{8,24},{9,... | collective-permute-start | bytes 1400840 | tf_op jit(solution)/shard_map/ppermute | solution.py:628
  468.9 7.4 %collective-permute-start.13 = (f32[96,128]{1,0:T(8,128)S(1)}, f32[96,128]{1,0:T(8,128)S(1)}, u32[]{:S(2)}, u32[]{:S(2)}) collective-permute-start(f32[96,128]{1,0:T(8,128)S(1)} %slice.35), channel_id=1, source_target_pairs={{1,0},{2,1},{3,2},{4,3},{5,4},{6,5},{7,6},{8,7},{9,8},{10,9},{11,1... | collective-permute-start | bytes 147464 | tf_op jit(solution)/shard_map/ppermute | solution.py:616
  470.2 6.0 %slice-start = ((f32[304,768]{1,0:T(8,128)}), f32[16,768]{1,0:T(8,128)S(1)}, s32[]{:S(2)}) async-start(f32[304,768]{1,0:T(8,128)} %convert_add_fusion), calls=%async_computation.3 | async-start | bytes 98304 | tf_op jit(solution)/shard_map/slice | solution.py:814
  470.2 6.1 %copy-start.7 = (f32[1731,128]{1,0:T(8,128)S(1)}, f32[1731,128]{1,0:T(8,128)}, u32[]{:S(2)}) copy-start(f32[1731,128]{1,0:T(8,128)} %param.10) | copy-start | bytes 2658820
Sparse Core Ops, SparseCore 0:
  14.6 129.9 all-gather.1
  232.7 232.9 reduce-scatter.1

commit v4 on v3

--- a/solution.py
+++ b/solution.py
@@ -12,6 +12,7 @@
 SEQ_MIN = 1024
 AXES = ("dp", "ctx")
 QB = 256
+PARTS = 3
 F32 = jnp.float32
 BF = jnp.bfloat16
 NT = (((1,), (1,)), ((), ()))
@@ -103,15 +104,41 @@
         l_ref[rs, :] = jnp.where(lane < 64, sums[1], sums[0])
 
 
-def att_fwd(state, projected, taps, rows):
+def call_in_parts(body, in_specs, out_specs, out_shape, earlier, part, **options):
+    used = len(in_specs)
+
+    def kernel(*refs):
+        body(*refs[:used], *refs[used + len(earlier) :])
+
+    return pl.pallas_call(
+        kernel,
+        grid=(6 // PARTS,),
+        in_specs=in_specs + [pl.BlockSpec(memory_space=pl.ANY)] * len(earlier),
+        out_specs=out_specs,
+        out_shape=out_shape,
+        input_output_aliases={used + i: i for i in range(len(earlier))},
+        compiler_params=pltpu.CompilerParams(vmem_limit_bytes=VMEM_LIMIT),
+        **options,
+    )
+
+
+def columns(part):
+    first = part * (6 // PARTS)
+
     def cols(height, row, off):
-        return pl.BlockSpec((height, 128), lambda p: (row, p + off))
-
-    taps_at = [pl.BlockSpec((3, 128), lambda p, off=off: (0, p + off)) for off in (0, 6, 12)]
-    return pl.pallas_call(
+        return pl.BlockSpec((height, 128), lambda p: (row, p + first + off))
+
+    taps_at = [
+        pl.BlockSpec((3, 128), lambda p, off=off: (0, p + first + off)) for off in (0, 6, 12)
+    ]
+    return cols, taps_at
+
+
+def att_fwd(state, projected, taps, earlier, part, rows):
+    cols, taps_at = columns(part)
+    return call_in_parts(
         att_fwd_kernel,
-        grid=(6,),
-        in_specs=[
+        [
             pl.BlockSpec(memory_space=pltpu.SMEM),
             cols(8, rows // 8 - 1, 0),
             cols(rows, 1, 0),
@@ -119,18 +146,23 @@
             cols(2 * rows, 0, 12),
             *taps_at,
         ],
-        out_specs=[cols(rows, 0, 0)] * 3 + [cols(2 * rows, 0, 0)] * 2,
-        out_shape=[
+        [cols(rows, 0, 0)] * 3 + [cols(2 * rows, 0, 0)] * 2,
+        [
             jax.ShapeDtypeStruct((rows, D), BF),
             jax.ShapeDtypeStruct((rows, D), F32),
             jax.ShapeDtypeStruct((rows, D), BF),
             jax.ShapeDtypeStruct((2 * rows, D), BF),
             jax.ShapeDtypeStruct((2 * rows, D), BF),
         ],
-        compiler_params=pltpu.CompilerParams(vmem_limit_bytes=VMEM_LIMIT),
-        cost_estimate=cost(2 * 2 * 12 * rows * rows * 1.5 * 256, rows * D * 30, 12 * rows * rows * 1.5),
+        earlier,
+        part,
+        cost_estimate=cost(
+            2 * 2 * 12 * rows * rows * 1.5 * 256 / PARTS,
+            rows * D * 30 / PARTS,
+            12 * rows * rows * 1.5 / PARTS,
+        ),
         name="att_fwd",
-    )(state, projected, projected, projected, projected, taps, taps, taps)
+    )(state, projected, projected, projected, projected, taps, taps, taps, *earlier)
 
 
 def three(x, lane, base):
@@ -219,17 +251,13 @@
             tg_ref[3 * j + m : 3 * j + m + 1, :] = s[j]
 
 
-def att_bwd(state, mixed, attended, logs, grad, projected, taps, rows):
-    def cols(height, row, off):
-        return pl.BlockSpec((height, 128), lambda p: (row, p + off))
-
-    taps_at = [pl.BlockSpec((3, 128), lambda p, off=off: (0, p + off)) for off in (0, 6, 12)]
+def att_bwd(state, mixed, attended, logs, grad, projected, taps, earlier, part, rows):
+    cols, taps_at = columns(part)
     own = cols(rows, 0, 0)
     both = cols(2 * rows, 0, 0)
-    return pl.pallas_call(
+    return call_in_parts(
         att_bwd_kernel,
-        grid=(6,),
-        in_specs=[
+        [
             pl.BlockSpec(memory_space=pltpu.SMEM),
             own, both, both, own, own, own,
             cols(8, rows // 8 - 1, 0),
@@ -238,14 +266,16 @@
             cols(2 * rows, 0, 12),
             *taps_at,
         ],
-        out_specs=[own, cols(8, 0, 0), both, both, cols(16, 0, 0)],
-        out_shape=[
+        [own, cols(8, 0, 0), both, both, cols(16, 0, 0)],
+        [
             jax.ShapeDtypeStruct((rows, D), BF),
             jax.ShapeDtypeStruct((8, D), BF),
             jax.ShapeDtypeStruct((2 * rows, D), BF),
             jax.ShapeDtypeStruct((2 * rows, D), BF),
             jax.ShapeDtypeStruct((16, D), F32),
         ],
+        earlier,
+        part,
         scratch_shapes=[
             pltpu.VMEM((rows, 128), BF),
             pltpu.VMEM((rows, 128), BF),
@@ -253,11 +283,14 @@
             pltpu.VMEM((2 * rows, 128), F32),
             pltpu.VMEM((2 * rows, 128), F32),
         ],
-        compiler_params=pltpu.CompilerParams(vmem_limit_bytes=VMEM_LIMIT),
-        cost_estimate=cost(5 * 2 * 12 * rows * rows * 1.5 * 256, rows * D * 40, 12 * rows * rows * 1.5),
+        cost_estimate=cost(
+            5 * 2 * 12 * rows * rows * 1.5 * 256 / PARTS,
+            rows * D * 40 / PARTS,
+            12 * rows * rows * 1.5 / PARTS,
+        ),
         name="att_bwd",
     )(state, *mixed, attended, logs, grad, projected, projected, projected, projected,
-      taps, taps, taps)
+      taps, taps, taps, *earlier)
 
 
 def qkv_bwd_kernel(
@@ -404,21 +437,78 @@
     )(index, keep, got)
 
 
-def join(own, got, height):
+def merge_grid(index, keep, got, taken):
+    height = keep.shape[1]
+
+    def body(index_ref, ka_ref, ga_ref, kb_ref, gb_ref, send_ref, stay_ref):
+        send_ref[...] = (ka_ref[...].astype(F32) + ga_ref[...].astype(F32)).astype(BF)
+        stay_ref[...] = kb_ref[...].astype(F32) + gb_ref[...].astype(F32)
+
+    away = pl.BlockSpec((1, height, D), lambda i, index: (index[i], 0, 0))
+    here = pl.BlockSpec((1, height, D), lambda i, index: (index[taken + i], 0, 0))
+    step = pl.BlockSpec((1, height, D), lambda i, index: (i, 0, 0))
+    return pl.pallas_call(
+        body,
+        grid_spec=pltpu.PrefetchScalarGridSpec(
+            num_scalar_prefetch=1,
+            grid=(taken,),
+            in_specs=[away, away, here, here],
+            out_specs=[step, step],
+        ),
+        out_shape=[
+            jax.ShapeDtypeStruct((taken, height, D), BF),
+            jax.ShapeDtypeStruct((taken, height, D), F32),
+        ],
+        compiler_params=pltpu.CompilerParams(vmem_limit_bytes=32 << 20),
+        cost_estimate=cost(taken * height * D * 2, taken * height * D * 16),
+        name="merge_grid",
+    )(index, keep, got, keep, got)
+
+
+def arrange(index, one, two, taken):
+    half = one.shape[0]
+    height = one.shape[1]
+
+    def body(index_ref, one_ref, two_ref, out_ref):
+        for i in range(taken):
+            at = index_ref[i]
+
+            @pl.when(at < half)
+            def _():
+                out_ref[i] = one_ref[jnp.minimum(at, half - 1)]
+
+            @pl.when(at >= half)
+            def _():
+                out_ref[i] = two_ref[jnp.maximum(at - half, 0)]
+
+    vmem = pl.BlockSpec(memory_space=pltpu.VMEM)
+    return pl.pallas_call(
+        body,
+        in_specs=[pl.BlockSpec(memory_space=pltpu.SMEM), vmem, vmem],
+        out_specs=vmem,
+        out_shape=jax.ShapeDtypeStruct((taken, height, D), BF),
+        compiler_params=pltpu.CompilerParams(vmem_limit_bytes=32 << 20),
+        cost_estimate=cost(taken * height * D, taken * height * D * 8),
+        name="arrange",
+    )(index, one, two)
+
+
+def join(own, got, shared=16):
     rows = own.shape[0]
-    body_rows = rows - 16
+    body_rows = rows - shared
 
     def body(own_ref, got_ref, out_ref):
         out_ref[0:body_rows, :] = own_ref[0:body_rows, :]
         out_ref[body_rows : 2 * body_rows, :] = got_ref[0:body_rows, :]
-        out_ref[2 * body_rows :, :] = own_ref[body_rows:, :] + got_ref[body_rows:, :]
+        if shared:
+            out_ref[2 * body_rows :, :] = own_ref[body_rows:, :] + got_ref[body_rows:, :]
 
     vmem = pl.BlockSpec(memory_space=pltpu.VMEM)
     return pl.pallas_call(
         body,
         in_specs=[vmem, vmem],
         out_specs=vmem,
-        out_shape=jax.ShapeDtypeStruct((2 * body_rows + 16, D), BF),
+        out_shape=jax.ShapeDtypeStruct((2 * body_rows + shared, D), BF),
         compiler_params=pltpu.CompilerParams(vmem_limit_bytes=32 << 20),
         cost_estimate=cost(rows * D, rows * D * 8),
         name="join",
@@ -476,12 +566,13 @@
         out_specs=[
             pl.BlockSpec((height, 3 * D), lambda i: (i, 0)),
             pl.BlockSpec((16, D), lambda i: (0, 0)),
-        ],
+        ]
+        + ([pl.BlockSpec((3 * D, D), lambda i: (0, 0))] if pieces else []),
         out_shape=[
             jax.ShapeDtypeStruct((2 * rows, 3 * D), BF),
             jax.ShapeDtypeStruct((16, D), F32),
-        ],
-        scratch_shapes=[pltpu.VMEM((3 * D, D), BF)] if pieces else [],
+        ]
+        + ([jax.ShapeDtypeStruct((3 * D, D), BF)] if pieces else []),
         compiler_params=pltpu.CompilerParams(vmem_limit_bytes=VMEM_LIMIT),
         cost_estimate=cost(2 * 2 * rows * D * 3 * D, rows * D * 20),
         name="qkv_fwd",
@@ -489,60 +580,99 @@
 
 
 def ffn_kernel(
-    state_ref, x_ref, att_ref, cot_ref, gain_ref, wo_ref, up_ref, down_ref,
-    out_ref, gh_ref, ga_ref, gain_grad_ref, flat_ref,
-    hidden, low, total, back, cot, sq, gb, stage_up, stage_down, stage_out, sems,
+    state_ref, index_ref, x_ref, att_ref, cot_ref, gain_ref, own_ref, got_ref,
+    out_ref, gh_ref, ga_ref, gain_grad_ref, away_ref, here_ref,
+    hidden, low, total, back, cot, sq, gb, weights, stage_up, stage_down, stage_out, in_sems, sems,
 ):
     c = pl.program_id(0)
     rows = x_ref.shape[0]
     blocks = [pl.ds(i * QB, QB) for i in range(rows // QB)]
     last = c == pl.num_programs(0) - 1
-
-    def put_zero(i):
-        return pltpu.make_async_copy(stage_out, flat_ref.at[pl.ds(8 * i, 8)], sems.at[8 + i])
-
-    def put_up(i):
-        return pltpu.make_async_copy(stage_up.at[i], flat_ref.at[pl.ds(32, 32), i], sems.at[i])
-
-    def put_down(i):
-        return pltpu.make_async_copy(stage_down.at[i], flat_ref.at[pl.ds(64 + 8 * i, 8)], sems.at[4 + i])
-
-    def put_out():
-        return pltpu.make_async_copy(stage_out, flat_ref.at[pl.ds(24, 8)], sems.at[11])
+    core = index_ref[24]
+
+    def fetch(k, j):
+        ref = own_ref if k == 0 else got_ref
+        to = weights.at[pl.ds(3 * index_ref[12 * k + j], 3)]
+        return pltpu.make_async_copy(ref.at[pl.ds(3 * j, 3)], to, in_sems.at[12 * k + j])
+
+    def put(source, group, count, column, sem, wait=False):
+        piece = group // 3
+        at = (piece // 2) * 3 + group % 3
+
+        def copy(ref):
+            to = ref.at[pl.ds(at, count)] if column is None else ref.at[pl.ds(at, count), column]
+            return pltpu.make_async_copy(source, to, sems.at[sem])
+
+        if wait:
+            copy(here_ref).wait()
+            return
+        mine = piece % 2 == core
+
+        @pl.when(mine)
+        def _():
+            copy(here_ref).start()
+
+        @pl.when(jnp.logical_not(mine))
+        def _():
+            copy(away_ref).start()
+
+    def put_up(i, wait=False):
+        start = 0
+        k = 0
+        while start < 32:
+            count = min(3 - (8 + start) % 3, 32 - start)
+            put(stage_up.at[i, pl.ds(start, count)], 8 + start, count, i, 20 * i + k, wait)
+            start += count
+            k += 1
+
+    def put_down(i, wait=False):
+        for k in range(8):
+            put(stage_down.at[i, pl.ds(k, 1)], 40 + 8 * i + k, 1, None, 20 * i + 12 + k, wait)
+
+    def put_out(wait=False):
+        for k in range(8):
+            put(stage_out.at[pl.ds(k, 1)], k, 1, None, 80 + k, wait)
+
+    def square(first):
+        return weights[first : first + 8].reshape(D, D)
 
     @pl.when(c == 0)
     def _():
-        stage_out[...] = jnp.zeros(stage_out.shape, BF)
-        for i in range(3):
-            put_zero(i).start()
+        for k in range(2):
+            for j in range(12):
+                fetch(k, j).start()
         cot[...] = jnp.where(state_ref[0] > 0, cot_ref[...], jnp.zeros((), BF))
         total[...] = jnp.zeros(total.shape, F32)
         back[...] = jnp.zeros(back.shape, F32)
+        for k in range(2):
+            for j in range(12):
+                fetch(k, j).wait()
+        wo = square(0)
         for b in blocks:
-            h = x_ref[b, :].astype(F32) + dot(att_ref[b, :], wo_ref[...])
+            h = x_ref[b, :].astype(F32) + dot(att_ref[b, :], wo)
             hidden[b, :] = h
             hat = h * lax.rsqrt(jnp.mean(h * h, axis=-1, keepdims=True) + norm_eps)
             low[b, :] = (hat * gain_ref[...]).astype(BF)
 
-    up = up_ref[...].reshape(D, D)
+    up = weights[8:40, c].reshape(D, D)
+    down = weights[pl.ds(40 + 8 * c, 8)].reshape(D, D)
     for b in blocks:
         act = jnp.maximum(dot(low[b, :], up), 0.0)
         s = (act * act).astype(BF)
         sq[b, :] = s
-        total[b, :] += dot(s, down_ref[...])
-        g = (dot_nt(cot[b, :], down_ref[...]) * 2.0 * act).astype(BF)
+        total[b, :] += dot(s, down)
+        g = (dot_nt(cot[b, :], down) * 2.0 * act).astype(BF)
         gb[b, :] = g
         back[b, :] += dot_nt(g, up)
     stage_down[c] = dot_tn(sq[...], cot[...]).reshape(8, 4, 24, D).astype(BF)
     stage_up[c] = dot_tn(low[...], gb[...]).reshape(32, 24, D).astype(BF)
-    put_down(c).start()
-    put_up(c).start()
+    put_down(c)
+    put_up(c)
 
     @pl.when(last)
     def _():
-        for i in range(3):
-            put_zero(i).wait()
         gain = gain_ref[...]
+        wo = square(0)
         sums = jnp.zeros((1, D), F32)
         for b in blocks:
             h = hidden[b, :]
@@ -557,39 +687,36 @@
             gh_ref[b, :] = grad
             grad_low = grad.astype(BF)
             gb[b, :] = grad_low
-            ga_ref[b, :] = dot_nt(grad_low, wo_ref[...]).astype(BF)
+            ga_ref[b, :] = dot_nt(grad_low, wo).astype(BF)
         gain_grad_ref[...] = sums
         stage_out[...] = dot_tn(att_ref[...], gb[...]).reshape(8, 4, 24, D).astype(BF)
-        put_out().start()
-        for i in range(pl.num_programs(0)):
-            put_down(i).wait()
-            put_up(i).wait()
-        put_out().wait()
-
-
-def ffn(state, tokens, attended, out_grad, gain, wide, rows):
+        put_out()
+        for i in range(4):
+            put_down(i, True)
+            put_up(i, True)
+        put_out(True)
+
+
+def ffn(state, index, tokens, attended, out_grad, gain, own, got, rows):
     def whole(shape):
-        return pl.BlockSpec(shape, lambda c: (0,) * len(shape))
+        return pl.BlockSpec(shape, lambda c: (0,) * len(shape), pipeline_mode=pl.Buffered(1))
 
     act = whole((rows, D))
-    square = wide.reshape(12 * D, D)
+    held = pl.BlockSpec(memory_space=pl.ANY)
+    scalars = pl.BlockSpec(memory_space=pltpu.SMEM)
+    half = (36, 4, 24, D)
     return pl.pallas_call(
         ffn_kernel,
         grid=(4,),
-        in_specs=[
-            pl.BlockSpec(memory_space=pltpu.SMEM),
-            act, act, act, whole((1, D)),
-            pl.BlockSpec((D, D), lambda c: (3, 0)),
-            pl.BlockSpec((32, 1, 24, D), lambda c: (1, c, 0, 0)),
-            pl.BlockSpec((D, D), lambda c: (8 + c, 0)),
-        ],
-        out_specs=[act, act, act, whole((1, D)), pl.BlockSpec(memory_space=pl.ANY)],
+        in_specs=[scalars, scalars, act, act, act, whole((1, D)), held, held],
+        out_specs=[act, act, act, whole((1, D)), held, held],
         out_shape=[
             jax.ShapeDtypeStruct((rows, D), BF),
             jax.ShapeDtypeStruct((rows, D), F32),
             jax.ShapeDtypeStruct((rows, D), BF),
             jax.ShapeDtypeStruct((1, D), F32),
-            jax.ShapeDtypeStruct((96, 4, 24, D), BF),
+            jax.ShapeDtypeStruct(half, BF),
+            jax.ShapeDtypeStruct(half, BF),
         ],
         scratch_shapes=[
             pltpu.VMEM((rows, D), F32),
@@ -599,15 +726,17 @@
             pltpu.VMEM((rows, D), BF),
             pltpu.VMEM((rows, D), BF),
             pltpu.VMEM((rows, D), BF),
+            pltpu.VMEM((72, 4, 24, D), BF),
             pltpu.VMEM((4, 32, 24, D), BF),
             pltpu.VMEM((4, 8, 4, 24, D), BF),
             pltpu.VMEM((8, 4, 24, D), BF),
-            pltpu.SemaphoreType.DMA((12,)),
+            pltpu.SemaphoreType.DMA((24,)),
+            pltpu.SemaphoreType.DMA((88,)),
         ],
         compiler_params=pltpu.CompilerParams(vmem_limit_bytes=60 << 20),
         cost_estimate=cost(2 * rows * D * D * (24 + 3), 2 * 12 * D * D * 2 + rows * D * 16),
         name="ffn",
-    )(state, tokens, attended, out_grad, gain, square, wide, square)
+    )(state, index, tokens, attended, out_grad, gain, own, got)
 
 
 def shift_flat(block, distance):
@@ -620,6 +749,10 @@
     count = lax.axis_size("ctx")
     route = [(i - distance, i) for i in range(count) if 0 <= i - distance < count]
     return lax.ppermute(block, "ctx", route)
+
+
+def after(value, *others):
+    return lax.optimization_barrier((value, *others))[0]
 
 
 def swap(block, even_bit, odd_bit):
@@ -744,49 +877,116 @@
         )
         mine = mine + swap(mine, 16, 16)
         mine = mine + swap(mine, 8, 8)
-        mine = join(mine, swap(mine, 2, 4), height)
-        mine = join(mine, swap(mine, 4, 2), height)
+        rest = after(chunk, mine)
+        mine = join(mine, swap(mine, 2, 4))
+        mine = join(mine, swap(mine, 4, 2))
         got = swap(mine, 1, 1)
-        where_at = []
+        z = place >> 3
+        rest = join(rest, swap(rest, 16, 16), 0)
+        across = swap(rest, 8, 8)
+        codes = [z ^ k for k in (1, 2, 3)]
+        order = [jnp.where(j == 1, 2, jnp.where(j == 2, 1, j)) for j in codes]
+        rest = arrange(
+            jnp.stack(order).astype(jnp.int32), rest.reshape(2, height, D), across.reshape(2, height, D), 3
+        ).reshape(-1, D)
+        across = swap(rest, 2, 4)
+        index = []
+        late_index = []
         for k in (0, 1):
             turn = even if k == 0 else jnp.logical_not(even)
             for j in range(4):
                 near, far = j & 1, j >> 1
                 x_of = x_bit ^ jnp.where(turn, near, far)
                 y_of = y_bit ^ jnp.where(turn, far, near)
-                where_at.append(4 * y_of + 2 * x_of + (core[0] ^ k))
-        index = jnp.stack(where_at).astype(jnp.int32)
-        projected, small = qkv_fwd(index, tokens_both, (mine, got), rows, 4)
-        wide = lax.all_gather(chunk, AXES, axis=0, tiled=True)
+                piece = 4 * y_of + 2 * x_of + (core[0] ^ k)
+                index.append(piece)
+                late_index += [piece, piece + 8, piece + 16]
+        index = jnp.stack(index).astype(jnp.int32)
+        late_index = jnp.stack(late_index + [core[0]]).astype(jnp.int32)
+        projected, small, in_weight = qkv_fwd(index, tokens_both, (mine, got), rows, 4)
     else:
         wide = lax.all_gather(chunk, AXES, axis=0, tiled=True)
         small = lax.psum(small, AXES)[:96].reshape(-1, D)
-        projected, small = qkv_fwd(core, tokens_both, (wide[: 3 * D], small), rows, 0)
+        in_weight = wide[: 3 * D]
+        projected, small = qkv_fwd(core, tokens_both, (in_weight, small), rows, 0)
+        late_index = jnp.arange(25, dtype=jnp.int32) % 24
     gain_first = small[0]
     gain_second = small[1]
     taps = small[2:11].reshape(3, 3 * D)
+
+    forward = []
     if staged:
-        grouped = wide.reshape(96, 4, 24, D)
+        rest = join(after(rest, projected), across, 0)
+        across = swap(rest, 4, 2)
+        forward = att_fwd(after(state_vec, rest), projected, taps, forward, 0, rows)
+        forward = att_fwd(state_vec, projected, taps, forward, 1, rows)
+        rest = join(after(rest, forward[0]), across, 0)
+        across = swap(rest, 1, 1)
+        forward = att_fwd(after(state_vec, rest), projected, taps, forward, 2, rows)
+        own_weights, got_weights = rest.reshape(36, 4, 24, D), across.reshape(36, 4, 24, D)
     else:
+        for part in range(PARTS):
+            forward = att_fwd(state_vec, projected, taps, forward, part, rows)
         grouped = jnp.concatenate(
-            [wide[: 4 * D].reshape(-1, 4, 24, D), regroup(wide[4 * D : 8 * D]), wide[8 * D :].reshape(-1, 4, 24, D)], 0
+            [
+                wide[3 * D : 4 * D].reshape(-1, 4, 24, D),
+                regroup(wide[4 * D : 8 * D]),
+                wide[8 * D :].reshape(-1, 4, 24, D),
+            ],
+            0,
         )
-
-    attn_low, logs, *mixed = att_fwd(state_vec, projected, taps, rows)
-
-    layer_out, grad_hidden, grad_attended, grad_gain_two, flat_grad = ffn(
-        state_vec, tokens, attn_low, out_grad, gain_second[None], grouped, rows
+        own_weights, got_weights = grouped[:36], grouped[36:]
+    attn_low, logs, *mixed = forward
+
+    layer_out, grad_hidden, grad_attended, grad_gain_two, away_grad, here_grad = ffn(
+        state_vec, late_index, tokens, attn_low, out_grad, gain_second[None], own_weights, got_weights, rows
     )
+
+    def backward(start, done, part):
+        return att_bwd(
+            start, mixed, attn_low, logs, grad_attended, projected, taps, done, part, rows
+        )
+
     if staged:
-        late_chunk = lax.psum_scatter(
-            flat_grad.reshape(12 * D, D), AXES, scatter_dimension=0, tiled=True
+        stay = [jnp.where(even, 2 * j + x_bit, 2 * y_bit + j) for j in range(2)]
+        away = [jnp.where(even, 2 * j + 1 - x_bit, 2 * (1 - y_bit) + j) for j in range(2)]
+        pick_plane = jnp.stack(away + stay).astype(jnp.int32)
+        other = jnp.where(even, y_bit, x_bit)
+        pick_line = jnp.stack([1 - other, other]).astype(jnp.int32)
+
+        def of_quarters(pick, held):
+            half = pick.shape[0] // 2
+            steps = [pick[s * half + j] + held * t for s in range(2) for t in range(3) for j in range(half)]
+            return jnp.stack(steps)
+
+        late_keep = here_grad.reshape(12, height, D)
+        late_got = swap(away_grad.reshape(12, height, D), 1, 1)
+        done = backward(state_vec, [], 0)
+        late_send, late_keep = merge_grid(
+            after(of_quarters(pick_plane, 4), done[4]), late_keep, late_got, 6
         )
-
-    *back, tap_grads = att_bwd(
-        state_vec, mixed, attn_low, logs, grad_attended, projected, taps, rows
-    )
+        late_got = swap(late_send, 2, 4)
+        done = backward(after(state_vec, late_send), done, 1)
+        late_send, late_keep = merge_grid(
+            after(of_quarters(pick_line, 2), done[4]), late_keep, late_got, 3
+        )
+        late_got = swap(late_send, 4, 2)
+        done = backward(after(state_vec, late_send), done, 2)
+        z_even = (z & 1) == 0
+        low_pair = [jnp.where(z_even, 0, 0), jnp.where(z_even, 2, 1)]
+        high_pair = [jnp.where(z_even, 0, 0), jnp.where(z_even, 1, 2)]
+        pick_z = jnp.stack(low_pair + high_pair).astype(jnp.int32)
+        late_send, late_keep = merge_grid(after(pick_z, done[4]), late_keep, late_got, 2)
+        late_got = swap(late_send, 8, 8)
+        sums_state = after(core, late_send)
+    else:
+        done = []
+        for part in range(PARTS):
+            done = backward(state_vec, done, part)
+        sums_state = core
+    *back, tap_grads = done
     sums = qkv_bwd(
-        core, tokens_both, back, wide, gain_first[None], grad_gain_two, tap_grads, rows,
+        sums_state, tokens_both, back, in_weight, gain_first[None], grad_gain_two, tap_grads, rows,
         4 if staged else 0,
     )
     grads_before, grad_normed_one = sums[2:]
@@ -799,29 +999,32 @@
     if staged:
         send, keep = sums[:2]
         got = swap(send, 1, 1)
-        stay = [jnp.where(even, 2 * j + x_bit, 2 * y_bit + j) for j in range(2)]
-        away = [jnp.where(even, 2 * j + 1 - x_bit, 2 * (1 - y_bit) + j) for j in range(2)]
-        send, keep = merge(jnp.stack(away + stay), keep, got, height, 2)
+        high = z >> 1
+        pick_last = jnp.stack([1 - high, high]).astype(jnp.int32)
+        late_send, late_keep = merge_grid(after(pick_last, send), late_keep, late_got, 1)
+        late_got = swap(late_send, 16, 16)
+        send, keep = merge(pick_plane, keep, got, height, 2)
         got = swap(send, 2, 4)
-        other = jnp.where(even, y_bit, x_bit)
-        send, keep = merge(jnp.stack([1 - other, other]), keep, got, height, 1)
+        send, keep = merge(pick_line, keep, got, height, 1)
         got = swap(send, 4, 2)
         send, keep = merge(core, keep, got, height, 0)
         got = swap(send, 8, 8)
         send, keep = merge(core, keep, got, height, 0)
         got = swap(send, 16, 16)
         first = keep + got.astype(F32)
+        late_chunk = late_keep[0] + late_got[0].astype(F32)
         small_grad = first[height:].reshape(-1, 128)
-        late_grad = late_chunk.astype(F32)
-        late_grad = jnp.where(in_up, ungroup(late_grad).reshape(3, 4, 24, D), late_grad.reshape(3, 4, 24, D))
+        late_grad = jnp.where(in_up, ungroup(late_chunk).reshape(3, 4, 24, D), late_chunk.reshape(3, 4, 24, D))
         chunk_grad = jnp.where(place < count // 4, first[:height], late_grad.reshape(-1, D))
     else:
+        flat_grad = jnp.stack([here_grad.reshape(12, 3, 4, 24, D), away_grad.reshape(12, 3, 4, 24, D)], 1)
+        flat_grad = flat_grad.reshape(72, 4, 24, D)
         wide_grad = jnp.concatenate(
             [
                 sums[0],
-                flat_grad[24:32].reshape(-1, D),
-                ungroup(flat_grad[32:64]).reshape(-1, D),
-                flat_grad[64:].reshape(-1, D),
+                flat_grad[:8].reshape(-1, D),
+                ungroup(flat_grad[8:40]).reshape(-1, D),
+                flat_grad[40:].reshape(-1, D),
             ],
             0,
         )

time: 493 us -> 483 us (0.980)
  waiting for transfers between devices: 170 us -> 128 us
  Pallas kernels: 166 us -> 200 us
  between operations: 16.8 us -> 3.44 us
  local copies, waits for them, and re-layouts: 17 us -> 28.8 us
    ppermute x10 -> x20, waiting for transfers between devices: 169 us -> 128 us  [swap(): return lax.ppermute(block, AXES, route)]
    pallas_call x3 -> x12, Pallas kernels: 127 us -> 155 us  [the longest x3 51 us: att_bwd(): call_in_parts(att_bwd_kernel, [pl.BlockSpec(memory_space=pltpu.SMEM), own...]
    unnamed x19 -> x53, local copies, waits for them, and re-layouts: 8.21 us -> 14.6 us
    pallas_call x2 -> x5, Pallas kernels: 0.18 us -> 6.11 us  [join(): pl.pallas_call(body, in_specs=[vmem, vmem], out_specs=vmem, out_shape=jax...]
    ppermute x10 -> x20, starting transfers between devices: 88.1 us -> 86.2 us  [swap(): return lax.ppermute(block, AXES, route)]
  transfers between devices with their start and end apart: 16 -> 24, of which waited for: 11 -> 14; matrix products, arithmetic and copies ran while one was open for 4% -> 5% of each run, Pallas kernels for 25% -> 24%
where the time goes in v4:
time: 483 us; the launch traced here: 474 us
  Pallas kernels  200 us (41%)
  waiting for transfers between devices  128 us (27%)
  starting transfers between devices  93.5 us (19%)
  local copies, waits for them, and re-layouts  28.8 us (6%)
  other arithmetic  19.9 us (4%)
    ppermute x20, waiting for transfers between devices, swap(): return lax.ppermute(block, AXES, route)  128 us
    ppermute x20, starting transfers between devices, swap(): return lax.ppermute(block, AXES, route)  86.2 us
    pallas_call x3, Pallas kernels, att_bwd(): call_in_parts(att_bwd_kernel, [pl.BlockSpec(memory_space=pltpu.SMEM), own...  51 us
    pallas_call x1, Pallas kernels, ffn(): pl.pallas_call(ffn_kernel, grid=(4,), in_specs=[scalars, scalars, act, ac...  48.3 us
    pallas_call x3, Pallas kernels, att_fwd(): call_in_parts(att_fwd_kernel, [pl.BlockSpec(memory_space=pltpu.SMEM), col...  44.2 us
    pallas_call x1, Pallas kernels, qkv_bwd(): pl.pallas_call(body, grid=(blocks,), in_specs=[pl.BlockSpec(memory_space=...  22 us
    unnamed x53, local copies, waits for them, and re-layouts  14.6 us
    pallas_call x1, Pallas kernels, qkv_fwd(): pl.pallas_call(body, grid=(blocks,), in_specs=[pl.BlockSpec(memory_space=...  13.5 us
  transfers between devices with their start and end apart: 24, of which 14 were waited for; matrix products, arithmetic and copies ran while one was open for 5% of the time, Pallas kernels for 24%

profile of v4, /device:TPU:0, one launch (start us, length us, event | category | flops | bytes accessed | tf_op | source)
XLA Modules:
  0.0 473.8 jit_solution(9708928216902961968)
XLA Ops:
  1.5 2.3 collective-permute-start
  3.8 2.3 concatenate.16
  8.8 6.2 %collective-permute-start.1 = (bf16[304,768]{1,0:T(8,128)(2,1)S(1)}, bf16[304,768]{1,0:T(8,128)(2,1)S(1)}, u32[]{:S(2)}, u32[]{:S(2)}) collective-permute-start(bf16[304,768]{1,0:T(8,128)(2,1)S(1)} %pad_maximum_fusion), channel_id=1, source_target_pairs={{0,16},{1,17},{2,18},{3,19},{4,20},{5,21},{6,22},{7,23},{8,24},{9,... | collective-permute-start | bytes 1400840 | tf_op jit(solution)/shard_map/ppermute | solution.py:761
  15.0 20.0 %collective-permute-done.1 = bf16[304,768]{1,0:T(8,128)(2,1)S(1)} collective-permute-done((bf16[304,768]{1,0:T(8,128)(2,1)S(1)}, bf16[304,768]{1,0:T(8,128)(2,1)S(1)}, u32[]{:S(2)}, u32[]{:S(2)}) %collective-permute-start.1) | collective-permute-done | bytes 466976 | tf_op jit(solution)/shard_map/ppermute | solution.py:761
  35.8 10.9 %collective-permute-done.2 = bf16[304,768]{1,0:T(8,128)(2,1)S(1)} collective-permute-done((bf16[304,768]{1,0:T(8,128)(2,1)S(1)}, bf16[304,768]{1,0:T(8,128)(2,1)S(1)}, u32[]{:S(2)}, u32[]{:S(2)}) %collective-permute-start.2) | collective-permute-done | bytes 466976 | tf_op jit(solution)/shard_map/ppermute | solution.py:761
  46.8 2.6 collective-permute-start.6
  49.4 6.5 %collective-permute-done.6.got_ref = bf16[304,768]{1,0:T(8,128)(2,1)S(1)} collective-permute-done((bf16[304,768]{1,0:T(8,128)(2,1)S(1)}, bf16[304,768]{1,0:T(8,128)(2,1)S(1)}, u32[]{:S(2)}, u32[]{:S(2)}) %collective-permute-start.6) | collective-permute-done | bytes 466976 | tf_op jit(solution)/shard_map/ppermute | solution.py:761
  56.0 1.6 collective-permute-start.7
  57.6 2.9 collective-permute-start.3
  60.5 2.5 collective-permute-start.5
  62.9 6.5 %collective-permute-done.7.got_ref = bf16[592,768]{1,0:T(8,128)(2,1)S(1)} collective-permute-done((bf16[592,768]{1,0:T(8,128)(2,1)S(1)}, bf16[592,768]{1,0:T(8,128)(2,1)S(1)}, u32[]{:S(2)}, u32[]{:S(2)}) %collective-permute-start.7) | collective-permute-done | bytes 909344 | tf_op jit(solution)/shard_map/ppermute | solution.py:761
  70.7 8.0 %collective-permute-done.3.got_ref = bf16[288,768]{1,0:T(8,128)(2,1)S(1)} collective-permute-done((bf16[288,768]{1,0:T(8,128)(2,1)S(1)}, bf16[288,768]{1,0:T(8,128)(2,1)S(1)}, u32[]{:S(2)}, u32[]{:S(2)}) %collective-permute-start.3) | collective-permute-done | bytes 442400 | tf_op jit(solution)/shard_map/ppermute | solution.py:761
  79.7 19.9 %collective-permute-done.4 = bf16[576,768]{1,0:T(8,128)(2,1)S(1)} collective-permute-done((bf16[576,768]{1,0:T(8,128)(2,1)S(1)}, bf16[576,768]{1,0:T(8,128)(2,1)S(1)}, u32[]{:S(2)}, u32[]{:S(2)}) %collective-permute-start.4) | collective-permute-done | bytes 884768 | tf_op jit(solution)/shard_map/ppermute | solution.py:761
  101.3 1.5 constant_dynamic-update-slice_fusion.1
  102.8 1.5 constant_dynamic-update-slice_fusion.refs_1_
  104.3 1.6 copy-done.17
  106.0 13.5 %qkv_fwd.1 = (bf16[2048,2304]{1,0:T(8,128)(2,1)}, f32[16,768]{1,0:T(8,128)}, bf16[2304,768]{1,0:T(8,128)(2,1)}) custom-call(s32[8]{0:T(128)} %stack.213.refs_0_, bf16[2048,768]{1,0:T(8,128)(2,1)} %copy-done.17, bf16[1168,768]{1,0:T(8,128)(2,1)} %join.7.refs_2_, bf16[1168,768]{1,0:T(8,128)(2,1)} %collective-permute-done.8.refs_3_), custom_call_target="tpu_custom_call" | custom-call | flops 7247757312 | bytes 15728640 | tf_op jit(solution)/shard_map/qkv_fwd/pallas_call | solution.py:558
  122.0 2.1 collective-permute-start.10
  127.3 14.5 %att_fwd.3 = (bf16[1024,768]{1,0:T(8,128)(2,1)}, f32[1024,768]{1,0:T(8,128)}, bf16[1024,768]{1,0:T(8,128)(2,1)}, bf16[2048,768]{1,0:T(8,128)(2,1)}, bf16[2048,768]{1,0:T(8,128)(2,1)}) custom-call(s32[1]{0:T(128)S(6)} %select_n.139.refs_0_.state_ref, bf16[2048,2304]{1,0:T(8,128)(2,1)} %get-tuple-element.78.refs_1_.refs_2_.refs_3_.refs_4_.refs_7_.refs_8_.refs_9_.refs_10_, ...), custom_call_target="tpu_custom_call" | custom-call | flops 6442450944 | bytes 7864320 | tf_op jit(solution)/shard_map/att_fwd/pallas_call | solution.py:139
  141.8 14.7 %att_fwd.4 = (bf16[1024,768]{1,0:T(8,128)(2,1)}, f32[1024,768]{1,0:T(8,128)}, bf16[1024,768]{1,0:T(8,128)(2,1)}, bf16[2048,768]{1,0:T(8,128)(2,1)}, bf16[2048,768]{1,0:T(8,128)(2,1)}) custom-call(s32[1]{0:T(128)S(6)} %select_n.139.refs_0_.state_ref, ...), custom_call_target="tpu_custom_call", output_to_operand_aliasing={{0}: (8, {}), {1}: (9, {}), {2}: (10, {}), {3}: (11, {}), {... | custom-call | flops 6442450944 | bytes 7864320 | tf_op jit(solution)/shard_map/att_fwd/pallas_call | solution.py:139
  156.6 4.5 join.9
  162.3 15.0 %att_fwd.5 = (bf16[1024,768]{1,0:T(8,128)(2,1)}, f32[1024,768]{1,0:T(8,128)}, bf16[1024,768]{1,0:T(8,128)(2,1)}, bf16[2048,768]{1,0:T(8,128)(2,1)}, bf16[2048,768]{1,0:T(8,128)(2,1)}) custom-call(s32[1]{0:T(128)S(6)} %select_n.139.refs_0_.state_ref, ...), custom_call_target="tpu_custom_call", output_to_operand_aliasing={{0}: (8, {}), {1}: (9, {}), {2}: (10, {}), {3}: (11, {}), {... | custom-call | flops 6442450944 | bytes 7864320 | tf_op jit(solution)/shard_map/att_fwd/pallas_call | solution.py:139
  177.3 48.3 %ffn.1 = (bf16[1024,768]{1,0:T(8,128)(2,1)}, f32[1024,768]{1,0:T(8,128)}, bf16[1024,768]{1,0:T(8,128)(2,1)}, f32[1,768]{1,0:T(1,128)}, bf16[36,4,24,768]{3,2,1,0...) custom-call(s32[1]{0:T(128)S(6)} %select_n.139.refs_0_.state_ref, s32[25]{0:T(128)} %stack.208.index_ref, ...), custom_call_target="tpu_custom_call" | custom-call | flops 32614907904 | bytes 40894464 | tf_op jit(solution)/shard_map/ffn/pallas_call | solution.py:708
  226.3 16.9 %att_bwd.3 = (bf16[1024,768]{1,0:T(8,128)(2,1)}, bf16[8,768]{1,0:T(8,128)(2,1)}, bf16[2048,768]{1,0:T(8,128)(2,1)}, bf16[2048,768]{1,0:T(8,128)(2,1)}, f32[16,768]{1,0:T(8,128)}) custom-call(s32[1]{0:T(128)S(6)} %select_n.139.refs_0_.state_ref, bf16[1024,768]{1,0:T(8,128)(2,1)} %get-tuple-element.97.refs_1_, bf16[2048,768]{1,0:T(8,128)(2,1)} %get-tuple-element.98.refs_2_, ...), custom_call_target="tpu_custom_call" | custom-call | flops 16106127360 | bytes 10485760 | tf_op jit(solution)/shard_map/att_bwd/pallas_call | solution.py:258
  243.2 6.3 %merge_grid.4 = (bf16[6,288,768]{2,1,0:T(8,128)(2,1)}, f32[6,288,768]{2,1,0:T(8,128)S(1)}) custom-call(s32[12]{0:T(128)S(1)} %stack.236.index_ref, bf16[12,288,768]{2,1,0:T(8,128)(2,1)S(1)} %bitcast.77, bf16[12,288,768]{2,1,0:T(8,128)(2,1)} %collective-permute-done.12.ga_ref.gb_ref, bf16[12,288,768]{2,1,0:T(8,128)(2,1)S(1)} %bitcast.78, ...), custom_call_target="tpu_custom_call" | custom-call | flops 2654208 | bytes 21233664 | tf_op jit(solution)/shard_map/merge_grid/pallas_call | solution.py:450
  249.6 2.4 copy-done
  251.9 42.1 %collective-permute-start.13 = (bf16[6,288,768]{2,1,0:T(8,128)(2,1)}, bf16[6,288,768]{2,1,0:T(8,128)(2,1)S(1)}, u32[]{:S(2)}, u32[]{:S(2)}) collective-permute-start(bf16[6,288,768]{2,1,0:T(8,128)(2,1)} %get-tuple-element.106), channel_id=1, source_target_pairs={{0,2},{1,5},{2,0},{3,7},{4,6},{5,1},{6,4},{7,3},{8,10},{9,13},{10,... | collective-permute-start | bytes 7962632 | tf_op jit(solution)/shard_map/ppermute | solution.py:761
  294.2 16.8 %att_bwd.4 = (bf16[1024,768]{1,0:T(8,128)(2,1)}, bf16[8,768]{1,0:T(8,128)(2,1)}, bf16[2048,768]{1,0:T(8,128)(2,1)}, bf16[2048,768]{1,0:T(8,128)(2,1)}, f32[16,768]{1,0:T(8,128)}) custom-call(s32[1]{0:T(128)S(6)} %select_n.139.refs_0_.state_ref, ...), custom_call_target="tpu_custom_call", output_to_operand_aliasing={{0}: (14, {}), {1}: (15, {}), {2}: (16, {}), {3}: (17, {}),... | custom-call | flops 16106127360 | bytes 10485760 | tf_op jit(solution)/shard_map/att_bwd/pallas_call | solution.py:258
  311.0 13.3 %collective-permute-done.13.ga_ref.gb_ref = bf16[6,288,768]{2,1,0:T(8,128)(2,1)S(1)} collective-permute-done((bf16[6,288,768]{2,1,0:T(8,128)(2,1)}, bf16[6,288,768]{2,1,0:T(8,128)(2,1)S(1)}, u32[]{:S(2)}, u32[]{:S(2)}) %collective-permute-start.13) | collective-permute-done | bytes 2654240 | tf_op jit(solution)/shard_map/ppermute | solution.py:761
  324.3 2.4 merge_grid.5
  326.6 1.5 copy-done.1
  328.2 17.4 %att_bwd.5 = (bf16[1024,768]{1,0:T(8,128)(2,1)}, bf16[8,768]{1,0:T(8,128)(2,1)}, bf16[2048,768]{1,0:T(8,128)(2,1)}, bf16[2048,768]{1,0:T(8,128)(2,1)}, f32[16,768]{1,0:T(8,128)}) custom-call(s32[1]{0:T(128)S(6)} %select_n.139.refs_0_.state_ref, ...), custom_call_target="tpu_custom_call", output_to_operand_aliasing={{0}: (14, {}), {1}: (15, {}), {2}: (16, {}), {3}: (17, {}),... | custom-call | flops 16106127360 | bytes 10485760 | tf_op jit(solution)/shard_map/att_bwd/pallas_call | solution.py:258
  347.1 22.0 %qkv_bwd.1 = (bf16[1168,768]{1,0:T(8,128)(2,1)}, f32[1168,768]{1,0:T(8,128)}, bf16[1024,768]{1,0:T(8,128)(2,1)}, f32[1024,768]{1,0:T(8,128)}) custom-call(s32[1]{0:T(128)} %bitcast.24.refs_0_.index_ref, bf16[2048,768]{1,0:T(8,128)(2,1)} %copy-done.17, bf16[1024,768]{1,0:T(8,128)(2,1)} %get-tuple-element.126.refs_2_, ...), custom_call_target="tpu_custom_call" | custom-call | flops 12079595520 | bytes 23592960 | tf_op jit(solution)/shard_map/qkv_bwd/pallas_call | solution.py:387
  369.3 3.8 collective-permute-done.16.got_ref
  373.1 2.0 copy-done.5
  376.1 13.1 %collective-permute-start.17 = (bf16[592,768]{1,0:T(8,128)(2,1)S(1)}, bf16[592,768]{1,0:T(8,128)(2,1)S(1)}, u32[]{:S(2)}, u32[]{:S(2)}) collective-permute-start(bf16[592,768]{1,0:T(8,128)(2,1)S(1)} %get-tuple-element.137), channel_id=1, source_target_pairs={{0,2},{1,5},{2,0},{3,7},{4,6},{5,1},{6,4},{7,3},{8,10},{9,13},{10,... | collective-permute-start | bytes 2727944 | tf_op jit(solution)/shard_map/ppermute | solution.py:761
  389.2 5.5 %collective-permute-start.21 = (bf16[2,288,768]{2,1,0:T(8,128)(2,1)S(1)}, bf16[2,288,768]{2,1,0:T(8,128)(2,1)S(1)}, u32[]{:S(2)}, u32[]{:S(2)}) collective-permute-start(bf16[2,288,768]{2,1,0:T(8,128)(2,1)S(1)} %copy-done.11), channel_id=1, source_target_pairs={{0,8},{1,9},{2,10},{3,11},{4,12},{5,13},{6,14},{7,15},{8,0},{9,1},... | collective-permute-start | bytes 2654216 | tf_op jit(solution)/shard_map/ppermute | solution.py:761
  396.1 4.4 collective-permute-done.17.got_ref
  403.0 5.1 %collective-permute-done.21.ga_ref.gb_ref = bf16[2,288,768]{2,1,0:T(8,128)(2,1)S(1)} collective-permute-done((bf16[2,288,768]{2,1,0:T(8,128)(2,1)S(1)}, bf16[2,288,768]{2,1,0:T(8,128)(2,1)S(1)}, u32[]{:S(2)}, u32[]{:S(2)}) %collective-permute-start.21) | collective-permute-done | bytes 884768 | tf_op jit(solution)/shard_map/ppermute | solution.py:761
  412.3 1.8 fusion.6
  416.4 3.2 collective-permute-start.19
  419.7 8.7 %collective-permute-done.22 = bf16[1,288,768]{2,1,0:T(8,128)(2,1)S(1)} collective-permute-done((bf16[1,288,768]{2,1,0:T(8,128)(2,1)}, bf16[1,288,768]{2,1,0:T(8,128)(2,1)S(1)}, u32[]{:S(2)}, u32[]{:S(2)}) %collective-permute-start.22) | collective-permute-done | bytes 442400 | tf_op jit(solution)/shard_map/ppermute | solution.py:761
  430.9 2.4 collective-permute-done.19.got_ref
  433.4 4.3 collective-permute-start.20
  437.7 3.9 fusion.2
  441.6 17.5 %collective-permute-done.20 = bf16[304,768]{1,0:T(8,128)(2,1)S(1)} collective-permute-done((bf16[304,768]{1,0:T(8,128)(2,1)S(1)}, bf16[304,768]{1,0:T(8,128)(2,1)S(1)}, u32[]{:S(2)}, u32[]{:S(2)}) %collective-permute-start.20) | collective-permute-done | bytes 466976 | tf_op jit(solution)/shard_map/ppermute | solution.py:761
  462.6 5.5 %fusion.5 = f32[1024,768]{1,0:T(8,128)} fusion(f32[1024,768]{1,0:T(8,128)} %get-tuple-element.96, bf16[1024,768]{1,0:T(8,128)(2,1)} %x_ref.1, f32[1024,768]{1,0:T(8,128)S(1)} %copy-done.12, bf16[1024,768]{1,0:T(8,128)(2,1)} %collective-permute-done.15, f32[1024]{0:T(1024)S(1)} %broadcast_multiply_fusion, f32[768]{0:T(1024)S(1)} %get-tuple-element.152, ...), kind=kLoop, calls=%fused_computation.7 | loop fusion | flops 7077888 | bytes 12594176 | tf_op jit(solution)/shard_map/add | solution.py:995
  469.4 4.3 fusion.17
  (128 shorter events, 34.4 us)
Async XLA Ops:
  1.5 4.8 %collective-permute-start = (bf16[96,128]{1,0:T(8,128)(2,1)S(1)}, bf16[96,128]{1,0:T(8,128)(2,1)S(1)}, u32[]{:S(2)}, u32[]{:S(2)}) collective-permute-start(bf16[96,128]{1,0:T(8,128)(2,1)S(1)} %slice.28), channel_id=1, source_target_pairs={{0,1},{1,2},{2,3},{3,4},{4,5},{5,6},{6,7},{7,8},{8,9},{9,10},{10,1... | collective-permute-start | bytes 73736 | tf_op jit(solution)/shard_map/ppermute | solution.py:745
  6.2 2.6 copy-start.20
  8.8 26.2 %collective-permute-start.1 = (bf16[304,768]{1,0:T(8,128)(2,1)S(1)}, bf16[304,768]{1,0:T(8,128)(2,1)S(1)}, u32[]{:S(2)}, u32[]{:S(2)}) collective-permute-start(bf16[304,768]{1,0:T(8,128)(2,1)S(1)} %pad_maximum_fusion), channel_id=1, source_target_pairs={{0,16},{1,17},{2,18},{3,19},{4,20},{5,21},{6,22},{7,23},{8,24},{9,... | collective-permute-start | bytes 1400840 | tf_op jit(solution)/shard_map/ppermute | solution.py:761
  35.1 11.6 %collective-permute-start.2 = (bf16[304,768]{1,0:T(8,128)(2,1)S(1)}, bf16[304,768]{1,0:T(8,128)(2,1)S(1)}, u32[]{:S(2)}, u32[]{:S(2)}) collective-permute-start(bf16[304,768]{1,0:T(8,128)(2,1)S(1)} %fusion.16), channel_id=1, source_target_pairs={{0,8},{1,9},{2,10},{3,11},{4,12},{5,13},{6,14},{7,15},{8,0},{9,1},... | collective-permute-start | bytes 1400840 | tf_op jit(solution)/shard_map/ppermute | solution.py:761
  46.8 9.2 %collective-permute-start.6 = (bf16[304,768]{1,0:T(8,128)(2,1)S(1)}, bf16[304,768]{1,0:T(8,128)(2,1)S(1)}, u32[]{:S(2)}, u32[]{:S(2)}) collective-permute-start(bf16[304,768]{1,0:T(8,128)(2,1)S(1)} %add.257.own_ref), channel_id=1, source_target_pairs={{0,2},{1,5},{2,0},{3,7},{4,6},{5,1},{6,4},{7,3},{8,10},{9,13},{10,... | collective-permute-start | bytes 1400840 | tf_op jit(solution)/shard_map/ppermute | solution.py:761
  56.0 13.4 %collective-permute-start.7 = (bf16[592,768]{1,0:T(8,128)(2,1)S(1)}, bf16[592,768]{1,0:T(8,128)(2,1)S(1)}, u32[]{:S(2)}, u32[]{:S(2)}) collective-permute-start(bf16[592,768]{1,0:T(8,128)(2,1)S(1)} %join.6.own_ref), channel_id=1, source_target_pairs={{0,4},{1,3},{2,6},{3,1},{4,0},{5,7},{6,2},{7,5},{8,12},{9,11},{10,... | collective-permute-start | bytes 2727944 | tf_op jit(solution)/shard_map/ppermute | solution.py:761
  57.6 21.2 %collective-permute-start.3 = (bf16[288,768]{1,0:T(8,128)(2,1)S(1)}, bf16[288,768]{1,0:T(8,128)(2,1)S(1)}, u32[]{:S(2)}, u32[]{:S(2)}) collective-permute-start(bf16[288,768]{1,0:T(8,128)(2,1)S(1)} %bitcast.81), channel_id=1, source_target_pairs={{0,16},{1,17},{2,18},{3,19},{4,20},{5,21},{6,22},{7,23},{8,24},{9,... | collective-permute-start | bytes 1327112 | tf_op jit(solution)/shard_map/ppermute | solution.py:761
  60.5 40.8 %collective-permute-start.5 = (bf16[1024,768]{1,0:T(8,128)(2,1)}, bf16[1024,768]{1,0:T(8,128)(2,1)}, u32[]{:S(2)}, u32[]{:S(2)}) collective-permute-start(bf16[1024,768]{1,0:T(8,128)(2,1)} %x_ref.1), channel_id=1, source_target_pairs={{0,1},{1,2},{2,3},{4,5},{5,6},{6,7},{8,9},{9,10},{10,11},{12,13},{... | collective-permute-start | bytes 4718600 | tf_op jit(solution)/shard_map/ppermute | solution.py:751
  70.7 33.6 %collective-permute-start.8 = (bf16[1168,768]{1,0:T(8,128)(2,1)}, bf16[1168,768]{1,0:T(8,128)(2,1)}, u32[]{:S(2)}, u32[]{:S(2)}) collective-permute-start(bf16[1168,768]{1,0:T(8,128)(2,1)} %join.7.refs_2_), channel_id=1, source_target_pairs={{0,1},{1,0},{2,3},{3,2},{4,5},{5,4},{6,7},{7,6},{8,9},{9,8},{10,11... | collective-permute-start | bytes 5382152 | tf_op jit(solution)/shard_map/ppermute | solution.py:761
  78.8 20.7 %collective-permute-start.4 = (bf16[576,768]{1,0:T(8,128)(2,1)S(1)}, bf16[576,768]{1,0:T(8,128)(2,1)S(1)}, u32[]{:S(2)}, u32[]{:S(2)}) collective-permute-start(bf16[576,768]{1,0:T(8,128)(2,1)S(1)} %join.5), channel_id=1, source_target_pairs={{0,8},{1,9},{2,10},{3,11},{4,12},{5,13},{6,14},{7,15},{8,0},{9,1},... | collective-permute-start | bytes 2654216 | tf_op jit(solution)/shard_map/ppermute | solution.py:761
  100.2 4.1 copy-start.3
  100.2 19.2 %collective-permute-start.9 = (bf16[864,768]{1,0:T(8,128)(2,1)S(1)}, bf16[864,768]{1,0:T(8,128)(2,1)S(1)}, u32[]{:S(2)}, u32[]{:S(2)}) collective-permute-start(bf16[864,768]{1,0:T(8,128)(2,1)S(1)} %bitcast.79), channel_id=1, source_target_pairs={{0,2},{1,5},{2,0},{3,7},{4,6},{5,1},{6,4},{7,3},{8,10},{9,13},{10,... | collective-permute-start | bytes 3981320 | tf_op jit(solution)/shard_map/ppermute | solution.py:761
  104.3 1.7 copy-start.17
  106.0 14.6 %copy-start.4 = (bf16[3,288,768]{2,1,0:T(8,128)(2,1)S(1)}, bf16[3,288,768]{2,1,0:T(8,128)(2,1)}, u32[]{:S(2)}) copy-start(bf16[3,288,768]{2,1,0:T(8,128)(2,1)} %copy-done.3) | copy-start | bytes 3981316
  120.5 1.3 copy-start.7
  121.9 4.8 %copy-start.18 = (f32[16,768]{1,0:T(8,128)S(1)}, f32[16,768]{1,0:T(8,128)}, u32[]{:S(2)}) copy-start(f32[16,768]{1,0:T(8,128)} %get-tuple-element.80) | copy-start | bytes 147460
  122.0 34.5 %collective-permute-start.10 = (bf16[1728,768]{1,0:T(8,128)(2,1)S(1)}, bf16[1728,768]{1,0:T(8,128)(2,1)}, u32[]{:S(2)}, u32[]{:S(2)}) collective-permute-start(bf16[1728,768]{1,0:T(8,128)(2,1)S(1)} %join.8.own_ref), channel_id=1, source_target_pairs={{0,4},{1,3},{2,6},{3,1},{4,0},{5,7},{6,2},{7,5},{8,12},{9,11},{10,... | collective-permute-start | bytes 7962632 | tf_op jit(solution)/shard_map/ppermute | solution.py:761
  161.1 16.2 %collective-permute-start.11 = (bf16[3456,768]{1,0:T(8,128)(2,1)}, bf16[3456,768]{1,0:T(8,128)(2,1)}, u32[]{:S(2)}, u32[]{:S(2)}) collective-permute-start(bf16[3456,768]{1,0:T(8,128)(2,1)} %join.9), channel_id=1, source_target_pairs={{0,1},{1,0},{2,3},{3,2},{4,5},{5,4},{6,7},{7,6},{8,9},{9,8},{10,11... | collective-permute-start | bytes 15925256 | tf_op jit(solution)/shard_map/ppermute | solution.py:761
  225.6 17.6 %collective-permute-start.12 = (bf16[12,288,768]{2,1,0:T(8,128)(2,1)}, bf16[12,288,768]{2,1,0:T(8,128)(2,1)}, u32[]{:S(2)}, u32[]{:S(2)}) collective-permute-start(bf16[12,288,768]{2,1,0:T(8,128)(2,1)} %bitcast.87), channel_id=1, source_target_pairs={{0,1},{1,0},{2,3},{3,2},{4,5},{5,4},{6,7},{7,6},{8,9},{9,8},{10,11... | collective-permute-start | bytes 15925256 | tf_op jit(solution)/shard_map/ppermute | solution.py:761
  226.2 17.0 %slice-start.2 = ((s8[5308416]{0:T(1024)(128)(4,1)}), s8[4194304]{0:T(1024)(128)(4,1)S(1)}, s32[]{:S(2)}) async-start(s8[5308416]{0:T(1024)(128)(4,1)} %bitcast.75), calls=%async_computation.2 | async-start | bytes 8388608
  226.3 17.0 %slice-start.3 = ((s8[5308416]{0:T(1024)(128)(4,1)}), s8[1114112]{0:T(1024)(128)(4,1)S(1)}, s32[]{:S(2)}) async-start(s8[5308416]{0:T(1024)(128)(4,1)} %bitcast.75), calls=%async_computation.3 | async-start | bytes 2228224
  249.6 2.4 copy-start
  251.9 72.3 %collective-permute-start.13 = (bf16[6,288,768]{2,1,0:T(8,128)(2,1)}, bf16[6,288,768]{2,1,0:T(8,128)(2,1)S(1)}, u32[]{:S(2)}, u32[]{:S(2)}) collective-permute-start(bf16[6,288,768]{2,1,0:T(8,128)(2,1)} %get-tuple-element.106), channel_id=1, source_target_pairs={{0,2},{1,5},{2,0},{3,7},{4,6},{5,1},{6,4},{7,3},{8,10},{9,13},{10,... | collective-permute-start | bytes 7962632 | tf_op jit(solution)/shard_map/ppermute | solution.py:761
  294.2 30.0 %slice-start = ((s8[5308416]{0:T(1024)(128)(4,1)}), s8[4194304]{0:T(1024)(128)(4,1)S(1)}, s32[]{:S(2)}) async-start(s8[5308416]{0:T(1024)(128)(4,1)} %bitcast.73), calls=%async_computation | async-start | bytes 8388608
  294.2 30.0 %slice-start.1 = ((s8[5308416]{0:T(1024)(128)(4,1)}), s8[1114112]{0:T(1024)(128)(4,1)S(1)}, s32[]{:S(2)}) async-start(s8[5308416]{0:T(1024)(128)(4,1)} %bitcast.73), calls=%async_computation.1 | async-start | bytes 2228224
  326.6 1.5 copy-start.1
  328.2 18.0 %collective-permute-start.14 = (bf16[3,288,768]{2,1,0:T(8,128)(2,1)}, bf16[3,288,768]{2,1,0:T(8,128)(2,1)S(1)}, u32[]{:S(2)}, u32[]{:S(2)}) collective-permute-start(bf16[3,288,768]{2,1,0:T(8,128)(2,1)} %get-tuple-element.115), channel_id=1, source_target_pairs={{0,4},{1,3},{2,6},{3,1},{4,0},{5,7},{6,2},{7,5},{8,12},{9,11},{10,... | collective-permute-start | bytes 3981320 | tf_op jit(solution)/shard_map/ppermute | solution.py:761
  328.2 18.0 %copy-start.2 = (f32[3,288,768]{2,1,0:T(8,128)S(1)}, f32[3,288,768]{2,1,0:T(8,128)}, u32[]{:S(2)}) copy-start(f32[3,288,768]{2,1,0:T(8,128)} %copy-done.1) | copy-start | bytes 7962628
  347.1 22.0 %copy-start.10 = (bf16[2,288,768]{2,1,0:T(8,128)(2,1)}, bf16[2,288,768]{2,1,0:T(8,128)(2,1)S(1)}, u32[]{:S(2)}) copy-start(bf16[2,288,768]{2,1,0:T(8,128)(2,1)S(1)} %get-tuple-element.124) | copy-start | bytes 2654212
  369.1 4.0 collective-permute-start.16
  373.1 2.0 copy-start.5
  375.1 14.1 %copy-start.11 = (bf16[2,288,768]{2,1,0:T(8,128)(2,1)S(1)}, bf16[2,288,768]{2,1,0:T(8,128)(2,1)}, u32[]{:S(2)}) copy-start(bf16[2,288,768]{2,1,0:T(8,128)(2,1)} %copy-done.10) | copy-start | bytes 2654212
  376.1 24.4 %collective-permute-start.17 = (bf16[592,768]{1,0:T(8,128)(2,1)S(1)}, bf16[592,768]{1,0:T(8,128)(2,1)S(1)}, u32[]{:S(2)}, u32[]{:S(2)}) collective-permute-start(bf16[592,768]{1,0:T(8,128)(2,1)S(1)} %get-tuple-element.137), channel_id=1, source_target_pairs={{0,2},{1,5},{2,0},{3,7},{4,6},{5,1},{6,4},{7,3},{8,10},{9,13},{10,... | collective-permute-start | bytes 2727944 | tf_op jit(solution)/shard_map/ppermute | solution.py:761
  389.2 18.9 %collective-permute-start.21 = (bf16[2,288,768]{2,1,0:T(8,128)(2,1)S(1)}, bf16[2,288,768]{2,1,0:T(8,128)(2,1)S(1)}, u32[]{:S(2)}, u32[]{:S(2)}) collective-permute-start(bf16[2,288,768]{2,1,0:T(8,128)(2,1)S(1)} %copy-done.11), channel_id=1, source_target_pairs={{0,8},{1,9},{2,10},{3,11},{4,12},{5,13},{6,14},{7,15},{8,0},{9,1},... | collective-permute-start | bytes 2654216 | tf_op jit(solution)/shard_map/ppermute | solution.py:761
  394.7 42.9 %collective-permute-start.15 = (bf16[1024,768]{1,0:T(8,128)(2,1)}, bf16[1024,768]{1,0:T(8,128)(2,1)}, u32[]{:S(2)}, u32[]{:S(2)}) collective-permute-start(bf16[1024,768]{1,0:T(8,128)(2,1)} %get-tuple-element.133), channel_id=1, source_target_pairs={{1,0},{2,1},{3,2},{5,4},{6,5},{7,6},{9,8},{10,9},{11,10},{13,12},{... | collective-permute-start | bytes 4718600 | tf_op jit(solution)/shard_map/ppermute | solution.py:751
  402.9 11.2 %collective-permute-start.18 = (bf16[304,768]{1,0:T(8,128)(2,1)}, bf16[304,768]{1,0:T(8,128)(2,1)}, u32[]{:S(2)}, u32[]{:S(2)}) collective-permute-start(bf16[304,768]{1,0:T(8,128)(2,1)} %get-tuple-element.139), channel_id=1, source_target_pairs={{0,4},{1,3},{2,6},{3,1},{4,0},{5,7},{6,2},{7,5},{8,12},{9,11},{10,... | collective-permute-start | bytes 1400840 | tf_op jit(solution)/shard_map/ppermute | solution.py:761
  409.5 18.8 %collective-permute-start.22 = (bf16[1,288,768]{2,1,0:T(8,128)(2,1)}, bf16[1,288,768]{2,1,0:T(8,128)(2,1)S(1)}, u32[]{:S(2)}, u32[]{:S(2)}) collective-permute-start(bf16[1,288,768]{2,1,0:T(8,128)(2,1)} %get-tuple-element.147), channel_id=1, source_target_pairs={{0,16},{1,17},{2,18},{3,19},{4,20},{5,21},{6,22},{7,23},{8,24},{9,... | collective-permute-start | bytes 1327112 | tf_op jit(solution)/shard_map/ppermute | solution.py:761
  414.1 1.2 copy-start.9
  416.4 16.9 %collective-permute-start.19 = (bf16[304,768]{1,0:T(8,128)(2,1)S(1)}, bf16[304,768]{1,0:T(8,128)(2,1)S(1)}, u32[]{:S(2)}, u32[]{:S(2)}) collective-permute-start(bf16[304,768]{1,0:T(8,128)(2,1)S(1)} %get-tuple-element.141), channel_id=1, source_target_pairs={{0,8},{1,9},{2,10},{3,11},{4,12},{5,13},{6,14},{7,15},{8,0},{9,1},... | collective-permute-start | bytes 1400840 | tf_op jit(solution)/shard_map/ppermute | solution.py:761
  433.4 25.7 %collective-permute-start.20 = (bf16[304,768]{1,0:T(8,128)(2,1)S(1)}, bf16[304,768]{1,0:T(8,128)(2,1)S(1)}, u32[]{:S(2)}, u32[]{:S(2)}) collective-permute-start(bf16[304,768]{1,0:T(8,128)(2,1)S(1)} %get-tuple-element.143), channel_id=1, source_target_pairs={{0,16},{1,17},{2,18},{3,19},{4,20},{5,21},{6,22},{7,23},{8,24},{9,... | collective-permute-start | bytes 1400840 | tf_op jit(solution)/shard_map/ppermute | solution.py:761
  437.7 21.5 %copy-start.14 = (f32[1,288,768]{2,1,0:T(8,128)S(1)}, f32[1,288,768]{2,1,0:T(8,128)}, u32[]{:S(2)}) copy-start(f32[1,288,768]{2,1,0:T(8,128)} %copy-done.13) | copy-start | bytes 2654212
  437.7 21.5 %copy-start.16 = (f32[288,768]{1,0:T(8,128)S(1)}, f32[288,768]{1,0:T(8,128)}, u32[]{:S(2)}) copy-start(f32[288,768]{1,0:T(8,128)} %reshape.127) | copy-start | bytes 2654212
  437.7 21.6 %copy-start.21 = (pred[288]{0:T(512)(128)(4,1)S(1)}, pred[288]{0:T(512)(128)(4,1)}, u32[]{:S(2)}) copy-start(pred[288]{0:T(512)(128)(4,1)} %broadcast_in_dim.57) | copy-start | bytes 868
  441.6 21.0 %copy-start.12 = (f32[1024,768]{1,0:T(8,128)S(1)}, f32[1024,768]{1,0:T(8,128)}, u32[]{:S(2)}) copy-start(f32[1024,768]{1,0:T(8,128)} %get-tuple-element.132) | copy-start | bytes 9437188
  459.3 1.2 copy-start.15
  461.3 8.0 %collective-permute-start.23 = (f32[96,128]{1,0:T(8,128)S(1)}, f32[96,128]{1,0:T(8,128)S(1)}, u32[]{:S(2)}, u32[]{:S(2)}) collective-permute-start(f32[96,128]{1,0:T(8,128)S(1)} %slice.35), channel_id=1, source_target_pairs={{1,0},{2,1},{3,2},{4,3},{5,4},{6,5},{7,6},{8,7},{9,8},{10,9},{11,1... | collective-permute-start | bytes 147464 | tf_op jit(solution)/shard_map/ppermute | solution.py:745
  462.6 6.7 %slice-start.4 = ((f32[304,768]{1,0:T(8,128)}), f32[16,768]{1,0:T(8,128)S(1)}, s32[]{:S(2)}) async-start(f32[304,768]{1,0:T(8,128)} %copy-done.15), calls=%async_computation.4 | async-start | bytes 98304 | tf_op jit(solution)/shard_map/slice | solution.py:1016
  462.6 6.8 %copy-start.19 = (f32[1731]{0:T(1024)S(1)}, f32[1731]{0:T(1024)}, u32[]{:S(2)}) copy-start(f32[1731]{0:T(1024)} %get-tuple-element.156) | copy-start | bytes 20776
  (3 other events, 2.9 us)

commit v5 on v4

--- a/solution.py
+++ b/solution.py
@@ -755,9 +755,13 @@
     return lax.optimization_barrier((value, *others))[0]
 
 
-def swap(block, even_bit, odd_bit):
+def swap(block, even_bit, odd_bit, planes=None):
     count = lax.axis_size(AXES)
-    route = [(i, i ^ (odd_bit if i & 1 else even_bit)) for i in range(count)]
+    route = [
+        (i, i ^ (odd_bit if i & 1 else even_bit))
+        for i in range(count)
+        if planes is None or i >> 3 in planes
+    ]
     return lax.ppermute(block, AXES, route)
 
 
@@ -875,21 +879,15 @@
         mine = jnp.concatenate(
             [jnp.where(place < count // 4, chunk, jnp.zeros((), BF)), small.astype(BF).reshape(-1, D)], 0
         )
-        mine = mine + swap(mine, 16, 16)
+        mine = mine + swap(mine, 16, 16, (0, 3))
         mine = mine + swap(mine, 8, 8)
         rest = after(chunk, mine)
         mine = join(mine, swap(mine, 2, 4))
         mine = join(mine, swap(mine, 4, 2))
         got = swap(mine, 1, 1)
         z = place >> 3
-        rest = join(rest, swap(rest, 16, 16), 0)
+        rest = join(rest, swap(rest, 16, 16, (1, 2, 3)), 0)
         across = swap(rest, 8, 8)
-        codes = [z ^ k for k in (1, 2, 3)]
-        order = [jnp.where(j == 1, 2, jnp.where(j == 2, 1, j)) for j in codes]
-        rest = arrange(
-            jnp.stack(order).astype(jnp.int32), rest.reshape(2, height, D), across.reshape(2, height, D), 3
-        ).reshape(-1, D)
-        across = swap(rest, 2, 4)
         index = []
         late_index = []
         for k in (0, 1):
@@ -904,6 +902,12 @@
         index = jnp.stack(index).astype(jnp.int32)
         late_index = jnp.stack(late_index + [core[0]]).astype(jnp.int32)
         projected, small, in_weight = qkv_fwd(index, tokens_both, (mine, got), rows, 4)
+        codes = [z ^ k for k in (1, 2, 3)]
+        order = [jnp.where(j == 1, 2, jnp.where(j == 2, 1, j)) for j in codes]
+        rest = arrange(
+            after(jnp.stack(order).astype(jnp.int32), projected), rest.reshape(2, height, D), across.reshape(2, height, D), 3
+        ).reshape(-1, D)
+        across = swap(rest, 2, 4)
     else:
         wide = lax.all_gather(chunk, AXES, axis=0, tiled=True)
         small = lax.psum(small, AXES)[:96].reshape(-1, D)
@@ -916,10 +920,10 @@
 
     forward = []
     if staged:
-        rest = join(after(rest, projected), across, 0)
+        forward = att_fwd(after(state_vec, rest), projected, taps, forward, 0, rows)
+        rest = join(after(rest, forward[0]), across, 0)
         across = swap(rest, 4, 2)
-        forward = att_fwd(after(state_vec, rest), projected, taps, forward, 0, rows)
-        forward = att_fwd(state_vec, projected, taps, forward, 1, rows)
+        forward = att_fwd(after(state_vec, rest), projected, taps, forward, 1, rows)
         rest = join(after(rest, forward[0]), across, 0)
         across = swap(rest, 1, 1)
         forward = att_fwd(after(state_vec, rest), projected, taps, forward, 2, rows)
@@ -998,21 +1002,21 @@
 
     if staged:
         send, keep = sums[:2]
-        got = swap(send, 1, 1)
         high = z >> 1
         pick_last = jnp.stack([1 - high, high]).astype(jnp.int32)
         late_send, late_keep = merge_grid(after(pick_last, send), late_keep, late_got, 1)
-        late_got = swap(late_send, 16, 16)
+        late_got = swap(late_send, 16, 16, (0, 1, 3))
+        got = swap(after(send, late_send), 1, 1)
         send, keep = merge(pick_plane, keep, got, height, 2)
         got = swap(send, 2, 4)
         send, keep = merge(pick_line, keep, got, height, 1)
         got = swap(send, 4, 2)
         send, keep = merge(core, keep, got, height, 0)
         got = swap(send, 8, 8)
-        send, keep = merge(core, keep, got, height, 0)
-        got = swap(send, 16, 16)
+        late_chunk = late_keep[0] + late_got[0].astype(F32)
+        send, keep = merge(after(core, input_grad, late_chunk), keep, got, height, 0)
+        got = swap(send, 16, 16, (1, 2))
         first = keep + got.astype(F32)
-        late_chunk = late_keep[0] + late_got[0].astype(F32)
         small_grad = first[height:].reshape(-1, 128)
         late_grad = jnp.where(in_up, ungroup(late_chunk).reshape(3, 4, 24, D), late_chunk.reshape(3, 4, 24, D))
         chunk_grad = jnp.where(place < count // 4, first[:height], late_grad.reshape(-1, D))

time: 483 us -> 456 us (0.944); the launches traced: 474 us -> 452 us
  starting transfers between devices: 93.5 us -> 78.3 us
  local copies, waits for them, and re-layouts: 28.8 us -> 19.6 us
  waiting for transfers between devices: 128 us -> 137 us
  Pallas kernels: 200 us -> 195 us
    ppermute x20, starting transfers between devices: 86.2 us -> 70.9 us  [swap(): return lax.ppermute(block, AXES, route)]
    ppermute x20, waiting for transfers between devices: 128 us -> 136 us  [swap(): return lax.ppermute(block, AXES, route)]
    unnamed x53 -> x39, local copies, waits for them, and re-layouts: 14.6 us -> 7.89 us
  transfers between devices with their start and end apart: 24 -> 24, of which waited for: 14 -> 15; matrix products, arithmetic and copies ran while one was open for 5% -> 5% of each run, Pallas kernels for 24% -> 29%
where the time goes in v5:
time: 456 us; the launch traced here: 452 us
  Pallas kernels  195 us (43%)
  waiting for transfers between devices  137 us (30%)
  starting transfers between devices  78.3 us (17%)
  local copies, waits for them, and re-layouts  19.6 us (4%)
  other arithmetic  19.1 us (4%)
    ppermute x20, waiting for transfers between devices, swap(): return lax.ppermute(block, AXES, route)  136 us
    ppermute x20, starting transfers between devices, swap(): return lax.ppermute(block, AXES, route)  70.9 us
    pallas_call x3, Pallas kernels, att_bwd(): call_in_parts(att_bwd_kernel, [pl.BlockSpec(memory_space=pltpu.SMEM), own...  51.1 us
    pallas_call x1, Pallas kernels, ffn(): pl.pallas_call(ffn_kernel, grid=(4,), in_specs=[scalars, scalars, act, ac...  48.3 us
    pallas_call x3, Pallas kernels, att_fwd(): call_in_parts(att_fwd_kernel, [pl.BlockSpec(memory_space=pltpu.SMEM), col...  44.2 us
    pallas_call x1, Pallas kernels, qkv_bwd(): pl.pallas_call(body, grid=(blocks,), in_specs=[pl.BlockSpec(memory_space=...  21.7 us
    pallas_call x1, Pallas kernels, qkv_fwd(): pl.pallas_call(body, grid=(blocks,), in_specs=[pl.BlockSpec(memory_space=...  13.2 us
    pallas_call x4, Pallas kernels, merge_grid(): pl.pallas_call(body, grid_spec=pltpu.PrefetchScalarGridSpec(num_scalar_pr...  10.3 us
  transfers between devices with their start and end apart: 24, of which 15 were waited for; matrix products, arithmetic and copies ran while one was open for 5% of the time, Pallas kernels for 29%

profile of v5, /device:TPU:0, one launch (start us, length us, event | category | flops | bytes accessed | tf_op | source)
XLA Modules:
  0.0 451.7 jit_solution(369521149023117587)
XLA Ops:
  1.5 2.3 collective-permute-start.1
  3.8 2.3 concatenate.17
  8.8 8.1 %collective-permute-start.2 = (bf16[304,768]{1,0:T(8,128)(2,1)S(1)}, bf16[304,768]{1,0:T(8,128)(2,1)S(1)}, u32[]{:S(2)}, u32[]{:S(2)}) collective-permute-start(bf16[304,768]{1,0:T(8,128)(2,1)S(1)} %pad_maximum_fusion), channel_id=1, source_target_pairs={{0,16},{1,17},{2,18},{3,19},{4,20},{5,21},{6,22},{7,23},{24,8},{25... | collective-permute-start | bytes 1400840 | tf_op jit(solution)/shard_map/ppermute | solution.py:765
  16.8 9.1 %collective-permute-done.2 = bf16[304,768]{1,0:T(8,128)(2,1)S(1)} collective-permute-done((bf16[304,768]{1,0:T(8,128)(2,1)S(1)}, bf16[304,768]{1,0:T(8,128)(2,1)S(1)}, u32[]{:S(2)}, u32[]{:S(2)}) %collective-permute-start.2) | collective-permute-done | bytes 466976 | tf_op jit(solution)/shard_map/ppermute | solution.py:765
  26.1 2.4 collective-permute-start.3
  28.5 9.0 %collective-permute-done.3 = bf16[304,768]{1,0:T(8,128)(2,1)S(1)} collective-permute-done((bf16[304,768]{1,0:T(8,128)(2,1)S(1)}, bf16[304,768]{1,0:T(8,128)(2,1)S(1)}, u32[]{:S(2)}, u32[]{:S(2)}) %collective-permute-start.3) | collective-permute-done | bytes 466976 | tf_op jit(solution)/shard_map/ppermute | solution.py:765
  37.6 3.4 collective-permute-start.4
  41.1 6.5 %collective-permute-done.4.got_ref = bf16[304,768]{1,0:T(8,128)(2,1)S(1)} collective-permute-done((bf16[304,768]{1,0:T(8,128)(2,1)S(1)}, bf16[304,768]{1,0:T(8,128)(2,1)S(1)}, u32[]{:S(2)}, u32[]{:S(2)}) %collective-permute-start.4) | collective-permute-done | bytes 466976 | tf_op jit(solution)/shard_map/ppermute | solution.py:765
  47.7 1.6 collective-permute-start.5
  49.3 2.5 collective-permute-start
  51.7 9.3 %collective-permute-done.5.got_ref = bf16[592,768]{1,0:T(8,128)(2,1)S(1)} collective-permute-done((bf16[592,768]{1,0:T(8,128)(2,1)S(1)}, bf16[592,768]{1,0:T(8,128)(2,1)S(1)}, u32[]{:S(2)}, u32[]{:S(2)}) %collective-permute-start.5) | collective-permute-done | bytes 909344 | tf_op jit(solution)/shard_map/ppermute | solution.py:765
  63.3 22.8 %collective-permute-done.7.got_ref = bf16[288,768]{1,0:T(8,128)(2,1)S(1)} collective-permute-done((bf16[288,768]{1,0:T(8,128)(2,1)S(1)}, bf16[288,768]{1,0:T(8,128)(2,1)S(1)}, u32[]{:S(2)}, u32[]{:S(2)}) %collective-permute-start.7) | collective-permute-done | bytes 442400 | tf_op jit(solution)/shard_map/ppermute | solution.py:765
  87.8 1.5 constant_dynamic-update-slice_fusion.refs_1_
  89.3 1.6 copy-done.9
  90.9 13.2 %qkv_fwd.1 = (bf16[2048,2304]{1,0:T(8,128)(2,1)}, f32[16,768]{1,0:T(8,128)}, bf16[2304,768]{1,0:T(8,128)(2,1)}) custom-call(s32[8]{0:T(128)} %stack.213.refs_0_, bf16[2048,768]{1,0:T(8,128)(2,1)} %copy-done.9, bf16[1168,768]{1,0:T(8,128)(2,1)} %copy-done.4, bf16[1168,768]{1,0:T(8,128)(2,1)} %collective-permute-done.6.refs_3_), custom_call_target="tpu_custom_call" | custom-call | flops 7247757312 | bytes 15728640 | tf_op jit(solution)/shard_map/qkv_fwd/pallas_call | solution.py:558
  104.2 3.3 collective-permute-done.8
  108.3 2.1 collective-permute-start.9
  113.6 14.6 %att_fwd.3 = (bf16[1024,768]{1,0:T(8,128)(2,1)}, f32[1024,768]{1,0:T(8,128)}, bf16[1024,768]{1,0:T(8,128)(2,1)}, bf16[2048,768]{1,0:T(8,128)(2,1)}, bf16[2048,768]{1,0:T(8,128)(2,1)}) custom-call(s32[1]{0:T(128)S(6)} %select_n.139.refs_0_.state_ref, bf16[2048,2304]{1,0:T(8,128)(2,1)} %get-tuple-element.81.refs_1_.refs_2_.refs_3_.refs_4_.refs_7_.refs_8_.refs_9_.refs_10_, ...), custom_call_target="tpu_custom_call" | custom-call | flops 6442450944 | bytes 7864320 | tf_op jit(solution)/shard_map/att_fwd/pallas_call | solution.py:139
  128.3 1.6 collective-permute-start.10
  129.9 14.7 %att_fwd.4 = (bf16[1024,768]{1,0:T(8,128)(2,1)}, f32[1024,768]{1,0:T(8,128)}, bf16[1024,768]{1,0:T(8,128)(2,1)}, bf16[2048,768]{1,0:T(8,128)(2,1)}, bf16[2048,768]{1,0:T(8,128)(2,1)}) custom-call(s32[1]{0:T(128)S(6)} %select_n.139.refs_0_.state_ref, ...), custom_call_target="tpu_custom_call", output_to_operand_aliasing={{0}: (8, {}), {1}: (9, {}), {2}: (10, {}), {3}: (11, {}), {... | custom-call | flops 6442450944 | bytes 7864320 | tf_op jit(solution)/shard_map/att_fwd/pallas_call | solution.py:139
  144.6 15.8 %collective-permute-done.10.got_ref = bf16[1728,768]{1,0:T(8,128)(2,1)S(1)} collective-permute-done((bf16[1728,768]{1,0:T(8,128)(2,1)S(1)}, bf16[1728,768]{1,0:T(8,128)(2,1)S(1)}, u32[]{:S(2)}, u32[]{:S(2)}) %collective-permute-start.10) | collective-permute-done | bytes 2654240 | tf_op jit(solution)/shard_map/ppermute | solution.py:765
  160.4 2.7 join.9
  164.3 14.9 %att_fwd.5 = (bf16[1024,768]{1,0:T(8,128)(2,1)}, f32[1024,768]{1,0:T(8,128)}, bf16[1024,768]{1,0:T(8,128)(2,1)}, bf16[2048,768]{1,0:T(8,128)(2,1)}, bf16[2048,768]{1,0:T(8,128)(2,1)}) custom-call(s32[1]{0:T(128)S(6)} %select_n.139.refs_0_.state_ref, ...), custom_call_target="tpu_custom_call", output_to_operand_aliasing={{0}: (8, {}), {1}: (9, {}), {2}: (10, {}), {3}: (11, {}), {... | custom-call | flops 6442450944 | bytes 7864320 | tf_op jit(solution)/shard_map/att_fwd/pallas_call | solution.py:139
  179.3 48.3 %ffn.1 = (bf16[1024,768]{1,0:T(8,128)(2,1)}, f32[1024,768]{1,0:T(8,128)}, bf16[1024,768]{1,0:T(8,128)(2,1)}, f32[1,768]{1,0:T(1,128)}, bf16[36,4,24,768]{3,2,1,0...) custom-call(s32[1]{0:T(128)S(6)} %select_n.139.refs_0_.state_ref, s32[25]{0:T(128)} %stack.208.index_ref, ...), custom_call_target="tpu_custom_call" | custom-call | flops 32614907904 | bytes 40894464 | tf_op jit(solution)/shard_map/ffn/pallas_call | solution.py:708
  228.2 16.9 %att_bwd.3 = (bf16[1024,768]{1,0:T(8,128)(2,1)}, bf16[8,768]{1,0:T(8,128)(2,1)}, bf16[2048,768]{1,0:T(8,128)(2,1)}, bf16[2048,768]{1,0:T(8,128)(2,1)}, f32[16,768]{1,0:T(8,128)}) custom-call(s32[1]{0:T(128)S(6)} %select_n.139.refs_0_.state_ref, bf16[1024,768]{1,0:T(8,128)(2,1)} %get-tuple-element.103.refs_1_, bf16[2048,768]{1,0:T(8,128)(2,1)} %get-tuple-element.104.refs_2_, ...), custom_call_target="tpu_custom_call" | custom-call | flops 16106127360 | bytes 10485760 | tf_op jit(solution)/shard_map/att_bwd/pallas_call | solution.py:258
  245.2 6.3 %merge_grid.4 = (bf16[6,288,768]{2,1,0:T(8,128)(2,1)}, f32[6,288,768]{2,1,0:T(8,128)S(1)}) custom-call(s32[12]{0:T(128)S(1)} %stack.236.index_ref, bf16[12,288,768]{2,1,0:T(8,128)(2,1)S(1)} %bitcast.76, bf16[12,288,768]{2,1,0:T(8,128)(2,1)} %collective-permute-done.12.ga_ref.gb_ref, bf16[12,288,768]{2,1,0:T(8,128)(2,1)S(1)} %bitcast.77, ...), custom_call_target="tpu_custom_call" | custom-call | flops 2654208 | bytes 21233664 | tf_op jit(solution)/shard_map/merge_grid/pallas_call | solution.py:450
  251.5 2.4 copy-done
  254.2 16.8 %att_bwd.4 = (bf16[1024,768]{1,0:T(8,128)(2,1)}, bf16[8,768]{1,0:T(8,128)(2,1)}, bf16[2048,768]{1,0:T(8,128)(2,1)}, bf16[2048,768]{1,0:T(8,128)(2,1)}, f32[16,768]{1,0:T(8,128)}) custom-call(s32[1]{0:T(128)S(6)} %select_n.139.refs_0_.state_ref, ...), custom_call_target="tpu_custom_call", output_to_operand_aliasing={{0}: (14, {}), {1}: (15, {}), {2}: (16, {}), {3}: (17, {}),... | custom-call | flops 16106127360 | bytes 10485760 | tf_op jit(solution)/shard_map/att_bwd/pallas_call | solution.py:258
  271.0 15.2 %collective-permute-done.13.ga_ref.gb_ref = bf16[6,288,768]{2,1,0:T(8,128)(2,1)S(1)} collective-permute-done((bf16[6,288,768]{2,1,0:T(8,128)(2,1)}, bf16[6,288,768]{2,1,0:T(8,128)(2,1)S(1)}, u32[]{:S(2)}, u32[]{:S(2)}) %collective-permute-start.13) | collective-permute-done | bytes 2654240 | tf_op jit(solution)/shard_map/ppermute | solution.py:765
  286.2 2.4 merge_grid.5
  288.6 1.5 copy-done.1
  290.1 16.3 %collective-permute-start.14 = (bf16[3,288,768]{2,1,0:T(8,128)(2,1)}, bf16[3,288,768]{2,1,0:T(8,128)(2,1)S(1)}, u32[]{:S(2)}, u32[]{:S(2)}) collective-permute-start(bf16[3,288,768]{2,1,0:T(8,128)(2,1)} %get-tuple-element.121), channel_id=1, source_target_pairs={{0,4},{1,3},{2,6},{3,1},{4,0},{5,7},{6,2},{7,5},{8,12},{9,11},{10,... | collective-permute-start | bytes 3981320 | tf_op jit(solution)/shard_map/ppermute | solution.py:765
  306.4 17.3 %att_bwd.5 = (bf16[1024,768]{1,0:T(8,128)(2,1)}, bf16[8,768]{1,0:T(8,128)(2,1)}, bf16[2048,768]{1,0:T(8,128)(2,1)}, bf16[2048,768]{1,0:T(8,128)(2,1)}, f32[16,768]{1,0:T(8,128)}) custom-call(s32[1]{0:T(128)S(6)} %select_n.139.refs_0_.state_ref, ...), custom_call_target="tpu_custom_call", output_to_operand_aliasing={{0}: (14, {}), {1}: (15, {}), {2}: (16, {}), {3}: (17, {}),... | custom-call | flops 16106127360 | bytes 10485760 | tf_op jit(solution)/shard_map/att_bwd/pallas_call | solution.py:258
  323.7 1.9 collective-permute-done.14.ga_ref.gb_ref
  326.5 2.2 collective-permute-start.16
  328.7 21.7 %qkv_bwd.1 = (bf16[1168,768]{1,0:T(8,128)(2,1)}, f32[1168,768]{1,0:T(8,128)}, bf16[1024,768]{1,0:T(8,128)(2,1)}, f32[1024,768]{1,0:T(8,128)}) custom-call(s32[1]{0:T(128)} %bitcast.24.refs_0_.index_ref, bf16[2048,768]{1,0:T(8,128)(2,1)} %copy-done.9, bf16[1024,768]{1,0:T(8,128)(2,1)} %get-tuple-element.132.refs_2_, ...), custom_call_target="tpu_custom_call" | custom-call | flops 12079595520 | bytes 23592960 | tf_op jit(solution)/shard_map/qkv_bwd/pallas_call | solution.py:387
  351.2 23.0 %collective-permute-start.17 = (bf16[1168,768]{1,0:T(8,128)(2,1)}, bf16[1168,768]{1,0:T(8,128)(2,1)S(1)}, u32[]{:S(2)}, u32[]{:S(2)}) collective-permute-start(bf16[1168,768]{1,0:T(8,128)(2,1)} %get-tuple-element.146), channel_id=1, source_target_pairs={{0,1},{1,0},{2,3},{3,2},{4,5},{5,4},{6,7},{7,6},{8,9},{9,8},{10,11... | collective-permute-start | bytes 5382152 | tf_op jit(solution)/shard_map/ppermute | solution.py:765
  375.6 2.2 collective-permute-done.17.got_ref
  379.6 1.8 fusion.6
  381.4 5.5 %collective-permute-start.22 = (bf16[1,288,768]{2,1,0:T(8,128)(2,1)S(1)}, bf16[1,288,768]{2,1,0:T(8,128)(2,1)S(1)}, u32[]{:S(2)}, u32[]{:S(2)}) collective-permute-start(bf16[1,288,768]{2,1,0:T(8,128)(2,1)S(1)} %get-tuple-element.145), channel_id=1, source_target_pairs={{0,16},{1,17},{2,18},{3,19},{4,20},{5,21},{6,22},{7,23},{8,24},{9,... | collective-permute-start | bytes 1327112 | tf_op jit(solution)/shard_map/ppermute | solution.py:765
  386.9 24.7 %collective-permute-done.18.got_ref = bf16[592,768]{1,0:T(8,128)(2,1)S(1)} collective-permute-done((bf16[592,768]{1,0:T(8,128)(2,1)S(1)}, bf16[592,768]{1,0:T(8,128)(2,1)S(1)}, u32[]{:S(2)}, u32[]{:S(2)}) %collective-permute-start.18) | collective-permute-done | bytes 909344 | tf_op jit(solution)/shard_map/ppermute | solution.py:765
  412.5 2.6 fusion.2
  415.1 5.9 %collective-permute-done.19.got_ref = bf16[304,768]{1,0:T(8,128)(2,1)S(1)} collective-permute-done((bf16[304,768]{1,0:T(8,128)(2,1)S(1)}, bf16[304,768]{1,0:T(8,128)(2,1)S(1)}, u32[]{:S(2)}, u32[]{:S(2)}) %collective-permute-start.19) | collective-permute-done | bytes 466976 | tf_op jit(solution)/shard_map/ppermute | solution.py:765
  421.5 4.1 fusion.5
  425.6 4.2 collective-permute-done.20.got_ref
  434.7 6.6 %collective-permute-done.21 = bf16[304,768]{1,0:T(8,128)(2,1)} collective-permute-done((bf16[304,768]{1,0:T(8,128)(2,1)S(1)}, bf16[304,768]{1,0:T(8,128)(2,1)}, u32[]{:S(2)}, u32[]{:S(2)}) %collective-permute-start.21) | collective-permute-done | bytes 466976 | tf_op jit(solution)/shard_map/ppermute | solution.py:765
  442.4 1.8 slice_select_fusion
  447.4 4.1 fusion.17
  (113 shorter events, 27.0 us)
Async XLA Ops:
  1.5 4.8 %collective-permute-start.1 = (bf16[96,128]{1,0:T(8,128)(2,1)S(1)}, bf16[96,128]{1,0:T(8,128)(2,1)S(1)}, u32[]{:S(2)}, u32[]{:S(2)}) collective-permute-start(bf16[96,128]{1,0:T(8,128)(2,1)S(1)} %slice.28), channel_id=1, source_target_pairs={{0,1},{1,2},{2,3},{3,4},{4,5},{5,6},{6,7},{7,8},{8,9},{9,10},{10,1... | collective-permute-start | bytes 73736 | tf_op jit(solution)/shard_map/ppermute | solution.py:745
  6.2 2.6 copy-start.12
  8.8 17.2 %collective-permute-start.2 = (bf16[304,768]{1,0:T(8,128)(2,1)S(1)}, bf16[304,768]{1,0:T(8,128)(2,1)S(1)}, u32[]{:S(2)}, u32[]{:S(2)}) collective-permute-start(bf16[304,768]{1,0:T(8,128)(2,1)S(1)} %pad_maximum_fusion), channel_id=1, source_target_pairs={{0,16},{1,17},{2,18},{3,19},{4,20},{5,21},{6,22},{7,23},{24,8},{25... | collective-permute-start | bytes 1400840 | tf_op jit(solution)/shard_map/ppermute | solution.py:765
  26.1 11.4 %collective-permute-start.3 = (bf16[304,768]{1,0:T(8,128)(2,1)S(1)}, bf16[304,768]{1,0:T(8,128)(2,1)S(1)}, u32[]{:S(2)}, u32[]{:S(2)}) collective-permute-start(bf16[304,768]{1,0:T(8,128)(2,1)S(1)} %fusion.16), channel_id=1, source_target_pairs={{0,8},{1,9},{2,10},{3,11},{4,12},{5,13},{6,14},{7,15},{8,0},{9,1},... | collective-permute-start | bytes 1400840 | tf_op jit(solution)/shard_map/ppermute | solution.py:765
  37.6 10.0 %collective-permute-start.4 = (bf16[304,768]{1,0:T(8,128)(2,1)S(1)}, bf16[304,768]{1,0:T(8,128)(2,1)S(1)}, u32[]{:S(2)}, u32[]{:S(2)}) collective-permute-start(bf16[304,768]{1,0:T(8,128)(2,1)S(1)} %add.257.own_ref), channel_id=1, source_target_pairs={{0,2},{1,5},{2,0},{3,7},{4,6},{5,1},{6,4},{7,3},{8,10},{9,13},{10,... | collective-permute-start | bytes 1400840 | tf_op jit(solution)/shard_map/ppermute | solution.py:765
  47.7 13.4 %collective-permute-start.5 = (bf16[592,768]{1,0:T(8,128)(2,1)S(1)}, bf16[592,768]{1,0:T(8,128)(2,1)S(1)}, u32[]{:S(2)}, u32[]{:S(2)}) collective-permute-start(bf16[592,768]{1,0:T(8,128)(2,1)S(1)} %join.5.own_ref), channel_id=1, source_target_pairs={{0,4},{1,3},{2,6},{3,1},{4,0},{5,7},{6,2},{7,5},{8,12},{9,11},{10,... | collective-permute-start | bytes 2727944 | tf_op jit(solution)/shard_map/ppermute | solution.py:765
  49.3 37.0 %collective-permute-start = (bf16[1024,768]{1,0:T(8,128)(2,1)}, bf16[1024,768]{1,0:T(8,128)(2,1)}, u32[]{:S(2)}, u32[]{:S(2)}) collective-permute-start(bf16[1024,768]{1,0:T(8,128)(2,1)} %x_ref.1), channel_id=1, source_target_pairs={{0,1},{1,2},{2,3},{4,5},{5,6},{6,7},{8,9},{9,10},{10,11},{12,13},{... | collective-permute-start | bytes 4718600 | tf_op jit(solution)/shard_map/ppermute | solution.py:751
  61.2 28.1 %copy-start.4 = (bf16[1168,768]{1,0:T(8,128)(2,1)}, bf16[1168,768]{1,0:T(8,128)(2,1)S(1)}, u32[]{:S(2)}) copy-start(bf16[1168,768]{1,0:T(8,128)(2,1)S(1)} %join.6.refs_2_) | copy-start | bytes 5382148
  61.2 28.1 %collective-permute-start.6 = (bf16[1168,768]{1,0:T(8,128)(2,1)S(1)}, bf16[1168,768]{1,0:T(8,128)(2,1)}, u32[]{:S(2)}, u32[]{:S(2)}) collective-permute-start(bf16[1168,768]{1,0:T(8,128)(2,1)S(1)} %join.6.refs_2_), channel_id=1, source_target_pairs={{0,1},{1,0},{2,3},{3,2},{4,5},{5,4},{6,7},{7,6},{8,9},{9,8},{10,11... | collective-permute-start | bytes 5382152 | tf_op jit(solution)/shard_map/ppermute | solution.py:765
  61.3 24.8 %collective-permute-start.7 = (bf16[288,768]{1,0:T(8,128)(2,1)S(1)}, bf16[288,768]{1,0:T(8,128)(2,1)S(1)}, u32[]{:S(2)}, u32[]{:S(2)}) collective-permute-start(bf16[288,768]{1,0:T(8,128)(2,1)S(1)} %bitcast.80), channel_id=1, source_target_pairs={{8,24},{9,25},{10,26},{11,27},{12,28},{13,29},{14,30},{15,31},{16,... | collective-permute-start | bytes 1327112 | tf_op jit(solution)/shard_map/ppermute | solution.py:765
  86.2 21.3 %collective-permute-start.8 = (bf16[576,768]{1,0:T(8,128)(2,1)S(1)}, bf16[576,768]{1,0:T(8,128)(2,1)S(1)}, u32[]{:S(2)}, u32[]{:S(2)}) collective-permute-start(bf16[576,768]{1,0:T(8,128)(2,1)S(1)} %join.7), channel_id=1, source_target_pairs={{0,8},{1,9},{2,10},{3,11},{4,12},{5,13},{6,14},{7,15},{8,0},{9,1},... | collective-permute-start | bytes 2654216 | tf_op jit(solution)/shard_map/ppermute | solution.py:765
  89.3 1.7 copy-start.9
  104.2 8.7 %copy-start.11 = (f32[16,768]{1,0:T(8,128)S(1)}, f32[16,768]{1,0:T(8,128)}, u32[]{:S(2)}) copy-start(f32[16,768]{1,0:T(8,128)} %get-tuple-element.85) | copy-start | bytes 147460
  108.3 19.8 %collective-permute-start.9 = (bf16[864,768]{1,0:T(8,128)(2,1)S(1)}, bf16[864,768]{1,0:T(8,128)(2,1)S(1)}, u32[]{:S(2)}, u32[]{:S(2)}) collective-permute-start(bf16[864,768]{1,0:T(8,128)(2,1)S(1)} %bitcast.78), channel_id=1, source_target_pairs={{0,2},{1,5},{2,0},{3,7},{4,6},{5,1},{6,4},{7,3},{8,10},{9,13},{10,... | collective-permute-start | bytes 3981320 | tf_op jit(solution)/shard_map/ppermute | solution.py:765
  128.3 32.1 %collective-permute-start.10 = (bf16[1728,768]{1,0:T(8,128)(2,1)S(1)}, bf16[1728,768]{1,0:T(8,128)(2,1)S(1)}, u32[]{:S(2)}, u32[]{:S(2)}) collective-permute-start(bf16[1728,768]{1,0:T(8,128)(2,1)S(1)} %join.8.own_ref), channel_id=1, source_target_pairs={{0,4},{1,3},{2,6},{3,1},{4,0},{5,7},{6,2},{7,5},{8,12},{9,11},{10,... | collective-permute-start | bytes 7962632 | tf_op jit(solution)/shard_map/ppermute | solution.py:765
  163.1 16.2 %collective-permute-start.11 = (bf16[3456,768]{1,0:T(8,128)(2,1)}, bf16[3456,768]{1,0:T(8,128)(2,1)}, u32[]{:S(2)}, u32[]{:S(2)}) collective-permute-start(bf16[3456,768]{1,0:T(8,128)(2,1)} %join.9), channel_id=1, source_target_pairs={{0,1},{1,0},{2,3},{3,2},{4,5},{5,4},{6,7},{7,6},{8,9},{9,8},{10,11... | collective-permute-start | bytes 15925256 | tf_op jit(solution)/shard_map/ppermute | solution.py:765
  227.6 17.6 %collective-permute-start.12 = (bf16[12,288,768]{2,1,0:T(8,128)(2,1)}, bf16[12,288,768]{2,1,0:T(8,128)(2,1)}, u32[]{:S(2)}, u32[]{:S(2)}) collective-permute-start(bf16[12,288,768]{2,1,0:T(8,128)(2,1)} %bitcast.85), channel_id=1, source_target_pairs={{0,1},{1,0},{2,3},{3,2},{4,5},{5,4},{6,7},{7,6},{8,9},{9,8},{10,11... | collective-permute-start | bytes 15925256 | tf_op jit(solution)/shard_map/ppermute | solution.py:765
  228.2 17.0 %slice-start.2 = ((s8[5308416]{0:T(1024)(128)(4,1)}), s8[4194304]{0:T(1024)(128)(4,1)S(1)}, s32[]{:S(2)}) async-start(s8[5308416]{0:T(1024)(128)(4,1)} %bitcast.74), calls=%async_computation.2 | async-start | bytes 8388608
  228.2 17.0 %slice-start.3 = ((s8[5308416]{0:T(1024)(128)(4,1)}), s8[1114112]{0:T(1024)(128)(4,1)S(1)}, s32[]{:S(2)}) async-start(s8[5308416]{0:T(1024)(128)(4,1)} %bitcast.74), calls=%async_computation.3 | async-start | bytes 2228224
  251.5 2.4 copy-start
  253.9 32.2 %collective-permute-start.13 = (bf16[6,288,768]{2,1,0:T(8,128)(2,1)}, bf16[6,288,768]{2,1,0:T(8,128)(2,1)S(1)}, u32[]{:S(2)}, u32[]{:S(2)}) collective-permute-start(bf16[6,288,768]{2,1,0:T(8,128)(2,1)} %get-tuple-element.112), channel_id=1, source_target_pairs={{0,2},{1,5},{2,0},{3,7},{4,6},{5,1},{6,4},{7,3},{8,10},{9,13},{10,... | collective-permute-start | bytes 7962632 | tf_op jit(solution)/shard_map/ppermute | solution.py:765
  254.2 31.9 %slice-start = ((s8[5308416]{0:T(1024)(128)(4,1)}), s8[4194304]{0:T(1024)(128)(4,1)S(1)}, s32[]{:S(2)}) async-start(s8[5308416]{0:T(1024)(128)(4,1)} %bitcast.72), calls=%async_computation | async-start | bytes 8388608
  254.2 31.9 %slice-start.1 = ((s8[5308416]{0:T(1024)(128)(4,1)}), s8[1114112]{0:T(1024)(128)(4,1)S(1)}, s32[]{:S(2)}) async-start(s8[5308416]{0:T(1024)(128)(4,1)} %bitcast.72), calls=%async_computation.1 | async-start | bytes 2228224
  288.6 1.5 copy-start.1
  290.1 35.5 %collective-permute-start.14 = (bf16[3,288,768]{2,1,0:T(8,128)(2,1)}, bf16[3,288,768]{2,1,0:T(8,128)(2,1)S(1)}, u32[]{:S(2)}, u32[]{:S(2)}) collective-permute-start(bf16[3,288,768]{2,1,0:T(8,128)(2,1)} %get-tuple-element.121), channel_id=1, source_target_pairs={{0,4},{1,3},{2,6},{3,1},{4,0},{5,7},{6,2},{7,5},{8,12},{9,11},{10,... | collective-permute-start | bytes 3981320 | tf_op jit(solution)/shard_map/ppermute | solution.py:765
  306.4 19.3 %copy-start.2 = (f32[3,288,768]{2,1,0:T(8,128)S(1)}, f32[3,288,768]{2,1,0:T(8,128)}, u32[]{:S(2)}) copy-start(f32[3,288,768]{2,1,0:T(8,128)} %copy-done.1) | copy-start | bytes 7962628
  326.5 23.9 %collective-permute-start.16 = (bf16[2,288,768]{2,1,0:T(8,128)(2,1)S(1)}, bf16[2,288,768]{2,1,0:T(8,128)(2,1)S(1)}, u32[]{:S(2)}, u32[]{:S(2)}) collective-permute-start(bf16[2,288,768]{2,1,0:T(8,128)(2,1)S(1)} %get-tuple-element.130), channel_id=1, source_target_pairs={{0,8},{1,9},{2,10},{3,11},{4,12},{5,13},{6,14},{7,15},{8,0},{9,1},... | collective-permute-start | bytes 2654216 | tf_op jit(solution)/shard_map/ppermute | solution.py:765
  350.4 23.8 %copy-start.14 = (bf16[1024,768]{1,0:T(8,128)(2,1)S(1)}, bf16[1024,768]{1,0:T(8,128)(2,1)}, u32[]{:S(2)}) copy-start(bf16[1024,768]{1,0:T(8,128)(2,1)} %get-tuple-element.139) | copy-start | bytes 4718596
  350.4 27.3 %copy-start.3 = (f32[1168,768]{1,0:T(8,128)S(1)}, f32[1168,768]{1,0:T(8,128)}, u32[]{:S(2)}) copy-start(f32[1168,768]{1,0:T(8,128)} %get-tuple-element.141.keep_ref) | copy-start | bytes 10764292
  351.2 26.6 %collective-permute-start.17 = (bf16[1168,768]{1,0:T(8,128)(2,1)}, bf16[1168,768]{1,0:T(8,128)(2,1)S(1)}, u32[]{:S(2)}, u32[]{:S(2)}) collective-permute-start(bf16[1168,768]{1,0:T(8,128)(2,1)} %get-tuple-element.146), channel_id=1, source_target_pairs={{0,1},{1,0},{2,3},{3,2},{4,5},{5,4},{6,7},{7,6},{8,9},{9,8},{10,11... | collective-permute-start | bytes 5382152 | tf_op jit(solution)/shard_map/ppermute | solution.py:765
  374.2 38.3 %collective-permute-start.15 = (bf16[1024,768]{1,0:T(8,128)(2,1)S(1)}, bf16[1024,768]{1,0:T(8,128)(2,1)S(1)}, u32[]{:S(2)}, u32[]{:S(2)}) collective-permute-start(bf16[1024,768]{1,0:T(8,128)(2,1)S(1)} %copy-done.14), channel_id=1, source_target_pairs={{1,0},{2,1},{3,2},{5,4},{6,5},{7,6},{9,8},{10,9},{11,10},{13,12},{... | collective-permute-start | bytes 4718600 | tf_op jit(solution)/shard_map/ppermute | solution.py:751
  378.6 33.9 %copy-start.5 = (f32[1024,768]{1,0:T(8,128)S(1)}, f32[1024,768]{1,0:T(8,128)}, u32[]{:S(2)}) copy-start(f32[1024,768]{1,0:T(8,128)} %get-tuple-element.138) | copy-start | bytes 9437188
  378.6 33.0 %collective-permute-start.18 = (bf16[592,768]{1,0:T(8,128)(2,1)S(1)}, bf16[592,768]{1,0:T(8,128)(2,1)S(1)}, u32[]{:S(2)}, u32[]{:S(2)}) collective-permute-start(bf16[592,768]{1,0:T(8,128)(2,1)S(1)} %get-tuple-element.148), channel_id=1, source_target_pairs={{0,2},{1,5},{2,0},{3,7},{4,6},{5,1},{6,4},{7,3},{8,10},{9,13},{10,... | collective-permute-start | bytes 2727944 | tf_op jit(solution)/shard_map/ppermute | solution.py:765
  381.4 50.0 %collective-permute-start.22 = (bf16[1,288,768]{2,1,0:T(8,128)(2,1)S(1)}, bf16[1,288,768]{2,1,0:T(8,128)(2,1)S(1)}, u32[]{:S(2)}, u32[]{:S(2)}) collective-permute-start(bf16[1,288,768]{2,1,0:T(8,128)(2,1)S(1)} %get-tuple-element.145), channel_id=1, source_target_pairs={{0,16},{1,17},{2,18},{3,19},{4,20},{5,21},{6,22},{7,23},{8,24},{9,... | collective-permute-start | bytes 1327112 | tf_op jit(solution)/shard_map/ppermute | solution.py:765
  412.4 8.6 %collective-permute-start.19 = (bf16[304,768]{1,0:T(8,128)(2,1)S(1)}, bf16[304,768]{1,0:T(8,128)(2,1)S(1)}, u32[]{:S(2)}, u32[]{:S(2)}) collective-permute-start(bf16[304,768]{1,0:T(8,128)(2,1)S(1)} %get-tuple-element.150), channel_id=1, source_target_pairs={{0,4},{1,3},{2,6},{3,1},{4,0},{5,7},{6,2},{7,5},{8,12},{9,11},{10,... | collective-permute-start | bytes 1400840 | tf_op jit(solution)/shard_map/ppermute | solution.py:765
  412.5 9.0 %copy-start.8 = (f32[1024,768]{1,0:T(8,128)S(1)}, f32[1024,768]{1,0:T(8,128)}, u32[]{:S(2)}) copy-start(f32[1024,768]{1,0:T(8,128)} %get-tuple-element.102) | copy-start | bytes 9437188
  421.1 8.6 %collective-permute-start.20 = (bf16[304,768]{1,0:T(8,128)(2,1)S(1)}, bf16[304,768]{1,0:T(8,128)(2,1)S(1)}, u32[]{:S(2)}, u32[]{:S(2)}) collective-permute-start(bf16[304,768]{1,0:T(8,128)(2,1)S(1)} %get-tuple-element.152), channel_id=1, source_target_pairs={{0,8},{1,9},{2,10},{3,11},{4,12},{5,13},{6,14},{7,15},{8,0},{9,1},... | collective-permute-start | bytes 1400840 | tf_op jit(solution)/shard_map/ppermute | solution.py:765
  421.5 9.7 %copy-start.13 = (pred[3]{0:T(512)(128)(4,1)S(1)}, pred[3]{0:T(512)(128)(4,1)}, u32[]{:S(2)}) copy-start(pred[3]{0:T(512)(128)(4,1)} %copy-done.12) | copy-start | bytes 13
  429.8 11.5 %collective-permute-start.21 = (bf16[304,768]{1,0:T(8,128)(2,1)S(1)}, bf16[304,768]{1,0:T(8,128)(2,1)}, u32[]{:S(2)}, u32[]{:S(2)}) collective-permute-start(bf16[304,768]{1,0:T(8,128)(2,1)S(1)} %get-tuple-element.154), channel_id=1, source_target_pairs={{8,24},{9,25},{10,26},{11,27},{12,28},{13,29},{14,30},{15,31},{16,... | collective-permute-start | bytes 1400840 | tf_op jit(solution)/shard_map/ppermute | solution.py:765
  431.3 0.8 copy-start.10
  442.4 1.8 copy-start.7
  442.4 5.0 %copy-start.6 = (f32[1731,128]{1,0:T(8,128)S(1)}, f32[1731,128]{1,0:T(8,128)}, u32[]{:S(2)}) copy-start(f32[1731,128]{1,0:T(8,128)} %param.10) | copy-start | bytes 2658820
  444.2 3.1 collective-permute-start.23

commit v6 on v5

--- a/solution.py
+++ b/solution.py
@@ -53,19 +53,27 @@
 
 def att_fwd_kernel(
     state_ref, tail_ref, q_ref, k_ref, v_ref, tq_ref, tk_ref, tv_ref,
-    o_ref, l_ref, qm_ref, km_ref, vm_ref,
+    o_ref, l_ref, qm_ref, km_ref, vm_ref, ka, va,
 ):
     rows = q_ref.shape[0]
     lane = lax.broadcasted_iota(jnp.int32, (1, 128), 1)
     state = state_ref[0]
-    second = state == 2
-    empty = state == 0
     one = taps_seen(2 * rows, 0, rows, state, 1, 0)
     two = taps_seen(2 * rows, 0, rows, state, 2, 0)
     x = jnp.concatenate([tail_ref[...].astype(F32), q_ref[...].astype(F32)], 0)
     qm_ref[...] = conv(x, tq_ref[...], one[rows - 8 :], two[rows - 8 :])[8:]
-    km_ref[...] = conv(k_ref[...].astype(F32), tk_ref[...], one, two)
-    vm_ref[...] = conv(v_ref[...].astype(F32), tv_ref[...], one, two)
+    k = conv(k_ref[...].astype(F32), tk_ref[...], one, two)
+    v = conv(v_ref[...].astype(F32), tv_ref[...], one, two)
+    km_ref[...] = k
+    vm_ref[...] = v
+    bias = jnp.where(state == 2, 0.0, -1e30)
+    for h in range(2):
+        mine = (lane < 64) if h == 0 else (lane >= 64)
+        base = 64 if h == 0 else 0
+        first = jnp.where(lane == base, bias, 0.0).astype(BF)
+        ka[h, 0:rows, :] = jnp.where(mine, k[:rows], first)
+        ka[h, rows:, :] = jnp.where(mine, k[rows:], jnp.zeros((), BF))
+        va[h] = jnp.where(mine, v, jnp.ones((), BF))
     for i in range(rows // QB):
         rs = pl.ds(i * QB, QB)
         outs = []
@@ -73,33 +81,23 @@
         qf = qm_ref[rs, :].astype(F32) * 0.125
         for h in range(2):
             mine = (lane < 64) if h == 0 else (lane >= 64)
-            qh = jnp.where(mine, qf, 0.0).astype(BF)
-            nk = (i + 1) * QB
-            vh = jnp.where(mine, vm_ref[rows : rows + nk, :], jnp.ones((), BF))
-            s = dot_nt(qh, km_ref[rows : rows + nk, :])
+            base = 64 if h == 0 else 0
+            qh = jnp.where(mine, qf, jnp.where(lane == base, 1.0, 0.0)).astype(BF)
+            nk = rows + (i + 1) * QB
+            s = dot_nt(qh, ka[h, 0:nk, :])
             r = lax.broadcasted_iota(jnp.int32, (QB, QB), 0)
             c = lax.broadcasted_iota(jnp.int32, (QB, QB), 1)
-            sd = jnp.where(c <= r, s[:, i * QB :], -1e30)
-            m = jnp.max(sd, axis=1, keepdims=True)
-            if i > 0:
-                m = jnp.maximum(m, jnp.max(s[:, : i * QB], axis=1, keepdims=True))
-            o = dot(jnp.exp(sd - m).astype(BF), vh[i * QB :])
-            if i > 0:
-                o = o + dot(jnp.exp(s[:, : i * QB] - m).astype(BF), vh[: i * QB])
-
-            def prev(args):
-                o1, m1 = args
-                s2 = dot_nt(qh, km_ref[0:rows, :])
-                m2 = jnp.maximum(m1, jnp.max(s2, axis=1, keepdims=True))
-                p2 = jnp.exp(s2 - m2).astype(BF)
-                vph = jnp.where(mine, vm_ref[0:rows, :], jnp.ones((), BF))
-                return o1 * jnp.exp(m1 - m2) + dot(p2, vph), m2
-
-            o, m = lax.cond(second, prev, lambda a: a, (o, m))
+            sd = jnp.where(c <= r, s[:, nk - QB :], -1e30)
+            se = s[:, : nk - QB]
+            m = jnp.maximum(
+                jnp.max(sd, axis=1, keepdims=True), jnp.max(se, axis=1, keepdims=True)
+            )
+            p = jnp.concatenate([jnp.exp(se - m).astype(BF), jnp.exp(sd - m).astype(BF)], 1)
+            o = dot(p, va[h, 0:nk, :])
             outs.append(o / pltpu.roll(o, 64, 1))
             sums.append(m + jnp.log(o))
         res = jnp.where(lane < 64, outs[0], outs[1])
-        res = jnp.where(empty, vm_ref[pl.ds(rows + i * QB, QB), :].astype(F32), res)
+        res = jnp.where(state == 0, vm_ref[pl.ds(rows + i * QB, QB), :].astype(F32), res)
         o_ref[rs, :] = res.astype(BF)
         l_ref[rs, :] = jnp.where(lane < 64, sums[1], sums[0])
 
@@ -156,6 +154,7 @@
         ],
         earlier,
         part,
+        scratch_shapes=[pltpu.VMEM((2, 2 * rows, 128), BF)] * 2,
         cost_estimate=cost(
             2 * 2 * 12 * rows * rows * 1.5 * 256 / PARTS,
             rows * D * 30 / PARTS,
@@ -187,7 +186,7 @@
 def att_bwd_kernel(
     state_ref, q_ref, k_ref, v_ref, o_ref, l_ref, do_ref, xt_ref, xq_ref, xk_ref, xv_ref,
     tq_ref, tk_ref, tv_ref,
-    pq_ref, pt_ref, pk_ref, pv_ref, tg_ref, qa, da, dqs, dks, dvs,
+    pq_ref, pt_ref, pk_ref, pv_ref, tg_ref, qa, da, qt, dt, kt, dqt, dqs, dks, dvs,
 ):
     rows = q_ref.shape[0]
     lane = lax.broadcasted_iota(jnp.int32, (1, 128), 1)
@@ -196,47 +195,60 @@
     od = do * o_ref[...].astype(F32)
     qf = q_ref[...].astype(F32) * 0.125
     lv = l_ref[...]
-    zero = jnp.zeros((), BF)
-    dks[...] = jnp.zeros(dks.shape, F32)
-    dvs[...] = jnp.zeros(dvs.shape, F32)
-    dqs[...] = jnp.zeros(dqs.shape, F32)
     for h in range(2):
         mine = (lane < 64) if h == 0 else (lane >= 64)
         base = 64 if h == 0 else 0
-        ones3 = ((lane >= base) & (lane < base + 3)).astype(BF)
         delta = jnp.sum(jnp.where(mine, od, 0.0), axis=1, keepdims=True)
-        qa[...] = jnp.where(mine, qf, three(-lv, lane, base)).astype(BF)
-        da[...] = jnp.where(mine, do, three(-delta, lane, base)).astype(BF)
-
-        def part(ks, qs, dos, mask):
-            kk = k_ref[ks, :]
-            st = dot_nt(jnp.where(mine, kk, ones3), qs)
-            dp = dot_nt(jnp.where(mine, v_ref[ks, :], ones3), dos)
+        qa[h] = jnp.where(mine, qf, three(-lv, lane, base)).astype(BF)
+        da[h] = jnp.where(mine, do, three(-delta, lane, base)).astype(BF)
+    qt[...] = jnp.transpose(qf).astype(BF)
+    dt[...] = jnp.transpose(do).astype(BF)
+    kt[...] = jnp.transpose(k_ref[...].astype(F32)).astype(BF)
+    dqt[...] = jnp.zeros(dqt.shape, F32)
+
+    def keys(ks, first, diagonal):
+        kk = k_ref[ks, :]
+        vv = v_ref[ks, :]
+        dv = []
+        dk = []
+        for h in range(2):
+            mine = (lane < 64) if h == 0 else (lane >= 64)
+            base = 64 if h == 0 else 0
+            ones3 = ((lane >= base) & (lane < base + 3)).astype(BF)
+            hs = slice(64 * h, 64 * h + 64)
+            st = dot_nt(jnp.where(mine, kk, ones3), qa[h, first:rows, :])
+            dp = dot_nt(jnp.where(mine, vv, ones3), da[h, first:rows, :])
             p = jnp.exp(st)
-            if mask is not None:
-                p = jnp.where(mask, p, 0.0)
+            if diagonal:
+                r = lax.broadcasted_iota(jnp.int32, (QB, QB), 0)
+                c = lax.broadcasted_iota(jnp.int32, (QB, QB), 1)
+                seen = jnp.where(r <= c, p[:, :QB], 0.0)
+                p = jnp.concatenate([seen, p[:, QB:]], 1) if first + QB < rows else seen
             ds = (p * dp).astype(BF)
-            dvs[ks, :] += dot(p.astype(BF), jnp.where(mine, dos, zero))
-            dks[ks, :] += dot(ds, jnp.where(mine, qs, zero))
-            return dot_tn(ds, jnp.where(mine, kk, zero))
-
-        for i in range(rows // QB):
-            qs = qa[pl.ds(i * QB, QB), :]
-            dos = da[pl.ds(i * QB, QB), :]
-            kr = lax.broadcasted_iota(jnp.int32, (QB, QB), 0)
-            qr = lax.broadcasted_iota(jnp.int32, (QB, QB), 1)
-            dq = part(pl.ds(rows + i * QB, QB), qs, dos, kr <= qr)
-            if i > 0:
-                dq = dq + part(pl.ds(rows, i * QB), qs, dos, None)
-            dqs[pl.ds(8 + i * QB, QB), :] += dq * 0.125
-
-        @pl.when(second)
-        def _():
-            for i in range(rows // QB):
-                rs = pl.ds(i * QB, QB)
-                dq = part(pl.ds(0, rows), qa[rs, :], da[rs, :], None)
-                dqs[pl.ds(8 + i * QB, QB), :] += dq * 0.125
-
+            dv.append(dot_nt(dt[hs, first:rows], p.astype(BF)))
+            dk.append(dot_nt(qt[hs, first:rows], ds))
+            dqt[hs, first:rows] += dot(kt[hs, ks], ds)
+        dvs[ks, :] = jnp.transpose(jnp.concatenate(dv, 0))
+        dks[ks, :] = jnp.transpose(jnp.concatenate(dk, 0))
+
+    for j in range(rows // QB):
+        keys(pl.ds(rows + j * QB, QB), j * QB, True)
+
+    @pl.when(second)
+    def _():
+        def step(j, carry):
+            keys(pl.ds(pl.multiple_of(j * QB, QB), QB), 0, False)
+            return carry
+
+        lax.fori_loop(0, rows // QB, step, 0)
+
+    @pl.when(jnp.logical_not(second))
+    def _():
+        dks[0:rows, :] = jnp.zeros((rows, 128), F32)
+        dvs[0:rows, :] = jnp.zeros((rows, 128), F32)
+
+    dqs[0:8, :] = jnp.zeros((8, 128), F32)
+    dqs[8:, :] = jnp.transpose(dqt[...]) * 0.125
     one = taps_seen(2 * rows, 0, rows, state_ref[0], 1, 1)
     two = taps_seen(2 * rows, 0, rows, state_ref[0], 2, 2)
     xq = jnp.concatenate([xt_ref[...].astype(F32), xq_ref[...].astype(F32)], 0)
@@ -277,8 +289,12 @@
         earlier,
         part,
         scratch_shapes=[
-            pltpu.VMEM((rows, 128), BF),
-            pltpu.VMEM((rows, 128), BF),
+            pltpu.VMEM((2, rows, 128), BF),
+            pltpu.VMEM((2, rows, 128), BF),
+            pltpu.VMEM((128, rows), BF),
+            pltpu.VMEM((128, rows), BF),
+            pltpu.VMEM((128, 2 * rows), BF),
+            pltpu.VMEM((128, rows), F32),
             pltpu.VMEM((rows + 8, 128), F32),
             pltpu.VMEM((2 * rows, 128), F32),
             pltpu.VMEM((2 * rows, 128), F32),
@@ -876,18 +892,18 @@
     even = (place & 1) == 0
     tokens_both = jnp.concatenate([tokens_before, tokens], 0)
     if staged:
-        mine = jnp.concatenate(
-            [jnp.where(place < count // 4, chunk, jnp.zeros((), BF)), small.astype(BF).reshape(-1, D)], 0
-        )
-        mine = mine + swap(mine, 16, 16, (0, 3))
+        z = place >> 3
+        mine = jnp.concatenate([chunk, small.astype(BF).reshape(-1, D)], 0)
+        got = swap(mine, 16, 16)
+        rest = jnp.concatenate([chunk, got[:height]], 0)
+        none = jnp.zeros((), BF)
+        first = jnp.where(z == 0, chunk, jnp.where(z == 2, got[:height], none))
+        mine = jnp.concatenate([first, mine[height:] + got[height:]], 0)
         mine = mine + swap(mine, 8, 8)
-        rest = after(chunk, mine)
+        across = swap(after(rest, mine), 8, 8)
         mine = join(mine, swap(mine, 2, 4))
         mine = join(mine, swap(mine, 4, 2))
         got = swap(mine, 1, 1)
-        z = place >> 3
-        rest = join(rest, swap(rest, 16, 16, (1, 2, 3)), 0)
-        across = swap(rest, 8, 8)
         index = []
         late_index = []
         for k in (0, 1):
@@ -994,12 +1010,6 @@
         4 if staged else 0,
     )
     grads_before, grad_normed_one = sums[2:]
-    from_next = shift_ctx(grads_before, -1)
-    scaled_one, factor_one, _ = normalize(tokens.astype(F32), gain_first)
-    input_grad = grad_hidden + norm_back(
-        grad_normed_one + from_next.astype(F32), scaled_one, factor_one, gain_first
-    )
-
     if staged:
         send, keep = sums[:2]
         high = z >> 1
@@ -1013,14 +1023,16 @@
         got = swap(send, 4, 2)
         send, keep = merge(core, keep, got, height, 0)
         got = swap(send, 8, 8)
+        from_next = shift_ctx(after(grads_before, send), -1)
         late_chunk = late_keep[0] + late_got[0].astype(F32)
-        send, keep = merge(after(core, input_grad, late_chunk), keep, got, height, 0)
+        send, keep = merge(after(core, late_chunk), keep, got, height, 0)
         got = swap(send, 16, 16, (1, 2))
         first = keep + got.astype(F32)
         small_grad = first[height:].reshape(-1, 128)
         late_grad = jnp.where(in_up, ungroup(late_chunk).reshape(3, 4, 24, D), late_chunk.reshape(3, 4, 24, D))
         chunk_grad = jnp.where(place < count // 4, first[:height], late_grad.reshape(-1, D))
     else:
+        from_next = shift_ctx(grads_before, -1)
         flat_grad = jnp.stack([here_grad.reshape(12, 3, 4, 24, D), away_grad.reshape(12, 3, 4, 24, D)], 1)
         flat_grad = flat_grad.reshape(72, 4, 24, D)
         wide_grad = jnp.concatenate(
@@ -1037,6 +1049,11 @@
         extra = count * delta
         small_grad = jnp.concatenate([used, jnp.zeros((extra - used.shape[0], 128), F32)], 0)
         small_grad = lax.psum(small_grad, AXES)
+    scaled_one, factor_one, _ = normalize(tokens.astype(F32), gain_first)
+    input_grad = grad_hidden + norm_back(
+        grad_normed_one + from_next.astype(F32), scaled_one, factor_one, gain_first
+    )
+
     gradient = from_aligned(chunk_grad.reshape(-1, 128), small_grad, place, count, delta, owned)
     new_weights, new_one, new_two = adam_update(
         master, first_moment, second_moment, gradient, step_count, place * owned

time: 456 us -> 440 us (0.965)
  the two profiles are of different devices: /device:TPU:0 before, /device:TPU:13 now
where the time goes in v6:
time: 440 us; the launch traced here: 433 us
  Pallas kernels  234 us (53%)
  waiting for transfers between devices  110 us (25%)
  starting transfers between devices  46.4 us (11%)
  other arithmetic  20.9 us (5%)
  local copies, waits for them, and re-layouts  17.5 us (4%)
    ppermute x19, waiting for transfers between devices, swap(): return lax.ppermute(block, AXES, route)  98.3 us
    pallas_call x3, Pallas kernels, att_bwd(): call_in_parts(att_bwd_kernel, [pl.BlockSpec(memory_space=pltpu.SMEM), own...  84.3 us
    pallas_call x3, Pallas kernels, att_fwd(): call_in_parts(att_fwd_kernel, [pl.BlockSpec(memory_space=pltpu.SMEM), col...  48.9 us
    pallas_call x1, Pallas kernels, ffn(): pl.pallas_call(ffn_kernel, grid=(4,), in_specs=[scalars, scalars, act, ac...  48.3 us
    ppermute x19, starting transfers between devices, swap(): return lax.ppermute(block, AXES, route)  29.1 us
    pallas_call x1, Pallas kernels, qkv_bwd(): pl.pallas_call(body, grid=(blocks,), in_specs=[pl.BlockSpec(memory_space=...  22 us
    pallas_call x1, Pallas kernels, qkv_fwd(): pl.pallas_call(body, grid=(blocks,), in_specs=[pl.BlockSpec(memory_space=...  13.3 us
    pallas_call x4, Pallas kernels, merge_grid(): pl.pallas_call(body, grid_spec=pltpu.PrefetchScalarGridSpec(num_scalar_pr...  11 us
  transfers between devices with their start and end apart: 23, of which 13 were waited for; matrix products, arithmetic and copies ran while one was open for 5% of the time, Pallas kernels for 39%

profile of v6, /device:TPU:13, one launch (start us, length us, event | category | flops | bytes accessed | tf_op | source)
XLA Modules:
  0.0 432.9 jit_solution(10281979910343509507)
XLA Ops:
  1.5 3.7 collective-permute-start.1
  5.2 2.3 concatenate.23
  7.6 1.4 fusion.9
  10.8 2.3 collective-permute-start.2
  13.1 20.6 %collective-permute-done.2 = bf16[304,768]{1,0:T(8,128)(2,1)S(1)} collective-permute-done((bf16[304,768]{1,0:T(8,128)(2,1)}, bf16[304,768]{1,0:T(8,128)(2,1)S(1)}, u32[]{:S(2)}, u32[]{:S(2)}) %collective-permute-start.2) | collective-permute-done | bytes 466976 | tf_op jit(solution)/shard_map/ppermute | solution.py:781
  34.8 11.7 %collective-permute-done.3 = bf16[304,768]{1,0:T(8,128)(2,1)S(1)} collective-permute-done((bf16[304,768]{1,0:T(8,128)(2,1)S(1)}, bf16[304,768]{1,0:T(8,128)(2,1)S(1)}, u32[]{:S(2)}, u32[]{:S(2)}) %collective-permute-start.3) | collective-permute-done | bytes 466976 | tf_op jit(solution)/shard_map/ppermute | solution.py:781
  46.9 7.5 %collective-permute-done.4.got_ref = bf16[304,768]{1,0:T(8,128)(2,1)S(1)} collective-permute-done((bf16[304,768]{1,0:T(8,128)(2,1)S(1)}, bf16[304,768]{1,0:T(8,128)(2,1)S(1)}, u32[]{:S(2)}, u32[]{:S(2)}) %collective-permute-start.4) | collective-permute-done | bytes 466976 | tf_op jit(solution)/shard_map/ppermute | solution.py:781
  55.5 4.8 %collective-permute-start = (bf16[1024,768]{1,0:T(8,128)(2,1)S(1)}, bf16[1024,768]{1,0:T(8,128)(2,1)}, u32[]{:S(2)}, u32[]{:S(2)}) collective-permute-start(bf16[1024,768]{1,0:T(8,128)(2,1)S(1)} %copy-done.5), channel_id=1, source_target_pairs={{0,1},{1,2},{2,3},{4,5},{5,6},{6,7},{8,9},{9,10},{10,11},{12,13},{... | collective-permute-start | bytes 4718600 | tf_op jit(solution)/shard_map/ppermute | solution.py:767
  60.3 6.7 %collective-permute-done.5.got_ref = bf16[592,768]{1,0:T(8,128)(2,1)S(1)} collective-permute-done((bf16[592,768]{1,0:T(8,128)(2,1)S(1)}, bf16[592,768]{1,0:T(8,128)(2,1)S(1)}, u32[]{:S(2)}, u32[]{:S(2)}) %collective-permute-start.5) | collective-permute-done | bytes 909344 | tf_op jit(solution)/shard_map/ppermute | solution.py:781
  67.1 3.1 collective-permute-start.6
  70.9 1.2 pad_maximum_fusion
  72.6 10.0 %collective-permute-done = bf16[1024,768]{1,0:T(8,128)(2,1)} collective-permute-done((bf16[1024,768]{1,0:T(8,128)(2,1)S(1)}, bf16[1024,768]{1,0:T(8,128)(2,1)}, u32[]{:S(2)}, u32[]{:S(2)}) %collective-permute-start) | collective-permute-done | bytes 1572896 | tf_op jit(solution)/shard_map/ppermute | solution.py:767
  82.6 1.5 constant_dynamic-update-slice_fusion.1
  84.3 1.7 copy-done.12
  85.9 13.3 %qkv_fwd.1 = (bf16[2048,2304]{1,0:T(8,128)(2,1)}, f32[16,768]{1,0:T(8,128)}, bf16[2304,768]{1,0:T(8,128)(2,1)}) custom-call(s32[8]{0:T(128)} %stack.213.refs_0_, bf16[2048,768]{1,0:T(8,128)(2,1)} %copy-done.12, bf16[1168,768]{1,0:T(8,128)(2,1)} %copy-done.4, bf16[1168,768]{1,0:T(8,128)(2,1)} %collective-permute-done.6.refs_3_), custom_call_target="tpu_custom_call" | custom-call | flops 7247757312 | bytes 15728640 | tf_op jit(solution)/shard_map/qkv_fwd/pallas_call | solution.py:574
  103.9 16.1 %att_fwd.3 = (bf16[1024,768]{1,0:T(8,128)(2,1)}, f32[1024,768]{1,0:T(8,128)}, bf16[1024,768]{1,0:T(8,128)(2,1)}, bf16[2048,768]{1,0:T(8,128)(2,1)}, bf16[2048,768]{1,0:T(8,128)(2,1)}) custom-call(s32[1]{0:T(128)S(6)} %select_n.149.refs_0_.state_ref, bf16[2048,2304]{1,0:T(8,128)(2,1)} %get-tuple-element.81.refs_1_.refs_2_.refs_3_.refs_4_.refs_7_.refs_8_.refs_9_.refs_10_, ...), custom_call_target="tpu_custom_call" | custom-call | flops 6442450944 | bytes 7864320 | tf_op jit(solution)/shard_map/att_fwd/pallas_call | solution.py:137
  120.3 16.4 %att_fwd.4 = (bf16[1024,768]{1,0:T(8,128)(2,1)}, f32[1024,768]{1,0:T(8,128)}, bf16[1024,768]{1,0:T(8,128)(2,1)}, bf16[2048,768]{1,0:T(8,128)(2,1)}, bf16[2048,768]{1,0:T(8,128)(2,1)}) custom-call(s32[1]{0:T(128)S(6)} %select_n.149.refs_0_.state_ref, ...), custom_call_target="tpu_custom_call", output_to_operand_aliasing={{0}: (8, {}), {1}: (9, {}), {2}: (10, {}), {3}: (11, {}), {... | custom-call | flops 6442450944 | bytes 7864320 | tf_op jit(solution)/shard_map/att_fwd/pallas_call | solution.py:137
  136.7 14.8 %collective-permute-done.9.got_ref = bf16[1728,768]{1,0:T(8,128)(2,1)S(1)} collective-permute-done((bf16[1728,768]{1,0:T(8,128)(2,1)S(1)}, bf16[1728,768]{1,0:T(8,128)(2,1)S(1)}, u32[]{:S(2)}, u32[]{:S(2)}) %collective-permute-start.9) | collective-permute-done | bytes 2654240 | tf_op jit(solution)/shard_map/ppermute | solution.py:781
  151.4 2.7 join.7
  154.2 3.2 collective-permute-start.10
  158.7 16.4 %att_fwd.5 = (bf16[1024,768]{1,0:T(8,128)(2,1)}, f32[1024,768]{1,0:T(8,128)}, bf16[1024,768]{1,0:T(8,128)(2,1)}, bf16[2048,768]{1,0:T(8,128)(2,1)}, bf16[2048,768]{1,0:T(8,128)(2,1)}) custom-call(s32[1]{0:T(128)S(6)} %select_n.149.refs_0_.state_ref, ...), custom_call_target="tpu_custom_call", output_to_operand_aliasing={{0}: (8, {}), {1}: (9, {}), {2}: (10, {}), {3}: (11, {}), {... | custom-call | flops 6442450944 | bytes 7864320 | tf_op jit(solution)/shard_map/att_fwd/pallas_call | solution.py:137
  175.1 48.3 %ffn.1 = (bf16[1024,768]{1,0:T(8,128)(2,1)}, f32[1024,768]{1,0:T(8,128)}, bf16[1024,768]{1,0:T(8,128)(2,1)}, f32[1,768]{1,0:T(1,128)}, bf16[36,4,24,768]{3,2,1,0...) custom-call(s32[1]{0:T(128)S(6)} %select_n.149.refs_0_.state_ref, s32[25]{0:T(128)} %stack.208.index_ref, ...), custom_call_target="tpu_custom_call" | custom-call | flops 32614907904 | bytes 40894464 | tf_op jit(solution)/shard_map/ffn/pallas_call | solution.py:724
  223.6 27.9 %att_bwd.3 = (bf16[1024,768]{1,0:T(8,128)(2,1)}, bf16[8,768]{1,0:T(8,128)(2,1)}, bf16[2048,768]{1,0:T(8,128)(2,1)}, bf16[2048,768]{1,0:T(8,128)(2,1)}, f32[16,768]{1,0:T(8,128)}) custom-call(s32[1]{0:T(128)S(6)} %select_n.149.refs_0_.state_ref, bf16[1024,768]{1,0:T(8,128)(2,1)} %get-tuple-element.103.refs_1_, bf16[2048,768]{1,0:T(8,128)(2,1)} %get-tuple-element.104.refs_2_, ...), custom_call_target="tpu_custom_call" | custom-call | flops 16106127360 | bytes 10485760 | tf_op jit(solution)/shard_map/att_bwd/pallas_call | solution.py:270
  251.6 6.3 %merge_grid.4 = (bf16[6,288,768]{2,1,0:T(8,128)(2,1)}, f32[6,288,768]{2,1,0:T(8,128)S(1)}) custom-call(s32[12]{0:T(128)S(1)} %stack.236.index_ref, bf16[12,288,768]{2,1,0:T(8,128)(2,1)S(1)} %bitcast.76, bf16[12,288,768]{2,1,0:T(8,128)(2,1)} %collective-permute-done.11.ga_ref.gb_ref, bf16[12,288,768]{2,1,0:T(8,128)(2,1)S(1)} %bitcast.77, ...), custom_call_target="tpu_custom_call" | custom-call | flops 2654208 | bytes 21233664 | tf_op jit(solution)/shard_map/merge_grid/pallas_call | solution.py:466
  257.9 2.4 copy-done
  260.5 28.1 %att_bwd.4 = (bf16[1024,768]{1,0:T(8,128)(2,1)}, bf16[8,768]{1,0:T(8,128)(2,1)}, bf16[2048,768]{1,0:T(8,128)(2,1)}, bf16[2048,768]{1,0:T(8,128)(2,1)}, f32[16,768]{1,0:T(8,128)}) custom-call(s32[1]{0:T(128)S(6)} %select_n.149.refs_0_.state_ref, ...), custom_call_target="tpu_custom_call", output_to_operand_aliasing={{0}: (14, {}), {1}: (15, {}), {2}: (16, {}), {3}: (17, {}),... | custom-call | flops 16106127360 | bytes 10485760 | tf_op jit(solution)/shard_map/att_bwd/pallas_call | solution.py:270
  288.6 5.3 %collective-permute-done.12.ga_ref.gb_ref = bf16[6,288,768]{2,1,0:T(8,128)(2,1)S(1)} collective-permute-done((bf16[6,288,768]{2,1,0:T(8,128)(2,1)}, bf16[6,288,768]{2,1,0:T(8,128)(2,1)S(1)}, u32[]{:S(2)}, u32[]{:S(2)}) %collective-permute-start.12) | collective-permute-done | bytes 2654240 | tf_op jit(solution)/shard_map/ppermute | solution.py:781
  293.9 2.4 merge_grid.5
  296.3 1.5 copy-done.1
  297.9 28.2 %att_bwd.5 = (bf16[1024,768]{1,0:T(8,128)(2,1)}, bf16[8,768]{1,0:T(8,128)(2,1)}, bf16[2048,768]{1,0:T(8,128)(2,1)}, bf16[2048,768]{1,0:T(8,128)(2,1)}, f32[16,768]{1,0:T(8,128)}) custom-call(s32[1]{0:T(128)S(6)} %select_n.149.refs_0_.state_ref, ...), custom_call_target="tpu_custom_call", output_to_operand_aliasing={{0}: (14, {}), {1}: (15, {}), {2}: (16, {}), {3}: (17, {}),... | custom-call | flops 16106127360 | bytes 10485760 | tf_op jit(solution)/shard_map/att_bwd/pallas_call | solution.py:270
  327.1 22.0 %qkv_bwd.1 = (bf16[1168,768]{1,0:T(8,128)(2,1)}, f32[1168,768]{1,0:T(8,128)}, bf16[1024,768]{1,0:T(8,128)(2,1)}, f32[1024,768]{1,0:T(8,128)}) custom-call(s32[1]{0:T(128)} %bitcast.24.refs_0_.index_ref, bf16[2048,768]{1,0:T(8,128)(2,1)} %copy-done.12, bf16[1024,768]{1,0:T(8,128)(2,1)} %get-tuple-element.132.refs_2_, ...), custom_call_target="tpu_custom_call" | custom-call | flops 12079595520 | bytes 23592960 | tf_op jit(solution)/shard_map/qkv_bwd/pallas_call | solution.py:403
  349.1 1.4 merge_grid.7
  350.7 3.9 collective-permute-done.15.got_ref
  355.5 12.4 %collective-permute-done.16.got_ref = bf16[592,768]{1,0:T(8,128)(2,1)S(1)} collective-permute-done((bf16[592,768]{1,0:T(8,128)(2,1)S(1)}, bf16[592,768]{1,0:T(8,128)(2,1)S(1)}, u32[]{:S(2)}, u32[]{:S(2)}) %collective-permute-start.16) | collective-permute-done | bytes 909344 | tf_op jit(solution)/shard_map/ppermute | solution.py:781
  368.7 7.7 %collective-permute-done.17.got_ref = bf16[304,768]{1,0:T(8,128)(2,1)S(1)} collective-permute-done((bf16[304,768]{1,0:T(8,128)(2,1)S(1)}, bf16[304,768]{1,0:T(8,128)(2,1)S(1)}, u32[]{:S(2)}, u32[]{:S(2)}) %collective-permute-start.17) | collective-permute-done | bytes 466976 | tf_op jit(solution)/shard_map/ppermute | solution.py:781
  376.5 1.5 collective-permute-start.19
  378.1 6.0 %collective-permute-start.21 = (bf16[1,288,768]{2,1,0:T(8,128)(2,1)}, bf16[1,288,768]{2,1,0:T(8,128)(2,1)}, u32[]{:S(2)}, u32[]{:S(2)}) collective-permute-start(bf16[1,288,768]{2,1,0:T(8,128)(2,1)} %get-tuple-element.144), channel_id=1, source_target_pairs={{0,16},{1,17},{2,18},{3,19},{4,20},{5,21},{6,22},{7,23},{8,24},{9,... | collective-permute-start | bytes 1327112 | tf_op jit(solution)/shard_map/ppermute | solution.py:781
  384.2 1.8 fusion.6
  387.8 10.0 %collective-permute-start.20 = (bf16[304,768]{1,0:T(8,128)(2,1)}, bf16[304,768]{1,0:T(8,128)(2,1)S(1)}, u32[]{:S(2)}, u32[]{:S(2)}) collective-permute-start(bf16[304,768]{1,0:T(8,128)(2,1)} %get-tuple-element.154), channel_id=1, source_target_pairs={{8,24},{9,25},{10,26},{11,27},{12,28},{13,29},{14,30},{15,31},{16,... | collective-permute-start | bytes 1400840 | tf_op jit(solution)/shard_map/ppermute | solution.py:781
  397.8 4.6 %collective-permute-start.18 = (bf16[1024,768]{1,0:T(8,128)(2,1)}, bf16[1024,768]{1,0:T(8,128)(2,1)}, u32[]{:S(2)}, u32[]{:S(2)}) collective-permute-start(bf16[1024,768]{1,0:T(8,128)(2,1)} %get-tuple-element.151), channel_id=1, source_target_pairs={{1,0},{2,1},{3,2},{5,4},{6,5},{7,6},{9,8},{10,9},{11,10},{13,12},{... | collective-permute-start | bytes 4718600 | tf_op jit(solution)/shard_map/ppermute | solution.py:767
  403.9 1.2 reshape.127
  405.1 6.9 %collective-permute-done.20 = bf16[304,768]{1,0:T(8,128)(2,1)S(1)} collective-permute-done((bf16[304,768]{1,0:T(8,128)(2,1)}, bf16[304,768]{1,0:T(8,128)(2,1)S(1)}, u32[]{:S(2)}, u32[]{:S(2)}) %collective-permute-start.20) | collective-permute-done | bytes 466976 | tf_op jit(solution)/shard_map/ppermute | solution.py:781
  412.1 1.7 slice_select_fusion
  413.8 4.2 collective-permute-start.22
  419.7 1.6 collective-permute-done.22
  421.3 4.3 fusion.17
  425.6 2.6 fusion.2
  428.3 4.1 fusion.5
  (114 shorter events, 19.3 us)
Async XLA Ops:
  1.5 6.1 %collective-permute-start.1 = (bf16[96,128]{1,0:T(8,128)(2,1)S(1)}, bf16[96,128]{1,0:T(8,128)(2,1)S(1)}, u32[]{:S(2)}, u32[]{:S(2)}) collective-permute-start(bf16[96,128]{1,0:T(8,128)(2,1)S(1)} %slice.35), channel_id=1, source_target_pairs={{0,1},{1,2},{2,3},{3,4},{4,5},{5,6},{6,7},{7,8},{8,9},{9,10},{10,1... | collective-permute-start | bytes 73736 | tf_op jit(solution)/shard_map/ppermute | solution.py:761
  7.5 2.5 copy-start.14
  10.0 50.4 %copy-start.9 = (bf16[3,4,24,768]{3,2,1,0:T(8,128)(2,1)}, bf16[3,4,24,768]{3,2,1,0:T(8,128)(2,1)S(1)}, u32[]{:S(2)}) copy-start(bf16[3,4,24,768]{3,2,1,0:T(8,128)(2,1)S(1)} %copy.37) | copy-start | bytes 1327108
  10.8 44.7 %copy-start.5 = (bf16[1024,768]{1,0:T(8,128)(2,1)S(1)}, bf16[1024,768]{1,0:T(8,128)(2,1)}, u32[]{:S(2)}) copy-start(bf16[1024,768]{1,0:T(8,128)(2,1)} %x_ref.1) | copy-start | bytes 4718596
  10.8 22.9 %collective-permute-start.2 = (bf16[304,768]{1,0:T(8,128)(2,1)}, bf16[304,768]{1,0:T(8,128)(2,1)S(1)}, u32[]{:S(2)}, u32[]{:S(2)}) collective-permute-start(bf16[304,768]{1,0:T(8,128)(2,1)} %pad_maximum_fusion.1), channel_id=1, source_target_pairs={{0,16},{1,17},{2,18},{3,19},{4,20},{5,21},{6,22},{7,23},{8,24},{9,... | collective-permute-start | bytes 1400840 | tf_op jit(solution)/shard_map/ppermute | solution.py:781
  34.7 11.8 %collective-permute-start.3 = (bf16[304,768]{1,0:T(8,128)(2,1)S(1)}, bf16[304,768]{1,0:T(8,128)(2,1)S(1)}, u32[]{:S(2)}, u32[]{:S(2)}) collective-permute-start(bf16[304,768]{1,0:T(8,128)(2,1)S(1)} %pad_maximum_fusion.2), channel_id=1, source_target_pairs={{0,8},{1,9},{2,10},{3,11},{4,12},{5,13},{6,14},{7,15},{8,0},{9,1},... | collective-permute-start | bytes 1400840 | tf_op jit(solution)/shard_map/ppermute | solution.py:781
  46.6 7.8 %collective-permute-start.4 = (bf16[304,768]{1,0:T(8,128)(2,1)S(1)}, bf16[304,768]{1,0:T(8,128)(2,1)S(1)}, u32[]{:S(2)}, u32[]{:S(2)}) collective-permute-start(bf16[304,768]{1,0:T(8,128)(2,1)S(1)} %fusion.16.own_ref), channel_id=1, source_target_pairs={{0,2},{1,5},{2,0},{3,7},{4,6},{5,1},{6,4},{7,3},{8,10},{9,13},{10,... | collective-permute-start | bytes 1400840 | tf_op jit(solution)/shard_map/ppermute | solution.py:781
  54.5 12.5 %collective-permute-start.5 = (bf16[592,768]{1,0:T(8,128)(2,1)S(1)}, bf16[592,768]{1,0:T(8,128)(2,1)S(1)}, u32[]{:S(2)}, u32[]{:S(2)}) collective-permute-start(bf16[592,768]{1,0:T(8,128)(2,1)S(1)} %join.4.own_ref), channel_id=1, source_target_pairs={{0,4},{1,3},{2,6},{3,1},{4,0},{5,7},{6,2},{7,5},{8,12},{9,11},{10,... | collective-permute-start | bytes 2727944 | tf_op jit(solution)/shard_map/ppermute | solution.py:781
  55.5 27.1 %collective-permute-start = (bf16[1024,768]{1,0:T(8,128)(2,1)S(1)}, bf16[1024,768]{1,0:T(8,128)(2,1)}, u32[]{:S(2)}, u32[]{:S(2)}) collective-permute-start(bf16[1024,768]{1,0:T(8,128)(2,1)S(1)} %copy-done.5), channel_id=1, source_target_pairs={{0,1},{1,2},{2,3},{4,5},{5,6},{6,7},{8,9},{9,10},{10,11},{12,13},{... | collective-permute-start | bytes 4718600 | tf_op jit(solution)/shard_map/ppermute | solution.py:767
  67.1 17.1 %copy-start.4 = (bf16[1168,768]{1,0:T(8,128)(2,1)}, bf16[1168,768]{1,0:T(8,128)(2,1)S(1)}, u32[]{:S(2)}) copy-start(bf16[1168,768]{1,0:T(8,128)(2,1)S(1)} %join.5.refs_2_) | copy-start | bytes 5382148
  67.1 18.8 %collective-permute-start.6 = (bf16[1168,768]{1,0:T(8,128)(2,1)S(1)}, bf16[1168,768]{1,0:T(8,128)(2,1)}, u32[]{:S(2)}, u32[]{:S(2)}) collective-permute-start(bf16[1168,768]{1,0:T(8,128)(2,1)S(1)} %join.5.refs_2_), channel_id=1, source_target_pairs={{0,1},{1,0},{2,3},{3,2},{4,5},{5,4},{6,7},{7,6},{8,9},{9,8},{10,11... | collective-permute-start | bytes 5382152 | tf_op jit(solution)/shard_map/ppermute | solution.py:781
  72.1 27.1 %collective-permute-start.7 = (bf16[576,768]{1,0:T(8,128)(2,1)S(1)}, bf16[576,768]{1,0:T(8,128)(2,1)S(1)}, u32[]{:S(2)}, u32[]{:S(2)}) collective-permute-start(bf16[576,768]{1,0:T(8,128)(2,1)S(1)} %pad_maximum_fusion), channel_id=1, source_target_pairs={{0,8},{1,9},{2,10},{3,11},{4,12},{5,13},{6,14},{7,15},{8,0},{9,1},... | collective-permute-start | bytes 2654216 | tf_op jit(solution)/shard_map/ppermute | solution.py:781
  84.2 1.7 copy-start.12
  99.2 4.1 copy-start.13
  100.0 20.0 %collective-permute-start.8 = (bf16[864,768]{1,0:T(8,128)(2,1)S(1)}, bf16[864,768]{1,0:T(8,128)(2,1)S(1)}, u32[]{:S(2)}, u32[]{:S(2)}) collective-permute-start(bf16[864,768]{1,0:T(8,128)(2,1)S(1)} %bitcast.78), channel_id=1, source_target_pairs={{0,2},{1,5},{2,0},{3,7},{4,6},{5,1},{6,4},{7,3},{8,10},{9,13},{10,... | collective-permute-start | bytes 3981320 | tf_op jit(solution)/shard_map/ppermute | solution.py:781
  120.2 31.2 %collective-permute-start.9 = (bf16[1728,768]{1,0:T(8,128)(2,1)S(1)}, bf16[1728,768]{1,0:T(8,128)(2,1)S(1)}, u32[]{:S(2)}, u32[]{:S(2)}) collective-permute-start(bf16[1728,768]{1,0:T(8,128)(2,1)S(1)} %join.6.own_ref), channel_id=1, source_target_pairs={{0,4},{1,3},{2,6},{3,1},{4,0},{5,7},{6,2},{7,5},{8,12},{9,11},{10,... | collective-permute-start | bytes 7962632 | tf_op jit(solution)/shard_map/ppermute | solution.py:781
  154.2 20.9 %collective-permute-start.10 = (bf16[3456,768]{1,0:T(8,128)(2,1)}, bf16[3456,768]{1,0:T(8,128)(2,1)}, u32[]{:S(2)}, u32[]{:S(2)}) collective-permute-start(bf16[3456,768]{1,0:T(8,128)(2,1)} %join.7), channel_id=1, source_target_pairs={{0,1},{1,0},{2,3},{3,2},{4,5},{5,4},{6,7},{7,6},{8,9},{9,8},{10,11... | collective-permute-start | bytes 15925256 | tf_op jit(solution)/shard_map/ppermute | solution.py:781
  223.4 28.1 %collective-permute-start.11 = (bf16[12,288,768]{2,1,0:T(8,128)(2,1)}, bf16[12,288,768]{2,1,0:T(8,128)(2,1)}, u32[]{:S(2)}, u32[]{:S(2)}) collective-permute-start(bf16[12,288,768]{2,1,0:T(8,128)(2,1)} %bitcast.85), channel_id=1, source_target_pairs={{0,1},{1,0},{2,3},{3,2},{4,5},{5,4},{6,7},{7,6},{8,9},{9,8},{10,11... | collective-permute-start | bytes 15925256 | tf_op jit(solution)/shard_map/ppermute | solution.py:781
  223.6 27.9 %slice-start.2 = ((s8[5308416]{0:T(1024)(128)(4,1)}), s8[4194304]{0:T(1024)(128)(4,1)S(1)}, s32[]{:S(2)}) async-start(s8[5308416]{0:T(1024)(128)(4,1)} %bitcast.74), calls=%async_computation.2 | async-start | bytes 8388608
  223.6 27.9 %slice-start.3 = ((s8[5308416]{0:T(1024)(128)(4,1)}), s8[1114112]{0:T(1024)(128)(4,1)S(1)}, s32[]{:S(2)}) async-start(s8[5308416]{0:T(1024)(128)(4,1)} %bitcast.74), calls=%async_computation.3 | async-start | bytes 2228224
  257.9 2.4 copy-start
  260.3 33.7 %collective-permute-start.12 = (bf16[6,288,768]{2,1,0:T(8,128)(2,1)}, bf16[6,288,768]{2,1,0:T(8,128)(2,1)S(1)}, u32[]{:S(2)}, u32[]{:S(2)}) collective-permute-start(bf16[6,288,768]{2,1,0:T(8,128)(2,1)} %get-tuple-element.112), channel_id=1, source_target_pairs={{0,2},{1,5},{2,0},{3,7},{4,6},{5,1},{6,4},{7,3},{8,10},{9,13},{10,... | collective-permute-start | bytes 7962632 | tf_op jit(solution)/shard_map/ppermute | solution.py:781
  260.5 33.4 %slice-start = ((s8[5308416]{0:T(1024)(128)(4,1)}), s8[4194304]{0:T(1024)(128)(4,1)S(1)}, s32[]{:S(2)}) async-start(s8[5308416]{0:T(1024)(128)(4,1)} %bitcast.72), calls=%async_computation | async-start | bytes 8388608
  260.5 33.4 %slice-start.1 = ((s8[5308416]{0:T(1024)(128)(4,1)}), s8[1114112]{0:T(1024)(128)(4,1)S(1)}, s32[]{:S(2)}) async-start(s8[5308416]{0:T(1024)(128)(4,1)} %bitcast.72), calls=%async_computation.1 | async-start | bytes 2228224
  296.3 1.5 copy-start.1
  297.9 28.3 %collective-permute-start.13 = (bf16[3,288,768]{2,1,0:T(8,128)(2,1)}, bf16[3,288,768]{2,1,0:T(8,128)(2,1)S(1)}, u32[]{:S(2)}, u32[]{:S(2)}) collective-permute-start(bf16[3,288,768]{2,1,0:T(8,128)(2,1)} %get-tuple-element.121), channel_id=1, source_target_pairs={{0,4},{1,3},{2,6},{3,1},{4,0},{5,7},{6,2},{7,5},{8,12},{9,11},{10,... | collective-permute-start | bytes 3981320 | tf_op jit(solution)/shard_map/ppermute | solution.py:781
  297.9 28.3 %copy-start.2 = (f32[3,288,768]{2,1,0:T(8,128)S(1)}, f32[3,288,768]{2,1,0:T(8,128)}, u32[]{:S(2)}) copy-start(f32[3,288,768]{2,1,0:T(8,128)} %copy-done.1) | copy-start | bytes 7962628
  327.0 22.1 %collective-permute-start.14 = (bf16[2,288,768]{2,1,0:T(8,128)(2,1)S(1)}, bf16[2,288,768]{2,1,0:T(8,128)(2,1)S(1)}, u32[]{:S(2)}, u32[]{:S(2)}) collective-permute-start(bf16[2,288,768]{2,1,0:T(8,128)(2,1)S(1)} %get-tuple-element.130), channel_id=1, source_target_pairs={{0,8},{1,9},{2,10},{3,11},{4,12},{5,13},{6,14},{7,15},{8,0},{9,1},... | collective-permute-start | bytes 2654216 | tf_op jit(solution)/shard_map/ppermute | solution.py:781
  349.1 5.4 %copy-start.3 = (f32[1168,768]{1,0:T(8,128)S(1)}, f32[1168,768]{1,0:T(8,128)}, u32[]{:S(2)}) copy-start(f32[1168,768]{1,0:T(8,128)} %get-tuple-element.140.keep_ref) | copy-start | bytes 10764292
  350.6 3.9 collective-permute-start.15
  355.4 28.7 %copy-start.15 = (pred[3]{0:T(512)(128)(4,1)S(1)}, pred[3]{0:T(512)(128)(4,1)}, u32[]{:S(2)}) copy-start(pred[3]{0:T(512)(128)(4,1)} %copy-done.14) | copy-start | bytes 13
  355.4 12.5 %collective-permute-start.16 = (bf16[592,768]{1,0:T(8,128)(2,1)S(1)}, bf16[592,768]{1,0:T(8,128)(2,1)S(1)}, u32[]{:S(2)}, u32[]{:S(2)}) collective-permute-start(bf16[592,768]{1,0:T(8,128)(2,1)S(1)} %get-tuple-element.147), channel_id=1, source_target_pairs={{0,2},{1,5},{2,0},{3,7},{4,6},{5,1},{6,4},{7,3},{8,10},{9,13},{10,... | collective-permute-start | bytes 2727944 | tf_op jit(solution)/shard_map/ppermute | solution.py:781
  368.7 7.8 %collective-permute-start.17 = (bf16[304,768]{1,0:T(8,128)(2,1)S(1)}, bf16[304,768]{1,0:T(8,128)(2,1)S(1)}, u32[]{:S(2)}, u32[]{:S(2)}) collective-permute-start(bf16[304,768]{1,0:T(8,128)(2,1)S(1)} %get-tuple-element.149), channel_id=1, source_target_pairs={{0,4},{1,3},{2,6},{3,1},{4,0},{5,7},{6,2},{7,5},{8,12},{9,11},{10,... | collective-permute-start | bytes 1400840 | tf_op jit(solution)/shard_map/ppermute | solution.py:781
  376.5 10.4 %collective-permute-start.19 = (bf16[304,768]{1,0:T(8,128)(2,1)S(1)}, bf16[304,768]{1,0:T(8,128)(2,1)S(1)}, u32[]{:S(2)}, u32[]{:S(2)}) collective-permute-start(bf16[304,768]{1,0:T(8,128)(2,1)S(1)} %get-tuple-element.150), channel_id=1, source_target_pairs={{0,8},{1,9},{2,10},{3,11},{4,12},{5,13},{6,14},{7,15},{8,0},{9,1},... | collective-permute-start | bytes 1400840 | tf_op jit(solution)/shard_map/ppermute | solution.py:781
  378.1 24.4 %collective-permute-start.21 = (bf16[1,288,768]{2,1,0:T(8,128)(2,1)}, bf16[1,288,768]{2,1,0:T(8,128)(2,1)}, u32[]{:S(2)}, u32[]{:S(2)}) collective-permute-start(bf16[1,288,768]{2,1,0:T(8,128)(2,1)} %get-tuple-element.144), channel_id=1, source_target_pairs={{0,16},{1,17},{2,18},{3,19},{4,20},{5,21},{6,22},{7,23},{8,24},{9,... | collective-permute-start | bytes 1327112 | tf_op jit(solution)/shard_map/ppermute | solution.py:781
  387.8 24.1 %collective-permute-start.20 = (bf16[304,768]{1,0:T(8,128)(2,1)}, bf16[304,768]{1,0:T(8,128)(2,1)S(1)}, u32[]{:S(2)}, u32[]{:S(2)}) collective-permute-start(bf16[304,768]{1,0:T(8,128)(2,1)} %get-tuple-element.154), channel_id=1, source_target_pairs={{8,24},{9,25},{10,26},{11,27},{12,28},{13,29},{14,30},{15,31},{16,... | collective-permute-start | bytes 1400840 | tf_op jit(solution)/shard_map/ppermute | solution.py:781
  397.8 27.8 %collective-permute-start.18 = (bf16[1024,768]{1,0:T(8,128)(2,1)}, bf16[1024,768]{1,0:T(8,128)(2,1)}, u32[]{:S(2)}, u32[]{:S(2)}) collective-permute-start(bf16[1024,768]{1,0:T(8,128)(2,1)} %get-tuple-element.151), channel_id=1, source_target_pairs={{1,0},{2,1},{3,2},{5,4},{6,5},{7,6},{9,8},{10,9},{11,10},{13,12},{... | collective-permute-start | bytes 4718600 | tf_op jit(solution)/shard_map/ppermute | solution.py:767
  412.0 1.8 copy-start.10
  412.1 9.2 %copy-start.8 = (f32[1731,128]{1,0:T(8,128)S(1)}, f32[1731,128]{1,0:T(8,128)}, u32[]{:S(2)}) copy-start(f32[1731,128]{1,0:T(8,128)} %param.10) | copy-start | bytes 2658820
  413.8 7.4 %collective-permute-start.22 = (f32[96,128]{1,0:T(8,128)S(1)}, f32[96,128]{1,0:T(8,128)S(1)}, u32[]{:S(2)}, u32[]{:S(2)}) collective-permute-start(f32[96,128]{1,0:T(8,128)S(1)} %slice.44), channel_id=1, source_target_pairs={{1,0},{2,1},{3,2},{4,3},{5,4},{6,5},{7,6},{8,7},{9,8},{10,9},{11,1... | collective-permute-start | bytes 147464 | tf_op jit(solution)/shard_map/ppermute | solution.py:761
  421.3 4.3 copy-start.6
  421.3 4.3 copy-start.7
  425.6 2.6 copy-start.11

commit v7 on v6

--- a/solution.py
+++ b/solution.py
@@ -37,18 +37,35 @@
     return pl.CostEstimate(flops=int(flops), bytes_accessed=int(nbytes), transcendentals=int(exps))
 
 
-def taps_seen(height, start, rows, state, distance, ahead):
-    row = lax.broadcasted_iota(jnp.int32, (height, 128), 0) + (start + ahead)
-    own = row - rows
-    inside = (own >= distance) | ((own < 0) & (row >= distance)) | ((own >= 0) & (state == 2))
-    filled = ((own < 0) | (state > 0)) & (row < 2 * rows)
-    return (inside & filled).astype(F32)
-
-
-def conv(x, taps, mask_one, mask_two):
-    one = pltpu.roll(x, 1, 0) * mask_one
-    two = pltpu.roll(x, 2, 0) * mask_two
-    return (taps[0:1] * x + taps[1:2] * one + taps[2:3] * two).astype(BF)
+def row_ids(height):
+    return lax.broadcasted_iota(jnp.int32, (height, 128), 0)
+
+
+def conv(out_ref, x_ref, start, tail_ref, taps, rows, state):
+    height = x_ref.shape[0]
+    for r in range(0, height, QB):
+        at = start + r
+        if r:
+            x = x_ref[r - 16 : r + QB, :].astype(F32)
+        else:
+            before = jnp.zeros((16, 128), F32)
+            if tail_ref is not None:
+                before = jnp.concatenate([before[8:], tail_ref[...].astype(F32)], 0)
+            x = jnp.concatenate([before, x_ref[0:QB, :].astype(F32)], 0)
+        one = pltpu.roll(x, 1, 0)[16:]
+        two = pltpu.roll(x, 2, 0)[16:]
+        x = x[16:]
+        scale = 1.0
+        if at >= rows:
+            scale = jnp.where(state > 0, 1.0, 0.0)
+        if at == 0 or at == rows:
+            seen = jnp.where(state == 2, 1.0, 0.0) if at else 0.0
+            row = row_ids(QB)
+            one = jnp.where(row < 1, one * seen, one)
+            two = jnp.where(row < 2, two * seen, two)
+        c_one = taps[1:2] * scale
+        c_two = taps[2:3] * scale
+        out_ref[r : r + QB, :] = (taps[0:1] * x + c_one * one + c_two * two).astype(BF)
 
 
 def att_fwd_kernel(
@@ -58,22 +75,18 @@
     rows = q_ref.shape[0]
     lane = lax.broadcasted_iota(jnp.int32, (1, 128), 1)
     state = state_ref[0]
-    one = taps_seen(2 * rows, 0, rows, state, 1, 0)
-    two = taps_seen(2 * rows, 0, rows, state, 2, 0)
-    x = jnp.concatenate([tail_ref[...].astype(F32), q_ref[...].astype(F32)], 0)
-    qm_ref[...] = conv(x, tq_ref[...], one[rows - 8 :], two[rows - 8 :])[8:]
-    k = conv(k_ref[...].astype(F32), tk_ref[...], one, two)
-    v = conv(v_ref[...].astype(F32), tv_ref[...], one, two)
-    km_ref[...] = k
-    vm_ref[...] = v
+    conv(qm_ref, q_ref, rows, tail_ref, tq_ref[...], rows, state)
+    conv(km_ref, k_ref, 0, None, tk_ref[...], rows, state)
+    conv(vm_ref, v_ref, 0, None, tv_ref[...], rows, state)
     bias = jnp.where(state == 2, 0.0, -1e30)
     for h in range(2):
         mine = (lane < 64) if h == 0 else (lane >= 64)
         base = 64 if h == 0 else 0
         first = jnp.where(lane == base, bias, 0.0).astype(BF)
-        ka[h, 0:rows, :] = jnp.where(mine, k[:rows], first)
-        ka[h, rows:, :] = jnp.where(mine, k[rows:], jnp.zeros((), BF))
-        va[h] = jnp.where(mine, v, jnp.ones((), BF))
+        for r in range(0, 2 * rows, QB):
+            at = pl.ds(r, QB)
+            ka[h, at, :] = jnp.where(mine, km_ref[at, :], first if r < rows else jnp.zeros((), BF))
+            va[h, at, :] = jnp.where(mine, vm_ref[at, :], jnp.ones((), BF))
     for i in range(rows // QB):
         rs = pl.ds(i * QB, QB)
         outs = []
@@ -174,13 +187,37 @@
     )
 
 
-def conv_back(grad, x, taps, mask_one, mask_two):
-    height = grad.shape[0]
-    one = pltpu.roll(grad, height - 1, 0) * mask_one
-    two = pltpu.roll(grad, height - 2, 0) * mask_two
-    back = (taps[0:1] * grad + taps[1:2] * one + taps[2:3] * two).astype(BF)
-    sums = [jnp.sum(g * x, axis=0, keepdims=True) for g in (grad, one, two)]
-    return back, sums
+def conv_back(out_ref, grad_ref, x_ref, start, tail, taps, rows, state):
+    height = grad_ref.shape[0]
+    joint = jnp.where(state == 2, 1.0, 0.0)
+    sums = [jnp.zeros((1, 128), F32)] * 3
+
+    def add(parts, x):
+        return [s + jnp.sum(g * x, axis=0, keepdims=True) for s, g in zip(sums, parts)]
+
+    for r in range(0, height, QB):
+        ends = r + QB == height
+        meets = start + r + QB == rows
+        if ends:
+            grad = jnp.concatenate([grad_ref[r : r + QB, :], jnp.zeros((8, 128), F32)], 0)
+        else:
+            grad = grad_ref[r : r + QB + 8, :]
+        one = pltpu.roll(grad, QB + 7, 0)[:QB]
+        two = pltpu.roll(grad, QB + 6, 0)[:QB]
+        grad = grad[:QB]
+        if meets and not ends:
+            row = row_ids(QB)
+            one = jnp.where(row >= QB - 1, one * joint, one)
+            two = jnp.where(row >= QB - 2, two * joint, two)
+        out_ref[r : r + QB, :] = (taps[0:1] * grad + taps[1:2] * one + taps[2:3] * two).astype(BF)
+        sums = add((grad, one, two), x_ref[r : r + QB, :].astype(F32))
+    if tail is not None:
+        grad = jnp.concatenate([jnp.zeros((8, 128), F32), grad_ref[0:8, :]], 0)
+        one = pltpu.roll(grad, 15, 0)[:8] * joint
+        two = pltpu.roll(grad, 14, 0)[:8] * joint
+        tail[0][...] = (taps[1:2] * one + taps[2:3] * two).astype(BF)
+        sums = add((grad[:8], one, two), tail[1][...].astype(F32))
+    return sums
 
 
 def att_bwd_kernel(
@@ -191,19 +228,23 @@
     rows = q_ref.shape[0]
     lane = lax.broadcasted_iota(jnp.int32, (1, 128), 1)
     second = state_ref[0] == 2
-    do = do_ref[...].astype(F32)
-    od = do * o_ref[...].astype(F32)
-    qf = q_ref[...].astype(F32) * 0.125
-    lv = l_ref[...]
-    for h in range(2):
-        mine = (lane < 64) if h == 0 else (lane >= 64)
-        base = 64 if h == 0 else 0
-        delta = jnp.sum(jnp.where(mine, od, 0.0), axis=1, keepdims=True)
-        qa[h] = jnp.where(mine, qf, three(-lv, lane, base)).astype(BF)
-        da[h] = jnp.where(mine, do, three(-delta, lane, base)).astype(BF)
-    qt[...] = jnp.transpose(qf).astype(BF)
-    dt[...] = jnp.transpose(do).astype(BF)
-    kt[...] = jnp.transpose(k_ref[...].astype(F32)).astype(BF)
+    for r in range(0, rows, QB):
+        at = pl.ds(r, QB)
+        do = do_ref[at, :].astype(F32)
+        od = do * o_ref[at, :].astype(F32)
+        qf = q_ref[at, :].astype(F32) * 0.125
+        lv = l_ref[at, :]
+        for h in range(2):
+            mine = (lane < 64) if h == 0 else (lane >= 64)
+            base = 64 if h == 0 else 0
+            delta = jnp.sum(jnp.where(mine, od, 0.0), axis=1, keepdims=True)
+            qa[h, at, :] = jnp.where(mine, qf, three(-lv, lane, base)).astype(BF)
+            da[h, at, :] = jnp.where(mine, do, three(-delta, lane, base)).astype(BF)
+        qt[:, at] = jnp.transpose(qf).astype(BF)
+        dt[:, at] = jnp.transpose(do).astype(BF)
+    for r in range(0, 2 * rows, QB):
+        at = pl.ds(r, QB)
+        kt[:, at] = jnp.transpose(k_ref[at, :].astype(F32)).astype(BF)
     dqt[...] = jnp.zeros(dqt.shape, F32)
 
     def keys(ks, first, diagonal):
@@ -247,16 +288,12 @@
         dks[0:rows, :] = jnp.zeros((rows, 128), F32)
         dvs[0:rows, :] = jnp.zeros((rows, 128), F32)
 
-    dqs[0:8, :] = jnp.zeros((8, 128), F32)
-    dqs[8:, :] = jnp.transpose(dqt[...]) * 0.125
-    one = taps_seen(2 * rows, 0, rows, state_ref[0], 1, 1)
-    two = taps_seen(2 * rows, 0, rows, state_ref[0], 2, 2)
-    xq = jnp.concatenate([xt_ref[...].astype(F32), xq_ref[...].astype(F32)], 0)
-    pq, sq = conv_back(dqs[...], xq, tq_ref[...], one[rows - 8 :], two[rows - 8 :])
-    pt_ref[...] = pq[:8]
-    pq_ref[...] = pq[8:]
-    pk_ref[...], sk = conv_back(dks[...], xk_ref[...].astype(F32), tk_ref[...], one, two)
-    pv_ref[...], sv = conv_back(dvs[...], xv_ref[...].astype(F32), tv_ref[...], one, two)
+    for r in range(0, rows, QB):
+        dqs[r : r + QB, :] = jnp.transpose(dqt[:, r : r + QB]) * 0.125
+    state = state_ref[0]
+    sq = conv_back(pq_ref, dqs, xq_ref, rows, (pt_ref, xt_ref), tq_ref[...], rows, state)
+    sk = conv_back(pk_ref, dks, xk_ref, 0, None, tk_ref[...], rows, state)
+    sv = conv_back(pv_ref, dvs, xv_ref, 0, None, tv_ref[...], rows, state)
     tg_ref[...] = jnp.zeros(tg_ref.shape, F32)
     for j in range(3):
         for m, s in enumerate((sq, sk, sv)):
@@ -295,7 +332,7 @@
             pltpu.VMEM((128, rows), BF),
             pltpu.VMEM((128, 2 * rows), BF),
             pltpu.VMEM((128, rows), F32),
-            pltpu.VMEM((rows + 8, 128), F32),
+            pltpu.VMEM((rows, 128), F32),
             pltpu.VMEM((2 * rows, 128), F32),
             pltpu.VMEM((2 * rows, 128), F32),
         ],
@@ -309,50 +346,84 @@
       taps, taps, taps, *earlier)
 
 
+def unit_rows(x):
+    return x * lax.rsqrt(jnp.mean(x * x, axis=-1, keepdims=True) + norm_eps)
+
+
+def before_bwd_kernel(x_ref, dt_ref, dk_ref, dv_ref, w_ref, out_ref, gain_ref):
+    i = pl.program_id(0)
+    hat = unit_rows(x_ref[...].astype(F32))
+    gn = dot_nt(dk_ref[...], w_ref[D : 2 * D, :]) + dot_nt(dv_ref[...], w_ref[2 * D : 3 * D, :])
+
+    @pl.when(i == 0)
+    def _():
+        out_ref[...] = gn.astype(BF)
+        gain_ref[...] = jnp.sum(gn * hat, axis=0, keepdims=True)
+
+    @pl.when(i > 0)
+    def _():
+        last = gn.shape[0] - 8
+        full = jnp.concatenate([gn[:last], gn[last:] + dot_nt(dt_ref[...], w_ref[0:D, :])], 0)
+        out_ref[...] = full.astype(BF)
+        gain_ref[...] += jnp.sum(full * hat, axis=0, keepdims=True)
+
+
+def before_bwd(x_both, back, weight, rows):
+    dt, dk, dv = back[1:]
+    height = rows // 2
+    step = pl.BlockSpec((height, D), lambda i: (i, 0))
+
+    def whole(shape):
+        return pl.BlockSpec(shape, lambda i: (0, 0))
+
+    return pl.pallas_call(
+        before_bwd_kernel,
+        grid=(2,),
+        in_specs=[step, whole((8, D)), step, step, whole((3 * D, D))],
+        out_specs=[step, whole((1, D))],
+        out_shape=[jax.ShapeDtypeStruct((rows, D), BF), jax.ShapeDtypeStruct((1, D), F32)],
+        compiler_params=pltpu.CompilerParams(vmem_limit_bytes=VMEM_LIMIT),
+        cost_estimate=cost(2 * rows * D * D * 2, rows * D * 12),
+        name="before_bwd",
+    )(x_both, dt, dk, dv, weight)
+
+
 def qkv_bwd_kernel(
-    core_ref, x_ref, dq_ref, dt_ref, dk_ref, dv_ref, w_ref, gain_ref, gain_two_ref, tg_ref,
+    core_ref, x_ref, dq_ref, dt_ref, dk_ref, dv_ref, w_ref, gain_ref, gain_one_ref, gain_two_ref, tg_ref,
     *refs, pieces, blocks,
 ):
     if pieces:
-        send_ref, keep_ref, prev_ref, own_ref, acc, gacc = refs
+        send_ref, keep_ref, own_ref, acc, gacc = refs
     else:
-        keep_ref, small_ref, prev_ref, own_ref, acc, gacc = refs
+        keep_ref, small_ref, own_ref, acc, gacc = refs
     i = pl.program_id(0)
     half = blocks // 2
 
     @pl.when(i == 0)
     def _():
         acc[...] = jnp.zeros(acc.shape, F32)
-        gacc[...] = jnp.zeros(gacc.shape, F32)
-
-    x = x_ref[...].astype(F32)
-    hat = x * lax.rsqrt(jnp.mean(x * x, axis=-1, keepdims=True) + norm_eps)
+        gacc[0:1, :] = gain_one_ref[...]
+
+    hat = unit_rows(x_ref[...].astype(F32))
     low = (hat * gain_ref[...]).astype(BF)
     dk = dk_ref[...]
     dv = dv_ref[...]
-    gn = dot_nt(dk, w_ref[D : 2 * D, :]) + dot_nt(dv, w_ref[2 * D : 3 * D, :])
     acc[D : 2 * D, :] += dot_tn(low, dk)
     acc[2 * D : 3 * D, :] += dot_tn(low, dv)
 
-    @pl.when(i < half - 1)
-    def _():
-        prev_ref[...] = gn.astype(BF)
-        gacc[0:1, :] += jnp.sum(gn * hat, axis=0, keepdims=True)
-
     @pl.when(i == half - 1)
     def _():
-        dt = dt_ref[...]
-        last = gn.shape[0] - 8
-        acc[0:D, :] += dot_tn(low[last:], dt)
-        full = jnp.concatenate([gn[:last], gn[last:] + dot_nt(dt, w_ref[0:D, :])], 0)
-        prev_ref[...] = full.astype(BF)
-        gacc[0:1, :] += jnp.sum(full * hat, axis=0, keepdims=True)
+        acc[0:D, :] += dot_tn(low[low.shape[0] - 8 :], dt_ref[...])
 
     @pl.when(i >= half)
     def _():
         dq = dq_ref[...]
         acc[0:D, :] += dot_tn(low, dq)
-        full = gn + dot_nt(dq, w_ref[0:D, :])
+        full = (
+            dot_nt(dk, w_ref[D : 2 * D, :])
+            + dot_nt(dv, w_ref[2 * D : 3 * D, :])
+            + dot_nt(dq, w_ref[0:D, :])
+        )
         own_ref[...] = full
         gacc[0:1, :] += jnp.sum(full * hat, axis=0, keepdims=True)
 
@@ -364,33 +435,33 @@
         if pieces:
             core = core_ref[0]
             height = 3 * D // (2 * pieces)
+            wide = height + 16
             for j in range(pieces):
-                to = pl.ds(j * height, height)
-                away = pl.ds(pl.multiple_of((2 * j + 1 - core) * height, 16), height)
-                here = pl.ds(pl.multiple_of((2 * j + core) * height, 16), height)
+                to = pl.ds(j * wide, wide)
+                away = pl.ds(pl.multiple_of((2 * j + 1 - core) * height, 16), wide)
+                here = pl.ds(pl.multiple_of((2 * j + core) * height, 16), wide)
                 send_ref[to, :] = acc[away, :].astype(BF)
                 keep_ref[to, :] = acc[here, :]
-            send_ref[pieces * height :, :] = small.astype(BF)
-            keep_ref[pieces * height :, :] = small
+            send_ref[pieces * wide :, :] = small.astype(BF)
+            keep_ref[pieces * wide :, :] = small
         else:
-            keep_ref[...] = acc[...].astype(BF)
+            keep_ref[...] = acc[0 : 3 * D, :].astype(BF)
             small_ref[...] = small
 
 
-def qkv_bwd(core, x_both, back, wide, gain, gain_two_grad, tap_grads, rows, pieces):
+def qkv_bwd(core, x_both, back, weight, gain, gain_one_grad, gain_two_grad, tap_grads, rows, pieces):
     dq, dt, dk, dv = back
     blocks = 4
     half = blocks // 2
     height = 2 * rows // blocks
     step = pl.BlockSpec((height, D), lambda i: (i, 0))
     late = pl.BlockSpec((height, D), lambda i: (jnp.maximum(i - half, 0), 0))
-    early = pl.BlockSpec((height, D), lambda i: (jnp.minimum(i, half - 1), 0))
 
     def whole(shape):
         return pl.BlockSpec(shape, lambda i: (0, 0))
 
     if pieces:
-        packed = 3 * D // 2 + 16
+        packed = 3 * D // 2 + 16 * pieces + 16
         outs = [jax.ShapeDtypeStruct((packed, D), BF), jax.ShapeDtypeStruct((packed, D), F32)]
         out_at = [whole((packed, D))] * 2
     else:
@@ -406,16 +477,15 @@
         in_specs=[
             pl.BlockSpec(memory_space=pltpu.SMEM),
             step, late, whole((8, D)), step, step, whole((3 * D, D)),
-            whole((1, D)), whole((1, D)), whole((16, D)),
+            whole((1, D)), whole((1, D)), whole((1, D)), whole((16, D)),
         ],
-        out_specs=out_at + [early, late],
-        out_shape=outs
-        + [jax.ShapeDtypeStruct((rows, D), BF), jax.ShapeDtypeStruct((rows, D), F32)],
-        scratch_shapes=[pltpu.VMEM((3 * D, D), F32), pltpu.VMEM((8, D), F32)],
+        out_specs=out_at + [late],
+        out_shape=outs + [jax.ShapeDtypeStruct((rows, D), F32)],
+        scratch_shapes=[pltpu.VMEM((3 * D + 16, D), F32), pltpu.VMEM((8, D), F32)],
         compiler_params=pltpu.CompilerParams(vmem_limit_bytes=VMEM_LIMIT),
-        cost_estimate=cost(2 * 2 * D * D * 5 * rows, rows * D * 30),
+        cost_estimate=cost(2 * 2 * D * D * 4 * rows, rows * D * 30),
         name="qkv_bwd",
-    )(core, x_both, dq, dt, dk, dv, wide, gain, gain_two_grad, tap_grads)
+    )(core, x_both, dq, dt, dk, dv, weight, gain, gain_one_grad, gain_two_grad, tap_grads)
 
 
 def merge(index, keep, got, height, taken):
@@ -895,6 +965,7 @@
         z = place >> 3
         mine = jnp.concatenate([chunk, small.astype(BF).reshape(-1, D)], 0)
         got = swap(mine, 16, 16)
+        got = after(got, tokens_both)
         rest = jnp.concatenate([chunk, got[:height]], 0)
         none = jnp.zeros((), BF)
         first = jnp.where(z == 0, chunk, jnp.where(z == 2, got[:height], none))
@@ -903,7 +974,13 @@
         across = swap(after(rest, mine), 8, 8)
         mine = join(mine, swap(mine, 2, 4))
         mine = join(mine, swap(mine, 4, 2))
-        got = swap(mine, 1, 1)
+        codes = [z ^ k for k in (1, 2, 3)]
+        order = [jnp.where(j == 1, 2, jnp.where(j == 2, 1, j)) for j in codes]
+        rest = arrange(
+            jnp.stack(order).astype(jnp.int32), rest.reshape(2, height, D), across.reshape(2, height, D), 3
+        ).reshape(-1, D)
+        across = swap(rest, 2, 4)
+        got = swap(after(mine, rest), 1, 1)
         index = []
         late_index = []
         for k in (0, 1):
@@ -918,12 +995,6 @@
         index = jnp.stack(index).astype(jnp.int32)
         late_index = jnp.stack(late_index + [core[0]]).astype(jnp.int32)
         projected, small, in_weight = qkv_fwd(index, tokens_both, (mine, got), rows, 4)
-        codes = [z ^ k for k in (1, 2, 3)]
-        order = [jnp.where(j == 1, 2, jnp.where(j == 2, 1, j)) for j in codes]
-        rest = arrange(
-            after(jnp.stack(order).astype(jnp.int32), projected), rest.reshape(2, height, D), across.reshape(2, height, D), 3
-        ).reshape(-1, D)
-        across = swap(rest, 2, 4)
     else:
         wide = lax.all_gather(chunk, AXES, axis=0, tiled=True)
         small = lax.psum(small, AXES)[:96].reshape(-1, D)
@@ -936,10 +1007,10 @@
 
     forward = []
     if staged:
+        rest = join(after(rest, projected), across, 0)
+        across = swap(rest, 4, 2)
         forward = att_fwd(after(state_vec, rest), projected, taps, forward, 0, rows)
-        rest = join(after(rest, forward[0]), across, 0)
-        across = swap(rest, 4, 2)
-        forward = att_fwd(after(state_vec, rest), projected, taps, forward, 1, rows)
+        forward = att_fwd(state_vec, projected, taps, forward, 1, rows)
         rest = join(after(rest, forward[0]), across, 0)
         across = swap(rest, 1, 1)
         forward = att_fwd(after(state_vec, rest), projected, taps, forward, 2, rows)
@@ -1005,34 +1076,45 @@
             done = backward(state_vec, done, part)
         sums_state = core
     *back, tap_grads = done
+    grads_before, gain_one_grad = before_bwd(tokens_both, back, in_weight, rows)
+    from_next = shift_ctx(grads_before, -1)
     sums = qkv_bwd(
-        sums_state, tokens_both, back, in_weight, gain_first[None], grad_gain_two, tap_grads, rows,
+        after(sums_state, grads_before), tokens_both, back, in_weight, gain_first[None], gain_one_grad, grad_gain_two, tap_grads, rows,
         4 if staged else 0,
     )
-    grads_before, grad_normed_one = sums[2:]
+    grad_normed_one = sums[2]
+    scaled_one, factor_one, _ = normalize(tokens.astype(F32), gain_first)
+    input_grad = grad_hidden + norm_back(
+        grad_normed_one + from_next.astype(F32), scaled_one, factor_one, gain_first
+    )
+
     if staged:
         send, keep = sums[:2]
         high = z >> 1
         pick_last = jnp.stack([1 - high, high]).astype(jnp.int32)
         late_send, late_keep = merge_grid(after(pick_last, send), late_keep, late_got, 1)
         late_got = swap(late_send, 16, 16, (0, 1, 3))
-        got = swap(after(send, late_send), 1, 1)
-        send, keep = merge(pick_plane, keep, got, height, 2)
+        got = swap(after(send, late_send, from_next), 1, 1)
+        send, keep = merge(pick_plane, keep, got, height + 16, 2)
         got = swap(send, 2, 4)
-        send, keep = merge(pick_line, keep, got, height, 1)
+        send, keep = merge(pick_line, keep, got, height + 16, 1)
         got = swap(send, 4, 2)
-        send, keep = merge(core, keep, got, height, 0)
+        send, keep = merge(core, keep, got, height + 16, 0)
         got = swap(send, 8, 8)
-        from_next = shift_ctx(after(grads_before, send), -1)
         late_chunk = late_keep[0] + late_got[0].astype(F32)
-        send, keep = merge(after(core, late_chunk), keep, got, height, 0)
+        late_chunk = jnp.where(in_up, ungroup(late_chunk).reshape(3, 4, 24, D), late_chunk.reshape(3, 4, 24, D))
+        late_chunk = late_chunk.reshape(-1, D)
+        late_next = shift_flat(late_chunk[:16], -1)
+        send, keep = merge(after(core, late_next, input_grad), keep, got, height + 16, 0)
         got = swap(send, 16, 16, (1, 2))
         first = keep + got.astype(F32)
-        small_grad = first[height:].reshape(-1, 128)
-        late_grad = jnp.where(in_up, ungroup(late_chunk).reshape(3, 4, 24, D), late_chunk.reshape(3, 4, 24, D))
-        chunk_grad = jnp.where(place < count // 4, first[:height], late_grad.reshape(-1, D))
+        quarter = count // 4
+        follow = jnp.where(place < quarter - 1, first[height : height + 16], late_next)
+        follow = jnp.where(place == count - 1, first[height + 16 :], follow)
+        chunk_grad = jnp.where(place < quarter, first[:height], late_chunk)
+        chunk_grad = jnp.concatenate([chunk_grad, follow], 0).reshape(-1, 128)
+        gradient = lax.dynamic_slice_in_dim(chunk_grad, delta * place, owned, 0)
     else:
-        from_next = shift_ctx(grads_before, -1)
         flat_grad = jnp.stack([here_grad.reshape(12, 3, 4, 24, D), away_grad.reshape(12, 3, 4, 24, D)], 1)
         flat_grad = flat_grad.reshape(72, 4, 24, D)
         wide_grad = jnp.concatenate(
@@ -1049,12 +1131,7 @@
         extra = count * delta
         small_grad = jnp.concatenate([used, jnp.zeros((extra - used.shape[0], 128), F32)], 0)
         small_grad = lax.psum(small_grad, AXES)
-    scaled_one, factor_one, _ = normalize(tokens.astype(F32), gain_first)
-    input_grad = grad_hidden + norm_back(
-        grad_normed_one + from_next.astype(F32), scaled_one, factor_one, gain_first
-    )
-
-    gradient = from_aligned(chunk_grad.reshape(-1, 128), small_grad, place, count, delta, owned)
+        gradient = from_aligned(chunk_grad.reshape(-1, 128), small_grad, place, count, delta, owned)
     new_weights, new_one, new_two = adam_update(
         master, first_moment, second_moment, gradient, step_count, place * owned
     )

time: 440 us -> 427 us (0.970)
  the two profiles are of different devices: /device:TPU:13 before, /device:TPU:0 now
where the time goes in v7:
time: 427 us; the launch traced here: 423 us
  Pallas kernels  209 us (49%)
  waiting for transfers between devices  87 us (20%)
  starting transfers between devices  79 us (19%)
  local copies, waits for them, and re-layouts  25 us (6%)
  other arithmetic  19.3 us (5%)
    ppermute x19, waiting for transfers between devices, swap(): return lax.ppermute(block, AXES, route)  87 us
    ppermute x19, starting transfers between devices, swap(): return lax.ppermute(block, AXES, route)  69.5 us
    pallas_call x3, Pallas kernels, att_fwd(): call_in_parts(att_fwd_kernel, [pl.BlockSpec(memory_space=pltpu.SMEM), col...  48.9 us
    pallas_call x3, Pallas kernels, att_bwd(): call_in_parts(att_bwd_kernel, [pl.BlockSpec(memory_space=pltpu.SMEM), own...  48.4 us
    pallas_call x1, Pallas kernels, ffn(): pl.pallas_call(ffn_kernel, grid=(4,), in_specs=[scalars, scalars, act, ac...  48.3 us
    pallas_call x1, Pallas kernels, qkv_bwd(): pl.pallas_call(body, grid=(blocks,), in_specs=[pl.BlockSpec(memory_space=...  19.2 us
    unnamed x51, local copies, waits for them, and re-layouts  14.3 us
    pallas_call x1, Pallas kernels, qkv_fwd(): pl.pallas_call(body, grid=(blocks,), in_specs=[pl.BlockSpec(memory_space=...  13.3 us
  transfers between devices with their start and end apart: 23, of which 13 were waited for; matrix products, arithmetic and copies ran while one was open for 6% of the time, Pallas kernels for 34%

profile of v7, /device:TPU:0, one launch (start us, length us, event | category | flops | bytes accessed | tf_op | source)
XLA Modules:
  0.0 423.1 jit_solution(3079027241568034279)
XLA Ops:
  0.6 3.6 collective-permute-start.2
  5.0 3.3 collective-permute-start
  8.4 2.3 concatenate.22
  13.2 4.6 %collective-permute-start.1 = (bf16[304,768]{1,0:T(8,128)(2,1)S(1)}, bf16[304,768]{1,0:T(8,128)(2,1)S(1)}, u32[]{:S(2)}, u32[]{:S(2)}) collective-permute-start(bf16[304,768]{1,0:T(8,128)(2,1)S(1)} %pad_maximum_fusion.2), channel_id=1, source_target_pairs={{0,16},{1,17},{2,18},{3,19},{4,20},{5,21},{6,22},{7,23},{8,24},{9,... | collective-permute-start | bytes 1400840 | tf_op jit(solution)/shard_map/ppermute | solution.py:851
  19.5 9.9 %collective-permute-done.1 = bf16[304,768]{1,0:T(8,128)(2,1)S(1)} collective-permute-done((bf16[304,768]{1,0:T(8,128)(2,1)S(1)}, bf16[304,768]{1,0:T(8,128)(2,1)S(1)}, u32[]{:S(2)}, u32[]{:S(2)}) %collective-permute-start.1) | collective-permute-done | bytes 466976 | tf_op jit(solution)/shard_map/ppermute | solution.py:851
  29.6 6.1 %collective-permute-start.3 = (bf16[304,768]{1,0:T(8,128)(2,1)S(1)}, bf16[304,768]{1,0:T(8,128)(2,1)S(1)}, u32[]{:S(2)}, u32[]{:S(2)}) collective-permute-start(bf16[304,768]{1,0:T(8,128)(2,1)S(1)} %pad_maximum_fusion.3), channel_id=1, source_target_pairs={{0,8},{1,9},{2,10},{3,11},{4,12},{5,13},{6,14},{7,15},{8,0},{9,1},... | collective-permute-start | bytes 1400840 | tf_op jit(solution)/shard_map/ppermute | solution.py:851
  35.7 11.0 %collective-permute-done.3 = bf16[304,768]{1,0:T(8,128)(2,1)S(1)} collective-permute-done((bf16[304,768]{1,0:T(8,128)(2,1)S(1)}, bf16[304,768]{1,0:T(8,128)(2,1)S(1)}, u32[]{:S(2)}, u32[]{:S(2)}) %collective-permute-start.3) | collective-permute-done | bytes 466976 | tf_op jit(solution)/shard_map/ppermute | solution.py:851
  46.7 4.5 %collective-permute-start.5 = (bf16[304,768]{1,0:T(8,128)(2,1)S(1)}, bf16[304,768]{1,0:T(8,128)(2,1)S(1)}, u32[]{:S(2)}, u32[]{:S(2)}) collective-permute-start(bf16[304,768]{1,0:T(8,128)(2,1)S(1)} %fusion.16.own_ref), channel_id=1, source_target_pairs={{0,2},{1,5},{2,0},{3,7},{4,6},{5,1},{6,4},{7,3},{8,10},{9,13},{10,... | collective-permute-start | bytes 1400840 | tf_op jit(solution)/shard_map/ppermute | solution.py:851
  51.2 6.5 %collective-permute-done.5.got_ref = bf16[304,768]{1,0:T(8,128)(2,1)S(1)} collective-permute-done((bf16[304,768]{1,0:T(8,128)(2,1)S(1)}, bf16[304,768]{1,0:T(8,128)(2,1)S(1)}, u32[]{:S(2)}, u32[]{:S(2)}) %collective-permute-start.5) | collective-permute-done | bytes 466976 | tf_op jit(solution)/shard_map/ppermute | solution.py:851
  57.8 3.0 collective-permute-start.6
  60.9 1.6 collective-permute-start.4
  62.6 16.4 %collective-permute-done.4 = bf16[576,768]{1,0:T(8,128)(2,1)S(1)} collective-permute-done((bf16[576,768]{1,0:T(8,128)(2,1)S(1)}, bf16[576,768]{1,0:T(8,128)(2,1)S(1)}, u32[]{:S(2)}, u32[]{:S(2)}) %collective-permute-start.4) | collective-permute-done | bytes 884768 | tf_op jit(solution)/shard_map/ppermute | solution.py:851
  81.9 3.0 join.5.refs_2_
  84.9 1.7 collective-permute-start.8
  87.2 1.7 collective-permute-done.7.refs_3_
  89.0 13.3 %qkv_fwd.1 = (bf16[2048,2304]{1,0:T(8,128)(2,1)}, f32[16,768]{1,0:T(8,128)}, bf16[2304,768]{1,0:T(8,128)(2,1)}) custom-call(s32[8]{0:T(128)} %stack.213.refs_0_, bf16[2048,768]{1,0:T(8,128)(2,1)} %copy-done.17, bf16[1168,768]{1,0:T(8,128)(2,1)} %join.5.refs_2_, bf16[1168,768]{1,0:T(8,128)(2,1)} %collective-permute-done.7.refs_3_), custom_call_target="tpu_custom_call" | custom-call | flops 7247757312 | bytes 15728640 | tf_op jit(solution)/shard_map/qkv_fwd/pallas_call | solution.py:644
  110.1 16.2 %att_fwd.3 = (bf16[1024,768]{1,0:T(8,128)(2,1)}, f32[1024,768]{1,0:T(8,128)}, bf16[1024,768]{1,0:T(8,128)(2,1)}, bf16[2048,768]{1,0:T(8,128)(2,1)}, bf16[2048,768]{1,0:T(8,128)(2,1)}) custom-call(s32[1]{0:T(128)S(6)} %select_n.155.refs_0_.state_ref, bf16[2048,2304]{1,0:T(8,128)(2,1)} %get-tuple-element.86.refs_1_.refs_2_.refs_3_.refs_4_.refs_7_.refs_8_.refs_9_.refs_10_, ...), custom_call_target="tpu_custom_call" | custom-call | flops 6442450944 | bytes 7864320 | tf_op jit(solution)/shard_map/att_fwd/pallas_call | solution.py:150
  126.4 16.5 %att_fwd.4 = (bf16[1024,768]{1,0:T(8,128)(2,1)}, f32[1024,768]{1,0:T(8,128)}, bf16[1024,768]{1,0:T(8,128)(2,1)}, bf16[2048,768]{1,0:T(8,128)(2,1)}, bf16[2048,768]{1,0:T(8,128)(2,1)}) custom-call(s32[1]{0:T(128)S(6)} %select_n.155.refs_0_.state_ref, ...), custom_call_target="tpu_custom_call", output_to_operand_aliasing={{0}: (8, {}), {1}: (9, {}), {2}: (10, {}), {3}: (11, {}), {... | custom-call | flops 6442450944 | bytes 7864320 | tf_op jit(solution)/shard_map/att_fwd/pallas_call | solution.py:150
  142.9 4.5 %join.7 = bf16[3456,768]{1,0:T(8,128)(2,1)} custom-call(bf16[1728,768]{1,0:T(8,128)(2,1)S(1)} %join.6.own_ref, bf16[1728,768]{1,0:T(8,128)(2,1)} %collective-permute-done.9.got_ref), custom_call_target="tpu_custom_call" | custom-call | flops 1327104 | bytes 10616832 | tf_op jit(solution)/shard_map/join/pallas_call | solution.py:593
  149.4 16.2 %att_fwd.5 = (bf16[1024,768]{1,0:T(8,128)(2,1)}, f32[1024,768]{1,0:T(8,128)}, bf16[1024,768]{1,0:T(8,128)(2,1)}, bf16[2048,768]{1,0:T(8,128)(2,1)}, bf16[2048,768]{1,0:T(8,128)(2,1)}) custom-call(s32[1]{0:T(128)S(6)} %select_n.155.refs_0_.state_ref, ...), custom_call_target="tpu_custom_call", output_to_operand_aliasing={{0}: (8, {}), {1}: (9, {}), {2}: (10, {}), {3}: (11, {}), {... | custom-call | flops 6442450944 | bytes 7864320 | tf_op jit(solution)/shard_map/att_fwd/pallas_call | solution.py:150
  165.6 48.3 %ffn.1 = (bf16[1024,768]{1,0:T(8,128)(2,1)}, f32[1024,768]{1,0:T(8,128)}, bf16[1024,768]{1,0:T(8,128)(2,1)}, f32[1,768]{1,0:T(1,128)}, bf16[36,4,24,768]{3,2,1,0...) custom-call(s32[1]{0:T(128)S(6)} %select_n.155.refs_0_.state_ref, s32[25]{0:T(128)} %stack.208.index_ref, ...), custom_call_target="tpu_custom_call" | custom-call | flops 32614907904 | bytes 40894464 | tf_op jit(solution)/shard_map/ffn/pallas_call | solution.py:794
  214.2 16.0 %att_bwd.3 = (bf16[1024,768]{1,0:T(8,128)(2,1)}, bf16[8,768]{1,0:T(8,128)(2,1)}, bf16[2048,768]{1,0:T(8,128)(2,1)}, bf16[2048,768]{1,0:T(8,128)(2,1)}, f32[16,768]{1,0:T(8,128)}) custom-call(s32[1]{0:T(128)S(6)} %select_n.155.refs_0_.state_ref, bf16[1024,768]{1,0:T(8,128)(2,1)} %get-tuple-element.105.refs_1_, bf16[2048,768]{1,0:T(8,128)(2,1)} %get-tuple-element.106.refs_2_, ...), custom_call_target="tpu_custom_call" | custom-call | flops 16106127360 | bytes 10485760 | tf_op jit(solution)/shard_map/att_bwd/pallas_call | solution.py:307
  230.2 6.3 %merge_grid.4 = (bf16[6,288,768]{2,1,0:T(8,128)(2,1)}, f32[6,288,768]{2,1,0:T(8,128)S(1)}) custom-call(s32[12]{0:T(128)S(1)} %stack.236.index_ref, bf16[12,288,768]{2,1,0:T(8,128)(2,1)S(1)} %bitcast.74, bf16[12,288,768]{2,1,0:T(8,128)(2,1)} %collective-permute-done.11.ga_ref.gb_ref, bf16[12,288,768]{2,1,0:T(8,128)(2,1)S(1)} %bitcast.75, ...), custom_call_target="tpu_custom_call" | custom-call | flops 2654208 | bytes 21233664 | tf_op jit(solution)/shard_map/merge_grid/pallas_call | solution.py:536
  236.5 2.4 copy-done
  238.9 12.4 %collective-permute-start.12 = (bf16[6,288,768]{2,1,0:T(8,128)(2,1)}, bf16[6,288,768]{2,1,0:T(8,128)(2,1)S(1)}, u32[]{:S(2)}, u32[]{:S(2)}) collective-permute-start(bf16[6,288,768]{2,1,0:T(8,128)(2,1)} %get-tuple-element.114), channel_id=1, source_target_pairs={{0,2},{1,5},{2,0},{3,7},{4,6},{5,1},{6,4},{7,3},{8,10},{9,13},{10,... | collective-permute-start | bytes 7962632 | tf_op jit(solution)/shard_map/ppermute | solution.py:851
  251.4 16.2 %att_bwd.4 = (bf16[1024,768]{1,0:T(8,128)(2,1)}, bf16[8,768]{1,0:T(8,128)(2,1)}, bf16[2048,768]{1,0:T(8,128)(2,1)}, bf16[2048,768]{1,0:T(8,128)(2,1)}, f32[16,768]{1,0:T(8,128)}) custom-call(s32[1]{0:T(128)S(6)} %select_n.155.refs_0_.state_ref, ...), custom_call_target="tpu_custom_call", output_to_operand_aliasing={{0}: (14, {}), {1}: (15, {}), {2}: (16, {}), {3}: (17, {}),... | custom-call | flops 16106127360 | bytes 10485760 | tf_op jit(solution)/shard_map/att_bwd/pallas_call | solution.py:307
  267.6 13.9 %collective-permute-done.12.ga_ref.gb_ref = bf16[6,288,768]{2,1,0:T(8,128)(2,1)S(1)} collective-permute-done((bf16[6,288,768]{2,1,0:T(8,128)(2,1)}, bf16[6,288,768]{2,1,0:T(8,128)(2,1)S(1)}, u32[]{:S(2)}, u32[]{:S(2)}) %collective-permute-start.12) | collective-permute-done | bytes 2654240 | tf_op jit(solution)/shard_map/ppermute | solution.py:851
  281.5 2.3 merge_grid.5
  283.9 1.5 copy-done.1
  285.4 16.2 %att_bwd.5 = (bf16[1024,768]{1,0:T(8,128)(2,1)}, bf16[8,768]{1,0:T(8,128)(2,1)}, bf16[2048,768]{1,0:T(8,128)(2,1)}, bf16[2048,768]{1,0:T(8,128)(2,1)}, f32[16,768]{1,0:T(8,128)}) custom-call(s32[1]{0:T(128)S(6)} %select_n.155.refs_0_.state_ref, ...), custom_call_target="tpu_custom_call", output_to_operand_aliasing={{0}: (14, {}), {1}: (15, {}), {2}: (16, {}), {3}: (17, {}),... | custom-call | flops 16106127360 | bytes 10485760 | tf_op jit(solution)/shard_map/att_bwd/pallas_call | solution.py:307
  301.6 7.8 %before_bwd.1 = (bf16[1024,768]{1,0:T(8,128)(2,1)}, f32[1,768]{1,0:T(1,128)}) custom-call(bf16[2048,768]{1,0:T(8,128)(2,1)} %copy-done.17, bf16[8,768]{1,0:T(8,128)(2,1)} %get-tuple-element.134.dt_ref.refs_3_, bf16[2048,768]{1,0:T(8,128)(2,1)} %get-tuple-element.135.dk_ref.refs_4_, bf16[2048,768]{1,0:T(8,128)(2,1)} %get-tuple-element.136.dv_ref.refs_5_, ...), custom_call_target="tpu_custom_call" | custom-call | flops 2415919104 | bytes 9437184 | tf_op jit(solution)/shard_map/before_bwd/pallas_call | solution.py:379
  310.9 2.6 merge_grid.6
  313.5 6.8 %collective-permute-start.15 = (bf16[2,288,768]{2,1,0:T(8,128)(2,1)S(1)}, bf16[2,288,768]{2,1,0:T(8,128)(2,1)S(1)}, u32[]{:S(2)}, u32[]{:S(2)}) collective-permute-start(bf16[2,288,768]{2,1,0:T(8,128)(2,1)S(1)} %get-tuple-element.132), channel_id=1, source_target_pairs={{0,8},{1,9},{2,10},{3,11},{4,12},{5,13},{6,14},{7,15},{8,0},{9,1},... | collective-permute-start | bytes 2654216 | tf_op jit(solution)/shard_map/ppermute | solution.py:851
  320.3 19.2 %qkv_bwd.1 = (bf16[1232,768]{1,0:T(8,128)(2,1)}, f32[1232,768]{1,0:T(8,128)}, f32[1024,768]{1,0:T(8,128)}) custom-call(s32[1]{0:T(128)} %bitcast.24.refs_0_.index_ref, bf16[2048,768]{1,0:T(8,128)(2,1)} %copy-done.17, bf16[1024,768]{1,0:T(8,128)(2,1)} %get-tuple-element.140.refs_2_, bf16[8,768]{1,0:T(8,128)(2,1)} %get-tuple-element.134.dt_ref.refs_3_, ...), custom_call_target="tpu_custom_call" | custom-call | flops 9663676416 | bytes 23592960 | tf_op jit(solution)/shard_map/qkv_bwd/pallas_call | solution.py:474
  343.1 1.9 fusion.6
  345.0 1.5 collective-permute-done.18.got_ref
  346.6 2.1 copy-done.5
  349.6 8.2 %collective-permute-start.19 = (bf16[624,768]{1,0:T(8,128)(2,1)S(1)}, bf16[624,768]{1,0:T(8,128)(2,1)S(1)}, u32[]{:S(2)}, u32[]{:S(2)}) collective-permute-start(bf16[624,768]{1,0:T(8,128)(2,1)S(1)} %get-tuple-element.153), channel_id=1, source_target_pairs={{0,2},{1,5},{2,0},{3,7},{4,6},{5,1},{6,4},{7,3},{8,10},{9,13},{10,... | collective-permute-start | bytes 2875400 | tf_op jit(solution)/shard_map/ppermute | solution.py:851
  357.9 4.5 %collective-permute-start.16 = (bf16[1,288,768]{2,1,0:T(8,128)(2,1)}, bf16[1,288,768]{2,1,0:T(8,128)(2,1)S(1)}, u32[]{:S(2)}, u32[]{:S(2)}) collective-permute-start(bf16[1,288,768]{2,1,0:T(8,128)(2,1)} %get-tuple-element.148), channel_id=1, source_target_pairs={{0,16},{1,17},{2,18},{3,19},{4,20},{5,21},{6,22},{7,23},{8,24},{9,... | collective-permute-start | bytes 1327112 | tf_op jit(solution)/shard_map/ppermute | solution.py:851
  362.4 2.5 fusion.2
  364.9 4.7 %collective-permute-done.19.got_ref = bf16[624,768]{1,0:T(8,128)(2,1)S(1)} collective-permute-done((bf16[624,768]{1,0:T(8,128)(2,1)S(1)}, bf16[624,768]{1,0:T(8,128)(2,1)S(1)}, u32[]{:S(2)}, u32[]{:S(2)}) %collective-permute-start.19) | collective-permute-done | bytes 958496 | tf_op jit(solution)/shard_map/ppermute | solution.py:851
  370.4 5.3 %collective-permute-start.20 = (bf16[320,768]{1,0:T(8,128)(2,1)S(1)}, bf16[320,768]{1,0:T(8,128)(2,1)S(1)}, u32[]{:S(2)}, u32[]{:S(2)}) collective-permute-start(bf16[320,768]{1,0:T(8,128)(2,1)S(1)} %get-tuple-element.155), channel_id=1, source_target_pairs={{0,4},{1,3},{2,6},{3,1},{4,0},{5,7},{6,2},{7,5},{8,12},{9,11},{10,... | collective-permute-start | bytes 1474568 | tf_op jit(solution)/shard_map/ppermute | solution.py:851
  379.4 1.7 bitcast_select_fusion
  382.6 7.2 %collective-permute-start.21 = (bf16[320,768]{1,0:T(8,128)(2,1)S(1)}, bf16[320,768]{1,0:T(8,128)(2,1)S(1)}, u32[]{:S(2)}, u32[]{:S(2)}) collective-permute-start(bf16[320,768]{1,0:T(8,128)(2,1)S(1)} %get-tuple-element.157), channel_id=1, source_target_pairs={{0,8},{1,9},{2,10},{3,11},{4,12},{5,13},{6,14},{7,15},{8,0},{9,1},... | collective-permute-start | bytes 1474568 | tf_op jit(solution)/shard_map/ppermute | solution.py:851
  389.8 6.0 %fusion.5 = f32[1024,768]{1,0:T(8,128)} fusion(f32[1024,768]{1,0:T(8,128)} %get-tuple-element.104, bf16[1024,768]{1,0:T(8,128)(2,1)S(1)} %copy-done.12, f32[1024,768]{1,0:T(8,128)} %get-tuple-element.143, bf16[1024,768]{1,0:T(8,128)(2,1)} %collective-permute-done.14, f32[1024]{0:T(1024)S(1)} %broadcast_multiply_fusion, f32[768]{0:T(1024)S(1)} %get-tuple-element.166, ...), kind=kLoop, calls=%fused_computation.7 | loop fusion | flops 7077888 | bytes 12594176 | tf_op jit(solution)/shard_map/add | solution.py:1087
  395.7 6.4 %collective-permute-done.21.got_ref = bf16[320,768]{1,0:T(8,128)(2,1)S(1)} collective-permute-done((bf16[320,768]{1,0:T(8,128)(2,1)S(1)}, bf16[320,768]{1,0:T(8,128)(2,1)S(1)}, u32[]{:S(2)}, u32[]{:S(2)}) %collective-permute-start.21) | collective-permute-done | bytes 491552 | tf_op jit(solution)/shard_map/ppermute | solution.py:851
  404.3 13.5 %collective-permute-done.22 = bf16[320,768]{1,0:T(8,128)(2,1)S(1)} collective-permute-done((bf16[320,768]{1,0:T(8,128)(2,1)S(1)}, bf16[320,768]{1,0:T(8,128)(2,1)S(1)}, u32[]{:S(2)}, u32[]{:S(2)}) %collective-permute-start.22) | collective-permute-done | bytes 491552 | tf_op jit(solution)/shard_map/ppermute | solution.py:851
  419.1 3.5 fusion.17
  (124 shorter events, 32.5 us)
Async XLA Ops:
  0.6 17.2 %collective-permute-start.2 = (bf16[1024,768]{1,0:T(8,128)(2,1)}, bf16[1024,768]{1,0:T(8,128)(2,1)}, u32[]{:S(2)}, u32[]{:S(2)}) collective-permute-start(bf16[1024,768]{1,0:T(8,128)(2,1)} %x_ref.1), channel_id=1, source_target_pairs={{0,1},{1,2},{2,3},{4,5},{5,6},{6,7},{8,9},{9,10},{10,11},{12,13},{... | collective-permute-start | bytes 4718600 | tf_op jit(solution)/shard_map/ppermute | solution.py:837
  5.0 5.8 %collective-permute-start = (bf16[96,128]{1,0:T(8,128)(2,1)S(1)}, bf16[96,128]{1,0:T(8,128)(2,1)S(1)}, u32[]{:S(2)}, u32[]{:S(2)}) collective-permute-start(bf16[96,128]{1,0:T(8,128)(2,1)S(1)} %slice.35), channel_id=1, source_target_pairs={{0,1},{1,2},{2,3},{3,4},{4,5},{5,6},{6,7},{7,8},{8,9},{9,10},{10,1... | collective-permute-start | bytes 73736 | tf_op jit(solution)/shard_map/ppermute | solution.py:831
  10.7 2.5 copy-start.19
  12.8 6.6 %copy-start.10 = (bf16[1024,768]{1,0:T(8,128)(2,1)S(1)}, bf16[1024,768]{1,0:T(8,128)(2,1)}, u32[]{:S(2)}) copy-start(bf16[1024,768]{1,0:T(8,128)(2,1)} %x_ref.1) | copy-start | bytes 4718596
  13.2 16.2 %copy-start.15 = (bf16[3,4,24,768]{3,2,1,0:T(8,128)(2,1)}, bf16[3,4,24,768]{3,2,1,0:T(8,128)(2,1)S(1)}, u32[]{:S(2)}) copy-start(bf16[3,4,24,768]{3,2,1,0:T(8,128)(2,1)S(1)} %copy.37) | copy-start | bytes 1327108
  13.2 16.2 %collective-permute-start.1 = (bf16[304,768]{1,0:T(8,128)(2,1)S(1)}, bf16[304,768]{1,0:T(8,128)(2,1)S(1)}, u32[]{:S(2)}, u32[]{:S(2)}) collective-permute-start(bf16[304,768]{1,0:T(8,128)(2,1)S(1)} %pad_maximum_fusion.2), channel_id=1, source_target_pairs={{0,16},{1,17},{2,18},{3,19},{4,20},{5,21},{6,22},{7,23},{8,24},{9,... | collective-permute-start | bytes 1400840 | tf_op jit(solution)/shard_map/ppermute | solution.py:851
  19.5 31.7 %copy-start.17 = (bf16[2048,768]{1,0:T(8,128)(2,1)}, bf16[2048,768]{1,0:T(8,128)(2,1)S(1)}, u32[]{:S(2)}) copy-start(bf16[2048,768]{1,0:T(8,128)(2,1)S(1)} %constant_dynamic-update-slice_fusion.refs_1_.x_ref) | copy-start | bytes 9437188
  29.5 31.4 %copy-start.16 = (bf16[3,4,24,768]{3,2,1,0:T(8,128)(2,1)S(1)}, bf16[3,4,24,768]{3,2,1,0:T(8,128)(2,1)}, u32[]{:S(2)}) copy-start(bf16[3,4,24,768]{3,2,1,0:T(8,128)(2,1)} %copy-done.15) | copy-start | bytes 1327108
  29.6 17.0 %collective-permute-start.3 = (bf16[304,768]{1,0:T(8,128)(2,1)S(1)}, bf16[304,768]{1,0:T(8,128)(2,1)S(1)}, u32[]{:S(2)}, u32[]{:S(2)}) collective-permute-start(bf16[304,768]{1,0:T(8,128)(2,1)S(1)} %pad_maximum_fusion.3), channel_id=1, source_target_pairs={{0,8},{1,9},{2,10},{3,11},{4,12},{5,13},{6,14},{7,15},{8,0},{9,1},... | collective-permute-start | bytes 1400840 | tf_op jit(solution)/shard_map/ppermute | solution.py:851
  46.7 11.0 %collective-permute-start.5 = (bf16[304,768]{1,0:T(8,128)(2,1)S(1)}, bf16[304,768]{1,0:T(8,128)(2,1)S(1)}, u32[]{:S(2)}, u32[]{:S(2)}) collective-permute-start(bf16[304,768]{1,0:T(8,128)(2,1)S(1)} %fusion.16.own_ref), channel_id=1, source_target_pairs={{0,2},{1,5},{2,0},{3,7},{4,6},{5,1},{6,4},{7,3},{8,10},{9,13},{10,... | collective-permute-start | bytes 1400840 | tf_op jit(solution)/shard_map/ppermute | solution.py:851
  57.8 24.1 %collective-permute-start.6 = (bf16[592,768]{1,0:T(8,128)(2,1)S(1)}, bf16[592,768]{1,0:T(8,128)(2,1)}, u32[]{:S(2)}, u32[]{:S(2)}) collective-permute-start(bf16[592,768]{1,0:T(8,128)(2,1)S(1)} %join.4.own_ref), channel_id=1, source_target_pairs={{0,4},{1,3},{2,6},{3,1},{4,0},{5,7},{6,2},{7,5},{8,12},{9,11},{10,... | collective-permute-start | bytes 2727944 | tf_op jit(solution)/shard_map/ppermute | solution.py:851
  60.9 18.1 %collective-permute-start.4 = (bf16[576,768]{1,0:T(8,128)(2,1)S(1)}, bf16[576,768]{1,0:T(8,128)(2,1)S(1)}, u32[]{:S(2)}, u32[]{:S(2)}) collective-permute-start(bf16[576,768]{1,0:T(8,128)(2,1)S(1)} %pad_maximum_fusion.1), channel_id=1, source_target_pairs={{0,8},{1,9},{2,10},{3,11},{4,12},{5,13},{6,14},{7,15},{8,0},{9,1},... | collective-permute-start | bytes 2654216 | tf_op jit(solution)/shard_map/ppermute | solution.py:851
  79.0 0.9 copy-start.8
  79.9 1.2 copy-start.9
  81.9 20.3 %copy-start.3 = (bf16[3,288,768]{2,1,0:T(8,128)(2,1)}, bf16[3,288,768]{2,1,0:T(8,128)(2,1)S(1)}, u32[]{:S(2)}) copy-start(bf16[3,288,768]{2,1,0:T(8,128)(2,1)S(1)} %arrange.1) | copy-start | bytes 3981316
  84.9 4.1 collective-permute-start.7
  84.9 17.8 %collective-permute-start.8 = (bf16[864,768]{1,0:T(8,128)(2,1)S(1)}, bf16[864,768]{1,0:T(8,128)(2,1)S(1)}, u32[]{:S(2)}, u32[]{:S(2)}) collective-permute-start(bf16[864,768]{1,0:T(8,128)(2,1)S(1)} %bitcast.76), channel_id=1, source_target_pairs={{0,2},{1,5},{2,0},{3,7},{4,6},{5,1},{6,4},{7,3},{8,10},{9,13},{10,... | collective-permute-start | bytes 3981320 | tf_op jit(solution)/shard_map/ppermute | solution.py:851
  102.7 1.1 copy-start.6
  103.8 1.3 copy-start.4
  105.1 1.3 copy-start.7
  106.4 3.0 copy-start.18
  106.6 36.3 %collective-permute-start.9 = (bf16[1728,768]{1,0:T(8,128)(2,1)S(1)}, bf16[1728,768]{1,0:T(8,128)(2,1)}, u32[]{:S(2)}, u32[]{:S(2)}) collective-permute-start(bf16[1728,768]{1,0:T(8,128)(2,1)S(1)} %join.6.own_ref), channel_id=1, source_target_pairs={{0,4},{1,3},{2,6},{3,1},{4,0},{5,7},{6,2},{7,5},{8,12},{9,11},{10,... | collective-permute-start | bytes 7962632 | tf_op jit(solution)/shard_map/ppermute | solution.py:851
  147.3 18.3 %collective-permute-start.10 = (bf16[3456,768]{1,0:T(8,128)(2,1)}, bf16[3456,768]{1,0:T(8,128)(2,1)}, u32[]{:S(2)}, u32[]{:S(2)}) collective-permute-start(bf16[3456,768]{1,0:T(8,128)(2,1)} %join.7), channel_id=1, source_target_pairs={{0,1},{1,0},{2,3},{3,2},{4,5},{5,4},{6,7},{7,6},{8,9},{9,8},{10,11... | collective-permute-start | bytes 15925256 | tf_op jit(solution)/shard_map/ppermute | solution.py:851
  213.9 16.3 %collective-permute-start.11 = (bf16[12,288,768]{2,1,0:T(8,128)(2,1)}, bf16[12,288,768]{2,1,0:T(8,128)(2,1)}, u32[]{:S(2)}, u32[]{:S(2)}) collective-permute-start(bf16[12,288,768]{2,1,0:T(8,128)(2,1)} %bitcast.82), channel_id=1, source_target_pairs={{0,1},{1,0},{2,3},{3,2},{4,5},{5,4},{6,7},{7,6},{8,9},{9,8},{10,11... | collective-permute-start | bytes 15925256 | tf_op jit(solution)/shard_map/ppermute | solution.py:851
  214.1 16.1 %slice-start.2 = ((s8[5308416]{0:T(1024)(128)(4,1)}), s8[4194304]{0:T(1024)(128)(4,1)S(1)}, s32[]{:S(2)}) async-start(s8[5308416]{0:T(1024)(128)(4,1)} %bitcast.72), calls=%async_computation.2 | async-start | bytes 8388608
  214.1 16.1 %slice-start.3 = ((s8[5308416]{0:T(1024)(128)(4,1)}), s8[1114112]{0:T(1024)(128)(4,1)S(1)}, s32[]{:S(2)}) async-start(s8[5308416]{0:T(1024)(128)(4,1)} %bitcast.72), calls=%async_computation.3 | async-start | bytes 2228224
  236.5 2.4 copy-start
  238.9 42.6 %collective-permute-start.12 = (bf16[6,288,768]{2,1,0:T(8,128)(2,1)}, bf16[6,288,768]{2,1,0:T(8,128)(2,1)S(1)}, u32[]{:S(2)}, u32[]{:S(2)}) collective-permute-start(bf16[6,288,768]{2,1,0:T(8,128)(2,1)} %get-tuple-element.114), channel_id=1, source_target_pairs={{0,2},{1,5},{2,0},{3,7},{4,6},{5,1},{6,4},{7,3},{8,10},{9,13},{10,... | collective-permute-start | bytes 7962632 | tf_op jit(solution)/shard_map/ppermute | solution.py:851
  251.4 30.1 %slice-start = ((s8[5308416]{0:T(1024)(128)(4,1)}), s8[4194304]{0:T(1024)(128)(4,1)S(1)}, s32[]{:S(2)}) async-start(s8[5308416]{0:T(1024)(128)(4,1)} %bitcast.70), calls=%async_computation | async-start | bytes 8388608
  251.4 30.1 %slice-start.1 = ((s8[5308416]{0:T(1024)(128)(4,1)}), s8[1114112]{0:T(1024)(128)(4,1)S(1)}, s32[]{:S(2)}) async-start(s8[5308416]{0:T(1024)(128)(4,1)} %bitcast.70), calls=%async_computation.1 | async-start | bytes 2228224
  283.9 1.5 copy-start.1
  285.4 25.5 %collective-permute-start.13 = (bf16[3,288,768]{2,1,0:T(8,128)(2,1)}, bf16[3,288,768]{2,1,0:T(8,128)(2,1)}, u32[]{:S(2)}, u32[]{:S(2)}) collective-permute-start(bf16[3,288,768]{2,1,0:T(8,128)(2,1)} %get-tuple-element.123), channel_id=1, source_target_pairs={{0,4},{1,3},{2,6},{3,1},{4,0},{5,7},{6,2},{7,5},{8,12},{9,11},{10,... | collective-permute-start | bytes 3981320 | tf_op jit(solution)/shard_map/ppermute | solution.py:851
  301.6 9.3 %copy-start.2 = (f32[3,288,768]{2,1,0:T(8,128)S(1)}, f32[3,288,768]{2,1,0:T(8,128)}, u32[]{:S(2)}) copy-start(f32[3,288,768]{2,1,0:T(8,128)} %copy-done.1) | copy-start | bytes 7962628
  309.4 32.5 %collective-permute-start.14 = (bf16[1024,768]{1,0:T(8,128)(2,1)}, bf16[1024,768]{1,0:T(8,128)(2,1)}, u32[]{:S(2)}, u32[]{:S(2)}) collective-permute-start(bf16[1024,768]{1,0:T(8,128)(2,1)} %get-tuple-element.138), channel_id=1, source_target_pairs={{1,0},{2,1},{3,2},{5,4},{6,5},{7,6},{9,8},{10,9},{11,10},{13,12},{... | collective-permute-start | bytes 4718600 | tf_op jit(solution)/shard_map/ppermute | solution.py:837
  313.5 26.9 %collective-permute-start.15 = (bf16[2,288,768]{2,1,0:T(8,128)(2,1)S(1)}, bf16[2,288,768]{2,1,0:T(8,128)(2,1)S(1)}, u32[]{:S(2)}, u32[]{:S(2)}) collective-permute-start(bf16[2,288,768]{2,1,0:T(8,128)(2,1)S(1)} %get-tuple-element.132), channel_id=1, source_target_pairs={{0,8},{1,9},{2,10},{3,11},{4,12},{5,13},{6,14},{7,15},{8,0},{9,1},... | collective-permute-start | bytes 2654216 | tf_op jit(solution)/shard_map/ppermute | solution.py:851
  339.5 3.3 copy-start.20
  341.9 4.7 %collective-permute-start.18 = (bf16[1232,768]{1,0:T(8,128)(2,1)}, bf16[1232,768]{1,0:T(8,128)(2,1)S(1)}, u32[]{:S(2)}, u32[]{:S(2)}) collective-permute-start(bf16[1232,768]{1,0:T(8,128)(2,1)} %get-tuple-element.151), channel_id=1, source_target_pairs={{0,1},{1,0},{2,3},{3,2},{4,5},{5,4},{6,7},{7,6},{8,9},{9,8},{10,11... | collective-permute-start | bytes 5677064 | tf_op jit(solution)/shard_map/ppermute | solution.py:851
  343.1 19.3 %copy-start.11 = (bf16[1024,768]{1,0:T(8,128)(2,1)S(1)}, bf16[1024,768]{1,0:T(8,128)(2,1)}, u32[]{:S(2)}) copy-start(bf16[1024,768]{1,0:T(8,128)(2,1)} %x_ref.1) | copy-start | bytes 4718596
  346.6 2.1 copy-start.5
  348.7 13.8 %copy-start.13 = (f32[1024,768]{1,0:T(8,128)S(1)}, f32[1024,768]{1,0:T(8,128)}, u32[]{:S(2)}) copy-start(f32[1024,768]{1,0:T(8,128)} %get-tuple-element.143) | copy-start | bytes 9437188
  349.6 20.0 %collective-permute-start.19 = (bf16[624,768]{1,0:T(8,128)(2,1)S(1)}, bf16[624,768]{1,0:T(8,128)(2,1)S(1)}, u32[]{:S(2)}, u32[]{:S(2)}) collective-permute-start(bf16[624,768]{1,0:T(8,128)(2,1)S(1)} %get-tuple-element.153), channel_id=1, source_target_pairs={{0,2},{1,5},{2,0},{3,7},{4,6},{5,1},{6,4},{7,3},{8,10},{9,13},{10,... | collective-permute-start | bytes 2875400 | tf_op jit(solution)/shard_map/ppermute | solution.py:851
  357.9 17.8 %collective-permute-start.16 = (bf16[1,288,768]{2,1,0:T(8,128)(2,1)}, bf16[1,288,768]{2,1,0:T(8,128)(2,1)S(1)}, u32[]{:S(2)}, u32[]{:S(2)}) collective-permute-start(bf16[1,288,768]{2,1,0:T(8,128)(2,1)} %get-tuple-element.148), channel_id=1, source_target_pairs={{0,16},{1,17},{2,18},{3,19},{4,20},{5,21},{6,22},{7,23},{8,24},{9,... | collective-permute-start | bytes 1327112 | tf_op jit(solution)/shard_map/ppermute | solution.py:851
  370.4 12.1 %collective-permute-start.20 = (bf16[320,768]{1,0:T(8,128)(2,1)S(1)}, bf16[320,768]{1,0:T(8,128)(2,1)S(1)}, u32[]{:S(2)}, u32[]{:S(2)}) collective-permute-start(bf16[320,768]{1,0:T(8,128)(2,1)S(1)} %get-tuple-element.155), channel_id=1, source_target_pairs={{0,4},{1,3},{2,6},{3,1},{4,0},{5,7},{6,2},{7,5},{8,12},{9,11},{10,... | collective-permute-start | bytes 1474568 | tf_op jit(solution)/shard_map/ppermute | solution.py:851
  379.4 10.4 %copy-start.12 = (bf16[1024,768]{1,0:T(8,128)(2,1)S(1)}, bf16[1024,768]{1,0:T(8,128)(2,1)}, u32[]{:S(2)}) copy-start(bf16[1024,768]{1,0:T(8,128)(2,1)} %x_ref.1) | copy-start | bytes 4718596
  381.1 14.6 %collective-permute-start.17 = (f32[16,768]{1,0:T(8,128)S(1)}, f32[16,768]{1,0:T(8,128)S(1)}, u32[]{:S(2)}, u32[]{:S(2)}) collective-permute-start(f32[16,768]{1,0:T(8,128)S(1)} %slice.45), channel_id=1, source_target_pairs={{1,0},{2,1},{3,2},{4,3},{5,4},{6,5},{7,6},{8,7},{9,8},{10,9},{11,1... | collective-permute-start | bytes 147464 | tf_op jit(solution)/shard_map/ppermute | solution.py:831
  382.6 19.6 %collective-permute-start.21 = (bf16[320,768]{1,0:T(8,128)(2,1)S(1)}, bf16[320,768]{1,0:T(8,128)(2,1)S(1)}, u32[]{:S(2)}, u32[]{:S(2)}) collective-permute-start(bf16[320,768]{1,0:T(8,128)(2,1)S(1)} %get-tuple-element.157), channel_id=1, source_target_pairs={{0,8},{1,9},{2,10},{3,11},{4,12},{5,13},{6,14},{7,15},{8,0},{9,1},... | collective-permute-start | bytes 1474568 | tf_op jit(solution)/shard_map/ppermute | solution.py:851
  402.3 15.5 %collective-permute-start.22 = (bf16[320,768]{1,0:T(8,128)(2,1)S(1)}, bf16[320,768]{1,0:T(8,128)(2,1)S(1)}, u32[]{:S(2)}, u32[]{:S(2)}) collective-permute-start(bf16[320,768]{1,0:T(8,128)(2,1)S(1)} %get-tuple-element.159), channel_id=1, source_target_pairs={{8,24},{9,25},{10,26},{11,27},{12,28},{13,29},{14,30},{15,31},{16,... | collective-permute-start | bytes 1474568 | tf_op jit(solution)/shard_map/ppermute | solution.py:851
  417.9 1.2 copy-start.14

commit v8 on v7

--- a/solution.py
+++ b/solution.py
@@ -542,8 +542,8 @@
             out_specs=[step, step],
         ),
         out_shape=[
-            jax.ShapeDtypeStruct((taken, height, D), BF),
-            jax.ShapeDtypeStruct((taken, height, D), F32),
+            pltpu.HBM((taken, height, D), BF),
+            pltpu.HBM((taken, height, D), F32),
         ],
         compiler_params=pltpu.CompilerParams(vmem_limit_bytes=32 << 20),
         cost_estimate=cost(taken * height * D * 2, taken * height * D * 16),
@@ -598,6 +598,36 @@
         compiler_params=pltpu.CompilerParams(vmem_limit_bytes=32 << 20),
         cost_estimate=cost(rows * D, rows * D * 8),
         name="join",
+    )(own, got)
+
+
+def join_held(own, got):
+    rows = own.shape[0]
+    cuts = 4
+    size = rows // cuts
+
+    def body(own_ref, got_ref, out_ref, sems):
+        copies = []
+        for k, ref in enumerate((own_ref, got_ref)):
+            for j in range(cuts):
+                source = ref.at[pl.ds(j * size, size)]
+                to = out_ref.at[pl.ds(k * rows + j * size, size)]
+                copies.append(pltpu.make_async_copy(source, to, sems.at[k * cuts + j]))
+        for copy in copies:
+            copy.start()
+        for copy in copies:
+            copy.wait()
+
+    held = pl.BlockSpec(memory_space=pltpu.HBM)
+    return pl.pallas_call(
+        body,
+        in_specs=[held, held],
+        out_specs=held,
+        out_shape=jax.ShapeDtypeStruct((2 * rows, D), BF),
+        scratch_shapes=[pltpu.SemaphoreType.DMA((2 * cuts,))],
+        compiler_params=pltpu.CompilerParams(vmem_limit_bytes=16 << 20),
+        cost_estimate=cost(0, rows * D * 8),
+        name="join_held",
     )(own, got)
 
 
@@ -948,7 +978,6 @@
     state = jnp.where(first_place < 0, 0, jnp.where(first_place >= SEQ_MIN, 2, 1)).astype(jnp.int32)
     state_vec = state[None]
 
-    tokens_before = shift_ctx(tokens, 1)
     chunk = to_aligned(master, place, count, delta).reshape(-1, D)
     if staged:
         group = 3 * place + jnp.arange(3, dtype=jnp.int32)
@@ -960,11 +989,12 @@
     x_bit = (place >> 1) & 1
     y_bit = (place >> 2) & 1
     even = (place & 1) == 0
-    tokens_both = jnp.concatenate([tokens_before, tokens], 0)
     if staged:
         z = place >> 3
         mine = jnp.concatenate([chunk, small.astype(BF).reshape(-1, D)], 0)
+        tokens_before = shift_ctx(after(tokens, mine), 1)
         got = swap(mine, 16, 16)
+        tokens_both = jnp.concatenate([tokens_before, tokens], 0)
         got = after(got, tokens_both)
         rest = jnp.concatenate([chunk, got[:height]], 0)
         none = jnp.zeros((), BF)
@@ -974,13 +1004,7 @@
         across = swap(after(rest, mine), 8, 8)
         mine = join(mine, swap(mine, 2, 4))
         mine = join(mine, swap(mine, 4, 2))
-        codes = [z ^ k for k in (1, 2, 3)]
-        order = [jnp.where(j == 1, 2, jnp.where(j == 2, 1, j)) for j in codes]
-        rest = arrange(
-            jnp.stack(order).astype(jnp.int32), rest.reshape(2, height, D), across.reshape(2, height, D), 3
-        ).reshape(-1, D)
-        across = swap(rest, 2, 4)
-        got = swap(after(mine, rest), 1, 1)
+        got = swap(mine, 1, 1)
         index = []
         late_index = []
         for k in (0, 1):
@@ -995,7 +1019,14 @@
         index = jnp.stack(index).astype(jnp.int32)
         late_index = jnp.stack(late_index + [core[0]]).astype(jnp.int32)
         projected, small, in_weight = qkv_fwd(index, tokens_both, (mine, got), rows, 4)
+        codes = [z ^ k for k in (1, 2, 3)]
+        order = [jnp.where(j == 1, 2, jnp.where(j == 2, 1, j)) for j in codes]
+        rest = arrange(
+            after(jnp.stack(order).astype(jnp.int32), projected), rest.reshape(2, height, D), across.reshape(2, height, D), 3
+        ).reshape(-1, D)
+        across = swap(rest, 2, 4)
     else:
+        tokens_both = jnp.concatenate([shift_ctx(tokens, 1), tokens], 0)
         wide = lax.all_gather(chunk, AXES, axis=0, tiled=True)
         small = lax.psum(small, AXES)[:96].reshape(-1, D)
         in_weight = wide[: 3 * D]
@@ -1007,13 +1038,13 @@
 
     forward = []
     if staged:
-        rest = join(after(rest, projected), across, 0)
+        forward = att_fwd(after(state_vec, rest), projected, taps, forward, 0, rows)
+        rest = join_held(after(rest, forward[0]), across)
         across = swap(rest, 4, 2)
-        forward = att_fwd(after(state_vec, rest), projected, taps, forward, 0, rows)
-        forward = att_fwd(state_vec, projected, taps, forward, 1, rows)
-        rest = join(after(rest, forward[0]), across, 0)
+        forward = att_fwd(after(state_vec, rest), projected, taps, forward, 1, rows)
+        forward = att_fwd(state_vec, projected, taps, forward, 2, rows)
+        rest = join_held(after(rest, forward[0]), across)
         across = swap(rest, 1, 1)
-        forward = att_fwd(after(state_vec, rest), projected, taps, forward, 2, rows)
         own_weights, got_weights = rest.reshape(36, 4, 24, D), across.reshape(36, 4, 24, D)
     else:
         for part in range(PARTS):

time: 427 us -> 429 us (level)
  waiting for transfers between devices: 87 us -> 106 us
  starting transfers between devices: 79 us -> 70.3 us
  local copies, waits for them, and re-layouts: 25 us -> 17.4 us
    ppermute x19, waiting for transfers between devices: 87 us -> 106 us  [swap(): return lax.ppermute(block, AXES, route)]
    ppermute x19, starting transfers between devices: 69.5 us -> 59.7 us  [swap(): return lax.ppermute(block, AXES, route)]
    unnamed x51 -> x45, local copies, waits for them, and re-layouts: 14.3 us -> 4.56 us
    pallas_call x4 -> x2, Pallas kernels: 7.69 us -> 1.4 us  [join(): pl.pallas_call(body, in_specs=[vmem, vmem], out_specs=vmem, out_shape=jax...]
where the time goes in v8:
time: 429 us; the launch traced here: 424 us
  Pallas kernels  210 us (49%)
  waiting for transfers between devices  106 us (25%)
  starting transfers between devices  70.3 us (16%)
  local copies, waits for them, and re-layouts  17.4 us (4%)
  other arithmetic  17.1 us (4%)
    ppermute x19, waiting for transfers between devices, swap(): return lax.ppermute(block, AXES, route)  106 us
    ppermute x19, starting transfers between devices, swap(): return lax.ppermute(block, AXES, route)  59.7 us
    pallas_call x3, Pallas kernels, att_fwd(): call_in_parts(att_fwd_kernel, [pl.BlockSpec(memory_space=pltpu.SMEM), col...  49.2 us
    pallas_call x3, Pallas kernels, att_bwd(): call_in_parts(att_bwd_kernel, [pl.BlockSpec(memory_space=pltpu.SMEM), own...  48.4 us
    pallas_call x1, Pallas kernels, ffn(): pl.pallas_call(ffn_kernel, grid=(4,), in_specs=[scalars, scalars, act, ac...  48.3 us
    pallas_call x1, Pallas kernels, qkv_bwd(): pl.pallas_call(body, grid=(blocks,), in_specs=[pl.BlockSpec(memory_space=...  19.3 us
    pallas_call x4, Pallas kernels, merge_grid(): pl.pallas_call(body, grid_spec=pltpu.PrefetchScalarGridSpec(num_scalar_pr...  16 us
    pallas_call x1, Pallas kernels, qkv_fwd(): pl.pallas_call(body, grid=(blocks,), in_specs=[pl.BlockSpec(memory_space=...  13.3 us
  transfers between devices with their start and end apart: 23, of which 13 were waited for; matrix products, arithmetic and copies ran while one was open for 6% of the time, Pallas kernels for 34%

profile of v8, /device:TPU:0, one launch (start us, length us, event | category | flops | bytes accessed | tf_op | source)
XLA Modules:
  0.0 424.1 jit_solution(3115333393727913397)
XLA Ops:
  1.5 2.3 collective-permute-start
  3.8 2.3 concatenate.22
  6.3 1.5 fusion.8
  8.8 5.7 %collective-permute-start.1 = (bf16[1024,768]{1,0:T(8,128)(2,1)S(1)}, bf16[1024,768]{1,0:T(8,128)(2,1)}, u32[]{:S(2)}, u32[]{:S(2)}) collective-permute-start(bf16[1024,768]{1,0:T(8,128)(2,1)S(1)} %copy-done.3), channel_id=1, source_target_pairs={{0,1},{1,2},{2,3},{4,5},{5,6},{6,7},{8,9},{9,10},{10,11},{12,13},{... | collective-permute-start | bytes 4718600 | tf_op jit(solution)/shard_map/ppermute | solution.py:867
  14.5 2.8 collective-permute-start.2
  17.3 1.5 constant_dynamic-update-slice_fusion.1
  19.0 18.6 %collective-permute-done.2 = bf16[304,768]{1,0:T(8,128)(2,1)S(1)} collective-permute-done((bf16[304,768]{1,0:T(8,128)(2,1)S(1)}, bf16[304,768]{1,0:T(8,128)(2,1)S(1)}, u32[]{:S(2)}, u32[]{:S(2)}) %collective-permute-start.2) | collective-permute-done | bytes 466976 | tf_op jit(solution)/shard_map/ppermute | solution.py:881
  38.4 10.9 %collective-permute-done.3 = bf16[304,768]{1,0:T(8,128)(2,1)S(1)} collective-permute-done((bf16[304,768]{1,0:T(8,128)(2,1)S(1)}, bf16[304,768]{1,0:T(8,128)(2,1)S(1)}, u32[]{:S(2)}, u32[]{:S(2)}) %collective-permute-start.3) | collective-permute-done | bytes 466976 | tf_op jit(solution)/shard_map/ppermute | solution.py:881
  49.7 8.3 %collective-permute-done.4.got_ref = bf16[304,768]{1,0:T(8,128)(2,1)S(1)} collective-permute-done((bf16[304,768]{1,0:T(8,128)(2,1)S(1)}, bf16[304,768]{1,0:T(8,128)(2,1)S(1)}, u32[]{:S(2)}, u32[]{:S(2)}) %collective-permute-start.4) | collective-permute-done | bytes 466976 | tf_op jit(solution)/shard_map/ppermute | solution.py:881
  58.1 1.6 collective-permute-start.5
  59.7 11.8 %collective-permute-done.5.got_ref = bf16[592,768]{1,0:T(8,128)(2,1)S(1)} collective-permute-done((bf16[592,768]{1,0:T(8,128)(2,1)S(1)}, bf16[592,768]{1,0:T(8,128)(2,1)S(1)}, u32[]{:S(2)}, u32[]{:S(2)}) %collective-permute-start.5) | collective-permute-done | bytes 909344 | tf_op jit(solution)/shard_map/ppermute | solution.py:881
  72.9 1.8 collective-permute-start.7
  75.4 1.5 collective-permute-done.6.refs_3_
  76.9 13.3 %qkv_fwd.1 = (bf16[2048,2304]{1,0:T(8,128)(2,1)}, f32[16,768]{1,0:T(8,128)}, bf16[2304,768]{1,0:T(8,128)(2,1)}) custom-call(s32[8]{0:T(128)} %stack.209.refs_0_, bf16[2048,768]{1,0:T(8,128)(2,1)} %copy-done.8, bf16[1168,768]{1,0:T(8,128)(2,1)} %join.3.refs_2_, bf16[1168,768]{1,0:T(8,128)(2,1)} %collective-permute-done.6.refs_3_), custom_call_target="tpu_custom_call" | custom-call | flops 7247757312 | bytes 15728640 | tf_op jit(solution)/shard_map/qkv_fwd/pallas_call | solution.py:674
  90.2 4.8 %collective-permute-done.7 = bf16[576,768]{1,0:T(8,128)(2,1)S(1)} collective-permute-done((bf16[576,768]{1,0:T(8,128)(2,1)S(1)}, bf16[576,768]{1,0:T(8,128)(2,1)S(1)}, u32[]{:S(2)}, u32[]{:S(2)}) %collective-permute-start.7) | collective-permute-done | bytes 884768 | tf_op jit(solution)/shard_map/ppermute | solution.py:881
  99.3 16.2 %att_fwd.3 = (bf16[1024,768]{1,0:T(8,128)(2,1)}, f32[1024,768]{1,0:T(8,128)}, bf16[1024,768]{1,0:T(8,128)(2,1)}, bf16[2048,768]{1,0:T(8,128)(2,1)}, bf16[2048,768]{1,0:T(8,128)(2,1)}) custom-call(s32[1]{0:T(128)S(6)} %select_n.155.refs_0_.state_ref, bf16[2048,2304]{1,0:T(8,128)(2,1)} %get-tuple-element.86.refs_1_.refs_2_.refs_3_.refs_4_.refs_7_.refs_8_.refs_9_.refs_10_, ...), custom_call_target="tpu_custom_call" | custom-call | flops 6442450944 | bytes 7864320 | tf_op jit(solution)/shard_map/att_fwd/pallas_call | solution.py:150
  116.5 1.6 collective-permute-start.9
  118.1 16.4 %att_fwd.4 = (bf16[1024,768]{1,0:T(8,128)(2,1)}, f32[1024,768]{1,0:T(8,128)}, bf16[1024,768]{1,0:T(8,128)(2,1)}, bf16[2048,768]{1,0:T(8,128)(2,1)}, bf16[2048,768]{1,0:T(8,128)(2,1)}) custom-call(s32[1]{0:T(128)S(6)} %select_n.155.refs_0_.state_ref, ...), custom_call_target="tpu_custom_call", output_to_operand_aliasing={{0}: (8, {}), {1}: (9, {}), {2}: (10, {}), {3}: (11, {}), {... | custom-call | flops 6442450944 | bytes 7864320 | tf_op jit(solution)/shard_map/att_fwd/pallas_call | solution.py:150
  134.5 16.5 %att_fwd.5 = (bf16[1024,768]{1,0:T(8,128)(2,1)}, f32[1024,768]{1,0:T(8,128)}, bf16[1024,768]{1,0:T(8,128)(2,1)}, bf16[2048,768]{1,0:T(8,128)(2,1)}, bf16[2048,768]{1,0:T(8,128)(2,1)}) custom-call(s32[1]{0:T(128)S(6)} %select_n.155.refs_0_.state_ref, ...), custom_call_target="tpu_custom_call", output_to_operand_aliasing={{0}: (8, {}), {1}: (9, {}), {2}: (10, {}), {3}: (11, {}), {... | custom-call | flops 6442450944 | bytes 7864320 | tf_op jit(solution)/shard_map/att_fwd/pallas_call | solution.py:150
  151.1 2.4 join_held.3
  154.8 7.8 %collective-permute-done.10 = bf16[3456,768]{1,0:T(8,128)(2,1)} collective-permute-done((bf16[3456,768]{1,0:T(8,128)(2,1)}, bf16[3456,768]{1,0:T(8,128)(2,1)}, u32[]{:S(2)}, u32[]{:S(2)}) %collective-permute-start.10) | collective-permute-done | bytes 5308448 | tf_op jit(solution)/shard_map/ppermute | solution.py:881
  162.6 48.3 %ffn.1 = (bf16[1024,768]{1,0:T(8,128)(2,1)}, f32[1024,768]{1,0:T(8,128)}, bf16[1024,768]{1,0:T(8,128)(2,1)}, f32[1,768]{1,0:T(1,128)}, bf16[36,4,24,768]{3,2,1,0...) custom-call(s32[1]{0:T(128)S(6)} %select_n.155.refs_0_.state_ref, s32[25]{0:T(128)} %stack.208.index_ref, ...), custom_call_target="tpu_custom_call" | custom-call | flops 32614907904 | bytes 40894464 | tf_op jit(solution)/shard_map/ffn/pallas_call | solution.py:824
  211.2 16.0 %att_bwd.3 = (bf16[1024,768]{1,0:T(8,128)(2,1)}, bf16[8,768]{1,0:T(8,128)(2,1)}, bf16[2048,768]{1,0:T(8,128)(2,1)}, bf16[2048,768]{1,0:T(8,128)(2,1)}, f32[16,768]{1,0:T(8,128)}) custom-call(s32[1]{0:T(128)S(6)} %select_n.155.refs_0_.state_ref, bf16[1024,768]{1,0:T(8,128)(2,1)} %get-tuple-element.107.refs_1_, bf16[2048,768]{1,0:T(8,128)(2,1)} %get-tuple-element.108.refs_2_, ...), custom_call_target="tpu_custom_call" | custom-call | flops 16106127360 | bytes 10485760 | tf_op jit(solution)/shard_map/att_bwd/pallas_call | solution.py:307
  227.3 7.5 %merge_grid.4 = (bf16[6,288,768]{2,1,0:T(8,128)(2,1)}, f32[6,288,768]{2,1,0:T(8,128)}) custom-call(s32[12]{0:T(128)S(1)} %stack.236.index_ref, bf16[12,288,768]{2,1,0:T(8,128)(2,1)S(1)} %bitcast.74, bf16[12,288,768]{2,1,0:T(8,128)(2,1)} %collective-permute-done.11.ga_ref.gb_ref, bf16[12,288,768]{2,1,0:T(8,128)(2,1)S(1)} %bitcast.75, ...), custom_call_target="tpu_custom_call" | custom-call | flops 2654208 | bytes 21233664 | tf_op jit(solution)/shard_map/merge_grid/pallas_call | solution.py:536
  234.8 12.8 %collective-permute-start.12 = (bf16[6,288,768]{2,1,0:T(8,128)(2,1)}, bf16[6,288,768]{2,1,0:T(8,128)(2,1)S(1)}, u32[]{:S(2)}, u32[]{:S(2)}) collective-permute-start(bf16[6,288,768]{2,1,0:T(8,128)(2,1)} %get-tuple-element.116), channel_id=1, source_target_pairs={{0,2},{1,5},{2,0},{3,7},{4,6},{5,1},{6,4},{7,3},{8,10},{9,13},{10,... | collective-permute-start | bytes 7962632 | tf_op jit(solution)/shard_map/ppermute | solution.py:881
  247.7 16.3 %att_bwd.4 = (bf16[1024,768]{1,0:T(8,128)(2,1)}, bf16[8,768]{1,0:T(8,128)(2,1)}, bf16[2048,768]{1,0:T(8,128)(2,1)}, bf16[2048,768]{1,0:T(8,128)(2,1)}, f32[16,768]{1,0:T(8,128)}) custom-call(s32[1]{0:T(128)S(6)} %select_n.155.refs_0_.state_ref, ...), custom_call_target="tpu_custom_call", output_to_operand_aliasing={{0}: (14, {}), {1}: (15, {}), {2}: (16, {}), {3}: (17, {}),... | custom-call | flops 16106127360 | bytes 10485760 | tf_op jit(solution)/shard_map/att_bwd/pallas_call | solution.py:307
  263.9 13.8 %collective-permute-done.12.ga_ref.gb_ref = bf16[6,288,768]{2,1,0:T(8,128)(2,1)S(1)} collective-permute-done((bf16[6,288,768]{2,1,0:T(8,128)(2,1)}, bf16[6,288,768]{2,1,0:T(8,128)(2,1)S(1)}, u32[]{:S(2)}, u32[]{:S(2)}) %collective-permute-start.12) | collective-permute-done | bytes 2654240 | tf_op jit(solution)/shard_map/ppermute | solution.py:881
  277.8 2.9 merge_grid.5
  280.7 16.1 %att_bwd.5 = (bf16[1024,768]{1,0:T(8,128)(2,1)}, bf16[8,768]{1,0:T(8,128)(2,1)}, bf16[2048,768]{1,0:T(8,128)(2,1)}, bf16[2048,768]{1,0:T(8,128)(2,1)}, f32[16,768]{1,0:T(8,128)}) custom-call(s32[1]{0:T(128)S(6)} %select_n.155.refs_0_.state_ref, ...), custom_call_target="tpu_custom_call", output_to_operand_aliasing={{0}: (14, {}), {1}: (15, {}), {2}: (16, {}), {3}: (17, {}),... | custom-call | flops 16106127360 | bytes 10485760 | tf_op jit(solution)/shard_map/att_bwd/pallas_call | solution.py:307
  296.8 7.9 %before_bwd.1 = (bf16[1024,768]{1,0:T(8,128)(2,1)}, f32[1,768]{1,0:T(1,128)}) custom-call(bf16[2048,768]{1,0:T(8,128)(2,1)} %copy-done.8, bf16[8,768]{1,0:T(8,128)(2,1)} %get-tuple-element.136.dt_ref.refs_3_, bf16[2048,768]{1,0:T(8,128)(2,1)} %get-tuple-element.137.dk_ref.refs_4_, bf16[2048,768]{1,0:T(8,128)(2,1)} %get-tuple-element.138.dv_ref.refs_5_, ...), custom_call_target="tpu_custom_call" | custom-call | flops 2415919104 | bytes 9437184 | tf_op jit(solution)/shard_map/before_bwd/pallas_call | solution.py:379
  306.1 3.9 merge_grid.6
  310.0 19.3 %qkv_bwd.1 = (bf16[1232,768]{1,0:T(8,128)(2,1)}, f32[1232,768]{1,0:T(8,128)}, f32[1024,768]{1,0:T(8,128)}) custom-call(s32[1]{0:T(128)} %bitcast.24.refs_0_.index_ref, bf16[2048,768]{1,0:T(8,128)(2,1)} %copy-done.8, bf16[1024,768]{1,0:T(8,128)(2,1)} %get-tuple-element.142.refs_2_, bf16[8,768]{1,0:T(8,128)(2,1)} %get-tuple-element.136.dt_ref.refs_3_, ...), custom_call_target="tpu_custom_call" | custom-call | flops 9663676416 | bytes 23592960 | tf_op jit(solution)/shard_map/qkv_bwd/pallas_call | solution.py:474
  329.4 1.7 merge_grid.7
  331.1 18.2 %collective-permute-start.18 = (bf16[1232,768]{1,0:T(8,128)(2,1)}, bf16[1232,768]{1,0:T(8,128)(2,1)S(1)}, u32[]{:S(2)}, u32[]{:S(2)}) collective-permute-start(bf16[1232,768]{1,0:T(8,128)(2,1)} %get-tuple-element.153), channel_id=1, source_target_pairs={{0,1},{1,0},{2,3},{3,2},{4,5},{5,4},{6,7},{7,6},{8,9},{9,8},{10,11... | collective-permute-start | bytes 5677064 | tf_op jit(solution)/shard_map/ppermute | solution.py:881
  349.9 3.1 collective-permute-done.18.got_ref
  353.0 2.1 copy-done.2
  355.9 2.3 collective-permute-start.19
  358.3 5.2 %collective-permute-start.16 = (bf16[1,288,768]{2,1,0:T(8,128)(2,1)S(1)}, bf16[1,288,768]{2,1,0:T(8,128)(2,1)S(1)}, u32[]{:S(2)}, u32[]{:S(2)}) collective-permute-start(bf16[1,288,768]{2,1,0:T(8,128)(2,1)S(1)} %copy-done.17), channel_id=1, source_target_pairs={{0,16},{1,17},{2,18},{3,19},{4,20},{5,21},{6,22},{7,23},{8,24},{9,... | collective-permute-start | bytes 1327112 | tf_op jit(solution)/shard_map/ppermute | solution.py:881
  363.5 2.5 fusion.2
  366.1 4.0 collective-permute-done.19.got_ref
  372.2 2.4 copy.38
  374.6 2.4 reshape.123
  377.0 1.7 bitcast_select_fusion
  380.2 10.4 %collective-permute-start.21 = (bf16[320,768]{1,0:T(8,128)(2,1)S(1)}, bf16[320,768]{1,0:T(8,128)(2,1)S(1)}, u32[]{:S(2)}, u32[]{:S(2)}) collective-permute-start(bf16[320,768]{1,0:T(8,128)(2,1)S(1)} %get-tuple-element.159), channel_id=1, source_target_pairs={{0,8},{1,9},{2,10},{3,11},{4,12},{5,13},{6,14},{7,15},{8,0},{9,1},... | collective-permute-start | bytes 1474568 | tf_op jit(solution)/shard_map/ppermute | solution.py:881
  390.6 5.1 %fusion.5 = f32[1024,768]{1,0:T(8,128)} fusion(f32[1024,768]{1,0:T(8,128)} %get-tuple-element.106, bf16[1024,768]{1,0:T(8,128)(2,1)S(1)} %copy-done.4, f32[1024,768]{1,0:T(8,128)S(1)} %copy-done.6, bf16[1024,768]{1,0:T(8,128)(2,1)} %collective-permute-done.14, f32[1024]{0:T(1024)S(1)} %broadcast_multiply_fusion, f32[768]{0:T(1024)S(1)} %get-tuple-element.168, ...), kind=kLoop, calls=%fused_computation.7 | loop fusion | flops 7077888 | bytes 12594176 | tf_op jit(solution)/shard_map/add | solution.py:1118
  395.7 7.3 %collective-permute-done.21.got_ref = bf16[320,768]{1,0:T(8,128)(2,1)S(1)} collective-permute-done((bf16[320,768]{1,0:T(8,128)(2,1)S(1)}, bf16[320,768]{1,0:T(8,128)(2,1)S(1)}, u32[]{:S(2)}, u32[]{:S(2)}) %collective-permute-start.21) | collective-permute-done | bytes 491552 | tf_op jit(solution)/shard_map/ppermute | solution.py:881
  405.3 13.5 %collective-permute-done.22 = bf16[320,768]{1,0:T(8,128)(2,1)S(1)} collective-permute-done((bf16[320,768]{1,0:T(8,128)(2,1)S(1)}, bf16[320,768]{1,0:T(8,128)(2,1)S(1)}, u32[]{:S(2)}, u32[]{:S(2)}) %collective-permute-start.22) | collective-permute-done | bytes 491552 | tf_op jit(solution)/shard_map/ppermute | solution.py:881
  420.0 3.5 fusion.17
  (118 shorter events, 20.4 us)
Async XLA Ops:
  1.5 4.8 %collective-permute-start = (bf16[96,128]{1,0:T(8,128)(2,1)S(1)}, bf16[96,128]{1,0:T(8,128)(2,1)S(1)}, u32[]{:S(2)}, u32[]{:S(2)}) collective-permute-start(bf16[96,128]{1,0:T(8,128)(2,1)S(1)} %slice.35), channel_id=1, source_target_pairs={{0,1},{1,2},{2,3},{3,4},{4,5},{5,6},{6,7},{7,8},{8,9},{9,10},{10,1... | collective-permute-start | bytes 73736 | tf_op jit(solution)/shard_map/ppermute | solution.py:861
  6.2 2.6 copy-start.15
  6.3 2.6 copy-start.3
  8.8 8.5 %collective-permute-start.1 = (bf16[1024,768]{1,0:T(8,128)(2,1)S(1)}, bf16[1024,768]{1,0:T(8,128)(2,1)}, u32[]{:S(2)}, u32[]{:S(2)}) collective-permute-start(bf16[1024,768]{1,0:T(8,128)(2,1)S(1)} %copy-done.3), channel_id=1, source_target_pairs={{0,1},{1,2},{2,3},{4,5},{5,6},{6,7},{8,9},{9,10},{10,11},{12,13},{... | collective-permute-start | bytes 4718600 | tf_op jit(solution)/shard_map/ppermute | solution.py:867
  14.5 23.0 %collective-permute-start.2 = (bf16[304,768]{1,0:T(8,128)(2,1)S(1)}, bf16[304,768]{1,0:T(8,128)(2,1)S(1)}, u32[]{:S(2)}, u32[]{:S(2)}) collective-permute-start(bf16[304,768]{1,0:T(8,128)(2,1)S(1)} %pad_maximum_fusion.2), channel_id=1, source_target_pairs={{0,16},{1,17},{2,18},{3,19},{4,20},{5,21},{6,22},{7,23},{8,24},{9,... | collective-permute-start | bytes 1400840 | tf_op jit(solution)/shard_map/ppermute | solution.py:881
  19.0 30.8 %copy-start.8 = (bf16[2048,768]{1,0:T(8,128)(2,1)}, bf16[2048,768]{1,0:T(8,128)(2,1)S(1)}, u32[]{:S(2)}) copy-start(bf16[2048,768]{1,0:T(8,128)(2,1)S(1)} %constant_dynamic-update-slice_fusion.refs_1_.x_ref) | copy-start | bytes 9437188
  37.7 11.6 %collective-permute-start.3 = (bf16[304,768]{1,0:T(8,128)(2,1)S(1)}, bf16[304,768]{1,0:T(8,128)(2,1)S(1)}, u32[]{:S(2)}, u32[]{:S(2)}) collective-permute-start(bf16[304,768]{1,0:T(8,128)(2,1)S(1)} %pad_maximum_fusion.3), channel_id=1, source_target_pairs={{0,8},{1,9},{2,10},{3,11},{4,12},{5,13},{6,14},{7,15},{8,0},{9,1},... | collective-permute-start | bytes 1400840 | tf_op jit(solution)/shard_map/ppermute | solution.py:881
  49.4 8.6 %collective-permute-start.4 = (bf16[304,768]{1,0:T(8,128)(2,1)S(1)}, bf16[304,768]{1,0:T(8,128)(2,1)S(1)}, u32[]{:S(2)}, u32[]{:S(2)}) collective-permute-start(bf16[304,768]{1,0:T(8,128)(2,1)S(1)} %fusion.16.own_ref), channel_id=1, source_target_pairs={{0,2},{1,5},{2,0},{3,7},{4,6},{5,1},{6,4},{7,3},{8,10},{9,13},{10,... | collective-permute-start | bytes 1400840 | tf_op jit(solution)/shard_map/ppermute | solution.py:881
  58.1 13.4 %collective-permute-start.5 = (bf16[592,768]{1,0:T(8,128)(2,1)S(1)}, bf16[592,768]{1,0:T(8,128)(2,1)S(1)}, u32[]{:S(2)}, u32[]{:S(2)}) collective-permute-start(bf16[592,768]{1,0:T(8,128)(2,1)S(1)} %join.2.own_ref), channel_id=1, source_target_pairs={{0,4},{1,3},{2,6},{3,1},{4,0},{5,7},{6,2},{7,5},{8,12},{9,11},{10,... | collective-permute-start | bytes 2727944 | tf_op jit(solution)/shard_map/ppermute | solution.py:881
  72.8 4.1 collective-permute-start.6
  72.9 22.1 %collective-permute-start.7 = (bf16[576,768]{1,0:T(8,128)(2,1)S(1)}, bf16[576,768]{1,0:T(8,128)(2,1)S(1)}, u32[]{:S(2)}, u32[]{:S(2)}) collective-permute-start(bf16[576,768]{1,0:T(8,128)(2,1)S(1)} %pad_maximum_fusion.1), channel_id=1, source_target_pairs={{0,8},{1,9},{2,10},{3,11},{4,12},{5,13},{6,14},{7,15},{8,0},{9,1},... | collective-permute-start | bytes 2654216 | tf_op jit(solution)/shard_map/ppermute | solution.py:881
  90.2 8.4 %copy-start.12 = (f32[16,768]{1,0:T(8,128)S(1)}, f32[16,768]{1,0:T(8,128)}, u32[]{:S(2)}) copy-start(f32[16,768]{1,0:T(8,128)} %get-tuple-element.87) | copy-start | bytes 147460
  95.9 19.7 %collective-permute-start.8 = (bf16[864,768]{1,0:T(8,128)(2,1)S(1)}, bf16[864,768]{1,0:T(8,128)(2,1)S(1)}, u32[]{:S(2)}, u32[]{:S(2)}) collective-permute-start(bf16[864,768]{1,0:T(8,128)(2,1)S(1)} %bitcast.76), channel_id=1, source_target_pairs={{0,2},{1,5},{2,0},{3,7},{4,6},{5,1},{6,4},{7,3},{8,10},{9,13},{10,... | collective-permute-start | bytes 3981320 | tf_op jit(solution)/shard_map/ppermute | solution.py:881
  116.5 34.5 %collective-permute-start.9 = (bf16[1728,768]{1,0:T(8,128)(2,1)S(1)}, bf16[1728,768]{1,0:T(8,128)(2,1)S(1)}, u32[]{:S(2)}, u32[]{:S(2)}) collective-permute-start(bf16[1728,768]{1,0:T(8,128)(2,1)S(1)} %join_held.2.own_ref), channel_id=1, source_target_pairs={{0,4},{1,3},{2,6},{3,1},{4,0},{5,7},{6,2},{7,5},{8,12},{9,11},{10,... | collective-permute-start | bytes 7962632 | tf_op jit(solution)/shard_map/ppermute | solution.py:881
  153.5 9.2 %collective-permute-start.10 = (bf16[3456,768]{1,0:T(8,128)(2,1)}, bf16[3456,768]{1,0:T(8,128)(2,1)}, u32[]{:S(2)}, u32[]{:S(2)}) collective-permute-start(bf16[3456,768]{1,0:T(8,128)(2,1)} %join_held.3), channel_id=1, source_target_pairs={{0,1},{1,0},{2,3},{3,2},{4,5},{5,4},{6,7},{7,6},{8,9},{9,8},{10,11... | collective-permute-start | bytes 15925256 | tf_op jit(solution)/shard_map/ppermute | solution.py:881
  210.9 16.3 %collective-permute-start.11 = (bf16[12,288,768]{2,1,0:T(8,128)(2,1)}, bf16[12,288,768]{2,1,0:T(8,128)(2,1)}, u32[]{:S(2)}, u32[]{:S(2)}) collective-permute-start(bf16[12,288,768]{2,1,0:T(8,128)(2,1)} %bitcast.82), channel_id=1, source_target_pairs={{0,1},{1,0},{2,3},{3,2},{4,5},{5,4},{6,7},{7,6},{8,9},{9,8},{10,11... | collective-permute-start | bytes 15925256 | tf_op jit(solution)/shard_map/ppermute | solution.py:881
  211.2 16.1 %slice-start.2 = ((s8[5308416]{0:T(1024)(128)(4,1)}), s8[4194304]{0:T(1024)(128)(4,1)S(1)}, s32[]{:S(2)}) async-start(s8[5308416]{0:T(1024)(128)(4,1)} %bitcast.72), calls=%async_computation.2 | async-start | bytes 8388608
  211.2 16.1 %slice-start.3 = ((s8[5308416]{0:T(1024)(128)(4,1)}), s8[1114112]{0:T(1024)(128)(4,1)S(1)}, s32[]{:S(2)}) async-start(s8[5308416]{0:T(1024)(128)(4,1)} %bitcast.72), calls=%async_computation.3 | async-start | bytes 2228224
  234.8 43.0 %collective-permute-start.12 = (bf16[6,288,768]{2,1,0:T(8,128)(2,1)}, bf16[6,288,768]{2,1,0:T(8,128)(2,1)S(1)}, u32[]{:S(2)}, u32[]{:S(2)}) collective-permute-start(bf16[6,288,768]{2,1,0:T(8,128)(2,1)} %get-tuple-element.116), channel_id=1, source_target_pairs={{0,2},{1,5},{2,0},{3,7},{4,6},{5,1},{6,4},{7,3},{8,10},{9,13},{10,... | collective-permute-start | bytes 7962632 | tf_op jit(solution)/shard_map/ppermute | solution.py:881
  247.6 30.1 %slice-start = ((s8[5308416]{0:T(1024)(128)(4,1)}), s8[4194304]{0:T(1024)(128)(4,1)S(1)}, s32[]{:S(2)}) async-start(s8[5308416]{0:T(1024)(128)(4,1)} %bitcast.70), calls=%async_computation | async-start | bytes 8388608
  247.6 30.1 %slice-start.1 = ((s8[5308416]{0:T(1024)(128)(4,1)}), s8[1114112]{0:T(1024)(128)(4,1)S(1)}, s32[]{:S(2)}) async-start(s8[5308416]{0:T(1024)(128)(4,1)} %bitcast.70), calls=%async_computation.1 | async-start | bytes 2228224
  280.7 25.4 %collective-permute-start.13 = (bf16[3,288,768]{2,1,0:T(8,128)(2,1)}, bf16[3,288,768]{2,1,0:T(8,128)(2,1)}, u32[]{:S(2)}, u32[]{:S(2)}) collective-permute-start(bf16[3,288,768]{2,1,0:T(8,128)(2,1)} %get-tuple-element.125), channel_id=1, source_target_pairs={{0,4},{1,3},{2,6},{3,1},{4,0},{5,7},{6,2},{7,5},{8,12},{9,11},{10,... | collective-permute-start | bytes 3981320 | tf_op jit(solution)/shard_map/ppermute | solution.py:881
  296.8 9.3 %copy-start = (f32[3,288,768]{2,1,0:T(8,128)S(1)}, f32[3,288,768]{2,1,0:T(8,128)}, u32[]{:S(2)}) copy-start(f32[3,288,768]{2,1,0:T(8,128)} %get-tuple-element.133.ka_ref.kb_ref) | copy-start | bytes 7962628
  304.7 26.4 %collective-permute-start.14 = (bf16[1024,768]{1,0:T(8,128)(2,1)}, bf16[1024,768]{1,0:T(8,128)(2,1)}, u32[]{:S(2)}, u32[]{:S(2)}) collective-permute-start(bf16[1024,768]{1,0:T(8,128)(2,1)} %get-tuple-element.140), channel_id=1, source_target_pairs={{1,0},{2,1},{3,2},{5,4},{6,5},{7,6},{9,8},{10,9},{11,10},{13,12},{... | collective-permute-start | bytes 4718600 | tf_op jit(solution)/shard_map/ppermute | solution.py:867
  310.0 19.3 %collective-permute-start.15 = (bf16[2,288,768]{2,1,0:T(8,128)(2,1)}, bf16[2,288,768]{2,1,0:T(8,128)(2,1)S(1)}, u32[]{:S(2)}, u32[]{:S(2)}) collective-permute-start(bf16[2,288,768]{2,1,0:T(8,128)(2,1)} %get-tuple-element.134), channel_id=1, source_target_pairs={{0,8},{1,9},{2,10},{3,11},{4,12},{5,13},{6,14},{7,15},{8,0},{9,1},... | collective-permute-start | bytes 2654216 | tf_op jit(solution)/shard_map/ppermute | solution.py:881
  310.0 19.3 %copy-start.1 = (f32[2,288,768]{2,1,0:T(8,128)S(1)}, f32[2,288,768]{2,1,0:T(8,128)}, u32[]{:S(2)}) copy-start(f32[2,288,768]{2,1,0:T(8,128)} %get-tuple-element.148.ka_ref.kb_ref) | copy-start | bytes 5308420
  329.3 19.9 %copy-start.16 = (pred[3]{0:T(512)(128)(4,1)S(1)}, pred[3]{0:T(512)(128)(4,1)}, u32[]{:S(2)}) copy-start(pred[3]{0:T(512)(128)(4,1)} %copy-done.15) | copy-start | bytes 13
  329.3 20.2 %copy-start.4 = (bf16[1024,768]{1,0:T(8,128)(2,1)S(1)}, bf16[1024,768]{1,0:T(8,128)(2,1)}, u32[]{:S(2)}) copy-start(bf16[1024,768]{1,0:T(8,128)(2,1)} %x_ref.1) | copy-start | bytes 4718596
  331.1 21.9 %collective-permute-start.18 = (bf16[1232,768]{1,0:T(8,128)(2,1)}, bf16[1232,768]{1,0:T(8,128)(2,1)S(1)}, u32[]{:S(2)}, u32[]{:S(2)}) collective-permute-start(bf16[1232,768]{1,0:T(8,128)(2,1)} %get-tuple-element.153), channel_id=1, source_target_pairs={{0,1},{1,0},{2,3},{3,2},{4,5},{5,4},{6,7},{7,6},{8,9},{9,8},{10,11... | collective-permute-start | bytes 5677064 | tf_op jit(solution)/shard_map/ppermute | solution.py:881
  349.5 8.8 %copy-start.17 = (bf16[1,288,768]{2,1,0:T(8,128)(2,1)S(1)}, bf16[1,288,768]{2,1,0:T(8,128)(2,1)}, u32[]{:S(2)}) copy-start(bf16[1,288,768]{2,1,0:T(8,128)(2,1)} %get-tuple-element.150) | copy-start | bytes 1327108
  352.9 2.1 copy-start.2
  355.0 8.5 %copy-start.5 = (f32[1024,768]{1,0:T(8,128)S(1)}, f32[1024,768]{1,0:T(8,128)}, u32[]{:S(2)}) copy-start(f32[1024,768]{1,0:T(8,128)} %get-tuple-element.145) | copy-start | bytes 9437188
  355.9 14.1 %collective-permute-start.19 = (bf16[624,768]{1,0:T(8,128)(2,1)S(1)}, bf16[624,768]{1,0:T(8,128)(2,1)S(1)}, u32[]{:S(2)}, u32[]{:S(2)}) collective-permute-start(bf16[624,768]{1,0:T(8,128)(2,1)S(1)} %get-tuple-element.155), channel_id=1, source_target_pairs={{0,2},{1,5},{2,0},{3,7},{4,6},{5,1},{6,4},{7,3},{8,10},{9,13},{10,... | collective-permute-start | bytes 2875400 | tf_op jit(solution)/shard_map/ppermute | solution.py:881
  358.3 12.9 %collective-permute-start.16 = (bf16[1,288,768]{2,1,0:T(8,128)(2,1)S(1)}, bf16[1,288,768]{2,1,0:T(8,128)(2,1)S(1)}, u32[]{:S(2)}, u32[]{:S(2)}) collective-permute-start(bf16[1,288,768]{2,1,0:T(8,128)(2,1)S(1)} %copy-done.17), channel_id=1, source_target_pairs={{0,16},{1,17},{2,18},{3,19},{4,20},{5,21},{6,22},{7,23},{8,24},{9,... | collective-permute-start | bytes 1327112 | tf_op jit(solution)/shard_map/ppermute | solution.py:881
  363.5 7.7 %copy-start.11 = (f32[1,288,768]{2,1,0:T(8,128)S(1)}, f32[1,288,768]{2,1,0:T(8,128)}, u32[]{:S(2)}) copy-start(f32[1,288,768]{2,1,0:T(8,128)} %get-tuple-element.149) | copy-start | bytes 2654212
  370.9 9.2 %collective-permute-start.20 = (bf16[320,768]{1,0:T(8,128)(2,1)S(1)}, bf16[320,768]{1,0:T(8,128)(2,1)S(1)}, u32[]{:S(2)}, u32[]{:S(2)}) collective-permute-start(bf16[320,768]{1,0:T(8,128)(2,1)S(1)} %get-tuple-element.157), channel_id=1, source_target_pairs={{0,4},{1,3},{2,6},{3,1},{4,0},{5,7},{6,2},{7,5},{8,12},{9,11},{10,... | collective-permute-start | bytes 1474568 | tf_op jit(solution)/shard_map/ppermute | solution.py:881
  377.0 13.6 %copy-start.6 = (f32[1024,768]{1,0:T(8,128)S(1)}, f32[1024,768]{1,0:T(8,128)}, u32[]{:S(2)}) copy-start(f32[1024,768]{1,0:T(8,128)} %get-tuple-element.145) | copy-start | bytes 9437188
  378.7 16.9 %copy-start.9 = (f32[288,768]{1,0:T(8,128)}, f32[288,768]{1,0:T(8,128)S(1)}, u32[]{:S(2)}) copy-start(f32[288,768]{1,0:T(8,128)S(1)} %bitcast_select_fusion) | copy-start | bytes 2654212
  378.8 16.9 %collective-permute-start.17 = (f32[16,768]{1,0:T(8,128)S(1)}, f32[16,768]{1,0:T(8,128)S(1)}, u32[]{:S(2)}, u32[]{:S(2)}) collective-permute-start(f32[16,768]{1,0:T(8,128)S(1)} %slice.45), channel_id=1, source_target_pairs={{1,0},{2,1},{3,2},{4,3},{5,4},{6,5},{7,6},{8,7},{9,8},{10,9},{11,1... | collective-permute-start | bytes 147464 | tf_op jit(solution)/shard_map/ppermute | solution.py:861
  380.2 22.8 %collective-permute-start.21 = (bf16[320,768]{1,0:T(8,128)(2,1)S(1)}, bf16[320,768]{1,0:T(8,128)(2,1)S(1)}, u32[]{:S(2)}, u32[]{:S(2)}) collective-permute-start(bf16[320,768]{1,0:T(8,128)(2,1)S(1)} %get-tuple-element.159), channel_id=1, source_target_pairs={{0,8},{1,9},{2,10},{3,11},{4,12},{5,13},{6,14},{7,15},{8,0},{9,1},... | collective-permute-start | bytes 1474568 | tf_op jit(solution)/shard_map/ppermute | solution.py:881
  395.7 7.4 %copy-start.13 = (f32[16,768]{1,0:T(8,128)}, f32[16,768]{1,0:T(8,128)S(1)}, u32[]{:S(2)}) copy-start(f32[16,768]{1,0:T(8,128)S(1)} %collective-permute-done.17) | copy-start | bytes 147460
  395.7 23.2 %copy-start.10 = (f32[288,768]{1,0:T(8,128)S(1)}, f32[288,768]{1,0:T(8,128)}, u32[]{:S(2)}) copy-start(f32[288,768]{1,0:T(8,128)} %copy-done.9) | copy-start | bytes 2654212
  403.1 15.9 %copy-start.14 = (f32[16,768]{1,0:T(8,128)S(1)}, f32[16,768]{1,0:T(8,128)}, u32[]{:S(2)}) copy-start(f32[16,768]{1,0:T(8,128)} %copy-done.13) | copy-start | bytes 147460
  403.1 15.7 %collective-permute-start.22 = (bf16[320,768]{1,0:T(8,128)(2,1)S(1)}, bf16[320,768]{1,0:T(8,128)(2,1)S(1)}, u32[]{:S(2)}, u32[]{:S(2)}) collective-permute-start(bf16[320,768]{1,0:T(8,128)(2,1)S(1)} %get-tuple-element.161), channel_id=1, source_target_pairs={{8,24},{9,25},{10,26},{11,27},{12,28},{13,29},{14,30},{15,31},{16,... | collective-permute-start | bytes 1474568 | tf_op jit(solution)/shard_map/ppermute | solution.py:881
  418.9 1.2 copy-start.7

commit v9 on v8

--- a/solution.py
+++ b/solution.py
@@ -355,12 +355,18 @@
     hat = unit_rows(x_ref[...].astype(F32))
     gn = dot_nt(dk_ref[...], w_ref[D : 2 * D, :]) + dot_nt(dv_ref[...], w_ref[2 * D : 3 * D, :])
 
+    last_step = pl.num_programs(0) - 1
+
     @pl.when(i == 0)
     def _():
+        gain_ref[...] = jnp.zeros(gain_ref.shape, F32)
+
+    @pl.when(i < last_step)
+    def _():
         out_ref[...] = gn.astype(BF)
-        gain_ref[...] = jnp.sum(gn * hat, axis=0, keepdims=True)
-
-    @pl.when(i > 0)
+        gain_ref[...] += jnp.sum(gn * hat, axis=0, keepdims=True)
+
+    @pl.when(i == last_step)
     def _():
         last = gn.shape[0] - 8
         full = jnp.concatenate([gn[:last], gn[last:] + dot_nt(dt_ref[...], w_ref[0:D, :])], 0)
@@ -370,7 +376,8 @@
 
 def before_bwd(x_both, back, weight, rows):
     dt, dk, dv = back[1:]
-    height = rows // 2
+    blocks = 4
+    height = rows // blocks
     step = pl.BlockSpec((height, D), lambda i: (i, 0))
 
     def whole(shape):
@@ -378,7 +385,7 @@
 
     return pl.pallas_call(
         before_bwd_kernel,
-        grid=(2,),
+        grid=(blocks,),
         in_specs=[step, whole((8, D)), step, step, whole((3 * D, D))],
         out_specs=[step, whole((1, D))],
         out_shape=[jax.ShapeDtypeStruct((rows, D), BF), jax.ShapeDtypeStruct((1, D), F32)],
@@ -629,6 +636,18 @@
         cost_estimate=cost(0, rows * D * 8),
         name="join_held",
     )(own, got)
+
+
+def hold(block, other):
+    held = pl.BlockSpec(memory_space=pl.ANY)
+    return pl.pallas_call(
+        lambda block_ref, other_ref, out_ref: None,
+        in_specs=[held, held],
+        out_specs=held,
+        out_shape=jax.ShapeDtypeStruct(block.shape, block.dtype),
+        input_output_aliases={0: 0},
+        name="hold",
+    )(block, other)
 
 
 def qkv_fwd_kernel(index_ref, x_ref, *refs, pieces, blocks):
@@ -696,7 +715,7 @@
 
 
 def ffn_kernel(
-    state_ref, index_ref, x_ref, att_ref, cot_ref, gain_ref, own_ref, got_ref,
+    state_ref, index_ref, x_ref, att_ref, cot_ref, gain_ref, own_ref, own_two_ref, got_ref, got_two_ref,
     out_ref, gh_ref, ga_ref, gain_grad_ref, away_ref, here_ref,
     hidden, low, total, back, cot, sq, gb, weights, stage_up, stage_down, stage_out, in_sems, sems,
 ):
@@ -707,9 +726,15 @@
     core = index_ref[24]
 
     def fetch(k, j):
-        ref = own_ref if k == 0 else got_ref
-        to = weights.at[pl.ds(3 * index_ref[12 * k + j], 3)]
-        return pltpu.make_async_copy(ref.at[pl.ds(3 * j, 3)], to, in_sems.at[12 * k + j])
+        ref = ((own_ref, own_two_ref), (got_ref, got_two_ref))[k][j // 6]
+        piece = index_ref[12 * k + j]
+        to = weights.at[pl.ds(3 * piece, 3)]
+        return pltpu.make_async_copy(ref.at[pl.ds(3 * (j % 6), 3)], to, in_sems.at[piece])
+
+    def fetched(pieces):
+        for piece in pieces:
+            at = weights.at[pl.ds(3 * piece, 3)]
+            pltpu.make_async_copy(own_ref.at[pl.ds(0, 3)], at, in_sems.at[piece]).wait()
 
     def put(source, group, count, column, sem, wait=False):
         piece = group // 3
@@ -760,15 +785,19 @@
         cot[...] = jnp.where(state_ref[0] > 0, cot_ref[...], jnp.zeros((), BF))
         total[...] = jnp.zeros(total.shape, F32)
         back[...] = jnp.zeros(back.shape, F32)
-        for k in range(2):
-            for j in range(12):
-                fetch(k, j).wait()
+        fetched(range(3))
         wo = square(0)
         for b in blocks:
             h = x_ref[b, :].astype(F32) + dot(att_ref[b, :], wo)
             hidden[b, :] = h
             hat = h * lax.rsqrt(jnp.mean(h * h, axis=-1, keepdims=True) + norm_eps)
             low[b, :] = (hat * gain_ref[...]).astype(BF)
+
+    for i, pieces in enumerate((range(3, 16), range(16, 19), range(19, 22), range(22, 24))):
+
+        @pl.when(c == i)
+        def _():
+            fetched(pieces)
 
     up = weights[8:40, c].reshape(D, D)
     down = weights[pl.ds(40 + 8 * c, 8)].reshape(D, D)
@@ -813,7 +842,7 @@
         put_out(True)
 
 
-def ffn(state, index, tokens, attended, out_grad, gain, own, got, rows):
+def ffn(state, index, tokens, attended, out_grad, gain, weights, rows):
     def whole(shape):
         return pl.BlockSpec(shape, lambda c: (0,) * len(shape), pipeline_mode=pl.Buffered(1))
 
@@ -824,7 +853,7 @@
     return pl.pallas_call(
         ffn_kernel,
         grid=(4,),
-        in_specs=[scalars, scalars, act, act, act, whole((1, D)), held, held],
+        in_specs=[scalars, scalars, act, act, act, whole((1, D)), held, held, held, held],
         out_specs=[act, act, act, whole((1, D)), held, held],
         out_shape=[
             jax.ShapeDtypeStruct((rows, D), BF),
@@ -852,7 +881,7 @@
         compiler_params=pltpu.CompilerParams(vmem_limit_bytes=60 << 20),
         cost_estimate=cost(2 * rows * D * D * (24 + 3), 2 * 12 * D * D * 2 + rows * D * 16),
         name="ffn",
-    )(state, index, tokens, attended, out_grad, gain, own, got)
+    )(state, index, tokens, attended, out_grad, gain, *weights)
 
 
 def shift_flat(block, distance):
@@ -1040,12 +1069,13 @@
     if staged:
         forward = att_fwd(after(state_vec, rest), projected, taps, forward, 0, rows)
         rest = join_held(after(rest, forward[0]), across)
-        across = swap(rest, 4, 2)
+        line = swap(rest, 4, 2)
+        core_rest = swap(rest, 1, 1)
         forward = att_fwd(after(state_vec, rest), projected, taps, forward, 1, rows)
-        forward = att_fwd(state_vec, projected, taps, forward, 2, rows)
-        rest = join_held(after(rest, forward[0]), across)
-        across = swap(rest, 1, 1)
-        own_weights, got_weights = rest.reshape(36, 4, 24, D), across.reshape(36, 4, 24, D)
+        forward = att_fwd(after(state_vec, core_rest), projected, taps, forward, 2, rows)
+        line = hold(line, forward[0])
+        core_line = swap(line, 1, 1)
+        late_weights = [w.reshape(18, 4, 24, D) for w in (rest, line, core_rest, core_line)]
     else:
         for part in range(PARTS):
             forward = att_fwd(state_vec, projected, taps, forward, part, rows)
@@ -1057,11 +1087,11 @@
             ],
             0,
         )
-        own_weights, got_weights = grouped[:36], grouped[36:]
+        late_weights = [grouped[18 * k : 18 * k + 18] for k in range(4)]
     attn_low, logs, *mixed = forward
 
     layer_out, grad_hidden, grad_attended, grad_gain_two, away_grad, here_grad = ffn(
-        state_vec, late_index, tokens, attn_low, out_grad, gain_second[None], own_weights, got_weights, rows
+        state_vec, late_index, tokens, attn_low, out_grad, gain_second[None], late_weights, rows
     )
 
     def backward(start, done, part):
@@ -1132,11 +1162,12 @@
         got = swap(send, 4, 2)
         send, keep = merge(core, keep, got, height + 16, 0)
         got = swap(send, 8, 8)
+        late_got = after(late_got, got)
+        send, keep = merge(core, keep, got, height + 16, 0)
         late_chunk = late_keep[0] + late_got[0].astype(F32)
         late_chunk = jnp.where(in_up, ungroup(late_chunk).reshape(3, 4, 24, D), late_chunk.reshape(3, 4, 24, D))
         late_chunk = late_chunk.reshape(-1, D)
         late_next = shift_flat(late_chunk[:16], -1)
-        send, keep = merge(after(core, late_next, input_grad), keep, got, height + 16, 0)
         got = swap(send, 16, 16, (1, 2))
         first = keep + got.astype(F32)
         quarter = count // 4

time: 429 us -> 428 us (level)
  starting transfers between devices: 70.3 us -> 59.6 us
  waiting for transfers between devices: 106 us -> 114 us
    ppermute x19 -> x20, starting transfers between devices: 59.7 us -> 49 us  [swap(): return lax.ppermute(block, AXES, route)]
    ppermute x19 -> x20, waiting for transfers between devices: 106 us -> 114 us  [swap(): return lax.ppermute(block, AXES, route)]
  transfers between devices with their start and end apart: 23 -> 24, of which waited for: 13 -> 15; matrix products, arithmetic and copies ran while one was open for 6% -> 6% of each run, Pallas kernels for 34% -> 34%
where the time goes in v9:
time: 428 us; the launch traced here: 422 us
  Pallas kernels  207 us (48%)
  waiting for transfers between devices  114 us (27%)
  starting transfers between devices  59.6 us (14%)
  other arithmetic  19.8 us (5%)
  local copies, waits for them, and re-layouts  18.3 us (4%)
    ppermute x20, waiting for transfers between devices, swap(): return lax.ppermute(block, AXES, route)  114 us
    pallas_call x3, Pallas kernels, att_fwd(): call_in_parts(att_fwd_kernel, [pl.BlockSpec(memory_space=pltpu.SMEM), col...  49.9 us
    ppermute x20, starting transfers between devices, swap(): return lax.ppermute(block, AXES, route)  49 us
    pallas_call x3, Pallas kernels, att_bwd(): call_in_parts(att_bwd_kernel, [pl.BlockSpec(memory_space=pltpu.SMEM), own...  48.7 us
    pallas_call x1, Pallas kernels, ffn(): pl.pallas_call(ffn_kernel, grid=(4,), in_specs=[scalars, scalars, act, ac...  46.7 us
    pallas_call x1, Pallas kernels, qkv_bwd(): pl.pallas_call(body, grid=(blocks,), in_specs=[pl.BlockSpec(memory_space=...  19.3 us
    pallas_call x4, Pallas kernels, merge_grid(): pl.pallas_call(body, grid_spec=pltpu.PrefetchScalarGridSpec(num_scalar_pr...  15.9 us
    pallas_call x1, Pallas kernels, qkv_fwd(): pl.pallas_call(body, grid=(blocks,), in_specs=[pl.BlockSpec(memory_space=...  13.3 us
  transfers between devices with their start and end apart: 24, of which 15 were waited for; matrix products, arithmetic and copies ran while one was open for 6% of the time, Pallas kernels for 34%

profile of v9, /device:TPU:0, one launch (start us, length us, event | category | flops | bytes accessed | tf_op | source)
XLA Modules:
  0.0 422.2 jit_solution(17352929236855115378)
XLA Ops:
  1.5 2.3 collective-permute-start
  3.8 2.3 concatenate.22
  6.3 1.5 fusion.8
  8.8 5.7 %collective-permute-start.1 = (bf16[1024,768]{1,0:T(8,128)(2,1)S(1)}, bf16[1024,768]{1,0:T(8,128)(2,1)}, u32[]{:S(2)}, u32[]{:S(2)}) collective-permute-start(bf16[1024,768]{1,0:T(8,128)(2,1)S(1)} %copy-done.4), channel_id=1, source_target_pairs={{0,1},{1,2},{2,3},{4,5},{5,6},{6,7},{8,9},{9,10},{10,11},{12,13},{... | collective-permute-start | bytes 4718600 | tf_op jit(solution)/shard_map/ppermute | solution.py:896
  14.5 2.8 collective-permute-start.2
  17.3 1.5 constant_dynamic-update-slice_fusion.1
  19.0 18.6 %collective-permute-done.2 = bf16[304,768]{1,0:T(8,128)(2,1)S(1)} collective-permute-done((bf16[304,768]{1,0:T(8,128)(2,1)S(1)}, bf16[304,768]{1,0:T(8,128)(2,1)S(1)}, u32[]{:S(2)}, u32[]{:S(2)}) %collective-permute-start.2) | collective-permute-done | bytes 466976 | tf_op jit(solution)/shard_map/ppermute | solution.py:910
  38.4 10.9 %collective-permute-done.3 = bf16[304,768]{1,0:T(8,128)(2,1)S(1)} collective-permute-done((bf16[304,768]{1,0:T(8,128)(2,1)S(1)}, bf16[304,768]{1,0:T(8,128)(2,1)S(1)}, u32[]{:S(2)}, u32[]{:S(2)}) %collective-permute-start.3) | collective-permute-done | bytes 466976 | tf_op jit(solution)/shard_map/ppermute | solution.py:910
  49.7 8.3 %collective-permute-done.4.got_ref = bf16[304,768]{1,0:T(8,128)(2,1)S(1)} collective-permute-done((bf16[304,768]{1,0:T(8,128)(2,1)S(1)}, bf16[304,768]{1,0:T(8,128)(2,1)S(1)}, u32[]{:S(2)}, u32[]{:S(2)}) %collective-permute-start.4) | collective-permute-done | bytes 466976 | tf_op jit(solution)/shard_map/ppermute | solution.py:910
  58.1 1.6 collective-permute-start.5
  59.7 11.8 %collective-permute-done.5.got_ref = bf16[592,768]{1,0:T(8,128)(2,1)S(1)} collective-permute-done((bf16[592,768]{1,0:T(8,128)(2,1)S(1)}, bf16[592,768]{1,0:T(8,128)(2,1)S(1)}, u32[]{:S(2)}, u32[]{:S(2)}) %collective-permute-start.5) | collective-permute-done | bytes 909344 | tf_op jit(solution)/shard_map/ppermute | solution.py:910
  71.5 1.3 join.3.refs_2_
  72.9 1.8 collective-permute-start.7
  75.4 1.5 collective-permute-done.6.refs_3_
  76.9 13.3 %qkv_fwd.1 = (bf16[2048,2304]{1,0:T(8,128)(2,1)}, f32[16,768]{1,0:T(8,128)}, bf16[2304,768]{1,0:T(8,128)(2,1)}) custom-call(s32[8]{0:T(128)} %stack.213.refs_0_, bf16[2048,768]{1,0:T(8,128)(2,1)} %copy-done.8, bf16[1168,768]{1,0:T(8,128)(2,1)} %join.3.refs_2_, bf16[1168,768]{1,0:T(8,128)(2,1)} %collective-permute-done.6.refs_3_), custom_call_target="tpu_custom_call" | custom-call | flops 7247757312 | bytes 15728640 | tf_op jit(solution)/shard_map/qkv_fwd/pallas_call | solution.py:693
  90.2 4.9 %collective-permute-done.7 = bf16[576,768]{1,0:T(8,128)(2,1)S(1)} collective-permute-done((bf16[576,768]{1,0:T(8,128)(2,1)S(1)}, bf16[576,768]{1,0:T(8,128)(2,1)S(1)}, u32[]{:S(2)}, u32[]{:S(2)}) %collective-permute-start.7) | collective-permute-done | bytes 884768 | tf_op jit(solution)/shard_map/ppermute | solution.py:910
  99.4 16.2 %att_fwd.3 = (bf16[1024,768]{1,0:T(8,128)(2,1)}, f32[1024,768]{1,0:T(8,128)}, bf16[1024,768]{1,0:T(8,128)(2,1)}, bf16[2048,768]{1,0:T(8,128)(2,1)}, bf16[2048,768]{1,0:T(8,128)(2,1)}) custom-call(s32[1]{0:T(128)S(6)} %select_n.155.refs_0_.state_ref, bf16[2048,2304]{1,0:T(8,128)(2,1)} %get-tuple-element.86.refs_1_.refs_2_.refs_3_.refs_4_.refs_7_.refs_8_.refs_9_.refs_10_, ...), custom_call_target="tpu_custom_call" | custom-call | flops 6442450944 | bytes 7864320 | tf_op jit(solution)/shard_map/att_fwd/pallas_call | solution.py:150
  118.3 16.5 %att_fwd.4 = (bf16[1024,768]{1,0:T(8,128)(2,1)}, f32[1024,768]{1,0:T(8,128)}, bf16[1024,768]{1,0:T(8,128)(2,1)}, bf16[2048,768]{1,0:T(8,128)(2,1)}, bf16[2048,768]{1,0:T(8,128)(2,1)}) custom-call(s32[1]{0:T(128)S(6)} %select_n.155.refs_0_.state_ref, ...), custom_call_target="tpu_custom_call", output_to_operand_aliasing={{0}: (8, {}), {1}: (9, {}), {2}: (10, {}), {3}: (11, {}), {... | custom-call | flops 6442450944 | bytes 7864320 | tf_op jit(solution)/shard_map/att_fwd/pallas_call | solution.py:150
  134.9 17.2 %att_fwd.5 = (bf16[1024,768]{1,0:T(8,128)(2,1)}, f32[1024,768]{1,0:T(8,128)}, bf16[1024,768]{1,0:T(8,128)(2,1)}, bf16[2048,768]{1,0:T(8,128)(2,1)}, bf16[2048,768]{1,0:T(8,128)(2,1)}) custom-call(s32[1]{0:T(128)S(6)} %select_n.155.refs_0_.state_ref, ...), custom_call_target="tpu_custom_call", output_to_operand_aliasing={{0}: (8, {}), {1}: (9, {}), {2}: (10, {}), {3}: (11, {}), {... | custom-call | flops 6442450944 | bytes 7864320 | tf_op jit(solution)/shard_map/att_fwd/pallas_call | solution.py:150
  153.8 3.6 collective-permute-done.11
  157.4 1.5 copy-done.18
  158.9 46.7 %ffn.1 = (bf16[1024,768]{1,0:T(8,128)(2,1)}, f32[1024,768]{1,0:T(8,128)}, bf16[1024,768]{1,0:T(8,128)(2,1)}, f32[1,768]{1,0:T(1,128)}, bf16[36,4,24,768]{3,2,1,0...) custom-call(s32[1]{0:T(128)S(6)} %select_n.155.refs_0_.state_ref, s32[25]{0:T(128)} %stack.208.index_ref, ...), custom_call_target="tpu_custom_call" | custom-call | flops 32614907904 | bytes 40894464 | tf_op jit(solution)/shard_map/ffn/pallas_call | solution.py:853
  206.5 16.0 %att_bwd.3 = (bf16[1024,768]{1,0:T(8,128)(2,1)}, bf16[8,768]{1,0:T(8,128)(2,1)}, bf16[2048,768]{1,0:T(8,128)(2,1)}, bf16[2048,768]{1,0:T(8,128)(2,1)}, f32[16,768]{1,0:T(8,128)}) custom-call(s32[1]{0:T(128)S(6)} %select_n.155.refs_0_.state_ref, bf16[1024,768]{1,0:T(8,128)(2,1)} %get-tuple-element.107.refs_1_, bf16[2048,768]{1,0:T(8,128)(2,1)} %get-tuple-element.108.refs_2_, ...), custom_call_target="tpu_custom_call" | custom-call | flops 16106127360 | bytes 10485760 | tf_op jit(solution)/shard_map/att_bwd/pallas_call | solution.py:307
  222.6 7.5 %merge_grid.4 = (bf16[6,288,768]{2,1,0:T(8,128)(2,1)}, f32[6,288,768]{2,1,0:T(8,128)}) custom-call(s32[12]{0:T(128)S(1)} %stack.236.index_ref, bf16[12,288,768]{2,1,0:T(8,128)(2,1)S(1)} %bitcast.77, bf16[12,288,768]{2,1,0:T(8,128)(2,1)} %collective-permute-done.12.ga_ref.gb_ref, bf16[12,288,768]{2,1,0:T(8,128)(2,1)S(1)} %bitcast.78, ...), custom_call_target="tpu_custom_call" | custom-call | flops 2654208 | bytes 21233664 | tf_op jit(solution)/shard_map/merge_grid/pallas_call | solution.py:543
  230.1 12.8 %collective-permute-start.13 = (bf16[6,288,768]{2,1,0:T(8,128)(2,1)}, bf16[6,288,768]{2,1,0:T(8,128)(2,1)S(1)}, u32[]{:S(2)}, u32[]{:S(2)}) collective-permute-start(bf16[6,288,768]{2,1,0:T(8,128)(2,1)} %get-tuple-element.116), channel_id=1, source_target_pairs={{0,2},{1,5},{2,0},{3,7},{4,6},{5,1},{6,4},{7,3},{8,10},{9,13},{10,... | collective-permute-start | bytes 7962632 | tf_op jit(solution)/shard_map/ppermute | solution.py:910
  243.0 16.3 %att_bwd.4 = (bf16[1024,768]{1,0:T(8,128)(2,1)}, bf16[8,768]{1,0:T(8,128)(2,1)}, bf16[2048,768]{1,0:T(8,128)(2,1)}, bf16[2048,768]{1,0:T(8,128)(2,1)}, f32[16,768]{1,0:T(8,128)}) custom-call(s32[1]{0:T(128)S(6)} %select_n.155.refs_0_.state_ref, ...), custom_call_target="tpu_custom_call", output_to_operand_aliasing={{0}: (14, {}), {1}: (15, {}), {2}: (16, {}), {3}: (17, {}),... | custom-call | flops 16106127360 | bytes 10485760 | tf_op jit(solution)/shard_map/att_bwd/pallas_call | solution.py:307
  259.3 13.8 %collective-permute-done.13.ga_ref.gb_ref = bf16[6,288,768]{2,1,0:T(8,128)(2,1)S(1)} collective-permute-done((bf16[6,288,768]{2,1,0:T(8,128)(2,1)}, bf16[6,288,768]{2,1,0:T(8,128)(2,1)S(1)}, u32[]{:S(2)}, u32[]{:S(2)}) %collective-permute-start.13) | collective-permute-done | bytes 2654240 | tf_op jit(solution)/shard_map/ppermute | solution.py:910
  273.2 3.0 merge_grid.5
  276.1 16.4 %att_bwd.5 = (bf16[1024,768]{1,0:T(8,128)(2,1)}, bf16[8,768]{1,0:T(8,128)(2,1)}, bf16[2048,768]{1,0:T(8,128)(2,1)}, bf16[2048,768]{1,0:T(8,128)(2,1)}, f32[16,768]{1,0:T(8,128)}) custom-call(s32[1]{0:T(128)S(6)} %select_n.155.refs_0_.state_ref, ...), custom_call_target="tpu_custom_call", output_to_operand_aliasing={{0}: (14, {}), {1}: (15, {}), {2}: (16, {}), {3}: (17, {}),... | custom-call | flops 16106127360 | bytes 10485760 | tf_op jit(solution)/shard_map/att_bwd/pallas_call | solution.py:307
  292.5 8.1 %before_bwd.1 = (bf16[1024,768]{1,0:T(8,128)(2,1)}, f32[1,768]{1,0:T(1,128)}) custom-call(bf16[2048,768]{1,0:T(8,128)(2,1)} %copy-done.8, bf16[8,768]{1,0:T(8,128)(2,1)} %get-tuple-element.136.dt_ref.refs_3_, bf16[2048,768]{1,0:T(8,128)(2,1)} %get-tuple-element.137.dk_ref.refs_4_, bf16[2048,768]{1,0:T(8,128)(2,1)} %get-tuple-element.138.dv_ref.refs_5_, ...), custom_call_target="tpu_custom_call" | custom-call | flops 2415919104 | bytes 9437184 | tf_op jit(solution)/shard_map/before_bwd/pallas_call | solution.py:386
  302.1 3.7 merge_grid.6
  305.7 6.9 %collective-permute-start.16 = (bf16[2,288,768]{2,1,0:T(8,128)(2,1)}, bf16[2,288,768]{2,1,0:T(8,128)(2,1)S(1)}, u32[]{:S(2)}, u32[]{:S(2)}) collective-permute-start(bf16[2,288,768]{2,1,0:T(8,128)(2,1)} %get-tuple-element.134), channel_id=1, source_target_pairs={{0,8},{1,9},{2,10},{3,11},{4,12},{5,13},{6,14},{7,15},{8,0},{9,1},... | collective-permute-start | bytes 2654216 | tf_op jit(solution)/shard_map/ppermute | solution.py:910
  312.6 19.3 %qkv_bwd.1 = (bf16[1232,768]{1,0:T(8,128)(2,1)}, f32[1232,768]{1,0:T(8,128)}, f32[1024,768]{1,0:T(8,128)}) custom-call(s32[1]{0:T(128)} %bitcast.24.refs_0_.index_ref, bf16[2048,768]{1,0:T(8,128)(2,1)} %copy-done.8, bf16[1024,768]{1,0:T(8,128)(2,1)} %get-tuple-element.142.refs_2_, bf16[8,768]{1,0:T(8,128)(2,1)} %get-tuple-element.136.dt_ref.refs_3_, ...), custom_call_target="tpu_custom_call" | custom-call | flops 9663676416 | bytes 23592960 | tf_op jit(solution)/shard_map/qkv_bwd/pallas_call | solution.py:481
  333.0 1.7 merge_grid.7
  335.0 3.8 collective-permute-done.17.got_ref
  339.7 14.0 %collective-permute-start.18 = (bf16[624,768]{1,0:T(8,128)(2,1)S(1)}, bf16[624,768]{1,0:T(8,128)(2,1)S(1)}, u32[]{:S(2)}, u32[]{:S(2)}) collective-permute-start(bf16[624,768]{1,0:T(8,128)(2,1)S(1)} %get-tuple-element.153), channel_id=1, source_target_pairs={{0,2},{1,5},{2,0},{3,7},{4,6},{5,1},{6,4},{7,3},{8,10},{9,13},{10,... | collective-permute-start | bytes 2875400 | tf_op jit(solution)/shard_map/ppermute | solution.py:910
  353.8 11.7 %collective-permute-done.18.got_ref = bf16[624,768]{1,0:T(8,128)(2,1)S(1)} collective-permute-done((bf16[624,768]{1,0:T(8,128)(2,1)S(1)}, bf16[624,768]{1,0:T(8,128)(2,1)S(1)}, u32[]{:S(2)}, u32[]{:S(2)}) %collective-permute-start.18) | collective-permute-done | bytes 958496 | tf_op jit(solution)/shard_map/ppermute | solution.py:910
  368.3 6.9 %collective-permute-done.19.got_ref = bf16[320,768]{1,0:T(8,128)(2,1)S(1)} collective-permute-done((bf16[320,768]{1,0:T(8,128)(2,1)S(1)}, bf16[320,768]{1,0:T(8,128)(2,1)S(1)}, u32[]{:S(2)}, u32[]{:S(2)}) %collective-permute-start.19) | collective-permute-done | bytes 491552 | tf_op jit(solution)/shard_map/ppermute | solution.py:910
  375.4 1.9 collective-permute-start.20
  379.2 3.4 fusion.2
  382.6 6.3 %collective-permute-done.20.got_ref = bf16[320,768]{1,0:T(8,128)(2,1)S(1)} collective-permute-done((bf16[320,768]{1,0:T(8,128)(2,1)S(1)}, bf16[320,768]{1,0:T(8,128)(2,1)S(1)}, u32[]{:S(2)}, u32[]{:S(2)}) %collective-permute-start.20) | collective-permute-done | bytes 491552 | tf_op jit(solution)/shard_map/ppermute | solution.py:910
  391.0 5.5 %collective-permute-done.22 = bf16[1,288,768]{2,1,0:T(8,128)(2,1)S(1)} collective-permute-done((bf16[1,288,768]{2,1,0:T(8,128)(2,1)}, bf16[1,288,768]{2,1,0:T(8,128)(2,1)S(1)}, u32[]{:S(2)}, u32[]{:S(2)}) %collective-permute-start.22) | collective-permute-done | bytes 442400 | tf_op jit(solution)/shard_map/ppermute | solution.py:910
  397.5 2.4 copy.39
  399.9 2.4 reshape.131
  402.3 5.3 %collective-permute-done.21 = bf16[320,768]{1,0:T(8,128)(2,1)S(1)} collective-permute-done((bf16[320,768]{1,0:T(8,128)(2,1)S(1)}, bf16[320,768]{1,0:T(8,128)(2,1)S(1)}, u32[]{:S(2)}, u32[]{:S(2)}) %collective-permute-start.21) | collective-permute-done | bytes 491552 | tf_op jit(solution)/shard_map/ppermute | solution.py:910
  409.6 2.2 slice_select_fusion
  413.2 4.1 fusion.5
  418.5 3.5 fusion.17
  (121 shorter events, 27.7 us)
Async XLA Ops:
  1.5 4.8 %collective-permute-start = (bf16[96,128]{1,0:T(8,128)(2,1)S(1)}, bf16[96,128]{1,0:T(8,128)(2,1)S(1)}, u32[]{:S(2)}, u32[]{:S(2)}) collective-permute-start(bf16[96,128]{1,0:T(8,128)(2,1)S(1)} %slice.35), channel_id=1, source_target_pairs={{0,1},{1,2},{2,3},{3,4},{4,5},{5,6},{6,7},{7,8},{8,9},{9,10},{10,1... | collective-permute-start | bytes 73736 | tf_op jit(solution)/shard_map/ppermute | solution.py:890
  6.2 2.6 copy-start.15
  6.3 2.6 copy-start.4
  8.8 8.5 %collective-permute-start.1 = (bf16[1024,768]{1,0:T(8,128)(2,1)S(1)}, bf16[1024,768]{1,0:T(8,128)(2,1)}, u32[]{:S(2)}, u32[]{:S(2)}) collective-permute-start(bf16[1024,768]{1,0:T(8,128)(2,1)S(1)} %copy-done.4), channel_id=1, source_target_pairs={{0,1},{1,2},{2,3},{4,5},{5,6},{6,7},{8,9},{9,10},{10,11},{12,13},{... | collective-permute-start | bytes 4718600 | tf_op jit(solution)/shard_map/ppermute | solution.py:896
  14.5 23.0 %collective-permute-start.2 = (bf16[304,768]{1,0:T(8,128)(2,1)S(1)}, bf16[304,768]{1,0:T(8,128)(2,1)S(1)}, u32[]{:S(2)}, u32[]{:S(2)}) collective-permute-start(bf16[304,768]{1,0:T(8,128)(2,1)S(1)} %pad_maximum_fusion.2), channel_id=1, source_target_pairs={{0,16},{1,17},{2,18},{3,19},{4,20},{5,21},{6,22},{7,23},{8,24},{9,... | collective-permute-start | bytes 1400840 | tf_op jit(solution)/shard_map/ppermute | solution.py:910
  19.0 30.8 %copy-start.8 = (bf16[2048,768]{1,0:T(8,128)(2,1)}, bf16[2048,768]{1,0:T(8,128)(2,1)S(1)}, u32[]{:S(2)}) copy-start(bf16[2048,768]{1,0:T(8,128)(2,1)S(1)} %constant_dynamic-update-slice_fusion.refs_1_.x_ref) | copy-start | bytes 9437188
  37.7 11.6 %collective-permute-start.3 = (bf16[304,768]{1,0:T(8,128)(2,1)S(1)}, bf16[304,768]{1,0:T(8,128)(2,1)S(1)}, u32[]{:S(2)}, u32[]{:S(2)}) collective-permute-start(bf16[304,768]{1,0:T(8,128)(2,1)S(1)} %pad_maximum_fusion.3), channel_id=1, source_target_pairs={{0,8},{1,9},{2,10},{3,11},{4,12},{5,13},{6,14},{7,15},{8,0},{9,1},... | collective-permute-start | bytes 1400840 | tf_op jit(solution)/shard_map/ppermute | solution.py:910
  49.4 8.6 %collective-permute-start.4 = (bf16[304,768]{1,0:T(8,128)(2,1)S(1)}, bf16[304,768]{1,0:T(8,128)(2,1)S(1)}, u32[]{:S(2)}, u32[]{:S(2)}) collective-permute-start(bf16[304,768]{1,0:T(8,128)(2,1)S(1)} %fusion.16.own_ref), channel_id=1, source_target_pairs={{0,2},{1,5},{2,0},{3,7},{4,6},{5,1},{6,4},{7,3},{8,10},{9,13},{10,... | collective-permute-start | bytes 1400840 | tf_op jit(solution)/shard_map/ppermute | solution.py:910
  58.1 13.4 %collective-permute-start.5 = (bf16[592,768]{1,0:T(8,128)(2,1)S(1)}, bf16[592,768]{1,0:T(8,128)(2,1)S(1)}, u32[]{:S(2)}, u32[]{:S(2)}) collective-permute-start(bf16[592,768]{1,0:T(8,128)(2,1)S(1)} %join.2.own_ref), channel_id=1, source_target_pairs={{0,4},{1,3},{2,6},{3,1},{4,0},{5,7},{6,2},{7,5},{8,12},{9,11},{10,... | collective-permute-start | bytes 2727944 | tf_op jit(solution)/shard_map/ppermute | solution.py:910
  72.8 4.1 collective-permute-start.6
  72.9 22.1 %collective-permute-start.7 = (bf16[576,768]{1,0:T(8,128)(2,1)S(1)}, bf16[576,768]{1,0:T(8,128)(2,1)S(1)}, u32[]{:S(2)}, u32[]{:S(2)}) collective-permute-start(bf16[576,768]{1,0:T(8,128)(2,1)S(1)} %pad_maximum_fusion.1), channel_id=1, source_target_pairs={{0,8},{1,9},{2,10},{3,11},{4,12},{5,13},{6,14},{7,15},{8,0},{9,1},... | collective-permute-start | bytes 2654216 | tf_op jit(solution)/shard_map/ppermute | solution.py:910
  90.2 8.6 %copy-start.12 = (f32[16,768]{1,0:T(8,128)S(1)}, f32[16,768]{1,0:T(8,128)}, u32[]{:S(2)}) copy-start(f32[16,768]{1,0:T(8,128)} %get-tuple-element.90) | copy-start | bytes 147460
  96.0 19.7 %collective-permute-start.8 = (bf16[864,768]{1,0:T(8,128)(2,1)S(1)}, bf16[864,768]{1,0:T(8,128)(2,1)S(1)}, u32[]{:S(2)}, u32[]{:S(2)}) collective-permute-start(bf16[864,768]{1,0:T(8,128)(2,1)S(1)} %bitcast.79), channel_id=1, source_target_pairs={{0,2},{1,5},{2,0},{3,7},{4,6},{5,1},{6,4},{7,3},{8,10},{9,13},{10,... | collective-permute-start | bytes 3981320 | tf_op jit(solution)/shard_map/ppermute | solution.py:910
  116.6 18.2 %copy-start.3 = (bf16[1728,768]{1,0:T(8,128)(2,1)}, bf16[1728,768]{1,0:T(8,128)(2,1)S(1)}, u32[]{:S(2)}) copy-start(bf16[1728,768]{1,0:T(8,128)(2,1)S(1)} %join_held.1) | copy-start | bytes 7962628
  116.6 18.2 %collective-permute-start.9 = (bf16[1728,768]{1,0:T(8,128)(2,1)S(1)}, bf16[1728,768]{1,0:T(8,128)(2,1)S(1)}, u32[]{:S(2)}, u32[]{:S(2)}) collective-permute-start(bf16[1728,768]{1,0:T(8,128)(2,1)S(1)} %join_held.1), channel_id=1, source_target_pairs={{0,1},{1,0},{2,3},{3,2},{4,5},{5,4},{6,7},{7,6},{8,9},{9,8},{10,11... | collective-permute-start | bytes 7962632 | tf_op jit(solution)/shard_map/ppermute | solution.py:910
  117.4 34.7 %collective-permute-start.10 = (bf16[1728,768]{1,0:T(8,128)(2,1)S(1)}, bf16[1728,768]{1,0:T(8,128)(2,1)}, u32[]{:S(2)}, u32[]{:S(2)}) collective-permute-start(bf16[1728,768]{1,0:T(8,128)(2,1)S(1)} %join_held.1), channel_id=1, source_target_pairs={{0,4},{1,3},{2,6},{3,1},{4,0},{5,7},{6,2},{7,5},{8,12},{9,11},{10,... | collective-permute-start | bytes 7962632 | tf_op jit(solution)/shard_map/ppermute | solution.py:910
  134.9 17.2 %copy-start.17 = (bf16[1728,768]{1,0:T(8,128)(2,1)}, bf16[1728,768]{1,0:T(8,128)(2,1)S(1)}, u32[]{:S(2)}) copy-start(bf16[1728,768]{1,0:T(8,128)(2,1)S(1)} %collective-permute-done.9) | copy-start | bytes 7962628
  152.1 5.3 %collective-permute-start.11 = (bf16[1728,768]{1,0:T(8,128)(2,1)}, bf16[1728,768]{1,0:T(8,128)(2,1)S(1)}, u32[]{:S(2)}, u32[]{:S(2)}) collective-permute-start(bf16[1728,768]{1,0:T(8,128)(2,1)} %hold.1), channel_id=1, source_target_pairs={{0,1},{1,0},{2,3},{3,2},{4,5},{5,4},{6,7},{7,6},{8,9},{9,8},{10,11... | collective-permute-start | bytes 7962632 | tf_op jit(solution)/shard_map/ppermute | solution.py:910
  157.4 1.5 copy-start.18
  205.6 17.0 %collective-permute-start.12 = (bf16[12,288,768]{2,1,0:T(8,128)(2,1)}, bf16[12,288,768]{2,1,0:T(8,128)(2,1)}, u32[]{:S(2)}, u32[]{:S(2)}) collective-permute-start(bf16[12,288,768]{2,1,0:T(8,128)(2,1)} %bitcast.86), channel_id=1, source_target_pairs={{0,1},{1,0},{2,3},{3,2},{4,5},{5,4},{6,7},{7,6},{8,9},{9,8},{10,11... | collective-permute-start | bytes 15925256 | tf_op jit(solution)/shard_map/ppermute | solution.py:910
  206.5 16.1 %slice-start.2 = ((s8[5308416]{0:T(1024)(128)(4,1)}), s8[4194304]{0:T(1024)(128)(4,1)S(1)}, s32[]{:S(2)}) async-start(s8[5308416]{0:T(1024)(128)(4,1)} %bitcast.75), calls=%async_computation.2 | async-start | bytes 8388608
  206.5 16.1 %slice-start.3 = ((s8[5308416]{0:T(1024)(128)(4,1)}), s8[1114112]{0:T(1024)(128)(4,1)S(1)}, s32[]{:S(2)}) async-start(s8[5308416]{0:T(1024)(128)(4,1)} %bitcast.75), calls=%async_computation.3 | async-start | bytes 2228224
  230.1 43.0 %collective-permute-start.13 = (bf16[6,288,768]{2,1,0:T(8,128)(2,1)}, bf16[6,288,768]{2,1,0:T(8,128)(2,1)S(1)}, u32[]{:S(2)}, u32[]{:S(2)}) collective-permute-start(bf16[6,288,768]{2,1,0:T(8,128)(2,1)} %get-tuple-element.116), channel_id=1, source_target_pairs={{0,2},{1,5},{2,0},{3,7},{4,6},{5,1},{6,4},{7,3},{8,10},{9,13},{10,... | collective-permute-start | bytes 7962632 | tf_op jit(solution)/shard_map/ppermute | solution.py:910
  243.0 30.1 %slice-start = ((s8[5308416]{0:T(1024)(128)(4,1)}), s8[4194304]{0:T(1024)(128)(4,1)S(1)}, s32[]{:S(2)}) async-start(s8[5308416]{0:T(1024)(128)(4,1)} %bitcast.73), calls=%async_computation | async-start | bytes 8388608
  243.0 30.1 %slice-start.1 = ((s8[5308416]{0:T(1024)(128)(4,1)}), s8[1114112]{0:T(1024)(128)(4,1)S(1)}, s32[]{:S(2)}) async-start(s8[5308416]{0:T(1024)(128)(4,1)} %bitcast.73), calls=%async_computation.1 | async-start | bytes 2228224
  276.1 25.9 %collective-permute-start.14 = (bf16[3,288,768]{2,1,0:T(8,128)(2,1)}, bf16[3,288,768]{2,1,0:T(8,128)(2,1)}, u32[]{:S(2)}, u32[]{:S(2)}) collective-permute-start(bf16[3,288,768]{2,1,0:T(8,128)(2,1)} %get-tuple-element.125), channel_id=1, source_target_pairs={{0,4},{1,3},{2,6},{3,1},{4,0},{5,7},{6,2},{7,5},{8,12},{9,11},{10,... | collective-permute-start | bytes 3981320 | tf_op jit(solution)/shard_map/ppermute | solution.py:910
  292.5 9.6 %copy-start = (f32[3,288,768]{2,1,0:T(8,128)S(1)}, f32[3,288,768]{2,1,0:T(8,128)}, u32[]{:S(2)}) copy-start(f32[3,288,768]{2,1,0:T(8,128)} %get-tuple-element.133.ka_ref.kb_ref) | copy-start | bytes 7962628
  300.6 34.1 %collective-permute-start.15 = (bf16[1024,768]{1,0:T(8,128)(2,1)}, bf16[1024,768]{1,0:T(8,128)(2,1)}, u32[]{:S(2)}, u32[]{:S(2)}) collective-permute-start(bf16[1024,768]{1,0:T(8,128)(2,1)} %get-tuple-element.140), channel_id=1, source_target_pairs={{1,0},{2,1},{3,2},{5,4},{6,5},{7,6},{9,8},{10,9},{11,10},{13,12},{... | collective-permute-start | bytes 4718600 | tf_op jit(solution)/shard_map/ppermute | solution.py:896
  305.7 27.3 %collective-permute-start.16 = (bf16[2,288,768]{2,1,0:T(8,128)(2,1)}, bf16[2,288,768]{2,1,0:T(8,128)(2,1)S(1)}, u32[]{:S(2)}, u32[]{:S(2)}) collective-permute-start(bf16[2,288,768]{2,1,0:T(8,128)(2,1)} %get-tuple-element.134), channel_id=1, source_target_pairs={{0,8},{1,9},{2,10},{3,11},{4,12},{5,13},{6,14},{7,15},{8,0},{9,1},... | collective-permute-start | bytes 2654216 | tf_op jit(solution)/shard_map/ppermute | solution.py:910
  312.6 20.4 %copy-start.1 = (f32[2,288,768]{2,1,0:T(8,128)S(1)}, f32[2,288,768]{2,1,0:T(8,128)}, u32[]{:S(2)}) copy-start(f32[2,288,768]{2,1,0:T(8,128)} %get-tuple-element.149.ka_ref.kb_ref) | copy-start | bytes 5308420
  331.9 6.9 %copy-start.2 = (f32[1232,768]{1,0:T(8,128)S(1)}, f32[1232,768]{1,0:T(8,128)}, u32[]{:S(2)}) copy-start(f32[1232,768]{1,0:T(8,128)} %get-tuple-element.146.keep_ref) | copy-start | bytes 11354116
  334.7 4.1 collective-permute-start.17
  338.8 27.6 %copy-start.16 = (pred[3]{0:T(512)(128)(4,1)S(1)}, pred[3]{0:T(512)(128)(4,1)}, u32[]{:S(2)}) copy-start(pred[3]{0:T(512)(128)(4,1)} %copy-done.15) | copy-start | bytes 13
  338.8 29.1 %copy-start.5 = (bf16[1024,768]{1,0:T(8,128)(2,1)S(1)}, bf16[1024,768]{1,0:T(8,128)(2,1)}, u32[]{:S(2)}) copy-start(bf16[1024,768]{1,0:T(8,128)(2,1)} %x_ref.1) | copy-start | bytes 4718596
  339.7 25.8 %collective-permute-start.18 = (bf16[624,768]{1,0:T(8,128)(2,1)S(1)}, bf16[624,768]{1,0:T(8,128)(2,1)S(1)}, u32[]{:S(2)}, u32[]{:S(2)}) collective-permute-start(bf16[624,768]{1,0:T(8,128)(2,1)S(1)} %get-tuple-element.153), channel_id=1, source_target_pairs={{0,2},{1,5},{2,0},{3,7},{4,6},{5,1},{6,4},{7,3},{8,10},{9,13},{10,... | collective-permute-start | bytes 2875400 | tf_op jit(solution)/shard_map/ppermute | solution.py:910
  366.4 8.9 %collective-permute-start.19 = (bf16[320,768]{1,0:T(8,128)(2,1)S(1)}, bf16[320,768]{1,0:T(8,128)(2,1)S(1)}, u32[]{:S(2)}, u32[]{:S(2)}) collective-permute-start(bf16[320,768]{1,0:T(8,128)(2,1)S(1)} %get-tuple-element.155), channel_id=1, source_target_pairs={{0,4},{1,3},{2,6},{3,1},{4,0},{5,7},{6,2},{7,5},{8,12},{9,11},{10,... | collective-permute-start | bytes 1474568 | tf_op jit(solution)/shard_map/ppermute | solution.py:910
  375.4 13.6 %collective-permute-start.20 = (bf16[320,768]{1,0:T(8,128)(2,1)S(1)}, bf16[320,768]{1,0:T(8,128)(2,1)S(1)}, u32[]{:S(2)}, u32[]{:S(2)}) collective-permute-start(bf16[320,768]{1,0:T(8,128)(2,1)S(1)} %get-tuple-element.157), channel_id=1, source_target_pairs={{0,8},{1,9},{2,10},{3,11},{4,12},{5,13},{6,14},{7,15},{8,0},{9,1},... | collective-permute-start | bytes 1474568 | tf_op jit(solution)/shard_map/ppermute | solution.py:910
  377.9 18.6 %collective-permute-start.22 = (bf16[1,288,768]{2,1,0:T(8,128)(2,1)}, bf16[1,288,768]{2,1,0:T(8,128)(2,1)S(1)}, u32[]{:S(2)}, u32[]{:S(2)}) collective-permute-start(bf16[1,288,768]{2,1,0:T(8,128)(2,1)} %get-tuple-element.150), channel_id=1, source_target_pairs={{0,16},{1,17},{2,18},{3,19},{4,20},{5,21},{6,22},{7,23},{8,24},{9,... | collective-permute-start | bytes 1327112 | tf_op jit(solution)/shard_map/ppermute | solution.py:910
  379.2 17.3 %copy-start.10 = (f32[1,288,768]{2,1,0:T(8,128)S(1)}, f32[1,288,768]{2,1,0:T(8,128)}, u32[]{:S(2)}) copy-start(f32[1,288,768]{2,1,0:T(8,128)} %get-tuple-element.160) | copy-start | bytes 2654212
  389.1 18.5 %collective-permute-start.21 = (bf16[320,768]{1,0:T(8,128)(2,1)S(1)}, bf16[320,768]{1,0:T(8,128)(2,1)S(1)}, u32[]{:S(2)}, u32[]{:S(2)}) collective-permute-start(bf16[320,768]{1,0:T(8,128)(2,1)S(1)} %get-tuple-element.159), channel_id=1, source_target_pairs={{8,24},{9,25},{10,26},{11,27},{12,28},{13,29},{14,30},{15,31},{16,... | collective-permute-start | bytes 1474568 | tf_op jit(solution)/shard_map/ppermute | solution.py:910
  407.6 0.8 copy-start.11
  408.4 4.8 %copy-start.6 = (f32[1024,768]{1,0:T(8,128)S(1)}, f32[1024,768]{1,0:T(8,128)}, u32[]{:S(2)}) copy-start(f32[1024,768]{1,0:T(8,128)} %get-tuple-element.145) | copy-start | bytes 9437188
  408.4 4.8 %copy-start.9 = (f32[1024,768]{1,0:T(8,128)S(1)}, f32[1024,768]{1,0:T(8,128)}, u32[]{:S(2)}) copy-start(f32[1024,768]{1,0:T(8,128)} %get-tuple-element.106) | copy-start | bytes 9437188
  408.4 4.8 %copy-start.14 = (f32[1024]{0:T(1024)S(1)}, f32[1024]{0:T(1024)}, u32[]{:S(2)}) copy-start(f32[1024]{0:T(1024)} %broadcast_multiply_fusion) | copy-start | bytes 12292
  411.9 5.4 %collective-permute-start.23 = (f32[16,768]{1,0:T(8,128)S(1)}, f32[16,768]{1,0:T(8,128)S(1)}, u32[]{:S(2)}, u32[]{:S(2)}) collective-permute-start(f32[16,768]{1,0:T(8,128)S(1)} %slice.48), channel_id=1, source_target_pairs={{1,0},{2,1},{3,2},{4,3},{5,4},{6,5},{7,6},{8,7},{9,8},{10,9},{11,1... | collective-permute-start | bytes 147464 | tf_op jit(solution)/shard_map/ppermute | solution.py:890
  417.3 1.2 copy-start.7
  417.3 1.2 copy-start.13

commit v10 on v9

--- a/solution.py
+++ b/solution.py
@@ -12,7 +12,8 @@
 SEQ_MIN = 1024
 AXES = ("dp", "ctx")
 QB = 256
-PARTS = 3
+FORWARD_PARTS = ((0, 2), (2, 2), (4, 2))
+BACKWARD_PARTS = ((0, 1), (1, 2), (3, 1), (4, 2))
 F32 = jnp.float32
 BF = jnp.bfloat16
 NT = (((1,), (1,)), ((), ()))
@@ -123,7 +124,7 @@
 
     return pl.pallas_call(
         kernel,
-        grid=(6 // PARTS,),
+        grid=(part[1],),
         in_specs=in_specs + [pl.BlockSpec(memory_space=pl.ANY)] * len(earlier),
         out_specs=out_specs,
         out_shape=out_shape,
@@ -134,7 +135,7 @@
 
 
 def columns(part):
-    first = part * (6 // PARTS)
+    first = part[0]
 
     def cols(height, row, off):
         return pl.BlockSpec((height, 128), lambda p: (row, p + first + off))
@@ -169,9 +170,9 @@
         part,
         scratch_shapes=[pltpu.VMEM((2, 2 * rows, 128), BF)] * 2,
         cost_estimate=cost(
-            2 * 2 * 12 * rows * rows * 1.5 * 256 / PARTS,
-            rows * D * 30 / PARTS,
-            12 * rows * rows * 1.5 / PARTS,
+            2 * 2 * 2 * rows * rows * 1.5 * 256 * part[1],
+            rows * D * 5 * part[1],
+            2 * rows * rows * 1.5 * part[1],
         ),
         name="att_fwd",
     )(state, projected, projected, projected, projected, taps, taps, taps, *earlier)
@@ -337,9 +338,9 @@
             pltpu.VMEM((2 * rows, 128), F32),
         ],
         cost_estimate=cost(
-            5 * 2 * 12 * rows * rows * 1.5 * 256 / PARTS,
-            rows * D * 40 / PARTS,
-            12 * rows * rows * 1.5 / PARTS,
+            5 * 2 * 2 * rows * rows * 1.5 * 256 * part[1],
+            rows * D * 7 * part[1],
+            2 * rows * rows * 1.5 * part[1],
         ),
         name="att_bwd",
     )(state, *mixed, attended, logs, grad, projected, projected, projected, projected,
@@ -1067,17 +1068,17 @@
 
     forward = []
     if staged:
-        forward = att_fwd(after(state_vec, rest), projected, taps, forward, 0, rows)
+        forward = att_fwd(after(state_vec, rest), projected, taps, forward, FORWARD_PARTS[0], rows)
         rest = join_held(after(rest, forward[0]), across)
         line = swap(rest, 4, 2)
         core_rest = swap(rest, 1, 1)
-        forward = att_fwd(after(state_vec, rest), projected, taps, forward, 1, rows)
-        forward = att_fwd(after(state_vec, core_rest), projected, taps, forward, 2, rows)
+        forward = att_fwd(after(state_vec, rest), projected, taps, forward, FORWARD_PARTS[1], rows)
+        forward = att_fwd(after(state_vec, core_rest), projected, taps, forward, FORWARD_PARTS[2], rows)
         line = hold(line, forward[0])
         core_line = swap(line, 1, 1)
         late_weights = [w.reshape(18, 4, 24, D) for w in (rest, line, core_rest, core_line)]
     else:
-        for part in range(PARTS):
+        for part in FORWARD_PARTS:
             forward = att_fwd(state_vec, projected, taps, forward, part, rows)
         grouped = jnp.concatenate(
             [
@@ -1096,7 +1097,7 @@
 
     def backward(start, done, part):
         return att_bwd(
-            start, mixed, attn_low, logs, grad_attended, projected, taps, done, part, rows
+            start, mixed, attn_low, logs, grad_attended, projected, taps, done, BACKWARD_PARTS[part], rows
         )
 
     if staged:
@@ -1130,10 +1131,15 @@
         pick_z = jnp.stack(low_pair + high_pair).astype(jnp.int32)
         late_send, late_keep = merge_grid(after(pick_z, done[4]), late_keep, late_got, 2)
         late_got = swap(late_send, 8, 8)
+        done = backward(after(state_vec, late_send), done, 3)
+        high = z >> 1
+        pick_last = jnp.stack([1 - high, high]).astype(jnp.int32)
+        late_send, late_keep = merge_grid(after(pick_last, done[4]), late_keep, late_got, 1)
+        late_got = swap(late_send, 16, 16, (0, 1, 3))
         sums_state = after(core, late_send)
     else:
         done = []
-        for part in range(PARTS):
+        for part in range(4):
             done = backward(state_vec, done, part)
         sums_state = core
     *back, tap_grads = done
@@ -1151,23 +1157,18 @@
 
     if staged:
         send, keep = sums[:2]
-        high = z >> 1
-        pick_last = jnp.stack([1 - high, high]).astype(jnp.int32)
-        late_send, late_keep = merge_grid(after(pick_last, send), late_keep, late_got, 1)
-        late_got = swap(late_send, 16, 16, (0, 1, 3))
-        got = swap(after(send, late_send, from_next), 1, 1)
+        got = swap(after(send, late_got, from_next), 1, 1)
         send, keep = merge(pick_plane, keep, got, height + 16, 2)
         got = swap(send, 2, 4)
-        send, keep = merge(pick_line, keep, got, height + 16, 1)
-        got = swap(send, 4, 2)
-        send, keep = merge(core, keep, got, height + 16, 0)
-        got = swap(send, 8, 8)
-        late_got = after(late_got, got)
-        send, keep = merge(core, keep, got, height + 16, 0)
         late_chunk = late_keep[0] + late_got[0].astype(F32)
         late_chunk = jnp.where(in_up, ungroup(late_chunk).reshape(3, 4, 24, D), late_chunk.reshape(3, 4, 24, D))
         late_chunk = late_chunk.reshape(-1, D)
         late_next = shift_flat(late_chunk[:16], -1)
+        send, keep = merge(after(pick_line, late_next), keep, got, height + 16, 1)
+        got = swap(send, 4, 2)
+        send, keep = merge(after(core, input_grad), keep, got, height + 16, 0)
+        got = swap(send, 8, 8)
+        send, keep = merge(core, keep, got, height + 16, 0)
         got = swap(send, 16, 16, (1, 2))
         first = keep + got.astype(F32)
         quarter = count // 4

time: 428 us -> 425 us (level)
  other arithmetic: 19.8 us -> 15 us
    pallas_call x3 -> x4, Pallas kernels: 48.7 us -> 50.8 us  [att_bwd(): call_in_parts(att_bwd_kernel, [pl.BlockSpec(memory_space=pltpu.SMEM), own...]
  transfers between devices with their start and end apart: 24 -> 24, of which waited for: 15 -> 14; matrix products, arithmetic and copies ran while one was open for 6% -> 5% of each run, Pallas kernels for 34% -> 34%
where the time goes in v10:
time: 425 us; the launch traced here: 420 us
  Pallas kernels  208 us (49%)
  waiting for transfers between devices  118 us (28%)
  starting transfers between devices  55.9 us (13%)
  local copies, waits for them, and re-layouts  19.4 us (5%)
  other arithmetic  15 us (4%)
    ppermute x20, waiting for transfers between devices, swap(): return lax.ppermute(block, AXES, route)  117 us
    pallas_call x4, Pallas kernels, att_bwd(): call_in_parts(att_bwd_kernel, [pl.BlockSpec(memory_space=pltpu.SMEM), own...  50.8 us
    pallas_call x3, Pallas kernels, att_fwd(): call_in_parts(att_fwd_kernel, [pl.BlockSpec(memory_space=pltpu.SMEM), col...  49.8 us
    pallas_call x1, Pallas kernels, ffn(): pl.pallas_call(ffn_kernel, grid=(4,), in_specs=[scalars, scalars, act, ac...  46.7 us
    ppermute x20, starting transfers between devices, swap(): return lax.ppermute(block, AXES, route)  45.3 us
    pallas_call x1, Pallas kernels, qkv_bwd(): pl.pallas_call(body, grid=(blocks,), in_specs=[pl.BlockSpec(memory_space=...  19.3 us
    pallas_call x4, Pallas kernels, merge_grid(): pl.pallas_call(body, grid_spec=pltpu.PrefetchScalarGridSpec(num_scalar_pr...  14.8 us
    pallas_call x1, Pallas kernels, qkv_fwd(): pl.pallas_call(body, grid=(blocks,), in_specs=[pl.BlockSpec(memory_space=...  13.2 us
  transfers between devices with their start and end apart: 24, of which 14 were waited for; matrix products, arithmetic and copies ran while one was open for 5% of the time, Pallas kernels for 34%

profile of v10, /device:TPU:0, one launch (start us, length us, event | category | flops | bytes accessed | tf_op | source)
XLA Modules:
  0.0 420.0 jit_solution(2854419223483552362)
XLA Ops:
  1.5 2.3 collective-permute-start
  3.8 2.3 concatenate.22
  6.3 1.5 fusion.8
  8.8 5.7 %collective-permute-start.1 = (bf16[1024,768]{1,0:T(8,128)(2,1)S(1)}, bf16[1024,768]{1,0:T(8,128)(2,1)}, u32[]{:S(2)}, u32[]{:S(2)}) collective-permute-start(bf16[1024,768]{1,0:T(8,128)(2,1)S(1)} %copy-done.4), channel_id=1, source_target_pairs={{0,1},{1,2},{2,3},{4,5},{5,6},{6,7},{8,9},{9,10},{10,11},{12,13},{... | collective-permute-start | bytes 4718600 | tf_op jit(solution)/shard_map/ppermute | solution.py:897
  14.5 2.8 collective-permute-start.2
  19.0 18.6 %collective-permute-done.2 = bf16[304,768]{1,0:T(8,128)(2,1)S(1)} collective-permute-done((bf16[304,768]{1,0:T(8,128)(2,1)S(1)}, bf16[304,768]{1,0:T(8,128)(2,1)S(1)}, u32[]{:S(2)}, u32[]{:S(2)}) %collective-permute-start.2) | collective-permute-done | bytes 466976 | tf_op jit(solution)/shard_map/ppermute | solution.py:911
  38.4 10.9 %collective-permute-done.3 = bf16[304,768]{1,0:T(8,128)(2,1)S(1)} collective-permute-done((bf16[304,768]{1,0:T(8,128)(2,1)S(1)}, bf16[304,768]{1,0:T(8,128)(2,1)S(1)}, u32[]{:S(2)}, u32[]{:S(2)}) %collective-permute-start.3) | collective-permute-done | bytes 466976 | tf_op jit(solution)/shard_map/ppermute | solution.py:911
  49.7 8.3 %collective-permute-done.4.got_ref = bf16[304,768]{1,0:T(8,128)(2,1)S(1)} collective-permute-done((bf16[304,768]{1,0:T(8,128)(2,1)S(1)}, bf16[304,768]{1,0:T(8,128)(2,1)S(1)}, u32[]{:S(2)}, u32[]{:S(2)}) %collective-permute-start.4) | collective-permute-done | bytes 466976 | tf_op jit(solution)/shard_map/ppermute | solution.py:911
  58.1 1.6 collective-permute-start.5
  59.7 11.8 %collective-permute-done.5.got_ref = bf16[592,768]{1,0:T(8,128)(2,1)S(1)} collective-permute-done((bf16[592,768]{1,0:T(8,128)(2,1)S(1)}, bf16[592,768]{1,0:T(8,128)(2,1)S(1)}, u32[]{:S(2)}, u32[]{:S(2)}) %collective-permute-start.5) | collective-permute-done | bytes 909344 | tf_op jit(solution)/shard_map/ppermute | solution.py:911
  72.9 1.8 collective-permute-start.7
  76.9 13.2 %qkv_fwd.1 = (bf16[2048,2304]{1,0:T(8,128)(2,1)}, f32[16,768]{1,0:T(8,128)}, bf16[2304,768]{1,0:T(8,128)(2,1)}) custom-call(s32[8]{0:T(128)} %stack.213.refs_0_, bf16[2048,768]{1,0:T(8,128)(2,1)} %copy-done.10, bf16[1168,768]{1,0:T(8,128)(2,1)} %join.3.refs_2_, bf16[1168,768]{1,0:T(8,128)(2,1)} %collective-permute-done.6.refs_3_), custom_call_target="tpu_custom_call" | custom-call | flops 7247757312 | bytes 15728640 | tf_op jit(solution)/shard_map/qkv_fwd/pallas_call | solution.py:694
  90.2 4.9 %collective-permute-done.7 = bf16[576,768]{1,0:T(8,128)(2,1)S(1)} collective-permute-done((bf16[576,768]{1,0:T(8,128)(2,1)S(1)}, bf16[576,768]{1,0:T(8,128)(2,1)S(1)}, u32[]{:S(2)}, u32[]{:S(2)}) %collective-permute-start.7) | collective-permute-done | bytes 884768 | tf_op jit(solution)/shard_map/ppermute | solution.py:911
  99.4 16.3 %att_fwd.3 = (bf16[1024,768]{1,0:T(8,128)(2,1)}, f32[1024,768]{1,0:T(8,128)}, bf16[1024,768]{1,0:T(8,128)(2,1)}, bf16[2048,768]{1,0:T(8,128)(2,1)}, bf16[2048,768]{1,0:T(8,128)(2,1)}) custom-call(s32[1]{0:T(128)S(6)} %select_n.155.refs_0_.state_ref, bf16[2048,2304]{1,0:T(8,128)(2,1)} %get-tuple-element.93.refs_1_.refs_2_.refs_3_.refs_4_.refs_7_.refs_8_.refs_9_.refs_10_, ...), custom_call_target="tpu_custom_call" | custom-call | flops 6442450944 | bytes 7864320 | tf_op jit(solution)/shard_map/att_fwd/pallas_call | solution.py:151
  118.3 16.5 %att_fwd.4 = (bf16[1024,768]{1,0:T(8,128)(2,1)}, f32[1024,768]{1,0:T(8,128)}, bf16[1024,768]{1,0:T(8,128)(2,1)}, bf16[2048,768]{1,0:T(8,128)(2,1)}, bf16[2048,768]{1,0:T(8,128)(2,1)}) custom-call(s32[1]{0:T(128)S(6)} %select_n.155.refs_0_.state_ref, ...), custom_call_target="tpu_custom_call", output_to_operand_aliasing={{0}: (8, {}), {1}: (9, {}), {2}: (10, {}), {3}: (11, {}), {... | custom-call | flops 6442450944 | bytes 7864320 | tf_op jit(solution)/shard_map/att_fwd/pallas_call | solution.py:151
  134.8 17.0 %att_fwd.5 = (bf16[1024,768]{1,0:T(8,128)(2,1)}, f32[1024,768]{1,0:T(8,128)}, bf16[1024,768]{1,0:T(8,128)(2,1)}, bf16[2048,768]{1,0:T(8,128)(2,1)}, bf16[2048,768]{1,0:T(8,128)(2,1)}) custom-call(s32[1]{0:T(128)S(6)} %select_n.155.refs_0_.state_ref, ...), custom_call_target="tpu_custom_call", output_to_operand_aliasing={{0}: (8, {}), {1}: (9, {}), {2}: (10, {}), {3}: (11, {}), {... | custom-call | flops 6442450944 | bytes 7864320 | tf_op jit(solution)/shard_map/att_fwd/pallas_call | solution.py:151
  153.6 3.6 collective-permute-done.11
  157.2 1.6 copy-done.20
  158.7 46.7 %ffn.1 = (bf16[1024,768]{1,0:T(8,128)(2,1)}, f32[1024,768]{1,0:T(8,128)}, bf16[1024,768]{1,0:T(8,128)(2,1)}, f32[1,768]{1,0:T(1,128)}, bf16[36,4,24,768]{3,2,1,0...) custom-call(s32[1]{0:T(128)S(6)} %select_n.155.refs_0_.state_ref, s32[25]{0:T(128)} %stack.208.index_ref, ...), custom_call_target="tpu_custom_call" | custom-call | flops 32614907904 | bytes 40894464 | tf_op jit(solution)/shard_map/ffn/pallas_call | solution.py:854
  206.3 9.3 %att_bwd.4 = (bf16[1024,768]{1,0:T(8,128)(2,1)}, bf16[8,768]{1,0:T(8,128)(2,1)}, bf16[2048,768]{1,0:T(8,128)(2,1)}, bf16[2048,768]{1,0:T(8,128)(2,1)}, f32[16,768]{1,0:T(8,128)}) custom-call(s32[1]{0:T(128)S(6)} %select_n.155.refs_0_.state_ref, bf16[1024,768]{1,0:T(8,128)(2,1)} %get-tuple-element.114.refs_1_, bf16[2048,768]{1,0:T(8,128)(2,1)} %get-tuple-element.115.refs_2_, ...), custom_call_target="tpu_custom_call" | custom-call | flops 8053063680 | bytes 5505024 | tf_op jit(solution)/shard_map/att_bwd/pallas_call | solution.py:308
  215.7 7.9 %merge_grid.4 = (bf16[6,288,768]{2,1,0:T(8,128)(2,1)}, f32[6,288,768]{2,1,0:T(8,128)}) custom-call(s32[12]{0:T(128)S(1)} %stack.239.index_ref, bf16[12,288,768]{2,1,0:T(8,128)(2,1)S(1)} %bitcast.76, bf16[12,288,768]{2,1,0:T(8,128)(2,1)} %collective-permute-done.12.ga_ref.gb_ref, bf16[12,288,768]{2,1,0:T(8,128)(2,1)S(1)} %bitcast.77, ...), custom_call_target="tpu_custom_call" | custom-call | flops 2654208 | bytes 21233664 | tf_op jit(solution)/shard_map/merge_grid/pallas_call | solution.py:544
  223.6 1.8 collective-permute-start.13
  225.5 16.1 %att_bwd.5 = (bf16[1024,768]{1,0:T(8,128)(2,1)}, bf16[8,768]{1,0:T(8,128)(2,1)}, bf16[2048,768]{1,0:T(8,128)(2,1)}, bf16[2048,768]{1,0:T(8,128)(2,1)}, f32[16,768]{1,0:T(8,128)}) custom-call(s32[1]{0:T(128)S(6)} %select_n.155.refs_0_.state_ref, ...), custom_call_target="tpu_custom_call", output_to_operand_aliasing={{0}: (14, {}), {1}: (15, {}), {2}: (16, {}), {3}: (17, {}),... | custom-call | flops 16106127360 | bytes 11010048 | tf_op jit(solution)/shard_map/att_bwd/pallas_call | solution.py:308
  241.5 14.2 %collective-permute-done.13.ga_ref.gb_ref = bf16[6,288,768]{2,1,0:T(8,128)(2,1)S(1)} collective-permute-done((bf16[6,288,768]{2,1,0:T(8,128)(2,1)}, bf16[6,288,768]{2,1,0:T(8,128)(2,1)S(1)}, u32[]{:S(2)}, u32[]{:S(2)}) %collective-permute-start.13) | collective-permute-done | bytes 2654240 | tf_op jit(solution)/shard_map/ppermute | solution.py:911
  255.8 3.0 merge_grid.5
  258.8 2.4 collective-permute-start.14
  261.2 9.5 %att_bwd.6 = (bf16[1024,768]{1,0:T(8,128)(2,1)}, bf16[8,768]{1,0:T(8,128)(2,1)}, bf16[2048,768]{1,0:T(8,128)(2,1)}, bf16[2048,768]{1,0:T(8,128)(2,1)}, f32[16,768]{1,0:T(8,128)}) custom-call(s32[1]{0:T(128)S(6)} %select_n.155.refs_0_.state_ref, ...), custom_call_target="tpu_custom_call", output_to_operand_aliasing={{0}: (14, {}), {1}: (15, {}), {2}: (16, {}), {3}: (17, {}),... | custom-call | flops 8053063680 | bytes 5505024 | tf_op jit(solution)/shard_map/att_bwd/pallas_call | solution.py:308
  270.7 6.4 %collective-permute-done.14.ga_ref.gb_ref = bf16[3,288,768]{2,1,0:T(8,128)(2,1)S(1)} collective-permute-done((bf16[3,288,768]{2,1,0:T(8,128)(2,1)}, bf16[3,288,768]{2,1,0:T(8,128)(2,1)S(1)}, u32[]{:S(2)}, u32[]{:S(2)}) %collective-permute-start.14) | collective-permute-done | bytes 1327136 | tf_op jit(solution)/shard_map/ppermute | solution.py:911
  277.1 2.2 merge_grid.6
  279.3 6.7 %collective-permute-start.15 = (bf16[2,288,768]{2,1,0:T(8,128)(2,1)}, bf16[2,288,768]{2,1,0:T(8,128)(2,1)S(1)}, u32[]{:S(2)}, u32[]{:S(2)}) collective-permute-start(bf16[2,288,768]{2,1,0:T(8,128)(2,1)} %get-tuple-element.141), channel_id=1, source_target_pairs={{0,8},{1,9},{2,10},{3,11},{4,12},{5,13},{6,14},{7,15},{8,0},{9,1},... | collective-permute-start | bytes 2654216 | tf_op jit(solution)/shard_map/ppermute | solution.py:911
  285.9 15.9 %att_bwd.7 = (bf16[1024,768]{1,0:T(8,128)(2,1)}, bf16[8,768]{1,0:T(8,128)(2,1)}, bf16[2048,768]{1,0:T(8,128)(2,1)}, bf16[2048,768]{1,0:T(8,128)(2,1)}, f32[16,768]{1,0:T(8,128)}) custom-call(s32[1]{0:T(128)S(6)} %select_n.155.refs_0_.state_ref, ...), custom_call_target="tpu_custom_call", output_to_operand_aliasing={{0}: (14, {}), {1}: (15, {}), {2}: (16, {}), {3}: (17, {}),... | custom-call | flops 16106127360 | bytes 11010048 | tf_op jit(solution)/shard_map/att_bwd/pallas_call | solution.py:308
  301.8 8.1 %before_bwd.1 = (bf16[1024,768]{1,0:T(8,128)(2,1)}, f32[1,768]{1,0:T(1,128)}) custom-call(bf16[2048,768]{1,0:T(8,128)(2,1)} %copy-done.10, bf16[8,768]{1,0:T(8,128)(2,1)} %get-tuple-element.152.dt_ref.refs_3_, bf16[2048,768]{1,0:T(8,128)(2,1)} %get-tuple-element.153.dk_ref.refs_4_, bf16[2048,768]{1,0:T(8,128)(2,1)} %get-tuple-element.154.dv_ref.refs_5_, ...), custom_call_target="tpu_custom_call" | custom-call | flops 2415919104 | bytes 9437184 | tf_op jit(solution)/shard_map/before_bwd/pallas_call | solution.py:387
  311.3 1.7 merge_grid.7
  313.0 2.8 collective-permute-start.17
  315.8 19.3 %qkv_bwd.1 = (bf16[1232,768]{1,0:T(8,128)(2,1)}, f32[1232,768]{1,0:T(8,128)}, f32[1024,768]{1,0:T(8,128)}) custom-call(s32[1]{0:T(128)} %bitcast.24.refs_0_.index_ref, bf16[2048,768]{1,0:T(8,128)(2,1)} %copy-done.10, bf16[1024,768]{1,0:T(8,128)(2,1)} %get-tuple-element.158.refs_2_, bf16[8,768]{1,0:T(8,128)(2,1)} %get-tuple-element.152.dt_ref.refs_3_, ...), custom_call_target="tpu_custom_call" | custom-call | flops 9663676416 | bytes 23592960 | tf_op jit(solution)/shard_map/qkv_bwd/pallas_call | solution.py:482
  335.9 12.4 %collective-permute-start.19 = (bf16[1232,768]{1,0:T(8,128)(2,1)}, bf16[1232,768]{1,0:T(8,128)(2,1)S(1)}, u32[]{:S(2)}, u32[]{:S(2)}) collective-permute-start(bf16[1232,768]{1,0:T(8,128)(2,1)} %get-tuple-element.167), channel_id=1, source_target_pairs={{0,1},{1,0},{2,3},{3,2},{4,5},{5,4},{6,7},{7,6},{8,9},{9,8},{10,11... | collective-permute-start | bytes 5677064 | tf_op jit(solution)/shard_map/ppermute | solution.py:911
  352.4 2.4 reshape.131
  354.8 2.1 copy-done.2
  357.8 2.0 collective-permute-start.20
  361.3 1.7 collective-permute-done.18
  363.1 2.6 fusion.2
  365.8 6.0 %collective-permute-done.20.got_ref = bf16[624,768]{1,0:T(8,128)(2,1)S(1)} collective-permute-done((bf16[624,768]{1,0:T(8,128)(2,1)S(1)}, bf16[624,768]{1,0:T(8,128)(2,1)S(1)}, u32[]{:S(2)}, u32[]{:S(2)}) %collective-permute-start.20) | collective-permute-done | bytes 958496 | tf_op jit(solution)/shard_map/ppermute | solution.py:911
  372.5 5.5 %collective-permute-start.21 = (bf16[320,768]{1,0:T(8,128)(2,1)S(1)}, bf16[320,768]{1,0:T(8,128)(2,1)S(1)}, u32[]{:S(2)}, u32[]{:S(2)}) collective-permute-start(bf16[320,768]{1,0:T(8,128)(2,1)S(1)} %get-tuple-element.171), channel_id=1, source_target_pairs={{0,4},{1,3},{2,6},{3,1},{4,0},{5,7},{6,2},{7,5},{8,12},{9,11},{10,... | collective-permute-start | bytes 1474568 | tf_op jit(solution)/shard_map/ppermute | solution.py:911
  378.0 4.1 fusion.5
  382.1 2.7 collective-permute-done.21.got_ref
  385.0 14.0 %collective-permute-done.22.got_ref = bf16[320,768]{1,0:T(8,128)(2,1)S(1)} collective-permute-done((bf16[320,768]{1,0:T(8,128)(2,1)S(1)}, bf16[320,768]{1,0:T(8,128)(2,1)S(1)}, u32[]{:S(2)}, u32[]{:S(2)}) %collective-permute-start.22) | collective-permute-done | bytes 491552 | tf_op jit(solution)/shard_map/ppermute | solution.py:911
  401.1 13.9 %collective-permute-done.23 = bf16[320,768]{1,0:T(8,128)(2,1)S(1)} collective-permute-done((bf16[320,768]{1,0:T(8,128)(2,1)S(1)}, bf16[320,768]{1,0:T(8,128)(2,1)S(1)}, u32[]{:S(2)}, u32[]{:S(2)}) %collective-permute-start.23) | collective-permute-done | bytes 491552 | tf_op jit(solution)/shard_map/ppermute | solution.py:911
  416.3 3.5 fusion.17
  (127 shorter events, 29.2 us)
Async XLA Ops:
  1.5 4.8 %collective-permute-start = (bf16[96,128]{1,0:T(8,128)(2,1)S(1)}, bf16[96,128]{1,0:T(8,128)(2,1)S(1)}, u32[]{:S(2)}, u32[]{:S(2)}) collective-permute-start(bf16[96,128]{1,0:T(8,128)(2,1)S(1)} %slice.35), channel_id=1, source_target_pairs={{0,1},{1,2},{2,3},{3,4},{4,5},{5,6},{6,7},{7,8},{8,9},{9,10},{10,1... | collective-permute-start | bytes 73736 | tf_op jit(solution)/shard_map/ppermute | solution.py:891
  6.2 2.6 copy-start.17
  6.3 2.6 copy-start.4
  8.8 8.5 %collective-permute-start.1 = (bf16[1024,768]{1,0:T(8,128)(2,1)S(1)}, bf16[1024,768]{1,0:T(8,128)(2,1)}, u32[]{:S(2)}, u32[]{:S(2)}) collective-permute-start(bf16[1024,768]{1,0:T(8,128)(2,1)S(1)} %copy-done.4), channel_id=1, source_target_pairs={{0,1},{1,2},{2,3},{4,5},{5,6},{6,7},{8,9},{9,10},{10,11},{12,13},{... | collective-permute-start | bytes 4718600 | tf_op jit(solution)/shard_map/ppermute | solution.py:897
  14.5 23.0 %collective-permute-start.2 = (bf16[304,768]{1,0:T(8,128)(2,1)S(1)}, bf16[304,768]{1,0:T(8,128)(2,1)S(1)}, u32[]{:S(2)}, u32[]{:S(2)}) collective-permute-start(bf16[304,768]{1,0:T(8,128)(2,1)S(1)} %pad_maximum_fusion.2), channel_id=1, source_target_pairs={{0,16},{1,17},{2,18},{3,19},{4,20},{5,21},{6,22},{7,23},{8,24},{9,... | collective-permute-start | bytes 1400840 | tf_op jit(solution)/shard_map/ppermute | solution.py:911
  18.9 30.8 %copy-start.10 = (bf16[2048,768]{1,0:T(8,128)(2,1)}, bf16[2048,768]{1,0:T(8,128)(2,1)S(1)}, u32[]{:S(2)}) copy-start(bf16[2048,768]{1,0:T(8,128)(2,1)S(1)} %constant_dynamic-update-slice_fusion.refs_1_.x_ref) | copy-start | bytes 9437188
  37.7 11.6 %collective-permute-start.3 = (bf16[304,768]{1,0:T(8,128)(2,1)S(1)}, bf16[304,768]{1,0:T(8,128)(2,1)S(1)}, u32[]{:S(2)}, u32[]{:S(2)}) collective-permute-start(bf16[304,768]{1,0:T(8,128)(2,1)S(1)} %pad_maximum_fusion.3), channel_id=1, source_target_pairs={{0,8},{1,9},{2,10},{3,11},{4,12},{5,13},{6,14},{7,15},{8,0},{9,1},... | collective-permute-start | bytes 1400840 | tf_op jit(solution)/shard_map/ppermute | solution.py:911
  49.4 8.6 %collective-permute-start.4 = (bf16[304,768]{1,0:T(8,128)(2,1)S(1)}, bf16[304,768]{1,0:T(8,128)(2,1)S(1)}, u32[]{:S(2)}, u32[]{:S(2)}) collective-permute-start(bf16[304,768]{1,0:T(8,128)(2,1)S(1)} %fusion.16.own_ref), channel_id=1, source_target_pairs={{0,2},{1,5},{2,0},{3,7},{4,6},{5,1},{6,4},{7,3},{8,10},{9,13},{10,... | collective-permute-start | bytes 1400840 | tf_op jit(solution)/shard_map/ppermute | solution.py:911
  58.1 13.4 %collective-permute-start.5 = (bf16[592,768]{1,0:T(8,128)(2,1)S(1)}, bf16[592,768]{1,0:T(8,128)(2,1)S(1)}, u32[]{:S(2)}, u32[]{:S(2)}) collective-permute-start(bf16[592,768]{1,0:T(8,128)(2,1)S(1)} %join.2.own_ref), channel_id=1, source_target_pairs={{0,4},{1,3},{2,6},{3,1},{4,0},{5,7},{6,2},{7,5},{8,12},{9,11},{10,... | collective-permute-start | bytes 2727944 | tf_op jit(solution)/shard_map/ppermute | solution.py:911
  72.8 4.1 collective-permute-start.6
  72.9 22.1 %collective-permute-start.7 = (bf16[576,768]{1,0:T(8,128)(2,1)S(1)}, bf16[576,768]{1,0:T(8,128)(2,1)S(1)}, u32[]{:S(2)}, u32[]{:S(2)}) collective-permute-start(bf16[576,768]{1,0:T(8,128)(2,1)S(1)} %pad_maximum_fusion.1), channel_id=1, source_target_pairs={{0,8},{1,9},{2,10},{3,11},{4,12},{5,13},{6,14},{7,15},{8,0},{9,1},... | collective-permute-start | bytes 2654216 | tf_op jit(solution)/shard_map/ppermute | solution.py:911
  90.2 8.6 %copy-start.16 = (f32[16,768]{1,0:T(8,128)S(1)}, f32[16,768]{1,0:T(8,128)}, u32[]{:S(2)}) copy-start(f32[16,768]{1,0:T(8,128)} %get-tuple-element.97) | copy-start | bytes 147460
  95.9 19.7 %collective-permute-start.8 = (bf16[864,768]{1,0:T(8,128)(2,1)S(1)}, bf16[864,768]{1,0:T(8,128)(2,1)S(1)}, u32[]{:S(2)}, u32[]{:S(2)}) collective-permute-start(bf16[864,768]{1,0:T(8,128)(2,1)S(1)} %bitcast.78), channel_id=1, source_target_pairs={{0,2},{1,5},{2,0},{3,7},{4,6},{5,1},{6,4},{7,3},{8,10},{9,13},{10,... | collective-permute-start | bytes 3981320 | tf_op jit(solution)/shard_map/ppermute | solution.py:911
  116.6 18.1 %copy-start.3 = (bf16[1728,768]{1,0:T(8,128)(2,1)}, bf16[1728,768]{1,0:T(8,128)(2,1)S(1)}, u32[]{:S(2)}) copy-start(bf16[1728,768]{1,0:T(8,128)(2,1)S(1)} %join_held.1) | copy-start | bytes 7962628
  116.6 18.1 %collective-permute-start.9 = (bf16[1728,768]{1,0:T(8,128)(2,1)S(1)}, bf16[1728,768]{1,0:T(8,128)(2,1)S(1)}, u32[]{:S(2)}, u32[]{:S(2)}) collective-permute-start(bf16[1728,768]{1,0:T(8,128)(2,1)S(1)} %join_held.1), channel_id=1, source_target_pairs={{0,1},{1,0},{2,3},{3,2},{4,5},{5,4},{6,7},{7,6},{8,9},{9,8},{10,11... | collective-permute-start | bytes 7962632 | tf_op jit(solution)/shard_map/ppermute | solution.py:911
  117.4 34.4 %collective-permute-start.10 = (bf16[1728,768]{1,0:T(8,128)(2,1)S(1)}, bf16[1728,768]{1,0:T(8,128)(2,1)}, u32[]{:S(2)}, u32[]{:S(2)}) collective-permute-start(bf16[1728,768]{1,0:T(8,128)(2,1)S(1)} %join_held.1), channel_id=1, source_target_pairs={{0,4},{1,3},{2,6},{3,1},{4,0},{5,7},{6,2},{7,5},{8,12},{9,11},{10,... | collective-permute-start | bytes 7962632 | tf_op jit(solution)/shard_map/ppermute | solution.py:911
  134.8 17.1 %copy-start.19 = (bf16[1728,768]{1,0:T(8,128)(2,1)}, bf16[1728,768]{1,0:T(8,128)(2,1)S(1)}, u32[]{:S(2)}) copy-start(bf16[1728,768]{1,0:T(8,128)(2,1)S(1)} %collective-permute-done.9) | copy-start | bytes 7962628
  151.9 5.3 %collective-permute-start.11 = (bf16[1728,768]{1,0:T(8,128)(2,1)}, bf16[1728,768]{1,0:T(8,128)(2,1)S(1)}, u32[]{:S(2)}, u32[]{:S(2)}) collective-permute-start(bf16[1728,768]{1,0:T(8,128)(2,1)} %hold.1), channel_id=1, source_target_pairs={{0,1},{1,0},{2,3},{3,2},{4,5},{5,4},{6,7},{7,6},{8,9},{9,8},{10,11... | collective-permute-start | bytes 7962632 | tf_op jit(solution)/shard_map/ppermute | solution.py:911
  157.1 1.6 copy-start.20
  205.4 10.2 %collective-permute-start.12 = (bf16[12,288,768]{2,1,0:T(8,128)(2,1)}, bf16[12,288,768]{2,1,0:T(8,128)(2,1)}, u32[]{:S(2)}, u32[]{:S(2)}) collective-permute-start(bf16[12,288,768]{2,1,0:T(8,128)(2,1)} %bitcast.86), channel_id=1, source_target_pairs={{0,1},{1,0},{2,3},{3,2},{4,5},{5,4},{6,7},{7,6},{8,9},{9,8},{10,11... | collective-permute-start | bytes 15925256 | tf_op jit(solution)/shard_map/ppermute | solution.py:911
  206.3 9.3 %slice-start.2 = ((s8[5308416]{0:T(1024)(128)(4,1)}), s8[4194304]{0:T(1024)(128)(4,1)S(1)}, s32[]{:S(2)}) async-start(s8[5308416]{0:T(1024)(128)(4,1)} %bitcast.74), calls=%async_computation.2 | async-start | bytes 8388608
  206.3 9.3 %slice-start.3 = ((s8[5308416]{0:T(1024)(128)(4,1)}), s8[1114112]{0:T(1024)(128)(4,1)S(1)}, s32[]{:S(2)}) async-start(s8[5308416]{0:T(1024)(128)(4,1)} %bitcast.74), calls=%async_computation.3 | async-start | bytes 2228224
  223.6 32.2 %collective-permute-start.13 = (bf16[6,288,768]{2,1,0:T(8,128)(2,1)}, bf16[6,288,768]{2,1,0:T(8,128)(2,1)S(1)}, u32[]{:S(2)}, u32[]{:S(2)}) collective-permute-start(bf16[6,288,768]{2,1,0:T(8,128)(2,1)} %get-tuple-element.123), channel_id=1, source_target_pairs={{0,2},{1,5},{2,0},{3,7},{4,6},{5,1},{6,4},{7,3},{8,10},{9,13},{10,... | collective-permute-start | bytes 7962632 | tf_op jit(solution)/shard_map/ppermute | solution.py:911
  225.5 30.3 %slice-start = ((s8[5308416]{0:T(1024)(128)(4,1)}), s8[4194304]{0:T(1024)(128)(4,1)S(1)}, s32[]{:S(2)}) async-start(s8[5308416]{0:T(1024)(128)(4,1)} %bitcast.72), calls=%async_computation | async-start | bytes 8388608
  225.5 30.3 %slice-start.1 = ((s8[5308416]{0:T(1024)(128)(4,1)}), s8[1114112]{0:T(1024)(128)(4,1)S(1)}, s32[]{:S(2)}) async-start(s8[5308416]{0:T(1024)(128)(4,1)} %bitcast.72), calls=%async_computation.1 | async-start | bytes 2228224
  258.8 18.3 %collective-permute-start.14 = (bf16[3,288,768]{2,1,0:T(8,128)(2,1)}, bf16[3,288,768]{2,1,0:T(8,128)(2,1)S(1)}, u32[]{:S(2)}, u32[]{:S(2)}) collective-permute-start(bf16[3,288,768]{2,1,0:T(8,128)(2,1)} %get-tuple-element.132), channel_id=1, source_target_pairs={{0,4},{1,3},{2,6},{3,1},{4,0},{5,7},{6,2},{7,5},{8,12},{9,11},{10,... | collective-permute-start | bytes 3981320 | tf_op jit(solution)/shard_map/ppermute | solution.py:911
  261.2 15.9 %copy-start = (f32[3,288,768]{2,1,0:T(8,128)S(1)}, f32[3,288,768]{2,1,0:T(8,128)}, u32[]{:S(2)}) copy-start(f32[3,288,768]{2,1,0:T(8,128)} %get-tuple-element.140.ka_ref.kb_ref) | copy-start | bytes 7962628
  279.3 32.0 %collective-permute-start.15 = (bf16[2,288,768]{2,1,0:T(8,128)(2,1)}, bf16[2,288,768]{2,1,0:T(8,128)(2,1)S(1)}, u32[]{:S(2)}, u32[]{:S(2)}) collective-permute-start(bf16[2,288,768]{2,1,0:T(8,128)(2,1)} %get-tuple-element.141), channel_id=1, source_target_pairs={{0,8},{1,9},{2,10},{3,11},{4,12},{5,13},{6,14},{7,15},{8,0},{9,1},... | collective-permute-start | bytes 2654216 | tf_op jit(solution)/shard_map/ppermute | solution.py:911
  301.8 9.4 %copy-start.1 = (f32[2,288,768]{2,1,0:T(8,128)S(1)}, f32[2,288,768]{2,1,0:T(8,128)}, u32[]{:S(2)}) copy-start(f32[2,288,768]{2,1,0:T(8,128)} %get-tuple-element.149.ka_ref.kb_ref) | copy-start | bytes 5308420
  309.9 25.2 %collective-permute-start.16 = (bf16[1024,768]{1,0:T(8,128)(2,1)}, bf16[1024,768]{1,0:T(8,128)(2,1)}, u32[]{:S(2)}, u32[]{:S(2)}) collective-permute-start(bf16[1024,768]{1,0:T(8,128)(2,1)} %get-tuple-element.156), channel_id=1, source_target_pairs={{1,0},{2,1},{3,2},{5,4},{6,5},{7,6},{9,8},{10,9},{11,10},{13,12},{... | collective-permute-start | bytes 4718600 | tf_op jit(solution)/shard_map/ppermute | solution.py:897
  313.0 22.1 %collective-permute-start.17 = (bf16[1,288,768]{2,1,0:T(8,128)(2,1)}, bf16[1,288,768]{2,1,0:T(8,128)(2,1)S(1)}, u32[]{:S(2)}, u32[]{:S(2)}) collective-permute-start(bf16[1,288,768]{2,1,0:T(8,128)(2,1)} %get-tuple-element.150), channel_id=1, source_target_pairs={{0,16},{1,17},{2,18},{3,19},{4,20},{5,21},{6,22},{7,23},{8,24},{9,... | collective-permute-start | bytes 1327112 | tf_op jit(solution)/shard_map/ppermute | solution.py:911
  315.8 32.5 %copy-start.18 = (pred[3]{0:T(512)(128)(4,1)S(1)}, pred[3]{0:T(512)(128)(4,1)}, u32[]{:S(2)}) copy-start(pred[3]{0:T(512)(128)(4,1)} %copy-done.17) | copy-start | bytes 13
  315.8 32.7 %copy-start.5 = (bf16[1024,768]{1,0:T(8,128)(2,1)S(1)}, bf16[1024,768]{1,0:T(8,128)(2,1)}, u32[]{:S(2)}) copy-start(bf16[1024,768]{1,0:T(8,128)(2,1)} %x_ref.1) | copy-start | bytes 4718596
  335.9 19.0 %collective-permute-start.19 = (bf16[1232,768]{1,0:T(8,128)(2,1)}, bf16[1232,768]{1,0:T(8,128)(2,1)S(1)}, u32[]{:S(2)}, u32[]{:S(2)}) collective-permute-start(bf16[1232,768]{1,0:T(8,128)(2,1)} %get-tuple-element.167), channel_id=1, source_target_pairs={{0,1},{1,0},{2,3},{3,2},{4,5},{5,4},{6,7},{7,6},{8,9},{9,8},{10,11... | collective-permute-start | bytes 5677064 | tf_op jit(solution)/shard_map/ppermute | solution.py:911
  350.3 0.9 copy-start.8
  354.8 2.1 copy-start.2
  356.9 2.9 copy-start.9
  356.9 2.9 copy-start.13
  356.9 6.2 %copy-start.6 = (f32[1024,768]{1,0:T(8,128)S(1)}, f32[1024,768]{1,0:T(8,128)}, u32[]{:S(2)}) copy-start(f32[1024,768]{1,0:T(8,128)} %get-tuple-element.161) | copy-start | bytes 9437188
  357.8 13.9 %collective-permute-start.20 = (bf16[624,768]{1,0:T(8,128)(2,1)S(1)}, bf16[624,768]{1,0:T(8,128)(2,1)S(1)}, u32[]{:S(2)}, u32[]{:S(2)}) collective-permute-start(bf16[624,768]{1,0:T(8,128)(2,1)S(1)} %get-tuple-element.169), channel_id=1, source_target_pairs={{0,2},{1,5},{2,0},{3,7},{4,6},{5,1},{6,4},{7,3},{8,10},{9,13},{10,... | collective-permute-start | bytes 2875400 | tf_op jit(solution)/shard_map/ppermute | solution.py:911
  359.9 5.8 %copy-start.11 = (f32[288,768]{1,0:T(8,128)}, f32[288,768]{1,0:T(8,128)S(1)}, u32[]{:S(2)}) copy-start(f32[288,768]{1,0:T(8,128)S(1)} %bitcast_select_fusion) | copy-start | bytes 2654212
  360.0 3.1 collective-permute-start.18
  363.1 14.9 %copy-start.14 = (f32[1024,768]{1,0:T(8,128)S(1)}, f32[1024,768]{1,0:T(8,128)}, u32[]{:S(2)}) copy-start(f32[1024,768]{1,0:T(8,128)} %get-tuple-element.113) | copy-start | bytes 9437188
  372.5 12.3 %collective-permute-start.21 = (bf16[320,768]{1,0:T(8,128)(2,1)S(1)}, bf16[320,768]{1,0:T(8,128)(2,1)S(1)}, u32[]{:S(2)}, u32[]{:S(2)}) collective-permute-start(bf16[320,768]{1,0:T(8,128)(2,1)S(1)} %get-tuple-element.171), channel_id=1, source_target_pairs={{0,4},{1,3},{2,6},{3,1},{4,0},{5,7},{6,2},{7,5},{8,12},{9,11},{10,... | collective-permute-start | bytes 1474568 | tf_op jit(solution)/shard_map/ppermute | solution.py:911
  382.1 33.0 %copy-start.12 = (f32[288,768]{1,0:T(8,128)S(1)}, f32[288,768]{1,0:T(8,128)}, u32[]{:S(2)}) copy-start(f32[288,768]{1,0:T(8,128)} %copy-done.11) | copy-start | bytes 2654212
  384.9 14.1 %collective-permute-start.22 = (bf16[320,768]{1,0:T(8,128)(2,1)S(1)}, bf16[320,768]{1,0:T(8,128)(2,1)S(1)}, u32[]{:S(2)}, u32[]{:S(2)}) collective-permute-start(bf16[320,768]{1,0:T(8,128)(2,1)S(1)} %get-tuple-element.173), channel_id=1, source_target_pairs={{0,8},{1,9},{2,10},{3,11},{4,12},{5,13},{6,14},{7,15},{8,0},{9,1},... | collective-permute-start | bytes 1474568 | tf_op jit(solution)/shard_map/ppermute | solution.py:911
  399.1 15.9 %collective-permute-start.23 = (bf16[320,768]{1,0:T(8,128)(2,1)S(1)}, bf16[320,768]{1,0:T(8,128)(2,1)S(1)}, u32[]{:S(2)}, u32[]{:S(2)}) collective-permute-start(bf16[320,768]{1,0:T(8,128)(2,1)S(1)} %get-tuple-element.175), channel_id=1, source_target_pairs={{8,24},{9,25},{10,26},{11,27},{12,28},{13,29},{14,30},{15,31},{16,... | collective-permute-start | bytes 1474568 | tf_op jit(solution)/shard_map/ppermute | solution.py:911
  415.1 1.2 copy-start.7
  (1 other events, 0.8 us)

commit v11 on v10

--- a/solution.py
+++ b/solution.py
@@ -36,6 +36,10 @@
 
 def cost(flops, nbytes, exps=0):
     return pl.CostEstimate(flops=int(flops), bytes_accessed=int(nbytes), transcendentals=int(exps))
+
+
+def taps_of(small, matrix):
+    return [small[2 + 3 * j + matrix : 3 + 3 * j + matrix, :] for j in range(3)]
 
 
 def row_ids(height):
@@ -64,21 +68,21 @@
             row = row_ids(QB)
             one = jnp.where(row < 1, one * seen, one)
             two = jnp.where(row < 2, two * seen, two)
-        c_one = taps[1:2] * scale
-        c_two = taps[2:3] * scale
-        out_ref[r : r + QB, :] = (taps[0:1] * x + c_one * one + c_two * two).astype(BF)
+        c_one = taps[1] * scale
+        c_two = taps[2] * scale
+        out_ref[r : r + QB, :] = (taps[0] * x + c_one * one + c_two * two).astype(BF)
 
 
 def att_fwd_kernel(
-    state_ref, tail_ref, q_ref, k_ref, v_ref, tq_ref, tk_ref, tv_ref,
+    state_ref, tail_ref, q_ref, k_ref, v_ref, small_ref,
     o_ref, l_ref, qm_ref, km_ref, vm_ref, ka, va,
 ):
     rows = q_ref.shape[0]
     lane = lax.broadcasted_iota(jnp.int32, (1, 128), 1)
     state = state_ref[0]
-    conv(qm_ref, q_ref, rows, tail_ref, tq_ref[...], rows, state)
-    conv(km_ref, k_ref, 0, None, tk_ref[...], rows, state)
-    conv(vm_ref, v_ref, 0, None, tv_ref[...], rows, state)
+    conv(qm_ref, q_ref, rows, tail_ref, taps_of(small_ref[...], 0), rows, state)
+    conv(km_ref, k_ref, 0, None, taps_of(small_ref[...], 1), rows, state)
+    conv(vm_ref, v_ref, 0, None, taps_of(small_ref[...], 2), rows, state)
     bias = jnp.where(state == 2, 0.0, -1e30)
     for h in range(2):
         mine = (lane < 64) if h == 0 else (lane >= 64)
@@ -140,14 +144,11 @@
     def cols(height, row, off):
         return pl.BlockSpec((height, 128), lambda p: (row, p + first + off))
 
-    taps_at = [
-        pl.BlockSpec((3, 128), lambda p, off=off: (0, p + first + off)) for off in (0, 6, 12)
-    ]
-    return cols, taps_at
-
-
-def att_fwd(state, projected, taps, earlier, part, rows):
-    cols, taps_at = columns(part)
+    return cols
+
+
+def att_fwd(state, projected, small, earlier, part, rows):
+    cols = columns(part)
     return call_in_parts(
         att_fwd_kernel,
         [
@@ -156,7 +157,7 @@
             cols(rows, 1, 0),
             cols(2 * rows, 0, 6),
             cols(2 * rows, 0, 12),
-            *taps_at,
+            cols(16, 0, 0),
         ],
         [cols(rows, 0, 0)] * 3 + [cols(2 * rows, 0, 0)] * 2,
         [
@@ -175,7 +176,7 @@
             2 * rows * rows * 1.5 * part[1],
         ),
         name="att_fwd",
-    )(state, projected, projected, projected, projected, taps, taps, taps, *earlier)
+    )(state, projected, projected, projected, projected, small, *earlier)
 
 
 def three(x, lane, base):
@@ -210,20 +211,20 @@
             row = row_ids(QB)
             one = jnp.where(row >= QB - 1, one * joint, one)
             two = jnp.where(row >= QB - 2, two * joint, two)
-        out_ref[r : r + QB, :] = (taps[0:1] * grad + taps[1:2] * one + taps[2:3] * two).astype(BF)
+        out_ref[r : r + QB, :] = (taps[0] * grad + taps[1] * one + taps[2] * two).astype(BF)
         sums = add((grad, one, two), x_ref[r : r + QB, :].astype(F32))
     if tail is not None:
         grad = jnp.concatenate([jnp.zeros((8, 128), F32), grad_ref[0:8, :]], 0)
         one = pltpu.roll(grad, 15, 0)[:8] * joint
         two = pltpu.roll(grad, 14, 0)[:8] * joint
-        tail[0][...] = (taps[1:2] * one + taps[2:3] * two).astype(BF)
+        tail[0][...] = (taps[1] * one + taps[2] * two).astype(BF)
         sums = add((grad[:8], one, two), tail[1][...].astype(F32))
     return sums
 
 
 def att_bwd_kernel(
     state_ref, q_ref, k_ref, v_ref, o_ref, l_ref, do_ref, xt_ref, xq_ref, xk_ref, xv_ref,
-    tq_ref, tk_ref, tv_ref,
+    small_ref,
     pq_ref, pt_ref, pk_ref, pv_ref, tg_ref, qa, da, qt, dt, kt, dqt, dqs, dks, dvs,
 ):
     rows = q_ref.shape[0]
@@ -292,17 +293,17 @@
     for r in range(0, rows, QB):
         dqs[r : r + QB, :] = jnp.transpose(dqt[:, r : r + QB]) * 0.125
     state = state_ref[0]
-    sq = conv_back(pq_ref, dqs, xq_ref, rows, (pt_ref, xt_ref), tq_ref[...], rows, state)
-    sk = conv_back(pk_ref, dks, xk_ref, 0, None, tk_ref[...], rows, state)
-    sv = conv_back(pv_ref, dvs, xv_ref, 0, None, tv_ref[...], rows, state)
+    sq = conv_back(pq_ref, dqs, xq_ref, rows, (pt_ref, xt_ref), taps_of(small_ref[...], 0), rows, state)
+    sk = conv_back(pk_ref, dks, xk_ref, 0, None, taps_of(small_ref[...], 1), rows, state)
+    sv = conv_back(pv_ref, dvs, xv_ref, 0, None, taps_of(small_ref[...], 2), rows, state)
     tg_ref[...] = jnp.zeros(tg_ref.shape, F32)
     for j in range(3):
         for m, s in enumerate((sq, sk, sv)):
             tg_ref[3 * j + m : 3 * j + m + 1, :] = s[j]
 
 
-def att_bwd(state, mixed, attended, logs, grad, projected, taps, earlier, part, rows):
-    cols, taps_at = columns(part)
+def att_bwd(state, mixed, attended, logs, grad, projected, small, earlier, part, rows):
+    cols = columns(part)
     own = cols(rows, 0, 0)
     both = cols(2 * rows, 0, 0)
     return call_in_parts(
@@ -314,7 +315,7 @@
             cols(rows, 1, 0),
             cols(2 * rows, 0, 6),
             cols(2 * rows, 0, 12),
-            *taps_at,
+            cols(16, 0, 0),
         ],
         [own, cols(8, 0, 0), both, both, cols(16, 0, 0)],
         [
@@ -344,7 +345,7 @@
         ),
         name="att_bwd",
     )(state, *mixed, attended, logs, grad, projected, projected, projected, projected,
-      taps, taps, taps, *earlier)
+      small, *earlier)
 
 
 def unit_rows(x):
@@ -531,12 +532,12 @@
     )(index, keep, got)
 
 
-def merge_grid(index, keep, got, taken):
+def merge_grid(index, keep, got, taken, kept=F32):
     height = keep.shape[1]
 
     def body(index_ref, ka_ref, ga_ref, kb_ref, gb_ref, send_ref, stay_ref):
         send_ref[...] = (ka_ref[...].astype(F32) + ga_ref[...].astype(F32)).astype(BF)
-        stay_ref[...] = kb_ref[...].astype(F32) + gb_ref[...].astype(F32)
+        stay_ref[...] = (kb_ref[...].astype(F32) + gb_ref[...].astype(F32)).astype(kept)
 
     away = pl.BlockSpec((1, height, D), lambda i, index: (index[i], 0, 0))
     here = pl.BlockSpec((1, height, D), lambda i, index: (index[taken + i], 0, 0))
@@ -551,7 +552,7 @@
         ),
         out_shape=[
             pltpu.HBM((taken, height, D), BF),
-            pltpu.HBM((taken, height, D), F32),
+            pltpu.HBM((taken, height, D), kept),
         ],
         compiler_params=pltpu.CompilerParams(vmem_limit_bytes=32 << 20),
         cost_estimate=cost(taken * height * D * 2, taken * height * D * 16),
@@ -780,9 +781,14 @@
 
     @pl.when(c == 0)
     def _():
-        for k in range(2):
-            for j in range(12):
-                fetch(k, j).start()
+        for early in (True, False):
+            for k in range(2):
+                for j in range(12):
+
+                    @pl.when((index_ref[12 * k + j] < 3) == early)
+                    def _():
+                        fetch(k, j).start()
+
         cot[...] = jnp.where(state_ref[0] > 0, cot_ref[...], jnp.zeros((), BF))
         total[...] = jnp.zeros(total.shape, F32)
         back[...] = jnp.zeros(back.shape, F32)
@@ -1034,6 +1040,12 @@
         across = swap(after(rest, mine), 8, 8)
         mine = join(mine, swap(mine, 2, 4))
         mine = join(mine, swap(mine, 4, 2))
+        codes = [z ^ k for k in (1, 2, 3)]
+        order = [jnp.where(j == 1, 2, jnp.where(j == 2, 1, j)) for j in codes]
+        rest = arrange(
+            jnp.stack(order).astype(jnp.int32), rest.reshape(2, height, D), across.reshape(2, height, D), 3
+        ).reshape(-1, D)
+        across = swap(rest, 2, 4)
         got = swap(mine, 1, 1)
         index = []
         late_index = []
@@ -1048,13 +1060,7 @@
                 late_index += [piece, piece + 8, piece + 16]
         index = jnp.stack(index).astype(jnp.int32)
         late_index = jnp.stack(late_index + [core[0]]).astype(jnp.int32)
-        projected, small, in_weight = qkv_fwd(index, tokens_both, (mine, got), rows, 4)
-        codes = [z ^ k for k in (1, 2, 3)]
-        order = [jnp.where(j == 1, 2, jnp.where(j == 2, 1, j)) for j in codes]
-        rest = arrange(
-            after(jnp.stack(order).astype(jnp.int32), projected), rest.reshape(2, height, D), across.reshape(2, height, D), 3
-        ).reshape(-1, D)
-        across = swap(rest, 2, 4)
+        projected, small, in_weight = qkv_fwd(after(index, rest), tokens_both, (mine, got), rows, 4)
     else:
         tokens_both = jnp.concatenate([shift_ctx(tokens, 1), tokens], 0)
         wide = lax.all_gather(chunk, AXES, axis=0, tiled=True)
@@ -1064,22 +1070,21 @@
         late_index = jnp.arange(25, dtype=jnp.int32) % 24
     gain_first = small[0]
     gain_second = small[1]
-    taps = small[2:11].reshape(3, 3 * D)
 
     forward = []
     if staged:
-        forward = att_fwd(after(state_vec, rest), projected, taps, forward, FORWARD_PARTS[0], rows)
-        rest = join_held(after(rest, forward[0]), across)
+        rest = join_held(after(rest, projected), across)
         line = swap(rest, 4, 2)
         core_rest = swap(rest, 1, 1)
-        forward = att_fwd(after(state_vec, rest), projected, taps, forward, FORWARD_PARTS[1], rows)
-        forward = att_fwd(after(state_vec, core_rest), projected, taps, forward, FORWARD_PARTS[2], rows)
+        forward = att_fwd(after(state_vec, rest), projected, small, forward, FORWARD_PARTS[0], rows)
+        forward = att_fwd(after(state_vec, core_rest), projected, small, forward, FORWARD_PARTS[1], rows)
         line = hold(line, forward[0])
         core_line = swap(line, 1, 1)
+        forward = att_fwd(after(state_vec, line), projected, small, forward, FORWARD_PARTS[2], rows)
         late_weights = [w.reshape(18, 4, 24, D) for w in (rest, line, core_rest, core_line)]
     else:
         for part in FORWARD_PARTS:
-            forward = att_fwd(state_vec, projected, taps, forward, part, rows)
+            forward = att_fwd(state_vec, projected, small, forward, part, rows)
         grouped = jnp.concatenate(
             [
                 wide[3 * D : 4 * D].reshape(-1, 4, 24, D),
@@ -1097,7 +1102,7 @@
 
     def backward(start, done, part):
         return att_bwd(
-            start, mixed, attn_low, logs, grad_attended, projected, taps, done, BACKWARD_PARTS[part], rows
+            start, mixed, attn_low, logs, grad_attended, projected, small, done, BACKWARD_PARTS[part], rows
         )
 
     if staged:
@@ -1116,7 +1121,7 @@
         late_got = swap(away_grad.reshape(12, height, D), 1, 1)
         done = backward(state_vec, [], 0)
         late_send, late_keep = merge_grid(
-            after(of_quarters(pick_plane, 4), done[4]), late_keep, late_got, 6
+            after(of_quarters(pick_plane, 4), done[4]), late_keep, late_got, 6, BF
         )
         late_got = swap(late_send, 2, 4)
         done = backward(after(state_vec, late_send), done, 1)
@@ -1160,15 +1165,16 @@
         got = swap(after(send, late_got, from_next), 1, 1)
         send, keep = merge(pick_plane, keep, got, height + 16, 2)
         got = swap(send, 2, 4)
+        late_got = after(late_got, send)
         late_chunk = late_keep[0] + late_got[0].astype(F32)
         late_chunk = jnp.where(in_up, ungroup(late_chunk).reshape(3, 4, 24, D), late_chunk.reshape(3, 4, 24, D))
         late_chunk = late_chunk.reshape(-1, D)
         late_next = shift_flat(late_chunk[:16], -1)
-        send, keep = merge(after(pick_line, late_next), keep, got, height + 16, 1)
+        send, keep = merge(pick_line, keep, got, height + 16, 1)
         got = swap(send, 4, 2)
+        send, keep = merge(after(core, late_next), keep, got, height + 16, 0)
+        got = swap(send, 8, 8)
         send, keep = merge(after(core, input_grad), keep, got, height + 16, 0)
-        got = swap(send, 8, 8)
-        send, keep = merge(core, keep, got, height + 16, 0)
         got = swap(send, 16, 16, (1, 2))
         first = keep + got.astype(F32)
         quarter = count // 4

time: 425 us -> 430 us (1.012); the launches traced: 420 us -> 430 us
  waiting for transfers between devices: 118 us -> 128 us
  Pallas kernels: 208 us -> 216 us
  starting transfers between devices: 55.9 us -> 48.1 us
    ppermute x20, waiting for transfers between devices: 117 us -> 126 us  [swap(): return lax.ppermute(block, AXES, route)]
    pallas_call x1, Pallas kernels: 46.7 us -> 55.2 us  [ffn(): pl.pallas_call(ffn_kernel, grid=(4,), in_specs=[scalars, scalars, act, ac...]
    ppermute x20, starting transfers between devices: 45.3 us -> 37.4 us  [swap(): return lax.ppermute(block, AXES, route)]
  transfers between devices with their start and end apart: 24 -> 24, of which waited for: 14 -> 14; matrix products, arithmetic and copies ran while one was open for 5% -> 5% of each run, Pallas kernels for 34% -> 33%
where the time goes in v11:
time: 430 us
  Pallas kernels  216 us (50%)
  waiting for transfers between devices  128 us (30%)
  starting transfers between devices  48.1 us (11%)
  local copies, waits for them, and re-layouts  18.8 us (4%)
  other arithmetic  15.9 us (4%)
    ppermute x20, waiting for transfers between devices, swap(): return lax.ppermute(block, AXES, route)  126 us
    pallas_call x1, Pallas kernels, ffn(): pl.pallas_call(ffn_kernel, grid=(4,), in_specs=[scalars, scalars, act, ac...  55.2 us
    pallas_call x4, Pallas kernels, att_bwd(): call_in_parts(att_bwd_kernel, [pl.BlockSpec(memory_space=pltpu.SMEM), own...  50.2 us
    pallas_call x3, Pallas kernels, att_fwd(): call_in_parts(att_fwd_kernel, [pl.BlockSpec(memory_space=pltpu.SMEM), col...  49.3 us
    ppermute x20, starting transfers between devices, swap(): return lax.ppermute(block, AXES, route)  37.4 us
    pallas_call x1, Pallas kernels, qkv_bwd(): pl.pallas_call(body, grid=(blocks,), in_specs=[pl.BlockSpec(memory_space=...  19.3 us
    pallas_call x4, Pallas kernels, merge_grid(): pl.pallas_call(body, grid_spec=pltpu.PrefetchScalarGridSpec(num_scalar_pr...  14.2 us
    pallas_call x1, Pallas kernels, qkv_fwd(): pl.pallas_call(body, grid=(blocks,), in_specs=[pl.BlockSpec(memory_space=...  13.3 us
  transfers between devices with their start and end apart: 24, of which 14 were waited for; matrix products, arithmetic and copies ran while one was open for 5% of the time, Pallas kernels for 33%

profile of v11, /device:TPU:0, one launch (start us, length us, event | category | flops | bytes accessed | tf_op | source)
XLA Modules:
  0.0 430.0 jit_solution(2763843296878296314)
XLA Ops:
  1.5 2.3 collective-permute-start
  3.8 2.3 concatenate.22
  6.3 1.5 fusion.8
  8.8 5.7 %collective-permute-start.2 = (bf16[1024,768]{1,0:T(8,128)(2,1)S(1)}, bf16[1024,768]{1,0:T(8,128)(2,1)}, u32[]{:S(2)}, u32[]{:S(2)}) collective-permute-start(bf16[1024,768]{1,0:T(8,128)(2,1)S(1)} %copy-done.5), channel_id=1, source_target_pairs={{0,1},{1,2},{2,3},{4,5},{5,6},{6,7},{8,9},{9,10},{10,11},{12,13},{... | collective-permute-start | bytes 4718600 | tf_op jit(solution)/shard_map/ppermute | solution.py:903
  14.5 2.8 collective-permute-start.1
  19.0 18.6 %collective-permute-done.1 = bf16[304,768]{1,0:T(8,128)(2,1)S(1)} collective-permute-done((bf16[304,768]{1,0:T(8,128)(2,1)S(1)}, bf16[304,768]{1,0:T(8,128)(2,1)S(1)}, u32[]{:S(2)}, u32[]{:S(2)}) %collective-permute-start.1) | collective-permute-done | bytes 466976 | tf_op jit(solution)/shard_map/ppermute | solution.py:917
  38.4 10.9 %collective-permute-done.3 = bf16[304,768]{1,0:T(8,128)(2,1)S(1)} collective-permute-done((bf16[304,768]{1,0:T(8,128)(2,1)S(1)}, bf16[304,768]{1,0:T(8,128)(2,1)S(1)}, u32[]{:S(2)}, u32[]{:S(2)}) %collective-permute-start.3) | collective-permute-done | bytes 466976 | tf_op jit(solution)/shard_map/ppermute | solution.py:917
  49.7 8.3 %collective-permute-done.5.got_ref = bf16[304,768]{1,0:T(8,128)(2,1)S(1)} collective-permute-done((bf16[304,768]{1,0:T(8,128)(2,1)S(1)}, bf16[304,768]{1,0:T(8,128)(2,1)S(1)}, u32[]{:S(2)}, u32[]{:S(2)}) %collective-permute-start.5) | collective-permute-done | bytes 466976 | tf_op jit(solution)/shard_map/ppermute | solution.py:917
  58.1 1.6 collective-permute-start.6
  59.7 11.8 %collective-permute-done.6.got_ref = bf16[592,768]{1,0:T(8,128)(2,1)S(1)} collective-permute-done((bf16[592,768]{1,0:T(8,128)(2,1)S(1)}, bf16[592,768]{1,0:T(8,128)(2,1)S(1)}, u32[]{:S(2)}, u32[]{:S(2)}) %collective-permute-start.6) | collective-permute-done | bytes 909344 | tf_op jit(solution)/shard_map/ppermute | solution.py:917
  72.9 1.8 collective-permute-start.4
  74.8 20.2 %collective-permute-done.4 = bf16[576,768]{1,0:T(8,128)(2,1)S(1)} collective-permute-done((bf16[576,768]{1,0:T(8,128)(2,1)S(1)}, bf16[576,768]{1,0:T(8,128)(2,1)S(1)}, u32[]{:S(2)}, u32[]{:S(2)}) %collective-permute-start.4) | collective-permute-done | bytes 884768 | tf_op jit(solution)/shard_map/ppermute | solution.py:917
  96.8 13.3 %qkv_fwd.1 = (bf16[2048,2304]{1,0:T(8,128)(2,1)}, f32[16,768]{1,0:T(8,128)}, bf16[2304,768]{1,0:T(8,128)(2,1)}) custom-call(s32[8]{0:T(128)} %stack.213.refs_0_, bf16[2048,768]{1,0:T(8,128)(2,1)} %copy-done.12, bf16[1168,768]{1,0:T(8,128)(2,1)} %join.3.refs_2_, bf16[1168,768]{1,0:T(8,128)(2,1)} %collective-permute-done.7.refs_3_), custom_call_target="tpu_custom_call" | custom-call | flops 7247757312 | bytes 15728640 | tf_op jit(solution)/shard_map/qkv_fwd/pallas_call | solution.py:695
  110.1 3.7 collective-permute-done.8.got_ref
  114.8 1.6 collective-permute-start.9
  118.9 16.1 %att_fwd.3 = (bf16[1024,768]{1,0:T(8,128)(2,1)}, f32[1024,768]{1,0:T(8,128)}, bf16[1024,768]{1,0:T(8,128)(2,1)}, bf16[2048,768]{1,0:T(8,128)(2,1)}, bf16[2048,768]{1,0:T(8,128)(2,1)}) custom-call(s32[1]{0:T(128)S(6)} %select_n.155.refs_0_.state_ref, bf16[2048,2304]{1,0:T(8,128)(2,1)} %get-tuple-element.96.refs_1_.refs_2_.refs_3_.refs_4_.refs_7_.refs_8_.refs_9_.refs_10_, ...), custom_call_target="tpu_custom_call" | custom-call | flops 6442450944 | bytes 7864320 | tf_op jit(solution)/shard_map/att_fwd/pallas_call | solution.py:152
  135.0 17.1 %att_fwd.4 = (bf16[1024,768]{1,0:T(8,128)(2,1)}, f32[1024,768]{1,0:T(8,128)}, bf16[1024,768]{1,0:T(8,128)(2,1)}, bf16[2048,768]{1,0:T(8,128)(2,1)}, bf16[2048,768]{1,0:T(8,128)(2,1)}) custom-call(s32[1]{0:T(128)S(6)} %select_n.155.refs_0_.state_ref, ...), custom_call_target="tpu_custom_call", output_to_operand_aliasing={{0}: (6, {}), {1}: (7, {}), {2}: (8, {}), {3}: (9, {}), {4}... | custom-call | flops 6442450944 | bytes 7864320 | tf_op jit(solution)/shard_map/att_fwd/pallas_call | solution.py:152
  154.3 16.1 %att_fwd.5 = (bf16[1024,768]{1,0:T(8,128)(2,1)}, f32[1024,768]{1,0:T(8,128)}, bf16[1024,768]{1,0:T(8,128)(2,1)}, bf16[2048,768]{1,0:T(8,128)(2,1)}, bf16[2048,768]{1,0:T(8,128)(2,1)}) custom-call(s32[1]{0:T(128)S(6)} %select_n.155.refs_0_.state_ref, ...), custom_call_target="tpu_custom_call", output_to_operand_aliasing={{0}: (6, {}), {1}: (7, {}), {2}: (8, {}), {3}: (9, {}), {4}... | custom-call | flops 6442450944 | bytes 7864320 | tf_op jit(solution)/shard_map/att_fwd/pallas_call | solution.py:152
  172.0 55.2 %ffn.1 = (bf16[1024,768]{1,0:T(8,128)(2,1)}, f32[1024,768]{1,0:T(8,128)}, bf16[1024,768]{1,0:T(8,128)(2,1)}, f32[1,768]{1,0:T(1,128)}, bf16[36,4,24,768]{3,2,1,0...) custom-call(s32[1]{0:T(128)S(6)} %select_n.155.refs_0_.state_ref, s32[25]{0:T(128)} %stack.208.index_ref, ...), custom_call_target="tpu_custom_call" | custom-call | flops 32614907904 | bytes 40894464 | tf_op jit(solution)/shard_map/ffn/pallas_call | solution.py:860
  227.8 9.3 %att_bwd.4 = (bf16[1024,768]{1,0:T(8,128)(2,1)}, bf16[8,768]{1,0:T(8,128)(2,1)}, bf16[2048,768]{1,0:T(8,128)(2,1)}, bf16[2048,768]{1,0:T(8,128)(2,1)}, f32[16,768]{1,0:T(8,128)}) custom-call(s32[1]{0:T(128)S(6)} %select_n.155.refs_0_.state_ref, bf16[1024,768]{1,0:T(8,128)(2,1)} %get-tuple-element.115.refs_1_, bf16[2048,768]{1,0:T(8,128)(2,1)} %get-tuple-element.116.refs_2_, ...), custom_call_target="tpu_custom_call" | custom-call | flops 8053063680 | bytes 5505024 | tf_op jit(solution)/shard_map/att_bwd/pallas_call | solution.py:309
  237.2 7.4 %merge_grid.4 = (bf16[6,288,768]{2,1,0:T(8,128)(2,1)}, bf16[6,288,768]{2,1,0:T(8,128)(2,1)}) custom-call(s32[12]{0:T(128)S(1)} %stack.239.index_ref, bf16[12,288,768]{2,1,0:T(8,128)(2,1)S(1)} %bitcast.74, bf16[12,288,768]{2,1,0:T(8,128)(2,1)} %collective-permute-done.12.ga_ref.gb_ref, bf16[12,288,768]{2,1,0:T(8,128)(2,1)S(1)} %bitcast.75, ...), custom_call_target="tpu_custom_call" | custom-call | flops 2654208 | bytes 21233664 | tf_op jit(solution)/shard_map/merge_grid/pallas_call | solution.py:545
  244.6 5.8 %collective-permute-start.13 = (bf16[6,288,768]{2,1,0:T(8,128)(2,1)}, bf16[6,288,768]{2,1,0:T(8,128)(2,1)S(1)}, u32[]{:S(2)}, u32[]{:S(2)}) collective-permute-start(bf16[6,288,768]{2,1,0:T(8,128)(2,1)} %get-tuple-element.124), channel_id=1, source_target_pairs={{0,2},{1,5},{2,0},{3,7},{4,6},{5,1},{6,4},{7,3},{8,10},{9,13},{10,... | collective-permute-start | bytes 7962632 | tf_op jit(solution)/shard_map/ppermute | solution.py:917
  250.4 15.8 %att_bwd.5 = (bf16[1024,768]{1,0:T(8,128)(2,1)}, bf16[8,768]{1,0:T(8,128)(2,1)}, bf16[2048,768]{1,0:T(8,128)(2,1)}, bf16[2048,768]{1,0:T(8,128)(2,1)}, f32[16,768]{1,0:T(8,128)}) custom-call(s32[1]{0:T(128)S(6)} %select_n.155.refs_0_.state_ref, ...), custom_call_target="tpu_custom_call", output_to_operand_aliasing={{0}: (12, {}), {1}: (13, {}), {2}: (14, {}), {3}: (15, {}),... | custom-call | flops 16106127360 | bytes 11010048 | tf_op jit(solution)/shard_map/att_bwd/pallas_call | solution.py:309
  266.2 14.3 %collective-permute-done.13.ga_ref.gb_ref = bf16[6,288,768]{2,1,0:T(8,128)(2,1)S(1)} collective-permute-done((bf16[6,288,768]{2,1,0:T(8,128)(2,1)}, bf16[6,288,768]{2,1,0:T(8,128)(2,1)S(1)}, u32[]{:S(2)}, u32[]{:S(2)}) %collective-permute-start.13) | collective-permute-done | bytes 2654240 | tf_op jit(solution)/shard_map/ppermute | solution.py:917
  280.5 2.9 merge_grid.5
  283.6 9.5 %att_bwd.6 = (bf16[1024,768]{1,0:T(8,128)(2,1)}, bf16[8,768]{1,0:T(8,128)(2,1)}, bf16[2048,768]{1,0:T(8,128)(2,1)}, bf16[2048,768]{1,0:T(8,128)(2,1)}, f32[16,768]{1,0:T(8,128)}) custom-call(s32[1]{0:T(128)S(6)} %select_n.155.refs_0_.state_ref, ...), custom_call_target="tpu_custom_call", output_to_operand_aliasing={{0}: (12, {}), {1}: (13, {}), {2}: (14, {}), {3}: (15, {}),... | custom-call | flops 8053063680 | bytes 5505024 | tf_op jit(solution)/shard_map/att_bwd/pallas_call | solution.py:309
  293.1 8.4 %collective-permute-done.14.ga_ref.gb_ref = bf16[3,288,768]{2,1,0:T(8,128)(2,1)S(1)} collective-permute-done((bf16[3,288,768]{2,1,0:T(8,128)(2,1)}, bf16[3,288,768]{2,1,0:T(8,128)(2,1)S(1)}, u32[]{:S(2)}, u32[]{:S(2)}) %collective-permute-start.14) | collective-permute-done | bytes 1327136 | tf_op jit(solution)/shard_map/ppermute | solution.py:917
  301.5 2.2 merge_grid.6
  304.9 15.6 %att_bwd.7 = (bf16[1024,768]{1,0:T(8,128)(2,1)}, bf16[8,768]{1,0:T(8,128)(2,1)}, bf16[2048,768]{1,0:T(8,128)(2,1)}, bf16[2048,768]{1,0:T(8,128)(2,1)}, f32[16,768]{1,0:T(8,128)}) custom-call(s32[1]{0:T(128)S(6)} %select_n.155.refs_0_.state_ref, ...), custom_call_target="tpu_custom_call", output_to_operand_aliasing={{0}: (12, {}), {1}: (13, {}), {2}: (14, {}), {3}: (15, {}),... | custom-call | flops 16106127360 | bytes 11010048 | tf_op jit(solution)/shard_map/att_bwd/pallas_call | solution.py:309
  320.5 8.1 %before_bwd.1 = (bf16[1024,768]{1,0:T(8,128)(2,1)}, f32[1,768]{1,0:T(1,128)}) custom-call(bf16[2048,768]{1,0:T(8,128)(2,1)} %copy-done.12, bf16[8,768]{1,0:T(8,128)(2,1)} %get-tuple-element.153.dt_ref.refs_3_, bf16[2048,768]{1,0:T(8,128)(2,1)} %get-tuple-element.154.dk_ref.refs_4_, bf16[2048,768]{1,0:T(8,128)(2,1)} %get-tuple-element.155.dv_ref.refs_5_, ...), custom_call_target="tpu_custom_call" | custom-call | flops 2415919104 | bytes 9437184 | tf_op jit(solution)/shard_map/before_bwd/pallas_call | solution.py:388
  329.9 1.7 merge_grid.7
  331.6 2.3 collective-permute-start.17
  334.0 19.3 %qkv_bwd.1 = (bf16[1232,768]{1,0:T(8,128)(2,1)}, f32[1232,768]{1,0:T(8,128)}, f32[1024,768]{1,0:T(8,128)}) custom-call(s32[1]{0:T(128)} %bitcast.24.refs_0_.index_ref, bf16[2048,768]{1,0:T(8,128)(2,1)} %copy-done.12, bf16[1024,768]{1,0:T(8,128)(2,1)} %get-tuple-element.159.refs_2_, bf16[8,768]{1,0:T(8,128)(2,1)} %get-tuple-element.153.dt_ref.refs_3_, ...), custom_call_target="tpu_custom_call" | custom-call | flops 9663676416 | bytes 23592960 | tf_op jit(solution)/shard_map/qkv_bwd/pallas_call | solution.py:483
  353.3 8.8 %collective-permute-start.18 = (bf16[1232,768]{1,0:T(8,128)(2,1)}, bf16[1232,768]{1,0:T(8,128)(2,1)S(1)}, u32[]{:S(2)}, u32[]{:S(2)}) collective-permute-start(bf16[1232,768]{1,0:T(8,128)(2,1)} %get-tuple-element.167), channel_id=1, source_target_pairs={{0,1},{1,0},{2,3},{3,2},{4,5},{5,4},{6,7},{7,6},{8,9},{9,8},{10,11... | collective-permute-start | bytes 5677064 | tf_op jit(solution)/shard_map/ppermute | solution.py:917
  362.6 3.2 collective-permute-done.18.got_ref
  365.8 2.1 copy-done.3
  367.9 1.8 merge.4
  369.7 5.9 %collective-permute-start.20 = (bf16[624,768]{1,0:T(8,128)(2,1)}, bf16[624,768]{1,0:T(8,128)(2,1)S(1)}, u32[]{:S(2)}, u32[]{:S(2)}) collective-permute-start(bf16[624,768]{1,0:T(8,128)(2,1)} %get-tuple-element.168), channel_id=1, source_target_pairs={{0,2},{1,5},{2,0},{3,7},{4,6},{5,1},{6,4},{7,3},{8,10},{9,13},{10,... | collective-permute-start | bytes 2875400 | tf_op jit(solution)/shard_map/ppermute | solution.py:917
  375.9 3.9 fusion.2
  382.1 2.4 reshape.127
  384.4 3.2 collective-permute-done.20.got_ref
  390.1 2.4 collective-permute-done.19
  392.5 4.7 %collective-permute-done.21.got_ref = bf16[320,768]{1,0:T(8,128)(2,1)S(1)} collective-permute-done((bf16[320,768]{1,0:T(8,128)(2,1)S(1)}, bf16[320,768]{1,0:T(8,128)(2,1)S(1)}, u32[]{:S(2)}, u32[]{:S(2)}) %collective-permute-start.21) | collective-permute-done | bytes 491552 | tf_op jit(solution)/shard_map/ppermute | solution.py:917
  397.4 2.3 collective-permute-start.22
  399.7 5.0 %fusion.5 = f32[1024,768]{1,0:T(8,128)} fusion(f32[1024,768]{1,0:T(8,128)} %get-tuple-element.114, bf16[1024,768]{1,0:T(8,128)(2,1)S(1)} %copy-done.7, f32[1024,768]{1,0:T(8,128)S(1)} %copy-done.8, bf16[1024,768]{1,0:T(8,128)(2,1)} %collective-permute-done.16, f32[1024]{0:T(1024)S(1)} %broadcast_multiply_fusion, f32[768]{0:T(1024)S(1)} %get-tuple-element.184, ...), kind=kLoop, calls=%fused_computation.7 | loop fusion | flops 7077888 | bytes 12594176 | tf_op jit(solution)/shard_map/add | solution.py:1159
  404.7 5.6 %collective-permute-done.22.got_ref = bf16[320,768]{1,0:T(8,128)(2,1)S(1)} collective-permute-done((bf16[320,768]{1,0:T(8,128)(2,1)S(1)}, bf16[320,768]{1,0:T(8,128)(2,1)S(1)}, u32[]{:S(2)}, u32[]{:S(2)}) %collective-permute-start.22) | collective-permute-done | bytes 491552 | tf_op jit(solution)/shard_map/ppermute | solution.py:917
  412.5 12.5 %collective-permute-done.23 = bf16[320,768]{1,0:T(8,128)(2,1)S(1)} collective-permute-done((bf16[320,768]{1,0:T(8,128)(2,1)S(1)}, bf16[320,768]{1,0:T(8,128)(2,1)S(1)}, u32[]{:S(2)}, u32[]{:S(2)}) %collective-permute-start.23) | collective-permute-done | bytes 491552 | tf_op jit(solution)/shard_map/ppermute | solution.py:917
  426.2 3.5 fusion.17
  (116 shorter events, 25.4 us)
Async XLA Ops:
  1.5 4.8 %collective-permute-start = (bf16[96,128]{1,0:T(8,128)(2,1)S(1)}, bf16[96,128]{1,0:T(8,128)(2,1)S(1)}, u32[]{:S(2)}, u32[]{:S(2)}) collective-permute-start(bf16[96,128]{1,0:T(8,128)(2,1)S(1)} %slice.32), channel_id=1, source_target_pairs={{0,1},{1,2},{2,3},{3,4},{4,5},{5,6},{6,7},{7,8},{8,9},{9,10},{10,1... | collective-permute-start | bytes 73736 | tf_op jit(solution)/shard_map/ppermute | solution.py:897
  6.2 2.6 copy-start.15
  6.3 2.6 copy-start.5
  8.8 8.5 %collective-permute-start.2 = (bf16[1024,768]{1,0:T(8,128)(2,1)S(1)}, bf16[1024,768]{1,0:T(8,128)(2,1)}, u32[]{:S(2)}, u32[]{:S(2)}) collective-permute-start(bf16[1024,768]{1,0:T(8,128)(2,1)S(1)} %copy-done.5), channel_id=1, source_target_pairs={{0,1},{1,2},{2,3},{4,5},{5,6},{6,7},{8,9},{9,10},{10,11},{12,13},{... | collective-permute-start | bytes 4718600 | tf_op jit(solution)/shard_map/ppermute | solution.py:903
  14.5 23.0 %collective-permute-start.1 = (bf16[304,768]{1,0:T(8,128)(2,1)S(1)}, bf16[304,768]{1,0:T(8,128)(2,1)S(1)}, u32[]{:S(2)}, u32[]{:S(2)}) collective-permute-start(bf16[304,768]{1,0:T(8,128)(2,1)S(1)} %pad_maximum_fusion.2), channel_id=1, source_target_pairs={{0,16},{1,17},{2,18},{3,19},{4,20},{5,21},{6,22},{7,23},{8,24},{9,... | collective-permute-start | bytes 1400840 | tf_op jit(solution)/shard_map/ppermute | solution.py:917
  18.9 30.8 %copy-start.12 = (bf16[2048,768]{1,0:T(8,128)(2,1)}, bf16[2048,768]{1,0:T(8,128)(2,1)S(1)}, u32[]{:S(2)}) copy-start(bf16[2048,768]{1,0:T(8,128)(2,1)S(1)} %constant_dynamic-update-slice_fusion.refs_1_.x_ref) | copy-start | bytes 9437188
  37.7 11.6 %collective-permute-start.3 = (bf16[304,768]{1,0:T(8,128)(2,1)S(1)}, bf16[304,768]{1,0:T(8,128)(2,1)S(1)}, u32[]{:S(2)}, u32[]{:S(2)}) collective-permute-start(bf16[304,768]{1,0:T(8,128)(2,1)S(1)} %pad_maximum_fusion.3), channel_id=1, source_target_pairs={{0,8},{1,9},{2,10},{3,11},{4,12},{5,13},{6,14},{7,15},{8,0},{9,1},... | collective-permute-start | bytes 1400840 | tf_op jit(solution)/shard_map/ppermute | solution.py:917
  49.4 8.6 %collective-permute-start.5 = (bf16[304,768]{1,0:T(8,128)(2,1)S(1)}, bf16[304,768]{1,0:T(8,128)(2,1)S(1)}, u32[]{:S(2)}, u32[]{:S(2)}) collective-permute-start(bf16[304,768]{1,0:T(8,128)(2,1)S(1)} %fusion.16.own_ref), channel_id=1, source_target_pairs={{0,2},{1,5},{2,0},{3,7},{4,6},{5,1},{6,4},{7,3},{8,10},{9,13},{10,... | collective-permute-start | bytes 1400840 | tf_op jit(solution)/shard_map/ppermute | solution.py:917
  58.1 13.4 %collective-permute-start.6 = (bf16[592,768]{1,0:T(8,128)(2,1)S(1)}, bf16[592,768]{1,0:T(8,128)(2,1)S(1)}, u32[]{:S(2)}, u32[]{:S(2)}) collective-permute-start(bf16[592,768]{1,0:T(8,128)(2,1)S(1)} %join.2.own_ref), channel_id=1, source_target_pairs={{0,4},{1,3},{2,6},{3,1},{4,0},{5,7},{6,2},{7,5},{8,12},{9,11},{10,... | collective-permute-start | bytes 2727944 | tf_op jit(solution)/shard_map/ppermute | solution.py:917
  72.9 24.0 %collective-permute-start.7 = (bf16[1168,768]{1,0:T(8,128)(2,1)}, bf16[1168,768]{1,0:T(8,128)(2,1)}, u32[]{:S(2)}, u32[]{:S(2)}) collective-permute-start(bf16[1168,768]{1,0:T(8,128)(2,1)} %join.3.refs_2_), channel_id=1, source_target_pairs={{0,1},{1,0},{2,3},{3,2},{4,5},{5,4},{6,7},{7,6},{8,9},{9,8},{10,11... | collective-permute-start | bytes 5382152 | tf_op jit(solution)/shard_map/ppermute | solution.py:917
  72.9 22.1 %collective-permute-start.4 = (bf16[576,768]{1,0:T(8,128)(2,1)S(1)}, bf16[576,768]{1,0:T(8,128)(2,1)S(1)}, u32[]{:S(2)}, u32[]{:S(2)}) collective-permute-start(bf16[576,768]{1,0:T(8,128)(2,1)S(1)} %pad_maximum_fusion.1), channel_id=1, source_target_pairs={{0,8},{1,9},{2,10},{3,11},{4,12},{5,13},{6,14},{7,15},{8,0},{9,1},... | collective-permute-start | bytes 2654216 | tf_op jit(solution)/shard_map/ppermute | solution.py:917
  95.9 17.8 %collective-permute-start.8 = (bf16[864,768]{1,0:T(8,128)(2,1)S(1)}, bf16[864,768]{1,0:T(8,128)(2,1)S(1)}, u32[]{:S(2)}, u32[]{:S(2)}) collective-permute-start(bf16[864,768]{1,0:T(8,128)(2,1)S(1)} %bitcast.76), channel_id=1, source_target_pairs={{0,2},{1,5},{2,0},{3,7},{4,6},{5,1},{6,4},{7,3},{8,10},{9,13},{10,... | collective-permute-start | bytes 3981320 | tf_op jit(solution)/shard_map/ppermute | solution.py:917
  114.7 20.2 %copy-start.4 = (bf16[1728,768]{1,0:T(8,128)(2,1)}, bf16[1728,768]{1,0:T(8,128)(2,1)S(1)}, u32[]{:S(2)}) copy-start(bf16[1728,768]{1,0:T(8,128)(2,1)S(1)} %join_held.1) | copy-start | bytes 7962628
  114.7 20.2 %collective-permute-start.10 = (bf16[1728,768]{1,0:T(8,128)(2,1)S(1)}, bf16[1728,768]{1,0:T(8,128)(2,1)S(1)}, u32[]{:S(2)}, u32[]{:S(2)}) collective-permute-start(bf16[1728,768]{1,0:T(8,128)(2,1)S(1)} %join_held.1), channel_id=1, source_target_pairs={{0,1},{1,0},{2,3},{3,2},{4,5},{5,4},{6,7},{7,6},{8,9},{9,8},{10,11... | collective-permute-start | bytes 7962632 | tf_op jit(solution)/shard_map/ppermute | solution.py:917
  114.8 37.3 %collective-permute-start.9 = (bf16[1728,768]{1,0:T(8,128)(2,1)S(1)}, bf16[1728,768]{1,0:T(8,128)(2,1)}, u32[]{:S(2)}, u32[]{:S(2)}) collective-permute-start(bf16[1728,768]{1,0:T(8,128)(2,1)S(1)} %join_held.1), channel_id=1, source_target_pairs={{0,4},{1,3},{2,6},{3,1},{4,0},{5,7},{6,2},{7,5},{8,12},{9,11},{10,... | collective-permute-start | bytes 7962632 | tf_op jit(solution)/shard_map/ppermute | solution.py:917
  135.0 17.1 %copy-start.17 = (bf16[1728,768]{1,0:T(8,128)(2,1)}, bf16[1728,768]{1,0:T(8,128)(2,1)S(1)}, u32[]{:S(2)}) copy-start(bf16[1728,768]{1,0:T(8,128)(2,1)S(1)} %collective-permute-done.10) | copy-start | bytes 7962628
  152.2 18.3 %collective-permute-start.11 = (bf16[1728,768]{1,0:T(8,128)(2,1)}, bf16[1728,768]{1,0:T(8,128)(2,1)S(1)}, u32[]{:S(2)}, u32[]{:S(2)}) collective-permute-start(bf16[1728,768]{1,0:T(8,128)(2,1)} %hold.1), channel_id=1, source_target_pairs={{0,1},{1,0},{2,3},{3,2},{4,5},{5,4},{6,7},{7,6},{8,9},{9,8},{10,11... | collective-permute-start | bytes 7962632 | tf_op jit(solution)/shard_map/ppermute | solution.py:917
  170.5 1.5 copy-start.18
  227.2 9.9 %collective-permute-start.12 = (bf16[12,288,768]{2,1,0:T(8,128)(2,1)}, bf16[12,288,768]{2,1,0:T(8,128)(2,1)}, u32[]{:S(2)}, u32[]{:S(2)}) collective-permute-start(bf16[12,288,768]{2,1,0:T(8,128)(2,1)} %bitcast.84), channel_id=1, source_target_pairs={{0,1},{1,0},{2,3},{3,2},{4,5},{5,4},{6,7},{7,6},{8,9},{9,8},{10,11... | collective-permute-start | bytes 15925256 | tf_op jit(solution)/shard_map/ppermute | solution.py:917
  227.8 9.3 %slice-start = ((s8[5308416]{0:T(1024)(128)(4,1)}), s8[4194304]{0:T(1024)(128)(4,1)S(1)}, s32[]{:S(2)}) async-start(s8[5308416]{0:T(1024)(128)(4,1)} %bitcast.72), calls=%async_computation | async-start | bytes 8388608
  227.8 9.3 %slice-start.1 = ((s8[5308416]{0:T(1024)(128)(4,1)}), s8[1114112]{0:T(1024)(128)(4,1)S(1)}, s32[]{:S(2)}) async-start(s8[5308416]{0:T(1024)(128)(4,1)} %bitcast.72), calls=%async_computation.1 | async-start | bytes 2228224
  244.6 35.9 %collective-permute-start.13 = (bf16[6,288,768]{2,1,0:T(8,128)(2,1)}, bf16[6,288,768]{2,1,0:T(8,128)(2,1)S(1)}, u32[]{:S(2)}, u32[]{:S(2)}) collective-permute-start(bf16[6,288,768]{2,1,0:T(8,128)(2,1)} %get-tuple-element.124), channel_id=1, source_target_pairs={{0,2},{1,5},{2,0},{3,7},{4,6},{5,1},{6,4},{7,3},{8,10},{9,13},{10,... | collective-permute-start | bytes 7962632 | tf_op jit(solution)/shard_map/ppermute | solution.py:917
  250.4 30.1 %copy-start = (bf16[6,288,768]{2,1,0:T(8,128)(2,1)S(1)}, bf16[6,288,768]{2,1,0:T(8,128)(2,1)}, u32[]{:S(2)}) copy-start(bf16[6,288,768]{2,1,0:T(8,128)(2,1)} %get-tuple-element.132.ka_ref.kb_ref) | copy-start | bytes 7962628
  283.5 18.0 %collective-permute-start.14 = (bf16[3,288,768]{2,1,0:T(8,128)(2,1)}, bf16[3,288,768]{2,1,0:T(8,128)(2,1)S(1)}, u32[]{:S(2)}, u32[]{:S(2)}) collective-permute-start(bf16[3,288,768]{2,1,0:T(8,128)(2,1)} %get-tuple-element.133), channel_id=1, source_target_pairs={{0,4},{1,3},{2,6},{3,1},{4,0},{5,7},{6,2},{7,5},{8,12},{9,11},{10,... | collective-permute-start | bytes 3981320 | tf_op jit(solution)/shard_map/ppermute | solution.py:917
  283.5 17.9 %copy-start.1 = (f32[3,288,768]{2,1,0:T(8,128)S(1)}, f32[3,288,768]{2,1,0:T(8,128)}, u32[]{:S(2)}) copy-start(f32[3,288,768]{2,1,0:T(8,128)} %get-tuple-element.141.ka_ref.kb_ref) | copy-start | bytes 7962628
  303.6 26.3 %collective-permute-start.15 = (bf16[2,288,768]{2,1,0:T(8,128)(2,1)}, bf16[2,288,768]{2,1,0:T(8,128)(2,1)S(1)}, u32[]{:S(2)}, u32[]{:S(2)}) collective-permute-start(bf16[2,288,768]{2,1,0:T(8,128)(2,1)} %get-tuple-element.142), channel_id=1, source_target_pairs={{0,8},{1,9},{2,10},{3,11},{4,12},{5,13},{6,14},{7,15},{8,0},{9,1},... | collective-permute-start | bytes 2654216 | tf_op jit(solution)/shard_map/ppermute | solution.py:917
  320.5 9.4 %copy-start.2 = (f32[2,288,768]{2,1,0:T(8,128)S(1)}, f32[2,288,768]{2,1,0:T(8,128)}, u32[]{:S(2)}) copy-start(f32[2,288,768]{2,1,0:T(8,128)} %get-tuple-element.150.ka_ref.kb_ref) | copy-start | bytes 5308420
  328.5 24.7 %collective-permute-start.16 = (bf16[1024,768]{1,0:T(8,128)(2,1)}, bf16[1024,768]{1,0:T(8,128)(2,1)}, u32[]{:S(2)}, u32[]{:S(2)}) collective-permute-start(bf16[1024,768]{1,0:T(8,128)(2,1)} %get-tuple-element.157), channel_id=1, source_target_pairs={{1,0},{2,1},{3,2},{5,4},{6,5},{7,6},{9,8},{10,9},{11,10},{13,12},{... | collective-permute-start | bytes 4718600 | tf_op jit(solution)/shard_map/ppermute | solution.py:903
  331.6 21.6 %collective-permute-start.17 = (bf16[1,288,768]{2,1,0:T(8,128)(2,1)}, bf16[1,288,768]{2,1,0:T(8,128)(2,1)S(1)}, u32[]{:S(2)}, u32[]{:S(2)}) collective-permute-start(bf16[1,288,768]{2,1,0:T(8,128)(2,1)} %get-tuple-element.151), channel_id=1, source_target_pairs={{0,16},{1,17},{2,18},{3,19},{4,20},{5,21},{6,22},{7,23},{8,24},{9,... | collective-permute-start | bytes 1327112 | tf_op jit(solution)/shard_map/ppermute | solution.py:917
  333.9 28.2 %copy-start.6 = (bf16[1024,768]{1,0:T(8,128)(2,1)S(1)}, bf16[1024,768]{1,0:T(8,128)(2,1)}, u32[]{:S(2)}) copy-start(bf16[1024,768]{1,0:T(8,128)(2,1)} %x_ref.1) | copy-start | bytes 4718596
  353.3 12.5 %collective-permute-start.18 = (bf16[1232,768]{1,0:T(8,128)(2,1)}, bf16[1232,768]{1,0:T(8,128)(2,1)S(1)}, u32[]{:S(2)}, u32[]{:S(2)}) collective-permute-start(bf16[1232,768]{1,0:T(8,128)(2,1)} %get-tuple-element.167), channel_id=1, source_target_pairs={{0,1},{1,0},{2,3},{3,2},{4,5},{5,4},{6,7},{7,6},{8,9},{9,8},{10,11... | collective-permute-start | bytes 5677064 | tf_op jit(solution)/shard_map/ppermute | solution.py:917
  362.5 13.2 %copy-start.16 = (pred[3]{0:T(512)(128)(4,1)S(1)}, pred[3]{0:T(512)(128)(4,1)}, u32[]{:S(2)}) copy-start(pred[3]{0:T(512)(128)(4,1)} %copy-done.15) | copy-start | bytes 13
  365.8 2.1 copy-start.3
  369.7 18.0 %collective-permute-start.20 = (bf16[624,768]{1,0:T(8,128)(2,1)}, bf16[624,768]{1,0:T(8,128)(2,1)S(1)}, u32[]{:S(2)}, u32[]{:S(2)}) collective-permute-start(bf16[624,768]{1,0:T(8,128)(2,1)} %get-tuple-element.168), channel_id=1, source_target_pairs={{0,2},{1,5},{2,0},{3,7},{4,6},{5,1},{6,4},{7,3},{8,10},{9,13},{10,... | collective-permute-start | bytes 2875400 | tf_op jit(solution)/shard_map/ppermute | solution.py:917
  375.9 3.9 copy-start.14
  379.9 0.9 copy-start.10
  384.4 4.0 copy-start.11
  384.4 4.0 copy-start.13
  387.7 12.0 %copy-start.7 = (bf16[1024,768]{1,0:T(8,128)(2,1)S(1)}, bf16[1024,768]{1,0:T(8,128)(2,1)}, u32[]{:S(2)}) copy-start(bf16[1024,768]{1,0:T(8,128)(2,1)} %x_ref.1) | copy-start | bytes 4718596
  387.7 12.0 %copy-start.8 = (f32[1024,768]{1,0:T(8,128)S(1)}, f32[1024,768]{1,0:T(8,128)}, u32[]{:S(2)}) copy-start(f32[1024,768]{1,0:T(8,128)} %get-tuple-element.162) | copy-start | bytes 9437188
  388.4 8.9 %collective-permute-start.21 = (bf16[320,768]{1,0:T(8,128)(2,1)S(1)}, bf16[320,768]{1,0:T(8,128)(2,1)S(1)}, u32[]{:S(2)}, u32[]{:S(2)}) collective-permute-start(bf16[320,768]{1,0:T(8,128)(2,1)S(1)} %get-tuple-element.173), channel_id=1, source_target_pairs={{0,4},{1,3},{2,6},{3,1},{4,0},{5,7},{6,2},{7,5},{8,12},{9,11},{10,... | collective-permute-start | bytes 1474568 | tf_op jit(solution)/shard_map/ppermute | solution.py:917
  388.7 3.9 collective-permute-start.19
  397.4 12.9 %collective-permute-start.22 = (bf16[320,768]{1,0:T(8,128)(2,1)S(1)}, bf16[320,768]{1,0:T(8,128)(2,1)S(1)}, u32[]{:S(2)}, u32[]{:S(2)}) collective-permute-start(bf16[320,768]{1,0:T(8,128)(2,1)S(1)} %get-tuple-element.175), channel_id=1, source_target_pairs={{0,8},{1,9},{2,10},{3,11},{4,12},{5,13},{6,14},{7,15},{8,0},{9,1},... | collective-permute-start | bytes 1474568 | tf_op jit(solution)/shard_map/ppermute | solution.py:917
  410.4 14.6 %collective-permute-start.23 = (bf16[320,768]{1,0:T(8,128)(2,1)S(1)}, bf16[320,768]{1,0:T(8,128)(2,1)S(1)}, u32[]{:S(2)}, u32[]{:S(2)}) collective-permute-start(bf16[320,768]{1,0:T(8,128)(2,1)S(1)} %get-tuple-element.177), channel_id=1, source_target_pairs={{8,24},{9,25},{10,26},{11,27},{12,28},{13,29},{14,30},{15,31},{16,... | collective-permute-start | bytes 1474568 | tf_op jit(solution)/shard_map/ppermute | solution.py:917
  425.1 1.2 copy-start.9

commit v12 on v11

--- a/solution.py
+++ b/solution.py
@@ -560,32 +560,39 @@
     )(index, keep, got, keep, got)
 
 
-def arrange(index, one, two, taken):
-    half = one.shape[0]
-    height = one.shape[1]
-
-    def body(index_ref, one_ref, two_ref, out_ref):
-        for i in range(taken):
-            at = index_ref[i]
-
-            @pl.when(at < half)
-            def _():
-                out_ref[i] = one_ref[jnp.minimum(at, half - 1)]
-
-            @pl.when(at >= half)
-            def _():
-                out_ref[i] = two_ref[jnp.maximum(at - half, 0)]
+def arrange(index, blocks):
+    height = blocks[0].shape[0] - 16
+
+    def body(index_ref, *refs):
+        first_ref, rest_ref = refs[4:]
+        refs = refs[:4]
+        for i in range(4):
+            for k in range(4):
+
+                @pl.when(index_ref[i] == k)
+                def _():
+                    piece = refs[k][0:height, :]
+                    if i == 0:
+                        first_ref[0:height, :] = piece
+                    else:
+                        rest_ref[(i - 1) * height : i * height, :] = piece
+
+        ends = [ref[height:, :].astype(F32) for ref in refs]
+        first_ref[height:, :] = (ends[0] + ends[1] + ends[2] + ends[3]).astype(BF)
 
     vmem = pl.BlockSpec(memory_space=pltpu.VMEM)
     return pl.pallas_call(
         body,
-        in_specs=[pl.BlockSpec(memory_space=pltpu.SMEM), vmem, vmem],
-        out_specs=vmem,
-        out_shape=jax.ShapeDtypeStruct((taken, height, D), BF),
+        in_specs=[pl.BlockSpec(memory_space=pltpu.SMEM)] + [vmem] * 4,
+        out_specs=[vmem, vmem],
+        out_shape=[
+            jax.ShapeDtypeStruct((height + 16, D), BF),
+            jax.ShapeDtypeStruct((3 * height, D), BF),
+        ],
         compiler_params=pltpu.CompilerParams(vmem_limit_bytes=32 << 20),
-        cost_estimate=cost(taken * height * D, taken * height * D * 8),
+        cost_estimate=cost(4 * height * D, 4 * height * D * 4),
         name="arrange",
-    )(index, one, two)
+    )(index, *blocks)
 
 
 def join(own, got, shared=16):
@@ -1029,22 +1036,14 @@
         z = place >> 3
         mine = jnp.concatenate([chunk, small.astype(BF).reshape(-1, D)], 0)
         tokens_before = shift_ctx(after(tokens, mine), 1)
-        got = swap(mine, 16, 16)
+        far = swap(mine, 16, 16)
+        near = swap(mine, 8, 8)
         tokens_both = jnp.concatenate([tokens_before, tokens], 0)
-        got = after(got, tokens_both)
-        rest = jnp.concatenate([chunk, got[:height]], 0)
-        none = jnp.zeros((), BF)
-        first = jnp.where(z == 0, chunk, jnp.where(z == 2, got[:height], none))
-        mine = jnp.concatenate([first, mine[height:] + got[height:]], 0)
-        mine = mine + swap(mine, 8, 8)
-        across = swap(after(rest, mine), 8, 8)
+        both = swap(after(far, tokens_both), 8, 8)
+        order = jnp.stack([z, z ^ 1, z ^ 2, z ^ 3]).astype(jnp.int32)
+        mine, rest = arrange(order, (mine, near, far, both))
         mine = join(mine, swap(mine, 2, 4))
         mine = join(mine, swap(mine, 4, 2))
-        codes = [z ^ k for k in (1, 2, 3)]
-        order = [jnp.where(j == 1, 2, jnp.where(j == 2, 1, j)) for j in codes]
-        rest = arrange(
-            jnp.stack(order).astype(jnp.int32), rest.reshape(2, height, D), across.reshape(2, height, D), 3
-        ).reshape(-1, D)
         across = swap(rest, 2, 4)
         got = swap(mine, 1, 1)
         index = []
@@ -1060,7 +1059,7 @@
                 late_index += [piece, piece + 8, piece + 16]
         index = jnp.stack(index).astype(jnp.int32)
         late_index = jnp.stack(late_index + [core[0]]).astype(jnp.int32)
-        projected, small, in_weight = qkv_fwd(after(index, rest), tokens_both, (mine, got), rows, 4)
+        projected, small, in_weight = qkv_fwd(index, tokens_both, (mine, got), rows, 4)
     else:
         tokens_both = jnp.concatenate([shift_ctx(tokens, 1), tokens], 0)
         wide = lax.all_gather(chunk, AXES, axis=0, tiled=True)

time: 430 us -> 414 us (0.963)
  waiting for transfers between devices: 128 us -> 111 us
    ppermute x20, waiting for transfers between devices: 126 us -> 108 us  [swap(): return lax.ppermute(block, AXES, route)]
    unnamed x43 -> x57, local copies, waits for them, and re-layouts: 6.98 us -> 10.5 us
  transfers between devices with their start and end apart: 24 -> 24, of which waited for: 14 -> 14; matrix products, arithmetic and copies ran while one was open for 5% -> 5% of each run, Pallas kernels for 33% -> 34%
where the time goes in v12:
time: 414 us; the launch traced here: 416 us
  Pallas kernels  215 us (52%)
  waiting for transfers between devices  111 us (27%)
  starting transfers between devices  47.9 us (12%)
  local copies, waits for them, and re-layouts  22.6 us (5%)
  other arithmetic  15.6 us (4%)
    ppermute x20, waiting for transfers between devices, swap(): return lax.ppermute(block, AXES, route)  108 us
    pallas_call x1, Pallas kernels, ffn(): pl.pallas_call(ffn_kernel, grid=(4,), in_specs=[scalars, scalars, act, ac...  55.1 us
    pallas_call x4, Pallas kernels, att_bwd(): call_in_parts(att_bwd_kernel, [pl.BlockSpec(memory_space=pltpu.SMEM), own...  50.3 us
    pallas_call x3, Pallas kernels, att_fwd(): call_in_parts(att_fwd_kernel, [pl.BlockSpec(memory_space=pltpu.SMEM), col...  49.3 us
    ppermute x20, starting transfers between devices, swap(): return lax.ppermute(block, AXES, route)  38.2 us
    pallas_call x1, Pallas kernels, qkv_bwd(): pl.pallas_call(body, grid=(blocks,), in_specs=[pl.BlockSpec(memory_space=...  19.3 us
    pallas_call x4, Pallas kernels, merge_grid(): pl.pallas_call(body, grid_spec=pltpu.PrefetchScalarGridSpec(num_scalar_pr...  14.3 us
    pallas_call x1, Pallas kernels, qkv_fwd(): pl.pallas_call(body, grid=(blocks,), in_specs=[pl.BlockSpec(memory_space=...  13.3 us
  transfers between devices with their start and end apart: 24, of which 14 were waited for; matrix products, arithmetic and copies ran while one was open for 5% of the time, Pallas kernels for 34%

profile of v12, /device:TPU:0, one launch (start us, length us, event | category | flops | bytes accessed | tf_op | source)
XLA Modules:
  0.0 415.7 jit_solution(13382262675960848)
XLA Ops:
  1.5 2.3 collective-permute-start
  3.8 2.3 concatenate.16
  6.3 1.5 fusion.8
  8.8 4.6 %collective-permute-start.3 = (bf16[1024,768]{1,0:T(8,128)(2,1)S(1)}, bf16[1024,768]{1,0:T(8,128)(2,1)S(1)}, u32[]{:S(2)}, u32[]{:S(2)}) collective-permute-start(bf16[1024,768]{1,0:T(8,128)(2,1)S(1)} %copy-done.12), channel_id=1, source_target_pairs={{0,1},{1,2},{2,3},{4,5},{5,6},{6,7},{8,9},{9,10},{10,11},{12,13},{... | collective-permute-start | bytes 4718600 | tf_op jit(solution)/shard_map/ppermute | solution.py:910
  13.4 2.9 collective-permute-start.2
  16.3 1.6 collective-permute-start.1
  18.1 19.6 %collective-permute-done.2.refs_2_ = bf16[304,768]{1,0:T(8,128)(2,1)S(1)} collective-permute-done((bf16[304,768]{1,0:T(8,128)(2,1)S(1)}, bf16[304,768]{1,0:T(8,128)(2,1)S(1)}, u32[]{:S(2)}, u32[]{:S(2)}) %collective-permute-start.2) | collective-permute-done | bytes 466976 | tf_op jit(solution)/shard_map/ppermute | solution.py:924
  39.1 10.9 %collective-permute-done.4.refs_3_ = bf16[304,768]{1,0:T(8,128)(2,1)S(1)} collective-permute-done((bf16[304,768]{1,0:T(8,128)(2,1)S(1)}, bf16[304,768]{1,0:T(8,128)(2,1)S(1)}, u32[]{:S(2)}, u32[]{:S(2)}) %collective-permute-start.4) | collective-permute-done | bytes 466976 | tf_op jit(solution)/shard_map/ppermute | solution.py:924
  53.9 8.6 %collective-permute-done.5.got_ref = bf16[304,768]{1,0:T(8,128)(2,1)S(1)} collective-permute-done((bf16[304,768]{1,0:T(8,128)(2,1)S(1)}, bf16[304,768]{1,0:T(8,128)(2,1)S(1)}, u32[]{:S(2)}, u32[]{:S(2)}) %collective-permute-start.5) | collective-permute-done | bytes 466976 | tf_op jit(solution)/shard_map/ppermute | solution.py:924
  62.5 1.6 collective-permute-start.6
  64.1 11.8 %collective-permute-done.6.got_ref = bf16[592,768]{1,0:T(8,128)(2,1)S(1)} collective-permute-done((bf16[592,768]{1,0:T(8,128)(2,1)S(1)}, bf16[592,768]{1,0:T(8,128)(2,1)S(1)}, u32[]{:S(2)}, u32[]{:S(2)}) %collective-permute-start.6) | collective-permute-done | bytes 909344 | tf_op jit(solution)/shard_map/ppermute | solution.py:924
  77.0 2.9 collective-permute-done.7.refs_3_
  79.9 13.3 %qkv_fwd.1 = (bf16[2048,2304]{1,0:T(8,128)(2,1)}, f32[16,768]{1,0:T(8,128)}, bf16[2304,768]{1,0:T(8,128)(2,1)}) custom-call(s32[8]{0:T(128)} %stack.217.refs_0_, bf16[2048,768]{1,0:T(8,128)(2,1)} %copy-done.19, bf16[1168,768]{1,0:T(8,128)(2,1)} %copy-done.5, bf16[1168,768]{1,0:T(8,128)(2,1)} %collective-permute-done.7.refs_3_), custom_call_target="tpu_custom_call" | custom-call | flops 7247757312 | bytes 15728640 | tf_op jit(solution)/shard_map/qkv_fwd/pallas_call | solution.py:702
  95.4 1.8 join_held.1
  97.2 1.6 collective-permute-start.9
  101.3 16.0 %att_fwd.3 = (bf16[1024,768]{1,0:T(8,128)(2,1)}, f32[1024,768]{1,0:T(8,128)}, bf16[1024,768]{1,0:T(8,128)(2,1)}, bf16[2048,768]{1,0:T(8,128)(2,1)}, bf16[2048,768]{1,0:T(8,128)(2,1)}) custom-call(s32[1]{0:T(128)S(6)} %select_n.120.refs_0_.state_ref, bf16[2048,2304]{1,0:T(8,128)(2,1)} %get-tuple-element.96.refs_1_.refs_2_.refs_3_.refs_4_.refs_7_.refs_8_.refs_9_.refs_10_, ...), custom_call_target="tpu_custom_call" | custom-call | flops 6442450944 | bytes 7864320 | tf_op jit(solution)/shard_map/att_fwd/pallas_call | solution.py:152
  117.3 17.1 %att_fwd.4 = (bf16[1024,768]{1,0:T(8,128)(2,1)}, f32[1024,768]{1,0:T(8,128)}, bf16[1024,768]{1,0:T(8,128)(2,1)}, bf16[2048,768]{1,0:T(8,128)(2,1)}, bf16[2048,768]{1,0:T(8,128)(2,1)}) custom-call(s32[1]{0:T(128)S(6)} %select_n.120.refs_0_.state_ref, ...), custom_call_target="tpu_custom_call", output_to_operand_aliasing={{0}: (6, {}), {1}: (7, {}), {2}: (8, {}), {3}: (9, {}), {4}... | custom-call | flops 6442450944 | bytes 7864320 | tf_op jit(solution)/shard_map/att_fwd/pallas_call | solution.py:152
  136.7 16.3 %att_fwd.5 = (bf16[1024,768]{1,0:T(8,128)(2,1)}, f32[1024,768]{1,0:T(8,128)}, bf16[1024,768]{1,0:T(8,128)(2,1)}, bf16[2048,768]{1,0:T(8,128)(2,1)}, bf16[2048,768]{1,0:T(8,128)(2,1)}) custom-call(s32[1]{0:T(128)S(6)} %select_n.120.refs_0_.state_ref, ...), custom_call_target="tpu_custom_call", output_to_operand_aliasing={{0}: (6, {}), {1}: (7, {}), {2}: (8, {}), {3}: (9, {}), {4}... | custom-call | flops 6442450944 | bytes 7864320 | tf_op jit(solution)/shard_map/att_fwd/pallas_call | solution.py:152
  153.0 1.5 copy-done.25
  154.5 55.1 %ffn.1 = (bf16[1024,768]{1,0:T(8,128)(2,1)}, f32[1024,768]{1,0:T(8,128)}, bf16[1024,768]{1,0:T(8,128)(2,1)}, f32[1,768]{1,0:T(1,128)}, bf16[36,4,24,768]{3,2,1,0...) custom-call(s32[1]{0:T(128)S(6)} %select_n.120.refs_0_.state_ref, s32[25]{0:T(128)} %stack.211.index_ref, ...), custom_call_target="tpu_custom_call" | custom-call | flops 32614907904 | bytes 40894464 | tf_op jit(solution)/shard_map/ffn/pallas_call | solution.py:867
  210.3 9.3 %att_bwd.4 = (bf16[1024,768]{1,0:T(8,128)(2,1)}, bf16[8,768]{1,0:T(8,128)(2,1)}, bf16[2048,768]{1,0:T(8,128)(2,1)}, bf16[2048,768]{1,0:T(8,128)(2,1)}, f32[16,768]{1,0:T(8,128)}) custom-call(s32[1]{0:T(128)S(6)} %select_n.120.refs_0_.state_ref, bf16[1024,768]{1,0:T(8,128)(2,1)} %get-tuple-element.115.refs_1_, bf16[2048,768]{1,0:T(8,128)(2,1)} %get-tuple-element.116.refs_2_, ...), custom_call_target="tpu_custom_call" | custom-call | flops 8053063680 | bytes 5505024 | tf_op jit(solution)/shard_map/att_bwd/pallas_call | solution.py:309
  219.7 7.4 %merge_grid.4 = (bf16[6,288,768]{2,1,0:T(8,128)(2,1)}, bf16[6,288,768]{2,1,0:T(8,128)(2,1)}) custom-call(s32[12]{0:T(128)S(1)} %stack.243.index_ref, bf16[12,288,768]{2,1,0:T(8,128)(2,1)S(1)} %bitcast.71, bf16[12,288,768]{2,1,0:T(8,128)(2,1)} %collective-permute-done.12.ga_ref.gb_ref, bf16[12,288,768]{2,1,0:T(8,128)(2,1)S(1)} %bitcast.72, ...), custom_call_target="tpu_custom_call" | custom-call | flops 2654208 | bytes 21233664 | tf_op jit(solution)/shard_map/merge_grid/pallas_call | solution.py:545
  227.1 5.7 %collective-permute-start.13 = (bf16[6,288,768]{2,1,0:T(8,128)(2,1)}, bf16[6,288,768]{2,1,0:T(8,128)(2,1)S(1)}, u32[]{:S(2)}, u32[]{:S(2)}) collective-permute-start(bf16[6,288,768]{2,1,0:T(8,128)(2,1)} %get-tuple-element.124), channel_id=1, source_target_pairs={{0,2},{1,5},{2,0},{3,7},{4,6},{5,1},{6,4},{7,3},{8,10},{9,13},{10,... | collective-permute-start | bytes 7962632 | tf_op jit(solution)/shard_map/ppermute | solution.py:924
  232.9 15.8 %att_bwd.5 = (bf16[1024,768]{1,0:T(8,128)(2,1)}, bf16[8,768]{1,0:T(8,128)(2,1)}, bf16[2048,768]{1,0:T(8,128)(2,1)}, bf16[2048,768]{1,0:T(8,128)(2,1)}, f32[16,768]{1,0:T(8,128)}) custom-call(s32[1]{0:T(128)S(6)} %select_n.120.refs_0_.state_ref, ...), custom_call_target="tpu_custom_call", output_to_operand_aliasing={{0}: (12, {}), {1}: (13, {}), {2}: (14, {}), {3}: (15, {}),... | custom-call | flops 16106127360 | bytes 11010048 | tf_op jit(solution)/shard_map/att_bwd/pallas_call | solution.py:309
  248.7 14.3 %collective-permute-done.13.ga_ref.gb_ref = bf16[6,288,768]{2,1,0:T(8,128)(2,1)S(1)} collective-permute-done((bf16[6,288,768]{2,1,0:T(8,128)(2,1)}, bf16[6,288,768]{2,1,0:T(8,128)(2,1)S(1)}, u32[]{:S(2)}, u32[]{:S(2)}) %collective-permute-start.13) | collective-permute-done | bytes 2654240 | tf_op jit(solution)/shard_map/ppermute | solution.py:924
  263.0 3.0 merge_grid.5
  266.0 9.5 %att_bwd.6 = (bf16[1024,768]{1,0:T(8,128)(2,1)}, bf16[8,768]{1,0:T(8,128)(2,1)}, bf16[2048,768]{1,0:T(8,128)(2,1)}, bf16[2048,768]{1,0:T(8,128)(2,1)}, f32[16,768]{1,0:T(8,128)}) custom-call(s32[1]{0:T(128)S(6)} %select_n.120.refs_0_.state_ref, ...), custom_call_target="tpu_custom_call", output_to_operand_aliasing={{0}: (12, {}), {1}: (13, {}), {2}: (14, {}), {3}: (15, {}),... | custom-call | flops 8053063680 | bytes 5505024 | tf_op jit(solution)/shard_map/att_bwd/pallas_call | solution.py:309
  275.5 8.4 %collective-permute-done.14.ga_ref.gb_ref = bf16[3,288,768]{2,1,0:T(8,128)(2,1)S(1)} collective-permute-done((bf16[3,288,768]{2,1,0:T(8,128)(2,1)}, bf16[3,288,768]{2,1,0:T(8,128)(2,1)S(1)}, u32[]{:S(2)}, u32[]{:S(2)}) %collective-permute-start.14) | collective-permute-done | bytes 1327136 | tf_op jit(solution)/shard_map/ppermute | solution.py:924
  283.9 2.2 merge_grid.6
  286.1 15.7 %att_bwd.7 = (bf16[1024,768]{1,0:T(8,128)(2,1)}, bf16[8,768]{1,0:T(8,128)(2,1)}, bf16[2048,768]{1,0:T(8,128)(2,1)}, bf16[2048,768]{1,0:T(8,128)(2,1)}, f32[16,768]{1,0:T(8,128)}) custom-call(s32[1]{0:T(128)S(6)} %select_n.120.refs_0_.state_ref, ...), custom_call_target="tpu_custom_call", output_to_operand_aliasing={{0}: (12, {}), {1}: (13, {}), {2}: (14, {}), {3}: (15, {}),... | custom-call | flops 16106127360 | bytes 11010048 | tf_op jit(solution)/shard_map/att_bwd/pallas_call | solution.py:309
  301.8 8.0 %before_bwd.1 = (bf16[1024,768]{1,0:T(8,128)(2,1)}, f32[1,768]{1,0:T(1,128)}) custom-call(bf16[2048,768]{1,0:T(8,128)(2,1)} %copy-done.19, bf16[8,768]{1,0:T(8,128)(2,1)} %get-tuple-element.153.dt_ref.refs_3_, bf16[2048,768]{1,0:T(8,128)(2,1)} %get-tuple-element.154.dk_ref.refs_4_, bf16[2048,768]{1,0:T(8,128)(2,1)} %get-tuple-element.155.dv_ref.refs_5_, ...), custom_call_target="tpu_custom_call" | custom-call | flops 2415919104 | bytes 9437184 | tf_op jit(solution)/shard_map/before_bwd/pallas_call | solution.py:388
  311.2 1.7 merge_grid.7
  313.0 6.4 %collective-permute-start.17 = (bf16[1,288,768]{2,1,0:T(8,128)(2,1)}, bf16[1,288,768]{2,1,0:T(8,128)(2,1)S(1)}, u32[]{:S(2)}, u32[]{:S(2)}) collective-permute-start(bf16[1,288,768]{2,1,0:T(8,128)(2,1)} %get-tuple-element.151), channel_id=1, source_target_pairs={{0,16},{1,17},{2,18},{3,19},{4,20},{5,21},{6,22},{7,23},{8,24},{9,... | collective-permute-start | bytes 1327112 | tf_op jit(solution)/shard_map/ppermute | solution.py:924
  319.4 19.3 %qkv_bwd.1 = (bf16[1232,768]{1,0:T(8,128)(2,1)}, f32[1232,768]{1,0:T(8,128)}, f32[1024,768]{1,0:T(8,128)}) custom-call(s32[1]{0:T(128)} %bitcast.24.refs_0_.index_ref, bf16[2048,768]{1,0:T(8,128)(2,1)} %copy-done.19, bf16[1024,768]{1,0:T(8,128)(2,1)} %get-tuple-element.159.refs_2_, bf16[8,768]{1,0:T(8,128)(2,1)} %get-tuple-element.153.dt_ref.refs_3_, ...), custom_call_target="tpu_custom_call" | custom-call | flops 9663676416 | bytes 23592960 | tf_op jit(solution)/shard_map/qkv_bwd/pallas_call | solution.py:483
  338.7 4.6 %collective-permute-start.18 = (bf16[1232,768]{1,0:T(8,128)(2,1)}, bf16[1232,768]{1,0:T(8,128)(2,1)S(1)}, u32[]{:S(2)}, u32[]{:S(2)}) collective-permute-start(bf16[1232,768]{1,0:T(8,128)(2,1)} %get-tuple-element.167), channel_id=1, source_target_pairs={{0,1},{1,0},{2,3},{3,2},{4,5},{5,4},{6,7},{7,6},{8,9},{9,8},{10,11... | collective-permute-start | bytes 5677064 | tf_op jit(solution)/shard_map/ppermute | solution.py:924
  343.8 3.2 collective-permute-done.18.got_ref
  347.0 2.1 copy-done.3
  349.1 1.8 merge.4
  350.9 10.7 %collective-permute-start.20 = (bf16[624,768]{1,0:T(8,128)(2,1)}, bf16[624,768]{1,0:T(8,128)(2,1)S(1)}, u32[]{:S(2)}, u32[]{:S(2)}) collective-permute-start(bf16[624,768]{1,0:T(8,128)(2,1)} %get-tuple-element.168), channel_id=1, source_target_pairs={{0,2},{1,5},{2,0},{3,7},{4,6},{5,1},{6,4},{7,3},{8,10},{9,13},{10,... | collective-permute-start | bytes 2875400 | tf_op jit(solution)/shard_map/ppermute | solution.py:924
  361.9 3.9 fusion.2
  368.0 2.4 reshape.115
  370.4 3.2 collective-permute-done.20.got_ref
  376.1 2.4 collective-permute-done.19
  378.5 4.7 %collective-permute-done.21.got_ref = bf16[320,768]{1,0:T(8,128)(2,1)S(1)} collective-permute-done((bf16[320,768]{1,0:T(8,128)(2,1)S(1)}, bf16[320,768]{1,0:T(8,128)(2,1)S(1)}, u32[]{:S(2)}, u32[]{:S(2)}) %collective-permute-start.21) | collective-permute-done | bytes 491552 | tf_op jit(solution)/shard_map/ppermute | solution.py:924
  383.7 5.0 %fusion.5 = f32[1024,768]{1,0:T(8,128)} fusion(f32[1024,768]{1,0:T(8,128)} %get-tuple-element.114, bf16[1024,768]{1,0:T(8,128)(2,1)S(1)} %copy-done.14, f32[1024,768]{1,0:T(8,128)S(1)} %copy-done.15, bf16[1024,768]{1,0:T(8,128)(2,1)} %collective-permute-done.16, f32[1024]{0:T(1024)S(1)} %broadcast_multiply_fusion, f32[768]{0:T(1024)S(1)} %get-tuple-element.182, ...), kind=kLoop, calls=%fused_computation.7 | loop fusion | flops 7077888 | bytes 12594176 | tf_op jit(solution)/shard_map/add | solution.py:1158
  388.7 7.3 %collective-permute-done.22.got_ref = bf16[320,768]{1,0:T(8,128)(2,1)S(1)} collective-permute-done((bf16[320,768]{1,0:T(8,128)(2,1)S(1)}, bf16[320,768]{1,0:T(8,128)(2,1)S(1)}, u32[]{:S(2)}, u32[]{:S(2)}) %collective-permute-start.22) | collective-permute-done | bytes 491552 | tf_op jit(solution)/shard_map/ppermute | solution.py:924
  398.2 12.5 %collective-permute-done.23 = bf16[320,768]{1,0:T(8,128)(2,1)S(1)} collective-permute-done((bf16[320,768]{1,0:T(8,128)(2,1)S(1)}, bf16[320,768]{1,0:T(8,128)(2,1)S(1)}, u32[]{:S(2)}, u32[]{:S(2)}) %collective-permute-start.23) | collective-permute-done | bytes 491552 | tf_op jit(solution)/shard_map/ppermute | solution.py:924
  411.9 3.5 fusion.16
  (125 shorter events, 24.8 us)
Async XLA Ops:
  1.5 4.8 %collective-permute-start = (bf16[96,128]{1,0:T(8,128)(2,1)S(1)}, bf16[96,128]{1,0:T(8,128)(2,1)S(1)}, u32[]{:S(2)}, u32[]{:S(2)}) collective-permute-start(bf16[96,128]{1,0:T(8,128)(2,1)S(1)} %slice.25), channel_id=1, source_target_pairs={{0,1},{1,2},{2,3},{3,4},{4,5},{5,6},{6,7},{7,8},{8,9},{9,10},{10,1... | collective-permute-start | bytes 73736 | tf_op jit(solution)/shard_map/ppermute | solution.py:904
  6.2 2.6 copy-start.22
  6.3 2.6 copy-start.12
  8.8 9.0 %collective-permute-start.3 = (bf16[1024,768]{1,0:T(8,128)(2,1)S(1)}, bf16[1024,768]{1,0:T(8,128)(2,1)S(1)}, u32[]{:S(2)}, u32[]{:S(2)}) collective-permute-start(bf16[1024,768]{1,0:T(8,128)(2,1)S(1)} %copy-done.12), channel_id=1, source_target_pairs={{0,1},{1,2},{2,3},{4,5},{5,6},{6,7},{8,9},{9,10},{10,11},{12,13},{... | collective-permute-start | bytes 4718600 | tf_op jit(solution)/shard_map/ppermute | solution.py:910
  13.4 24.2 %collective-permute-start.2 = (bf16[304,768]{1,0:T(8,128)(2,1)S(1)}, bf16[304,768]{1,0:T(8,128)(2,1)S(1)}, u32[]{:S(2)}, u32[]{:S(2)}) collective-permute-start(bf16[304,768]{1,0:T(8,128)(2,1)S(1)} %pad_maximum_fusion.1.refs_0_), channel_id=1, source_target_pairs={{0,16},{1,17},{2,18},{3,19},{4,20},{5,21},{6,22},{7,23},{8,24},{9,... | collective-permute-start | bytes 1400840 | tf_op jit(solution)/shard_map/ppermute | solution.py:924
  16.3 22.0 %collective-permute-start.1 = (bf16[304,768]{1,0:T(8,128)(2,1)S(1)}, bf16[304,768]{1,0:T(8,128)(2,1)S(1)}, u32[]{:S(2)}, u32[]{:S(2)}) collective-permute-start(bf16[304,768]{1,0:T(8,128)(2,1)S(1)} %pad_maximum_fusion.1.refs_0_), channel_id=1, source_target_pairs={{0,8},{1,9},{2,10},{3,11},{4,12},{5,13},{6,14},{7,15},{8,0},{9,1},... | collective-permute-start | bytes 1400840 | tf_op jit(solution)/shard_map/ppermute | solution.py:924
  18.1 19.6 %copy-start.19 = (bf16[2048,768]{1,0:T(8,128)(2,1)}, bf16[2048,768]{1,0:T(8,128)(2,1)S(1)}, u32[]{:S(2)}) copy-start(bf16[2048,768]{1,0:T(8,128)(2,1)S(1)} %constant_dynamic-update-slice_fusion.refs_1_.x_ref) | copy-start | bytes 9437188
  37.7 12.3 %collective-permute-start.4 = (bf16[304,768]{1,0:T(8,128)(2,1)S(1)}, bf16[304,768]{1,0:T(8,128)(2,1)S(1)}, u32[]{:S(2)}, u32[]{:S(2)}) collective-permute-start(bf16[304,768]{1,0:T(8,128)(2,1)S(1)} %collective-permute-done.2.refs_2_), channel_id=1, source_target_pairs={{0,8},{1,9},{2,10},{3,11},{4,12},{5,13},{6,14},{7,15},{8,0},{9,1},... | collective-permute-start | bytes 1400840 | tf_op jit(solution)/shard_map/ppermute | solution.py:924
  50.7 1.0 copy-start.9
  53.8 39.4 %copy-start.6 = (bf16[864,768]{1,0:T(8,128)(2,1)}, bf16[864,768]{1,0:T(8,128)(2,1)S(1)}, u32[]{:S(2)}) copy-start(bf16[864,768]{1,0:T(8,128)(2,1)S(1)} %get-tuple-element.97.own_ref) | copy-start | bytes 3981316
  53.8 8.6 %collective-permute-start.5 = (bf16[304,768]{1,0:T(8,128)(2,1)S(1)}, bf16[304,768]{1,0:T(8,128)(2,1)S(1)}, u32[]{:S(2)}, u32[]{:S(2)}) collective-permute-start(bf16[304,768]{1,0:T(8,128)(2,1)S(1)} %get-tuple-element.95.own_ref), channel_id=1, source_target_pairs={{0,2},{1,5},{2,0},{3,7},{4,6},{5,1},{6,4},{7,3},{8,10},{9,13},{10,... | collective-permute-start | bytes 1400840 | tf_op jit(solution)/shard_map/ppermute | solution.py:924
  62.5 13.4 %collective-permute-start.6 = (bf16[592,768]{1,0:T(8,128)(2,1)S(1)}, bf16[592,768]{1,0:T(8,128)(2,1)S(1)}, u32[]{:S(2)}, u32[]{:S(2)}) collective-permute-start(bf16[592,768]{1,0:T(8,128)(2,1)S(1)} %join.2.own_ref), channel_id=1, source_target_pairs={{0,4},{1,3},{2,6},{3,1},{4,0},{5,7},{6,2},{7,5},{8,12},{9,11},{10,... | collective-permute-start | bytes 2727944 | tf_op jit(solution)/shard_map/ppermute | solution.py:924
  76.0 3.9 copy-start.5
  76.0 3.9 collective-permute-start.7
  76.1 18.0 %collective-permute-start.8 = (bf16[864,768]{1,0:T(8,128)(2,1)S(1)}, bf16[864,768]{1,0:T(8,128)(2,1)}, u32[]{:S(2)}, u32[]{:S(2)}) collective-permute-start(bf16[864,768]{1,0:T(8,128)(2,1)S(1)} %get-tuple-element.97.own_ref), channel_id=1, source_target_pairs={{0,2},{1,5},{2,0},{3,7},{4,6},{5,1},{6,4},{7,3},{8,10},{9,13},{10,... | collective-permute-start | bytes 3981320 | tf_op jit(solution)/shard_map/ppermute | solution.py:924
  94.0 1.3 copy-start.7
  97.1 20.1 %copy-start.4 = (bf16[1728,768]{1,0:T(8,128)(2,1)}, bf16[1728,768]{1,0:T(8,128)(2,1)S(1)}, u32[]{:S(2)}) copy-start(bf16[1728,768]{1,0:T(8,128)(2,1)S(1)} %join_held.1) | copy-start | bytes 7962628
  97.1 20.1 %collective-permute-start.10 = (bf16[1728,768]{1,0:T(8,128)(2,1)S(1)}, bf16[1728,768]{1,0:T(8,128)(2,1)S(1)}, u32[]{:S(2)}, u32[]{:S(2)}) collective-permute-start(bf16[1728,768]{1,0:T(8,128)(2,1)S(1)} %join_held.1), channel_id=1, source_target_pairs={{0,1},{1,0},{2,3},{3,2},{4,5},{5,4},{6,7},{7,6},{8,9},{9,8},{10,11... | collective-permute-start | bytes 7962632 | tf_op jit(solution)/shard_map/ppermute | solution.py:924
  97.2 37.2 %collective-permute-start.9 = (bf16[1728,768]{1,0:T(8,128)(2,1)S(1)}, bf16[1728,768]{1,0:T(8,128)(2,1)}, u32[]{:S(2)}, u32[]{:S(2)}) collective-permute-start(bf16[1728,768]{1,0:T(8,128)(2,1)S(1)} %join_held.1), channel_id=1, source_target_pairs={{0,4},{1,3},{2,6},{3,1},{4,0},{5,7},{6,2},{7,5},{8,12},{9,11},{10,... | collective-permute-start | bytes 7962632 | tf_op jit(solution)/shard_map/ppermute | solution.py:924
  117.3 17.1 %copy-start.24 = (bf16[1728,768]{1,0:T(8,128)(2,1)}, bf16[1728,768]{1,0:T(8,128)(2,1)S(1)}, u32[]{:S(2)}) copy-start(bf16[1728,768]{1,0:T(8,128)(2,1)S(1)} %collective-permute-done.10) | copy-start | bytes 7962628
  134.4 18.5 %collective-permute-start.11 = (bf16[1728,768]{1,0:T(8,128)(2,1)}, bf16[1728,768]{1,0:T(8,128)(2,1)S(1)}, u32[]{:S(2)}, u32[]{:S(2)}) collective-permute-start(bf16[1728,768]{1,0:T(8,128)(2,1)} %hold.1), channel_id=1, source_target_pairs={{0,1},{1,0},{2,3},{3,2},{4,5},{5,4},{6,7},{7,6},{8,9},{9,8},{10,11... | collective-permute-start | bytes 7962632 | tf_op jit(solution)/shard_map/ppermute | solution.py:924
  152.9 1.5 copy-start.25
  209.6 10.0 %collective-permute-start.12 = (bf16[12,288,768]{2,1,0:T(8,128)(2,1)}, bf16[12,288,768]{2,1,0:T(8,128)(2,1)}, u32[]{:S(2)}, u32[]{:S(2)}) collective-permute-start(bf16[12,288,768]{2,1,0:T(8,128)(2,1)} %bitcast.76), channel_id=1, source_target_pairs={{0,1},{1,0},{2,3},{3,2},{4,5},{5,4},{6,7},{7,6},{8,9},{9,8},{10,11... | collective-permute-start | bytes 15925256 | tf_op jit(solution)/shard_map/ppermute | solution.py:924
  210.3 9.4 %slice-start = ((s8[5308416]{0:T(1024)(128)(4,1)}), s8[4194304]{0:T(1024)(128)(4,1)S(1)}, s32[]{:S(2)}) async-start(s8[5308416]{0:T(1024)(128)(4,1)} %bitcast.69), calls=%async_computation | async-start | bytes 8388608
  210.3 9.4 %slice-start.1 = ((s8[5308416]{0:T(1024)(128)(4,1)}), s8[1114112]{0:T(1024)(128)(4,1)S(1)}, s32[]{:S(2)}) async-start(s8[5308416]{0:T(1024)(128)(4,1)} %bitcast.69), calls=%async_computation.1 | async-start | bytes 2228224
  227.1 35.9 %collective-permute-start.13 = (bf16[6,288,768]{2,1,0:T(8,128)(2,1)}, bf16[6,288,768]{2,1,0:T(8,128)(2,1)S(1)}, u32[]{:S(2)}, u32[]{:S(2)}) collective-permute-start(bf16[6,288,768]{2,1,0:T(8,128)(2,1)} %get-tuple-element.124), channel_id=1, source_target_pairs={{0,2},{1,5},{2,0},{3,7},{4,6},{5,1},{6,4},{7,3},{8,10},{9,13},{10,... | collective-permute-start | bytes 7962632 | tf_op jit(solution)/shard_map/ppermute | solution.py:924
  232.9 30.1 %copy-start = (bf16[6,288,768]{2,1,0:T(8,128)(2,1)S(1)}, bf16[6,288,768]{2,1,0:T(8,128)(2,1)}, u32[]{:S(2)}) copy-start(bf16[6,288,768]{2,1,0:T(8,128)(2,1)} %get-tuple-element.132.ka_ref.kb_ref) | copy-start | bytes 7962628
  265.9 18.0 %collective-permute-start.14 = (bf16[3,288,768]{2,1,0:T(8,128)(2,1)}, bf16[3,288,768]{2,1,0:T(8,128)(2,1)S(1)}, u32[]{:S(2)}, u32[]{:S(2)}) collective-permute-start(bf16[3,288,768]{2,1,0:T(8,128)(2,1)} %get-tuple-element.133), channel_id=1, source_target_pairs={{0,4},{1,3},{2,6},{3,1},{4,0},{5,7},{6,2},{7,5},{8,12},{9,11},{10,... | collective-permute-start | bytes 3981320 | tf_op jit(solution)/shard_map/ppermute | solution.py:924
  266.0 17.9 %copy-start.1 = (f32[3,288,768]{2,1,0:T(8,128)S(1)}, f32[3,288,768]{2,1,0:T(8,128)}, u32[]{:S(2)}) copy-start(f32[3,288,768]{2,1,0:T(8,128)} %get-tuple-element.141.ka_ref.kb_ref) | copy-start | bytes 7962628
  286.1 25.1 %collective-permute-start.15 = (bf16[2,288,768]{2,1,0:T(8,128)(2,1)}, bf16[2,288,768]{2,1,0:T(8,128)(2,1)S(1)}, u32[]{:S(2)}, u32[]{:S(2)}) collective-permute-start(bf16[2,288,768]{2,1,0:T(8,128)(2,1)} %get-tuple-element.142), channel_id=1, source_target_pairs={{0,8},{1,9},{2,10},{3,11},{4,12},{5,13},{6,14},{7,15},{8,0},{9,1},... | collective-permute-start | bytes 2654216 | tf_op jit(solution)/shard_map/ppermute | solution.py:924
  301.8 9.4 %copy-start.2 = (f32[2,288,768]{2,1,0:T(8,128)S(1)}, f32[2,288,768]{2,1,0:T(8,128)}, u32[]{:S(2)}) copy-start(f32[2,288,768]{2,1,0:T(8,128)} %get-tuple-element.150.ka_ref.kb_ref) | copy-start | bytes 5308420
  309.9 28.8 %collective-permute-start.16 = (bf16[1024,768]{1,0:T(8,128)(2,1)}, bf16[1024,768]{1,0:T(8,128)(2,1)}, u32[]{:S(2)}, u32[]{:S(2)}) collective-permute-start(bf16[1024,768]{1,0:T(8,128)(2,1)} %get-tuple-element.157), channel_id=1, source_target_pairs={{1,0},{2,1},{3,2},{5,4},{6,5},{7,6},{9,8},{10,9},{11,10},{13,12},{... | collective-permute-start | bytes 4718600 | tf_op jit(solution)/shard_map/ppermute | solution.py:910
  313.0 25.7 %collective-permute-start.17 = (bf16[1,288,768]{2,1,0:T(8,128)(2,1)}, bf16[1,288,768]{2,1,0:T(8,128)(2,1)S(1)}, u32[]{:S(2)}, u32[]{:S(2)}) collective-permute-start(bf16[1,288,768]{2,1,0:T(8,128)(2,1)} %get-tuple-element.151), channel_id=1, source_target_pairs={{0,16},{1,17},{2,18},{3,19},{4,20},{5,21},{6,22},{7,23},{8,24},{9,... | collective-permute-start | bytes 1327112 | tf_op jit(solution)/shard_map/ppermute | solution.py:924
  319.4 24.0 %copy-start.13 = (bf16[1024,768]{1,0:T(8,128)(2,1)S(1)}, bf16[1024,768]{1,0:T(8,128)(2,1)}, u32[]{:S(2)}) copy-start(bf16[1024,768]{1,0:T(8,128)(2,1)} %x_ref.1) | copy-start | bytes 4718596
  338.7 8.3 %collective-permute-start.18 = (bf16[1232,768]{1,0:T(8,128)(2,1)}, bf16[1232,768]{1,0:T(8,128)(2,1)S(1)}, u32[]{:S(2)}, u32[]{:S(2)}) collective-permute-start(bf16[1232,768]{1,0:T(8,128)(2,1)} %get-tuple-element.167), channel_id=1, source_target_pairs={{0,1},{1,0},{2,3},{3,2},{4,5},{5,4},{6,7},{7,6},{8,9},{9,8},{10,11... | collective-permute-start | bytes 5677064 | tf_op jit(solution)/shard_map/ppermute | solution.py:924
  343.8 17.9 %copy-start.23 = (pred[3]{0:T(512)(128)(4,1)S(1)}, pred[3]{0:T(512)(128)(4,1)}, u32[]{:S(2)}) copy-start(pred[3]{0:T(512)(128)(4,1)} %copy-done.22) | copy-start | bytes 13
  347.0 2.1 copy-start.3
  350.9 22.7 %collective-permute-start.20 = (bf16[624,768]{1,0:T(8,128)(2,1)}, bf16[624,768]{1,0:T(8,128)(2,1)S(1)}, u32[]{:S(2)}, u32[]{:S(2)}) collective-permute-start(bf16[624,768]{1,0:T(8,128)(2,1)} %get-tuple-element.168), channel_id=1, source_target_pairs={{0,2},{1,5},{2,0},{3,7},{4,6},{5,1},{6,4},{7,3},{8,10},{9,13},{10,... | collective-permute-start | bytes 2875400 | tf_op jit(solution)/shard_map/ppermute | solution.py:924
  361.9 3.9 copy-start.21
  370.4 4.0 copy-start.18
  370.4 4.0 copy-start.20
  373.6 10.1 %copy-start.14 = (bf16[1024,768]{1,0:T(8,128)(2,1)S(1)}, bf16[1024,768]{1,0:T(8,128)(2,1)}, u32[]{:S(2)}) copy-start(bf16[1024,768]{1,0:T(8,128)(2,1)} %x_ref.1) | copy-start | bytes 4718596
  373.6 10.1 %copy-start.15 = (f32[1024,768]{1,0:T(8,128)S(1)}, f32[1024,768]{1,0:T(8,128)}, u32[]{:S(2)}) copy-start(f32[1024,768]{1,0:T(8,128)} %get-tuple-element.162) | copy-start | bytes 9437188
  374.4 8.9 %collective-permute-start.21 = (bf16[320,768]{1,0:T(8,128)(2,1)S(1)}, bf16[320,768]{1,0:T(8,128)(2,1)S(1)}, u32[]{:S(2)}, u32[]{:S(2)}) collective-permute-start(bf16[320,768]{1,0:T(8,128)(2,1)S(1)} %get-tuple-element.173), channel_id=1, source_target_pairs={{0,4},{1,3},{2,6},{3,1},{4,0},{5,7},{6,2},{7,5},{8,12},{9,11},{10,... | collective-permute-start | bytes 1474568 | tf_op jit(solution)/shard_map/ppermute | solution.py:924
  374.6 3.9 collective-permute-start.19
  383.4 12.7 %collective-permute-start.22 = (bf16[320,768]{1,0:T(8,128)(2,1)S(1)}, bf16[320,768]{1,0:T(8,128)(2,1)S(1)}, u32[]{:S(2)}, u32[]{:S(2)}) collective-permute-start(bf16[320,768]{1,0:T(8,128)(2,1)S(1)} %get-tuple-element.175), channel_id=1, source_target_pairs={{0,8},{1,9},{2,10},{3,11},{4,12},{5,13},{6,14},{7,15},{8,0},{9,1},... | collective-permute-start | bytes 1474568 | tf_op jit(solution)/shard_map/ppermute | solution.py:924
  396.2 14.5 %collective-permute-start.23 = (bf16[320,768]{1,0:T(8,128)(2,1)S(1)}, bf16[320,768]{1,0:T(8,128)(2,1)S(1)}, u32[]{:S(2)}, u32[]{:S(2)}) collective-permute-start(bf16[320,768]{1,0:T(8,128)(2,1)S(1)} %get-tuple-element.177), channel_id=1, source_target_pairs={{8,24},{9,25},{10,26},{11,27},{12,28},{13,29},{14,30},{15,31},{16,... | collective-permute-start | bytes 1474568 | tf_op jit(solution)/shard_map/ppermute | solution.py:924
  410.8 1.2 copy-start.16
  (4 other events, 3.5 us)

commit v13 on v12

--- a/solution.py
+++ b/solution.py
@@ -398,13 +398,13 @@
 
 
 def qkv_bwd_kernel(
-    core_ref, x_ref, dq_ref, dt_ref, dk_ref, dv_ref, w_ref, gain_ref, gain_one_ref, gain_two_ref, tg_ref,
+    core_ref, x_ref, dq_ref, dt_ref, dk_ref, dv_ref, w_ref, small_ref, gain_one_ref, gain_two_ref, tg_ref,
     *refs, pieces, blocks,
 ):
     if pieces:
         send_ref, keep_ref, own_ref, acc, gacc = refs
     else:
-        keep_ref, small_ref, own_ref, acc, gacc = refs
+        keep_ref, ends_ref, own_ref, acc, gacc = refs
     i = pl.program_id(0)
     half = blocks // 2
 
@@ -414,7 +414,7 @@
         gacc[0:1, :] = gain_one_ref[...]
 
     hat = unit_rows(x_ref[...].astype(F32))
-    low = (hat * gain_ref[...]).astype(BF)
+    low = (hat * small_ref[0:1, :]).astype(BF)
     dk = dk_ref[...]
     dv = dv_ref[...]
     acc[D : 2 * D, :] += dot_tn(low, dk)
@@ -455,10 +455,10 @@
             keep_ref[pieces * wide :, :] = small
         else:
             keep_ref[...] = acc[0 : 3 * D, :].astype(BF)
-            small_ref[...] = small
-
-
-def qkv_bwd(core, x_both, back, weight, gain, gain_one_grad, gain_two_grad, tap_grads, rows, pieces):
+            ends_ref[...] = small
+
+
+def qkv_bwd(core, x_both, back, weight, small, gain_one_grad, gain_two_grad, tap_grads, rows, pieces):
     dq, dt, dk, dv = back
     blocks = 4
     half = blocks // 2
@@ -486,7 +486,7 @@
         in_specs=[
             pl.BlockSpec(memory_space=pltpu.SMEM),
             step, late, whole((8, D)), step, step, whole((3 * D, D)),
-            whole((1, D)), whole((1, D)), whole((1, D)), whole((16, D)),
+            whole((16, D)), whole((1, D)), whole((1, D)), whole((16, D)),
         ],
         out_specs=out_at + [late],
         out_shape=outs + [jax.ShapeDtypeStruct((rows, D), F32)],
@@ -494,7 +494,7 @@
         compiler_params=pltpu.CompilerParams(vmem_limit_bytes=VMEM_LIMIT),
         cost_estimate=cost(2 * 2 * D * D * 4 * rows, rows * D * 30),
         name="qkv_bwd",
-    )(core, x_both, dq, dt, dk, dv, weight, gain, gain_one_grad, gain_two_grad, tap_grads)
+    )(core, x_both, dq, dt, dk, dv, weight, small, gain_one_grad, gain_two_grad, tap_grads)
 
 
 def merge(index, keep, got, height, taken):
@@ -564,30 +564,42 @@
     height = blocks[0].shape[0] - 16
 
     def body(index_ref, *refs):
-        first_ref, rest_ref = refs[4:]
+        first_ref, rest_ref, ends, total, sems = refs[4:]
         refs = refs[:4]
+        tail = pl.ds(height, 16)
+        places = [first_ref.at[pl.ds(0, height)]] + [rest_ref.at[pl.ds(i * height, height)] for i in range(3)]
+        for k in range(4):
+            pltpu.make_async_copy(refs[k].at[tail], ends.at[k], sems.at[4 + k]).start()
         for i in range(4):
             for k in range(4):
 
                 @pl.when(index_ref[i] == k)
                 def _():
-                    piece = refs[k][0:height, :]
-                    if i == 0:
-                        first_ref[0:height, :] = piece
-                    else:
-                        rest_ref[(i - 1) * height : i * height, :] = piece
-
-        ends = [ref[height:, :].astype(F32) for ref in refs]
-        first_ref[height:, :] = (ends[0] + ends[1] + ends[2] + ends[3]).astype(BF)
-
-    vmem = pl.BlockSpec(memory_space=pltpu.VMEM)
+                    pltpu.make_async_copy(refs[k].at[pl.ds(0, height)], places[i], sems.at[i]).start()
+
+        for k in range(4):
+            pltpu.make_async_copy(refs[k].at[tail], ends.at[k], sems.at[4 + k]).wait()
+        sums = [ends[k].astype(F32) for k in range(4)]
+        total[...] = (sums[0] + sums[1] + sums[2] + sums[3]).astype(BF)
+        last = pltpu.make_async_copy(total, first_ref.at[tail], sems.at[8])
+        last.start()
+        for i in range(4):
+            pltpu.make_async_copy(refs[0].at[pl.ds(0, height)], places[i], sems.at[i]).wait()
+        last.wait()
+
+    held = pl.BlockSpec(memory_space=pltpu.HBM)
     return pl.pallas_call(
         body,
-        in_specs=[pl.BlockSpec(memory_space=pltpu.SMEM)] + [vmem] * 4,
-        out_specs=[vmem, vmem],
+        in_specs=[pl.BlockSpec(memory_space=pltpu.SMEM)] + [held] * 4,
+        out_specs=[held, held],
         out_shape=[
             jax.ShapeDtypeStruct((height + 16, D), BF),
             jax.ShapeDtypeStruct((3 * height, D), BF),
+        ],
+        scratch_shapes=[
+            pltpu.VMEM((4, 16, D), BF),
+            pltpu.VMEM((16, D), BF),
+            pltpu.SemaphoreType.DMA((9,)),
         ],
         compiler_params=pltpu.CompilerParams(vmem_limit_bytes=32 << 20),
         cost_estimate=cost(4 * height * D, 4 * height * D * 4),
@@ -724,7 +736,7 @@
 
 
 def ffn_kernel(
-    state_ref, index_ref, x_ref, att_ref, cot_ref, gain_ref, own_ref, own_two_ref, got_ref, got_two_ref,
+    state_ref, index_ref, x_ref, att_ref, cot_ref, small_ref, own_ref, own_two_ref, got_ref, got_two_ref,
     out_ref, gh_ref, ga_ref, gain_grad_ref, away_ref, here_ref,
     hidden, low, total, back, cot, sq, gb, weights, stage_up, stage_down, stage_out, in_sems, sems,
 ):
@@ -805,7 +817,7 @@
             h = x_ref[b, :].astype(F32) + dot(att_ref[b, :], wo)
             hidden[b, :] = h
             hat = h * lax.rsqrt(jnp.mean(h * h, axis=-1, keepdims=True) + norm_eps)
-            low[b, :] = (hat * gain_ref[...]).astype(BF)
+            low[b, :] = (hat * small_ref[1:2, :]).astype(BF)
 
     for i, pieces in enumerate((range(3, 16), range(16, 19), range(19, 22), range(22, 24))):
 
@@ -830,7 +842,7 @@
 
     @pl.when(last)
     def _():
-        gain = gain_ref[...]
+        gain = small_ref[1:2, :]
         wo = square(0)
         sums = jnp.zeros((1, D), F32)
         for b in blocks:
@@ -856,7 +868,7 @@
         put_out(True)
 
 
-def ffn(state, index, tokens, attended, out_grad, gain, weights, rows):
+def ffn(state, index, tokens, attended, out_grad, small, weights, rows):
     def whole(shape):
         return pl.BlockSpec(shape, lambda c: (0,) * len(shape), pipeline_mode=pl.Buffered(1))
 
@@ -867,7 +879,7 @@
     return pl.pallas_call(
         ffn_kernel,
         grid=(4,),
-        in_specs=[scalars, scalars, act, act, act, whole((1, D)), held, held, held, held],
+        in_specs=[scalars, scalars, act, act, act, whole((16, D)), held, held, held, held],
         out_specs=[act, act, act, whole((1, D)), held, held],
         out_shape=[
             jax.ShapeDtypeStruct((rows, D), BF),
@@ -895,7 +907,7 @@
         compiler_params=pltpu.CompilerParams(vmem_limit_bytes=60 << 20),
         cost_estimate=cost(2 * rows * D * D * (24 + 3), 2 * 12 * D * D * 2 + rows * D * 16),
         name="ffn",
-    )(state, index, tokens, attended, out_grad, gain, *weights)
+    )(state, index, tokens, attended, out_grad, small, *weights)
 
 
 def shift_flat(block, distance):
@@ -1027,7 +1039,11 @@
         in_up = ((group >= 32) & (group < 64))[:, None, None, None]
         chunk = jnp.where(in_up, regroup(chunk), chunk.reshape(3, 4, 24, D)).reshape(-1, D)
     chunk = chunk.astype(BF)
-    small = lax.reduce_precision(small_part(master, place, count, delta), 8, 7)
+    if staged:
+        small = jnp.where(place == count - 1, master[owned - count * delta :], 0.0)
+    else:
+        small = small_part(master, place, count, delta)
+    small = lax.reduce_precision(small, 8, 7)
     core = (place & 1)[None]
     x_bit = (place >> 1) & 1
     y_bit = (place >> 2) & 1
@@ -1041,7 +1057,7 @@
         tokens_both = jnp.concatenate([tokens_before, tokens], 0)
         both = swap(after(far, tokens_both), 8, 8)
         order = jnp.stack([z, z ^ 1, z ^ 2, z ^ 3]).astype(jnp.int32)
-        mine, rest = arrange(order, (mine, near, far, both))
+        mine, rest = arrange(after(order, state_vec), (mine, near, far, both))
         mine = join(mine, swap(mine, 2, 4))
         mine = join(mine, swap(mine, 4, 2))
         across = swap(rest, 2, 4)
@@ -1068,7 +1084,6 @@
         projected, small = qkv_fwd(core, tokens_both, (in_weight, small), rows, 0)
         late_index = jnp.arange(25, dtype=jnp.int32) % 24
     gain_first = small[0]
-    gain_second = small[1]
 
     forward = []
     if staged:
@@ -1096,7 +1111,7 @@
     attn_low, logs, *mixed = forward
 
     layer_out, grad_hidden, grad_attended, grad_gain_two, away_grad, here_grad = ffn(
-        state_vec, late_index, tokens, attn_low, out_grad, gain_second[None], late_weights, rows
+        state_vec, late_index, tokens, attn_low, out_grad, small, late_weights, rows
     )
 
     def backward(start, done, part):
@@ -1150,7 +1165,7 @@
     grads_before, gain_one_grad = before_bwd(tokens_both, back, in_weight, rows)
     from_next = shift_ctx(grads_before, -1)
     sums = qkv_bwd(
-        after(sums_state, grads_before), tokens_both, back, in_weight, gain_first[None], gain_one_grad, grad_gain_two, tap_grads, rows,
+        after(sums_state, grads_before), tokens_both, back, in_weight, small, gain_one_grad, grad_gain_two, tap_grads, rows,
         4 if staged else 0,
     )
     grad_normed_one = sums[2]
@@ -1171,9 +1186,9 @@
         late_next = shift_flat(late_chunk[:16], -1)
         send, keep = merge(pick_line, keep, got, height + 16, 1)
         got = swap(send, 4, 2)
-        send, keep = merge(after(core, late_next), keep, got, height + 16, 0)
+        send, keep = merge(core, keep, got, height + 16, 0)
         got = swap(send, 8, 8)
-        send, keep = merge(after(core, input_grad), keep, got, height + 16, 0)
+        send, keep = merge(after(core, input_grad, late_next), keep, got, height + 16, 0)
         got = swap(send, 16, 16, (1, 2))
         first = keep + got.astype(F32)
         quarter = count // 4

time: 414 us -> 413 us (level)
    unnamed x57 -> x63, local copies, waits for them, and re-layouts: 10.5 us -> 10.4 us
  transfers between devices with their start and end apart: 24 -> 24, of which waited for: 14 -> 12; matrix products, arithmetic and copies ran while one was open for 5% -> 5% of each run, Pallas kernels for 34% -> 35%
where the time goes in v13:
time: 413 us; the launch traced here: 412 us
  Pallas kernels  216 us (52%)
  waiting for transfers between devices  108 us (26%)
  starting transfers between devices  46.8 us (11%)
  local copies, waits for them, and re-layouts  20.6 us (5%)
  other arithmetic  17.5 us (4%)
    ppermute x20, waiting for transfers between devices, swap(): return lax.ppermute(block, AXES, route)  108 us
    pallas_call x1, Pallas kernels, ffn(): pl.pallas_call(ffn_kernel, grid=(4,), in_specs=[scalars, scalars, act, ac...  55 us
    pallas_call x4, Pallas kernels, att_bwd(): call_in_parts(att_bwd_kernel, [pl.BlockSpec(memory_space=pltpu.SMEM), own...  50.3 us
    pallas_call x3, Pallas kernels, att_fwd(): call_in_parts(att_fwd_kernel, [pl.BlockSpec(memory_space=pltpu.SMEM), col...  49.3 us
    ppermute x20, starting transfers between devices, swap(): return lax.ppermute(block, AXES, route)  37.3 us
    pallas_call x1, Pallas kernels, qkv_bwd(): pl.pallas_call(body, grid=(blocks,), in_specs=[pl.BlockSpec(memory_space=...  19.3 us
    pallas_call x4, Pallas kernels, merge_grid(): pl.pallas_call(body, grid_spec=pltpu.PrefetchScalarGridSpec(num_scalar_pr...  14.3 us
    pallas_call x1, Pallas kernels, qkv_fwd(): pl.pallas_call(body, grid=(blocks,), in_specs=[pl.BlockSpec(memory_space=...  13.3 us
  transfers between devices with their start and end apart: 24, of which 12 were waited for; matrix products, arithmetic and copies ran while one was open for 5% of the time, Pallas kernels for 35%

profile of v13, /device:TPU:0, one launch (start us, length us, event | category | flops | bytes accessed | tf_op | source)
XLA Modules:
  0.0 411.7 jit_solution(5122645523640675166)
XLA Ops:
  1.5 2.3 collective-permute-start
  4.7 1.5 fusion.8
  7.3 4.6 %collective-permute-start.3 = (bf16[1024,768]{1,0:T(8,128)(2,1)S(1)}, bf16[1024,768]{1,0:T(8,128)(2,1)S(1)}, u32[]{:S(2)}, u32[]{:S(2)}) collective-permute-start(bf16[1024,768]{1,0:T(8,128)(2,1)S(1)} %copy-done.12), channel_id=1, source_target_pairs={{0,1},{1,2},{2,3},{4,5},{5,6},{6,7},{8,9},{9,10},{10,11},{12,13},{... | collective-permute-start | bytes 4718600 | tf_op jit(solution)/shard_map/ppermute | solution.py:922
  11.9 4.4 %collective-permute-start.2 = (bf16[304,768]{1,0:T(8,128)(2,1)S(1)}, bf16[304,768]{1,0:T(8,128)(2,1)S(1)}, u32[]{:S(2)}, u32[]{:S(2)}) collective-permute-start(bf16[304,768]{1,0:T(8,128)(2,1)S(1)} %pad_maximum_fusion.1.refs_0_), channel_id=1, source_target_pairs={{0,16},{1,17},{2,18},{3,19},{4,20},{5,21},{6,22},{7,23},{8,24},{9,... | collective-permute-start | bytes 1400840 | tf_op jit(solution)/shard_map/ppermute | solution.py:936
  16.3 1.6 collective-permute-start.1
  18.1 19.6 %collective-permute-done.2.refs_2_ = bf16[304,768]{1,0:T(8,128)(2,1)S(1)} collective-permute-done((bf16[304,768]{1,0:T(8,128)(2,1)S(1)}, bf16[304,768]{1,0:T(8,128)(2,1)S(1)}, u32[]{:S(2)}, u32[]{:S(2)}) %collective-permute-start.2) | collective-permute-done | bytes 466976 | tf_op jit(solution)/shard_map/ppermute | solution.py:936
  41.6 8.4 %collective-permute-done.4.refs_3_ = bf16[304,768]{1,0:T(8,128)(2,1)S(1)} collective-permute-done((bf16[304,768]{1,0:T(8,128)(2,1)S(1)}, bf16[304,768]{1,0:T(8,128)(2,1)S(1)}, u32[]{:S(2)}, u32[]{:S(2)}) %collective-permute-start.4) | collective-permute-done | bytes 466976 | tf_op jit(solution)/shard_map/ppermute | solution.py:936
  52.8 2.1 arrange.1
  55.1 8.6 %collective-permute-done.5.got_ref = bf16[304,768]{1,0:T(8,128)(2,1)S(1)} collective-permute-done((bf16[304,768]{1,0:T(8,128)(2,1)S(1)}, bf16[304,768]{1,0:T(8,128)(2,1)S(1)}, u32[]{:S(2)}, u32[]{:S(2)}) %collective-permute-start.5) | collective-permute-done | bytes 466976 | tf_op jit(solution)/shard_map/ppermute | solution.py:936
  65.1 12.0 %collective-permute-done.6.got_ref = bf16[592,768]{1,0:T(8,128)(2,1)S(1)} collective-permute-done((bf16[592,768]{1,0:T(8,128)(2,1)S(1)}, bf16[592,768]{1,0:T(8,128)(2,1)S(1)}, u32[]{:S(2)}, u32[]{:S(2)}) %collective-permute-start.6) | collective-permute-done | bytes 909344 | tf_op jit(solution)/shard_map/ppermute | solution.py:936
  78.2 2.9 collective-permute-done.7.refs_3_
  81.1 13.3 %qkv_fwd.1 = (bf16[2048,2304]{1,0:T(8,128)(2,1)}, f32[16,768]{1,0:T(8,128)}, bf16[2304,768]{1,0:T(8,128)(2,1)}) custom-call(s32[8]{0:T(128)} %stack.217.refs_0_, bf16[2048,768]{1,0:T(8,128)(2,1)} %copy-done.16, bf16[1168,768]{1,0:T(8,128)(2,1)} %copy-done.5, bf16[1168,768]{1,0:T(8,128)(2,1)} %collective-permute-done.7.refs_3_), custom_call_target="tpu_custom_call" | custom-call | flops 7247757312 | bytes 15728640 | tf_op jit(solution)/shard_map/qkv_fwd/pallas_call | solution.py:714
  96.5 1.8 join_held.1
  98.4 1.4 collective-permute-start.9
  99.8 15.9 %att_fwd.3 = (bf16[1024,768]{1,0:T(8,128)(2,1)}, f32[1024,768]{1,0:T(8,128)}, bf16[1024,768]{1,0:T(8,128)(2,1)}, bf16[2048,768]{1,0:T(8,128)(2,1)}, bf16[2048,768]{1,0:T(8,128)(2,1)}) custom-call(s32[1]{0:T(128)S(6)} %select_n.125.refs_0_.state_ref, bf16[2048,2304]{1,0:T(8,128)(2,1)} %get-tuple-element.97.refs_1_.refs_2_.refs_3_.refs_4_.refs_7_.refs_8_.refs_9_.refs_10_, ...), custom_call_target="tpu_custom_call" | custom-call | flops 6442450944 | bytes 7864320 | tf_op jit(solution)/shard_map/att_fwd/pallas_call | solution.py:152
  115.8 17.1 %att_fwd.4 = (bf16[1024,768]{1,0:T(8,128)(2,1)}, f32[1024,768]{1,0:T(8,128)}, bf16[1024,768]{1,0:T(8,128)(2,1)}, bf16[2048,768]{1,0:T(8,128)(2,1)}, bf16[2048,768]{1,0:T(8,128)(2,1)}) custom-call(s32[1]{0:T(128)S(6)} %select_n.125.refs_0_.state_ref, ...), custom_call_target="tpu_custom_call", output_to_operand_aliasing={{0}: (6, {}), {1}: (7, {}), {2}: (8, {}), {3}: (9, {}), {4}... | custom-call | flops 6442450944 | bytes 7864320 | tf_op jit(solution)/shard_map/att_fwd/pallas_call | solution.py:152
  133.7 16.3 %att_fwd.5 = (bf16[1024,768]{1,0:T(8,128)(2,1)}, f32[1024,768]{1,0:T(8,128)}, bf16[1024,768]{1,0:T(8,128)(2,1)}, bf16[2048,768]{1,0:T(8,128)(2,1)}, bf16[2048,768]{1,0:T(8,128)(2,1)}) custom-call(s32[1]{0:T(128)S(6)} %select_n.125.refs_0_.state_ref, ...), custom_call_target="tpu_custom_call", output_to_operand_aliasing={{0}: (6, {}), {1}: (7, {}), {2}: (8, {}), {3}: (9, {}), {4}... | custom-call | flops 6442450944 | bytes 7864320 | tf_op jit(solution)/shard_map/att_fwd/pallas_call | solution.py:152
  150.0 1.5 copy-done.28
  151.5 55.0 %ffn.1 = (bf16[1024,768]{1,0:T(8,128)(2,1)}, f32[1024,768]{1,0:T(8,128)}, bf16[1024,768]{1,0:T(8,128)(2,1)}, f32[1,768]{1,0:T(1,128)}, bf16[36,4,24,768]{3,2,1,0...) custom-call(s32[1]{0:T(128)S(6)} %select_n.125.refs_0_.state_ref, s32[25]{0:T(128)} %stack.211.index_ref, ...), custom_call_target="tpu_custom_call" | custom-call | flops 32614907904 | bytes 40894464 | tf_op jit(solution)/shard_map/ffn/pallas_call | solution.py:879
  207.2 9.3 %att_bwd.4 = (bf16[1024,768]{1,0:T(8,128)(2,1)}, bf16[8,768]{1,0:T(8,128)(2,1)}, bf16[2048,768]{1,0:T(8,128)(2,1)}, bf16[2048,768]{1,0:T(8,128)(2,1)}, f32[16,768]{1,0:T(8,128)}) custom-call(s32[1]{0:T(128)S(6)} %select_n.125.refs_0_.state_ref, bf16[1024,768]{1,0:T(8,128)(2,1)} %get-tuple-element.116.refs_1_, bf16[2048,768]{1,0:T(8,128)(2,1)} %get-tuple-element.117.refs_2_, ...), custom_call_target="tpu_custom_call" | custom-call | flops 8053063680 | bytes 5505024 | tf_op jit(solution)/shard_map/att_bwd/pallas_call | solution.py:309
  216.6 7.4 %merge_grid.4 = (bf16[6,288,768]{2,1,0:T(8,128)(2,1)}, bf16[6,288,768]{2,1,0:T(8,128)(2,1)}) custom-call(s32[12]{0:T(128)S(1)} %stack.243.index_ref, bf16[12,288,768]{2,1,0:T(8,128)(2,1)S(1)} %bitcast.71, bf16[12,288,768]{2,1,0:T(8,128)(2,1)} %collective-permute-done.12.ga_ref.gb_ref, bf16[12,288,768]{2,1,0:T(8,128)(2,1)S(1)} %bitcast.72, ...), custom_call_target="tpu_custom_call" | custom-call | flops 2654208 | bytes 21233664 | tf_op jit(solution)/shard_map/merge_grid/pallas_call | solution.py:545
  224.0 5.9 %collective-permute-start.13 = (bf16[6,288,768]{2,1,0:T(8,128)(2,1)}, bf16[6,288,768]{2,1,0:T(8,128)(2,1)S(1)}, u32[]{:S(2)}, u32[]{:S(2)}) collective-permute-start(bf16[6,288,768]{2,1,0:T(8,128)(2,1)} %get-tuple-element.125), channel_id=1, source_target_pairs={{0,2},{1,5},{2,0},{3,7},{4,6},{5,1},{6,4},{7,3},{8,10},{9,13},{10,... | collective-permute-start | bytes 7962632 | tf_op jit(solution)/shard_map/ppermute | solution.py:936
  230.0 15.8 %att_bwd.5 = (bf16[1024,768]{1,0:T(8,128)(2,1)}, bf16[8,768]{1,0:T(8,128)(2,1)}, bf16[2048,768]{1,0:T(8,128)(2,1)}, bf16[2048,768]{1,0:T(8,128)(2,1)}, f32[16,768]{1,0:T(8,128)}) custom-call(s32[1]{0:T(128)S(6)} %select_n.125.refs_0_.state_ref, ...), custom_call_target="tpu_custom_call", output_to_operand_aliasing={{0}: (12, {}), {1}: (13, {}), {2}: (14, {}), {3}: (15, {}),... | custom-call | flops 16106127360 | bytes 11010048 | tf_op jit(solution)/shard_map/att_bwd/pallas_call | solution.py:309
  245.8 14.3 %collective-permute-done.13.ga_ref.gb_ref = bf16[6,288,768]{2,1,0:T(8,128)(2,1)S(1)} collective-permute-done((bf16[6,288,768]{2,1,0:T(8,128)(2,1)}, bf16[6,288,768]{2,1,0:T(8,128)(2,1)S(1)}, u32[]{:S(2)}, u32[]{:S(2)}) %collective-permute-start.13) | collective-permute-done | bytes 2654240 | tf_op jit(solution)/shard_map/ppermute | solution.py:936
  260.1 3.0 merge_grid.5
  263.1 9.5 %att_bwd.6 = (bf16[1024,768]{1,0:T(8,128)(2,1)}, bf16[8,768]{1,0:T(8,128)(2,1)}, bf16[2048,768]{1,0:T(8,128)(2,1)}, bf16[2048,768]{1,0:T(8,128)(2,1)}, f32[16,768]{1,0:T(8,128)}) custom-call(s32[1]{0:T(128)S(6)} %select_n.125.refs_0_.state_ref, ...), custom_call_target="tpu_custom_call", output_to_operand_aliasing={{0}: (12, {}), {1}: (13, {}), {2}: (14, {}), {3}: (15, {}),... | custom-call | flops 8053063680 | bytes 5505024 | tf_op jit(solution)/shard_map/att_bwd/pallas_call | solution.py:309
  272.6 8.5 %collective-permute-done.14.ga_ref.gb_ref = bf16[3,288,768]{2,1,0:T(8,128)(2,1)S(1)} collective-permute-done((bf16[3,288,768]{2,1,0:T(8,128)(2,1)}, bf16[3,288,768]{2,1,0:T(8,128)(2,1)S(1)}, u32[]{:S(2)}, u32[]{:S(2)}) %collective-permute-start.14) | collective-permute-done | bytes 1327136 | tf_op jit(solution)/shard_map/ppermute | solution.py:936
  281.1 2.2 merge_grid.6
  283.2 15.7 %att_bwd.7 = (bf16[1024,768]{1,0:T(8,128)(2,1)}, bf16[8,768]{1,0:T(8,128)(2,1)}, bf16[2048,768]{1,0:T(8,128)(2,1)}, bf16[2048,768]{1,0:T(8,128)(2,1)}, f32[16,768]{1,0:T(8,128)}) custom-call(s32[1]{0:T(128)S(6)} %select_n.125.refs_0_.state_ref, ...), custom_call_target="tpu_custom_call", output_to_operand_aliasing={{0}: (12, {}), {1}: (13, {}), {2}: (14, {}), {3}: (15, {}),... | custom-call | flops 16106127360 | bytes 11010048 | tf_op jit(solution)/shard_map/att_bwd/pallas_call | solution.py:309
  298.9 8.0 %before_bwd.1 = (bf16[1024,768]{1,0:T(8,128)(2,1)}, f32[1,768]{1,0:T(1,128)}) custom-call(bf16[2048,768]{1,0:T(8,128)(2,1)} %copy-done.16, bf16[8,768]{1,0:T(8,128)(2,1)} %get-tuple-element.154.dt_ref.refs_3_, bf16[2048,768]{1,0:T(8,128)(2,1)} %get-tuple-element.155.dk_ref.refs_4_, bf16[2048,768]{1,0:T(8,128)(2,1)} %get-tuple-element.156.dv_ref.refs_5_, ...), custom_call_target="tpu_custom_call" | custom-call | flops 2415919104 | bytes 9437184 | tf_op jit(solution)/shard_map/before_bwd/pallas_call | solution.py:388
  308.4 1.7 merge_grid.7
  310.1 2.4 collective-permute-start.17
  312.5 19.3 %qkv_bwd.1 = (bf16[1232,768]{1,0:T(8,128)(2,1)}, f32[1232,768]{1,0:T(8,128)}, f32[1024,768]{1,0:T(8,128)}) custom-call(s32[1]{0:T(128)} %bitcast.24.refs_0_.index_ref, bf16[2048,768]{1,0:T(8,128)(2,1)} %copy-done.16, bf16[1024,768]{1,0:T(8,128)(2,1)} %get-tuple-element.160.refs_2_, bf16[8,768]{1,0:T(8,128)(2,1)} %get-tuple-element.154.dt_ref.refs_3_, ...), custom_call_target="tpu_custom_call" | custom-call | flops 9663676416 | bytes 23592960 | tf_op jit(solution)/shard_map/qkv_bwd/pallas_call | solution.py:483
  332.6 7.8 %collective-permute-start.18 = (bf16[1232,768]{1,0:T(8,128)(2,1)}, bf16[1232,768]{1,0:T(8,128)(2,1)S(1)}, u32[]{:S(2)}, u32[]{:S(2)}) collective-permute-start(bf16[1232,768]{1,0:T(8,128)(2,1)} %get-tuple-element.167), channel_id=1, source_target_pairs={{0,1},{1,0},{2,3},{3,2},{4,5},{5,4},{6,7},{7,6},{8,9},{9,8},{10,11... | collective-permute-start | bytes 5677064 | tf_op jit(solution)/shard_map/ppermute | solution.py:936
  341.1 3.0 collective-permute-done.18.got_ref
  344.1 2.1 copy-done.3
  347.1 6.7 %collective-permute-start.20 = (bf16[624,768]{1,0:T(8,128)(2,1)S(1)}, bf16[624,768]{1,0:T(8,128)(2,1)S(1)}, u32[]{:S(2)}, u32[]{:S(2)}) collective-permute-start(bf16[624,768]{1,0:T(8,128)(2,1)S(1)} %get-tuple-element.168), channel_id=1, source_target_pairs={{0,2},{1,5},{2,0},{3,7},{4,6},{5,1},{6,4},{7,3},{8,10},{9,13},{10,... | collective-permute-start | bytes 2875400 | tf_op jit(solution)/shard_map/ppermute | solution.py:936
  354.6 2.6 fusion.2
  357.2 8.4 %collective-permute-done.20.got_ref = bf16[624,768]{1,0:T(8,128)(2,1)S(1)} collective-permute-done((bf16[624,768]{1,0:T(8,128)(2,1)S(1)}, bf16[624,768]{1,0:T(8,128)(2,1)S(1)}, u32[]{:S(2)}, u32[]{:S(2)}) %collective-permute-start.20) | collective-permute-done | bytes 958496 | tf_op jit(solution)/shard_map/ppermute | solution.py:936
  367.5 2.4 copy.44
  369.9 2.4 reshape.115
  372.3 1.7 bitcast_select_fusion
  375.5 2.7 collective-permute-start.22
  378.2 5.0 %fusion.5 = f32[1024,768]{1,0:T(8,128)} fusion(f32[1024,768]{1,0:T(8,128)} %get-tuple-element.115, bf16[1024,768]{1,0:T(8,128)(2,1)S(1)} %copy-done.13, f32[1024,768]{1,0:T(8,128)S(1)} %copy-done.15, bf16[1024,768]{1,0:T(8,128)(2,1)} %collective-permute-done.16, f32[1024]{0:T(1024)S(1)} %broadcast_multiply_fusion, f32[768]{0:T(1024)S(1)} %slice_reduce_fusion, ...), kind=kLoop, calls=%fused_computation.7 | loop fusion | flops 7077888 | bytes 12594176 | tf_op jit(solution)/shard_map/add | solution.py:1173
  383.2 7.3 %collective-permute-done.22.got_ref = bf16[320,768]{1,0:T(8,128)(2,1)S(1)} collective-permute-done((bf16[320,768]{1,0:T(8,128)(2,1)S(1)}, bf16[320,768]{1,0:T(8,128)(2,1)S(1)}, u32[]{:S(2)}, u32[]{:S(2)}) %collective-permute-start.22) | collective-permute-done | bytes 491552 | tf_op jit(solution)/shard_map/ppermute | solution.py:936
  390.7 1.4 collective-permute-start.23
  392.9 13.8 %collective-permute-done.23 = bf16[320,768]{1,0:T(8,128)(2,1)S(1)} collective-permute-done((bf16[320,768]{1,0:T(8,128)(2,1)S(1)}, bf16[320,768]{1,0:T(8,128)(2,1)S(1)}, u32[]{:S(2)}, u32[]{:S(2)}) %collective-permute-start.23) | collective-permute-done | bytes 491552 | tf_op jit(solution)/shard_map/ppermute | solution.py:936
  408.0 3.5 fusion.16
  (128 shorter events, 23.8 us)
Async XLA Ops:
  1.5 3.3 collective-permute-start
  4.7 2.6 copy-start.25
  4.7 2.6 copy-start.12
  7.3 10.6 %collective-permute-start.3 = (bf16[1024,768]{1,0:T(8,128)(2,1)S(1)}, bf16[1024,768]{1,0:T(8,128)(2,1)S(1)}, u32[]{:S(2)}, u32[]{:S(2)}) collective-permute-start(bf16[1024,768]{1,0:T(8,128)(2,1)S(1)} %copy-done.12), channel_id=1, source_target_pairs={{0,1},{1,2},{2,3},{4,5},{5,6},{6,7},{8,9},{9,10},{10,11},{12,13},{... | collective-permute-start | bytes 4718600 | tf_op jit(solution)/shard_map/ppermute | solution.py:922
  11.9 25.7 %collective-permute-start.2 = (bf16[304,768]{1,0:T(8,128)(2,1)S(1)}, bf16[304,768]{1,0:T(8,128)(2,1)S(1)}, u32[]{:S(2)}, u32[]{:S(2)}) collective-permute-start(bf16[304,768]{1,0:T(8,128)(2,1)S(1)} %pad_maximum_fusion.1.refs_0_), channel_id=1, source_target_pairs={{0,16},{1,17},{2,18},{3,19},{4,20},{5,21},{6,22},{7,23},{8,24},{9,... | collective-permute-start | bytes 1400840 | tf_op jit(solution)/shard_map/ppermute | solution.py:936
  16.3 24.5 %collective-permute-start.1 = (bf16[304,768]{1,0:T(8,128)(2,1)S(1)}, bf16[304,768]{1,0:T(8,128)(2,1)S(1)}, u32[]{:S(2)}, u32[]{:S(2)}) collective-permute-start(bf16[304,768]{1,0:T(8,128)(2,1)S(1)} %pad_maximum_fusion.1.refs_0_), channel_id=1, source_target_pairs={{0,8},{1,9},{2,10},{3,11},{4,12},{5,13},{6,14},{7,15},{8,0},{9,1},... | collective-permute-start | bytes 1400840 | tf_op jit(solution)/shard_map/ppermute | solution.py:936
  18.1 19.6 %copy-start.16 = (bf16[2048,768]{1,0:T(8,128)(2,1)}, bf16[2048,768]{1,0:T(8,128)(2,1)S(1)}, u32[]{:S(2)}) copy-start(bf16[2048,768]{1,0:T(8,128)(2,1)S(1)} %constant_dynamic-update-slice_fusion.refs_1_.x_ref) | copy-start | bytes 9437188
  37.7 12.3 %collective-permute-start.4 = (bf16[304,768]{1,0:T(8,128)(2,1)S(1)}, bf16[304,768]{1,0:T(8,128)(2,1)S(1)}, u32[]{:S(2)}, u32[]{:S(2)}) collective-permute-start(bf16[304,768]{1,0:T(8,128)(2,1)S(1)} %collective-permute-done.2.refs_2_), channel_id=1, source_target_pairs={{0,8},{1,9},{2,10},{3,11},{4,12},{5,13},{6,14},{7,15},{8,0},{9,1},... | collective-permute-start | bytes 1400840 | tf_op jit(solution)/shard_map/ppermute | solution.py:936
  55.0 39.4 %copy-start.6 = (bf16[864,768]{1,0:T(8,128)(2,1)}, bf16[864,768]{1,0:T(8,128)(2,1)S(1)}, u32[]{:S(2)}) copy-start(bf16[864,768]{1,0:T(8,128)(2,1)S(1)} %get-tuple-element.98.own_ref) | copy-start | bytes 3981316
  55.0 8.6 %collective-permute-start.5 = (bf16[304,768]{1,0:T(8,128)(2,1)S(1)}, bf16[304,768]{1,0:T(8,128)(2,1)S(1)}, u32[]{:S(2)}, u32[]{:S(2)}) collective-permute-start(bf16[304,768]{1,0:T(8,128)(2,1)S(1)} %get-tuple-element.96.own_ref), channel_id=1, source_target_pairs={{0,2},{1,5},{2,0},{3,7},{4,6},{5,1},{6,4},{7,3},{8,10},{9,13},{10,... | collective-permute-start | bytes 1400840 | tf_op jit(solution)/shard_map/ppermute | solution.py:936
  63.7 13.4 %collective-permute-start.6 = (bf16[592,768]{1,0:T(8,128)(2,1)S(1)}, bf16[592,768]{1,0:T(8,128)(2,1)S(1)}, u32[]{:S(2)}, u32[]{:S(2)}) collective-permute-start(bf16[592,768]{1,0:T(8,128)(2,1)S(1)} %join.2.own_ref), channel_id=1, source_target_pairs={{0,4},{1,3},{2,6},{3,1},{4,0},{5,7},{6,2},{7,5},{8,12},{9,11},{10,... | collective-permute-start | bytes 2727944 | tf_op jit(solution)/shard_map/ppermute | solution.py:936
  77.2 3.9 copy-start.5
  77.2 3.9 collective-permute-start.7
  77.3 18.0 %collective-permute-start.8 = (bf16[864,768]{1,0:T(8,128)(2,1)S(1)}, bf16[864,768]{1,0:T(8,128)(2,1)}, u32[]{:S(2)}, u32[]{:S(2)}) collective-permute-start(bf16[864,768]{1,0:T(8,128)(2,1)S(1)} %get-tuple-element.98.own_ref), channel_id=1, source_target_pairs={{0,2},{1,5},{2,0},{3,7},{4,6},{5,1},{6,4},{7,3},{8,10},{9,13},{10,... | collective-permute-start | bytes 3981320 | tf_op jit(solution)/shard_map/ppermute | solution.py:936
  98.3 17.4 %copy-start.4 = (bf16[1728,768]{1,0:T(8,128)(2,1)}, bf16[1728,768]{1,0:T(8,128)(2,1)S(1)}, u32[]{:S(2)}) copy-start(bf16[1728,768]{1,0:T(8,128)(2,1)S(1)} %join_held.1) | copy-start | bytes 7962628
  98.3 17.4 %collective-permute-start.10 = (bf16[1728,768]{1,0:T(8,128)(2,1)S(1)}, bf16[1728,768]{1,0:T(8,128)(2,1)S(1)}, u32[]{:S(2)}, u32[]{:S(2)}) collective-permute-start(bf16[1728,768]{1,0:T(8,128)(2,1)S(1)} %join_held.1), channel_id=1, source_target_pairs={{0,1},{1,0},{2,3},{3,2},{4,5},{5,4},{6,7},{7,6},{8,9},{9,8},{10,11... | collective-permute-start | bytes 7962632 | tf_op jit(solution)/shard_map/ppermute | solution.py:936
  98.4 34.5 %collective-permute-start.9 = (bf16[1728,768]{1,0:T(8,128)(2,1)S(1)}, bf16[1728,768]{1,0:T(8,128)(2,1)}, u32[]{:S(2)}, u32[]{:S(2)}) collective-permute-start(bf16[1728,768]{1,0:T(8,128)(2,1)S(1)} %join_held.1), channel_id=1, source_target_pairs={{0,4},{1,3},{2,6},{3,1},{4,0},{5,7},{6,2},{7,5},{8,12},{9,11},{10,... | collective-permute-start | bytes 7962632 | tf_op jit(solution)/shard_map/ppermute | solution.py:936
  115.8 17.1 %copy-start.27 = (bf16[1728,768]{1,0:T(8,128)(2,1)}, bf16[1728,768]{1,0:T(8,128)(2,1)S(1)}, u32[]{:S(2)}) copy-start(bf16[1728,768]{1,0:T(8,128)(2,1)S(1)} %collective-permute-done.10) | copy-start | bytes 7962628
  132.9 17.0 %collective-permute-start.11 = (bf16[1728,768]{1,0:T(8,128)(2,1)}, bf16[1728,768]{1,0:T(8,128)(2,1)S(1)}, u32[]{:S(2)}, u32[]{:S(2)}) collective-permute-start(bf16[1728,768]{1,0:T(8,128)(2,1)} %hold.1), channel_id=1, source_target_pairs={{0,1},{1,0},{2,3},{3,2},{4,5},{5,4},{6,7},{7,6},{8,9},{9,8},{10,11... | collective-permute-start | bytes 7962632 | tf_op jit(solution)/shard_map/ppermute | solution.py:936
  150.0 1.6 copy-start.28
  206.6 10.0 %collective-permute-start.12 = (bf16[12,288,768]{2,1,0:T(8,128)(2,1)}, bf16[12,288,768]{2,1,0:T(8,128)(2,1)}, u32[]{:S(2)}, u32[]{:S(2)}) collective-permute-start(bf16[12,288,768]{2,1,0:T(8,128)(2,1)} %bitcast.75), channel_id=1, source_target_pairs={{0,1},{1,0},{2,3},{3,2},{4,5},{5,4},{6,7},{7,6},{8,9},{9,8},{10,11... | collective-permute-start | bytes 15925256 | tf_op jit(solution)/shard_map/ppermute | solution.py:936
  207.2 9.4 %slice-start = ((s8[5308416]{0:T(1024)(128)(4,1)}), s8[4194304]{0:T(1024)(128)(4,1)S(1)}, s32[]{:S(2)}) async-start(s8[5308416]{0:T(1024)(128)(4,1)} %bitcast.69), calls=%async_computation | async-start | bytes 8388608
  207.2 9.4 %slice-start.1 = ((s8[5308416]{0:T(1024)(128)(4,1)}), s8[1114112]{0:T(1024)(128)(4,1)S(1)}, s32[]{:S(2)}) async-start(s8[5308416]{0:T(1024)(128)(4,1)} %bitcast.69), calls=%async_computation.1 | async-start | bytes 2228224
  224.0 36.1 %collective-permute-start.13 = (bf16[6,288,768]{2,1,0:T(8,128)(2,1)}, bf16[6,288,768]{2,1,0:T(8,128)(2,1)S(1)}, u32[]{:S(2)}, u32[]{:S(2)}) collective-permute-start(bf16[6,288,768]{2,1,0:T(8,128)(2,1)} %get-tuple-element.125), channel_id=1, source_target_pairs={{0,2},{1,5},{2,0},{3,7},{4,6},{5,1},{6,4},{7,3},{8,10},{9,13},{10,... | collective-permute-start | bytes 7962632 | tf_op jit(solution)/shard_map/ppermute | solution.py:936
  230.0 30.1 %copy-start = (bf16[6,288,768]{2,1,0:T(8,128)(2,1)S(1)}, bf16[6,288,768]{2,1,0:T(8,128)(2,1)}, u32[]{:S(2)}) copy-start(bf16[6,288,768]{2,1,0:T(8,128)(2,1)} %get-tuple-element.133.ka_ref.kb_ref) | copy-start | bytes 7962628
  263.1 18.0 %collective-permute-start.14 = (bf16[3,288,768]{2,1,0:T(8,128)(2,1)}, bf16[3,288,768]{2,1,0:T(8,128)(2,1)S(1)}, u32[]{:S(2)}, u32[]{:S(2)}) collective-permute-start(bf16[3,288,768]{2,1,0:T(8,128)(2,1)} %get-tuple-element.134), channel_id=1, source_target_pairs={{0,4},{1,3},{2,6},{3,1},{4,0},{5,7},{6,2},{7,5},{8,12},{9,11},{10,... | collective-permute-start | bytes 3981320 | tf_op jit(solution)/shard_map/ppermute | solution.py:936
  263.1 18.0 %copy-start.1 = (f32[3,288,768]{2,1,0:T(8,128)S(1)}, f32[3,288,768]{2,1,0:T(8,128)}, u32[]{:S(2)}) copy-start(f32[3,288,768]{2,1,0:T(8,128)} %get-tuple-element.142.ka_ref.kb_ref) | copy-start | bytes 7962628
  283.2 25.1 %collective-permute-start.15 = (bf16[2,288,768]{2,1,0:T(8,128)(2,1)}, bf16[2,288,768]{2,1,0:T(8,128)(2,1)S(1)}, u32[]{:S(2)}, u32[]{:S(2)}) collective-permute-start(bf16[2,288,768]{2,1,0:T(8,128)(2,1)} %get-tuple-element.143), channel_id=1, source_target_pairs={{0,8},{1,9},{2,10},{3,11},{4,12},{5,13},{6,14},{7,15},{8,0},{9,1},... | collective-permute-start | bytes 2654216 | tf_op jit(solution)/shard_map/ppermute | solution.py:936
  298.9 9.4 %copy-start.2 = (f32[2,288,768]{2,1,0:T(8,128)S(1)}, f32[2,288,768]{2,1,0:T(8,128)}, u32[]{:S(2)}) copy-start(f32[2,288,768]{2,1,0:T(8,128)} %get-tuple-element.151.ka_ref.kb_ref) | copy-start | bytes 5308420
  307.0 24.9 %collective-permute-start.16 = (bf16[1024,768]{1,0:T(8,128)(2,1)}, bf16[1024,768]{1,0:T(8,128)(2,1)}, u32[]{:S(2)}, u32[]{:S(2)}) collective-permute-start(bf16[1024,768]{1,0:T(8,128)(2,1)} %get-tuple-element.158), channel_id=1, source_target_pairs={{1,0},{2,1},{3,2},{5,4},{6,5},{7,6},{9,8},{10,9},{11,10},{13,12},{... | collective-permute-start | bytes 4718600 | tf_op jit(solution)/shard_map/ppermute | solution.py:922
  310.1 21.7 %collective-permute-start.17 = (bf16[1,288,768]{2,1,0:T(8,128)(2,1)}, bf16[1,288,768]{2,1,0:T(8,128)(2,1)S(1)}, u32[]{:S(2)}, u32[]{:S(2)}) collective-permute-start(bf16[1,288,768]{2,1,0:T(8,128)(2,1)} %get-tuple-element.152), channel_id=1, source_target_pairs={{0,16},{1,17},{2,18},{3,19},{4,20},{5,21},{6,22},{7,23},{8,24},{9,... | collective-permute-start | bytes 1327112 | tf_op jit(solution)/shard_map/ppermute | solution.py:936
  312.5 27.9 %copy-start.26 = (pred[3]{0:T(512)(128)(4,1)S(1)}, pred[3]{0:T(512)(128)(4,1)}, u32[]{:S(2)}) copy-start(pred[3]{0:T(512)(128)(4,1)} %copy-done.25) | copy-start | bytes 13
  312.5 28.2 %copy-start.13 = (bf16[1024,768]{1,0:T(8,128)(2,1)S(1)}, bf16[1024,768]{1,0:T(8,128)(2,1)}, u32[]{:S(2)}) copy-start(bf16[1024,768]{1,0:T(8,128)(2,1)} %x_ref.1) | copy-start | bytes 4718596
  332.6 11.5 %collective-permute-start.18 = (bf16[1232,768]{1,0:T(8,128)(2,1)}, bf16[1232,768]{1,0:T(8,128)(2,1)S(1)}, u32[]{:S(2)}, u32[]{:S(2)}) collective-permute-start(bf16[1232,768]{1,0:T(8,128)(2,1)} %get-tuple-element.167), channel_id=1, source_target_pairs={{0,1},{1,0},{2,3},{3,2},{4,5},{5,4},{6,7},{7,6},{8,9},{9,8},{10,11... | collective-permute-start | bytes 5677064 | tf_op jit(solution)/shard_map/ppermute | solution.py:936
  344.1 2.1 copy-start.3
  346.2 8.4 %copy-start.14 = (f32[1024,768]{1,0:T(8,128)S(1)}, f32[1024,768]{1,0:T(8,128)}, u32[]{:S(2)}) copy-start(f32[1024,768]{1,0:T(8,128)} %get-tuple-element.163) | copy-start | bytes 9437188
  347.1 18.5 %collective-permute-start.20 = (bf16[624,768]{1,0:T(8,128)(2,1)S(1)}, bf16[624,768]{1,0:T(8,128)(2,1)S(1)}, u32[]{:S(2)}, u32[]{:S(2)}) collective-permute-start(bf16[624,768]{1,0:T(8,128)(2,1)S(1)} %get-tuple-element.168), channel_id=1, source_target_pairs={{0,2},{1,5},{2,0},{3,7},{4,6},{5,1},{6,4},{7,3},{8,10},{9,13},{10,... | collective-permute-start | bytes 2875400 | tf_op jit(solution)/shard_map/ppermute | solution.py:936
  354.6 11.9 %copy-start.20 = (f32[1,288,768]{2,1,0:T(8,128)S(1)}, f32[1,288,768]{2,1,0:T(8,128)}, u32[]{:S(2)}) copy-start(f32[1,288,768]{2,1,0:T(8,128)} %get-tuple-element.164) | copy-start | bytes 2654212
  354.6 11.9 %copy-start.22 = (bf16[1,288,768]{2,1,0:T(8,128)(2,1)S(1)}, bf16[1,288,768]{2,1,0:T(8,128)(2,1)}, u32[]{:S(2)}) copy-start(bf16[1,288,768]{2,1,0:T(8,128)(2,1)} %copy-done.21) | copy-start | bytes 1327108
  366.4 9.0 %collective-permute-start.21 = (bf16[320,768]{1,0:T(8,128)(2,1)S(1)}, bf16[320,768]{1,0:T(8,128)(2,1)S(1)}, u32[]{:S(2)}, u32[]{:S(2)}) collective-permute-start(bf16[320,768]{1,0:T(8,128)(2,1)S(1)} %get-tuple-element.173), channel_id=1, source_target_pairs={{0,4},{1,3},{2,6},{3,1},{4,0},{5,7},{6,2},{7,5},{8,12},{9,11},{10,... | collective-permute-start | bytes 1474568 | tf_op jit(solution)/shard_map/ppermute | solution.py:936
  372.3 5.9 %copy-start.15 = (f32[1024,768]{1,0:T(8,128)S(1)}, f32[1024,768]{1,0:T(8,128)}, u32[]{:S(2)}) copy-start(f32[1024,768]{1,0:T(8,128)} %get-tuple-element.163) | copy-start | bytes 9437188
  374.1 9.2 %copy-start.18 = (f32[288,768]{1,0:T(8,128)}, f32[288,768]{1,0:T(8,128)S(1)}, u32[]{:S(2)}) copy-start(f32[288,768]{1,0:T(8,128)S(1)} %bitcast_select_fusion) | copy-start | bytes 2654212
  374.1 9.1 %collective-permute-start.19 = (f32[16,768]{1,0:T(8,128)S(1)}, f32[16,768]{1,0:T(8,128)S(1)}, u32[]{:S(2)}, u32[]{:S(2)}) collective-permute-start(f32[16,768]{1,0:T(8,128)S(1)} %slice.29), channel_id=1, source_target_pairs={{1,0},{2,1},{3,2},{4,3},{5,4},{6,5},{7,6},{8,7},{9,8},{10,9},{11,1... | collective-permute-start | bytes 147464 | tf_op jit(solution)/shard_map/ppermute | solution.py:916
  375.5 15.1 %collective-permute-start.22 = (bf16[320,768]{1,0:T(8,128)(2,1)S(1)}, bf16[320,768]{1,0:T(8,128)(2,1)S(1)}, u32[]{:S(2)}, u32[]{:S(2)}) collective-permute-start(bf16[320,768]{1,0:T(8,128)(2,1)S(1)} %get-tuple-element.175), channel_id=1, source_target_pairs={{0,8},{1,9},{2,10},{3,11},{4,12},{5,13},{6,14},{7,15},{8,0},{9,1},... | collective-permute-start | bytes 1474568 | tf_op jit(solution)/shard_map/ppermute | solution.py:936
  383.2 7.4 %copy-start.23 = (f32[16,768]{1,0:T(8,128)}, f32[16,768]{1,0:T(8,128)S(1)}, u32[]{:S(2)}) copy-start(f32[16,768]{1,0:T(8,128)S(1)} %collective-permute-done.19) | copy-start | bytes 147460
  383.2 23.6 %copy-start.19 = (f32[288,768]{1,0:T(8,128)S(1)}, f32[288,768]{1,0:T(8,128)}, u32[]{:S(2)}) copy-start(f32[288,768]{1,0:T(8,128)} %copy-done.18) | copy-start | bytes 2654212
  390.7 16.3 %copy-start.24 = (f32[16,768]{1,0:T(8,128)S(1)}, f32[16,768]{1,0:T(8,128)}, u32[]{:S(2)}) copy-start(f32[16,768]{1,0:T(8,128)} %copy-done.23) | copy-start | bytes 147460
  390.7 16.0 %collective-permute-start.23 = (bf16[320,768]{1,0:T(8,128)(2,1)S(1)}, bf16[320,768]{1,0:T(8,128)(2,1)S(1)}, u32[]{:S(2)}, u32[]{:S(2)}) collective-permute-start(bf16[320,768]{1,0:T(8,128)(2,1)S(1)} %get-tuple-element.177), channel_id=1, source_target_pairs={{8,24},{9,25},{10,26},{11,27},{12,28},{13,29},{14,30},{15,31},{16,... | collective-permute-start | bytes 1474568 | tf_op jit(solution)/shard_map/ppermute | solution.py:936
  (7 other events, 6.8 us)

commit v14 on v13

--- a/solution.py
+++ b/solution.py
@@ -1184,7 +1184,7 @@
         late_chunk = jnp.where(in_up, ungroup(late_chunk).reshape(3, 4, 24, D), late_chunk.reshape(3, 4, 24, D))
         late_chunk = late_chunk.reshape(-1, D)
         late_next = shift_flat(late_chunk[:16], -1)
-        send, keep = merge(pick_line, keep, got, height + 16, 1)
+        send, keep = merge(after(pick_line, late_chunk), keep, got, height + 16, 1)
         got = swap(send, 4, 2)
         send, keep = merge(core, keep, got, height + 16, 0)
         got = swap(send, 8, 8)

time: 413 us -> 408 us (0.988)
    unnamed x63 -> x55, local copies, waits for them, and re-layouts: 10.4 us -> 9.6 us
  transfers between devices with their start and end apart: 24 -> 24, of which waited for: 12 -> 13; matrix products, arithmetic and copies ran while one was open for 5% -> 5% of each run, Pallas kernels for 35% -> 35%
where the time goes in v14:
time: 408 us; the launch traced here: 410 us
  Pallas kernels  216 us (53%)
  waiting for transfers between devices  104 us (25%)
  starting transfers between devices  48.5 us (12%)
  local copies, waits for them, and re-layouts  19.9 us (5%)
  other arithmetic  17.7 us (4%)
    ppermute x20, waiting for transfers between devices, swap(): return lax.ppermute(block, AXES, route)  104 us
    pallas_call x1, Pallas kernels, ffn(): pl.pallas_call(ffn_kernel, grid=(4,), in_specs=[scalars, scalars, act, ac...  55.1 us
    pallas_call x4, Pallas kernels, att_bwd(): call_in_parts(att_bwd_kernel, [pl.BlockSpec(memory_space=pltpu.SMEM), own...  50.3 us
    pallas_call x3, Pallas kernels, att_fwd(): call_in_parts(att_fwd_kernel, [pl.BlockSpec(memory_space=pltpu.SMEM), col...  49.3 us
    ppermute x20, starting transfers between devices, swap(): return lax.ppermute(block, AXES, route)  39 us
    pallas_call x1, Pallas kernels, qkv_bwd(): pl.pallas_call(body, grid=(blocks,), in_specs=[pl.BlockSpec(memory_space=...  19.3 us
    pallas_call x4, Pallas kernels, merge_grid(): pl.pallas_call(body, grid_spec=pltpu.PrefetchScalarGridSpec(num_scalar_pr...  14.3 us
    pallas_call x1, Pallas kernels, qkv_fwd(): pl.pallas_call(body, grid=(blocks,), in_specs=[pl.BlockSpec(memory_space=...  13.3 us
  transfers between devices with their start and end apart: 24, of which 13 were waited for; matrix products, arithmetic and copies ran while one was open for 5% of the time, Pallas kernels for 35%

profile of v14, /device:TPU:0, one launch (start us, length us, event | category | flops | bytes accessed | tf_op | source)
XLA Modules:
  0.0 409.7 jit_solution(3728546663926291547)
XLA Ops:
  1.5 2.3 collective-permute-start
  4.7 1.5 fusion.8
  7.3 4.6 %collective-permute-start.3 = (bf16[1024,768]{1,0:T(8,128)(2,1)S(1)}, bf16[1024,768]{1,0:T(8,128)(2,1)S(1)}, u32[]{:S(2)}, u32[]{:S(2)}) collective-permute-start(bf16[1024,768]{1,0:T(8,128)(2,1)S(1)} %copy-done.12), channel_id=1, source_target_pairs={{0,1},{1,2},{2,3},{4,5},{5,6},{6,7},{8,9},{9,10},{10,11},{12,13},{... | collective-permute-start | bytes 4718600 | tf_op jit(solution)/shard_map/ppermute | solution.py:922
  11.9 4.4 %collective-permute-start.2 = (bf16[304,768]{1,0:T(8,128)(2,1)S(1)}, bf16[304,768]{1,0:T(8,128)(2,1)S(1)}, u32[]{:S(2)}, u32[]{:S(2)}) collective-permute-start(bf16[304,768]{1,0:T(8,128)(2,1)S(1)} %pad_maximum_fusion.1.refs_0_), channel_id=1, source_target_pairs={{0,16},{1,17},{2,18},{3,19},{4,20},{5,21},{6,22},{7,23},{8,24},{9,... | collective-permute-start | bytes 1400840 | tf_op jit(solution)/shard_map/ppermute | solution.py:936
  16.3 1.6 collective-permute-start.1
  18.1 19.6 %collective-permute-done.2.refs_2_ = bf16[304,768]{1,0:T(8,128)(2,1)S(1)} collective-permute-done((bf16[304,768]{1,0:T(8,128)(2,1)S(1)}, bf16[304,768]{1,0:T(8,128)(2,1)S(1)}, u32[]{:S(2)}, u32[]{:S(2)}) %collective-permute-start.2) | collective-permute-done | bytes 466976 | tf_op jit(solution)/shard_map/ppermute | solution.py:936
  41.6 8.4 %collective-permute-done.4.refs_3_ = bf16[304,768]{1,0:T(8,128)(2,1)S(1)} collective-permute-done((bf16[304,768]{1,0:T(8,128)(2,1)S(1)}, bf16[304,768]{1,0:T(8,128)(2,1)S(1)}, u32[]{:S(2)}, u32[]{:S(2)}) %collective-permute-start.4) | collective-permute-done | bytes 466976 | tf_op jit(solution)/shard_map/ppermute | solution.py:936
  52.8 2.1 arrange.1
  55.1 8.6 %collective-permute-done.5.got_ref = bf16[304,768]{1,0:T(8,128)(2,1)S(1)} collective-permute-done((bf16[304,768]{1,0:T(8,128)(2,1)S(1)}, bf16[304,768]{1,0:T(8,128)(2,1)S(1)}, u32[]{:S(2)}, u32[]{:S(2)}) %collective-permute-start.5) | collective-permute-done | bytes 466976 | tf_op jit(solution)/shard_map/ppermute | solution.py:936
  65.1 12.0 %collective-permute-done.6.got_ref = bf16[592,768]{1,0:T(8,128)(2,1)S(1)} collective-permute-done((bf16[592,768]{1,0:T(8,128)(2,1)S(1)}, bf16[592,768]{1,0:T(8,128)(2,1)S(1)}, u32[]{:S(2)}, u32[]{:S(2)}) %collective-permute-start.6) | collective-permute-done | bytes 909344 | tf_op jit(solution)/shard_map/ppermute | solution.py:936
  78.2 2.9 collective-permute-done.7.refs_3_
  81.1 13.3 %qkv_fwd.1 = (bf16[2048,2304]{1,0:T(8,128)(2,1)}, f32[16,768]{1,0:T(8,128)}, bf16[2304,768]{1,0:T(8,128)(2,1)}) custom-call(s32[8]{0:T(128)} %stack.217.refs_0_, bf16[2048,768]{1,0:T(8,128)(2,1)} %copy-done.16, bf16[1168,768]{1,0:T(8,128)(2,1)} %copy-done.5, bf16[1168,768]{1,0:T(8,128)(2,1)} %collective-permute-done.7.refs_3_), custom_call_target="tpu_custom_call" | custom-call | flops 7247757312 | bytes 15728640 | tf_op jit(solution)/shard_map/qkv_fwd/pallas_call | solution.py:714
  96.5 1.8 join_held.1
  99.8 15.9 %att_fwd.3 = (bf16[1024,768]{1,0:T(8,128)(2,1)}, f32[1024,768]{1,0:T(8,128)}, bf16[1024,768]{1,0:T(8,128)(2,1)}, bf16[2048,768]{1,0:T(8,128)(2,1)}, bf16[2048,768]{1,0:T(8,128)(2,1)}) custom-call(s32[1]{0:T(128)S(6)} %select_n.125.refs_0_.state_ref, bf16[2048,2304]{1,0:T(8,128)(2,1)} %get-tuple-element.98.refs_1_.refs_2_.refs_3_.refs_4_.refs_7_.refs_8_.refs_9_.refs_10_, ...), custom_call_target="tpu_custom_call" | custom-call | flops 6442450944 | bytes 7864320 | tf_op jit(solution)/shard_map/att_fwd/pallas_call | solution.py:152
  115.8 17.1 %att_fwd.4 = (bf16[1024,768]{1,0:T(8,128)(2,1)}, f32[1024,768]{1,0:T(8,128)}, bf16[1024,768]{1,0:T(8,128)(2,1)}, bf16[2048,768]{1,0:T(8,128)(2,1)}, bf16[2048,768]{1,0:T(8,128)(2,1)}) custom-call(s32[1]{0:T(128)S(6)} %select_n.125.refs_0_.state_ref, ...), custom_call_target="tpu_custom_call", output_to_operand_aliasing={{0}: (6, {}), {1}: (7, {}), {2}: (8, {}), {3}: (9, {}), {4}... | custom-call | flops 6442450944 | bytes 7864320 | tf_op jit(solution)/shard_map/att_fwd/pallas_call | solution.py:152
  133.7 16.3 %att_fwd.5 = (bf16[1024,768]{1,0:T(8,128)(2,1)}, f32[1024,768]{1,0:T(8,128)}, bf16[1024,768]{1,0:T(8,128)(2,1)}, bf16[2048,768]{1,0:T(8,128)(2,1)}, bf16[2048,768]{1,0:T(8,128)(2,1)}) custom-call(s32[1]{0:T(128)S(6)} %select_n.125.refs_0_.state_ref, ...), custom_call_target="tpu_custom_call", output_to_operand_aliasing={{0}: (6, {}), {1}: (7, {}), {2}: (8, {}), {3}: (9, {}), {4}... | custom-call | flops 6442450944 | bytes 7864320 | tf_op jit(solution)/shard_map/att_fwd/pallas_call | solution.py:152
  151.6 55.1 %ffn.1 = (bf16[1024,768]{1,0:T(8,128)(2,1)}, f32[1024,768]{1,0:T(8,128)}, bf16[1024,768]{1,0:T(8,128)(2,1)}, f32[1,768]{1,0:T(1,128)}, bf16[36,4,24,768]{3,2,1,0...) custom-call(s32[1]{0:T(128)S(6)} %select_n.125.refs_0_.state_ref, s32[25]{0:T(128)} %stack.211.index_ref, ...), custom_call_target="tpu_custom_call" | custom-call | flops 32614907904 | bytes 40894464 | tf_op jit(solution)/shard_map/ffn/pallas_call | solution.py:879
  207.3 9.3 %att_bwd.4 = (bf16[1024,768]{1,0:T(8,128)(2,1)}, bf16[8,768]{1,0:T(8,128)(2,1)}, bf16[2048,768]{1,0:T(8,128)(2,1)}, bf16[2048,768]{1,0:T(8,128)(2,1)}, f32[16,768]{1,0:T(8,128)}) custom-call(s32[1]{0:T(128)S(6)} %select_n.125.refs_0_.state_ref, bf16[1024,768]{1,0:T(8,128)(2,1)} %get-tuple-element.117.refs_1_, bf16[2048,768]{1,0:T(8,128)(2,1)} %get-tuple-element.118.refs_2_, ...), custom_call_target="tpu_custom_call" | custom-call | flops 8053063680 | bytes 5505024 | tf_op jit(solution)/shard_map/att_bwd/pallas_call | solution.py:309
  216.7 7.4 %merge_grid.4 = (bf16[6,288,768]{2,1,0:T(8,128)(2,1)}, bf16[6,288,768]{2,1,0:T(8,128)(2,1)}) custom-call(s32[12]{0:T(128)S(1)} %stack.243.index_ref, bf16[12,288,768]{2,1,0:T(8,128)(2,1)S(1)} %bitcast.71, bf16[12,288,768]{2,1,0:T(8,128)(2,1)} %collective-permute-done.12.ga_ref.gb_ref, bf16[12,288,768]{2,1,0:T(8,128)(2,1)S(1)} %bitcast.72, ...), custom_call_target="tpu_custom_call" | custom-call | flops 2654208 | bytes 21233664 | tf_op jit(solution)/shard_map/merge_grid/pallas_call | solution.py:545
  224.1 5.9 %collective-permute-start.13 = (bf16[6,288,768]{2,1,0:T(8,128)(2,1)}, bf16[6,288,768]{2,1,0:T(8,128)(2,1)S(1)}, u32[]{:S(2)}, u32[]{:S(2)}) collective-permute-start(bf16[6,288,768]{2,1,0:T(8,128)(2,1)} %get-tuple-element.126), channel_id=1, source_target_pairs={{0,2},{1,5},{2,0},{3,7},{4,6},{5,1},{6,4},{7,3},{8,10},{9,13},{10,... | collective-permute-start | bytes 7962632 | tf_op jit(solution)/shard_map/ppermute | solution.py:936
  230.1 15.8 %att_bwd.5 = (bf16[1024,768]{1,0:T(8,128)(2,1)}, bf16[8,768]{1,0:T(8,128)(2,1)}, bf16[2048,768]{1,0:T(8,128)(2,1)}, bf16[2048,768]{1,0:T(8,128)(2,1)}, f32[16,768]{1,0:T(8,128)}) custom-call(s32[1]{0:T(128)S(6)} %select_n.125.refs_0_.state_ref, ...), custom_call_target="tpu_custom_call", output_to_operand_aliasing={{0}: (12, {}), {1}: (13, {}), {2}: (14, {}), {3}: (15, {}),... | custom-call | flops 16106127360 | bytes 11010048 | tf_op jit(solution)/shard_map/att_bwd/pallas_call | solution.py:309
  245.9 14.3 %collective-permute-done.13.ga_ref.gb_ref = bf16[6,288,768]{2,1,0:T(8,128)(2,1)S(1)} collective-permute-done((bf16[6,288,768]{2,1,0:T(8,128)(2,1)}, bf16[6,288,768]{2,1,0:T(8,128)(2,1)S(1)}, u32[]{:S(2)}, u32[]{:S(2)}) %collective-permute-start.13) | collective-permute-done | bytes 2654240 | tf_op jit(solution)/shard_map/ppermute | solution.py:936
  260.2 3.0 merge_grid.5
  263.1 9.5 %att_bwd.6 = (bf16[1024,768]{1,0:T(8,128)(2,1)}, bf16[8,768]{1,0:T(8,128)(2,1)}, bf16[2048,768]{1,0:T(8,128)(2,1)}, bf16[2048,768]{1,0:T(8,128)(2,1)}, f32[16,768]{1,0:T(8,128)}) custom-call(s32[1]{0:T(128)S(6)} %select_n.125.refs_0_.state_ref, ...), custom_call_target="tpu_custom_call", output_to_operand_aliasing={{0}: (12, {}), {1}: (13, {}), {2}: (14, {}), {3}: (15, {}),... | custom-call | flops 8053063680 | bytes 5505024 | tf_op jit(solution)/shard_map/att_bwd/pallas_call | solution.py:309
  272.6 8.5 %collective-permute-done.14.ga_ref.gb_ref = bf16[3,288,768]{2,1,0:T(8,128)(2,1)S(1)} collective-permute-done((bf16[3,288,768]{2,1,0:T(8,128)(2,1)}, bf16[3,288,768]{2,1,0:T(8,128)(2,1)S(1)}, u32[]{:S(2)}, u32[]{:S(2)}) %collective-permute-start.14) | collective-permute-done | bytes 1327136 | tf_op jit(solution)/shard_map/ppermute | solution.py:936
  281.1 2.2 merge_grid.6
  283.3 15.7 %att_bwd.7 = (bf16[1024,768]{1,0:T(8,128)(2,1)}, bf16[8,768]{1,0:T(8,128)(2,1)}, bf16[2048,768]{1,0:T(8,128)(2,1)}, bf16[2048,768]{1,0:T(8,128)(2,1)}, f32[16,768]{1,0:T(8,128)}) custom-call(s32[1]{0:T(128)S(6)} %select_n.125.refs_0_.state_ref, ...), custom_call_target="tpu_custom_call", output_to_operand_aliasing={{0}: (12, {}), {1}: (13, {}), {2}: (14, {}), {3}: (15, {}),... | custom-call | flops 16106127360 | bytes 11010048 | tf_op jit(solution)/shard_map/att_bwd/pallas_call | solution.py:309
  299.0 8.0 %before_bwd.1 = (bf16[1024,768]{1,0:T(8,128)(2,1)}, f32[1,768]{1,0:T(1,128)}) custom-call(bf16[2048,768]{1,0:T(8,128)(2,1)} %copy-done.16, bf16[8,768]{1,0:T(8,128)(2,1)} %get-tuple-element.155.dt_ref.refs_3_, bf16[2048,768]{1,0:T(8,128)(2,1)} %get-tuple-element.156.dk_ref.refs_4_, bf16[2048,768]{1,0:T(8,128)(2,1)} %get-tuple-element.157.dv_ref.refs_5_, ...), custom_call_target="tpu_custom_call" | custom-call | flops 2415919104 | bytes 9437184 | tf_op jit(solution)/shard_map/before_bwd/pallas_call | solution.py:388
  308.4 1.7 merge_grid.7
  310.2 3.9 collective-permute-start.17
  314.1 19.3 %qkv_bwd.1 = (bf16[1232,768]{1,0:T(8,128)(2,1)}, f32[1232,768]{1,0:T(8,128)}, f32[1024,768]{1,0:T(8,128)}) custom-call(s32[1]{0:T(128)} %bitcast.24.refs_0_.index_ref, bf16[2048,768]{1,0:T(8,128)(2,1)} %copy-done.16, bf16[1024,768]{1,0:T(8,128)(2,1)} %get-tuple-element.161.refs_2_, bf16[8,768]{1,0:T(8,128)(2,1)} %get-tuple-element.155.dt_ref.refs_3_, ...), custom_call_target="tpu_custom_call" | custom-call | flops 9663676416 | bytes 23592960 | tf_op jit(solution)/shard_map/qkv_bwd/pallas_call | solution.py:483
  333.4 7.1 %collective-permute-start.18 = (bf16[1232,768]{1,0:T(8,128)(2,1)}, bf16[1232,768]{1,0:T(8,128)(2,1)S(1)}, u32[]{:S(2)}, u32[]{:S(2)}) collective-permute-start(bf16[1232,768]{1,0:T(8,128)(2,1)} %get-tuple-element.168), channel_id=1, source_target_pairs={{0,1},{1,0},{2,3},{3,2},{4,5},{5,4},{6,7},{7,6},{8,9},{9,8},{10,11... | collective-permute-start | bytes 5677064 | tf_op jit(solution)/shard_map/ppermute | solution.py:936
  340.6 3.6 collective-permute-done.18.got_ref
  344.2 2.1 copy-done.3
  346.3 1.8 merge.4
  348.1 5.9 %collective-permute-start.20 = (bf16[624,768]{1,0:T(8,128)(2,1)}, bf16[624,768]{1,0:T(8,128)(2,1)S(1)}, u32[]{:S(2)}, u32[]{:S(2)}) collective-permute-start(bf16[624,768]{1,0:T(8,128)(2,1)} %get-tuple-element.169), channel_id=1, source_target_pairs={{0,2},{1,5},{2,0},{3,7},{4,6},{5,1},{6,4},{7,3},{8,10},{9,13},{10,... | collective-permute-start | bytes 2875400 | tf_op jit(solution)/shard_map/ppermute | solution.py:936
  355.4 2.2 convert_add_fusion.1
  357.6 2.4 copy.44
  360.0 2.4 reshape.115
  362.4 1.7 bitcast_select_fusion
  364.1 2.0 collective-permute-done.20.got_ref
  366.8 4.3 %collective-permute-start.21 = (bf16[320,768]{1,0:T(8,128)(2,1)S(1)}, bf16[320,768]{1,0:T(8,128)(2,1)S(1)}, u32[]{:S(2)}, u32[]{:S(2)}) collective-permute-start(bf16[320,768]{1,0:T(8,128)(2,1)S(1)} %get-tuple-element.175), channel_id=1, source_target_pairs={{0,4},{1,3},{2,6},{3,1},{4,0},{5,7},{6,2},{7,5},{8,12},{9,11},{10,... | collective-permute-start | bytes 1474568 | tf_op jit(solution)/shard_map/ppermute | solution.py:936
  371.1 2.6 fusion.2
  375.1 2.9 collective-permute-done.21.got_ref
  378.3 4.1 fusion.5
  382.4 8.0 %collective-permute-done.22.got_ref = bf16[320,768]{1,0:T(8,128)(2,1)S(1)} collective-permute-done((bf16[320,768]{1,0:T(8,128)(2,1)S(1)}, bf16[320,768]{1,0:T(8,128)(2,1)S(1)}, u32[]{:S(2)}, u32[]{:S(2)}) %collective-permute-start.22) | collective-permute-done | bytes 491552 | tf_op jit(solution)/shard_map/ppermute | solution.py:936
  392.5 12.1 %collective-permute-done.23 = bf16[320,768]{1,0:T(8,128)(2,1)S(1)} collective-permute-done((bf16[320,768]{1,0:T(8,128)(2,1)S(1)}, bf16[320,768]{1,0:T(8,128)(2,1)S(1)}, u32[]{:S(2)}, u32[]{:S(2)}) %collective-permute-start.23) | collective-permute-done | bytes 491552 | tf_op jit(solution)/shard_map/ppermute | solution.py:936
  405.9 3.5 fusion.16
  (119 shorter events, 25.4 us)
Async XLA Ops:
  1.5 3.3 collective-permute-start
  4.7 2.6 copy-start.21
  4.7 2.6 copy-start.12
  7.3 10.6 %collective-permute-start.3 = (bf16[1024,768]{1,0:T(8,128)(2,1)S(1)}, bf16[1024,768]{1,0:T(8,128)(2,1)S(1)}, u32[]{:S(2)}, u32[]{:S(2)}) collective-permute-start(bf16[1024,768]{1,0:T(8,128)(2,1)S(1)} %copy-done.12), channel_id=1, source_target_pairs={{0,1},{1,2},{2,3},{4,5},{5,6},{6,7},{8,9},{9,10},{10,11},{12,13},{... | collective-permute-start | bytes 4718600 | tf_op jit(solution)/shard_map/ppermute | solution.py:922
  11.9 25.7 %collective-permute-start.2 = (bf16[304,768]{1,0:T(8,128)(2,1)S(1)}, bf16[304,768]{1,0:T(8,128)(2,1)S(1)}, u32[]{:S(2)}, u32[]{:S(2)}) collective-permute-start(bf16[304,768]{1,0:T(8,128)(2,1)S(1)} %pad_maximum_fusion.1.refs_0_), channel_id=1, source_target_pairs={{0,16},{1,17},{2,18},{3,19},{4,20},{5,21},{6,22},{7,23},{8,24},{9,... | collective-permute-start | bytes 1400840 | tf_op jit(solution)/shard_map/ppermute | solution.py:936
  16.3 24.5 %collective-permute-start.1 = (bf16[304,768]{1,0:T(8,128)(2,1)S(1)}, bf16[304,768]{1,0:T(8,128)(2,1)S(1)}, u32[]{:S(2)}, u32[]{:S(2)}) collective-permute-start(bf16[304,768]{1,0:T(8,128)(2,1)S(1)} %pad_maximum_fusion.1.refs_0_), channel_id=1, source_target_pairs={{0,8},{1,9},{2,10},{3,11},{4,12},{5,13},{6,14},{7,15},{8,0},{9,1},... | collective-permute-start | bytes 1400840 | tf_op jit(solution)/shard_map/ppermute | solution.py:936
  18.1 19.6 %copy-start.16 = (bf16[2048,768]{1,0:T(8,128)(2,1)}, bf16[2048,768]{1,0:T(8,128)(2,1)S(1)}, u32[]{:S(2)}) copy-start(bf16[2048,768]{1,0:T(8,128)(2,1)S(1)} %constant_dynamic-update-slice_fusion.refs_1_.x_ref) | copy-start | bytes 9437188
  37.7 12.3 %collective-permute-start.4 = (bf16[304,768]{1,0:T(8,128)(2,1)S(1)}, bf16[304,768]{1,0:T(8,128)(2,1)S(1)}, u32[]{:S(2)}, u32[]{:S(2)}) collective-permute-start(bf16[304,768]{1,0:T(8,128)(2,1)S(1)} %collective-permute-done.2.refs_2_), channel_id=1, source_target_pairs={{0,8},{1,9},{2,10},{3,11},{4,12},{5,13},{6,14},{7,15},{8,0},{9,1},... | collective-permute-start | bytes 1400840 | tf_op jit(solution)/shard_map/ppermute | solution.py:936
  50.8 1.0 copy-start.9
  55.0 39.4 %copy-start.6 = (bf16[864,768]{1,0:T(8,128)(2,1)}, bf16[864,768]{1,0:T(8,128)(2,1)S(1)}, u32[]{:S(2)}) copy-start(bf16[864,768]{1,0:T(8,128)(2,1)S(1)} %get-tuple-element.99.own_ref) | copy-start | bytes 3981316
  55.0 8.6 %collective-permute-start.5 = (bf16[304,768]{1,0:T(8,128)(2,1)S(1)}, bf16[304,768]{1,0:T(8,128)(2,1)S(1)}, u32[]{:S(2)}, u32[]{:S(2)}) collective-permute-start(bf16[304,768]{1,0:T(8,128)(2,1)S(1)} %get-tuple-element.97.own_ref), channel_id=1, source_target_pairs={{0,2},{1,5},{2,0},{3,7},{4,6},{5,1},{6,4},{7,3},{8,10},{9,13},{10,... | collective-permute-start | bytes 1400840 | tf_op jit(solution)/shard_map/ppermute | solution.py:936
  63.7 13.4 %collective-permute-start.6 = (bf16[592,768]{1,0:T(8,128)(2,1)S(1)}, bf16[592,768]{1,0:T(8,128)(2,1)S(1)}, u32[]{:S(2)}, u32[]{:S(2)}) collective-permute-start(bf16[592,768]{1,0:T(8,128)(2,1)S(1)} %join.2.own_ref), channel_id=1, source_target_pairs={{0,4},{1,3},{2,6},{3,1},{4,0},{5,7},{6,2},{7,5},{8,12},{9,11},{10,... | collective-permute-start | bytes 2727944 | tf_op jit(solution)/shard_map/ppermute | solution.py:936
  77.2 3.9 copy-start.5
  77.2 3.9 collective-permute-start.7
  77.3 18.0 %collective-permute-start.8 = (bf16[864,768]{1,0:T(8,128)(2,1)S(1)}, bf16[864,768]{1,0:T(8,128)(2,1)}, u32[]{:S(2)}, u32[]{:S(2)}) collective-permute-start(bf16[864,768]{1,0:T(8,128)(2,1)S(1)} %get-tuple-element.99.own_ref), channel_id=1, source_target_pairs={{0,2},{1,5},{2,0},{3,7},{4,6},{5,1},{6,4},{7,3},{8,10},{9,13},{10,... | collective-permute-start | bytes 3981320 | tf_op jit(solution)/shard_map/ppermute | solution.py:936
  95.2 1.3 copy-start.7
  98.3 17.4 %copy-start.4 = (bf16[1728,768]{1,0:T(8,128)(2,1)}, bf16[1728,768]{1,0:T(8,128)(2,1)S(1)}, u32[]{:S(2)}) copy-start(bf16[1728,768]{1,0:T(8,128)(2,1)S(1)} %join_held.1) | copy-start | bytes 7962628
  98.3 17.4 %collective-permute-start.10 = (bf16[1728,768]{1,0:T(8,128)(2,1)S(1)}, bf16[1728,768]{1,0:T(8,128)(2,1)S(1)}, u32[]{:S(2)}, u32[]{:S(2)}) collective-permute-start(bf16[1728,768]{1,0:T(8,128)(2,1)S(1)} %join_held.1), channel_id=1, source_target_pairs={{0,1},{1,0},{2,3},{3,2},{4,5},{5,4},{6,7},{7,6},{8,9},{9,8},{10,11... | collective-permute-start | bytes 7962632 | tf_op jit(solution)/shard_map/ppermute | solution.py:936
  98.4 34.5 %collective-permute-start.9 = (bf16[1728,768]{1,0:T(8,128)(2,1)S(1)}, bf16[1728,768]{1,0:T(8,128)(2,1)}, u32[]{:S(2)}, u32[]{:S(2)}) collective-permute-start(bf16[1728,768]{1,0:T(8,128)(2,1)S(1)} %join_held.1), channel_id=1, source_target_pairs={{0,4},{1,3},{2,6},{3,1},{4,0},{5,7},{6,2},{7,5},{8,12},{9,11},{10,... | collective-permute-start | bytes 7962632 | tf_op jit(solution)/shard_map/ppermute | solution.py:936
  115.8 17.1 %copy-start.23 = (bf16[1728,768]{1,0:T(8,128)(2,1)}, bf16[1728,768]{1,0:T(8,128)(2,1)S(1)}, u32[]{:S(2)}) copy-start(bf16[1728,768]{1,0:T(8,128)(2,1)S(1)} %collective-permute-done.10) | copy-start | bytes 7962628
  132.9 17.1 %collective-permute-start.11 = (bf16[1728,768]{1,0:T(8,128)(2,1)}, bf16[1728,768]{1,0:T(8,128)(2,1)S(1)}, u32[]{:S(2)}, u32[]{:S(2)}) collective-permute-start(bf16[1728,768]{1,0:T(8,128)(2,1)} %hold.1), channel_id=1, source_target_pairs={{0,1},{1,0},{2,3},{3,2},{4,5},{5,4},{6,7},{7,6},{8,9},{9,8},{10,11... | collective-permute-start | bytes 7962632 | tf_op jit(solution)/shard_map/ppermute | solution.py:936
  150.0 1.5 copy-start.24
  206.7 10.0 %collective-permute-start.12 = (bf16[12,288,768]{2,1,0:T(8,128)(2,1)}, bf16[12,288,768]{2,1,0:T(8,128)(2,1)}, u32[]{:S(2)}, u32[]{:S(2)}) collective-permute-start(bf16[12,288,768]{2,1,0:T(8,128)(2,1)} %bitcast.75), channel_id=1, source_target_pairs={{0,1},{1,0},{2,3},{3,2},{4,5},{5,4},{6,7},{7,6},{8,9},{9,8},{10,11... | collective-permute-start | bytes 15925256 | tf_op jit(solution)/shard_map/ppermute | solution.py:936
  207.3 9.4 %slice-start = ((s8[5308416]{0:T(1024)(128)(4,1)}), s8[4194304]{0:T(1024)(128)(4,1)S(1)}, s32[]{:S(2)}) async-start(s8[5308416]{0:T(1024)(128)(4,1)} %bitcast.69), calls=%async_computation | async-start | bytes 8388608
  207.3 9.4 %slice-start.1 = ((s8[5308416]{0:T(1024)(128)(4,1)}), s8[1114112]{0:T(1024)(128)(4,1)S(1)}, s32[]{:S(2)}) async-start(s8[5308416]{0:T(1024)(128)(4,1)} %bitcast.69), calls=%async_computation.1 | async-start | bytes 2228224
  224.1 36.1 %collective-permute-start.13 = (bf16[6,288,768]{2,1,0:T(8,128)(2,1)}, bf16[6,288,768]{2,1,0:T(8,128)(2,1)S(1)}, u32[]{:S(2)}, u32[]{:S(2)}) collective-permute-start(bf16[6,288,768]{2,1,0:T(8,128)(2,1)} %get-tuple-element.126), channel_id=1, source_target_pairs={{0,2},{1,5},{2,0},{3,7},{4,6},{5,1},{6,4},{7,3},{8,10},{9,13},{10,... | collective-permute-start | bytes 7962632 | tf_op jit(solution)/shard_map/ppermute | solution.py:936
  230.1 30.1 %copy-start = (bf16[6,288,768]{2,1,0:T(8,128)(2,1)S(1)}, bf16[6,288,768]{2,1,0:T(8,128)(2,1)}, u32[]{:S(2)}) copy-start(bf16[6,288,768]{2,1,0:T(8,128)(2,1)} %get-tuple-element.134.ka_ref.kb_ref) | copy-start | bytes 7962628
  263.1 18.0 %collective-permute-start.14 = (bf16[3,288,768]{2,1,0:T(8,128)(2,1)}, bf16[3,288,768]{2,1,0:T(8,128)(2,1)S(1)}, u32[]{:S(2)}, u32[]{:S(2)}) collective-permute-start(bf16[3,288,768]{2,1,0:T(8,128)(2,1)} %get-tuple-element.135), channel_id=1, source_target_pairs={{0,4},{1,3},{2,6},{3,1},{4,0},{5,7},{6,2},{7,5},{8,12},{9,11},{10,... | collective-permute-start | bytes 3981320 | tf_op jit(solution)/shard_map/ppermute | solution.py:936
  263.1 18.0 %copy-start.1 = (f32[3,288,768]{2,1,0:T(8,128)S(1)}, f32[3,288,768]{2,1,0:T(8,128)}, u32[]{:S(2)}) copy-start(f32[3,288,768]{2,1,0:T(8,128)} %get-tuple-element.143.ka_ref.kb_ref) | copy-start | bytes 7962628
  283.3 25.1 %collective-permute-start.15 = (bf16[2,288,768]{2,1,0:T(8,128)(2,1)}, bf16[2,288,768]{2,1,0:T(8,128)(2,1)S(1)}, u32[]{:S(2)}, u32[]{:S(2)}) collective-permute-start(bf16[2,288,768]{2,1,0:T(8,128)(2,1)} %get-tuple-element.144), channel_id=1, source_target_pairs={{0,8},{1,9},{2,10},{3,11},{4,12},{5,13},{6,14},{7,15},{8,0},{9,1},... | collective-permute-start | bytes 2654216 | tf_op jit(solution)/shard_map/ppermute | solution.py:936
  299.0 9.4 %copy-start.2 = (f32[2,288,768]{2,1,0:T(8,128)S(1)}, f32[2,288,768]{2,1,0:T(8,128)}, u32[]{:S(2)}) copy-start(f32[2,288,768]{2,1,0:T(8,128)} %get-tuple-element.152.ka_ref.kb_ref) | copy-start | bytes 5308420
  307.1 26.3 %collective-permute-start.16 = (bf16[1024,768]{1,0:T(8,128)(2,1)}, bf16[1024,768]{1,0:T(8,128)(2,1)}, u32[]{:S(2)}, u32[]{:S(2)}) collective-permute-start(bf16[1024,768]{1,0:T(8,128)(2,1)} %get-tuple-element.159), channel_id=1, source_target_pairs={{1,0},{2,1},{3,2},{5,4},{6,5},{7,6},{9,8},{10,9},{11,10},{13,12},{... | collective-permute-start | bytes 4718600 | tf_op jit(solution)/shard_map/ppermute | solution.py:922
  310.2 23.2 %collective-permute-start.17 = (bf16[1,288,768]{2,1,0:T(8,128)(2,1)}, bf16[1,288,768]{2,1,0:T(8,128)(2,1)S(1)}, u32[]{:S(2)}, u32[]{:S(2)}) collective-permute-start(bf16[1,288,768]{2,1,0:T(8,128)(2,1)} %get-tuple-element.153), channel_id=1, source_target_pairs={{0,16},{1,17},{2,18},{3,19},{4,20},{5,21},{6,22},{7,23},{8,24},{9,... | collective-permute-start | bytes 1327112 | tf_op jit(solution)/shard_map/ppermute | solution.py:936
  314.1 40.0 %copy-start.13 = (bf16[1024,768]{1,0:T(8,128)(2,1)S(1)}, bf16[1024,768]{1,0:T(8,128)(2,1)}, u32[]{:S(2)}) copy-start(bf16[1024,768]{1,0:T(8,128)(2,1)} %x_ref.1) | copy-start | bytes 4718596
  333.4 10.8 %collective-permute-start.18 = (bf16[1232,768]{1,0:T(8,128)(2,1)}, bf16[1232,768]{1,0:T(8,128)(2,1)S(1)}, u32[]{:S(2)}, u32[]{:S(2)}) collective-permute-start(bf16[1232,768]{1,0:T(8,128)(2,1)} %get-tuple-element.168), channel_id=1, source_target_pairs={{0,1},{1,0},{2,3},{3,2},{4,5},{5,4},{6,7},{7,6},{8,9},{9,8},{10,11... | collective-permute-start | bytes 5677064 | tf_op jit(solution)/shard_map/ppermute | solution.py:936
  344.2 2.1 copy-start.3
  346.3 8.1 %copy-start.22 = (pred[3]{0:T(512)(128)(4,1)S(1)}, pred[3]{0:T(512)(128)(4,1)}, u32[]{:S(2)}) copy-start(pred[3]{0:T(512)(128)(4,1)} %copy-done.21) | copy-start | bytes 13
  348.1 17.9 %collective-permute-start.20 = (bf16[624,768]{1,0:T(8,128)(2,1)}, bf16[624,768]{1,0:T(8,128)(2,1)S(1)}, u32[]{:S(2)}, u32[]{:S(2)}) collective-permute-start(bf16[624,768]{1,0:T(8,128)(2,1)} %get-tuple-element.169), channel_id=1, source_target_pairs={{0,2},{1,5},{2,0},{3,7},{4,6},{5,1},{6,4},{7,3},{8,10},{9,13},{10,... | collective-permute-start | bytes 2875400 | tf_op jit(solution)/shard_map/ppermute | solution.py:936
  362.4 8.8 %copy-start.14 = (bf16[1024,768]{1,0:T(8,128)(2,1)S(1)}, bf16[1024,768]{1,0:T(8,128)(2,1)}, u32[]{:S(2)}) copy-start(bf16[1024,768]{1,0:T(8,128)(2,1)} %x_ref.1) | copy-start | bytes 4718596
  362.4 8.8 %copy-start.15 = (f32[1024,768]{1,0:T(8,128)S(1)}, f32[1024,768]{1,0:T(8,128)}, u32[]{:S(2)}) copy-start(f32[1024,768]{1,0:T(8,128)} %get-tuple-element.164) | copy-start | bytes 9437188
  364.1 9.7 %copy-start.18 = (f32[288,768]{1,0:T(8,128)}, f32[288,768]{1,0:T(8,128)S(1)}, u32[]{:S(2)}) copy-start(f32[288,768]{1,0:T(8,128)S(1)} %bitcast_select_fusion) | copy-start | bytes 2654212
  366.8 11.1 %collective-permute-start.21 = (bf16[320,768]{1,0:T(8,128)(2,1)S(1)}, bf16[320,768]{1,0:T(8,128)(2,1)S(1)}, u32[]{:S(2)}, u32[]{:S(2)}) collective-permute-start(bf16[320,768]{1,0:T(8,128)(2,1)S(1)} %get-tuple-element.175), channel_id=1, source_target_pairs={{0,4},{1,3},{2,6},{3,1},{4,0},{5,7},{6,2},{7,5},{8,12},{9,11},{10,... | collective-permute-start | bytes 1474568 | tf_op jit(solution)/shard_map/ppermute | solution.py:936
  371.1 7.2 %copy-start.20 = (f32[1024,768]{1,0:T(8,128)S(1)}, f32[1024,768]{1,0:T(8,128)}, u32[]{:S(2)}) copy-start(f32[1024,768]{1,0:T(8,128)} %get-tuple-element.116) | copy-start | bytes 9437188
  373.8 8.6 %collective-permute-start.19 = (f32[16,768]{1,0:T(8,128)S(1)}, f32[16,768]{1,0:T(8,128)S(1)}, u32[]{:S(2)}, u32[]{:S(2)}) collective-permute-start(f32[16,768]{1,0:T(8,128)S(1)} %slice.29), channel_id=1, source_target_pairs={{1,0},{2,1},{3,2},{4,3},{5,4},{6,5},{7,6},{8,7},{9,8},{10,9},{11,1... | collective-permute-start | bytes 147464 | tf_op jit(solution)/shard_map/ppermute | solution.py:916
  378.0 12.3 %collective-permute-start.22 = (bf16[320,768]{1,0:T(8,128)(2,1)S(1)}, bf16[320,768]{1,0:T(8,128)(2,1)S(1)}, u32[]{:S(2)}, u32[]{:S(2)}) collective-permute-start(bf16[320,768]{1,0:T(8,128)(2,1)S(1)} %get-tuple-element.177), channel_id=1, source_target_pairs={{0,8},{1,9},{2,10},{3,11},{4,12},{5,13},{6,14},{7,15},{8,0},{9,1},... | collective-permute-start | bytes 1474568 | tf_op jit(solution)/shard_map/ppermute | solution.py:936
  382.4 22.3 %copy-start.19 = (f32[288,768]{1,0:T(8,128)S(1)}, f32[288,768]{1,0:T(8,128)}, u32[]{:S(2)}) copy-start(f32[288,768]{1,0:T(8,128)} %copy-done.18) | copy-start | bytes 2654212
  390.5 14.1 %collective-permute-start.23 = (bf16[320,768]{1,0:T(8,128)(2,1)S(1)}, bf16[320,768]{1,0:T(8,128)(2,1)S(1)}, u32[]{:S(2)}, u32[]{:S(2)}) collective-permute-start(bf16[320,768]{1,0:T(8,128)(2,1)S(1)} %get-tuple-element.179), channel_id=1, source_target_pairs={{8,24},{9,25},{10,26},{11,27},{12,28},{13,29},{14,30},{15,31},{16,... | collective-permute-start | bytes 1474568 | tf_op jit(solution)/shard_map/ppermute | solution.py:936
  404.7 1.2 copy-start.17
  (3 other events, 2.6 us)

commit v15 on v14

--- a/solution.py
+++ b/solution.py
@@ -92,32 +92,56 @@
             at = pl.ds(r, QB)
             ka[h, at, :] = jnp.where(mine, km_ref[at, :], first if r < rows else jnp.zeros((), BF))
             va[h, at, :] = jnp.where(mine, vm_ref[at, :], jnp.ones((), BF))
-    for i in range(rows // QB):
-        rs = pl.ds(i * QB, QB)
-        outs = []
-        sums = []
-        qf = qm_ref[rs, :].astype(F32) * 0.125
-        for h in range(2):
-            mine = (lane < 64) if h == 0 else (lane >= 64)
-            base = 64 if h == 0 else 0
-            qh = jnp.where(mine, qf, jnp.where(lane == base, 1.0, 0.0)).astype(BF)
-            nk = rows + (i + 1) * QB
-            s = dot_nt(qh, ka[h, 0:nk, :])
-            r = lax.broadcasted_iota(jnp.int32, (QB, QB), 0)
-            c = lax.broadcasted_iota(jnp.int32, (QB, QB), 1)
-            sd = jnp.where(c <= r, s[:, nk - QB :], -1e30)
-            se = s[:, : nk - QB]
-            m = jnp.maximum(
-                jnp.max(sd, axis=1, keepdims=True), jnp.max(se, axis=1, keepdims=True)
-            )
-            p = jnp.concatenate([jnp.exp(se - m).astype(BF), jnp.exp(sd - m).astype(BF)], 1)
-            o = dot(p, va[h, 0:nk, :])
-            outs.append(o / pltpu.roll(o, 64, 1))
-            sums.append(m + jnp.log(o))
-        res = jnp.where(lane < 64, outs[0], outs[1])
-        res = jnp.where(state == 0, vm_ref[pl.ds(rows + i * QB, QB), :].astype(F32), res)
-        o_ref[rs, :] = res.astype(BF)
-        l_ref[rs, :] = jnp.where(lane < 64, sums[1], sums[0])
+    heads = (row_ids(128) < 64) == (lane < 64)
+    heads = heads.astype(BF)
+    q_most = jnp.zeros((1, 128), F32)
+    k_most = jnp.zeros((1, 128), F32)
+    for r in range(0, rows, QB):
+        q = qm_ref[r : r + QB, :].astype(F32) * 0.125
+        q_most = jnp.maximum(q_most, jnp.max(dot((q * q).astype(BF), heads), axis=0, keepdims=True))
+    for r in range(0, 2 * rows, QB):
+        k = km_ref[r : r + QB, :].astype(F32)
+        k_most = jnp.maximum(k_most, jnp.max(dot((k * k).astype(BF), heads), axis=0, keepdims=True))
+    small_scores = jnp.max(q_most * k_most) <= 3025.0
+
+    def attend(subtract):
+        for i in range(rows // QB):
+            rs = pl.ds(i * QB, QB)
+            outs = []
+            sums = []
+            qf = qm_ref[rs, :].astype(F32) * 0.125
+            for h in range(2):
+                mine = (lane < 64) if h == 0 else (lane >= 64)
+                base = 64 if h == 0 else 0
+                qh = jnp.where(mine, qf, jnp.where(lane == base, 1.0, 0.0)).astype(BF)
+                nk = rows + (i + 1) * QB
+                s = dot_nt(qh, ka[h, 0:nk, :])
+                r = lax.broadcasted_iota(jnp.int32, (QB, QB), 0)
+                c = lax.broadcasted_iota(jnp.int32, (QB, QB), 1)
+                sd = jnp.where(c <= r, s[:, nk - QB :], -1e30)
+                se = s[:, : nk - QB]
+                if subtract:
+                    m = jnp.maximum(
+                        jnp.max(sd, axis=1, keepdims=True), jnp.max(se, axis=1, keepdims=True)
+                    )
+                    se = se - m
+                    sd = sd - m
+                p = jnp.concatenate([jnp.exp(se).astype(BF), jnp.exp(sd).astype(BF)], 1)
+                o = dot(p, va[h, 0:nk, :])
+                outs.append(o / pltpu.roll(o, 64, 1))
+                sums.append(m + jnp.log(o) if subtract else jnp.log(o))
+            res = jnp.where(lane < 64, outs[0], outs[1])
+            res = jnp.where(state == 0, vm_ref[pl.ds(rows + i * QB, QB), :].astype(F32), res)
+            o_ref[rs, :] = res.astype(BF)
+            l_ref[rs, :] = jnp.where(lane < 64, sums[1], sums[0])
+
+    @pl.when(small_scores)
+    def _():
+        attend(False)
+
+    @pl.when(jnp.logical_not(small_scores))
+    def _():
+        attend(True)
 
 
 def call_in_parts(body, in_specs, out_specs, out_shape, earlier, part, **options):
@@ -450,9 +474,9 @@
                 away = pl.ds(pl.multiple_of((2 * j + 1 - core) * height, 16), wide)
                 here = pl.ds(pl.multiple_of((2 * j + core) * height, 16), wide)
                 send_ref[to, :] = acc[away, :].astype(BF)
-                keep_ref[to, :] = acc[here, :]
+                keep_ref[to, :] = acc[here, :].astype(BF)
             send_ref[pieces * wide :, :] = small.astype(BF)
-            keep_ref[pieces * wide :, :] = small
+            keep_ref[pieces * wide :, :] = small.astype(BF)
         else:
             keep_ref[...] = acc[0 : 3 * D, :].astype(BF)
             ends_ref[...] = small
@@ -471,7 +495,7 @@
 
     if pieces:
         packed = 3 * D // 2 + 16 * pieces + 16
-        outs = [jax.ShapeDtypeStruct((packed, D), BF), jax.ShapeDtypeStruct((packed, D), F32)]
+        outs = [jax.ShapeDtypeStruct((packed, D), BF), jax.ShapeDtypeStruct((packed, D), BF)]
         out_at = [whole((packed, D))] * 2
     else:
         outs = [jax.ShapeDtypeStruct((3 * D, D), BF), jax.ShapeDtypeStruct((16, D), F32)]
@@ -503,7 +527,7 @@
 
     def body(index_ref, keep_ref, got_ref, send_ref, stay_ref):
         if not taken:
-            total = keep_ref[...] + got_ref[...].astype(F32)
+            total = keep_ref[...].astype(F32) + got_ref[...].astype(F32)
             send_ref[...] = total.astype(BF)
             stay_ref[...] = total
             return
@@ -511,9 +535,9 @@
             to = pl.ds(j * height, height)
             away = pl.ds(pl.multiple_of(index_ref[j] * height, 16), height)
             here = pl.ds(pl.multiple_of(index_ref[taken + j] * height, 16), height)
-            send_ref[to, :] = (keep_ref[away, :] + got_ref[away, :].astype(F32)).astype(BF)
-            stay_ref[to, :] = keep_ref[here, :] + got_ref[here, :].astype(F32)
-        end = keep_ref[rows - 16 :, :] + got_ref[rows - 16 :, :].astype(F32)
+            send_ref[to, :] = (keep_ref[away, :].astype(F32) + got_ref[away, :].astype(F32)).astype(BF)
+            stay_ref[to, :] = keep_ref[here, :].astype(F32) + got_ref[here, :].astype(F32)
+        end = keep_ref[rows - 16 :, :].astype(F32) + got_ref[rows - 16 :, :].astype(F32)
         send_ref[taken * height :, :] = end.astype(BF)
         stay_ref[taken * height :, :] = end
 
@@ -879,7 +903,7 @@
     return pl.pallas_call(
         ffn_kernel,
         grid=(4,),
-        in_specs=[scalars, scalars, act, act, act, whole((16, D)), held, held, held, held],
+        in_specs=[scalars, scalars, act, act, act, whole((16, D)), held, held, held, pl.BlockSpec(memory_space=pltpu.VMEM)],
         out_specs=[act, act, act, whole((1, D)), held, held],
         out_shape=[
             jax.ShapeDtypeStruct((rows, D), BF),

time: 408 us -> 401 us (0.983); the launches traced: 410 us -> 397 us
  Pallas kernels: 216 us -> 202 us
    pallas_call x1, Pallas kernels: 55.1 us -> 47.3 us  [ffn(): pl.pallas_call(ffn_kernel, grid=(4,), in_specs=[scalars, scalars, act, ac...]
    pallas_call x3, Pallas kernels: 49.3 us -> 44.2 us  [att_fwd(): call_in_parts(att_fwd_kernel, [pl.BlockSpec(memory_space=pltpu.SMEM), col...]
  transfers between devices with their start and end apart: 24 -> 24, of which waited for: 13 -> 14; matrix products, arithmetic and copies ran while one was open for 5% -> 5% of each run, Pallas kernels for 35% -> 34%
where the time goes in v15:
time: 401 us; the launch traced here: 397 us
  Pallas kernels  202 us (50%)
  waiting for transfers between devices  104 us (26%)
  starting transfers between devices  49.8 us (12%)
  local copies, waits for them, and re-layouts  19.3 us (5%)
  other arithmetic  17.7 us (4%)
    ppermute x20, waiting for transfers between devices, swap(): return lax.ppermute(block, AXES, route)  103 us
    pallas_call x4, Pallas kernels, att_bwd(): call_in_parts(att_bwd_kernel, [pl.BlockSpec(memory_space=pltpu.SMEM), own...  50.4 us
    pallas_call x1, Pallas kernels, ffn(): pl.pallas_call(ffn_kernel, grid=(4,), in_specs=[scalars, scalars, act, ac...  47.3 us
    pallas_call x3, Pallas kernels, att_fwd(): call_in_parts(att_fwd_kernel, [pl.BlockSpec(memory_space=pltpu.SMEM), col...  44.2 us
    ppermute x20, starting transfers between devices, swap(): return lax.ppermute(block, AXES, route)  40.3 us
    pallas_call x1, Pallas kernels, qkv_bwd(): pl.pallas_call(body, grid=(blocks,), in_specs=[pl.BlockSpec(memory_space=...  18.6 us
    pallas_call x4, Pallas kernels, merge_grid(): pl.pallas_call(body, grid_spec=pltpu.PrefetchScalarGridSpec(num_scalar_pr...  14 us
    pallas_call x1, Pallas kernels, qkv_fwd(): pl.pallas_call(body, grid=(blocks,), in_specs=[pl.BlockSpec(memory_space=...  13.3 us
  transfers between devices with their start and end apart: 24, of which 14 were waited for; matrix products, arithmetic and copies ran while one was open for 5% of the time, Pallas kernels for 34%

profile of v15, /device:TPU:0, one launch (start us, length us, event | category | flops | bytes accessed | tf_op | source)
XLA Modules:
  0.0 396.6 jit_solution(16836885081646732020)
XLA Ops:
  1.5 2.3 collective-permute-start
  4.7 1.5 fusion.8
  7.3 4.6 %collective-permute-start.3 = (bf16[1024,768]{1,0:T(8,128)(2,1)S(1)}, bf16[1024,768]{1,0:T(8,128)(2,1)S(1)}, u32[]{:S(2)}, u32[]{:S(2)}) collective-permute-start(bf16[1024,768]{1,0:T(8,128)(2,1)S(1)} %copy-done.12), channel_id=1, source_target_pairs={{0,1},{1,2},{2,3},{4,5},{5,6},{6,7},{8,9},{9,10},{10,11},{12,13},{... | collective-permute-start | bytes 4718600 | tf_op jit(solution)/shard_map/ppermute | solution.py:946
  11.9 4.4 %collective-permute-start.2 = (bf16[304,768]{1,0:T(8,128)(2,1)S(1)}, bf16[304,768]{1,0:T(8,128)(2,1)S(1)}, u32[]{:S(2)}, u32[]{:S(2)}) collective-permute-start(bf16[304,768]{1,0:T(8,128)(2,1)S(1)} %pad_maximum_fusion.1.refs_0_), channel_id=1, source_target_pairs={{0,16},{1,17},{2,18},{3,19},{4,20},{5,21},{6,22},{7,23},{8,24},{9,... | collective-permute-start | bytes 1400840 | tf_op jit(solution)/shard_map/ppermute | solution.py:960
  16.3 1.6 collective-permute-start.1
  18.1 19.6 %collective-permute-done.2.refs_2_ = bf16[304,768]{1,0:T(8,128)(2,1)S(1)} collective-permute-done((bf16[304,768]{1,0:T(8,128)(2,1)S(1)}, bf16[304,768]{1,0:T(8,128)(2,1)S(1)}, u32[]{:S(2)}, u32[]{:S(2)}) %collective-permute-start.2) | collective-permute-done | bytes 466976 | tf_op jit(solution)/shard_map/ppermute | solution.py:960
  41.6 8.4 %collective-permute-done.4.refs_3_ = bf16[304,768]{1,0:T(8,128)(2,1)S(1)} collective-permute-done((bf16[304,768]{1,0:T(8,128)(2,1)S(1)}, bf16[304,768]{1,0:T(8,128)(2,1)S(1)}, u32[]{:S(2)}, u32[]{:S(2)}) %collective-permute-start.4) | collective-permute-done | bytes 466976 | tf_op jit(solution)/shard_map/ppermute | solution.py:960
  52.8 1.9 arrange.1
  54.9 8.6 %collective-permute-done.5.got_ref = bf16[304,768]{1,0:T(8,128)(2,1)S(1)} collective-permute-done((bf16[304,768]{1,0:T(8,128)(2,1)S(1)}, bf16[304,768]{1,0:T(8,128)(2,1)S(1)}, u32[]{:S(2)}, u32[]{:S(2)}) %collective-permute-start.5) | collective-permute-done | bytes 466976 | tf_op jit(solution)/shard_map/ppermute | solution.py:960
  64.9 12.0 %collective-permute-done.6.got_ref = bf16[592,768]{1,0:T(8,128)(2,1)S(1)} collective-permute-done((bf16[592,768]{1,0:T(8,128)(2,1)S(1)}, bf16[592,768]{1,0:T(8,128)(2,1)S(1)}, u32[]{:S(2)}, u32[]{:S(2)}) %collective-permute-start.6) | collective-permute-done | bytes 909344 | tf_op jit(solution)/shard_map/ppermute | solution.py:960
  78.0 2.9 collective-permute-done.7.refs_3_
  80.9 13.3 %qkv_fwd.1 = (bf16[2048,2304]{1,0:T(8,128)(2,1)}, f32[16,768]{1,0:T(8,128)}, bf16[2304,768]{1,0:T(8,128)(2,1)}) custom-call(s32[8]{0:T(128)} %stack.217.refs_0_, bf16[2048,768]{1,0:T(8,128)(2,1)} %copy-done.16, bf16[1168,768]{1,0:T(8,128)(2,1)} %copy-done.5, bf16[1168,768]{1,0:T(8,128)(2,1)} %collective-permute-done.7.refs_3_), custom_call_target="tpu_custom_call" | custom-call | flops 7247757312 | bytes 15728640 | tf_op jit(solution)/shard_map/qkv_fwd/pallas_call | solution.py:738
  96.3 1.8 join_held.1
  99.6 14.5 %att_fwd.3 = (bf16[1024,768]{1,0:T(8,128)(2,1)}, f32[1024,768]{1,0:T(8,128)}, bf16[1024,768]{1,0:T(8,128)(2,1)}, bf16[2048,768]{1,0:T(8,128)(2,1)}, bf16[2048,768]{1,0:T(8,128)(2,1)}) custom-call(s32[1]{0:T(128)S(6)} %select_n.125.refs_0_.state_ref, bf16[2048,2304]{1,0:T(8,128)(2,1)} %get-tuple-element.98.refs_1_.refs_2_.refs_3_.refs_4_.refs_7_.refs_8_.refs_9_.refs_10_, ...), custom_call_target="tpu_custom_call" | custom-call | flops 6442450944 | bytes 7864320 | tf_op jit(solution)/shard_map/att_fwd/pallas_call | solution.py:176
  114.1 15.2 %att_fwd.4 = (bf16[1024,768]{1,0:T(8,128)(2,1)}, f32[1024,768]{1,0:T(8,128)}, bf16[1024,768]{1,0:T(8,128)(2,1)}, bf16[2048,768]{1,0:T(8,128)(2,1)}, bf16[2048,768]{1,0:T(8,128)(2,1)}) custom-call(s32[1]{0:T(128)S(6)} %select_n.125.refs_0_.state_ref, ...), custom_call_target="tpu_custom_call", output_to_operand_aliasing={{0}: (6, {}), {1}: (7, {}), {2}: (8, {}), {3}: (9, {}), {4}... | custom-call | flops 6442450944 | bytes 7864320 | tf_op jit(solution)/shard_map/att_fwd/pallas_call | solution.py:176
  131.1 14.6 %att_fwd.5 = (bf16[1024,768]{1,0:T(8,128)(2,1)}, f32[1024,768]{1,0:T(8,128)}, bf16[1024,768]{1,0:T(8,128)(2,1)}, bf16[2048,768]{1,0:T(8,128)(2,1)}, bf16[2048,768]{1,0:T(8,128)(2,1)}) custom-call(s32[1]{0:T(128)S(6)} %select_n.125.refs_0_.state_ref, ...), custom_call_target="tpu_custom_call", output_to_operand_aliasing={{0}: (6, {}), {1}: (7, {}), {2}: (8, {}), {3}: (9, {}), {4}... | custom-call | flops 6442450944 | bytes 7864320 | tf_op jit(solution)/shard_map/att_fwd/pallas_call | solution.py:176
  145.7 1.5 copy-done.24
  147.2 47.3 %ffn.1 = (bf16[1024,768]{1,0:T(8,128)(2,1)}, f32[1024,768]{1,0:T(8,128)}, bf16[1024,768]{1,0:T(8,128)(2,1)}, f32[1,768]{1,0:T(1,128)}, bf16[36,4,24,768]{3,2,1,0...) custom-call(s32[1]{0:T(128)S(6)} %select_n.125.refs_0_.state_ref, s32[25]{0:T(128)} %stack.211.index_ref, ...), custom_call_target="tpu_custom_call" | custom-call | flops 32614907904 | bytes 40894464 | tf_op jit(solution)/shard_map/ffn/pallas_call | solution.py:903
  195.2 9.3 %att_bwd.4 = (bf16[1024,768]{1,0:T(8,128)(2,1)}, bf16[8,768]{1,0:T(8,128)(2,1)}, bf16[2048,768]{1,0:T(8,128)(2,1)}, bf16[2048,768]{1,0:T(8,128)(2,1)}, f32[16,768]{1,0:T(8,128)}) custom-call(s32[1]{0:T(128)S(6)} %select_n.125.refs_0_.state_ref, bf16[1024,768]{1,0:T(8,128)(2,1)} %get-tuple-element.117.refs_1_, bf16[2048,768]{1,0:T(8,128)(2,1)} %get-tuple-element.118.refs_2_, ...), custom_call_target="tpu_custom_call" | custom-call | flops 8053063680 | bytes 5505024 | tf_op jit(solution)/shard_map/att_bwd/pallas_call | solution.py:333
  204.5 7.2 %merge_grid.4 = (bf16[6,288,768]{2,1,0:T(8,128)(2,1)}, bf16[6,288,768]{2,1,0:T(8,128)(2,1)}) custom-call(s32[12]{0:T(128)S(1)} %stack.243.index_ref, bf16[12,288,768]{2,1,0:T(8,128)(2,1)S(1)} %bitcast.71, bf16[12,288,768]{2,1,0:T(8,128)(2,1)} %collective-permute-done.12.ga_ref.gb_ref, bf16[12,288,768]{2,1,0:T(8,128)(2,1)S(1)} %bitcast.72, ...), custom_call_target="tpu_custom_call" | custom-call | flops 2654208 | bytes 21233664 | tf_op jit(solution)/shard_map/merge_grid/pallas_call | solution.py:569
  211.8 15.8 %att_bwd.5 = (bf16[1024,768]{1,0:T(8,128)(2,1)}, bf16[8,768]{1,0:T(8,128)(2,1)}, bf16[2048,768]{1,0:T(8,128)(2,1)}, bf16[2048,768]{1,0:T(8,128)(2,1)}, f32[16,768]{1,0:T(8,128)}) custom-call(s32[1]{0:T(128)S(6)} %select_n.125.refs_0_.state_ref, ...), custom_call_target="tpu_custom_call", output_to_operand_aliasing={{0}: (12, {}), {1}: (13, {}), {2}: (14, {}), {3}: (15, {}),... | custom-call | flops 16106127360 | bytes 11010048 | tf_op jit(solution)/shard_map/att_bwd/pallas_call | solution.py:333
  227.6 16.3 %collective-permute-done.13.ga_ref.gb_ref = bf16[6,288,768]{2,1,0:T(8,128)(2,1)S(1)} collective-permute-done((bf16[6,288,768]{2,1,0:T(8,128)(2,1)}, bf16[6,288,768]{2,1,0:T(8,128)(2,1)S(1)}, u32[]{:S(2)}, u32[]{:S(2)}) %collective-permute-start.13) | collective-permute-done | bytes 2654240 | tf_op jit(solution)/shard_map/ppermute | solution.py:960
  243.9 3.0 merge_grid.5
  248.2 9.5 %att_bwd.6 = (bf16[1024,768]{1,0:T(8,128)(2,1)}, bf16[8,768]{1,0:T(8,128)(2,1)}, bf16[2048,768]{1,0:T(8,128)(2,1)}, bf16[2048,768]{1,0:T(8,128)(2,1)}, f32[16,768]{1,0:T(8,128)}) custom-call(s32[1]{0:T(128)S(6)} %select_n.125.refs_0_.state_ref, ...), custom_call_target="tpu_custom_call", output_to_operand_aliasing={{0}: (12, {}), {1}: (13, {}), {2}: (14, {}), {3}: (15, {}),... | custom-call | flops 8053063680 | bytes 5505024 | tf_op jit(solution)/shard_map/att_bwd/pallas_call | solution.py:333
  257.8 7.1 %collective-permute-done.14.ga_ref.gb_ref = bf16[3,288,768]{2,1,0:T(8,128)(2,1)S(1)} collective-permute-done((bf16[3,288,768]{2,1,0:T(8,128)(2,1)}, bf16[3,288,768]{2,1,0:T(8,128)(2,1)S(1)}, u32[]{:S(2)}, u32[]{:S(2)}) %collective-permute-start.14) | collective-permute-done | bytes 1327136 | tf_op jit(solution)/shard_map/ppermute | solution.py:960
  264.9 2.2 merge_grid.6
  267.9 15.7 %att_bwd.7 = (bf16[1024,768]{1,0:T(8,128)(2,1)}, bf16[8,768]{1,0:T(8,128)(2,1)}, bf16[2048,768]{1,0:T(8,128)(2,1)}, bf16[2048,768]{1,0:T(8,128)(2,1)}, f32[16,768]{1,0:T(8,128)}) custom-call(s32[1]{0:T(128)S(6)} %select_n.125.refs_0_.state_ref, ...), custom_call_target="tpu_custom_call", output_to_operand_aliasing={{0}: (12, {}), {1}: (13, {}), {2}: (14, {}), {3}: (15, {}),... | custom-call | flops 16106127360 | bytes 11010048 | tf_op jit(solution)/shard_map/att_bwd/pallas_call | solution.py:333
  283.6 8.0 %before_bwd.1 = (bf16[1024,768]{1,0:T(8,128)(2,1)}, f32[1,768]{1,0:T(1,128)}) custom-call(bf16[2048,768]{1,0:T(8,128)(2,1)} %copy-done.16, bf16[8,768]{1,0:T(8,128)(2,1)} %get-tuple-element.155.dt_ref.refs_3_, bf16[2048,768]{1,0:T(8,128)(2,1)} %get-tuple-element.156.dk_ref.refs_4_, bf16[2048,768]{1,0:T(8,128)(2,1)} %get-tuple-element.157.dv_ref.refs_5_, ...), custom_call_target="tpu_custom_call" | custom-call | flops 2415919104 | bytes 9437184 | tf_op jit(solution)/shard_map/before_bwd/pallas_call | solution.py:412
  293.1 1.7 merge_grid.7
  294.8 9.0 %collective-permute-start.17 = (bf16[1,288,768]{2,1,0:T(8,128)(2,1)}, bf16[1,288,768]{2,1,0:T(8,128)(2,1)S(1)}, u32[]{:S(2)}, u32[]{:S(2)}) collective-permute-start(bf16[1,288,768]{2,1,0:T(8,128)(2,1)} %get-tuple-element.153), channel_id=1, source_target_pairs={{0,16},{1,17},{2,18},{3,19},{4,20},{5,21},{6,22},{7,23},{8,24},{9,... | collective-permute-start | bytes 1327112 | tf_op jit(solution)/shard_map/ppermute | solution.py:960
  303.8 18.6 %qkv_bwd.1 = (bf16[1232,768]{1,0:T(8,128)(2,1)}, bf16[1232,768]{1,0:T(8,128)(2,1)}, f32[1024,768]{1,0:T(8,128)}) custom-call(s32[1]{0:T(128)} %bitcast.24.refs_0_.index_ref, bf16[2048,768]{1,0:T(8,128)(2,1)} %copy-done.16, bf16[1024,768]{1,0:T(8,128)(2,1)} %get-tuple-element.161.refs_2_, bf16[8,768]{1,0:T(8,128)(2,1)} %get-tuple-element.155.dt_ref.refs_3_, ...), custom_call_target="tpu_custom_call" | custom-call | flops 9663676416 | bytes 23592960 | tf_op jit(solution)/shard_map/qkv_bwd/pallas_call | solution.py:507
  323.5 3.6 collective-permute-done.18.got_ref
  327.1 1.5 copy-done.4
  328.6 1.8 merge.4
  330.4 3.5 collective-permute-start.20
  335.2 2.2 convert_add_fusion.1
  337.4 2.4 copy.44
  339.8 2.4 reshape.115
  342.2 1.7 bitcast_select_fusion
  343.9 2.0 collective-permute-done.20.got_ref
  346.6 8.8 %collective-permute-start.21 = (bf16[320,768]{1,0:T(8,128)(2,1)S(1)}, bf16[320,768]{1,0:T(8,128)(2,1)S(1)}, u32[]{:S(2)}, u32[]{:S(2)}) collective-permute-start(bf16[320,768]{1,0:T(8,128)(2,1)S(1)} %get-tuple-element.175), channel_id=1, source_target_pairs={{0,4},{1,3},{2,6},{3,1},{4,0},{5,7},{6,2},{7,5},{8,12},{9,11},{10,... | collective-permute-start | bytes 1474568 | tf_op jit(solution)/shard_map/ppermute | solution.py:960
  355.4 2.6 fusion.2
  359.3 2.9 collective-permute-done.21.got_ref
  362.3 4.4 %collective-permute-start.22 = (bf16[320,768]{1,0:T(8,128)(2,1)S(1)}, bf16[320,768]{1,0:T(8,128)(2,1)S(1)}, u32[]{:S(2)}, u32[]{:S(2)}) collective-permute-start(bf16[320,768]{1,0:T(8,128)(2,1)S(1)} %get-tuple-element.177), channel_id=1, source_target_pairs={{0,8},{1,9},{2,10},{3,11},{4,12},{5,13},{6,14},{7,15},{8,0},{9,1},... | collective-permute-start | bytes 1474568 | tf_op jit(solution)/shard_map/ppermute | solution.py:960
  366.7 4.1 %fusion.5 = f32[1024,768]{1,0:T(8,128)} fusion(f32[1024,768]{1,0:T(8,128)S(1)} %copy-done.20, bf16[1024,768]{1,0:T(8,128)(2,1)S(1)} %copy-done.14, f32[1024,768]{1,0:T(8,128)S(1)} %copy-done.15, bf16[1024,768]{1,0:T(8,128)(2,1)} %collective-permute-done.16, f32[1024]{0:T(1024)S(1)} %broadcast_multiply_fusion, f32[768]{0:T(1024)S(1)} %slice_reduce_fusion, ...), kind=kLoop, calls=%fused_computation.7 | loop fusion | flops 7077888 | bytes 12594176 | tf_op jit(solution)/shard_map/add | solution.py:1197
  370.8 6.2 %collective-permute-done.22.got_ref = bf16[320,768]{1,0:T(8,128)(2,1)S(1)} collective-permute-done((bf16[320,768]{1,0:T(8,128)(2,1)S(1)}, bf16[320,768]{1,0:T(8,128)(2,1)S(1)}, u32[]{:S(2)}, u32[]{:S(2)}) %collective-permute-start.22) | collective-permute-done | bytes 491552 | tf_op jit(solution)/shard_map/ppermute | solution.py:960
  379.2 12.2 %collective-permute-done.23 = bf16[320,768]{1,0:T(8,128)(2,1)S(1)} collective-permute-done((bf16[320,768]{1,0:T(8,128)(2,1)S(1)}, bf16[320,768]{1,0:T(8,128)(2,1)S(1)}, u32[]{:S(2)}, u32[]{:S(2)}) %collective-permute-start.23) | collective-permute-done | bytes 491552 | tf_op jit(solution)/shard_map/ppermute | solution.py:960
  392.6 3.5 fusion.16
  (119 shorter events, 27.8 us)
Async XLA Ops:
  1.5 3.3 collective-permute-start
  4.7 2.6 copy-start.21
  4.7 2.6 copy-start.12
  7.3 10.6 %collective-permute-start.3 = (bf16[1024,768]{1,0:T(8,128)(2,1)S(1)}, bf16[1024,768]{1,0:T(8,128)(2,1)S(1)}, u32[]{:S(2)}, u32[]{:S(2)}) collective-permute-start(bf16[1024,768]{1,0:T(8,128)(2,1)S(1)} %copy-done.12), channel_id=1, source_target_pairs={{0,1},{1,2},{2,3},{4,5},{5,6},{6,7},{8,9},{9,10},{10,11},{12,13},{... | collective-permute-start | bytes 4718600 | tf_op jit(solution)/shard_map/ppermute | solution.py:946
  11.9 25.7 %collective-permute-start.2 = (bf16[304,768]{1,0:T(8,128)(2,1)S(1)}, bf16[304,768]{1,0:T(8,128)(2,1)S(1)}, u32[]{:S(2)}, u32[]{:S(2)}) collective-permute-start(bf16[304,768]{1,0:T(8,128)(2,1)S(1)} %pad_maximum_fusion.1.refs_0_), channel_id=1, source_target_pairs={{0,16},{1,17},{2,18},{3,19},{4,20},{5,21},{6,22},{7,23},{8,24},{9,... | collective-permute-start | bytes 1400840 | tf_op jit(solution)/shard_map/ppermute | solution.py:960
  16.3 24.5 %collective-permute-start.1 = (bf16[304,768]{1,0:T(8,128)(2,1)S(1)}, bf16[304,768]{1,0:T(8,128)(2,1)S(1)}, u32[]{:S(2)}, u32[]{:S(2)}) collective-permute-start(bf16[304,768]{1,0:T(8,128)(2,1)S(1)} %pad_maximum_fusion.1.refs_0_), channel_id=1, source_target_pairs={{0,8},{1,9},{2,10},{3,11},{4,12},{5,13},{6,14},{7,15},{8,0},{9,1},... | collective-permute-start | bytes 1400840 | tf_op jit(solution)/shard_map/ppermute | solution.py:960
  18.1 19.6 %copy-start.16 = (bf16[2048,768]{1,0:T(8,128)(2,1)}, bf16[2048,768]{1,0:T(8,128)(2,1)S(1)}, u32[]{:S(2)}) copy-start(bf16[2048,768]{1,0:T(8,128)(2,1)S(1)} %constant_dynamic-update-slice_fusion.refs_1_.x_ref) | copy-start | bytes 9437188
  37.7 12.3 %collective-permute-start.4 = (bf16[304,768]{1,0:T(8,128)(2,1)S(1)}, bf16[304,768]{1,0:T(8,128)(2,1)S(1)}, u32[]{:S(2)}, u32[]{:S(2)}) collective-permute-start(bf16[304,768]{1,0:T(8,128)(2,1)S(1)} %collective-permute-done.2.refs_2_), channel_id=1, source_target_pairs={{0,8},{1,9},{2,10},{3,11},{4,12},{5,13},{6,14},{7,15},{8,0},{9,1},... | collective-permute-start | bytes 1400840 | tf_op jit(solution)/shard_map/ppermute | solution.py:960
  50.8 1.0 copy-start.9
  54.8 39.4 %copy-start.6 = (bf16[864,768]{1,0:T(8,128)(2,1)}, bf16[864,768]{1,0:T(8,128)(2,1)S(1)}, u32[]{:S(2)}) copy-start(bf16[864,768]{1,0:T(8,128)(2,1)S(1)} %get-tuple-element.99.own_ref) | copy-start | bytes 3981316
  54.8 8.6 %collective-permute-start.5 = (bf16[304,768]{1,0:T(8,128)(2,1)S(1)}, bf16[304,768]{1,0:T(8,128)(2,1)S(1)}, u32[]{:S(2)}, u32[]{:S(2)}) collective-permute-start(bf16[304,768]{1,0:T(8,128)(2,1)S(1)} %get-tuple-element.97.own_ref), channel_id=1, source_target_pairs={{0,2},{1,5},{2,0},{3,7},{4,6},{5,1},{6,4},{7,3},{8,10},{9,13},{10,... | collective-permute-start | bytes 1400840 | tf_op jit(solution)/shard_map/ppermute | solution.py:960
  63.5 13.4 %collective-permute-start.6 = (bf16[592,768]{1,0:T(8,128)(2,1)S(1)}, bf16[592,768]{1,0:T(8,128)(2,1)S(1)}, u32[]{:S(2)}, u32[]{:S(2)}) collective-permute-start(bf16[592,768]{1,0:T(8,128)(2,1)S(1)} %join.2.own_ref), channel_id=1, source_target_pairs={{0,4},{1,3},{2,6},{3,1},{4,0},{5,7},{6,2},{7,5},{8,12},{9,11},{10,... | collective-permute-start | bytes 2727944 | tf_op jit(solution)/shard_map/ppermute | solution.py:960
  77.0 3.9 copy-start.5
  77.0 3.9 collective-permute-start.7
  77.1 18.0 %collective-permute-start.8 = (bf16[864,768]{1,0:T(8,128)(2,1)S(1)}, bf16[864,768]{1,0:T(8,128)(2,1)}, u32[]{:S(2)}, u32[]{:S(2)}) collective-permute-start(bf16[864,768]{1,0:T(8,128)(2,1)S(1)} %get-tuple-element.99.own_ref), channel_id=1, source_target_pairs={{0,2},{1,5},{2,0},{3,7},{4,6},{5,1},{6,4},{7,3},{8,10},{9,13},{10,... | collective-permute-start | bytes 3981320 | tf_op jit(solution)/shard_map/ppermute | solution.py:960
  95.0 1.3 copy-start.7
  98.1 16.0 %copy-start.3 = (bf16[1728,768]{1,0:T(8,128)(2,1)}, bf16[1728,768]{1,0:T(8,128)(2,1)S(1)}, u32[]{:S(2)}) copy-start(bf16[1728,768]{1,0:T(8,128)(2,1)S(1)} %join_held.1) | copy-start | bytes 7962628
  98.1 16.0 %collective-permute-start.10 = (bf16[1728,768]{1,0:T(8,128)(2,1)S(1)}, bf16[1728,768]{1,0:T(8,128)(2,1)S(1)}, u32[]{:S(2)}, u32[]{:S(2)}) collective-permute-start(bf16[1728,768]{1,0:T(8,128)(2,1)S(1)} %join_held.1), channel_id=1, source_target_pairs={{0,1},{1,0},{2,3},{3,2},{4,5},{5,4},{6,7},{7,6},{8,9},{9,8},{10,11... | collective-permute-start | bytes 7962632 | tf_op jit(solution)/shard_map/ppermute | solution.py:960
  98.2 32.2 %collective-permute-start.9 = (bf16[1728,768]{1,0:T(8,128)(2,1)S(1)}, bf16[1728,768]{1,0:T(8,128)(2,1)}, u32[]{:S(2)}, u32[]{:S(2)}) collective-permute-start(bf16[1728,768]{1,0:T(8,128)(2,1)S(1)} %join_held.1), channel_id=1, source_target_pairs={{0,4},{1,3},{2,6},{3,1},{4,0},{5,7},{6,2},{7,5},{8,12},{9,11},{10,... | collective-permute-start | bytes 7962632 | tf_op jit(solution)/shard_map/ppermute | solution.py:960
  114.1 15.2 %copy-start.23 = (bf16[1728,768]{1,0:T(8,128)(2,1)}, bf16[1728,768]{1,0:T(8,128)(2,1)S(1)}, u32[]{:S(2)}) copy-start(bf16[1728,768]{1,0:T(8,128)(2,1)S(1)} %collective-permute-done.10) | copy-start | bytes 7962628
  130.4 15.3 %collective-permute-start.11 = (bf16[1728,768]{1,0:T(8,128)(2,1)}, bf16[1728,768]{1,0:T(8,128)(2,1)S(1)}, u32[]{:S(2)}, u32[]{:S(2)}) collective-permute-start(bf16[1728,768]{1,0:T(8,128)(2,1)} %hold.1), channel_id=1, source_target_pairs={{0,1},{1,0},{2,3},{3,2},{4,5},{5,4},{6,7},{7,6},{8,9},{9,8},{10,11... | collective-permute-start | bytes 7962632 | tf_op jit(solution)/shard_map/ppermute | solution.py:960
  145.6 1.5 copy-start.24
  194.5 10.0 %collective-permute-start.12 = (bf16[12,288,768]{2,1,0:T(8,128)(2,1)}, bf16[12,288,768]{2,1,0:T(8,128)(2,1)}, u32[]{:S(2)}, u32[]{:S(2)}) collective-permute-start(bf16[12,288,768]{2,1,0:T(8,128)(2,1)} %bitcast.75), channel_id=1, source_target_pairs={{0,1},{1,0},{2,3},{3,2},{4,5},{5,4},{6,7},{7,6},{8,9},{9,8},{10,11... | collective-permute-start | bytes 15925256 | tf_op jit(solution)/shard_map/ppermute | solution.py:960
  195.2 9.4 %slice-start = ((s8[5308416]{0:T(1024)(128)(4,1)}), s8[4194304]{0:T(1024)(128)(4,1)S(1)}, s32[]{:S(2)}) async-start(s8[5308416]{0:T(1024)(128)(4,1)} %bitcast.69), calls=%async_computation | async-start | bytes 8388608
  195.2 9.4 %slice-start.1 = ((s8[5308416]{0:T(1024)(128)(4,1)}), s8[1114112]{0:T(1024)(128)(4,1)S(1)}, s32[]{:S(2)}) async-start(s8[5308416]{0:T(1024)(128)(4,1)} %bitcast.69), calls=%async_computation.1 | async-start | bytes 2228224
  211.7 32.2 %collective-permute-start.13 = (bf16[6,288,768]{2,1,0:T(8,128)(2,1)}, bf16[6,288,768]{2,1,0:T(8,128)(2,1)S(1)}, u32[]{:S(2)}, u32[]{:S(2)}) collective-permute-start(bf16[6,288,768]{2,1,0:T(8,128)(2,1)} %get-tuple-element.126), channel_id=1, source_target_pairs={{0,2},{1,5},{2,0},{3,7},{4,6},{5,1},{6,4},{7,3},{8,10},{9,13},{10,... | collective-permute-start | bytes 7962632 | tf_op jit(solution)/shard_map/ppermute | solution.py:960
  211.8 32.1 %copy-start = (bf16[6,288,768]{2,1,0:T(8,128)(2,1)S(1)}, bf16[6,288,768]{2,1,0:T(8,128)(2,1)}, u32[]{:S(2)}) copy-start(bf16[6,288,768]{2,1,0:T(8,128)(2,1)} %get-tuple-element.134.ka_ref.kb_ref) | copy-start | bytes 7962628
  246.9 18.0 %collective-permute-start.14 = (bf16[3,288,768]{2,1,0:T(8,128)(2,1)}, bf16[3,288,768]{2,1,0:T(8,128)(2,1)S(1)}, u32[]{:S(2)}, u32[]{:S(2)}) collective-permute-start(bf16[3,288,768]{2,1,0:T(8,128)(2,1)} %get-tuple-element.135), channel_id=1, source_target_pairs={{0,4},{1,3},{2,6},{3,1},{4,0},{5,7},{6,2},{7,5},{8,12},{9,11},{10,... | collective-permute-start | bytes 3981320 | tf_op jit(solution)/shard_map/ppermute | solution.py:960
  248.2 16.6 %copy-start.1 = (f32[3,288,768]{2,1,0:T(8,128)S(1)}, f32[3,288,768]{2,1,0:T(8,128)}, u32[]{:S(2)}) copy-start(f32[3,288,768]{2,1,0:T(8,128)} %get-tuple-element.143.ka_ref.kb_ref) | copy-start | bytes 7962628
  267.1 26.0 %collective-permute-start.15 = (bf16[2,288,768]{2,1,0:T(8,128)(2,1)}, bf16[2,288,768]{2,1,0:T(8,128)(2,1)S(1)}, u32[]{:S(2)}, u32[]{:S(2)}) collective-permute-start(bf16[2,288,768]{2,1,0:T(8,128)(2,1)} %get-tuple-element.144), channel_id=1, source_target_pairs={{0,8},{1,9},{2,10},{3,11},{4,12},{5,13},{6,14},{7,15},{8,0},{9,1},... | collective-permute-start | bytes 2654216 | tf_op jit(solution)/shard_map/ppermute | solution.py:960
  283.6 9.4 %copy-start.2 = (f32[2,288,768]{2,1,0:T(8,128)S(1)}, f32[2,288,768]{2,1,0:T(8,128)}, u32[]{:S(2)}) copy-start(f32[2,288,768]{2,1,0:T(8,128)} %get-tuple-element.152.ka_ref.kb_ref) | copy-start | bytes 5308420
  291.7 30.8 %collective-permute-start.16 = (bf16[1024,768]{1,0:T(8,128)(2,1)}, bf16[1024,768]{1,0:T(8,128)(2,1)}, u32[]{:S(2)}, u32[]{:S(2)}) collective-permute-start(bf16[1024,768]{1,0:T(8,128)(2,1)} %get-tuple-element.159), channel_id=1, source_target_pairs={{1,0},{2,1},{3,2},{5,4},{6,5},{7,6},{9,8},{10,9},{11,10},{13,12},{... | collective-permute-start | bytes 4718600 | tf_op jit(solution)/shard_map/ppermute | solution.py:946
  294.8 27.7 %collective-permute-start.17 = (bf16[1,288,768]{2,1,0:T(8,128)(2,1)}, bf16[1,288,768]{2,1,0:T(8,128)(2,1)S(1)}, u32[]{:S(2)}, u32[]{:S(2)}) collective-permute-start(bf16[1,288,768]{2,1,0:T(8,128)(2,1)} %get-tuple-element.153), channel_id=1, source_target_pairs={{0,16},{1,17},{2,18},{3,19},{4,20},{5,21},{6,22},{7,23},{8,24},{9,... | collective-permute-start | bytes 1327112 | tf_op jit(solution)/shard_map/ppermute | solution.py:960
  303.8 30.1 %copy-start.13 = (bf16[1024,768]{1,0:T(8,128)(2,1)S(1)}, bf16[1024,768]{1,0:T(8,128)(2,1)}, u32[]{:S(2)}) copy-start(bf16[1024,768]{1,0:T(8,128)(2,1)} %x_ref.1) | copy-start | bytes 4718596
  322.5 11.8 %copy-start.22 = (pred[3]{0:T(512)(128)(4,1)S(1)}, pred[3]{0:T(512)(128)(4,1)}, u32[]{:S(2)}) copy-start(pred[3]{0:T(512)(128)(4,1)} %copy-done.21) | copy-start | bytes 13
  322.5 4.6 %collective-permute-start.18 = (bf16[1232,768]{1,0:T(8,128)(2,1)}, bf16[1232,768]{1,0:T(8,128)(2,1)S(1)}, u32[]{:S(2)}, u32[]{:S(2)}) collective-permute-start(bf16[1232,768]{1,0:T(8,128)(2,1)} %get-tuple-element.168), channel_id=1, source_target_pairs={{0,1},{1,0},{2,3},{3,2},{4,5},{5,4},{6,7},{7,6},{8,9},{9,8},{10,11... | collective-permute-start | bytes 5677064 | tf_op jit(solution)/shard_map/ppermute | solution.py:960
  327.1 1.5 copy-start.4
  330.4 15.5 %collective-permute-start.20 = (bf16[624,768]{1,0:T(8,128)(2,1)}, bf16[624,768]{1,0:T(8,128)(2,1)S(1)}, u32[]{:S(2)}, u32[]{:S(2)}) collective-permute-start(bf16[624,768]{1,0:T(8,128)(2,1)} %get-tuple-element.169), channel_id=1, source_target_pairs={{0,2},{1,5},{2,0},{3,7},{4,6},{5,1},{6,4},{7,3},{8,10},{9,13},{10,... | collective-permute-start | bytes 2875400 | tf_op jit(solution)/shard_map/ppermute | solution.py:960
  342.2 13.2 %copy-start.14 = (bf16[1024,768]{1,0:T(8,128)(2,1)S(1)}, bf16[1024,768]{1,0:T(8,128)(2,1)}, u32[]{:S(2)}) copy-start(bf16[1024,768]{1,0:T(8,128)(2,1)} %x_ref.1) | copy-start | bytes 4718596
  342.2 13.2 %copy-start.15 = (f32[1024,768]{1,0:T(8,128)S(1)}, f32[1024,768]{1,0:T(8,128)}, u32[]{:S(2)}) copy-start(f32[1024,768]{1,0:T(8,128)} %get-tuple-element.164) | copy-start | bytes 9437188
  343.9 14.1 %copy-start.18 = (f32[288,768]{1,0:T(8,128)}, f32[288,768]{1,0:T(8,128)S(1)}, u32[]{:S(2)}) copy-start(f32[288,768]{1,0:T(8,128)S(1)} %bitcast_select_fusion) | copy-start | bytes 2654212
  346.6 15.6 %collective-permute-start.21 = (bf16[320,768]{1,0:T(8,128)(2,1)S(1)}, bf16[320,768]{1,0:T(8,128)(2,1)S(1)}, u32[]{:S(2)}, u32[]{:S(2)}) collective-permute-start(bf16[320,768]{1,0:T(8,128)(2,1)S(1)} %get-tuple-element.175), channel_id=1, source_target_pairs={{0,4},{1,3},{2,6},{3,1},{4,0},{5,7},{6,2},{7,5},{8,12},{9,11},{10,... | collective-permute-start | bytes 1474568 | tf_op jit(solution)/shard_map/ppermute | solution.py:960
  355.4 11.3 %copy-start.20 = (f32[1024,768]{1,0:T(8,128)S(1)}, f32[1024,768]{1,0:T(8,128)}, u32[]{:S(2)}) copy-start(f32[1024,768]{1,0:T(8,128)} %get-tuple-element.116) | copy-start | bytes 9437188
  358.0 12.8 %collective-permute-start.19 = (f32[16,768]{1,0:T(8,128)S(1)}, f32[16,768]{1,0:T(8,128)S(1)}, u32[]{:S(2)}, u32[]{:S(2)}) collective-permute-start(f32[16,768]{1,0:T(8,128)S(1)} %slice.29), channel_id=1, source_target_pairs={{1,0},{2,1},{3,2},{4,3},{5,4},{6,5},{7,6},{8,7},{9,8},{10,9},{11,1... | collective-permute-start | bytes 147464 | tf_op jit(solution)/shard_map/ppermute | solution.py:940
  362.3 14.7 %collective-permute-start.22 = (bf16[320,768]{1,0:T(8,128)(2,1)S(1)}, bf16[320,768]{1,0:T(8,128)(2,1)S(1)}, u32[]{:S(2)}, u32[]{:S(2)}) collective-permute-start(bf16[320,768]{1,0:T(8,128)(2,1)S(1)} %get-tuple-element.177), channel_id=1, source_target_pairs={{0,8},{1,9},{2,10},{3,11},{4,12},{5,13},{6,14},{7,15},{8,0},{9,1},... | collective-permute-start | bytes 1474568 | tf_op jit(solution)/shard_map/ppermute | solution.py:960
  370.8 20.7 %copy-start.19 = (f32[288,768]{1,0:T(8,128)S(1)}, f32[288,768]{1,0:T(8,128)}, u32[]{:S(2)}) copy-start(f32[288,768]{1,0:T(8,128)} %copy-done.18) | copy-start | bytes 2654212
  377.1 14.2 %collective-permute-start.23 = (bf16[320,768]{1,0:T(8,128)(2,1)S(1)}, bf16[320,768]{1,0:T(8,128)(2,1)S(1)}, u32[]{:S(2)}, u32[]{:S(2)}) collective-permute-start(bf16[320,768]{1,0:T(8,128)(2,1)S(1)} %get-tuple-element.179), channel_id=1, source_target_pairs={{8,24},{9,25},{10,26},{11,27},{12,28},{13,29},{14,30},{15,31},{16,... | collective-permute-start | bytes 1474568 | tf_op jit(solution)/shard_map/ppermute | solution.py:960
  391.5 1.2 copy-start.17
  (3 other events, 2.6 us)

commit v16 on v15

--- a/solution.py
+++ b/solution.py
@@ -13,7 +13,7 @@
 AXES = ("dp", "ctx")
 QB = 256
 FORWARD_PARTS = ((0, 2), (2, 2), (4, 2))
-BACKWARD_PARTS = ((0, 1), (1, 2), (3, 1), (4, 2))
+BACKWARD_PARTS = ((0, 1), (1, 3), (4, 1), (5, 1))
 F32 = jnp.float32
 BF = jnp.bfloat16
 NT = (((1,), (1,)), ((), ()))

time: 401 us -> 396 us (0.988)
  transfers between devices with their start and end apart: 24 -> 24, of which waited for: 14 -> 15; matrix products, arithmetic and copies ran while one was open for 5% -> 5% of each run, Pallas kernels for 34% -> 35%
where the time goes in v16:
time: 396 us; the launch traced here: 392 us
  Pallas kernels  202 us (51%)
  waiting for transfers between devices  102 us (26%)
  starting transfers between devices  47.4 us (12%)
  local copies, waits for them, and re-layouts  19.3 us (5%)
  other arithmetic  17.7 us (4%)
    ppermute x20, waiting for transfers between devices, swap(): return lax.ppermute(block, AXES, route)  102 us
    pallas_call x4, Pallas kernels, att_bwd(): call_in_parts(att_bwd_kernel, [pl.BlockSpec(memory_space=pltpu.SMEM), own...  50.3 us
    pallas_call x1, Pallas kernels, ffn(): pl.pallas_call(ffn_kernel, grid=(4,), in_specs=[scalars, scalars, act, ac...  47.3 us
    pallas_call x3, Pallas kernels, att_fwd(): call_in_parts(att_fwd_kernel, [pl.BlockSpec(memory_space=pltpu.SMEM), col...  44.2 us
    ppermute x20, starting transfers between devices, swap(): return lax.ppermute(block, AXES, route)  37.8 us
    pallas_call x1, Pallas kernels, qkv_bwd(): pl.pallas_call(body, grid=(blocks,), in_specs=[pl.BlockSpec(memory_space=...  18.6 us
    pallas_call x4, Pallas kernels, merge_grid(): pl.pallas_call(body, grid_spec=pltpu.PrefetchScalarGridSpec(num_scalar_pr...  14 us
    pallas_call x1, Pallas kernels, qkv_fwd(): pl.pallas_call(body, grid=(blocks,), in_specs=[pl.BlockSpec(memory_space=...  13.3 us
  transfers between devices with their start and end apart: 24, of which 15 were waited for; matrix products, arithmetic and copies ran while one was open for 5% of the time, Pallas kernels for 35%

profile of v16, /device:TPU:0, one launch (start us, length us, event | category | flops | bytes accessed | tf_op | source)
XLA Modules:
  0.0 392.5 jit_solution(6171847538872613680)
XLA Ops:
  1.5 2.3 collective-permute-start
  4.7 1.5 fusion.8
  7.3 4.6 %collective-permute-start.3 = (bf16[1024,768]{1,0:T(8,128)(2,1)S(1)}, bf16[1024,768]{1,0:T(8,128)(2,1)S(1)}, u32[]{:S(2)}, u32[]{:S(2)}) collective-permute-start(bf16[1024,768]{1,0:T(8,128)(2,1)S(1)} %copy-done.12), channel_id=1, source_target_pairs={{0,1},{1,2},{2,3},{4,5},{5,6},{6,7},{8,9},{9,10},{10,11},{12,13},{... | collective-permute-start | bytes 4718600 | tf_op jit(solution)/shard_map/ppermute | solution.py:946
  11.9 4.4 %collective-permute-start.2 = (bf16[304,768]{1,0:T(8,128)(2,1)S(1)}, bf16[304,768]{1,0:T(8,128)(2,1)S(1)}, u32[]{:S(2)}, u32[]{:S(2)}) collective-permute-start(bf16[304,768]{1,0:T(8,128)(2,1)S(1)} %pad_maximum_fusion.1.refs_0_), channel_id=1, source_target_pairs={{0,16},{1,17},{2,18},{3,19},{4,20},{5,21},{6,22},{7,23},{8,24},{9,... | collective-permute-start | bytes 1400840 | tf_op jit(solution)/shard_map/ppermute | solution.py:960
  16.3 1.6 collective-permute-start.1
  18.1 19.6 %collective-permute-done.2.refs_2_ = bf16[304,768]{1,0:T(8,128)(2,1)S(1)} collective-permute-done((bf16[304,768]{1,0:T(8,128)(2,1)S(1)}, bf16[304,768]{1,0:T(8,128)(2,1)S(1)}, u32[]{:S(2)}, u32[]{:S(2)}) %collective-permute-start.2) | collective-permute-done | bytes 466976 | tf_op jit(solution)/shard_map/ppermute | solution.py:960
  41.6 8.4 %collective-permute-done.4.refs_3_ = bf16[304,768]{1,0:T(8,128)(2,1)S(1)} collective-permute-done((bf16[304,768]{1,0:T(8,128)(2,1)S(1)}, bf16[304,768]{1,0:T(8,128)(2,1)S(1)}, u32[]{:S(2)}, u32[]{:S(2)}) %collective-permute-start.4) | collective-permute-done | bytes 466976 | tf_op jit(solution)/shard_map/ppermute | solution.py:960
  52.8 1.9 arrange.1
  54.9 8.6 %collective-permute-done.5.got_ref = bf16[304,768]{1,0:T(8,128)(2,1)S(1)} collective-permute-done((bf16[304,768]{1,0:T(8,128)(2,1)S(1)}, bf16[304,768]{1,0:T(8,128)(2,1)S(1)}, u32[]{:S(2)}, u32[]{:S(2)}) %collective-permute-start.5) | collective-permute-done | bytes 466976 | tf_op jit(solution)/shard_map/ppermute | solution.py:960
  64.9 12.0 %collective-permute-done.6.got_ref = bf16[592,768]{1,0:T(8,128)(2,1)S(1)} collective-permute-done((bf16[592,768]{1,0:T(8,128)(2,1)S(1)}, bf16[592,768]{1,0:T(8,128)(2,1)S(1)}, u32[]{:S(2)}, u32[]{:S(2)}) %collective-permute-start.6) | collective-permute-done | bytes 909344 | tf_op jit(solution)/shard_map/ppermute | solution.py:960
  78.0 2.9 collective-permute-done.7.refs_3_
  80.9 13.3 %qkv_fwd.1 = (bf16[2048,2304]{1,0:T(8,128)(2,1)}, f32[16,768]{1,0:T(8,128)}, bf16[2304,768]{1,0:T(8,128)(2,1)}) custom-call(s32[8]{0:T(128)} %stack.217.refs_0_, bf16[2048,768]{1,0:T(8,128)(2,1)} %copy-done.16, bf16[1168,768]{1,0:T(8,128)(2,1)} %copy-done.5, bf16[1168,768]{1,0:T(8,128)(2,1)} %collective-permute-done.7.refs_3_), custom_call_target="tpu_custom_call" | custom-call | flops 7247757312 | bytes 15728640 | tf_op jit(solution)/shard_map/qkv_fwd/pallas_call | solution.py:738
  96.3 1.8 join_held.1
  99.6 14.5 %att_fwd.3 = (bf16[1024,768]{1,0:T(8,128)(2,1)}, f32[1024,768]{1,0:T(8,128)}, bf16[1024,768]{1,0:T(8,128)(2,1)}, bf16[2048,768]{1,0:T(8,128)(2,1)}, bf16[2048,768]{1,0:T(8,128)(2,1)}) custom-call(s32[1]{0:T(128)S(6)} %select_n.125.refs_0_.state_ref, bf16[2048,2304]{1,0:T(8,128)(2,1)} %get-tuple-element.98.refs_1_.refs_2_.refs_3_.refs_4_.refs_7_.refs_8_.refs_9_.refs_10_, ...), custom_call_target="tpu_custom_call" | custom-call | flops 6442450944 | bytes 7864320 | tf_op jit(solution)/shard_map/att_fwd/pallas_call | solution.py:176
  114.1 15.2 %att_fwd.4 = (bf16[1024,768]{1,0:T(8,128)(2,1)}, f32[1024,768]{1,0:T(8,128)}, bf16[1024,768]{1,0:T(8,128)(2,1)}, bf16[2048,768]{1,0:T(8,128)(2,1)}, bf16[2048,768]{1,0:T(8,128)(2,1)}) custom-call(s32[1]{0:T(128)S(6)} %select_n.125.refs_0_.state_ref, ...), custom_call_target="tpu_custom_call", output_to_operand_aliasing={{0}: (6, {}), {1}: (7, {}), {2}: (8, {}), {3}: (9, {}), {4}... | custom-call | flops 6442450944 | bytes 7864320 | tf_op jit(solution)/shard_map/att_fwd/pallas_call | solution.py:176
  131.1 14.6 %att_fwd.5 = (bf16[1024,768]{1,0:T(8,128)(2,1)}, f32[1024,768]{1,0:T(8,128)}, bf16[1024,768]{1,0:T(8,128)(2,1)}, bf16[2048,768]{1,0:T(8,128)(2,1)}, bf16[2048,768]{1,0:T(8,128)(2,1)}) custom-call(s32[1]{0:T(128)S(6)} %select_n.125.refs_0_.state_ref, ...), custom_call_target="tpu_custom_call", output_to_operand_aliasing={{0}: (6, {}), {1}: (7, {}), {2}: (8, {}), {3}: (9, {}), {4}... | custom-call | flops 6442450944 | bytes 7864320 | tf_op jit(solution)/shard_map/att_fwd/pallas_call | solution.py:176
  145.7 1.5 copy-done.24
  147.2 47.3 %ffn.1 = (bf16[1024,768]{1,0:T(8,128)(2,1)}, f32[1024,768]{1,0:T(8,128)}, bf16[1024,768]{1,0:T(8,128)(2,1)}, f32[1,768]{1,0:T(1,128)}, bf16[36,4,24,768]{3,2,1,0...) custom-call(s32[1]{0:T(128)S(6)} %select_n.125.refs_0_.state_ref, s32[25]{0:T(128)} %stack.211.index_ref, ...), custom_call_target="tpu_custom_call" | custom-call | flops 32614907904 | bytes 40894464 | tf_op jit(solution)/shard_map/ffn/pallas_call | solution.py:903
  195.2 9.3 %att_bwd.4 = (bf16[1024,768]{1,0:T(8,128)(2,1)}, bf16[8,768]{1,0:T(8,128)(2,1)}, bf16[2048,768]{1,0:T(8,128)(2,1)}, bf16[2048,768]{1,0:T(8,128)(2,1)}, f32[16,768]{1,0:T(8,128)}) custom-call(s32[1]{0:T(128)S(6)} %select_n.125.refs_0_.state_ref, bf16[1024,768]{1,0:T(8,128)(2,1)} %get-tuple-element.117.refs_1_, bf16[2048,768]{1,0:T(8,128)(2,1)} %get-tuple-element.118.refs_2_, ...), custom_call_target="tpu_custom_call" | custom-call | flops 8053063680 | bytes 5505024 | tf_op jit(solution)/shard_map/att_bwd/pallas_call | solution.py:333
  204.5 7.2 %merge_grid.4 = (bf16[6,288,768]{2,1,0:T(8,128)(2,1)}, bf16[6,288,768]{2,1,0:T(8,128)(2,1)}) custom-call(s32[12]{0:T(128)S(1)} %stack.243.index_ref, bf16[12,288,768]{2,1,0:T(8,128)(2,1)S(1)} %bitcast.71, bf16[12,288,768]{2,1,0:T(8,128)(2,1)} %collective-permute-done.12.ga_ref.gb_ref, bf16[12,288,768]{2,1,0:T(8,128)(2,1)S(1)} %bitcast.72, ...), custom_call_target="tpu_custom_call" | custom-call | flops 2654208 | bytes 21233664 | tf_op jit(solution)/shard_map/merge_grid/pallas_call | solution.py:569
  211.8 22.2 %att_bwd.5 = (bf16[1024,768]{1,0:T(8,128)(2,1)}, bf16[8,768]{1,0:T(8,128)(2,1)}, bf16[2048,768]{1,0:T(8,128)(2,1)}, bf16[2048,768]{1,0:T(8,128)(2,1)}, f32[16,768]{1,0:T(8,128)}) custom-call(s32[1]{0:T(128)S(6)} %select_n.125.refs_0_.state_ref, ...), custom_call_target="tpu_custom_call", output_to_operand_aliasing={{0}: (12, {}), {1}: (13, {}), {2}: (14, {}), {3}: (15, {}),... | custom-call | flops 24159191040 | bytes 16515072 | tf_op jit(solution)/shard_map/att_bwd/pallas_call | solution.py:333
  234.0 9.9 %collective-permute-done.13.ga_ref.gb_ref = bf16[6,288,768]{2,1,0:T(8,128)(2,1)S(1)} collective-permute-done((bf16[6,288,768]{2,1,0:T(8,128)(2,1)}, bf16[6,288,768]{2,1,0:T(8,128)(2,1)S(1)}, u32[]{:S(2)}, u32[]{:S(2)}) %collective-permute-start.13) | collective-permute-done | bytes 2654240 | tf_op jit(solution)/shard_map/ppermute | solution.py:960
  243.9 3.0 merge_grid.5
  248.2 9.5 %att_bwd.6 = (bf16[1024,768]{1,0:T(8,128)(2,1)}, bf16[8,768]{1,0:T(8,128)(2,1)}, bf16[2048,768]{1,0:T(8,128)(2,1)}, bf16[2048,768]{1,0:T(8,128)(2,1)}, f32[16,768]{1,0:T(8,128)}) custom-call(s32[1]{0:T(128)S(6)} %select_n.125.refs_0_.state_ref, ...), custom_call_target="tpu_custom_call", output_to_operand_aliasing={{0}: (12, {}), {1}: (13, {}), {2}: (14, {}), {3}: (15, {}),... | custom-call | flops 8053063680 | bytes 5505024 | tf_op jit(solution)/shard_map/att_bwd/pallas_call | solution.py:333
  257.8 7.1 %collective-permute-done.14.ga_ref.gb_ref = bf16[3,288,768]{2,1,0:T(8,128)(2,1)S(1)} collective-permute-done((bf16[3,288,768]{2,1,0:T(8,128)(2,1)}, bf16[3,288,768]{2,1,0:T(8,128)(2,1)S(1)}, u32[]{:S(2)}, u32[]{:S(2)}) %collective-permute-start.14) | collective-permute-done | bytes 1327136 | tf_op jit(solution)/shard_map/ppermute | solution.py:960
  264.9 2.2 merge_grid.6
  267.1 4.4 %collective-permute-start.15 = (bf16[2,288,768]{2,1,0:T(8,128)(2,1)}, bf16[2,288,768]{2,1,0:T(8,128)(2,1)S(1)}, u32[]{:S(2)}, u32[]{:S(2)}) collective-permute-start(bf16[2,288,768]{2,1,0:T(8,128)(2,1)} %get-tuple-element.144), channel_id=1, source_target_pairs={{0,8},{1,9},{2,10},{3,11},{4,12},{5,13},{6,14},{7,15},{8,0},{9,1},... | collective-permute-start | bytes 2654216 | tf_op jit(solution)/shard_map/ppermute | solution.py:960
  271.4 9.2 %att_bwd.7 = (bf16[1024,768]{1,0:T(8,128)(2,1)}, bf16[8,768]{1,0:T(8,128)(2,1)}, bf16[2048,768]{1,0:T(8,128)(2,1)}, bf16[2048,768]{1,0:T(8,128)(2,1)}, f32[16,768]{1,0:T(8,128)}) custom-call(s32[1]{0:T(128)S(6)} %select_n.125.refs_0_.state_ref, ...), custom_call_target="tpu_custom_call", output_to_operand_aliasing={{0}: (12, {}), {1}: (13, {}), {2}: (14, {}), {3}: (15, {}),... | custom-call | flops 8053063680 | bytes 5505024 | tf_op jit(solution)/shard_map/att_bwd/pallas_call | solution.py:333
  280.7 8.0 %before_bwd.1 = (bf16[1024,768]{1,0:T(8,128)(2,1)}, f32[1,768]{1,0:T(1,128)}) custom-call(bf16[2048,768]{1,0:T(8,128)(2,1)} %copy-done.16, bf16[8,768]{1,0:T(8,128)(2,1)} %get-tuple-element.155.dt_ref.refs_3_, bf16[2048,768]{1,0:T(8,128)(2,1)} %get-tuple-element.156.dk_ref.refs_4_, bf16[2048,768]{1,0:T(8,128)(2,1)} %get-tuple-element.157.dv_ref.refs_5_, ...), custom_call_target="tpu_custom_call" | custom-call | flops 2415919104 | bytes 9437184 | tf_op jit(solution)/shard_map/before_bwd/pallas_call | solution.py:412
  290.1 1.6 collective-permute-done.15.ga_ref.gb_ref
  291.7 1.7 merge_grid.7
  293.4 3.9 %collective-permute-start.17 = (bf16[1,288,768]{2,1,0:T(8,128)(2,1)}, bf16[1,288,768]{2,1,0:T(8,128)(2,1)S(1)}, u32[]{:S(2)}, u32[]{:S(2)}) collective-permute-start(bf16[1,288,768]{2,1,0:T(8,128)(2,1)} %get-tuple-element.153), channel_id=1, source_target_pairs={{0,16},{1,17},{2,18},{3,19},{4,20},{5,21},{6,22},{7,23},{8,24},{9,... | collective-permute-start | bytes 1327112 | tf_op jit(solution)/shard_map/ppermute | solution.py:960
  297.4 18.6 %qkv_bwd.1 = (bf16[1232,768]{1,0:T(8,128)(2,1)}, bf16[1232,768]{1,0:T(8,128)(2,1)}, f32[1024,768]{1,0:T(8,128)}) custom-call(s32[1]{0:T(128)} %bitcast.24.refs_0_.index_ref, bf16[2048,768]{1,0:T(8,128)(2,1)} %copy-done.16, bf16[1024,768]{1,0:T(8,128)(2,1)} %get-tuple-element.161.refs_2_, bf16[8,768]{1,0:T(8,128)(2,1)} %get-tuple-element.155.dt_ref.refs_3_, ...), custom_call_target="tpu_custom_call" | custom-call | flops 9663676416 | bytes 23592960 | tf_op jit(solution)/shard_map/qkv_bwd/pallas_call | solution.py:507
  316.0 1.7 collective-permute-start.18
  317.8 3.6 collective-permute-done.18.got_ref
  322.9 1.8 merge.4
  324.8 14.5 %collective-permute-start.20 = (bf16[624,768]{1,0:T(8,128)(2,1)}, bf16[624,768]{1,0:T(8,128)(2,1)S(1)}, u32[]{:S(2)}, u32[]{:S(2)}) collective-permute-start(bf16[624,768]{1,0:T(8,128)(2,1)} %get-tuple-element.169), channel_id=1, source_target_pairs={{0,2},{1,5},{2,0},{3,7},{4,6},{5,1},{6,4},{7,3},{8,10},{9,13},{10,... | collective-permute-start | bytes 2875400 | tf_op jit(solution)/shard_map/ppermute | solution.py:960
  340.6 2.2 convert_add_fusion.1
  342.8 2.4 copy.44
  345.2 2.4 reshape.115
  347.6 1.7 bitcast_select_fusion
  349.4 2.0 collective-permute-done.20.got_ref
  352.2 2.6 fusion.2
  356.1 4.8 %collective-permute-done.21.got_ref = bf16[320,768]{1,0:T(8,128)(2,1)S(1)} collective-permute-done((bf16[320,768]{1,0:T(8,128)(2,1)S(1)}, bf16[320,768]{1,0:T(8,128)(2,1)S(1)}, u32[]{:S(2)}, u32[]{:S(2)}) %collective-permute-start.21) | collective-permute-done | bytes 491552 | tf_op jit(solution)/shard_map/ppermute | solution.py:960
  361.4 4.1 %fusion.5 = f32[1024,768]{1,0:T(8,128)} fusion(f32[1024,768]{1,0:T(8,128)S(1)} %copy-done.20, bf16[1024,768]{1,0:T(8,128)(2,1)S(1)} %copy-done.14, f32[1024,768]{1,0:T(8,128)S(1)} %copy-done.15, bf16[1024,768]{1,0:T(8,128)(2,1)} %collective-permute-done.16, f32[1024]{0:T(1024)S(1)} %broadcast_multiply_fusion, f32[768]{0:T(1024)S(1)} %slice_reduce_fusion, ...), kind=kLoop, calls=%fused_computation.7 | loop fusion | flops 7077888 | bytes 12594176 | tf_op jit(solution)/shard_map/add | solution.py:1197
  365.5 7.7 %collective-permute-done.22.got_ref = bf16[320,768]{1,0:T(8,128)(2,1)S(1)} collective-permute-done((bf16[320,768]{1,0:T(8,128)(2,1)S(1)}, bf16[320,768]{1,0:T(8,128)(2,1)S(1)}, u32[]{:S(2)}, u32[]{:S(2)}) %collective-permute-start.22) | collective-permute-done | bytes 491552 | tf_op jit(solution)/shard_map/ppermute | solution.py:960
  375.3 11.9 %collective-permute-done.23 = bf16[320,768]{1,0:T(8,128)(2,1)S(1)} collective-permute-done((bf16[320,768]{1,0:T(8,128)(2,1)S(1)}, bf16[320,768]{1,0:T(8,128)(2,1)S(1)}, u32[]{:S(2)}, u32[]{:S(2)}) %collective-permute-start.23) | collective-permute-done | bytes 491552 | tf_op jit(solution)/shard_map/ppermute | solution.py:960
  388.5 3.5 fusion.16
  (119 shorter events, 28.0 us)
Async XLA Ops:
  1.5 3.3 collective-permute-start
  4.7 2.6 copy-start.21
  4.7 2.6 copy-start.12
  7.3 10.6 %collective-permute-start.3 = (bf16[1024,768]{1,0:T(8,128)(2,1)S(1)}, bf16[1024,768]{1,0:T(8,128)(2,1)S(1)}, u32[]{:S(2)}, u32[]{:S(2)}) collective-permute-start(bf16[1024,768]{1,0:T(8,128)(2,1)S(1)} %copy-done.12), channel_id=1, source_target_pairs={{0,1},{1,2},{2,3},{4,5},{5,6},{6,7},{8,9},{9,10},{10,11},{12,13},{... | collective-permute-start | bytes 4718600 | tf_op jit(solution)/shard_map/ppermute | solution.py:946
  11.9 25.7 %collective-permute-start.2 = (bf16[304,768]{1,0:T(8,128)(2,1)S(1)}, bf16[304,768]{1,0:T(8,128)(2,1)S(1)}, u32[]{:S(2)}, u32[]{:S(2)}) collective-permute-start(bf16[304,768]{1,0:T(8,128)(2,1)S(1)} %pad_maximum_fusion.1.refs_0_), channel_id=1, source_target_pairs={{0,16},{1,17},{2,18},{3,19},{4,20},{5,21},{6,22},{7,23},{8,24},{9,... | collective-permute-start | bytes 1400840 | tf_op jit(solution)/shard_map/ppermute | solution.py:960
  16.3 24.5 %collective-permute-start.1 = (bf16[304,768]{1,0:T(8,128)(2,1)S(1)}, bf16[304,768]{1,0:T(8,128)(2,1)S(1)}, u32[]{:S(2)}, u32[]{:S(2)}) collective-permute-start(bf16[304,768]{1,0:T(8,128)(2,1)S(1)} %pad_maximum_fusion.1.refs_0_), channel_id=1, source_target_pairs={{0,8},{1,9},{2,10},{3,11},{4,12},{5,13},{6,14},{7,15},{8,0},{9,1},... | collective-permute-start | bytes 1400840 | tf_op jit(solution)/shard_map/ppermute | solution.py:960
  18.1 19.6 %copy-start.16 = (bf16[2048,768]{1,0:T(8,128)(2,1)}, bf16[2048,768]{1,0:T(8,128)(2,1)S(1)}, u32[]{:S(2)}) copy-start(bf16[2048,768]{1,0:T(8,128)(2,1)S(1)} %constant_dynamic-update-slice_fusion.refs_1_.x_ref) | copy-start | bytes 9437188
  37.7 12.3 %collective-permute-start.4 = (bf16[304,768]{1,0:T(8,128)(2,1)S(1)}, bf16[304,768]{1,0:T(8,128)(2,1)S(1)}, u32[]{:S(2)}, u32[]{:S(2)}) collective-permute-start(bf16[304,768]{1,0:T(8,128)(2,1)S(1)} %collective-permute-done.2.refs_2_), channel_id=1, source_target_pairs={{0,8},{1,9},{2,10},{3,11},{4,12},{5,13},{6,14},{7,15},{8,0},{9,1},... | collective-permute-start | bytes 1400840 | tf_op jit(solution)/shard_map/ppermute | solution.py:960
  50.8 1.0 copy-start.9
  54.8 39.4 %copy-start.6 = (bf16[864,768]{1,0:T(8,128)(2,1)}, bf16[864,768]{1,0:T(8,128)(2,1)S(1)}, u32[]{:S(2)}) copy-start(bf16[864,768]{1,0:T(8,128)(2,1)S(1)} %get-tuple-element.99.own_ref) | copy-start | bytes 3981316
  54.8 8.6 %collective-permute-start.5 = (bf16[304,768]{1,0:T(8,128)(2,1)S(1)}, bf16[304,768]{1,0:T(8,128)(2,1)S(1)}, u32[]{:S(2)}, u32[]{:S(2)}) collective-permute-start(bf16[304,768]{1,0:T(8,128)(2,1)S(1)} %get-tuple-element.97.own_ref), channel_id=1, source_target_pairs={{0,2},{1,5},{2,0},{3,7},{4,6},{5,1},{6,4},{7,3},{8,10},{9,13},{10,... | collective-permute-start | bytes 1400840 | tf_op jit(solution)/shard_map/ppermute | solution.py:960
  63.5 13.4 %collective-permute-start.6 = (bf16[592,768]{1,0:T(8,128)(2,1)S(1)}, bf16[592,768]{1,0:T(8,128)(2,1)S(1)}, u32[]{:S(2)}, u32[]{:S(2)}) collective-permute-start(bf16[592,768]{1,0:T(8,128)(2,1)S(1)} %join.2.own_ref), channel_id=1, source_target_pairs={{0,4},{1,3},{2,6},{3,1},{4,0},{5,7},{6,2},{7,5},{8,12},{9,11},{10,... | collective-permute-start | bytes 2727944 | tf_op jit(solution)/shard_map/ppermute | solution.py:960
  77.0 3.9 %copy-start.5 = (bf16[1168,768]{1,0:T(8,128)(2,1)}, bf16[1168,768]{1,0:T(8,128)(2,1)S(1)}, u32[]{:S(2)}) copy-start(bf16[1168,768]{1,0:T(8,128)(2,1)S(1)} %join.3.refs_2_) | copy-start | bytes 5382148
  77.0 3.9 collective-permute-start.7
  77.1 18.0 %collective-permute-start.8 = (bf16[864,768]{1,0:T(8,128)(2,1)S(1)}, bf16[864,768]{1,0:T(8,128)(2,1)}, u32[]{:S(2)}, u32[]{:S(2)}) collective-permute-start(bf16[864,768]{1,0:T(8,128)(2,1)S(1)} %get-tuple-element.99.own_ref), channel_id=1, source_target_pairs={{0,2},{1,5},{2,0},{3,7},{4,6},{5,1},{6,4},{7,3},{8,10},{9,13},{10,... | collective-permute-start | bytes 3981320 | tf_op jit(solution)/shard_map/ppermute | solution.py:960
  95.0 1.3 copy-start.7
  98.1 16.0 %copy-start.3 = (bf16[1728,768]{1,0:T(8,128)(2,1)}, bf16[1728,768]{1,0:T(8,128)(2,1)S(1)}, u32[]{:S(2)}) copy-start(bf16[1728,768]{1,0:T(8,128)(2,1)S(1)} %join_held.1) | copy-start | bytes 7962628
  98.1 16.0 %collective-permute-start.10 = (bf16[1728,768]{1,0:T(8,128)(2,1)S(1)}, bf16[1728,768]{1,0:T(8,128)(2,1)S(1)}, u32[]{:S(2)}, u32[]{:S(2)}) collective-permute-start(bf16[1728,768]{1,0:T(8,128)(2,1)S(1)} %join_held.1), channel_id=1, source_target_pairs={{0,1},{1,0},{2,3},{3,2},{4,5},{5,4},{6,7},{7,6},{8,9},{9,8},{10,11... | collective-permute-start | bytes 7962632 | tf_op jit(solution)/shard_map/ppermute | solution.py:960
  98.2 32.2 %collective-permute-start.9 = (bf16[1728,768]{1,0:T(8,128)(2,1)S(1)}, bf16[1728,768]{1,0:T(8,128)(2,1)}, u32[]{:S(2)}, u32[]{:S(2)}) collective-permute-start(bf16[1728,768]{1,0:T(8,128)(2,1)S(1)} %join_held.1), channel_id=1, source_target_pairs={{0,4},{1,3},{2,6},{3,1},{4,0},{5,7},{6,2},{7,5},{8,12},{9,11},{10,... | collective-permute-start | bytes 7962632 | tf_op jit(solution)/shard_map/ppermute | solution.py:960
  114.1 15.2 %copy-start.23 = (bf16[1728,768]{1,0:T(8,128)(2,1)}, bf16[1728,768]{1,0:T(8,128)(2,1)S(1)}, u32[]{:S(2)}) copy-start(bf16[1728,768]{1,0:T(8,128)(2,1)S(1)} %collective-permute-done.10) | copy-start | bytes 7962628
  130.4 15.3 %collective-permute-start.11 = (bf16[1728,768]{1,0:T(8,128)(2,1)}, bf16[1728,768]{1,0:T(8,128)(2,1)S(1)}, u32[]{:S(2)}, u32[]{:S(2)}) collective-permute-start(bf16[1728,768]{1,0:T(8,128)(2,1)} %hold.1), channel_id=1, source_target_pairs={{0,1},{1,0},{2,3},{3,2},{4,5},{5,4},{6,7},{7,6},{8,9},{9,8},{10,11... | collective-permute-start | bytes 7962632 | tf_op jit(solution)/shard_map/ppermute | solution.py:960
  145.6 1.5 copy-start.24
  194.5 10.0 %collective-permute-start.12 = (bf16[12,288,768]{2,1,0:T(8,128)(2,1)}, bf16[12,288,768]{2,1,0:T(8,128)(2,1)}, u32[]{:S(2)}, u32[]{:S(2)}) collective-permute-start(bf16[12,288,768]{2,1,0:T(8,128)(2,1)} %bitcast.75), channel_id=1, source_target_pairs={{0,1},{1,0},{2,3},{3,2},{4,5},{5,4},{6,7},{7,6},{8,9},{9,8},{10,11... | collective-permute-start | bytes 15925256 | tf_op jit(solution)/shard_map/ppermute | solution.py:960
  195.2 9.4 %slice-start = ((s8[5308416]{0:T(1024)(128)(4,1)}), s8[4194304]{0:T(1024)(128)(4,1)S(1)}, s32[]{:S(2)}) async-start(s8[5308416]{0:T(1024)(128)(4,1)} %bitcast.69), calls=%async_computation | async-start | bytes 8388608
  195.2 9.4 %slice-start.1 = ((s8[5308416]{0:T(1024)(128)(4,1)}), s8[1114112]{0:T(1024)(128)(4,1)S(1)}, s32[]{:S(2)}) async-start(s8[5308416]{0:T(1024)(128)(4,1)} %bitcast.69), calls=%async_computation.1 | async-start | bytes 2228224
  211.7 32.2 %collective-permute-start.13 = (bf16[6,288,768]{2,1,0:T(8,128)(2,1)}, bf16[6,288,768]{2,1,0:T(8,128)(2,1)S(1)}, u32[]{:S(2)}, u32[]{:S(2)}) collective-permute-start(bf16[6,288,768]{2,1,0:T(8,128)(2,1)} %get-tuple-element.126), channel_id=1, source_target_pairs={{0,2},{1,5},{2,0},{3,7},{4,6},{5,1},{6,4},{7,3},{8,10},{9,13},{10,... | collective-permute-start | bytes 7962632 | tf_op jit(solution)/shard_map/ppermute | solution.py:960
  211.8 32.1 %copy-start = (bf16[6,288,768]{2,1,0:T(8,128)(2,1)S(1)}, bf16[6,288,768]{2,1,0:T(8,128)(2,1)}, u32[]{:S(2)}) copy-start(bf16[6,288,768]{2,1,0:T(8,128)(2,1)} %get-tuple-element.134.ka_ref.kb_ref) | copy-start | bytes 7962628
  246.9 18.0 %collective-permute-start.14 = (bf16[3,288,768]{2,1,0:T(8,128)(2,1)}, bf16[3,288,768]{2,1,0:T(8,128)(2,1)S(1)}, u32[]{:S(2)}, u32[]{:S(2)}) collective-permute-start(bf16[3,288,768]{2,1,0:T(8,128)(2,1)} %get-tuple-element.135), channel_id=1, source_target_pairs={{0,4},{1,3},{2,6},{3,1},{4,0},{5,7},{6,2},{7,5},{8,12},{9,11},{10,... | collective-permute-start | bytes 3981320 | tf_op jit(solution)/shard_map/ppermute | solution.py:960
  248.2 16.6 %copy-start.1 = (f32[3,288,768]{2,1,0:T(8,128)S(1)}, f32[3,288,768]{2,1,0:T(8,128)}, u32[]{:S(2)}) copy-start(f32[3,288,768]{2,1,0:T(8,128)} %get-tuple-element.143.ka_ref.kb_ref) | copy-start | bytes 7962628
  267.1 24.6 %collective-permute-start.15 = (bf16[2,288,768]{2,1,0:T(8,128)(2,1)}, bf16[2,288,768]{2,1,0:T(8,128)(2,1)S(1)}, u32[]{:S(2)}, u32[]{:S(2)}) collective-permute-start(bf16[2,288,768]{2,1,0:T(8,128)(2,1)} %get-tuple-element.144), channel_id=1, source_target_pairs={{0,8},{1,9},{2,10},{3,11},{4,12},{5,13},{6,14},{7,15},{8,0},{9,1},... | collective-permute-start | bytes 2654216 | tf_op jit(solution)/shard_map/ppermute | solution.py:960
  280.7 11.0 %copy-start.2 = (f32[2,288,768]{2,1,0:T(8,128)S(1)}, f32[2,288,768]{2,1,0:T(8,128)}, u32[]{:S(2)}) copy-start(f32[2,288,768]{2,1,0:T(8,128)} %get-tuple-element.152.ka_ref.kb_ref) | copy-start | bytes 5308420
  288.7 27.3 %collective-permute-start.16 = (bf16[1024,768]{1,0:T(8,128)(2,1)}, bf16[1024,768]{1,0:T(8,128)(2,1)}, u32[]{:S(2)}, u32[]{:S(2)}) collective-permute-start(bf16[1024,768]{1,0:T(8,128)(2,1)} %get-tuple-element.159), channel_id=1, source_target_pairs={{1,0},{2,1},{3,2},{5,4},{6,5},{7,6},{9,8},{10,9},{11,10},{13,12},{... | collective-permute-start | bytes 4718600 | tf_op jit(solution)/shard_map/ppermute | solution.py:946
  293.4 22.6 %collective-permute-start.17 = (bf16[1,288,768]{2,1,0:T(8,128)(2,1)}, bf16[1,288,768]{2,1,0:T(8,128)(2,1)S(1)}, u32[]{:S(2)}, u32[]{:S(2)}) collective-permute-start(bf16[1,288,768]{2,1,0:T(8,128)(2,1)} %get-tuple-element.153), channel_id=1, source_target_pairs={{0,16},{1,17},{2,18},{3,19},{4,20},{5,21},{6,22},{7,23},{8,24},{9,... | collective-permute-start | bytes 1327112 | tf_op jit(solution)/shard_map/ppermute | solution.py:960
  297.4 41.9 %copy-start.13 = (bf16[1024,768]{1,0:T(8,128)(2,1)S(1)}, bf16[1024,768]{1,0:T(8,128)(2,1)}, u32[]{:S(2)}) copy-start(bf16[1024,768]{1,0:T(8,128)(2,1)} %x_ref.1) | copy-start | bytes 4718596
  316.0 23.7 %copy-start.22 = (pred[3]{0:T(512)(128)(4,1)S(1)}, pred[3]{0:T(512)(128)(4,1)}, u32[]{:S(2)}) copy-start(pred[3]{0:T(512)(128)(4,1)} %copy-done.21) | copy-start | bytes 13
  316.0 5.4 %collective-permute-start.18 = (bf16[1232,768]{1,0:T(8,128)(2,1)}, bf16[1232,768]{1,0:T(8,128)(2,1)S(1)}, u32[]{:S(2)}, u32[]{:S(2)}) collective-permute-start(bf16[1232,768]{1,0:T(8,128)(2,1)} %get-tuple-element.168), channel_id=1, source_target_pairs={{0,1},{1,0},{2,3},{3,2},{4,5},{5,4},{6,7},{7,6},{8,9},{9,8},{10,11... | collective-permute-start | bytes 5677064 | tf_op jit(solution)/shard_map/ppermute | solution.py:960
  321.4 1.5 copy-start.4
  324.8 26.6 %collective-permute-start.20 = (bf16[624,768]{1,0:T(8,128)(2,1)}, bf16[624,768]{1,0:T(8,128)(2,1)S(1)}, u32[]{:S(2)}, u32[]{:S(2)}) collective-permute-start(bf16[624,768]{1,0:T(8,128)(2,1)} %get-tuple-element.169), channel_id=1, source_target_pairs={{0,2},{1,5},{2,0},{3,7},{4,6},{5,1},{6,4},{7,3},{8,10},{9,13},{10,... | collective-permute-start | bytes 2875400 | tf_op jit(solution)/shard_map/ppermute | solution.py:960
  347.6 4.5 %copy-start.14 = (bf16[1024,768]{1,0:T(8,128)(2,1)S(1)}, bf16[1024,768]{1,0:T(8,128)(2,1)}, u32[]{:S(2)}) copy-start(bf16[1024,768]{1,0:T(8,128)(2,1)} %x_ref.1) | copy-start | bytes 4718596
  347.6 4.5 %copy-start.15 = (f32[1024,768]{1,0:T(8,128)S(1)}, f32[1024,768]{1,0:T(8,128)}, u32[]{:S(2)}) copy-start(f32[1024,768]{1,0:T(8,128)} %get-tuple-element.164) | copy-start | bytes 9437188
  349.3 5.4 %copy-start.18 = (f32[288,768]{1,0:T(8,128)}, f32[288,768]{1,0:T(8,128)S(1)}, u32[]{:S(2)}) copy-start(f32[288,768]{1,0:T(8,128)S(1)} %bitcast_select_fusion) | copy-start | bytes 2654212
  352.0 8.9 %collective-permute-start.21 = (bf16[320,768]{1,0:T(8,128)(2,1)S(1)}, bf16[320,768]{1,0:T(8,128)(2,1)S(1)}, u32[]{:S(2)}, u32[]{:S(2)}) collective-permute-start(bf16[320,768]{1,0:T(8,128)(2,1)S(1)} %get-tuple-element.175), channel_id=1, source_target_pairs={{0,4},{1,3},{2,6},{3,1},{4,0},{5,7},{6,2},{7,5},{8,12},{9,11},{10,... | collective-permute-start | bytes 1474568 | tf_op jit(solution)/shard_map/ppermute | solution.py:960
  352.1 9.3 %copy-start.20 = (f32[1024,768]{1,0:T(8,128)S(1)}, f32[1024,768]{1,0:T(8,128)}, u32[]{:S(2)}) copy-start(f32[1024,768]{1,0:T(8,128)} %get-tuple-element.116) | copy-start | bytes 9437188
  354.8 10.7 %collective-permute-start.19 = (f32[16,768]{1,0:T(8,128)S(1)}, f32[16,768]{1,0:T(8,128)S(1)}, u32[]{:S(2)}, u32[]{:S(2)}) collective-permute-start(f32[16,768]{1,0:T(8,128)S(1)} %slice.29), channel_id=1, source_target_pairs={{1,0},{2,1},{3,2},{4,3},{5,4},{6,5},{7,6},{8,7},{9,8},{10,9},{11,1... | collective-permute-start | bytes 147464 | tf_op jit(solution)/shard_map/ppermute | solution.py:940
  361.0 12.1 %collective-permute-start.22 = (bf16[320,768]{1,0:T(8,128)(2,1)S(1)}, bf16[320,768]{1,0:T(8,128)(2,1)S(1)}, u32[]{:S(2)}, u32[]{:S(2)}) collective-permute-start(bf16[320,768]{1,0:T(8,128)(2,1)S(1)} %get-tuple-element.177), channel_id=1, source_target_pairs={{0,8},{1,9},{2,10},{3,11},{4,12},{5,13},{6,14},{7,15},{8,0},{9,1},... | collective-permute-start | bytes 1474568 | tf_op jit(solution)/shard_map/ppermute | solution.py:960
  365.5 21.8 %copy-start.19 = (f32[288,768]{1,0:T(8,128)S(1)}, f32[288,768]{1,0:T(8,128)}, u32[]{:S(2)}) copy-start(f32[288,768]{1,0:T(8,128)} %copy-done.18) | copy-start | bytes 2654212
  373.3 13.9 %collective-permute-start.23 = (bf16[320,768]{1,0:T(8,128)(2,1)S(1)}, bf16[320,768]{1,0:T(8,128)(2,1)S(1)}, u32[]{:S(2)}, u32[]{:S(2)}) collective-permute-start(bf16[320,768]{1,0:T(8,128)(2,1)S(1)} %get-tuple-element.179), channel_id=1, source_target_pairs={{8,24},{9,25},{10,26},{11,27},{12,28},{13,29},{14,30},{15,31},{16,... | collective-permute-start | bytes 1474568 | tf_op jit(solution)/shard_map/ppermute | solution.py:960
  387.3 1.2 copy-start.17
  (3 other events, 2.6 us)

commit v17 on v16

--- a/solution.py
+++ b/solution.py
@@ -12,7 +12,7 @@
 SEQ_MIN = 1024
 AXES = ("dp", "ctx")
 QB = 256
-FORWARD_PARTS = ((0, 2), (2, 2), (4, 2))
+FORWARD_PARTS = ((0, 5), (5, 1))
 BACKWARD_PARTS = ((0, 1), (1, 3), (4, 1), (5, 1))
 F32 = jnp.float32
 BF = jnp.bfloat16
@@ -1115,10 +1115,9 @@
         line = swap(rest, 4, 2)
         core_rest = swap(rest, 1, 1)
         forward = att_fwd(after(state_vec, rest), projected, small, forward, FORWARD_PARTS[0], rows)
-        forward = att_fwd(after(state_vec, core_rest), projected, small, forward, FORWARD_PARTS[1], rows)
         line = hold(line, forward[0])
         core_line = swap(line, 1, 1)
-        forward = att_fwd(after(state_vec, line), projected, small, forward, FORWARD_PARTS[2], rows)
+        forward = att_fwd(after(state_vec, line, core_rest), projected, small, forward, FORWARD_PARTS[1], rows)
         late_weights = [w.reshape(18, 4, 24, D) for w in (rest, line, core_rest, core_line)]
     else:
         for part in FORWARD_PARTS:

time: 396 us -> 390 us (0.985)
  waiting for transfers between devices: 102 us -> 96.7 us
    ppermute x20, waiting for transfers between devices: 102 us -> 96.7 us  [swap(): return lax.ppermute(block, AXES, route)]
    pallas_call x3 -> x2, Pallas kernels: 44.2 us -> 40.9 us  [att_fwd(): call_in_parts(att_fwd_kernel, [pl.BlockSpec(memory_space=pltpu.SMEM), col...]
    unnamed x55 -> x51, local copies, waits for them, and re-layouts: 9.04 us -> 7.5 us
  transfers between devices with their start and end apart: 24 -> 24, of which waited for: 15 -> 13; matrix products, arithmetic and copies ran while one was open for 5% -> 5% of each run, Pallas kernels for 35% -> 35%
where the time goes in v17:
time: 390 us; the launch traced here: 383 us
  Pallas kernels  199 us (51%)
  waiting for transfers between devices  96.7 us (25%)
  starting transfers between devices  48.3 us (12%)
  local copies, waits for them, and re-layouts  17.7 us (5%)
  other arithmetic  17.7 us (5%)
    ppermute x20, waiting for transfers between devices, swap(): return lax.ppermute(block, AXES, route)  96.7 us
    pallas_call x4, Pallas kernels, att_bwd(): call_in_parts(att_bwd_kernel, [pl.BlockSpec(memory_space=pltpu.SMEM), own...  50.4 us
    pallas_call x1, Pallas kernels, ffn(): pl.pallas_call(ffn_kernel, grid=(4,), in_specs=[scalars, scalars, act, ac...  47.3 us
    pallas_call x2, Pallas kernels, att_fwd(): call_in_parts(att_fwd_kernel, [pl.BlockSpec(memory_space=pltpu.SMEM), col...  40.9 us
    ppermute x20, starting transfers between devices, swap(): return lax.ppermute(block, AXES, route)  38.8 us
    pallas_call x1, Pallas kernels, qkv_bwd(): pl.pallas_call(body, grid=(blocks,), in_specs=[pl.BlockSpec(memory_space=...  18.6 us
    pallas_call x4, Pallas kernels, merge_grid(): pl.pallas_call(body, grid_spec=pltpu.PrefetchScalarGridSpec(num_scalar_pr...  14.1 us
    pallas_call x1, Pallas kernels, qkv_fwd(): pl.pallas_call(body, grid=(blocks,), in_specs=[pl.BlockSpec(memory_space=...  13.3 us
  transfers between devices with their start and end apart: 24, of which 13 were waited for; matrix products, arithmetic and copies ran while one was open for 5% of the time, Pallas kernels for 35%

profile of v17, /device:TPU:0, one launch (start us, length us, event | category | flops | bytes accessed | tf_op | source)
XLA Modules:
  0.0 383.4 jit_solution(1227095924265881008)
XLA Ops:
  1.5 2.3 collective-permute-start
  4.7 1.5 fusion.8
  7.3 4.6 %collective-permute-start.3 = (bf16[1024,768]{1,0:T(8,128)(2,1)S(1)}, bf16[1024,768]{1,0:T(8,128)(2,1)S(1)}, u32[]{:S(2)}, u32[]{:S(2)}) collective-permute-start(bf16[1024,768]{1,0:T(8,128)(2,1)S(1)} %copy-done.12), channel_id=1, source_target_pairs={{0,1},{1,2},{2,3},{4,5},{5,6},{6,7},{8,9},{9,10},{10,11},{12,13},{... | collective-permute-start | bytes 4718600 | tf_op jit(solution)/shard_map/ppermute | solution.py:946
  11.9 4.4 %collective-permute-start.2 = (bf16[304,768]{1,0:T(8,128)(2,1)S(1)}, bf16[304,768]{1,0:T(8,128)(2,1)S(1)}, u32[]{:S(2)}, u32[]{:S(2)}) collective-permute-start(bf16[304,768]{1,0:T(8,128)(2,1)S(1)} %pad_maximum_fusion.1.refs_0_), channel_id=1, source_target_pairs={{0,16},{1,17},{2,18},{3,19},{4,20},{5,21},{6,22},{7,23},{8,24},{9,... | collective-permute-start | bytes 1400840 | tf_op jit(solution)/shard_map/ppermute | solution.py:960
  16.3 1.6 collective-permute-start.1
  18.1 19.6 %collective-permute-done.2.refs_2_ = bf16[304,768]{1,0:T(8,128)(2,1)S(1)} collective-permute-done((bf16[304,768]{1,0:T(8,128)(2,1)S(1)}, bf16[304,768]{1,0:T(8,128)(2,1)S(1)}, u32[]{:S(2)}, u32[]{:S(2)}) %collective-permute-start.2) | collective-permute-done | bytes 466976 | tf_op jit(solution)/shard_map/ppermute | solution.py:960
  41.6 8.4 %collective-permute-done.4.refs_3_ = bf16[304,768]{1,0:T(8,128)(2,1)S(1)} collective-permute-done((bf16[304,768]{1,0:T(8,128)(2,1)S(1)}, bf16[304,768]{1,0:T(8,128)(2,1)S(1)}, u32[]{:S(2)}, u32[]{:S(2)}) %collective-permute-start.4) | collective-permute-done | bytes 466976 | tf_op jit(solution)/shard_map/ppermute | solution.py:960
  52.8 1.9 arrange.1
  54.9 8.6 %collective-permute-done.5.got_ref = bf16[304,768]{1,0:T(8,128)(2,1)S(1)} collective-permute-done((bf16[304,768]{1,0:T(8,128)(2,1)S(1)}, bf16[304,768]{1,0:T(8,128)(2,1)S(1)}, u32[]{:S(2)}, u32[]{:S(2)}) %collective-permute-start.5) | collective-permute-done | bytes 466976 | tf_op jit(solution)/shard_map/ppermute | solution.py:960
  63.5 1.4 collective-permute-start.6
  64.9 12.0 %collective-permute-done.6.got_ref = bf16[592,768]{1,0:T(8,128)(2,1)S(1)} collective-permute-done((bf16[592,768]{1,0:T(8,128)(2,1)S(1)}, bf16[592,768]{1,0:T(8,128)(2,1)S(1)}, u32[]{:S(2)}, u32[]{:S(2)}) %collective-permute-start.6) | collective-permute-done | bytes 909344 | tf_op jit(solution)/shard_map/ppermute | solution.py:960
  78.0 2.9 collective-permute-done.7.refs_3_
  80.9 13.3 %qkv_fwd.1 = (bf16[2048,2304]{1,0:T(8,128)(2,1)}, f32[16,768]{1,0:T(8,128)}, bf16[2304,768]{1,0:T(8,128)(2,1)}) custom-call(s32[8]{0:T(128)} %stack.217.refs_0_, bf16[2048,768]{1,0:T(8,128)(2,1)} %copy-done.16, bf16[1168,768]{1,0:T(8,128)(2,1)} %copy-done.5, bf16[1168,768]{1,0:T(8,128)(2,1)} %collective-permute-done.7.refs_3_), custom_call_target="tpu_custom_call" | custom-call | flops 7247757312 | bytes 15728640 | tf_op jit(solution)/shard_map/qkv_fwd/pallas_call | solution.py:738
  96.3 1.8 join_held.1
  99.5 32.4 %att_fwd.2 = (bf16[1024,768]{1,0:T(8,128)(2,1)}, f32[1024,768]{1,0:T(8,128)}, bf16[1024,768]{1,0:T(8,128)(2,1)}, bf16[2048,768]{1,0:T(8,128)(2,1)}, bf16[2048,768]{1,0:T(8,128)(2,1)}) custom-call(s32[1]{0:T(128)S(6)} %select_n.125.refs_0_.state_ref, bf16[2048,2304]{1,0:T(8,128)(2,1)} %get-tuple-element.92.refs_1_.refs_2_.refs_3_.refs_4_.refs_7_.refs_8_.refs_9_.refs_10_, ...), custom_call_target="tpu_custom_call" | custom-call | flops 16106127360 | bytes 19660800 | tf_op jit(solution)/shard_map/att_fwd/pallas_call | solution.py:176
  133.2 8.5 %att_fwd.3 = (bf16[1024,768]{1,0:T(8,128)(2,1)}, f32[1024,768]{1,0:T(8,128)}, bf16[1024,768]{1,0:T(8,128)(2,1)}, bf16[2048,768]{1,0:T(8,128)(2,1)}, bf16[2048,768]{1,0:T(8,128)(2,1)}) custom-call(s32[1]{0:T(128)S(6)} %select_n.125.refs_0_.state_ref, ...), custom_call_target="tpu_custom_call", output_to_operand_aliasing={{0}: (6, {}), {1}: (7, {}), {2}: (8, {}), {3}: (9, {}), {4}... | custom-call | flops 3221225472 | bytes 3932160 | tf_op jit(solution)/shard_map/att_fwd/pallas_call | solution.py:176
  141.7 47.3 %ffn.1 = (bf16[1024,768]{1,0:T(8,128)(2,1)}, f32[1024,768]{1,0:T(8,128)}, bf16[1024,768]{1,0:T(8,128)(2,1)}, f32[1,768]{1,0:T(1,128)}, bf16[36,4,24,768]{3,2,1,0...) custom-call(s32[1]{0:T(128)S(6)} %select_n.125.refs_0_.state_ref, s32[25]{0:T(128)} %stack.211.index_ref, ...), custom_call_target="tpu_custom_call" | custom-call | flops 32614907904 | bytes 40894464 | tf_op jit(solution)/shard_map/ffn/pallas_call | solution.py:903
  189.2 9.3 %att_bwd.4 = (bf16[1024,768]{1,0:T(8,128)(2,1)}, bf16[8,768]{1,0:T(8,128)(2,1)}, bf16[2048,768]{1,0:T(8,128)(2,1)}, bf16[2048,768]{1,0:T(8,128)(2,1)}, f32[16,768]{1,0:T(8,128)}) custom-call(s32[1]{0:T(128)S(6)} %select_n.125.refs_0_.state_ref, bf16[1024,768]{1,0:T(8,128)(2,1)} %get-tuple-element.105.refs_1_, bf16[2048,768]{1,0:T(8,128)(2,1)} %get-tuple-element.106.refs_2_, ...), custom_call_target="tpu_custom_call" | custom-call | flops 8053063680 | bytes 5505024 | tf_op jit(solution)/shard_map/att_bwd/pallas_call | solution.py:333
  198.6 7.2 %merge_grid.4 = (bf16[6,288,768]{2,1,0:T(8,128)(2,1)}, bf16[6,288,768]{2,1,0:T(8,128)(2,1)}) custom-call(s32[12]{0:T(128)S(1)} %stack.243.index_ref, bf16[12,288,768]{2,1,0:T(8,128)(2,1)S(1)} %bitcast.71, bf16[12,288,768]{2,1,0:T(8,128)(2,1)} %collective-permute-done.12.ga_ref.gb_ref, bf16[12,288,768]{2,1,0:T(8,128)(2,1)S(1)} %bitcast.72, ...), custom_call_target="tpu_custom_call" | custom-call | flops 2654208 | bytes 21233664 | tf_op jit(solution)/shard_map/merge_grid/pallas_call | solution.py:569
  205.8 5.5 %collective-permute-start.13 = (bf16[6,288,768]{2,1,0:T(8,128)(2,1)}, bf16[6,288,768]{2,1,0:T(8,128)(2,1)S(1)}, u32[]{:S(2)}, u32[]{:S(2)}) collective-permute-start(bf16[6,288,768]{2,1,0:T(8,128)(2,1)} %get-tuple-element.114), channel_id=1, source_target_pairs={{0,2},{1,5},{2,0},{3,7},{4,6},{5,1},{6,4},{7,3},{8,10},{9,13},{10,... | collective-permute-start | bytes 7962632 | tf_op jit(solution)/shard_map/ppermute | solution.py:960
  211.4 22.2 %att_bwd.5 = (bf16[1024,768]{1,0:T(8,128)(2,1)}, bf16[8,768]{1,0:T(8,128)(2,1)}, bf16[2048,768]{1,0:T(8,128)(2,1)}, bf16[2048,768]{1,0:T(8,128)(2,1)}, f32[16,768]{1,0:T(8,128)}) custom-call(s32[1]{0:T(128)S(6)} %select_n.125.refs_0_.state_ref, ...), custom_call_target="tpu_custom_call", output_to_operand_aliasing={{0}: (12, {}), {1}: (13, {}), {2}: (14, {}), {3}: (15, {}),... | custom-call | flops 24159191040 | bytes 16515072 | tf_op jit(solution)/shard_map/att_bwd/pallas_call | solution.py:333
  233.6 7.9 %collective-permute-done.13.ga_ref.gb_ref = bf16[6,288,768]{2,1,0:T(8,128)(2,1)S(1)} collective-permute-done((bf16[6,288,768]{2,1,0:T(8,128)(2,1)}, bf16[6,288,768]{2,1,0:T(8,128)(2,1)S(1)}, u32[]{:S(2)}, u32[]{:S(2)}) %collective-permute-start.13) | collective-permute-done | bytes 2654240 | tf_op jit(solution)/shard_map/ppermute | solution.py:960
  241.5 3.0 merge_grid.5
  244.5 9.6 %att_bwd.6 = (bf16[1024,768]{1,0:T(8,128)(2,1)}, bf16[8,768]{1,0:T(8,128)(2,1)}, bf16[2048,768]{1,0:T(8,128)(2,1)}, bf16[2048,768]{1,0:T(8,128)(2,1)}, f32[16,768]{1,0:T(8,128)}) custom-call(s32[1]{0:T(128)S(6)} %select_n.125.refs_0_.state_ref, ...), custom_call_target="tpu_custom_call", output_to_operand_aliasing={{0}: (12, {}), {1}: (13, {}), {2}: (14, {}), {3}: (15, {}),... | custom-call | flops 8053063680 | bytes 5505024 | tf_op jit(solution)/shard_map/att_bwd/pallas_call | solution.py:333
  254.1 8.4 %collective-permute-done.14.ga_ref.gb_ref = bf16[3,288,768]{2,1,0:T(8,128)(2,1)S(1)} collective-permute-done((bf16[3,288,768]{2,1,0:T(8,128)(2,1)}, bf16[3,288,768]{2,1,0:T(8,128)(2,1)S(1)}, u32[]{:S(2)}, u32[]{:S(2)}) %collective-permute-start.14) | collective-permute-done | bytes 1327136 | tf_op jit(solution)/shard_map/ppermute | solution.py:960
  262.5 2.2 merge_grid.6
  264.6 9.2 %att_bwd.7 = (bf16[1024,768]{1,0:T(8,128)(2,1)}, bf16[8,768]{1,0:T(8,128)(2,1)}, bf16[2048,768]{1,0:T(8,128)(2,1)}, bf16[2048,768]{1,0:T(8,128)(2,1)}, f32[16,768]{1,0:T(8,128)}) custom-call(s32[1]{0:T(128)S(6)} %select_n.125.refs_0_.state_ref, ...), custom_call_target="tpu_custom_call", output_to_operand_aliasing={{0}: (12, {}), {1}: (13, {}), {2}: (14, {}), {3}: (15, {}),... | custom-call | flops 8053063680 | bytes 5505024 | tf_op jit(solution)/shard_map/att_bwd/pallas_call | solution.py:333
  273.9 8.0 %before_bwd.1 = (bf16[1024,768]{1,0:T(8,128)(2,1)}, f32[1,768]{1,0:T(1,128)}) custom-call(bf16[2048,768]{1,0:T(8,128)(2,1)} %copy-done.16, bf16[8,768]{1,0:T(8,128)(2,1)} %get-tuple-element.143.dt_ref.refs_3_, bf16[2048,768]{1,0:T(8,128)(2,1)} %get-tuple-element.144.dk_ref.refs_4_, bf16[2048,768]{1,0:T(8,128)(2,1)} %get-tuple-element.145.dv_ref.refs_5_, ...), custom_call_target="tpu_custom_call" | custom-call | flops 2415919104 | bytes 9437184 | tf_op jit(solution)/shard_map/before_bwd/pallas_call | solution.py:412
  283.3 1.7 merge_grid.7
  285.0 2.9 collective-permute-start.17
  287.9 18.6 %qkv_bwd.1 = (bf16[1232,768]{1,0:T(8,128)(2,1)}, bf16[1232,768]{1,0:T(8,128)(2,1)}, f32[1024,768]{1,0:T(8,128)}) custom-call(s32[1]{0:T(128)} %bitcast.24.refs_0_.index_ref, bf16[2048,768]{1,0:T(8,128)(2,1)} %copy-done.16, bf16[1024,768]{1,0:T(8,128)(2,1)} %get-tuple-element.149.refs_2_, bf16[8,768]{1,0:T(8,128)(2,1)} %get-tuple-element.143.dt_ref.refs_3_, ...), custom_call_target="tpu_custom_call" | custom-call | flops 9663676416 | bytes 23592960 | tf_op jit(solution)/shard_map/qkv_bwd/pallas_call | solution.py:507
  306.6 10.1 %collective-permute-start.18 = (bf16[1232,768]{1,0:T(8,128)(2,1)}, bf16[1232,768]{1,0:T(8,128)(2,1)S(1)}, u32[]{:S(2)}, u32[]{:S(2)}) collective-permute-start(bf16[1232,768]{1,0:T(8,128)(2,1)} %get-tuple-element.156), channel_id=1, source_target_pairs={{0,1},{1,0},{2,3},{3,2},{4,5},{5,4},{6,7},{7,6},{8,9},{9,8},{10,11... | collective-permute-start | bytes 5677064 | tf_op jit(solution)/shard_map/ppermute | solution.py:960
  316.7 3.6 collective-permute-done.18.got_ref
  320.4 1.5 copy-done.4
  321.9 1.8 merge.4
  323.7 5.0 %collective-permute-start.20 = (bf16[624,768]{1,0:T(8,128)(2,1)}, bf16[624,768]{1,0:T(8,128)(2,1)S(1)}, u32[]{:S(2)}, u32[]{:S(2)}) collective-permute-start(bf16[624,768]{1,0:T(8,128)(2,1)} %get-tuple-element.157), channel_id=1, source_target_pairs={{0,2},{1,5},{2,0},{3,7},{4,6},{5,1},{6,4},{7,3},{8,10},{9,13},{10,... | collective-permute-start | bytes 2875400 | tf_op jit(solution)/shard_map/ppermute | solution.py:960
  330.0 2.2 convert_add_fusion.1
  332.2 2.4 copy.39
  334.6 2.4 reshape.115
  337.0 1.7 bitcast_select_fusion
  338.8 2.0 collective-permute-done.20.got_ref
  342.2 2.6 fusion.2
  346.2 4.2 %collective-permute-done.21.got_ref = bf16[320,768]{1,0:T(8,128)(2,1)S(1)} collective-permute-done((bf16[320,768]{1,0:T(8,128)(2,1)S(1)}, bf16[320,768]{1,0:T(8,128)(2,1)S(1)}, u32[]{:S(2)}, u32[]{:S(2)}) %collective-permute-start.21) | collective-permute-done | bytes 491552 | tf_op jit(solution)/shard_map/ppermute | solution.py:960
  350.5 3.1 collective-permute-start.22
  353.5 4.1 %fusion.5 = f32[1024,768]{1,0:T(8,128)} fusion(f32[1024,768]{1,0:T(8,128)S(1)} %copy-done.20, bf16[1024,768]{1,0:T(8,128)(2,1)S(1)} %copy-done.14, f32[1024,768]{1,0:T(8,128)S(1)} %copy-done.15, bf16[1024,768]{1,0:T(8,128)(2,1)} %collective-permute-done.16, f32[1024]{0:T(1024)S(1)} %broadcast_multiply_fusion, f32[768]{0:T(1024)S(1)} %slice_reduce_fusion, ...), kind=kLoop, calls=%fused_computation.7 | loop fusion | flops 7077888 | bytes 12594176 | tf_op jit(solution)/shard_map/add | solution.py:1196
  357.6 6.2 %collective-permute-done.22.got_ref = bf16[320,768]{1,0:T(8,128)(2,1)S(1)} collective-permute-done((bf16[320,768]{1,0:T(8,128)(2,1)S(1)}, bf16[320,768]{1,0:T(8,128)(2,1)S(1)}, u32[]{:S(2)}, u32[]{:S(2)}) %collective-permute-start.22) | collective-permute-done | bytes 491552 | tf_op jit(solution)/shard_map/ppermute | solution.py:960
  366.0 12.2 %collective-permute-done.23 = bf16[320,768]{1,0:T(8,128)(2,1)S(1)} collective-permute-done((bf16[320,768]{1,0:T(8,128)(2,1)S(1)}, bf16[320,768]{1,0:T(8,128)(2,1)S(1)}, u32[]{:S(2)}, u32[]{:S(2)}) %collective-permute-start.23) | collective-permute-done | bytes 491552 | tf_op jit(solution)/shard_map/ppermute | solution.py:960
  379.5 3.5 fusion.16
  (114 shorter events, 22.9 us)
Async XLA Ops:
  1.5 3.3 collective-permute-start
  4.7 2.6 copy-start.21
  4.7 2.6 copy-start.12
  7.3 10.6 %collective-permute-start.3 = (bf16[1024,768]{1,0:T(8,128)(2,1)S(1)}, bf16[1024,768]{1,0:T(8,128)(2,1)S(1)}, u32[]{:S(2)}, u32[]{:S(2)}) collective-permute-start(bf16[1024,768]{1,0:T(8,128)(2,1)S(1)} %copy-done.12), channel_id=1, source_target_pairs={{0,1},{1,2},{2,3},{4,5},{5,6},{6,7},{8,9},{9,10},{10,11},{12,13},{... | collective-permute-start | bytes 4718600 | tf_op jit(solution)/shard_map/ppermute | solution.py:946
  11.9 25.7 %collective-permute-start.2 = (bf16[304,768]{1,0:T(8,128)(2,1)S(1)}, bf16[304,768]{1,0:T(8,128)(2,1)S(1)}, u32[]{:S(2)}, u32[]{:S(2)}) collective-permute-start(bf16[304,768]{1,0:T(8,128)(2,1)S(1)} %pad_maximum_fusion.1.refs_0_), channel_id=1, source_target_pairs={{0,16},{1,17},{2,18},{3,19},{4,20},{5,21},{6,22},{7,23},{8,24},{9,... | collective-permute-start | bytes 1400840 | tf_op jit(solution)/shard_map/ppermute | solution.py:960
  16.3 24.5 %collective-permute-start.1 = (bf16[304,768]{1,0:T(8,128)(2,1)S(1)}, bf16[304,768]{1,0:T(8,128)(2,1)S(1)}, u32[]{:S(2)}, u32[]{:S(2)}) collective-permute-start(bf16[304,768]{1,0:T(8,128)(2,1)S(1)} %pad_maximum_fusion.1.refs_0_), channel_id=1, source_target_pairs={{0,8},{1,9},{2,10},{3,11},{4,12},{5,13},{6,14},{7,15},{8,0},{9,1},... | collective-permute-start | bytes 1400840 | tf_op jit(solution)/shard_map/ppermute | solution.py:960
  18.1 19.6 %copy-start.16 = (bf16[2048,768]{1,0:T(8,128)(2,1)}, bf16[2048,768]{1,0:T(8,128)(2,1)S(1)}, u32[]{:S(2)}) copy-start(bf16[2048,768]{1,0:T(8,128)(2,1)S(1)} %constant_dynamic-update-slice_fusion.refs_1_.x_ref) | copy-start | bytes 9437188
  37.7 12.3 %collective-permute-start.4 = (bf16[304,768]{1,0:T(8,128)(2,1)S(1)}, bf16[304,768]{1,0:T(8,128)(2,1)S(1)}, u32[]{:S(2)}, u32[]{:S(2)}) collective-permute-start(bf16[304,768]{1,0:T(8,128)(2,1)S(1)} %collective-permute-done.2.refs_2_), channel_id=1, source_target_pairs={{0,8},{1,9},{2,10},{3,11},{4,12},{5,13},{6,14},{7,15},{8,0},{9,1},... | collective-permute-start | bytes 1400840 | tf_op jit(solution)/shard_map/ppermute | solution.py:960
  40.8 0.8 copy-start.8
  50.8 1.0 copy-start.9
  51.8 1.0 copy-start.11
  54.8 39.4 %copy-start.6 = (bf16[864,768]{1,0:T(8,128)(2,1)}, bf16[864,768]{1,0:T(8,128)(2,1)S(1)}, u32[]{:S(2)}) copy-start(bf16[864,768]{1,0:T(8,128)(2,1)S(1)} %get-tuple-element.93.own_ref) | copy-start | bytes 3981316
  54.8 8.6 %collective-permute-start.5 = (bf16[304,768]{1,0:T(8,128)(2,1)S(1)}, bf16[304,768]{1,0:T(8,128)(2,1)S(1)}, u32[]{:S(2)}, u32[]{:S(2)}) collective-permute-start(bf16[304,768]{1,0:T(8,128)(2,1)S(1)} %get-tuple-element.91.own_ref), channel_id=1, source_target_pairs={{0,2},{1,5},{2,0},{3,7},{4,6},{5,1},{6,4},{7,3},{8,10},{9,13},{10,... | collective-permute-start | bytes 1400840 | tf_op jit(solution)/shard_map/ppermute | solution.py:960
  63.5 13.4 %collective-permute-start.6 = (bf16[592,768]{1,0:T(8,128)(2,1)S(1)}, bf16[592,768]{1,0:T(8,128)(2,1)S(1)}, u32[]{:S(2)}, u32[]{:S(2)}) collective-permute-start(bf16[592,768]{1,0:T(8,128)(2,1)S(1)} %join.2.own_ref), channel_id=1, source_target_pairs={{0,4},{1,3},{2,6},{3,1},{4,0},{5,7},{6,2},{7,5},{8,12},{9,11},{10,... | collective-permute-start | bytes 2727944 | tf_op jit(solution)/shard_map/ppermute | solution.py:960
  77.0 3.9 %copy-start.5 = (bf16[1168,768]{1,0:T(8,128)(2,1)}, bf16[1168,768]{1,0:T(8,128)(2,1)S(1)}, u32[]{:S(2)}) copy-start(bf16[1168,768]{1,0:T(8,128)(2,1)S(1)} %join.3.refs_2_) | copy-start | bytes 5382148
  77.0 3.9 %collective-permute-start.7 = (bf16[1168,768]{1,0:T(8,128)(2,1)S(1)}, bf16[1168,768]{1,0:T(8,128)(2,1)}, u32[]{:S(2)}, u32[]{:S(2)}) collective-permute-start(bf16[1168,768]{1,0:T(8,128)(2,1)S(1)} %join.3.refs_2_), channel_id=1, source_target_pairs={{0,1},{1,0},{2,3},{3,2},{4,5},{5,4},{6,7},{7,6},{8,9},{9,8},{10,11... | collective-permute-start | bytes 5382152 | tf_op jit(solution)/shard_map/ppermute | solution.py:960
  77.1 18.0 %collective-permute-start.8 = (bf16[864,768]{1,0:T(8,128)(2,1)S(1)}, bf16[864,768]{1,0:T(8,128)(2,1)}, u32[]{:S(2)}, u32[]{:S(2)}) collective-permute-start(bf16[864,768]{1,0:T(8,128)(2,1)S(1)} %get-tuple-element.93.own_ref), channel_id=1, source_target_pairs={{0,2},{1,5},{2,0},{3,7},{4,6},{5,1},{6,4},{7,3},{8,10},{9,13},{10,... | collective-permute-start | bytes 3981320 | tf_op jit(solution)/shard_map/ppermute | solution.py:960
  95.0 1.3 copy-start.7
  98.1 33.8 %copy-start.3 = (bf16[1728,768]{1,0:T(8,128)(2,1)}, bf16[1728,768]{1,0:T(8,128)(2,1)S(1)}, u32[]{:S(2)}) copy-start(bf16[1728,768]{1,0:T(8,128)(2,1)S(1)} %join_held.1) | copy-start | bytes 7962628
  98.1 33.8 %collective-permute-start.9 = (bf16[1728,768]{1,0:T(8,128)(2,1)S(1)}, bf16[1728,768]{1,0:T(8,128)(2,1)}, u32[]{:S(2)}, u32[]{:S(2)}) collective-permute-start(bf16[1728,768]{1,0:T(8,128)(2,1)S(1)} %join_held.1), channel_id=1, source_target_pairs={{0,4},{1,3},{2,6},{3,1},{4,0},{5,7},{6,2},{7,5},{8,12},{9,11},{10,... | collective-permute-start | bytes 7962632 | tf_op jit(solution)/shard_map/ppermute | solution.py:960
  99.5 33.7 %collective-permute-start.10 = (bf16[1728,768]{1,0:T(8,128)(2,1)S(1)}, bf16[1728,768]{1,0:T(8,128)(2,1)}, u32[]{:S(2)}, u32[]{:S(2)}) collective-permute-start(bf16[1728,768]{1,0:T(8,128)(2,1)S(1)} %join_held.1), channel_id=1, source_target_pairs={{0,1},{1,0},{2,3},{3,2},{4,5},{5,4},{6,7},{7,6},{8,9},{9,8},{10,11... | collective-permute-start | bytes 7962632 | tf_op jit(solution)/shard_map/ppermute | solution.py:960
  132.0 9.7 %collective-permute-start.11 = (bf16[1728,768]{1,0:T(8,128)(2,1)}, bf16[1728,768]{1,0:T(8,128)(2,1)}, u32[]{:S(2)}, u32[]{:S(2)}) collective-permute-start(bf16[1728,768]{1,0:T(8,128)(2,1)} %hold.1), channel_id=1, source_target_pairs={{0,1},{1,0},{2,3},{3,2},{4,5},{5,4},{6,7},{7,6},{8,9},{9,8},{10,11... | collective-permute-start | bytes 7962632 | tf_op jit(solution)/shard_map/ppermute | solution.py:960
  189.0 9.6 %collective-permute-start.12 = (bf16[12,288,768]{2,1,0:T(8,128)(2,1)}, bf16[12,288,768]{2,1,0:T(8,128)(2,1)}, u32[]{:S(2)}, u32[]{:S(2)}) collective-permute-start(bf16[12,288,768]{2,1,0:T(8,128)(2,1)} %bitcast.75), channel_id=1, source_target_pairs={{0,1},{1,0},{2,3},{3,2},{4,5},{5,4},{6,7},{7,6},{8,9},{9,8},{10,11... | collective-permute-start | bytes 15925256 | tf_op jit(solution)/shard_map/ppermute | solution.py:960
  189.2 9.4 %slice-start = ((s8[5308416]{0:T(1024)(128)(4,1)}), s8[4194304]{0:T(1024)(128)(4,1)S(1)}, s32[]{:S(2)}) async-start(s8[5308416]{0:T(1024)(128)(4,1)} %bitcast.69), calls=%async_computation | async-start | bytes 8388608
  189.2 9.4 %slice-start.1 = ((s8[5308416]{0:T(1024)(128)(4,1)}), s8[1114112]{0:T(1024)(128)(4,1)S(1)}, s32[]{:S(2)}) async-start(s8[5308416]{0:T(1024)(128)(4,1)} %bitcast.69), calls=%async_computation.1 | async-start | bytes 2228224
  205.8 35.7 %collective-permute-start.13 = (bf16[6,288,768]{2,1,0:T(8,128)(2,1)}, bf16[6,288,768]{2,1,0:T(8,128)(2,1)S(1)}, u32[]{:S(2)}, u32[]{:S(2)}) collective-permute-start(bf16[6,288,768]{2,1,0:T(8,128)(2,1)} %get-tuple-element.114), channel_id=1, source_target_pairs={{0,2},{1,5},{2,0},{3,7},{4,6},{5,1},{6,4},{7,3},{8,10},{9,13},{10,... | collective-permute-start | bytes 7962632 | tf_op jit(solution)/shard_map/ppermute | solution.py:960
  211.4 30.1 %copy-start = (bf16[6,288,768]{2,1,0:T(8,128)(2,1)S(1)}, bf16[6,288,768]{2,1,0:T(8,128)(2,1)}, u32[]{:S(2)}) copy-start(bf16[6,288,768]{2,1,0:T(8,128)(2,1)} %get-tuple-element.122.ka_ref.kb_ref) | copy-start | bytes 7962628
  244.5 18.0 %collective-permute-start.14 = (bf16[3,288,768]{2,1,0:T(8,128)(2,1)}, bf16[3,288,768]{2,1,0:T(8,128)(2,1)S(1)}, u32[]{:S(2)}, u32[]{:S(2)}) collective-permute-start(bf16[3,288,768]{2,1,0:T(8,128)(2,1)} %get-tuple-element.123), channel_id=1, source_target_pairs={{0,4},{1,3},{2,6},{3,1},{4,0},{5,7},{6,2},{7,5},{8,12},{9,11},{10,... | collective-permute-start | bytes 3981320 | tf_op jit(solution)/shard_map/ppermute | solution.py:960
  244.5 18.0 %copy-start.1 = (f32[3,288,768]{2,1,0:T(8,128)S(1)}, f32[3,288,768]{2,1,0:T(8,128)}, u32[]{:S(2)}) copy-start(f32[3,288,768]{2,1,0:T(8,128)} %get-tuple-element.131.ka_ref.kb_ref) | copy-start | bytes 7962628
  264.6 18.6 %collective-permute-start.15 = (bf16[2,288,768]{2,1,0:T(8,128)(2,1)}, bf16[2,288,768]{2,1,0:T(8,128)(2,1)S(1)}, u32[]{:S(2)}, u32[]{:S(2)}) collective-permute-start(bf16[2,288,768]{2,1,0:T(8,128)(2,1)} %get-tuple-element.132), channel_id=1, source_target_pairs={{0,8},{1,9},{2,10},{3,11},{4,12},{5,13},{6,14},{7,15},{8,0},{9,1},... | collective-permute-start | bytes 2654216 | tf_op jit(solution)/shard_map/ppermute | solution.py:960
  273.9 9.4 %copy-start.2 = (f32[2,288,768]{2,1,0:T(8,128)S(1)}, f32[2,288,768]{2,1,0:T(8,128)}, u32[]{:S(2)}) copy-start(f32[2,288,768]{2,1,0:T(8,128)} %get-tuple-element.140.ka_ref.kb_ref) | copy-start | bytes 5308420
  281.9 24.7 %collective-permute-start.16 = (bf16[1024,768]{1,0:T(8,128)(2,1)}, bf16[1024,768]{1,0:T(8,128)(2,1)}, u32[]{:S(2)}, u32[]{:S(2)}) collective-permute-start(bf16[1024,768]{1,0:T(8,128)(2,1)} %get-tuple-element.147), channel_id=1, source_target_pairs={{1,0},{2,1},{3,2},{5,4},{6,5},{7,6},{9,8},{10,9},{11,10},{13,12},{... | collective-permute-start | bytes 4718600 | tf_op jit(solution)/shard_map/ppermute | solution.py:946
  285.0 21.5 %collective-permute-start.17 = (bf16[1,288,768]{2,1,0:T(8,128)(2,1)}, bf16[1,288,768]{2,1,0:T(8,128)(2,1)S(1)}, u32[]{:S(2)}, u32[]{:S(2)}) collective-permute-start(bf16[1,288,768]{2,1,0:T(8,128)(2,1)} %get-tuple-element.141), channel_id=1, source_target_pairs={{0,16},{1,17},{2,18},{3,19},{4,20},{5,21},{6,22},{7,23},{8,24},{9,... | collective-permute-start | bytes 1327112 | tf_op jit(solution)/shard_map/ppermute | solution.py:960
  287.9 40.8 %copy-start.13 = (bf16[1024,768]{1,0:T(8,128)(2,1)S(1)}, bf16[1024,768]{1,0:T(8,128)(2,1)}, u32[]{:S(2)}) copy-start(bf16[1024,768]{1,0:T(8,128)(2,1)} %x_ref.1) | copy-start | bytes 4718596
  306.5 22.6 %copy-start.22 = (pred[3]{0:T(512)(128)(4,1)S(1)}, pred[3]{0:T(512)(128)(4,1)}, u32[]{:S(2)}) copy-start(pred[3]{0:T(512)(128)(4,1)} %copy-done.21) | copy-start | bytes 13
  306.6 13.8 %collective-permute-start.18 = (bf16[1232,768]{1,0:T(8,128)(2,1)}, bf16[1232,768]{1,0:T(8,128)(2,1)S(1)}, u32[]{:S(2)}, u32[]{:S(2)}) collective-permute-start(bf16[1232,768]{1,0:T(8,128)(2,1)} %get-tuple-element.156), channel_id=1, source_target_pairs={{0,1},{1,0},{2,3},{3,2},{4,5},{5,4},{6,7},{7,6},{8,9},{9,8},{10,11... | collective-permute-start | bytes 5677064 | tf_op jit(solution)/shard_map/ppermute | solution.py:960
  320.4 1.5 copy-start.4
  323.7 17.0 %collective-permute-start.20 = (bf16[624,768]{1,0:T(8,128)(2,1)}, bf16[624,768]{1,0:T(8,128)(2,1)S(1)}, u32[]{:S(2)}, u32[]{:S(2)}) collective-permute-start(bf16[624,768]{1,0:T(8,128)(2,1)} %get-tuple-element.157), channel_id=1, source_target_pairs={{0,2},{1,5},{2,0},{3,7},{4,6},{5,1},{6,4},{7,3},{8,10},{9,13},{10,... | collective-permute-start | bytes 2875400 | tf_op jit(solution)/shard_map/ppermute | solution.py:960
  337.0 5.2 %copy-start.14 = (bf16[1024,768]{1,0:T(8,128)(2,1)S(1)}, bf16[1024,768]{1,0:T(8,128)(2,1)}, u32[]{:S(2)}) copy-start(bf16[1024,768]{1,0:T(8,128)(2,1)} %x_ref.1) | copy-start | bytes 4718596
  337.0 5.2 %copy-start.15 = (f32[1024,768]{1,0:T(8,128)S(1)}, f32[1024,768]{1,0:T(8,128)}, u32[]{:S(2)}) copy-start(f32[1024,768]{1,0:T(8,128)} %get-tuple-element.152) | copy-start | bytes 9437188
  338.8 6.1 %copy-start.18 = (f32[288,768]{1,0:T(8,128)}, f32[288,768]{1,0:T(8,128)S(1)}, u32[]{:S(2)}) copy-start(f32[288,768]{1,0:T(8,128)S(1)} %bitcast_select_fusion) | copy-start | bytes 2654212
  341.5 8.9 %collective-permute-start.21 = (bf16[320,768]{1,0:T(8,128)(2,1)S(1)}, bf16[320,768]{1,0:T(8,128)(2,1)S(1)}, u32[]{:S(2)}, u32[]{:S(2)}) collective-permute-start(bf16[320,768]{1,0:T(8,128)(2,1)S(1)} %get-tuple-element.163), channel_id=1, source_target_pairs={{0,4},{1,3},{2,6},{3,1},{4,0},{5,7},{6,2},{7,5},{8,12},{9,11},{10,... | collective-permute-start | bytes 1474568 | tf_op jit(solution)/shard_map/ppermute | solution.py:960
  342.2 11.3 %copy-start.20 = (f32[1024,768]{1,0:T(8,128)S(1)}, f32[1024,768]{1,0:T(8,128)}, u32[]{:S(2)}) copy-start(f32[1024,768]{1,0:T(8,128)} %get-tuple-element.104) | copy-start | bytes 9437188
  344.9 12.8 %collective-permute-start.19 = (f32[16,768]{1,0:T(8,128)S(1)}, f32[16,768]{1,0:T(8,128)S(1)}, u32[]{:S(2)}, u32[]{:S(2)}) collective-permute-start(f32[16,768]{1,0:T(8,128)S(1)} %slice.29), channel_id=1, source_target_pairs={{1,0},{2,1},{3,2},{4,3},{5,4},{6,5},{7,6},{8,7},{9,8},{10,9},{11,1... | collective-permute-start | bytes 147464 | tf_op jit(solution)/shard_map/ppermute | solution.py:940
  350.5 13.4 %collective-permute-start.22 = (bf16[320,768]{1,0:T(8,128)(2,1)S(1)}, bf16[320,768]{1,0:T(8,128)(2,1)S(1)}, u32[]{:S(2)}, u32[]{:S(2)}) collective-permute-start(bf16[320,768]{1,0:T(8,128)(2,1)S(1)} %get-tuple-element.165), channel_id=1, source_target_pairs={{0,8},{1,9},{2,10},{3,11},{4,12},{5,13},{6,14},{7,15},{8,0},{9,1},... | collective-permute-start | bytes 1474568 | tf_op jit(solution)/shard_map/ppermute | solution.py:960
  357.6 20.7 %copy-start.19 = (f32[288,768]{1,0:T(8,128)S(1)}, f32[288,768]{1,0:T(8,128)}, u32[]{:S(2)}) copy-start(f32[288,768]{1,0:T(8,128)} %copy-done.18) | copy-start | bytes 2654212
  364.0 14.2 %collective-permute-start.23 = (bf16[320,768]{1,0:T(8,128)(2,1)S(1)}, bf16[320,768]{1,0:T(8,128)(2,1)S(1)}, u32[]{:S(2)}, u32[]{:S(2)}) collective-permute-start(bf16[320,768]{1,0:T(8,128)(2,1)S(1)} %get-tuple-element.167), channel_id=1, source_target_pairs={{8,24},{9,25},{10,26},{11,27},{12,28},{13,29},{14,30},{15,31},{16,... | collective-permute-start | bytes 1474568 | tf_op jit(solution)/shard_map/ppermute | solution.py:960
  378.3 1.2 copy-start.17
  (1 other events, 0.8 us)
